TPU v7x, 32 devices: a whole 2x2x4 slice. The times are simulated.
32 devices in a mesh: dp: 2 (over core), space: 16 (over z, y, x).
Axes of the slice: x: 2, y: 2, z: 4, core: 2. Of those that a mesh axis runs over, the one named last changes fastest.
Arguments:
- master: float32 [1156352], P(('dp', 'space')), may hold values from -0.375 to 0.375
- moment1: float32 [1156352], P(('dp', 'space')), may hold values from -7.6293945e-05 to 7.6293945e-05
- moment2: float32 [1156352], P(('dp', 'space')), may hold values from 2.1619713e-12 to 8.647885e-12
- inputs: bfloat16 [2, 78, 8192], P('dp', None, 'space'), may hold values from -6 to 6
- targets: bfloat16 [2, 78, 8192], P('dp', None, 'space'), may hold values from -6 to 6
- valid: int32 [2, 78, 8192], P('dp', None, 'space'), may hold values from 0 to 1
- owner: int32 [2, 8192, 1], P('dp', 'space'), may hold values from 0 to 15; in each aligned block of 512 rows (0 to 511, 512 to 1023, ..., all dimensions but the last counted through in order) at most 64 rows name the same one
- slot: int32 [2, 8192], P('dp', 'space'), may hold values from 0 to 2047
- neighbours: int32 [32768, 6], P('space'), may hold values from 0 to 32767, as said below
- partner: int32 [8192], P('space'), may hold values from 0 to 8191, as said below
Outputs:
- loss_total: float32 [1], replicated
- valid_count: float32 [1], replicated
- grad_norm: float32 [1], replicated
- new_master: float32 [1156352], P(('dp', 'space'))
- new_moment1: float32 [1156352], P(('dp', 'space'))
- new_moment2: float32 [1156352], P(('dp', 'space'))
- new_copy: bfloat16 [1156352], P(('dp', 'space'))
- final_mesh: float32 [2, 32768, 256], P('dp', 'space')
- node_grads: float32 [2, 32768, 256], P('dp', 'space')
- pred_grads: float32 [2, 78, 8192], P('dp', None, 'space')
Inputs may be any that keep to these rules, and one draw needn't show every extreme that they name: `neighbours`: each entry is a node number within 2048 of its row's own number, counted cyclically over 32768; a distance of exactly 2048 occurs in both directions. partner[g] - g lies in 358 to 360; where that passes the last point, partner[g] = g.
All inputs are finite; a program needn't handle non-finite values.
Results may differ from a plain program's by a relative error of at most 0.014.
Values may be sent and summed in bfloat16 or wider, within the bound.
No kernel may reach another device: no remote copies, remote signals or barrier semaphores. Data moves between devices by JAX's collectives and lax.ppermute only.
A program may use at most 192 MiB of HBM per device.

v0:
```python
import math

import jax
import jax.numpy as jnp
from jax import lax
from jax.sharding import PartitionSpec as P

D = 256
CH = 78
ROUNDS = 3
K = 6
ROWW = 360
STEP = 10
H = 2048


def extended(shard, sides, width):
    for axis, dim in sides:
        peers, length = (lax.axis_size(axis), shard.shape[dim])
        up = [(i, (i + 1) % peers) for i in range(peers)]
        down = [(j, i) for i, j in up]
        last = lax.slice_in_dim(shard, length - width, length, axis=dim)
        initial = lax.slice_in_dim(shard, 0, width, axis=dim)
        before = lax.ppermute(last, axis, up)
        after = lax.ppermute(initial, axis, down)
        shard = jnp.concatenate([before, shard, after], axis=dim)
    return shard


def shifted(shard, axis, by):
    peers = lax.axis_size(axis)
    pairs = [(i, i + by) for i in range(peers) if 0 <= i + by < peers]
    return lax.ppermute(shard, axis, pairs)


def layout():
    return [(CH, D), (D, D), (D, D), (D, CH), (ROUNDS, 5, D, D), (3, D), (ROUNDS, 2, D)]


def unpack(flat):
    pieces = []
    start = 0
    for shape in layout():
        count = math.prod(shape)
        pieces.append(flat[start : start + count].reshape(shape))
        start = start + count
    return pieces


def inner(left, right, left_dim, right_dim):
    return lax.dot_general(
        left, right, (((left_dim,), (right_dim,)), ((), ())), preferred_element_type=jnp.float32
    )


def slope(value):
    sigma = jax.nn.sigmoid(value)
    return sigma * (1.0 + value * (1.0 - sigma))


def edge_inputs(padded, dest, places, edge):
    return padded[places[:, edge]].astype(jnp.float32) + dest


def round_forward(mesh, mats, bias, places):
    lowered = mesh.astype(jnp.bfloat16)
    sent = inner(lowered, mats[0], 1, 0).astype(jnp.bfloat16)
    padded = extended(sent, (("space", 0),), H)
    dest = inner(lowered, mats[1], 1, 0) + bias[0]
    agg = jnp.zeros_like(mesh)
    for edge in range(K):
        agg = agg + jax.nn.silu(edge_inputs(padded, dest, places, edge))
    agg = agg / K
    update_in = (
        inner(agg.astype(jnp.bfloat16), mats[2], 1, 0) + inner(lowered, mats[3], 1, 0) + bias[1]
    )
    update = jax.nn.silu(update_in).astype(jnp.bfloat16)
    return (mesh + inner(update, mats[4], 1, 0), padded)


def round_backward(grad_mesh, mesh, padded, mats, bias, places):
    blocks = mesh.shape[0]
    lowered = mesh.astype(jnp.bfloat16)
    dest = inner(lowered, mats[1], 1, 0) + bias[0]
    agg = jnp.zeros_like(mesh)
    for edge in range(K):
        agg = agg + jax.nn.silu(edge_inputs(padded, dest, places, edge))
    agg = agg / K
    agg_low = agg.astype(jnp.bfloat16)
    update_in = inner(agg_low, mats[2], 1, 0) + inner(lowered, mats[3], 1, 0) + bias[1]
    update = jax.nn.silu(update_in).astype(jnp.bfloat16)
    grad_out = grad_mesh.astype(jnp.bfloat16)
    grad_final = inner(update, grad_out, 0, 0)
    grad_update = inner(grad_out, mats[4], 1, 1)
    grad_uin = (grad_update * slope(update_in)).astype(jnp.bfloat16)
    grad_bupd = jnp.sum(grad_uin.astype(jnp.float32), 0)
    grad_aggw = inner(agg_low, grad_uin, 0, 0)
    grad_selfw = inner(lowered, grad_uin, 0, 0)
    grad_agg = inner(grad_uin, mats[2], 1, 1) / K
    grad_low = inner(grad_uin, mats[3], 1, 1)
    grad_pad = jnp.zeros((padded.shape[0], mesh.shape[1]), jnp.float32)
    grad_dest = jnp.zeros_like(mesh)
    for edge in range(K):
        grad_edge = grad_agg * slope(edge_inputs(padded, dest, places, edge))
        grad_dest = grad_dest + grad_edge
        grad_pad = grad_pad.at[places[:, edge]].add(grad_edge)
    dest_low = grad_dest.astype(jnp.bfloat16)
    grad_bedge = jnp.sum(dest_low.astype(jnp.float32), 0)
    grad_dstw = inner(lowered, dest_low, 0, 0)
    grad_low = grad_low + inner(dest_low, mats[1], 1, 1)
    edges = jnp.concatenate([grad_pad[:H], grad_pad[blocks + H :]], 0)
    widened = extended(edges.astype(jnp.bfloat16), (("space", 0),), H).astype(edges.dtype)
    grad_sent = grad_pad[H : H + blocks]
    grad_sent = grad_sent.at[:H].add(widened[:H]).at[blocks - H :].add(widened[3 * H :])
    sent_low = grad_sent.astype(jnp.bfloat16)
    grad_srcw = inner(lowered, sent_low, 0, 0)
    grad_low = grad_low + inner(sent_low, mats[0], 1, 1)
    mats_grad = jnp.stack([grad_srcw, grad_dstw, grad_aggw, grad_selfw, grad_final])
    return (grad_mesh + grad_low, mats_grad, jnp.stack([grad_bedge, grad_bupd]))


def shards(master, moment1, moment2, inputs, targets, valid, owner, slot, neighbours, partner):
    bands = lax.axis_size("space")
    band = lax.axis_index("space")
    shard = master.shape[0]
    everything = lax.all_gather(master.astype(jnp.bfloat16), ("dp", "space"), axis=0, tiled=True)
    w_in, w_node, w_dec, w_out, w_round, b_head, b_round = unpack(everything)
    state_in = inputs[0]
    wanted = targets[0].astype(jnp.float32)
    counted = valid[0].astype(jnp.float32)
    points = state_in.shape[1]
    blocks = neighbours.shape[0]
    capacity = max(2, 2 * points // bands)
    target_band = owner[0, :, 0]
    hits = (target_band[:, None] == jnp.arange(bands, dtype=jnp.int32)[None, :]).astype(jnp.int32)
    ranks = jnp.sum(jnp.cumsum(hits, 0) * hits, 1) - 1
    places_out = target_band * capacity + ranks
    enc_in = inner(state_in, w_in, 0, 0) + b_head[0]
    encoded = jax.nn.silu(enc_in).astype(jnp.bfloat16)
    outbox = jnp.zeros((bands * capacity, D), jnp.bfloat16).at[places_out].set(encoded)
    labels = jnp.full((bands * capacity,), -1, jnp.int32).at[places_out].set(slot[0])
    arrived, arrived_ids = (
        lax.all_to_all(
            outbox.reshape(bands, capacity, D), "space", split_axis=0, concat_axis=0, tiled=True
        ),
        lax.all_to_all(
            labels.reshape(bands, capacity), "space", split_axis=0, concat_axis=0, tiled=True
        ),
    )
    chooser = (
        arrived_ids.reshape(-1)[:, None] == jnp.arange(blocks, dtype=jnp.int32)[None, :]
    ).astype(jnp.bfloat16)
    gathered = inner(chooser, arrived.reshape(-1, D), 0, 0).astype(jnp.bfloat16)
    node_in = inner(gathered, w_node, 1, 0) + b_head[1]
    mesh = jax.nn.silu(node_in)
    places = (neighbours - band * blocks + H) % (blocks * bands)
    kept_mesh = []
    kept_pad = []
    for layer in range(ROUNDS):
        kept_mesh.append(mesh)
        mesh, padded = round_forward(mesh, w_round[layer], b_round[layer], places)
        kept_pad.append(padded)
    reply = inner(chooser, mesh.astype(jnp.bfloat16), 1, 0).astype(jnp.bfloat16)
    returned = lax.all_to_all(
        reply.reshape(bands, capacity, D), "space", split_axis=0, concat_axis=0, tiled=True
    )
    fetched = returned.reshape(-1, D)[places_out]
    dec_in = inner(fetched, w_dec, 1, 0) + b_head[2]
    decoded = jax.nn.silu(dec_in).astype(jnp.bfloat16)
    err = state_in.astype(jnp.float32) + inner(w_out, decoded, 0, 1) - wanted
    head_err, head_valid = (
        shifted(err[:, :ROWW].astype(jnp.bfloat16), "space", -1).astype(jnp.float32),
        shifted(counted[:, :ROWW].astype(jnp.bfloat16), "space", -1).astype(jnp.float32),
    )
    wide_err = jnp.concatenate([err, head_err], 1)
    wide_valid = jnp.concatenate([counted, head_valid], 1)
    partner_at = partner - band * points
    err_far = wide_err[:, partner_at]
    valid_far = wide_valid[:, partner_at]
    gap = err - err_far
    local_total = jnp.sum(counted * err * err) + 0.5 * jnp.sum(counted * valid_far * gap * gap)
    total, count = lax.psum((local_total, jnp.sum(counted)), ("dp", "space"))
    paired = counted * valid_far * gap / count
    grad_err = 2.0 * counted * err / count + paired
    grad_wide = jnp.zeros(wide_err.shape, jnp.float32).at[:, partner_at].add(-paired)
    carried = shifted(grad_wide[:, points:].astype(jnp.bfloat16), "space", 1).astype(jnp.float32)
    grad_pred = (grad_err + grad_wide[:, :points]).at[:, :ROWW].add(carried)
    grad_branch = grad_pred.astype(jnp.bfloat16)
    grad_wout = inner(decoded, grad_branch, 0, 1)
    grad_dec = (inner(grad_branch, w_out, 0, 1) * slope(dec_in)).astype(jnp.bfloat16)
    grad_bdec = jnp.sum(grad_dec.astype(jnp.float32), 0)
    grad_wdec = inner(fetched, grad_dec, 0, 0)
    grad_fetched = inner(grad_dec, w_dec, 1, 1).astype(jnp.bfloat16)
    backbox = jnp.zeros((bands * capacity, D), jnp.bfloat16).at[places_out].set(grad_fetched)
    landed = lax.all_to_all(
        backbox.reshape(bands, capacity, D), "space", split_axis=0, concat_axis=0, tiled=True
    )
    grad_mesh = inner(chooser, landed.reshape(-1, D), 0, 0)
    mats_grads = []
    bias_grads = []
    for layer in reversed(range(ROUNDS)):
        grad_mesh, mats_grad, bias_grad = round_backward(
            grad_mesh, kept_mesh[layer], kept_pad[layer], w_round[layer], b_round[layer], places
        )
        mats_grads.insert(0, mats_grad)
        bias_grads.insert(0, bias_grad)
    grad_node = (grad_mesh * slope(node_in)).astype(jnp.bfloat16)
    grad_bnode = jnp.sum(grad_node.astype(jnp.float32), 0)
    grad_wnode = inner(gathered, grad_node, 0, 0)
    grad_gathered = inner(grad_node, w_node, 1, 1).astype(jnp.bfloat16)
    sendback = inner(chooser, grad_gathered, 1, 0).astype(jnp.bfloat16)
    homeward = lax.all_to_all(
        sendback.reshape(bands, capacity, D), "space", split_axis=0, concat_axis=0, tiled=True
    )
    grad_encoded = homeward.reshape(-1, D)[places_out].astype(jnp.float32)
    grad_enc = (grad_encoded * slope(enc_in)).astype(jnp.bfloat16)
    grad_bin = jnp.sum(grad_enc.astype(jnp.float32), 0)
    grad_win = inner(state_in, grad_enc, 1, 0)
    pieces = [
        grad_win,
        grad_wnode,
        grad_wdec,
        grad_wout,
        jnp.stack(mats_grads),
        jnp.stack([grad_bin, grad_bnode, grad_bdec]),
        jnp.stack(bias_grads),
    ]
    flat = jnp.concatenate([piece.reshape(-1) for piece in pieces])
    flat = jnp.concatenate([flat, jnp.zeros((everything.shape[0] - flat.shape[0],), jnp.float32)])
    summed = lax.psum(flat, ("dp", "space"))
    norm = jnp.sqrt(jnp.sum(summed * summed))
    mine = lax.dynamic_slice_in_dim(summed, lax.axis_index(("dp", "space")) * shard, shard)
    clipped = mine * jnp.minimum(1.0, 0.05 / norm)
    first = 0.9 * moment1 + 0.1 * clipped
    second = 0.999 * moment2 + 0.001 * clipped * clipped
    first_hat = first / (1.0 - 0.9**STEP)
    second_hat = second / (1.0 - 0.999**STEP)
    updated = master - 0.1 * (first_hat / (jnp.sqrt(second_hat) + 1e-08) + 0.1 * master)
    return (
        total.reshape(1),
        count.reshape(1),
        norm.reshape(1),
        updated,
        first,
        second,
        updated.astype(jnp.bfloat16),
        mesh.reshape(1, blocks, D),
        grad_mesh.reshape(1, blocks, D),
        grad_pred.reshape(1, grad_pred.shape[0], points),
    )


def solution(mesh):
    return jax.shard_map(
        shards,
        mesh=mesh,
        in_specs=(
            P(("dp", "space")),
            P(("dp", "space")),
            P(("dp", "space")),
            P("dp", None, "space"),
            P("dp", None, "space"),
            P("dp", None, "space"),
            P("dp", "space", None),
            P("dp", "space"),
            P("space", None),
            P("space"),
        ),
        out_specs=(
            P(),
            P(),
            P(),
            P(("dp", "space")),
            P(("dp", "space")),
            P(("dp", "space")),
            P(("dp", "space")),
            P("dp", "space", None),
            P("dp", "space", None),
            P("dp", None, "space"),
        ),
        check_vma=False,
    )
```

profile of v0, /device:TPU:0, one launch (start us, length us, event | category | flops | bytes accessed | tf_op | source)
XLA Modules:
  0.0 1434.8 jit_solution(12356482560449952227)
XLA Ops:
  32.4 118.8 %all-reduce.7.cloned.1.call-done = bf16[1156352]{0:T(1024)(128)(2,1)} async-done(((bf16[1156352]{0:T(1024)(128)(2,1)}), bf16[1156352]{0:T(1024)(128)(2,1)}) %all-reduce.7.cloned.1.call-update) | async-done | bytes 2312720
  164.6 12.9 all-to-all-done.1
  193.3 33.7 %collective-permute-done = bf16[2048,256]{1,0:T(8,128)(2,1)S(1)} collective-permute-done((bf16[2048,256]{1,0:T(8,128)(2,1)S(1)}, bf16[2048,256]{1,0:T(8,128)(2,1)S(1)}, u32[]{:S(2)}, u32[]{:S(2)}) %collective-permute-start) | collective-permute-done | bytes 1048608 | tf_op jit(solution)/shard_map/ppermute | solution.py:24
  231.2 9.0 gather_fusion.1
  240.2 9.7 gather_fusion.2
  249.9 9.7 gather_fusion.3
  259.6 9.7 gather_fusion.4
  269.4 9.7 gather_fusion.5
  311.6 35.0 %collective-permute-done.2 = bf16[2048,256]{1,0:T(8,128)(2,1)S(1)} collective-permute-done((bf16[2048,256]{1,0:T(8,128)(2,1)S(1)}, bf16[2048,256]{1,0:T(8,128)(2,1)S(1)}, u32[]{:S(2)}, u32[]{:S(2)}) %collective-permute-start.2) | collective-permute-done | bytes 1048608 | tf_op jit(solution)/shard_map/ppermute | solution.py:24
  356.2 9.7 gather_fusion.10
  365.9 9.7 gather_fusion.11
  375.6 9.0 gather_fusion.7
  384.6 9.7 gather_fusion.8
  394.4 9.7 gather_fusion.9
  404.1 9.0 gather_fusion.6
  435.2 38.1 %collective-permute-done.4 = bf16[2048,256]{1,0:T(8,128)(2,1)S(1)} collective-permute-done((bf16[2048,256]{1,0:T(8,128)(2,1)S(1)}, bf16[2048,256]{1,0:T(8,128)(2,1)S(1)}, u32[]{:S(2)}, u32[]{:S(2)}) %collective-permute-start.4) | collective-permute-done | bytes 1048608 | tf_op jit(solution)/shard_map/ppermute | solution.py:24
  477.5 9.0 gather_fusion.13
  486.5 9.9 gather_fusion.14
  496.4 9.0 gather_fusion.15
  505.4 9.9 gather_fusion.16
  524.2 9.0 gather_fusion.12
  593.9 47.1 %all-reduce.1 = (f32[1]{0:T(128)}, f32[]{:T(128)}) all-reduce(f32[1]{0:T(128)} %bitcast.23, f32[]{:T(128)} %fusion.67), channel_id=1, replica_groups=mesh['dp'=2,'space'=16] {'dp','space'}, use_global_device_ids=true, to_apply=%region_7.8 | all-reduce | flops 2 | bytes 16 | tf_op jit(solution)/shard_map/psum | solution.py:182
  676.7 12.3 all-to-all-done.3
  703.4 15.8 %scatter_custom_fusion.4 = f32[6144,256]{1,0:T(8,128)} fusion(s32[2048]{0:T(1024)} %bitcast.315, f32[]{:T(128)} %constant.352.clone.1, f32[2048,256]{1,0:T(8,128)} %get-tuple-element.236, f32[2048,256]{1,0:T(8,128)S(1)} %get-tuple-element.233, bf16[2048,256]{1,0:T(8,128)(2,1)} %gather_fusion.12), kind=kCustom, calls=%fused_computation.62 | custom fusion | flops 5767168 | bytes 11534848 | tf_op jit(solution)/shard_map/scatter-add | solution.py:106
  719.2 18.3 %scatter_custom_fusion.5 = f32[6144,256]{1,0:T(8,128)} fusion(f32[6144,256]{1,0:T(8,128)} %scatter_custom_fusion.4, s32[2048]{0:T(1024)} %bitcast.311, f32[2048,256]{1,0:T(8,128)} %get-tuple-element.236, f32[2048,256]{1,0:T(8,128)S(1)} %get-tuple-element.233, bf16[2048,256]{1,0:T(8,128)(2,1)} %gather_fusion.13), kind=kCustom, calls=%fused_computation.339 | custom fusion | flops 5767168 | bytes 11534336 | tf_op jit(solution)/shard_map/scatter-add | solution.py:106
  737.5 18.2 %scatter_custom_fusion.6 = f32[6144,256]{1,0:T(8,128)} fusion(f32[6144,256]{1,0:T(8,128)} %scatter_custom_fusion.5, s32[2048]{0:T(1024)} %bitcast.307, f32[2048,256]{1,0:T(8,128)} %get-tuple-element.236, f32[2048,256]{1,0:T(8,128)S(1)} %get-tuple-element.233, bf16[2048,256]{1,0:T(8,128)(2,1)} %gather_fusion.14), kind=kCustom, calls=%fused_computation.340 | custom fusion | flops 5767168 | bytes 11534336 | tf_op jit(solution)/shard_map/scatter-add | solution.py:106
  755.7 18.2 %scatter_custom_fusion.7 = f32[6144,256]{1,0:T(8,128)} fusion(f32[6144,256]{1,0:T(8,128)} %scatter_custom_fusion.6, s32[2048]{0:T(1024)} %bitcast.303, f32[2048,256]{1,0:T(8,128)} %get-tuple-element.236, f32[2048,256]{1,0:T(8,128)S(1)} %get-tuple-element.233, bf16[2048,256]{1,0:T(8,128)(2,1)} %gather_fusion.15), kind=kCustom, calls=%fused_computation.341 | custom fusion | flops 5767168 | bytes 11534336 | tf_op jit(solution)/shard_map/scatter-add | solution.py:106
  773.8 18.2 %scatter_custom_fusion.8 = f32[6144,256]{1,0:T(8,128)} fusion(f32[6144,256]{1,0:T(8,128)} %scatter_custom_fusion.7, s32[2048]{0:T(1024)} %bitcast.299, f32[2048,256]{1,0:T(8,128)} %get-tuple-element.236, f32[2048,256]{1,0:T(8,128)S(1)} %get-tuple-element.233, bf16[2048,256]{1,0:T(8,128)(2,1)} %gather_fusion.16), kind=kCustom, calls=%fused_computation.342 | custom fusion | flops 5767168 | bytes 11534336 | tf_op jit(solution)/shard_map/scatter-add | solution.py:106
  792.0 18.2 %scatter_custom_fusion.9 = f32[6144,256]{1,0:T(8,128)} fusion(f32[6144,256]{1,0:T(8,128)} %scatter_custom_fusion.8, s32[2048]{0:T(1024)} %bitcast.295, f32[2048,256]{1,0:T(8,128)} %get-tuple-element.236, f32[2048,256]{1,0:T(8,128)S(1)} %get-tuple-element.233, bf16[2048,256]{1,0:T(8,128)(2,1)} %gather_fusion.17), kind=kCustom, calls=%fused_computation.343 | custom fusion | flops 5767168 | bytes 11534336 | tf_op jit(solution)/shard_map/scatter-add | solution.py:106
  822.1 18.7 %collective-permute-done.10 = bf16[2048,256]{1,0:T(8,128)(2,1)} collective-permute-done((bf16[2048,256]{1,0:T(8,128)(2,1)}, bf16[2048,256]{1,0:T(8,128)(2,1)}, u32[]{:S(2)}, u32[]{:S(2)}) %collective-permute-start.10) | collective-permute-done | bytes 1048608 | tf_op jit(solution)/shard_map/ppermute | solution.py:25
  840.8 15.8 %collective-permute-done.9 = bf16[2048,256]{1,0:T(8,128)(2,1)} collective-permute-done((bf16[2048,256]{1,0:T(8,128)(2,1)S(1)}, bf16[2048,256]{1,0:T(8,128)(2,1)}, u32[]{:S(2)}, u32[]{:S(2)}) %collective-permute-start.9) | collective-permute-done | bytes 1048608 | tf_op jit(solution)/shard_map/ppermute | solution.py:24
  878.6 15.9 %scatter_custom_fusion.10 = f32[6144,256]{1,0:T(8,128)} fusion(s32[2048]{0:T(1024)} %bitcast.316, f32[]{:T(128)} %constant.352.clone.1, f32[2048,256]{1,0:T(8,128)} %get-tuple-element.237, f32[2048,256]{1,0:T(8,128)S(1)} %copy-done.1, bf16[2048,256]{1,0:T(8,128)(2,1)} %gather_fusion.6), kind=kCustom, calls=%fused_computation.60 | custom fusion | flops 5767168 | bytes 11534848 | tf_op jit(solution)/shard_map/scatter-add | solution.py:106
  894.5 18.2 %scatter_custom_fusion.11 = f32[6144,256]{1,0:T(8,128)} fusion(f32[6144,256]{1,0:T(8,128)} %scatter_custom_fusion.10, s32[2048]{0:T(1024)} %bitcast.312, f32[2048,256]{1,0:T(8,128)} %get-tuple-element.237, f32[2048,256]{1,0:T(8,128)S(1)} %copy-done.1, bf16[2048,256]{1,0:T(8,128)(2,1)} %gather_fusion.7), kind=kCustom, calls=%fused_computation.344 | custom fusion | flops 5767168 | bytes 11534336 | tf_op jit(solution)/shard_map/scatter-add | solution.py:106
  912.7 18.2 %scatter_custom_fusion.12 = f32[6144,256]{1,0:T(8,128)} fusion(f32[6144,256]{1,0:T(8,128)} %scatter_custom_fusion.11, s32[2048]{0:T(1024)} %bitcast.308, f32[2048,256]{1,0:T(8,128)} %get-tuple-element.237, f32[2048,256]{1,0:T(8,128)S(1)} %copy-done.1, bf16[2048,256]{1,0:T(8,128)(2,1)} %gather_fusion.8), kind=kCustom, calls=%fused_computation.345 | custom fusion | flops 5767168 | bytes 11534336 | tf_op jit(solution)/shard_map/scatter-add | solution.py:106
  930.8 18.2 %scatter_custom_fusion.13 = f32[6144,256]{1,0:T(8,128)} fusion(f32[6144,256]{1,0:T(8,128)} %scatter_custom_fusion.12, s32[2048]{0:T(1024)} %bitcast.304, f32[2048,256]{1,0:T(8,128)} %get-tuple-element.237, f32[2048,256]{1,0:T(8,128)S(1)} %copy-done.1, bf16[2048,256]{1,0:T(8,128)(2,1)} %gather_fusion.9), kind=kCustom, calls=%fused_computation.346 | custom fusion | flops 5767168 | bytes 11534336 | tf_op jit(solution)/shard_map/scatter-add | solution.py:106
  949.0 18.2 %scatter_custom_fusion.14 = f32[6144,256]{1,0:T(8,128)} fusion(f32[6144,256]{1,0:T(8,128)} %scatter_custom_fusion.13, s32[2048]{0:T(1024)} %bitcast.300, f32[2048,256]{1,0:T(8,128)} %get-tuple-element.237, f32[2048,256]{1,0:T(8,128)S(1)} %copy-done.1, bf16[2048,256]{1,0:T(8,128)(2,1)} %gather_fusion.10), kind=kCustom, calls=%fused_computation.347 | custom fusion | flops 5767168 | bytes 11534336 | tf_op jit(solution)/shard_map/scatter-add | solution.py:106
  967.1 18.2 %scatter_custom_fusion.15 = f32[6144,256]{1,0:T(8,128)} fusion(f32[6144,256]{1,0:T(8,128)} %scatter_custom_fusion.14, s32[2048]{0:T(1024)} %bitcast.296, f32[2048,256]{1,0:T(8,128)} %get-tuple-element.237, f32[2048,256]{1,0:T(8,128)S(1)} %copy-done.1, bf16[2048,256]{1,0:T(8,128)(2,1)} %gather_fusion.11), kind=kCustom, calls=%fused_computation.348 | custom fusion | flops 5767168 | bytes 11534336 | tf_op jit(solution)/shard_map/scatter-add | solution.py:106
  1000.3 36.0 %collective-permute-done.11 = bf16[2048,256]{1,0:T(8,128)(2,1)S(1)} collective-permute-done((bf16[2048,256]{1,0:T(8,128)(2,1)S(1)}, bf16[2048,256]{1,0:T(8,128)(2,1)S(1)}, u32[]{:S(2)}, u32[]{:S(2)}) %collective-permute-start.11) | collective-permute-done | bytes 1048608 | tf_op jit(solution)/shard_map/ppermute | solution.py:24
  1037.0 10.8 fusion.27
  1063.2 15.9 %scatter_custom_fusion.16 = f32[6144,256]{1,0:T(8,128)} fusion(s32[2048]{0:T(1024)} %bitcast.317, f32[]{:T(128)} %constant.352.clone.1, f32[2048,256]{1,0:T(8,128)} %get-tuple-element.238, f32[2048,256]{1,0:T(8,128)S(1)} %copy-done, bf16[2048,256]{1,0:T(8,128)(2,1)} %gather_fusion), kind=kCustom, calls=%fused_computation.58 | custom fusion | flops 5767168 | bytes 11534848 | tf_op jit(solution)/shard_map/scatter-add | solution.py:106
  1079.2 18.2 %scatter_custom_fusion.17 = f32[6144,256]{1,0:T(8,128)} fusion(f32[6144,256]{1,0:T(8,128)} %scatter_custom_fusion.16, s32[2048]{0:T(1024)} %bitcast.313, f32[2048,256]{1,0:T(8,128)} %get-tuple-element.238, f32[2048,256]{1,0:T(8,128)S(1)} %copy-done, bf16[2048,256]{1,0:T(8,128)(2,1)} %gather_fusion.1), kind=kCustom, calls=%fused_computation.349 | custom fusion | flops 5767168 | bytes 11534336 | tf_op jit(solution)/shard_map/scatter-add | solution.py:106
  1097.3 18.2 %scatter_custom_fusion.18 = f32[6144,256]{1,0:T(8,128)} fusion(f32[6144,256]{1,0:T(8,128)} %scatter_custom_fusion.17, s32[2048]{0:T(1024)} %bitcast.309, f32[2048,256]{1,0:T(8,128)} %get-tuple-element.238, f32[2048,256]{1,0:T(8,128)S(1)} %copy-done, bf16[2048,256]{1,0:T(8,128)(2,1)} %gather_fusion.2), kind=kCustom, calls=%fused_computation.350 | custom fusion | flops 5767168 | bytes 11534336 | tf_op jit(solution)/shard_map/scatter-add | solution.py:106
  1115.5 18.2 %scatter_custom_fusion.19 = f32[6144,256]{1,0:T(8,128)} fusion(f32[6144,256]{1,0:T(8,128)} %scatter_custom_fusion.18, s32[2048]{0:T(1024)} %bitcast.305, f32[2048,256]{1,0:T(8,128)} %get-tuple-element.238, f32[2048,256]{1,0:T(8,128)S(1)} %copy-done, bf16[2048,256]{1,0:T(8,128)(2,1)} %gather_fusion.3), kind=kCustom, calls=%fused_computation.351 | custom fusion | flops 5767168 | bytes 11534336 | tf_op jit(solution)/shard_map/scatter-add | solution.py:106
  1133.6 18.3 %scatter_custom_fusion.20 = f32[6144,256]{1,0:T(8,128)} fusion(f32[6144,256]{1,0:T(8,128)} %scatter_custom_fusion.19, s32[2048]{0:T(1024)} %bitcast.301, f32[2048,256]{1,0:T(8,128)} %get-tuple-element.238, f32[2048,256]{1,0:T(8,128)S(1)} %copy-done, bf16[2048,256]{1,0:T(8,128)(2,1)} %gather_fusion.4), kind=kCustom, calls=%fused_computation.352 | custom fusion | flops 5767168 | bytes 11534336 | tf_op jit(solution)/shard_map/scatter-add | solution.py:106
  1152.0 18.2 %scatter_custom_fusion.21 = f32[6144,256]{1,0:T(8,128)} fusion(f32[6144,256]{1,0:T(8,128)} %scatter_custom_fusion.20, s32[2048]{0:T(1024)} %bitcast.297, f32[2048,256]{1,0:T(8,128)} %get-tuple-element.238, f32[2048,256]{1,0:T(8,128)S(1)} %copy-done, bf16[2048,256]{1,0:T(8,128)(2,1)} %gather_fusion.5), kind=kCustom, calls=%fused_computation.353 | custom fusion | flops 5767168 | bytes 11534336 | tf_op jit(solution)/shard_map/scatter-add | solution.py:106
  1184.6 35.1 %collective-permute-done.13 = bf16[2048,256]{1,0:T(8,128)(2,1)S(1)} collective-permute-done((bf16[2048,256]{1,0:T(8,128)(2,1)S(1)}, bf16[2048,256]{1,0:T(8,128)(2,1)S(1)}, u32[]{:S(2)}, u32[]{:S(2)}) %collective-permute-start.13) | collective-permute-done | bytes 1048608 | tf_op jit(solution)/shard_map/ppermute | solution.py:24
  1220.4 10.5 fusion.25
  1277.2 143.0 %all-reduce.5.cloned.1.call-done = f32[1156352]{0:T(1024)} async-done(((f32[1156352]{0:T(1024)}), f32[1156352]{0:T(1024)}) %all-reduce.5.cloned.1.call-update) | async-done | bytes 4625424 | tf_op jit(solution)/shard_map/psum | solution.py:230
  (557 shorter events, 375.3 us)
Async XLA Ops:
  7.2 144.1 %all-reduce.7.cloned.1.call-start = ((), (), s32[]{:S(2)}) async-start(), calls=%async_computation.6 | async-start | bytes 4628480
  8.4 145.8 %copy-start.128 = (bf16[1,78,512]{2,1,0:T(8,128)(2,1)S(1)}, bf16[1,78,512]{2,1,0:T(8,128)(2,1)}, u32[]{:S(2)}) copy-start(bf16[1,78,512]{2,1,0:T(8,128)(2,1)} %param.39) | copy-start | bytes 239620
  12.3 146.2 %copy-start.156 = (s32[512,1]{0,1:T(1,128)}, s32[512,1]{0,1:T(1,128)S(1)}, u32[]{:S(2)}) copy-start(s32[512,1]{0,1:T(1,128)S(1)} %compare_select_fusion.6) | copy-start | bytes 6148
  15.6 15.6 %all-to-all-start = ((s32[16,1,64]{2,1,0:T(1,128)}), s32[16,1,64]{2,1,0:T(1,128)S(1)}, u32[]{:S(2)}, u32[]{:S(2)}) async-start(s32[16,1,64]{2,1,0:T(1,128)} %all_to_all.18), calls=%async_computation | async-start | bytes 16384 | tf_op jit(solution)/shard_map/all_to_all | solution.py:146
  32.4 145.1 %copy-start.162 = (s32[1024]{0:T(1024)}, s32[1024]{0:T(1024)S(1)}, u32[]{:S(2)}) copy-start(s32[1024]{0:T(1024)S(1)} %eq.50) | copy-start | bytes 12292
  158.5 19.1 %all-to-all-start.1 = ((bf16[16,64,256]{2,1,0:T(8,128)(2,1)}), bf16[16,64,256]{2,1,0:T(8,128)(2,1)}, u32[]{:S(2)}, u32[]{:S(2)}) async-start(bf16[16,64,256]{2,1,0:T(8,128)(2,1)} %bitcast.10), calls=%async_computation.1 | async-start | bytes 1048576 | tf_op jit(solution)/shard_map/all_to_all | solution.py:143
  184.5 42.5 %copy-start.34 = (bf16[2048,256]{1,0:T(8,128)(2,1)}, bf16[2048,256]{1,0:T(8,128)(2,1)S(1)}, u32[]{:S(2)}) copy-start(bf16[2048,256]{1,0:T(8,128)(2,1)S(1)} %convolution_convert_fusion.3) | copy-start | bytes 3145732
  184.5 42.5 %collective-permute-start = (bf16[2048,256]{1,0:T(8,128)(2,1)S(1)}, bf16[2048,256]{1,0:T(8,128)(2,1)S(1)}, u32[]{:S(2)}, u32[]{:S(2)}) collective-permute-start(bf16[2048,256]{1,0:T(8,128)(2,1)S(1)} %convolution_convert_fusion.3), channel_id=1, source_target_pairs={{0,1},{1,2},{2,3},{3,4},{4,5},{5,6},{6,7},{7,8},{8,9},{9,10},{10,1... | collective-permute-start | bytes 3145736 | tf_op jit(solution)/shard_map/ppermute | solution.py:24
  185.1 44.0 %collective-permute-start.1 = (bf16[2048,256]{1,0:T(8,128)(2,1)S(1)}, bf16[2048,256]{1,0:T(8,128)(2,1)}, u32[]{:S(2)}, u32[]{:S(2)}) collective-permute-start(bf16[2048,256]{1,0:T(8,128)(2,1)S(1)} %convolution_convert_fusion.3), channel_id=1, source_target_pairs={{1,0},{2,1},{3,2},{4,3},{5,4},{6,5},{7,6},{8,7},{9,8},{10,9},{11,1... | collective-permute-start | bytes 3145736 | tf_op jit(solution)/shard_map/ppermute | solution.py:25
  190.4 36.6 %copy-start.148 = (s32[2048,1]{0,1:T(1,128)}, s32[2048,1]{0,1:T(1,128)S(1)}, u32[]{:S(2)}) copy-start(s32[2048,1]{0,1:T(1,128)S(1)} %get-tuple-element.214) | copy-start | bytes 24580
  190.5 36.6 %copy-start.149 = (s32[2048,1]{0,1:T(1,128)}, s32[2048,1]{0,1:T(1,128)S(1)}, u32[]{:S(2)}) copy-start(s32[2048,1]{0,1:T(1,128)S(1)} %get-tuple-element.215) | copy-start | bytes 24580
  190.5 36.6 %copy-start.150 = (s32[2048,1]{0,1:T(1,128)}, s32[2048,1]{0,1:T(1,128)S(1)}, u32[]{:S(2)}) copy-start(s32[2048,1]{0,1:T(1,128)S(1)} %get-tuple-element.216) | copy-start | bytes 24580
  190.5 36.6 %copy-start.151 = (s32[2048,1]{0,1:T(1,128)}, s32[2048,1]{0,1:T(1,128)S(1)}, u32[]{:S(2)}) copy-start(s32[2048,1]{0,1:T(1,128)S(1)} %get-tuple-element.217) | copy-start | bytes 24580
  190.5 36.6 %copy-start.152 = (s32[2048,1]{0,1:T(1,128)}, s32[2048,1]{0,1:T(1,128)S(1)}, u32[]{:S(2)}) copy-start(s32[2048,1]{0,1:T(1,128)S(1)} %get-tuple-element.218) | copy-start | bytes 24580
  192.5 103.7 %copy-start.107 = (bf16[256,256]{1,0:T(8,128)(2,1)}, bf16[256,256]{1,0:T(8,128)(2,1)S(1)}, u32[]{:S(2)}) copy-start(bf16[256,256]{1,0:T(8,128)(2,1)S(1)} %slice.654) | copy-start | bytes 393220
  192.5 104.1 %copy-start.84 = (bf16[256,256]{1,0:T(8,128)(2,1)}, bf16[256,256]{1,0:T(8,128)(2,1)S(1)}, u32[]{:S(2)}) copy-start(bf16[256,256]{1,0:T(8,128)(2,1)S(1)} %slice.656) | copy-start | bytes 393220
  193.3 109.2 %copy-start.80 = (bf16[256,256]{1,0:T(8,128)(2,1)}, bf16[256,256]{1,0:T(8,128)(2,1)S(1)}, u32[]{:S(2)}) copy-start(bf16[256,256]{1,0:T(8,128)(2,1)S(1)} %slice.661) | copy-start | bytes 393220
  303.9 42.7 %copy-start.35 = (bf16[2048,256]{1,0:T(8,128)(2,1)}, bf16[2048,256]{1,0:T(8,128)(2,1)S(1)}, u32[]{:S(2)}) copy-start(bf16[2048,256]{1,0:T(8,128)(2,1)S(1)} %convolution_convert_fusion.2) | copy-start | bytes 3145732
  303.9 42.7 %collective-permute-start.2 = (bf16[2048,256]{1,0:T(8,128)(2,1)S(1)}, bf16[2048,256]{1,0:T(8,128)(2,1)S(1)}, u32[]{:S(2)}, u32[]{:S(2)}) collective-permute-start(bf16[2048,256]{1,0:T(8,128)(2,1)S(1)} %convolution_convert_fusion.2), channel_id=1, source_target_pairs={{0,1},{1,2},{2,3},{3,4},{4,5},{5,6},{6,7},{7,8},{8,9},{9,10},{10,1... | collective-permute-start | bytes 3145736 | tf_op jit(solution)/shard_map/ppermute | solution.py:24
  305.5 48.6 %collective-permute-start.3 = (bf16[2048,256]{1,0:T(8,128)(2,1)S(1)}, bf16[2048,256]{1,0:T(8,128)(2,1)}, u32[]{:S(2)}, u32[]{:S(2)}) collective-permute-start(bf16[2048,256]{1,0:T(8,128)(2,1)S(1)} %convolution_convert_fusion.2), channel_id=1, source_target_pairs={{1,0},{2,1},{3,2},{4,3},{5,4},{6,5},{7,6},{8,7},{9,8},{10,9},{11,1... | collective-permute-start | bytes 3145736 | tf_op jit(solution)/shard_map/ppermute | solution.py:25
  310.7 110.4 %copy-start.109 = (bf16[256,256]{1,0:T(8,128)(2,1)}, bf16[256,256]{1,0:T(8,128)(2,1)S(1)}, u32[]{:S(2)}) copy-start(bf16[256,256]{1,0:T(8,128)(2,1)S(1)} %slice.666) | copy-start | bytes 393220
  310.8 110.8 %copy-start.86 = (bf16[256,256]{1,0:T(8,128)(2,1)}, bf16[256,256]{1,0:T(8,128)(2,1)S(1)}, u32[]{:S(2)}) copy-start(bf16[256,256]{1,0:T(8,128)(2,1)S(1)} %slice.668) | copy-start | bytes 393220
  311.6 115.4 %copy-start.82 = (bf16[256,256]{1,0:T(8,128)(2,1)}, bf16[256,256]{1,0:T(8,128)(2,1)S(1)}, u32[]{:S(2)}) copy-start(bf16[256,256]{1,0:T(8,128)(2,1)S(1)} %slice.673) | copy-start | bytes 393220
  428.4 44.9 %copy-start.36 = (bf16[2048,256]{1,0:T(8,128)(2,1)}, bf16[2048,256]{1,0:T(8,128)(2,1)S(1)}, u32[]{:S(2)}) copy-start(bf16[2048,256]{1,0:T(8,128)(2,1)S(1)} %convolution_convert_fusion.1) | copy-start | bytes 3145732
  428.4 44.9 %collective-permute-start.4 = (bf16[2048,256]{1,0:T(8,128)(2,1)S(1)}, bf16[2048,256]{1,0:T(8,128)(2,1)S(1)}, u32[]{:S(2)}, u32[]{:S(2)}) collective-permute-start(bf16[2048,256]{1,0:T(8,128)(2,1)S(1)} %convolution_convert_fusion.1), channel_id=1, source_target_pairs={{0,1},{1,2},{2,3},{3,4},{4,5},{5,6},{6,7},{7,8},{8,9},{9,10},{10,1... | collective-permute-start | bytes 3145736 | tf_op jit(solution)/shard_map/ppermute | solution.py:24
  428.8 46.6 %collective-permute-start.5 = (bf16[2048,256]{1,0:T(8,128)(2,1)S(1)}, bf16[2048,256]{1,0:T(8,128)(2,1)}, u32[]{:S(2)}, u32[]{:S(2)}) collective-permute-start(bf16[2048,256]{1,0:T(8,128)(2,1)S(1)} %convolution_convert_fusion.1), channel_id=1, source_target_pairs={{1,0},{2,1},{3,2},{4,3},{5,4},{6,5},{7,6},{8,7},{9,8},{10,9},{11,1... | collective-permute-start | bytes 3145736 | tf_op jit(solution)/shard_map/ppermute | solution.py:25
  434.3 98.9 %copy-start.125 = (bf16[256,256]{1,0:T(8,128)(2,1)}, bf16[256,256]{1,0:T(8,128)(2,1)S(1)}, u32[]{:S(2)}) copy-start(bf16[256,256]{1,0:T(8,128)(2,1)S(1)} %slice.675) | copy-start | bytes 393220
  434.4 105.4 %copy-start.111 = (bf16[256,256]{1,0:T(8,128)(2,1)}, bf16[256,256]{1,0:T(8,128)(2,1)S(1)}, u32[]{:S(2)}) copy-start(bf16[256,256]{1,0:T(8,128)(2,1)S(1)} %slice.678) | copy-start | bytes 393220
  434.4 105.7 %copy-start.88 = (bf16[256,256]{1,0:T(8,128)(2,1)}, bf16[256,256]{1,0:T(8,128)(2,1)S(1)}, u32[]{:S(2)}) copy-start(bf16[256,256]{1,0:T(8,128)(2,1)S(1)} %slice.680) | copy-start | bytes 393220
  546.7 20.7 %all-to-all-start.2 = ((bf16[16,64,256]{2,1,0:T(8,128)(2,1)}), bf16[16,64,256]{2,1,0:T(8,128)(2,1)}, u32[]{:S(2)}, u32[]{:S(2)}) async-start(bf16[16,64,256]{2,1,0:T(8,128)(2,1)} %bitcast.293), calls=%async_computation.2 | async-start | bytes 1048576 | tf_op jit(solution)/shard_map/all_to_all | solution.py:164
  552.8 6.5 collective-permute-start.6
  574.6 9.3 collective-permute-start.7
  655.2 6.4 collective-permute-start.8
  670.4 18.6 %all-to-all-start.3 = ((bf16[16,64,256]{2,1,0:T(8,128)(2,1)}), bf16[16,64,256]{2,1,0:T(8,128)(2,1)}, u32[]{:S(2)}, u32[]{:S(2)}) async-start(bf16[16,64,256]{2,1,0:T(8,128)(2,1)} %bitcast.287), calls=%async_computation.3 | async-start | bytes 1048576 | tf_op jit(solution)/shard_map/all_to_all | solution.py:195
  814.4 26.4 %collective-permute-start.10 = (bf16[2048,256]{1,0:T(8,128)(2,1)}, bf16[2048,256]{1,0:T(8,128)(2,1)}, u32[]{:S(2)}, u32[]{:S(2)}) collective-permute-start(bf16[2048,256]{1,0:T(8,128)(2,1)} %get-tuple-element.185), channel_id=1, source_target_pairs={{1,0},{2,1},{3,2},{4,3},{5,4},{6,5},{7,6},{8,7},{9,8},{10,9},{11,1... | collective-permute-start | bytes 3145736 | tf_op jit(solution)/shard_map/ppermute | solution.py:25
  816.9 39.7 %collective-permute-start.9 = (bf16[2048,256]{1,0:T(8,128)(2,1)S(1)}, bf16[2048,256]{1,0:T(8,128)(2,1)}, u32[]{:S(2)}, u32[]{:S(2)}) collective-permute-start(bf16[2048,256]{1,0:T(8,128)(2,1)S(1)} %get-tuple-element.184), channel_id=1, source_target_pairs={{0,1},{1,2},{2,3},{3,4},{4,5},{5,6},{6,7},{7,8},{8,9},{9,10},{10,1... | collective-permute-start | bytes 3145736 | tf_op jit(solution)/shard_map/ppermute | solution.py:24
  988.6 47.7 %collective-permute-start.11 = (bf16[2048,256]{1,0:T(8,128)(2,1)S(1)}, bf16[2048,256]{1,0:T(8,128)(2,1)S(1)}, u32[]{:S(2)}, u32[]{:S(2)}) collective-permute-start(bf16[2048,256]{1,0:T(8,128)(2,1)S(1)} %get-tuple-element.182), channel_id=1, source_target_pairs={{0,1},{1,2},{2,3},{3,4},{4,5},{5,6},{6,7},{7,8},{8,9},{9,10},{10,1... | collective-permute-start | bytes 3145736 | tf_op jit(solution)/shard_map/ppermute | solution.py:24
  991.2 45.8 %collective-permute-start.12 = (bf16[2048,256]{1,0:T(8,128)(2,1)S(1)}, bf16[2048,256]{1,0:T(8,128)(2,1)S(1)}, u32[]{:S(2)}, u32[]{:S(2)}) collective-permute-start(bf16[2048,256]{1,0:T(8,128)(2,1)S(1)} %get-tuple-element.183), channel_id=1, source_target_pairs={{1,0},{2,1},{3,2},{4,3},{5,4},{6,5},{7,6},{8,7},{9,8},{10,9},{11,1... | collective-permute-start | bytes 3145736 | tf_op jit(solution)/shard_map/ppermute | solution.py:25
  1000.2 47.5 %copy-start.78 = (f32[5,256,256]{2,1,0:T(8,128)}, f32[5,256,256]{2,1,0:T(8,128)S(1)}, u32[]{:S(2)}) copy-start(f32[5,256,256]{2,1,0:T(8,128)S(1)} %fusion.35) | copy-start | bytes 3932164
  1000.3 47.5 %copy-start.7 = (bf16[2048,256]{1,0:T(8,128)(2,1)S(1)}, bf16[2048,256]{1,0:T(8,128)(2,1)}, u32[]{:S(2)}) copy-start(bf16[2048,256]{1,0:T(8,128)(2,1)} %copy-done.5) | copy-start | bytes 3145732
  1173.4 46.3 %collective-permute-start.13 = (bf16[2048,256]{1,0:T(8,128)(2,1)S(1)}, bf16[2048,256]{1,0:T(8,128)(2,1)S(1)}, u32[]{:S(2)}, u32[]{:S(2)}) collective-permute-start(bf16[2048,256]{1,0:T(8,128)(2,1)S(1)} %get-tuple-element.180), channel_id=1, source_target_pairs={{0,1},{1,2},{2,3},{3,4},{4,5},{5,6},{6,7},{7,8},{8,9},{9,10},{10,1... | collective-permute-start | bytes 3145736 | tf_op jit(solution)/shard_map/ppermute | solution.py:24
  1175.2 45.2 %collective-permute-start.14 = (bf16[2048,256]{1,0:T(8,128)(2,1)S(1)}, bf16[2048,256]{1,0:T(8,128)(2,1)S(1)}, u32[]{:S(2)}, u32[]{:S(2)}) collective-permute-start(bf16[2048,256]{1,0:T(8,128)(2,1)S(1)} %get-tuple-element.181), channel_id=1, source_target_pairs={{1,0},{2,1},{3,2},{4,3},{5,4},{6,5},{7,6},{8,7},{9,8},{10,9},{11,1... | collective-permute-start | bytes 3145736 | tf_op jit(solution)/shard_map/ppermute | solution.py:25
  1184.6 46.4 %copy-start.4 = (bf16[2048,256]{1,0:T(8,128)(2,1)S(1)}, bf16[2048,256]{1,0:T(8,128)(2,1)}, u32[]{:S(2)}) copy-start(bf16[2048,256]{1,0:T(8,128)(2,1)} %copy-done.2) | copy-start | bytes 3145732
  1239.5 20.8 %all-to-all-start.4 = ((bf16[16,64,256]{2,1,0:T(8,128)(2,1)}), bf16[16,64,256]{2,1,0:T(8,128)(2,1)S(1)}, u32[]{:S(2)}, u32[]{:S(2)}) async-start(bf16[16,64,256]{2,1,0:T(8,128)(2,1)} %bitcast.28), calls=%async_computation.4 | async-start | bytes 1048576 | tf_op jit(solution)/shard_map/all_to_all | solution.py:212
  1245.5 174.7 %all-reduce.5.cloned.1.call-start = ((), (), s32[]{:S(2)}) async-start(), calls=%async_computation.5 | async-start | bytes 9256960 | tf_op jit(solution)/shard_map/psum | solution.py:230
  1277.2 147.3 %copy-start.103 = (f32[36136]{0:T(1024)S(1)}, f32[36136]{0:T(1024)}, u32[]{:S(2)}) copy-start(f32[36136]{0:T(1024)} %param.36) | copy-start | bytes 433636
  1277.2 147.3 %copy-start.134 = (f32[36136]{0:T(1024)S(1)}, f32[36136]{0:T(1024)}, u32[]{:S(2)}) copy-start(f32[36136]{0:T(1024)} %param.37) | copy-start | bytes 433636
  1277.2 147.3 %copy-start.135 = (f32[36136]{0:T(1024)S(1)}, f32[36136]{0:T(1024)}, u32[]{:S(2)}) copy-start(f32[36136]{0:T(1024)} %param.38) | copy-start | bytes 433636
  (148 other events, 745.5 us)
Sparse Core Ops, SparseCore 0:
  13.6 137.6 all-reduce.6
  1276.5 143.6 all-reduce.4
where the time goes:
time: 1450 us; the launch traced here: 1430 us
  waiting for transfers between devices  526 us (36%)
  other arithmetic  393 us (27%)
  local copies, waits for them, and re-layouts  277 us (19%)
  matrix products  102 us (7%)
  starting transfers between devices  70.4 us (5%)
  blocking collectives  47.1 us (3%)
  between operations  19.7 us (1%)
    scatter-add x18, other arithmetic, round_backward(): grad_pad = grad_pad.at[places[:, edge]].add(grad_edge)  320 us
    ppermute x6, waiting for transfers between devices, extended(): before = lax.ppermute(last, axis, up)  194 us
    gather x18, local copies, waits for them, and re-layouts, edge_inputs(): return padded[places[:, edge]].astype(jnp.float32) + dest  169 us
    psum x1, waiting for transfers between devices, shards(): summed = lax.psum(flat, ('dp', 'space'))  143 us
    unnamed x3, waiting for transfers between devices  119 us
    dot_general x59, matrix products, inner(): lax.dot_general(left, right, (((left_dim,), (right_dim,)), ((), ())), pre...  102 us
    unnamed x362, local copies, waits for them, and re-layouts  58.1 us
    psum x1, blocking collectives, shards(): total, count = lax.psum((local_total, jnp.sum(counted)), ('dp', 'space'))  47.1 us
  transfers between devices with their start and end apart: 22, of which 21 were waited for; matrix products, arithmetic and copies ran while one was open for 4% of the time, Pallas kernels for 0%

commit v1 on v0

v1 whole, which is shorter than its diff:
```python
import math

import jax
import jax.numpy as jnp
from jax import lax
from jax.experimental import pallas as pl
from jax.experimental.pallas import tpu as pltpu
from jax.sharding import PartitionSpec as P

D = 256
HALF = 128
CH = 78
ROUNDS = 3
K = 6
ROWW = 360
NEAR = 358
STEP = 10
H = 2048
TABLES = 4
UNROLL = 32
ALL = ("dp", "space")
LIMIT = pltpu.CompilerParams(vmem_limit_bytes=56 * 2**20)


def inner(left, right, left_dim, right_dim):
    return lax.dot_general(
        left, right, (((left_dim,), (right_dim,)), ((), ())), preferred_element_type=jnp.float32
    )


def sigmoid(value):
    return 0.5 * jnp.tanh(0.5 * value) + 0.5


def silu(value):
    return value * sigmoid(value)


def slope(value):
    sigma = sigmoid(value)
    return sigma * (1.0 + value * (1.0 - sigma))


def shifted(shard, axis, by):
    peers = lax.axis_size(axis)
    pairs = [(i, i + by) for i in range(peers) if 0 <= i + by < peers]
    return lax.ppermute(shard, axis, pairs)


def halo(last, initial):
    peers = lax.axis_size("space")
    up = [(i, (i + 1) % peers) for i in range(peers)]
    down = [(j, i) for i, j in up]
    return lax.ppermute(last, "space", up), lax.ppermute(initial, "space", down)


def pieces_of(total, peers):
    share = total // peers
    starts = [share * d // D for d in range(peers)]
    counts = [-(-share * (d + 1) // D) - starts[d] for d in range(peers)]
    shared = [share * d % D != 0 for d in range(peers)]
    height = -(-max(counts) // 16) * 16
    return starts, counts, shared, height


def parts_of():
    return [CH, D, D, CH, ROUNDS * 5 * D, 3 + 2 * ROUNDS]


def spread_rows(gathered, total):
    peers, height, _ = gathered.shape
    starts, counts, shared, _ = pieces_of(total, peers)
    rows = -(-total // D)
    sizes = parts_of()

    def body(source, *refs):
        outs, buffer = refs[:-1], refs[-1]
        for d in range(peers):
            piece = source[d].astype(jnp.float32)
            at, count = starts[d], counts[d]
            if shared[d]:
                buffer[at : at + 1, :] = buffer[at : at + 1, :] + piece[:1]
                buffer[at + 1 : at + count, :] = piece[1:count]
            else:
                buffer[at : at + count, :] = piece[:count]
        start = 0
        for out, size in zip(outs, sizes):
            out[...] = buffer[start : start + size, :].astype(out.dtype)
            start = start + size

    kinds = [jnp.bfloat16] * 5 + [jnp.float32]
    return pl.pallas_call(
        body,
        out_shape=[jax.ShapeDtypeStruct((size, D), kind) for size, kind in zip(sizes, kinds)],
        scratch_shapes=[pltpu.VMEM((-(-rows // 8) * 8 + 8, D), jnp.float32)],
        compiler_params=LIMIT,
        name="spread_rows",
    )(gathered)


def collect_rows(parts, total, peers):
    starts, counts, shared, height = pieces_of(total, peers)
    rows = -(-total // D)
    used = sum(part.shape[0] for part in parts)

    def body(*refs):
        sources, out, buffer = refs[:-2], refs[-2], refs[-1]
        start = 0
        for source in sources:
            size = source.shape[0]
            buffer[start : start + size, :] = source[...]
            start = start + size
        if buffer.shape[0] > start:
            buffer[start:, :] = jnp.zeros((buffer.shape[0] - start, D), jnp.float32)
        for d in range(peers):
            out[d] = buffer[starts[d] : starts[d] + height, :]

    return pl.pallas_call(
        body,
        out_shape=jax.ShapeDtypeStruct((peers, height, D), jnp.float32),
        scratch_shapes=[pltpu.VMEM((-(-max(rows, used) // 8) * 8 + height + 8, D), jnp.float32)],
        compiler_params=LIMIT,
        name="collect_rows",
    )(*parts)


def gather_rows(index, before, own, after):
    edges = index.shape[0]
    chunk = 1024
    spans = [before.shape[0], own.shape[0], after.shape[0]]

    def body(index_ref, before_ref, own_ref, after_ref, out_ref, table, sems):
        step = pl.program_id(0)

        @pl.when(step == 0)
        def _():
            copies = []
            start = 0
            for n, (source, span) in enumerate(zip((before_ref, own_ref, after_ref), spans)):
                copies.append(
                    pltpu.make_async_copy(source, table.at[pl.ds(start, span)], sems.at[n])
                )
                start = start + span
            for copy in copies:
                copy.start()
            for copy in copies:
                copy.wait()

        def some(i, carry):
            at = i * UNROLL
            base = step * chunk + at
            rows = [table[index_ref[base + u]] for u in range(UNROLL)]
            for u in range(UNROLL):
                out_ref[at + u] = rows[u]
            return carry

        lax.fori_loop(0, chunk // UNROLL, some, 0)

    return pl.pallas_call(
        body,
        grid_spec=pltpu.PrefetchScalarGridSpec(
            num_scalar_prefetch=1,
            grid=(edges // chunk,),
            in_specs=[pl.BlockSpec(memory_space=pl.ANY)] * 3,
            out_specs=pl.BlockSpec((chunk, 2, HALF), lambda i, *_: (i, 0, 0)),
            scratch_shapes=[
                pltpu.VMEM((sum(spans), 2, HALF), own.dtype),
                pltpu.SemaphoreType.DMA((3,)),
            ],
        ),
        out_shape=jax.ShapeDtypeStruct((edges, 2, HALF), own.dtype),
        compiler_params=LIMIT,
        name="gather_rows",
    )(index, before, own, after)


def weave(ref, value):
    rows = value.shape[0]
    ref[pl.ds(0, rows, stride=2), :] = value[:, :HALF]
    ref[pl.ds(1, rows, stride=2), :] = value[:, HALF:]


def unweave(ref):
    rows = ref.shape[0] // 2
    return ref[pl.ds(0, rows, stride=2), :], ref[pl.ds(1, rows, stride=2), :]


def whole(shape):
    return pl.BlockSpec(shape, lambda *_: (0,) * len(shape))


def round_forward(mesh, edges, mats, bias, following):
    blocks = mesh.shape[0]
    tile = 256
    more = following is not None

    def body(*refs):
        if more:
            (mesh_ref, edge_ref, mats_ref, bias_ref, next_ref, new_ref, uin_ref, agg_ref, sent_ref, wide) = refs
        else:
            (mesh_ref, edge_ref, mats_ref, bias_ref, new_ref, uin_ref, agg_ref, wide) = refs
        mesh_in = mesh_ref[...]
        lowered = mesh_in.astype(jnp.bfloat16)
        weave(wide, inner(lowered, mats_ref[1], 1, 0) + bias_ref[0:1, :])
        dest = wide[...]
        total = jnp.zeros(dest.shape, jnp.float32)
        for edge in range(K):
            total = total + silu(edge_ref[edge].astype(jnp.float32) + dest)
        wide[...] = total * (1.0 / K)
        first, second = unweave(wide)
        first, second = first.astype(jnp.bfloat16), second.astype(jnp.bfloat16)
        agg_ref[:, :HALF] = first
        agg_ref[:, HALF:] = second
        update_in = (
            inner(first, mats_ref[2, :HALF, :], 1, 0)
            + inner(second, mats_ref[2, HALF:, :], 1, 0)
            + inner(lowered, mats_ref[3], 1, 0)
            + bias_ref[1:2, :]
        )
        uin_ref[...] = update_in
        update = silu(update_in).astype(jnp.bfloat16)
        new = mesh_in + inner(update, mats_ref[4], 1, 0)
        new_ref[...] = new
        if more:
            weave(wide, inner(new.astype(jnp.bfloat16), next_ref[...], 1, 0))
            sent_ref[...] = wide[...].astype(jnp.bfloat16)

    rows = pl.BlockSpec((tile, D), lambda i: (i, 0))
    woven = pl.BlockSpec((2 * tile, HALF), lambda i: (i, 0))
    ins = [rows, pl.BlockSpec((K, 2 * tile, HALF), lambda i: (0, i, 0)), whole(mats.shape), whole(bias.shape)]
    outs = [rows, rows, rows]
    shapes = [
        jax.ShapeDtypeStruct((blocks, D), jnp.float32),
        jax.ShapeDtypeStruct((blocks, D), jnp.float32),
        jax.ShapeDtypeStruct((blocks, D), jnp.bfloat16),
    ]
    args = [mesh, edges, mats, bias]
    if more:
        ins.append(whole(following.shape))
        outs.append(woven)
        shapes.append(jax.ShapeDtypeStruct((2 * blocks, HALF), jnp.bfloat16))
        args.append(following)
    return pl.pallas_call(
        body,
        grid=(blocks // tile,),
        in_specs=ins,
        out_specs=outs,
        out_shape=shapes,
        scratch_shapes=[pltpu.VMEM((2 * tile, HALF), jnp.float32)],
        compiler_params=LIMIT,
        name="round_forward",
    )(*args)


def edges_backward(index, grad_mesh, mesh, uin, edges, mats, bias):
    blocks = mesh.shape[0]
    tile = 256
    steps = blocks // tile
    reach = 2 * (blocks + 2 * H)

    def body(
        index_ref, grad_ref, mesh_ref, uin_ref, edge_ref, mats_ref, bias_ref,
        guin_ref, low_ref, before_ref, own_ref, after_ref, wide, wider, flows, *tables,
    ):
        step = pl.program_id(0)

        @pl.when(step == 0)
        def _():
            for table in tables:
                table[...] = jnp.zeros(table.shape, jnp.float32)

        grad_out = grad_ref[...].astype(jnp.bfloat16)
        grad_update = inner(grad_out, mats_ref[4], 1, 1)
        grad_uin = (grad_update * slope(uin_ref[...])).astype(jnp.bfloat16)
        guin_ref[...] = grad_uin
        weave(wide, inner(grad_uin, mats_ref[2], 1, 1) * (1.0 / K))
        lowered = mesh_ref[...].astype(jnp.bfloat16)
        weave(wider, inner(lowered, mats_ref[1], 1, 0) + bias_ref[0:1, :])
        grad_agg = wide[...]
        dest = wider[...]
        grad_dest = jnp.zeros(dest.shape, jnp.float32)
        for edge in range(K):
            flow = grad_agg * slope(edge_ref[edge].astype(jnp.float32) + dest)
            grad_dest = grad_dest + flow
            flows[edge * 2 * tile : (edge + 1) * 2 * tile, :] = flow
        wide[...] = grad_dest
        first, second = unweave(wide)
        low_ref[:, :HALF] = first.astype(jnp.bfloat16)
        low_ref[:, HALF:] = second.astype(jnp.bfloat16)
        for edge in range(K):

            def some(i, carry):
                at = i * UNROLL
                base = edge * blocks + step * tile + at
                for first in range(0, UNROLL, TABLES):
                    spots, rows, sums = [], [], []
                    for u in range(first, first + TABLES):
                        spots.append(pl.multiple_of(index_ref[base + u] * 2, 2))
                        spot = pl.multiple_of(2 * (edge * tile + at + u), 2)
                        rows.append(flows[pl.ds(spot, 2), :])
                    for u in range(TABLES):
                        sums.append(tables[u][pl.ds(spots[u], 2), :] + rows[u])
                    for u in range(TABLES):
                        tables[u][pl.ds(spots[u], 2), :] = sums[u]
                return carry

            lax.fori_loop(0, tile // UNROLL, some, 0)

        @pl.when(step == steps - 1)
        def _():
            def summed(start, size):
                value = tables[0][start : start + size, :]
                for table in tables[1:]:
                    value = value + table[start : start + size, :]
                return value

            before_ref[...] = summed(0, 2 * H).astype(jnp.bfloat16)
            own_ref[...] = summed(2 * H, 2 * blocks)
            after_ref[...] = summed(2 * H + 2 * blocks, 2 * H).astype(jnp.bfloat16)

    rows = pl.BlockSpec((tile, D), lambda i, *_: (i, 0))
    return pl.pallas_call(
        body,
        grid_spec=pltpu.PrefetchScalarGridSpec(
            num_scalar_prefetch=1,
            grid=(steps,),
            in_specs=[
                rows, rows, rows,
                pl.BlockSpec((K, 2 * tile, HALF), lambda i, *_: (0, i, 0)),
                whole(mats.shape), whole(bias.shape),
            ],
            out_specs=[
                rows, rows,
                whole((2 * H, HALF)), whole((2 * blocks, HALF)), whole((2 * H, HALF)),
            ],
            scratch_shapes=[
                pltpu.VMEM((2 * tile, HALF), jnp.float32),
                pltpu.VMEM((2 * tile, HALF), jnp.float32),
                pltpu.VMEM((2 * tile * K, HALF), jnp.float32),
            ]
            + [pltpu.VMEM((reach, HALF), jnp.float32)] * TABLES,
        ),
        out_shape=[
            jax.ShapeDtypeStruct((blocks, D), jnp.bfloat16),
            jax.ShapeDtypeStruct((blocks, D), jnp.bfloat16),
            jax.ShapeDtypeStruct((2 * H, HALF), jnp.bfloat16),
            jax.ShapeDtypeStruct((2 * blocks, HALF), jnp.float32),
            jax.ShapeDtypeStruct((2 * H, HALF), jnp.bfloat16),
        ],
        compiler_params=LIMIT,
        name="edges_backward",
    )(index, grad_mesh, mesh, uin, edges, mats, bias)


def round_backward(grad_mesh, own, first, last, grad_uin, dest_low, mats):
    blocks = grad_mesh.shape[0]
    tile = 256

    def body(grad_ref, own_ref, first_ref, last_ref, guin_ref, dest_ref, mats_ref, new_ref, sent_ref, wide):
        wide[...] = (
            own_ref[...] + first_ref[...].astype(jnp.float32) + last_ref[...].astype(jnp.float32)
        )
        one, two = unweave(wide)
        one, two = one.astype(jnp.bfloat16), two.astype(jnp.bfloat16)
        sent_ref[:, :HALF] = one
        sent_ref[:, HALF:] = two
        new_ref[...] = (
            grad_ref[...]
            + inner(guin_ref[...], mats_ref[3], 1, 1)
            + inner(dest_ref[...], mats_ref[1], 1, 1)
            + inner(one, mats_ref[0, :, :HALF], 1, 1)
            + inner(two, mats_ref[0, :, HALF:], 1, 1)
        )

    rows = pl.BlockSpec((tile, D), lambda i: (i, 0))
    woven = pl.BlockSpec((2 * tile, HALF), lambda i: (i, 0))
    return pl.pallas_call(
        body,
        grid=(blocks // tile,),
        in_specs=[rows, woven, woven, woven, rows, rows, whole(mats.shape)],
        out_specs=[rows, rows],
        out_shape=[
            jax.ShapeDtypeStruct((blocks, D), jnp.float32),
            jax.ShapeDtypeStruct((blocks, D), jnp.bfloat16),
        ],
        scratch_shapes=[pltpu.VMEM((2 * tile, HALF), jnp.float32)],
        compiler_params=LIMIT,
        name="round_backward",
    )(grad_mesh, own, first, last, grad_uin, dest_low, mats)


def shards(master, moment1, moment2, inputs, targets, valid, owner, slot, neighbours, partner):
    bands = lax.axis_size("space")
    band = lax.axis_index("space")
    peers = lax.axis_size(ALL)
    place = lax.axis_index(ALL)
    shard = master.shape[0]
    total_size = shard * peers
    height = pieces_of(total_size, peers)[3]
    offset = lax.rem(lax.rem(shard, D) * place, D)
    piece = lax.dynamic_update_slice_in_dim(
        jnp.zeros((height * D,), jnp.bfloat16), master.astype(jnp.bfloat16), offset, 0
    )
    everything = lax.all_gather(piece.reshape(height, D), ALL, axis=0, tiled=True)
    w_in, w_node, w_dec, w_out, w_round, biases = spread_rows(
        everything.reshape(peers, height, D), total_size
    )
    w_out = w_out.reshape(D, CH)
    w_round = w_round.reshape(ROUNDS, 5, D, D)
    b_head = biases[:3]
    b_round = biases[3:].reshape(ROUNDS, 2, D)
    state_in = inputs[0]
    wanted = targets[0].astype(jnp.float32)
    counted = valid[0].astype(jnp.float32)
    points = state_in.shape[1]
    blocks = neighbours.shape[0]
    count = lax.psum(jnp.sum(counted), ALL)
    capacity = max(2, 2 * points // bands)
    target_band = owner[0, :, 0]
    hits = (target_band[:, None] == jnp.arange(bands, dtype=jnp.int32)[None, :]).astype(jnp.int32)
    ranks = jnp.sum(jnp.cumsum(hits, 0) * hits, 1) - 1
    places_out = target_band * capacity + ranks
    enc_in = inner(state_in, w_in, 0, 0) + b_head[0]
    encoded = jax.nn.silu(enc_in).astype(jnp.bfloat16)
    outbox = jnp.zeros((bands * capacity, D), jnp.bfloat16).at[places_out].set(encoded)
    labels = jnp.full((bands * capacity,), -1, jnp.int32).at[places_out].set(slot[0])
    arrived, arrived_ids = (
        lax.all_to_all(
            outbox.reshape(bands, capacity, D), "space", split_axis=0, concat_axis=0, tiled=True
        ),
        lax.all_to_all(
            labels.reshape(bands, capacity), "space", split_axis=0, concat_axis=0, tiled=True
        ),
    )
    chooser = (
        arrived_ids.reshape(-1)[:, None] == jnp.arange(blocks, dtype=jnp.int32)[None, :]
    ).astype(jnp.bfloat16)
    gathered = inner(chooser, arrived.reshape(-1, D), 0, 0).astype(jnp.bfloat16)
    node_in = inner(gathered, w_node, 1, 0) + b_head[1]
    mesh = jax.nn.silu(node_in)
    index = ((neighbours - band * blocks + H) % (blocks * bands)).T.reshape(-1)
    kept = []
    sent = inner(mesh.astype(jnp.bfloat16), w_round[0, 0], 1, 0).astype(jnp.bfloat16)
    sent = sent.reshape(2 * blocks, HALF)
    for layer in range(ROUNDS):
        before, after = halo(sent[2 * (blocks - H) :], sent[: 2 * H])
        edges = gather_rows(
            index,
            before.reshape(H, 2, HALF),
            sent.reshape(blocks, 2, HALF),
            after.reshape(H, 2, HALF),
        ).reshape(K, 2 * blocks, HALF)
        following = w_round[layer + 1, 0] if layer + 1 < ROUNDS else None
        new, uin, agg, *rest = round_forward(mesh, edges, w_round[layer], b_round[layer], following)
        kept.append((mesh, edges, uin, agg))
        mesh = new
        sent = rest[0] if rest else None
    reply = inner(chooser, mesh.astype(jnp.bfloat16), 1, 0).astype(jnp.bfloat16)
    returned = lax.all_to_all(
        reply.reshape(bands, capacity, D), "space", split_axis=0, concat_axis=0, tiled=True
    )
    fetched = returned.reshape(-1, D)[places_out]
    dec_in = inner(fetched, w_dec, 1, 0) + b_head[2]
    decoded = jax.nn.silu(dec_in).astype(jnp.bfloat16)
    err = state_in.astype(jnp.float32) + inner(w_out, decoded, 0, 1) - wanted
    head_err, head_valid = (
        shifted(err[:, :ROWW].astype(jnp.bfloat16), "space", -1).astype(jnp.float32),
        shifted(counted[:, :ROWW].astype(jnp.bfloat16), "space", -1).astype(jnp.float32),
    )
    wide_err = jnp.concatenate([err, head_err], 1)
    wide_valid = jnp.concatenate([counted, head_valid], 1)
    ahead = partner - band * points - jnp.arange(points, dtype=jnp.int32)
    picks = [(ahead == by)[None, :] for by in range(NEAR, ROWW + 1)]
    err_far = err
    valid_far = counted
    for by, pick in zip(range(NEAR, ROWW + 1), picks):
        err_far = jnp.where(pick, wide_err[:, by : by + points], err_far)
        valid_far = jnp.where(pick, wide_valid[:, by : by + points], valid_far)
    gap = err - err_far
    local_total = jnp.sum(counted * err * err) + 0.5 * jnp.sum(counted * valid_far * gap * gap)
    total = lax.psum(local_total, ALL)
    paired = counted * valid_far * gap / count
    grad_err = 2.0 * counted * err / count + paired
    grad_wide = jnp.zeros(wide_err.shape, jnp.float32)
    for by, pick in zip(range(NEAR, ROWW + 1), picks):
        grad_wide = grad_wide - jnp.pad(
            jnp.where(pick, paired, 0.0), ((0, 0), (by, ROWW - by))
        )
    carried = shifted(grad_wide[:, points:].astype(jnp.bfloat16), "space", 1).astype(jnp.float32)
    stays = jnp.where((ahead == 0)[None, :], paired, 0.0)
    grad_pred = (
        grad_err - stays + grad_wide[:, :points] + jnp.pad(carried, ((0, 0), (0, points - ROWW)))
    )
    grad_branch = grad_pred.astype(jnp.bfloat16)
    grad_wout = inner(decoded, grad_branch, 0, 1)
    grad_dec = (inner(grad_branch, w_out, 0, 1) * slope(dec_in)).astype(jnp.bfloat16)
    grad_bdec = jnp.sum(grad_dec.astype(jnp.float32), 0)
    grad_wdec = inner(fetched, grad_dec, 0, 0)
    grad_fetched = inner(grad_dec, w_dec, 1, 1).astype(jnp.bfloat16)
    backbox = jnp.zeros((bands * capacity, D), jnp.bfloat16).at[places_out].set(grad_fetched)
    landed = lax.all_to_all(
        backbox.reshape(bands, capacity, D), "space", split_axis=0, concat_axis=0, tiled=True
    )
    grad_mesh = inner(chooser, landed.reshape(-1, D), 0, 0)
    mats_grads = [None] * (5 * ROUNDS)
    bias_grads = [None] * (2 * ROUNDS)
    for layer in reversed(range(ROUNDS)):
        old, edges, uin, agg = kept[layer]
        mats = w_round[layer]
        grad_uin, dest_low, to_before, own, to_after = edges_backward(
            index, grad_mesh, old, uin, edges, mats, b_round[layer]
        )
        from_before, from_after = halo(to_after, to_before)
        lowered = old.astype(jnp.bfloat16)
        grad_out = grad_mesh.astype(jnp.bfloat16)
        update = silu(uin).astype(jnp.bfloat16)
        grads = [
            None,
            inner(lowered, dest_low, 0, 0),
            inner(agg, grad_uin, 0, 0),
            inner(lowered, grad_uin, 0, 0),
            inner(update, grad_out, 0, 0),
        ]
        bias_grads[2 * layer] = jnp.sum(dest_low.astype(jnp.float32), 0, keepdims=True)
        bias_grads[2 * layer + 1] = jnp.sum(grad_uin.astype(jnp.float32), 0, keepdims=True)
        grad_mesh, sent_low = round_backward(
            grad_mesh, own, from_before, from_after, grad_uin, dest_low, mats
        )
        grads[0] = inner(lowered, sent_low, 0, 0)
        mats_grads[5 * layer : 5 * layer + 5] = grads
    grad_node = (grad_mesh * slope(node_in)).astype(jnp.bfloat16)
    grad_bnode = jnp.sum(grad_node.astype(jnp.float32), 0)
    grad_wnode = inner(gathered, grad_node, 0, 0)
    grad_gathered = inner(grad_node, w_node, 1, 1).astype(jnp.bfloat16)
    sendback = inner(chooser, grad_gathered, 1, 0).astype(jnp.bfloat16)
    homeward = lax.all_to_all(
        sendback.reshape(bands, capacity, D), "space", split_axis=0, concat_axis=0, tiled=True
    )
    grad_encoded = homeward.reshape(-1, D)[places_out].astype(jnp.float32)
    grad_enc = (grad_encoded * slope(enc_in)).astype(jnp.bfloat16)
    grad_bin = jnp.sum(grad_enc.astype(jnp.float32), 0)
    grad_win = inner(state_in, grad_enc, 1, 0)
    parts = [grad_win, grad_wnode, grad_wdec, grad_wout.reshape(CH, D)]
    parts = parts + mats_grads
    parts.append(jnp.concatenate([jnp.stack([grad_bin, grad_bnode, grad_bdec])] + bias_grads, 0))
    packed = collect_rows(parts, total_size, peers)
    summed = lax.psum_scatter(
        packed.reshape(peers * height, D), ALL, scatter_dimension=0, tiled=True
    )
    mine = lax.dynamic_slice_in_dim(summed.reshape(-1), offset, shard)
    norm = jnp.sqrt(lax.psum(jnp.sum(mine * mine), ALL))
    clipped = mine * jnp.minimum(1.0, 0.05 / norm)
    first = 0.9 * moment1 + 0.1 * clipped
    second = 0.999 * moment2 + 0.001 * clipped * clipped
    first_hat = first / (1.0 - 0.9**STEP)
    second_hat = second / (1.0 - 0.999**STEP)
    updated = master - 0.1 * (first_hat / (jnp.sqrt(second_hat) + 1e-08) + 0.1 * master)
    return (
        total.reshape(1),
        count.reshape(1),
        norm.reshape(1),
        updated,
        first,
        second,
        updated.astype(jnp.bfloat16),
        mesh.reshape(1, blocks, D),
        grad_mesh.reshape(1, blocks, D),
        grad_pred.reshape(1, grad_pred.shape[0], points),
    )


def solution(mesh):
    return jax.shard_map(
        shards,
        mesh=mesh,
        in_specs=(
            P(("dp", "space")),
            P(("dp", "space")),
            P(("dp", "space")),
            P("dp", None, "space"),
            P("dp", None, "space"),
            P("dp", None, "space"),
            P("dp", "space", None),
            P("dp", "space"),
            P("space", None),
            P("space"),
        ),
        out_specs=(
            P(),
            P(),
            P(),
            P(("dp", "space")),
            P(("dp", "space")),
            P(("dp", "space")),
            P(("dp", "space")),
            P("dp", "space", None),
            P("dp", "space", None),
            P("dp", None, "space"),
        ),
        check_vma=False,
    )
```

time: 1450 us -> 920 us (0.63)
  other arithmetic: 393 us -> 15.4 us
  local copies, waits for them, and re-layouts: 277 us -> 41.7 us
  Pallas kernels: 0 us -> 217 us
  waiting for transfers between devices: 526 us -> 418 us
  matrix products: 102 us -> 47.4 us
  blocking collectives: 47.1 us -> 82.4 us
    scatter-add x19 -> x0, other arithmetic: 324 us -> none  [the longest x18 320 us: round_backward(): grad_pad = grad_pad.at[places[:, edge]].add(grad_edge)]
    pallas_call x0 -> x14, Pallas kernels: none -> 217 us  [the longest x3 99.3 us: edges_backward(): pl.pallas_call(body, grid_spec=pltpu.PrefetchScalarGridSpec(num_scalar_pr...]
    gather x22 -> x0, local copies, waits for them, and re-layouts: 178 us -> none  [the longest x18 169 us: edge_inputs(): return padded[places[:, edge]].astype(jnp.float32) + dest]
    psum x1 -> x0, waiting for transfers between devices: 143 us -> none  [shards(): summed = lax.psum(flat, ('dp', 'space'))]
    unnamed x3 -> x2, waiting for transfers between devices: 119 us -> 0.03 us
    reduce_scatter x0 -> x1, waiting for transfers between devices: none -> 103 us  [shards(): lax.psum_scatter(packed.reshape(peers * height, D), ALL, scatter_dimensio...]
    dot_general x59 -> x30, matrix products: 102 us -> 47.4 us  [inner(): lax.dot_general(left, right, (((left_dim,), (right_dim,)), ((), ())), pre...]
    all_gather x0 -> x1, waiting for transfers between devices: none -> 46.6 us  [shards(): lax.all_gather(piece.reshape(height, D), ALL, axis=0, tiled=True)]
  transfers between devices with their start and end apart: 22 -> 22, of which waited for: 21 -> 19; matrix products, arithmetic and copies ran while one was open for 4% -> 6% of each run, Pallas kernels for 0% -> 0%
where the time goes in v1:
time: 920 us; the launch traced here: 909 us
  waiting for transfers between devices  418 us (45%)
  Pallas kernels  217 us (24%)
  blocking collectives  82.4 us (9%)
  starting transfers between devices  68.7 us (7%)
  matrix products  47.4 us (5%)
  local copies, waits for them, and re-layouts  41.7 us (5%)
  between operations  18.2 us (2%)
  other arithmetic  15.4 us (2%)
    ppermute x6, waiting for transfers between devices, halo(): lax.ppermute(last, 'space', up)  150 us
    reduce_scatter x1, waiting for transfers between devices, shards(): lax.psum_scatter(packed.reshape(peers * height, D), ALL, scatter_dimensio...  103 us
    pallas_call x3, Pallas kernels, edges_backward(): pl.pallas_call(body, grid_spec=pltpu.PrefetchScalarGridSpec(num_scalar_pr...  99.3 us
    ppermute x6, waiting for transfers between devices, halo(): lax.ppermute(initial, 'space', down)  72.8 us
    pallas_call x3, Pallas kernels, gather_rows(): pl.pallas_call(body, grid_spec=pltpu.PrefetchScalarGridSpec(num_scalar_pr...  48.3 us
    dot_general x30, matrix products, inner(): lax.dot_general(left, right, (((left_dim,), (right_dim,)), ((), ())), pre...  47.4 us
    all_gather x1, waiting for transfers between devices, shards(): lax.all_gather(piece.reshape(height, D), ALL, axis=0, tiled=True)  46.6 us
    psum x1, blocking collectives, shards(): count = lax.psum(jnp.sum(counted), ALL)  41.6 us
  transfers between devices with their start and end apart: 22, of which 19 were waited for; matrix products, arithmetic and copies ran while one was open for 6% of the time, Pallas kernels for 0%

profile of v1, /device:TPU:0, one launch (start us, length us, event | category | flops | bytes accessed | tf_op | source)
XLA Modules:
  0.0 908.9 jit_solution(11399907540486602189)
XLA Ops:
  16.6 8.3 all-to-all-start
  24.9 46.6 %all-gather.2.cloned.1.call-done = bf16[4608,256]{1,0:T(8,128)(2,1)} async-done(((bf16[144,256]{1,0:T(8,128)(2,1)}), bf16[4608,256]{1,0:T(8,128)(2,1)}) %all-gather.2.cloned.1.call-update) | async-done | bytes 2359312 | tf_op jit(solution)/shard_map/all_gather | solution.py:404
  71.5 3.9 spread_rows.1
  78.2 3.1 scatter_custom_fusion.1
  81.3 4.5 all-to-all-start.1
  87.1 14.2 %all-to-all-done.1 = bf16[16,64,256]{2,1,0:T(8,128)(2,1)S(1)} async-done(((bf16[16,64,256]{2,1,0:T(8,128)(2,1)}), bf16[16,64,256]{2,1,0:T(8,128)(2,1)S(1)}, u32[]{:S(2)}, u32[]{:S(2)}) %all-to-all-start.1) | async-done | bytes 524320 | tf_op jit(solution)/shard_map/all_to_all | solution.py:428
  121.8 15.1 %collective-permute-done.1 = bf16[4096,128]{1,0:T(8,128)(2,1)S(1)} collective-permute-done((bf16[4096,128]{1,0:T(8,128)(2,1)}, bf16[4096,128]{1,0:T(8,128)(2,1)S(1)}, u32[]{:S(2)}, u32[]{:S(2)}) %collective-permute-start.1) | collective-permute-done | bytes 1048608 | tf_op jit(solution)/shard_map/ppermute | solution.py:54
  136.9 19.1 %collective-permute-done = bf16[4096,128]{1,0:T(8,128)(2,1)S(1)} collective-permute-done((bf16[4096,128]{1,0:T(8,128)(2,1)}, bf16[4096,128]{1,0:T(8,128)(2,1)S(1)}, u32[]{:S(2)}, u32[]{:S(2)}) %collective-permute-start) | collective-permute-done | bytes 1048608 | tf_op jit(solution)/shard_map/ppermute | solution.py:54
  157.0 16.1 %gather_rows.3 = bf16[12288,2,128]{2,1,0:T(2,128)(2,1)} custom-call(s32[12288]{0:T(1024)} %reshape.204.index_ref, bf16[2048,2,128]{2,1,0:T(2,128)(2,1)} %bitcast.168, bf16[2048,2,128]{2,1,0:T(2,128)(2,1)} %copy.41.own_ref, bf16[2048,2,128]{2,1,0:T(2,128)(2,1)} %bitcast.167), custom_call_target="tpu_custom_call" | custom-call | tf_op jit(solution)/shard_map/gather_rows/pallas_call | solution.py:159
  173.1 11.8 %round_forward.3 = (f32[2048,256]{1,0:T(8,128)}, f32[2048,256]{1,0:T(8,128)}, bf16[2048,256]{1,0:T(8,128)(2,1)}, bf16[4096,128]{1,0:T(8,128)(2,1)}) custom-call(f32[2048,256]{1,0:T(8,128)} %get-tuple-element.120.refs_0_.mesh_ref, bf16[6,4096,128]{2,1,0:T(8,128)(2,1)} %bitcast.142, bf16[5,256,256]{2,1,0:T(8,128)(2,1)} %bitcast.150, ...), custom_call_target="tpu_custom_call" | custom-call | tf_op jit(solution)/shard_map/round_forward/pallas_call | solution.py:243
  184.9 3.8 collective-permute-start.3
  188.9 22.5 %collective-permute-done.3 = bf16[4096,128]{1,0:T(8,128)(2,1)S(1)} collective-permute-done((bf16[4096,128]{1,0:T(8,128)(2,1)}, bf16[4096,128]{1,0:T(8,128)(2,1)S(1)}, u32[]{:S(2)}, u32[]{:S(2)}) %collective-permute-start.3) | collective-permute-done | bytes 1048608 | tf_op jit(solution)/shard_map/ppermute | solution.py:54
  211.4 19.6 %collective-permute-done.2 = bf16[4096,128]{1,0:T(8,128)(2,1)S(1)} collective-permute-done((bf16[4096,128]{1,0:T(8,128)(2,1)}, bf16[4096,128]{1,0:T(8,128)(2,1)S(1)}, u32[]{:S(2)}, u32[]{:S(2)}) %collective-permute-start.2) | collective-permute-done | bytes 1048608 | tf_op jit(solution)/shard_map/ppermute | solution.py:54
  232.0 16.1 %gather_rows.4 = bf16[12288,2,128]{2,1,0:T(2,128)(2,1)} custom-call(s32[12288]{0:T(1024)} %reshape.204.index_ref, bf16[2048,2,128]{2,1,0:T(2,128)(2,1)} %bitcast.173, bf16[2048,2,128]{2,1,0:T(2,128)(2,1)} %bitcast.169, bf16[2048,2,128]{2,1,0:T(2,128)(2,1)} %bitcast.171), custom_call_target="tpu_custom_call" | custom-call | tf_op jit(solution)/shard_map/gather_rows/pallas_call | solution.py:159
  248.1 11.8 %round_forward.4 = (f32[2048,256]{1,0:T(8,128)}, f32[2048,256]{1,0:T(8,128)}, bf16[2048,256]{1,0:T(8,128)(2,1)}, bf16[4096,128]{1,0:T(8,128)(2,1)}) custom-call(f32[2048,256]{1,0:T(8,128)} %get-tuple-element.53.refs_0_.mesh_ref, bf16[6,4096,128]{2,1,0:T(8,128)(2,1)} %bitcast.144, bf16[5,256,256]{2,1,0:T(8,128)(2,1)} %bitcast.153, ...), custom_call_target="tpu_custom_call" | custom-call | tf_op jit(solution)/shard_map/round_forward/pallas_call | solution.py:243
  259.9 4.4 collective-permute-start.5
  264.3 22.1 %collective-permute-done.5 = bf16[4096,128]{1,0:T(8,128)(2,1)S(1)} collective-permute-done((bf16[4096,128]{1,0:T(8,128)(2,1)}, bf16[4096,128]{1,0:T(8,128)(2,1)S(1)}, u32[]{:S(2)}, u32[]{:S(2)}) %collective-permute-start.5) | collective-permute-done | bytes 1048608 | tf_op jit(solution)/shard_map/ppermute | solution.py:54
  286.4 21.3 %collective-permute-done.4 = bf16[4096,128]{1,0:T(8,128)(2,1)S(1)} collective-permute-done((bf16[4096,128]{1,0:T(8,128)(2,1)}, bf16[4096,128]{1,0:T(8,128)(2,1)S(1)}, u32[]{:S(2)}, u32[]{:S(2)}) %collective-permute-start.4) | collective-permute-done | bytes 1048608 | tf_op jit(solution)/shard_map/ppermute | solution.py:54
  308.7 16.1 %gather_rows.5 = bf16[12288,2,128]{2,1,0:T(2,128)(2,1)} custom-call(s32[12288]{0:T(1024)} %reshape.204.index_ref, bf16[2048,2,128]{2,1,0:T(2,128)(2,1)} %bitcast.174, bf16[2048,2,128]{2,1,0:T(2,128)(2,1)} %bitcast.170, bf16[2048,2,128]{2,1,0:T(2,128)(2,1)} %bitcast.172), custom_call_target="tpu_custom_call" | custom-call | tf_op jit(solution)/shard_map/gather_rows/pallas_call | solution.py:159
  324.8 11.2 %round_forward.5 = (f32[2048,256]{1,0:T(8,128)}, f32[2048,256]{1,0:T(8,128)}, bf16[2048,256]{1,0:T(8,128)(2,1)}) custom-call(f32[2048,256]{1,0:T(8,128)} %get-tuple-element.55.refs_0_.mesh_ref, bf16[6,4096,128]{2,1,0:T(8,128)(2,1)} %bitcast.146, bf16[5,256,256]{2,1,0:T(8,128)(2,1)} %bitcast.156, f32[2,256]{1,0:T(2,128)} %get-tuple-element.134.refs_3_.bias_ref), custom_call_target="tpu_custom_call" | custom-call | tf_op jit(solution)/shard_map/round_forward/pallas_call | solution.py:243
  336.0 4.0 fusion.9
  340.0 7.0 all-to-all-start.2
  349.2 12.4 %all-to-all-done.2 = bf16[16,64,256]{2,1,0:T(8,128)(2,1)S(1)} async-done(((bf16[16,64,256]{2,1,0:T(8,128)(2,1)}), bf16[16,64,256]{2,1,0:T(8,128)(2,1)S(1)}, u32[]{:S(2)}, u32[]{:S(2)}) %all-to-all-start.2) | async-done | bytes 524320 | tf_op jit(solution)/shard_map/all_to_all | solution.py:459
  365.5 41.6 %psum.22 = f32[]{:T(128)} all-reduce(f32[]{:T(128)} %fusion.43), channel_id=1, replica_groups=mesh['dp'=2,'space'=16] {'dp','space'}, use_global_device_ids=true, to_apply=%region_9.10 | all-reduce | flops 1 | bytes 8 | tf_op jit(solution)/shard_map/psum | solution.py:417
  409.1 4.2 collective-permute-start.8
  417.1 3.2 scatter_custom_fusion.2
  420.2 7.0 all-to-all-start.3
  429.3 10.4 %all-to-all-done.3 = bf16[16,64,256]{2,1,0:T(8,128)(2,1)S(1)} async-done(((bf16[16,64,256]{2,1,0:T(8,128)(2,1)}), bf16[16,64,256]{2,1,0:T(8,128)(2,1)S(1)}, u32[]{:S(2)}, u32[]{:S(2)}) %all-to-all-start.3) | async-done | bytes 524320 | tf_op jit(solution)/shard_map/all_to_all | solution.py:501
  439.6 3.8 fusion.1.grad_ref
  443.4 33.1 %edges_backward.3 = (bf16[2048,256]{1,0:T(8,128)(2,1)}, bf16[2048,256]{1,0:T(8,128)(2,1)}, bf16[4096,128]{1,0:T(8,128)(2,1)}, f32[4096,128]{1,0:T(8,128)}, bf16[4096,128]{1,0:T(8,128)(2,1)}) custom-call(s32[12288]{0:T(1024)} %reshape.204.index_ref, f32[2048,256]{1,0:T(8,128)} %fusion.1.grad_ref, f32[2048,256]{1,0:T(8,128)} %get-tuple-element.55.refs_0_.mesh_ref, ...), custom_call_target="tpu_custom_call" | custom-call | tf_op jit(solution)/shard_map/edges_backward/pallas_call | solution.py:322
  477.1 5.2 collective-permute-start.10
  489.6 28.0 %collective-permute-done.9.first_ref = bf16[4096,128]{1,0:T(8,128)(2,1)S(1)} collective-permute-done((bf16[4096,128]{1,0:T(8,128)(2,1)}, bf16[4096,128]{1,0:T(8,128)(2,1)S(1)}, u32[]{:S(2)}, u32[]{:S(2)}) %collective-permute-start.9) | collective-permute-done | bytes 1048608 | tf_op jit(solution)/shard_map/ppermute | solution.py:54
  520.4 8.5 round_backward.3
  528.9 33.1 %edges_backward.4 = (bf16[2048,256]{1,0:T(8,128)(2,1)}, bf16[2048,256]{1,0:T(8,128)(2,1)}, bf16[4096,128]{1,0:T(8,128)(2,1)}, f32[4096,128]{1,0:T(8,128)}, bf16[4096,128]{1,0:T(8,128)(2,1)}) custom-call(s32[12288]{0:T(1024)} %reshape.204.index_ref, f32[2048,256]{1,0:T(8,128)} %get-tuple-element.65.grad_ref, f32[2048,256]{1,0:T(8,128)} %get-tuple-element.53.refs_0_.mesh_ref, ...), custom_call_target="tpu_custom_call" | custom-call | tf_op jit(solution)/shard_map/edges_backward/pallas_call | solution.py:322
  565.5 5.0 collective-permute-start.12
  576.4 29.6 %collective-permute-done.11.first_ref = bf16[4096,128]{1,0:T(8,128)(2,1)S(1)} collective-permute-done((bf16[4096,128]{1,0:T(8,128)(2,1)}, bf16[4096,128]{1,0:T(8,128)(2,1)S(1)}, u32[]{:S(2)}, u32[]{:S(2)}) %collective-permute-start.11) | collective-permute-done | bytes 1048608 | tf_op jit(solution)/shard_map/ppermute | solution.py:54
  606.0 7.7 collective-permute-done.12.last_ref
  614.7 8.5 round_backward.4
  623.2 33.1 %edges_backward.5 = (bf16[2048,256]{1,0:T(8,128)(2,1)}, bf16[2048,256]{1,0:T(8,128)(2,1)}, bf16[4096,128]{1,0:T(8,128)(2,1)}, f32[4096,128]{1,0:T(8,128)}, bf16[4096,128]{1,0:T(8,128)(2,1)}) custom-call(s32[12288]{0:T(1024)} %reshape.204.index_ref, f32[2048,256]{1,0:T(8,128)} %get-tuple-element.72.grad_ref, f32[2048,256]{1,0:T(8,128)} %get-tuple-element.120.refs_0_.mesh_ref, ...), custom_call_target="tpu_custom_call" | custom-call | tf_op jit(solution)/shard_map/edges_backward/pallas_call | solution.py:322
  656.6 5.3 collective-permute-start.14
  668.1 31.9 %collective-permute-done.13.first_ref = bf16[4096,128]{1,0:T(8,128)(2,1)S(1)} collective-permute-done((bf16[4096,128]{1,0:T(8,128)(2,1)}, bf16[4096,128]{1,0:T(8,128)(2,1)S(1)}, u32[]{:S(2)}, u32[]{:S(2)}) %collective-permute-start.13) | collective-permute-done | bytes 1048608 | tf_op jit(solution)/shard_map/ppermute | solution.py:54
  700.0 3.5 collective-permute-done.14.last_ref
  704.5 8.6 round_backward.5
  719.4 6.4 all-to-all-start.4
  733.5 7.1 all-to-all-done.4
  745.8 5.0 collect_rows.1
  753.1 103.3 %reduce-scatter.2.cloned.1.call-done = f32[144,256]{1,0:T(8,128)} async-done(((f32[4608,256]{1,0:T(8,128)}), f32[144,256]{1,0:T(8,128)}) %reduce-scatter.2.cloned.1.call-update) | async-done | bytes 147472 | tf_op jit(solution)/shard_map/reduce_scatter | solution.py:547
  858.1 40.8 %all-reduce.4 = (f32[1]{0:T(128)}, f32[]{:T(128)}) all-reduce(f32[1]{0:T(128)} %bitcast.39, f32[]{:T(128)} %multiply_reduce_fusion.1), channel_id=1, replica_groups=mesh['dp'=2,'space'=16] {'dp','space'}, use_global_device_ids=true, to_apply=%region_7.8 | all-reduce | flops 2 | bytes 16 | tf_op jit(solution)/shard_map/psum | solution.py:481
  (209 shorter events, 101.7 us)
Async XLA Ops:
  7.2 69.0 %copy-start.43 = (bf16[1,78,512]{2,1,0:T(8,128)(2,1)S(1)}, bf16[1,78,512]{2,1,0:T(8,128)(2,1)}, u32[]{:S(2)}) copy-start(bf16[1,78,512]{2,1,0:T(8,128)(2,1)} %param.13) | copy-start | bytes 239620
  7.2 64.3 %all-gather.2.cloned.1.call-start = ((), (), s32[]{:S(2)}) async-start(), calls=%async_computation.6 | async-start | bytes 2433024 | tf_op jit(solution)/shard_map/all_gather | solution.py:404
  16.6 64.8 %all-to-all-start = ((s32[16,1,64]{2,1,0:T(1,128)}), s32[16,1,64]{2,1,0:T(1,128)S(1)}, u32[]{:S(2)}, u32[]{:S(2)}) async-start(s32[16,1,64]{2,1,0:T(1,128)} %all_to_all.18), calls=%async_computation | async-start | bytes 16384 | tf_op jit(solution)/shard_map/all_to_all | solution.py:431
  81.3 20.0 %all-to-all-start.1 = ((bf16[16,64,256]{2,1,0:T(8,128)(2,1)}), bf16[16,64,256]{2,1,0:T(8,128)(2,1)S(1)}, u32[]{:S(2)}, u32[]{:S(2)}) async-start(bf16[16,64,256]{2,1,0:T(8,128)(2,1)} %bitcast.12), calls=%async_computation.1 | async-start | bytes 1048576 | tf_op jit(solution)/shard_map/all_to_all | solution.py:428
  108.9 4.4 copy-start.48
  110.6 26.3 %collective-permute-start.1 = (bf16[4096,128]{1,0:T(8,128)(2,1)}, bf16[4096,128]{1,0:T(8,128)(2,1)S(1)}, u32[]{:S(2)}, u32[]{:S(2)}) collective-permute-start(bf16[4096,128]{1,0:T(8,128)(2,1)} %reshape.206), channel_id=1, source_target_pairs={{1,0},{2,1},{3,2},{4,3},{5,4},{6,5},{7,6},{8,7},{9,8},{10,9},{11,1... | collective-permute-start | bytes 3145736 | tf_op jit(solution)/shard_map/ppermute | solution.py:54
  113.2 42.8 %collective-permute-start = (bf16[4096,128]{1,0:T(8,128)(2,1)}, bf16[4096,128]{1,0:T(8,128)(2,1)S(1)}, u32[]{:S(2)}, u32[]{:S(2)}) collective-permute-start(bf16[4096,128]{1,0:T(8,128)(2,1)} %reshape.206), channel_id=1, source_target_pairs={{0,1},{1,2},{2,3},{3,4},{4,5},{5,6},{6,7},{7,8},{8,9},{9,10},{10,1... | collective-permute-start | bytes 3145736 | tf_op jit(solution)/shard_map/ppermute | solution.py:54
  136.9 19.1 %copy-start.22 = (bf16[4096,128]{1,0:T(8,128)(2,1)}, bf16[4096,128]{1,0:T(8,128)(2,1)S(1)}, u32[]{:S(2)}) copy-start(bf16[4096,128]{1,0:T(8,128)(2,1)S(1)} %collective-permute-done.1) | copy-start | bytes 3145732
  184.9 26.6 %collective-permute-start.3 = (bf16[4096,128]{1,0:T(8,128)(2,1)}, bf16[4096,128]{1,0:T(8,128)(2,1)S(1)}, u32[]{:S(2)}, u32[]{:S(2)}) collective-permute-start(bf16[4096,128]{1,0:T(8,128)(2,1)} %get-tuple-element.54), channel_id=1, source_target_pairs={{1,0},{2,1},{3,2},{4,3},{5,4},{6,5},{7,6},{8,7},{9,8},{10,9},{11,1... | collective-permute-start | bytes 3145736 | tf_op jit(solution)/shard_map/ppermute | solution.py:54
  188.7 42.4 %collective-permute-start.2 = (bf16[4096,128]{1,0:T(8,128)(2,1)}, bf16[4096,128]{1,0:T(8,128)(2,1)S(1)}, u32[]{:S(2)}, u32[]{:S(2)}) collective-permute-start(bf16[4096,128]{1,0:T(8,128)(2,1)} %get-tuple-element.54), channel_id=1, source_target_pairs={{0,1},{1,2},{2,3},{3,4},{4,5},{5,6},{6,7},{7,8},{8,9},{9,10},{10,1... | collective-permute-start | bytes 3145736 | tf_op jit(solution)/shard_map/ppermute | solution.py:54
  211.4 19.6 %copy-start.29 = (bf16[4096,128]{1,0:T(8,128)(2,1)}, bf16[4096,128]{1,0:T(8,128)(2,1)S(1)}, u32[]{:S(2)}) copy-start(bf16[4096,128]{1,0:T(8,128)(2,1)S(1)} %collective-permute-done.3) | copy-start | bytes 3145732
  259.9 26.6 %collective-permute-start.5 = (bf16[4096,128]{1,0:T(8,128)(2,1)}, bf16[4096,128]{1,0:T(8,128)(2,1)S(1)}, u32[]{:S(2)}, u32[]{:S(2)}) collective-permute-start(bf16[4096,128]{1,0:T(8,128)(2,1)} %get-tuple-element.56), channel_id=1, source_target_pairs={{1,0},{2,1},{3,2},{4,3},{5,4},{6,5},{7,6},{8,7},{9,8},{10,9},{11,1... | collective-permute-start | bytes 3145736 | tf_op jit(solution)/shard_map/ppermute | solution.py:54
  264.3 43.4 %collective-permute-start.4 = (bf16[4096,128]{1,0:T(8,128)(2,1)}, bf16[4096,128]{1,0:T(8,128)(2,1)S(1)}, u32[]{:S(2)}, u32[]{:S(2)}) collective-permute-start(bf16[4096,128]{1,0:T(8,128)(2,1)} %get-tuple-element.56), channel_id=1, source_target_pairs={{0,1},{1,2},{2,3},{3,4},{4,5},{5,6},{6,7},{7,8},{8,9},{9,10},{10,1... | collective-permute-start | bytes 3145736 | tf_op jit(solution)/shard_map/ppermute | solution.py:54
  286.4 21.3 %copy-start.30 = (bf16[4096,128]{1,0:T(8,128)(2,1)}, bf16[4096,128]{1,0:T(8,128)(2,1)S(1)}, u32[]{:S(2)}) copy-start(bf16[4096,128]{1,0:T(8,128)(2,1)S(1)} %collective-permute-done.5) | copy-start | bytes 3145732
  336.0 11.0 %copy-start.20 = (s32[1,78,512]{2,0,1:T(1,128)S(1)}, s32[1,78,512]{2,0,1:T(1,128)}, u32[]{:S(2)}) copy-start(s32[1,78,512]{2,0,1:T(1,128)} %param.15) | copy-start | bytes 479236
  336.0 13.0 %copy-start.49 = (bf16[78,256]{1,0:T(8,128)(2,1)S(1)}, bf16[78,256]{1,0:T(8,128)(2,1)}, u32[]{:S(2)}) copy-start(bf16[78,256]{1,0:T(8,128)(2,1)} %get-tuple-element.48) | copy-start | bytes 119812
  340.0 23.6 %copy-start.46 = (bf16[256,256]{1,0:T(8,128)(2,1)S(1)}, bf16[256,256]{1,0:T(8,128)(2,1)}, u32[]{:S(2)}) copy-start(bf16[256,256]{1,0:T(8,128)(2,1)} %get-tuple-element.58) | copy-start | bytes 393220
  340.0 21.6 %all-to-all-start.2 = ((bf16[16,64,256]{2,1,0:T(8,128)(2,1)}), bf16[16,64,256]{2,1,0:T(8,128)(2,1)S(1)}, u32[]{:S(2)}, u32[]{:S(2)}) async-start(bf16[16,64,256]{2,1,0:T(8,128)(2,1)} %bitcast.35), calls=%async_computation.2 | async-start | bytes 1048576 | tf_op jit(solution)/shard_map/all_to_all | solution.py:459
  347.1 60.0 %collective-permute-start.6 = (bf16[78,360]{1,0:T(8,128)(2,1)S(1)}, bf16[78,360]{1,0:T(8,128)(2,1)S(1)}, u32[]{:S(2)}, u32[]{:S(2)}) collective-permute-start(bf16[78,360]{1,0:T(8,128)(2,1)S(1)} %slice.194), channel_id=1, source_target_pairs={{1,0},{2,1},{3,2},{4,3},{5,4},{6,5},{7,6},{8,7},{9,8},{10,9},{11,1... | collective-permute-start | bytes 168488 | tf_op jit(solution)/shard_map/ppermute | solution.py:47
  364.2 42.9 %collective-permute-start.7 = (bf16[78,360]{1,0:T(8,128)(2,1)S(1)}, bf16[78,360]{1,0:T(8,128)(2,1)S(1)}, u32[]{:S(2)}, u32[]{:S(2)}) collective-permute-start(bf16[78,360]{1,0:T(8,128)(2,1)S(1)} %slice.193), channel_id=1, source_target_pairs={{1,0},{2,1},{3,2},{4,3},{5,4},{6,5},{7,6},{8,7},{9,8},{10,9},{11,1... | collective-permute-start | bytes 168488 | tf_op jit(solution)/shard_map/ppermute | solution.py:47
  409.1 6.0 collective-permute-start.8
  420.2 19.4 %all-to-all-start.3 = ((bf16[16,64,256]{2,1,0:T(8,128)(2,1)}), bf16[16,64,256]{2,1,0:T(8,128)(2,1)S(1)}, u32[]{:S(2)}, u32[]{:S(2)}) async-start(bf16[16,64,256]{2,1,0:T(8,128)(2,1)} %bitcast.41), calls=%async_computation.3 | async-start | bytes 1048576 | tf_op jit(solution)/shard_map/all_to_all | solution.py:501
  443.4 38.9 %copy-start.37 = (bf16[2048,256]{1,0:T(8,128)(2,1)S(1)}, bf16[2048,256]{1,0:T(8,128)(2,1)}, u32[]{:S(2)}) copy-start(bf16[2048,256]{1,0:T(8,128)(2,1)} %get-tuple-element.85) | copy-start | bytes 3145732
  476.5 8.4 copy-start.8
  476.5 8.4 copy-start.14
  476.5 41.0 %collective-permute-start.9 = (bf16[4096,128]{1,0:T(8,128)(2,1)}, bf16[4096,128]{1,0:T(8,128)(2,1)S(1)}, u32[]{:S(2)}, u32[]{:S(2)}) collective-permute-start(bf16[4096,128]{1,0:T(8,128)(2,1)} %get-tuple-element.61), channel_id=1, source_target_pairs={{0,1},{1,2},{2,3},{3,4},{4,5},{5,6},{6,7},{7,8},{8,9},{9,10},{10,1... | collective-permute-start | bytes 3145736 | tf_op jit(solution)/shard_map/ppermute | solution.py:54
  477.1 42.2 %collective-permute-start.10 = (bf16[4096,128]{1,0:T(8,128)(2,1)}, bf16[4096,128]{1,0:T(8,128)(2,1)S(1)}, u32[]{:S(2)}, u32[]{:S(2)}) collective-permute-start(bf16[4096,128]{1,0:T(8,128)(2,1)} %get-tuple-element.62), channel_id=1, source_target_pairs={{1,0},{2,1},{3,2},{4,3},{5,4},{6,5},{7,6},{8,7},{9,8},{10,9},{11,1... | collective-permute-start | bytes 3145736 | tf_op jit(solution)/shard_map/ppermute | solution.py:54
  528.9 33.2 %copy-start = (f32[2048,256]{1,0:T(8,128)S(1)}, f32[2048,256]{1,0:T(8,128)}, u32[]{:S(2)}) copy-start(f32[2048,256]{1,0:T(8,128)} %get-tuple-element.53.refs_0_.mesh_ref) | copy-start | bytes 6291460
  562.0 8.4 copy-start.7
  562.1 8.4 copy-start.36
  562.1 9.6 %copy-start.13 = (bf16[2048,256]{1,0:T(8,128)(2,1)S(1)}, bf16[2048,256]{1,0:T(8,128)(2,1)}, u32[]{:S(2)}) copy-start(bf16[2048,256]{1,0:T(8,128)(2,1)} %get-tuple-element.71.dest_ref) | copy-start | bytes 3145732
  564.6 41.4 %collective-permute-start.11 = (bf16[4096,128]{1,0:T(8,128)(2,1)}, bf16[4096,128]{1,0:T(8,128)(2,1)S(1)}, u32[]{:S(2)}, u32[]{:S(2)}) collective-permute-start(bf16[4096,128]{1,0:T(8,128)(2,1)} %get-tuple-element.68), channel_id=1, source_target_pairs={{0,1},{1,2},{2,3},{3,4},{4,5},{5,6},{6,7},{7,8},{8,9},{9,10},{10,1... | collective-permute-start | bytes 3145736 | tf_op jit(solution)/shard_map/ppermute | solution.py:54
  565.5 48.2 %collective-permute-start.12 = (bf16[4096,128]{1,0:T(8,128)(2,1)S(1)}, bf16[4096,128]{1,0:T(8,128)(2,1)S(1)}, u32[]{:S(2)}, u32[]{:S(2)}) collective-permute-start(bf16[4096,128]{1,0:T(8,128)(2,1)S(1)} %copy-done.51), channel_id=1, source_target_pairs={{1,0},{2,1},{3,2},{4,3},{5,4},{6,5},{7,6},{8,7},{9,8},{10,9},{11,1... | collective-permute-start | bytes 3145736 | tf_op jit(solution)/shard_map/ppermute | solution.py:54
  606.0 7.7 copy-start.21
  623.2 38.8 %copy-start.10 = (bf16[2048,256]{1,0:T(8,128)(2,1)S(1)}, bf16[2048,256]{1,0:T(8,128)(2,1)}, u32[]{:S(2)}) copy-start(bf16[2048,256]{1,0:T(8,128)(2,1)} %copy-done.9) | copy-start | bytes 3145732
  656.3 8.2 copy-start.5
  656.3 8.2 copy-start.35
  656.3 43.7 %collective-permute-start.13 = (bf16[4096,128]{1,0:T(8,128)(2,1)}, bf16[4096,128]{1,0:T(8,128)(2,1)S(1)}, u32[]{:S(2)}, u32[]{:S(2)}) collective-permute-start(bf16[4096,128]{1,0:T(8,128)(2,1)} %get-tuple-element.75), channel_id=1, source_target_pairs={{0,1},{1,2},{2,3},{3,4},{4,5},{5,6},{6,7},{7,8},{8,9},{9,10},{10,1... | collective-permute-start | bytes 3145736 | tf_op jit(solution)/shard_map/ppermute | solution.py:54
  656.6 46.9 %collective-permute-start.14 = (bf16[4096,128]{1,0:T(8,128)(2,1)}, bf16[4096,128]{1,0:T(8,128)(2,1)S(1)}, u32[]{:S(2)}, u32[]{:S(2)}) collective-permute-start(bf16[4096,128]{1,0:T(8,128)(2,1)} %get-tuple-element.76), channel_id=1, source_target_pairs={{1,0},{2,1},{3,2},{4,3},{5,4},{6,5},{7,6},{8,7},{9,8},{10,9},{11,1... | collective-permute-start | bytes 3145736 | tf_op jit(solution)/shard_map/ppermute | solution.py:54
  704.5 8.6 copy-start.19
  716.5 9.6 %copy-start.6 = (bf16[2048,256]{1,0:T(8,128)(2,1)S(1)}, bf16[2048,256]{1,0:T(8,128)(2,1)}, u32[]{:S(2)}) copy-start(bf16[2048,256]{1,0:T(8,128)(2,1)} %get-tuple-element.77.guin_ref) | copy-start | bytes 3145732
  719.4 8.3 copy-start.2
  719.4 21.2 %all-to-all-start.4 = ((bf16[16,64,256]{2,1,0:T(8,128)(2,1)}), bf16[16,64,256]{2,1,0:T(8,128)(2,1)}, u32[]{:S(2)}, u32[]{:S(2)}) async-start(bf16[16,64,256]{2,1,0:T(8,128)(2,1)} %bitcast.175), calls=%async_computation.4 | async-start | bytes 1048576 | tf_op jit(solution)/shard_map/all_to_all | solution.py:536
  725.8 130.6 %reduce-scatter.2.cloned.1.call-start = ((), (), s32[]{:S(2)}) async-start(), calls=%async_computation.7 | async-start | bytes 4866048 | tf_op jit(solution)/shard_map/reduce_scatter | solution.py:547
  732.4 11.1 %copy-start.42 = (f32[512,256]{0,1:T(8,128)S(1)}, f32[512,256]{0,1:T(8,128)}, u32[]{:S(2)}) copy-start(f32[512,256]{0,1:T(8,128)} %get-tuple-element.142) | copy-start | bytes 1572868
  750.9 148.7 %copy-start.41 = (f32[36136]{0:T(1024)S(1)}, f32[36136]{0:T(1024)}, u32[]{:S(2)}) copy-start(f32[36136]{0:T(1024)} %param.10) | copy-start | bytes 433636
  750.9 148.8 %copy-start.44 = (f32[36136]{0:T(1024)S(1)}, f32[36136]{0:T(1024)}, u32[]{:S(2)}) copy-start(f32[36136]{0:T(1024)} %param.11) | copy-start | bytes 433636
  750.9 148.8 %copy-start.45 = (f32[36136]{0:T(1024)S(1)}, f32[36136]{0:T(1024)}, u32[]{:S(2)}) copy-start(f32[36136]{0:T(1024)} %param.12) | copy-start | bytes 433636
  (28 other events, 57.1 us)
Sparse Core Ops, SparseCore 0:
  11.5 59.9 all-gather.1
  751.1 105.2 reduce-scatter.1

commit v2 on v1

--- a/solution.py
+++ b/solution.py
@@ -67,61 +67,168 @@
     return [CH, D, D, CH, ROUNDS * 5 * D, 3 + 2 * ROUNDS]
 
 
-def spread_rows(gathered, total):
-    peers, height, _ = gathered.shape
-    starts, counts, shared, _ = pieces_of(total, peers)
+def swapped(value, axis, bit):
+    return lax.ppermute(value, axis, [(i, i ^ bit) for i in range(lax.axis_size(axis))])
+
+
+def bits_of(axis):
+    return [1 << n for n in range(lax.axis_size(axis).bit_length() - 1)]
+
+
+def summed_everywhere(value):
+    for axis in ALL:
+        for bit in bits_of(axis):
+            value = value + swapped(value, axis, bit)
+    return value
+
+
+def orders():
+    bits = bits_of("space")
+    return bits, bits[1:2] + bits[:1] + bits[2:]
+
+
+def gathered_blocks(piece):
+    half = piece.shape[0] // 2
+    held = []
+    for part, order in zip((piece[:half], piece[half:]), orders()):
+        names, part = [], part[None]
+        for bit in reversed(order):
+            part = jnp.concatenate([part, swapped(part, "space", bit)], 0)
+            names.insert(0, bit)
+        held.append(part)
+    return held, [swapped(part, "dp", 1) for part in held]
+
+
+def spread_rows(gathered, total, peers, place):
+    (first, second), (first_far, second_far) = gathered
+    starts, counts, shared, height = pieces_of(total, peers)
+    half, group = height // 2, first.shape[0]
     rows = -(-total // D)
     sizes = parts_of()
-
-    def body(source, *refs):
-        outs, buffer = refs[:-1], refs[-1]
+    ranks = []
+    for order in orders():
+        ranks.append({bit: group >> (n + 1) for n, bit in enumerate(order)})
+
+    def at(rank, relative):
+        spot = 0
+        for bit, weight in rank.items():
+            spot = spot + jnp.where((relative & bit) != 0, weight, 0)
+        return spot
+
+    def body(place_ref, *refs):
+        sources, outs, buffer = refs[:4], refs[4:-1], refs[-1]
+        me = place_ref[0]
+        mine = me // group
         for d in range(peers):
-            piece = source[d].astype(jnp.float32)
-            at, count = starts[d], counts[d]
-            if shared[d]:
-                buffer[at : at + 1, :] = buffer[at : at + 1, :] + piece[:1]
-                buffer[at + 1 : at + count, :] = piece[1:count]
-            else:
-                buffer[at : at + count, :] = piece[:count]
+            relative = (me ^ d) & (group - 1)
+            spots = [at(rank, relative) for rank in ranks]
+
+            def lay(one, two, d=d, spots=spots):
+                piece = jnp.concatenate([one[spots[0]], two[spots[1]]], 0).astype(jnp.float32)
+                start, count = starts[d], counts[d]
+                if shared[d]:
+                    buffer[start : start + 1, :] = buffer[start : start + 1, :] + piece[:1]
+                    buffer[start + 1 : start + count, :] = piece[1:count]
+                else:
+                    buffer[start : start + count, :] = piece[:count]
+
+            @pl.when(mine == d // group)
+            def _():
+                lay(sources[0], sources[1])
+
+            @pl.when(mine != d // group)
+            def _():
+                lay(sources[2], sources[3])
+
         start = 0
         for out, size in zip(outs, sizes):
-            out[...] = buffer[start : start + size, :].astype(out.dtype)
+            out[:size, :] = buffer[start : start + size, :].astype(out.dtype)
+            if out.shape[0] > size:
+                out[size:, :] = jnp.zeros((out.shape[0] - size, D), out.dtype)
             start = start + size
 
     kinds = [jnp.bfloat16] * 5 + [jnp.float32]
+    talls = [HALF] + sizes[1:]
     return pl.pallas_call(
         body,
-        out_shape=[jax.ShapeDtypeStruct((size, D), kind) for size, kind in zip(sizes, kinds)],
-        scratch_shapes=[pltpu.VMEM((-(-rows // 8) * 8 + 8, D), jnp.float32)],
+        grid_spec=pltpu.PrefetchScalarGridSpec(
+            num_scalar_prefetch=1,
+            grid=(1,),
+            in_specs=[whole(first.shape)] * 4,
+            out_specs=[whole((tall, D)) for tall in talls],
+            scratch_shapes=[pltpu.VMEM((-(-rows // 8) * 8 + 8, D), jnp.float32)],
+        ),
+        out_shape=[jax.ShapeDtypeStruct((tall, D), kind) for tall, kind in zip(talls, kinds)],
         compiler_params=LIMIT,
         name="spread_rows",
-    )(gathered)
-
-
-def collect_rows(parts, total, peers):
+    )(place.reshape(1), first, second, first_far, second_far)
+
+
+def collect_rows(parts, total, peers, place):
     starts, counts, shared, height = pieces_of(total, peers)
     rows = -(-total // D)
-    used = sum(part.shape[0] for part in parts)
-
-    def body(*refs):
-        sources, out, buffer = refs[:-2], refs[-2], refs[-1]
+    sizes = [min(part.shape[0], size) for part, size in zip(parts, tall_parts())]
+    group = lax.axis_size("space")
+
+    def body(place_ref, *refs):
+        sources, keep, send, buffer = refs[:-3], refs[-3], refs[-2], refs[-1]
         start = 0
-        for source in sources:
-            size = source.shape[0]
-            buffer[start : start + size, :] = source[...]
+        for source, size in zip(sources, sizes):
+            buffer[start : start + size, :] = source[:size, :]
             start = start + size
         if buffer.shape[0] > start:
             buffer[start:, :] = jnp.zeros((buffer.shape[0] - start, D), jnp.float32)
+        me = place_ref[0]
+        mine = me // group
         for d in range(peers):
-            out[d] = buffer[starts[d] : starts[d] + height, :]
-
+            relative = (me ^ d) & (group - 1)
+
+            @pl.when(mine == d // group)
+            def _():
+                keep[relative] = buffer[starts[d] : starts[d] + height, :]
+
+            @pl.when(mine != d // group)
+            def _():
+                send[relative] = buffer[starts[d] : starts[d] + height, :].astype(jnp.bfloat16)
+
+    shape = (group, height, D)
     return pl.pallas_call(
         body,
-        out_shape=jax.ShapeDtypeStruct((peers, height, D), jnp.float32),
-        scratch_shapes=[pltpu.VMEM((-(-max(rows, used) // 8) * 8 + height + 8, D), jnp.float32)],
+        grid_spec=pltpu.PrefetchScalarGridSpec(
+            num_scalar_prefetch=1,
+            grid=(1,),
+            in_specs=[whole(part.shape) for part in parts],
+            out_specs=[whole(shape), whole(shape)],
+            scratch_shapes=[pltpu.VMEM((-(-rows // 8) * 8 + height + 8, D), jnp.float32)],
+        ),
+        out_shape=[
+            jax.ShapeDtypeStruct(shape, jnp.float32),
+            jax.ShapeDtypeStruct(shape, jnp.bfloat16),
+        ],
         compiler_params=LIMIT,
         name="collect_rows",
-    )(*parts)
+    )(place.reshape(1), *parts)
+
+
+def reduced_piece(keep, send):
+    kept = keep + swapped(send, "dp", 1).astype(jnp.float32)
+    half = kept.shape[1] // 2
+    done = []
+    for part, order in zip((kept[:, :half], kept[:, half:]), orders()):
+        names = bits_of("space")[::-1]
+        part = part.reshape((2,) * len(names) + (half, D))
+        for bit in order:
+            spot = names.index(bit)
+            names.pop(spot)
+            stay = lax.index_in_dim(part, 0, spot, keepdims=False)
+            leave = lax.index_in_dim(part, 1, spot, keepdims=False)
+            part = stay + swapped(leave.astype(jnp.bfloat16), "space", bit).astype(jnp.float32)
+        done.append(part)
+    return jnp.concatenate(done, 0)
+
+
+def tall_parts():
+    return [CH, D, D, CH] + [D] * (5 * ROUNDS) + [3 + 2 * ROUNDS]
 
 
 def gather_rows(index, before, own, after):
@@ -401,43 +508,53 @@
     piece = lax.dynamic_update_slice_in_dim(
         jnp.zeros((height * D,), jnp.bfloat16), master.astype(jnp.bfloat16), offset, 0
     )
-    everything = lax.all_gather(piece.reshape(height, D), ALL, axis=0, tiled=True)
-    w_in, w_node, w_dec, w_out, w_round, biases = spread_rows(
-        everything.reshape(peers, height, D), total_size
-    )
-    w_out = w_out.reshape(D, CH)
-    w_round = w_round.reshape(ROUNDS, 5, D, D)
-    b_head = biases[:3]
-    b_round = biases[3:].reshape(ROUNDS, 2, D)
     state_in = inputs[0]
-    wanted = targets[0].astype(jnp.float32)
     counted = valid[0].astype(jnp.float32)
     points = state_in.shape[1]
     blocks = neighbours.shape[0]
-    count = lax.psum(jnp.sum(counted), ALL)
+    assert blocks == H
     capacity = max(2, 2 * points // bands)
     target_band = owner[0, :, 0]
     hits = (target_band[:, None] == jnp.arange(bands, dtype=jnp.int32)[None, :]).astype(jnp.int32)
     ranks = jnp.sum(jnp.cumsum(hits, 0) * hits, 1) - 1
     places_out = target_band * capacity + ranks
-    enc_in = inner(state_in, w_in, 0, 0) + b_head[0]
-    encoded = jax.nn.silu(enc_in).astype(jnp.bfloat16)
-    outbox = jnp.zeros((bands * capacity, D), jnp.bfloat16).at[places_out].set(encoded)
-    labels = jnp.full((bands * capacity,), -1, jnp.int32).at[places_out].set(slot[0])
-    arrived, arrived_ids = (
-        lax.all_to_all(
-            outbox.reshape(bands, capacity, D), "space", split_axis=0, concat_axis=0, tiled=True
-        ),
-        lax.all_to_all(
-            labels.reshape(bands, capacity), "space", split_axis=0, concat_axis=0, tiled=True
-        ),
+    poster = (
+        jnp.arange(bands * capacity, dtype=jnp.int32)[:, None] == places_out[None, :]
+    ).astype(jnp.bfloat16)
+    spots = slot[0][None, :]
+    columns = jnp.concatenate(
+        [
+            state_in,
+            (spots // 64).astype(jnp.bfloat16),
+            (spots % 64).astype(jnp.bfloat16),
+            jnp.ones((1, points), jnp.bfloat16),
+            jnp.zeros((HALF - CH - 3, points), jnp.bfloat16),
+        ],
+        0,
     )
-    chooser = (
-        arrived_ids.reshape(-1)[:, None] == jnp.arange(blocks, dtype=jnp.int32)[None, :]
-    ).astype(jnp.bfloat16)
-    gathered = inner(chooser, arrived.reshape(-1, D), 0, 0).astype(jnp.bfloat16)
+
+    def exchanged(rows):
+        return lax.all_to_all(
+            rows.reshape(bands, capacity, HALF), "space", split_axis=0, concat_axis=0, tiled=True
+        ).reshape(bands * capacity, HALF)
+
+    arrived = exchanged(inner(poster, columns, 1, 1).astype(jnp.bfloat16))
+    w_in, w_node, w_dec, w_out, w_round, biases = spread_rows(
+        gathered_blocks(piece.reshape(height, D)), total_size, peers, place
+    )
+    w_out = jnp.pad(w_out.reshape(D, CH), ((0, 0), (0, HALF - CH)))
+    w_round = w_round.reshape(ROUNDS, 5, D, D)
+    b_head = biases[:3]
+    b_round = biases[3:].reshape(ROUNDS, 2, D)
+    count = summed_everywhere(jnp.full((8, HALF), jnp.sum(counted)))[0, 0]
+    ids = arrived[:, CH : CH + 3].astype(jnp.int32)
+    ids = jnp.where(ids[:, 2:3] > 0, ids[:, 0:1] * 64 + ids[:, 1:2], -1)
+    chooser = (ids == jnp.arange(blocks, dtype=jnp.int32)[None, :]).astype(jnp.bfloat16)
+    enc_in = inner(arrived, w_in, 1, 0) + b_head[0]
+    encoded = silu(enc_in).astype(jnp.bfloat16)
+    gathered = inner(chooser, encoded, 0, 0).astype(jnp.bfloat16)
     node_in = inner(gathered, w_node, 1, 0) + b_head[1]
-    mesh = jax.nn.silu(node_in)
+    mesh = silu(node_in)
     index = ((neighbours - band * blocks + H) % (blocks * bands)).T.reshape(-1)
     kept = []
     sent = inner(mesh.astype(jnp.bfloat16), w_round[0, 0], 1, 0).astype(jnp.bfloat16)
@@ -455,14 +572,12 @@
         kept.append((mesh, edges, uin, agg))
         mesh = new
         sent = rest[0] if rest else None
-    reply = inner(chooser, mesh.astype(jnp.bfloat16), 1, 0).astype(jnp.bfloat16)
-    returned = lax.all_to_all(
-        reply.reshape(bands, capacity, D), "space", split_axis=0, concat_axis=0, tiled=True
-    )
-    fetched = returned.reshape(-1, D)[places_out]
+    fetched = inner(chooser, mesh.astype(jnp.bfloat16), 1, 0).astype(jnp.bfloat16)
     dec_in = inner(fetched, w_dec, 1, 0) + b_head[2]
-    decoded = jax.nn.silu(dec_in).astype(jnp.bfloat16)
-    err = state_in.astype(jnp.float32) + inner(w_out, decoded, 0, 1) - wanted
+    decoded = silu(dec_in).astype(jnp.bfloat16)
+    returned = exchanged(inner(decoded, w_out, 1, 0).astype(jnp.bfloat16))
+    branch = inner(returned, poster, 0, 0)[:CH]
+    err = state_in.astype(jnp.float32) + branch - targets[0].astype(jnp.float32)
     head_err, head_valid = (
         shifted(err[:, :ROWW].astype(jnp.bfloat16), "space", -1).astype(jnp.float32),
         shifted(counted[:, :ROWW].astype(jnp.bfloat16), "space", -1).astype(jnp.float32),
@@ -478,7 +593,6 @@
         valid_far = jnp.where(pick, wide_valid[:, by : by + points], valid_far)
     gap = err - err_far
     local_total = jnp.sum(counted * err * err) + 0.5 * jnp.sum(counted * valid_far * gap * gap)
-    total = lax.psum(local_total, ALL)
     paired = counted * valid_far * gap / count
     grad_err = 2.0 * counted * err / count + paired
     grad_wide = jnp.zeros(wide_err.shape, jnp.float32)
@@ -491,17 +605,14 @@
     grad_pred = (
         grad_err - stays + grad_wide[:, :points] + jnp.pad(carried, ((0, 0), (0, points - ROWW)))
     )
-    grad_branch = grad_pred.astype(jnp.bfloat16)
-    grad_wout = inner(decoded, grad_branch, 0, 1)
-    grad_dec = (inner(grad_branch, w_out, 0, 1) * slope(dec_in)).astype(jnp.bfloat16)
+    grad_rows = jnp.pad(grad_pred.astype(jnp.bfloat16), ((0, HALF - CH), (0, 0)))
+    landed = exchanged(inner(poster, grad_rows, 1, 1).astype(jnp.bfloat16))
+    grad_wout = inner(decoded, landed, 0, 0)[:, :CH]
+    grad_dec = (inner(landed, w_out, 1, 1) * slope(dec_in)).astype(jnp.bfloat16)
     grad_bdec = jnp.sum(grad_dec.astype(jnp.float32), 0)
     grad_wdec = inner(fetched, grad_dec, 0, 0)
     grad_fetched = inner(grad_dec, w_dec, 1, 1).astype(jnp.bfloat16)
-    backbox = jnp.zeros((bands * capacity, D), jnp.bfloat16).at[places_out].set(grad_fetched)
-    landed = lax.all_to_all(
-        backbox.reshape(bands, capacity, D), "space", split_axis=0, concat_axis=0, tiled=True
-    )
-    grad_mesh = inner(chooser, landed.reshape(-1, D), 0, 0)
+    grad_mesh = inner(chooser, grad_fetched, 0, 0)
     mats_grads = [None] * (5 * ROUNDS)
     bias_grads = [None] * (2 * ROUNDS)
     for layer in reversed(range(ROUNDS)):
@@ -532,23 +643,18 @@
     grad_bnode = jnp.sum(grad_node.astype(jnp.float32), 0)
     grad_wnode = inner(gathered, grad_node, 0, 0)
     grad_gathered = inner(grad_node, w_node, 1, 1).astype(jnp.bfloat16)
-    sendback = inner(chooser, grad_gathered, 1, 0).astype(jnp.bfloat16)
-    homeward = lax.all_to_all(
-        sendback.reshape(bands, capacity, D), "space", split_axis=0, concat_axis=0, tiled=True
-    )
-    grad_encoded = homeward.reshape(-1, D)[places_out].astype(jnp.float32)
+    grad_encoded = inner(chooser, grad_gathered, 1, 0)
     grad_enc = (grad_encoded * slope(enc_in)).astype(jnp.bfloat16)
     grad_bin = jnp.sum(grad_enc.astype(jnp.float32), 0)
-    grad_win = inner(state_in, grad_enc, 1, 0)
+    grad_win = inner(arrived, grad_enc, 0, 0)
     parts = [grad_win, grad_wnode, grad_wdec, grad_wout.reshape(CH, D)]
     parts = parts + mats_grads
     parts.append(jnp.concatenate([jnp.stack([grad_bin, grad_bnode, grad_bdec])] + bias_grads, 0))
-    packed = collect_rows(parts, total_size, peers)
-    summed = lax.psum_scatter(
-        packed.reshape(peers * height, D), ALL, scatter_dimension=0, tiled=True
-    )
-    mine = lax.dynamic_slice_in_dim(summed.reshape(-1), offset, shard)
-    norm = jnp.sqrt(lax.psum(jnp.sum(mine * mine), ALL))
+    mine = reduced_piece(*collect_rows(parts, total_size, peers, place))
+    mine = lax.dynamic_slice_in_dim(mine.reshape(-1), offset, shard)
+    lane = lax.broadcasted_iota(jnp.int32, (8, HALF), 1)
+    sums = summed_everywhere(jnp.where(lane == 0, local_total, jnp.sum(mine * mine)))
+    total, norm = sums[0, 0], jnp.sqrt(sums[0, 1])
     clipped = mine * jnp.minimum(1.0, 0.05 / norm)
     first = 0.9 * moment1 + 0.1 * clipped
     second = 0.999 * moment2 + 0.001 * clipped * clipped

time: 920 us -> 709 us (0.77)
  waiting for transfers between devices: 418 us -> 266 us
  blocking collectives: 82.4 us -> 15.2 us
  starting transfers between devices: 68.7 us -> 92.2 us
  local copies, waits for them, and re-layouts: 41.7 us -> 24.9 us
  between operations: 18.2 us -> 5.28 us
    reduce_scatter x1 -> x0, waiting for transfers between devices: 103 us -> none  [shards(): lax.psum_scatter(packed.reshape(peers * height, D), ALL, scatter_dimensio...]
    psum x2 -> x0, blocking collectives: 82.4 us -> none  [the longest x1 41.6 us: shards(): count = lax.psum(jnp.sum(counted), ALL)]
    all_gather x1 -> x0, waiting for transfers between devices: 46.6 us -> none  [shards(): lax.all_gather(piece.reshape(height, D), ALL, axis=0, tiled=True)]
    ppermute x0 -> x29, waiting for transfers between devices: none -> 45.5 us  [swapped(): lax.ppermute(value, axis, [(i, i ^ bit) for i in range(lax.axis_size(axis...]
    all_to_all x5 -> x2, waiting for transfers between devices: 44.1 us -> 0.01 us  [exchanged(): lax.all_to_all(rows.reshape(bands, capacity, HALF), 'space', split_axis=0...]
    ppermute x0 -> x29, starting transfers between devices: none -> 43.7 us  [swapped(): lax.ppermute(value, axis, [(i, i ^ bit) for i in range(lax.axis_size(axis...]
    all_to_all x5 -> x2, starting transfers between devices: 33.2 us -> 11.7 us  [exchanged(): lax.all_to_all(rows.reshape(bands, capacity, HALF), 'space', split_axis=0...]
    all_to_all x0 -> x1, blocking collectives: none -> 15.2 us  [exchanged(): lax.all_to_all(rows.reshape(bands, capacity, HALF), 'space', split_axis=0...]
  transfers between devices with their start and end apart: 22 -> 46, of which waited for: 19 -> 33; matrix products, arithmetic and copies ran while one was open for 6% -> 7% of each run, Pallas kernels for 0% -> 4%
where the time goes in v2:
time: 709 us; the launch traced here: 698 us
  waiting for transfers between devices  266 us (38%)
  Pallas kernels  217 us (31%)
  starting transfers between devices  92.2 us (13%)
  matrix products  53.8 us (8%)
  local copies, waits for them, and re-layouts  24.9 us (4%)
  other arithmetic  24.2 us (3%)
  blocking collectives  15.2 us (2%)
    ppermute x6, waiting for transfers between devices, halo(): lax.ppermute(last, 'space', up)  155 us
    pallas_call x3, Pallas kernels, edges_backward(): pl.pallas_call(body, grid_spec=pltpu.PrefetchScalarGridSpec(num_scalar_pr...  99 us
    ppermute x6, waiting for transfers between devices, halo(): lax.ppermute(initial, 'space', down)  61.3 us
    dot_general x31, matrix products, inner(): lax.dot_general(left, right, (((left_dim,), (right_dim,)), ((), ())), pre...  53.4 us
    pallas_call x3, Pallas kernels, gather_rows(): pl.pallas_call(body, grid_spec=pltpu.PrefetchScalarGridSpec(num_scalar_pr...  48.2 us
    ppermute x29, waiting for transfers between devices, swapped(): lax.ppermute(value, axis, [(i, i ^ bit) for i in range(lax.axis_size(axis...  45.5 us
    ppermute x29, starting transfers between devices, swapped(): lax.ppermute(value, axis, [(i, i ^ bit) for i in range(lax.axis_size(axis...  43.7 us
    pallas_call x3, Pallas kernels, round_forward(): pl.pallas_call(body, grid=(blocks // tile,), in_specs=ins, out_specs=outs...  34.8 us
  transfers between devices with their start and end apart: 46, of which 33 were waited for; matrix products, arithmetic and copies ran while one was open for 7% of the time, Pallas kernels for 4%

profile of v2, /device:TPU:0, one launch (start us, length us, event | category | flops | bytes accessed | tf_op | source)
XLA Modules:
  0.0 698.3 jit_solution(2694734730581028526)
XLA Ops:
  2.5 4.1 collective-permute-start
  14.0 7.2 %all-to-all-start = ((bf16[16,64,128]{2,1,0:T(8,128)(2,1)}), bf16[16,64,128]{2,1,0:T(8,128)(2,1)S(1)}, u32[]{:S(2)}, u32[]{:S(2)}) async-start(bf16[16,64,128]{2,1,0:T(8,128)(2,1)} %bitcast.5), calls=%async_computation | async-start | bytes 524288 | tf_op jit(solution)/shard_map/all_to_all | solution.py:537
  23.4 6.0 collective-permute-done.1
  32.4 3.7 collective-permute-done.6
  38.4 4.4 collective-permute-done.7
  46.6 4.2 spread_rows.1
  61.1 4.2 collective-permute-start.11
  73.8 14.4 %collective-permute-done.11 = bf16[4096,128]{1,0:T(8,128)(2,1)S(1)} collective-permute-done((bf16[4096,128]{1,0:T(8,128)(2,1)}, bf16[4096,128]{1,0:T(8,128)(2,1)S(1)}, u32[]{:S(2)}, u32[]{:S(2)}) %collective-permute-start.11) | collective-permute-done | bytes 1048608 | tf_op jit(solution)/shard_map/ppermute | solution.py:54
  88.3 21.4 %collective-permute-done.10 = bf16[4096,128]{1,0:T(8,128)(2,1)} collective-permute-done((bf16[4096,128]{1,0:T(8,128)(2,1)}, bf16[4096,128]{1,0:T(8,128)(2,1)}, u32[]{:S(2)}, u32[]{:S(2)}) %collective-permute-start.10) | collective-permute-done | bytes 1048608 | tf_op jit(solution)/shard_map/ppermute | solution.py:54
  109.6 16.1 %gather_rows.3 = bf16[12288,2,128]{2,1,0:T(2,128)(2,1)} custom-call(s32[12288]{0:T(1024)} %reshape.196.index_ref, bf16[2048,2,128]{2,1,0:T(2,128)(2,1)} %bitcast.13.before_ref, bf16[2048,2,128]{2,1,0:T(2,128)(2,1)} %copy.52.own_ref, bf16[2048,2,128]{2,1,0:T(2,128)(2,1)} %bitcast.205), custom_call_target="tpu_custom_call" | custom-call | tf_op jit(solution)/shard_map/gather_rows/pallas_call | solution.py:266
  125.7 11.8 %round_forward.3 = (f32[2048,256]{1,0:T(8,128)}, f32[2048,256]{1,0:T(8,128)}, bf16[2048,256]{1,0:T(8,128)(2,1)}, bf16[4096,128]{1,0:T(8,128)(2,1)}) custom-call(f32[2048,256]{1,0:T(8,128)} %get-tuple-element.135.refs_0_.mesh_ref, bf16[6,4096,128]{2,1,0:T(8,128)(2,1)} %bitcast.177, bf16[5,256,256]{2,1,0:T(8,128)(2,1)} %bitcast.183, ...), custom_call_target="tpu_custom_call" | custom-call | tf_op jit(solution)/shard_map/round_forward/pallas_call | solution.py:350
  137.5 3.9 collective-permute-start.13
  141.8 22.3 %collective-permute-done.13 = bf16[4096,128]{1,0:T(8,128)(2,1)S(1)} collective-permute-done((bf16[4096,128]{1,0:T(8,128)(2,1)}, bf16[4096,128]{1,0:T(8,128)(2,1)S(1)}, u32[]{:S(2)}, u32[]{:S(2)}) %collective-permute-start.13) | collective-permute-done | bytes 1048608 | tf_op jit(solution)/shard_map/ppermute | solution.py:54
  164.2 20.7 %collective-permute-done.12 = bf16[4096,128]{1,0:T(8,128)(2,1)S(1)} collective-permute-done((bf16[4096,128]{1,0:T(8,128)(2,1)}, bf16[4096,128]{1,0:T(8,128)(2,1)S(1)}, u32[]{:S(2)}, u32[]{:S(2)}) %collective-permute-start.12) | collective-permute-done | bytes 1048608 | tf_op jit(solution)/shard_map/ppermute | solution.py:54
  185.8 16.1 %gather_rows.4 = bf16[12288,2,128]{2,1,0:T(2,128)(2,1)} custom-call(s32[12288]{0:T(1024)} %reshape.196.index_ref, bf16[2048,2,128]{2,1,0:T(2,128)(2,1)} %bitcast.210, bf16[2048,2,128]{2,1,0:T(2,128)(2,1)} %bitcast.207, bf16[2048,2,128]{2,1,0:T(2,128)(2,1)} %bitcast.209), custom_call_target="tpu_custom_call" | custom-call | tf_op jit(solution)/shard_map/gather_rows/pallas_call | solution.py:266
  201.9 11.8 %round_forward.4 = (f32[2048,256]{1,0:T(8,128)}, f32[2048,256]{1,0:T(8,128)}, bf16[2048,256]{1,0:T(8,128)(2,1)}, bf16[4096,128]{1,0:T(8,128)(2,1)}) custom-call(f32[2048,256]{1,0:T(8,128)} %get-tuple-element.54.refs_0_.mesh_ref, bf16[6,4096,128]{2,1,0:T(8,128)(2,1)} %bitcast.179, bf16[5,256,256]{2,1,0:T(8,128)(2,1)} %bitcast.186, ...), custom_call_target="tpu_custom_call" | custom-call | tf_op jit(solution)/shard_map/round_forward/pallas_call | solution.py:350
  213.7 5.1 collective-permute-start.15
  220.4 19.8 %collective-permute-done.15 = bf16[4096,128]{1,0:T(8,128)(2,1)S(1)} collective-permute-done((bf16[4096,128]{1,0:T(8,128)(2,1)}, bf16[4096,128]{1,0:T(8,128)(2,1)S(1)}, u32[]{:S(2)}, u32[]{:S(2)}) %collective-permute-start.15) | collective-permute-done | bytes 1048608 | tf_op jit(solution)/shard_map/ppermute | solution.py:54
  240.3 22.3 %collective-permute-done.14 = bf16[4096,128]{1,0:T(8,128)(2,1)} collective-permute-done((bf16[4096,128]{1,0:T(8,128)(2,1)}, bf16[4096,128]{1,0:T(8,128)(2,1)}, u32[]{:S(2)}, u32[]{:S(2)}) %collective-permute-start.14) | collective-permute-done | bytes 1048608 | tf_op jit(solution)/shard_map/ppermute | solution.py:54
  262.6 16.1 %gather_rows.5 = bf16[12288,2,128]{2,1,0:T(2,128)(2,1)} custom-call(s32[12288]{0:T(1024)} %reshape.196.index_ref, bf16[2048,2,128]{2,1,0:T(2,128)(2,1)} %bitcast.25.before_ref, bf16[2048,2,128]{2,1,0:T(2,128)(2,1)} %bitcast.206, bf16[2048,2,128]{2,1,0:T(2,128)(2,1)} %bitcast.208), custom_call_target="tpu_custom_call" | custom-call | tf_op jit(solution)/shard_map/gather_rows/pallas_call | solution.py:266
  278.7 11.2 %round_forward.5 = (f32[2048,256]{1,0:T(8,128)}, f32[2048,256]{1,0:T(8,128)}, bf16[2048,256]{1,0:T(8,128)(2,1)}) custom-call(f32[2048,256]{1,0:T(8,128)} %get-tuple-element.56.refs_0_.mesh_ref, bf16[6,4096,128]{2,1,0:T(8,128)(2,1)} %bitcast.181, bf16[5,256,256]{2,1,0:T(8,128)(2,1)} %bitcast.189, f32[2,256]{1,0:T(2,128)} %get-tuple-element.150.refs_3_.bias_ref), custom_call_target="tpu_custom_call" | custom-call | tf_op jit(solution)/shard_map/round_forward/pallas_call | solution.py:350
  289.9 3.2 fusion.16
  294.5 4.5 all-to-all-start.1
  312.3 4.7 collective-permute-start.22
  326.5 3.1 collective-permute-start.23
  333.9 15.2 %all_to_all.15 = bf16[16,64,128]{2,1,0:T(8,128)(2,1)S(1)} all-to-all(bf16[16,64,128]{2,1,0:T(8,128)(2,1)S(1)} %bitcast.216), channel_id=1, replica_groups=mesh['dp'=2,'space'=16] {'space'}, dimensions={0} | all-to-all | bytes 524288 | tf_op jit(solution)/shard_map/all_to_all | solution.py:537
  352.5 4.9 fusion.1.grad_ref
  357.4 33.0 %edges_backward.3 = (bf16[2048,256]{1,0:T(8,128)(2,1)}, bf16[2048,256]{1,0:T(8,128)(2,1)}, bf16[4096,128]{1,0:T(8,128)(2,1)}, f32[4096,128]{1,0:T(8,128)}, bf16[4096,128]{1,0:T(8,128)(2,1)}) custom-call(s32[12288]{0:T(1024)} %reshape.196.index_ref, f32[2048,256]{1,0:T(8,128)} %fusion.1.grad_ref, f32[2048,256]{1,0:T(8,128)} %get-tuple-element.56.refs_0_.mesh_ref, ...), custom_call_target="tpu_custom_call" | custom-call | tf_op jit(solution)/shard_map/edges_backward/pallas_call | solution.py:429
  391.9 4.4 collective-permute-start.25
  405.5 24.7 %collective-permute-done.24.first_ref = bf16[4096,128]{1,0:T(8,128)(2,1)} collective-permute-done((bf16[4096,128]{1,0:T(8,128)(2,1)}, bf16[4096,128]{1,0:T(8,128)(2,1)}, u32[]{:S(2)}, u32[]{:S(2)}) %collective-permute-start.24) | collective-permute-done | bytes 1048608 | tf_op jit(solution)/shard_map/ppermute | solution.py:54
  431.4 8.5 %round_backward.3 = (f32[2048,256]{1,0:T(8,128)}, bf16[2048,256]{1,0:T(8,128)(2,1)}) custom-call(f32[2048,256]{1,0:T(8,128)} %fusion.1.grad_ref, f32[4096,128]{1,0:T(8,128)} %get-tuple-element.62.own_ref, bf16[4096,128]{1,0:T(8,128)(2,1)} %collective-permute-done.24.first_ref, bf16[4096,128]{1,0:T(8,128)(2,1)} %collective-permute-done.25.last_ref, ...), custom_call_target="tpu_custom_call" | custom-call | tf_op jit(solution)/shard_map/round_backward/pallas_call | solution.py:484
  439.9 33.2 %edges_backward.4 = (bf16[2048,256]{1,0:T(8,128)(2,1)}, bf16[2048,256]{1,0:T(8,128)(2,1)}, bf16[4096,128]{1,0:T(8,128)(2,1)}, f32[4096,128]{1,0:T(8,128)}, bf16[4096,128]{1,0:T(8,128)(2,1)}) custom-call(s32[12288]{0:T(1024)} %reshape.196.index_ref, f32[2048,256]{1,0:T(8,128)} %get-tuple-element.67.grad_ref, f32[2048,256]{1,0:T(8,128)} %get-tuple-element.54.refs_0_.mesh_ref, ...), custom_call_target="tpu_custom_call" | custom-call | tf_op jit(solution)/shard_map/edges_backward/pallas_call | solution.py:429
  477.0 4.6 collective-permute-start.27
  487.5 32.3 %collective-permute-done.26.first_ref = bf16[4096,128]{1,0:T(8,128)(2,1)} collective-permute-done((bf16[4096,128]{1,0:T(8,128)(2,1)}, bf16[4096,128]{1,0:T(8,128)(2,1)}, u32[]{:S(2)}, u32[]{:S(2)}) %collective-permute-start.26) | collective-permute-done | bytes 1048608 | tf_op jit(solution)/shard_map/ppermute | solution.py:54
  522.3 8.5 %round_backward.4 = (f32[2048,256]{1,0:T(8,128)}, bf16[2048,256]{1,0:T(8,128)(2,1)}) custom-call(f32[2048,256]{1,0:T(8,128)} %get-tuple-element.67.grad_ref, f32[4096,128]{1,0:T(8,128)} %get-tuple-element.69.own_ref, bf16[4096,128]{1,0:T(8,128)(2,1)} %collective-permute-done.26.first_ref, bf16[4096,128]{1,0:T(8,128)(2,1)} %collective-permute-done.27.last_ref, ...), custom_call_target="tpu_custom_call" | custom-call | tf_op jit(solution)/shard_map/round_backward/pallas_call | solution.py:484
  530.8 32.9 %edges_backward.5 = (bf16[2048,256]{1,0:T(8,128)(2,1)}, bf16[2048,256]{1,0:T(8,128)(2,1)}, bf16[4096,128]{1,0:T(8,128)(2,1)}, f32[4096,128]{1,0:T(8,128)}, bf16[4096,128]{1,0:T(8,128)(2,1)}) custom-call(s32[12288]{0:T(1024)} %reshape.196.index_ref, f32[2048,256]{1,0:T(8,128)} %get-tuple-element.74.grad_ref, f32[2048,256]{1,0:T(8,128)} %get-tuple-element.135.refs_0_.mesh_ref, ...), custom_call_target="tpu_custom_call" | custom-call | tf_op jit(solution)/shard_map/edges_backward/pallas_call | solution.py:429
  567.8 5.6 collective-permute-start.29
  578.6 33.5 %collective-permute-done.28.first_ref = bf16[4096,128]{1,0:T(8,128)(2,1)S(1)} collective-permute-done((bf16[4096,128]{1,0:T(8,128)(2,1)S(1)}, bf16[4096,128]{1,0:T(8,128)(2,1)S(1)}, u32[]{:S(2)}, u32[]{:S(2)}) %collective-permute-start.28) | collective-permute-done | bytes 1048608 | tf_op jit(solution)/shard_map/ppermute | solution.py:54
  614.1 8.6 %round_backward.5 = (f32[2048,256]{1,0:T(8,128)}, bf16[2048,256]{1,0:T(8,128)(2,1)}) custom-call(f32[2048,256]{1,0:T(8,128)} %get-tuple-element.74.grad_ref, f32[4096,128]{1,0:T(8,128)} %get-tuple-element.76.own_ref, bf16[4096,128]{1,0:T(8,128)(2,1)} %copy-done.19, bf16[4096,128]{1,0:T(8,128)(2,1)} %copy-done.21, ...), custom_call_target="tpu_custom_call" | custom-call | tf_op jit(solution)/shard_map/round_backward/pallas_call | solution.py:484
  627.0 4.2 convert_reduce_fusion.8
  635.9 5.0 collect_rows.1
  640.9 3.0 collective-permute-done.30
  650.6 4.7 collective-permute-done.31
  655.4 3.1 collective-permute-start.32
  667.4 3.6 collective-permute-start.34
  673.0 3.3 collective-permute-done.38
  679.5 3.1 collective-permute-done.40
  686.6 3.3 collective-permute-done.42
  (321 shorter events, 147.7 us)
Async XLA Ops:
  2.5 18.7 %collective-permute-start = (bf16[1,72,256]{2,1,0:T(8,128)(2,1)S(1)}, bf16[1,72,256]{2,1,0:T(8,128)(2,1)S(1)}, u32[]{:S(2)}, u32[]{:S(2)}) collective-permute-start(bf16[1,72,256]{2,1,0:T(8,128)(2,1)S(1)} %slice.219), channel_id=1, source_target_pairs={{0,8},{1,9},{2,10},{3,11},{4,12},{5,13},{6,14},{7,15},{8,0},{9,1},... | collective-permute-start | bytes 110600 | tf_op jit(solution)/shard_map/ppermute | solution.py:71
  6.6 16.6 %collective-permute-start.4 = (bf16[1,72,256]{2,1,0:T(8,128)(2,1)S(1)}, bf16[1,72,256]{2,1,0:T(8,128)(2,1)S(1)}, u32[]{:S(2)}, u32[]{:S(2)}) collective-permute-start(bf16[1,72,256]{2,1,0:T(8,128)(2,1)S(1)} %slice.221), channel_id=1, source_target_pairs={{0,8},{1,9},{2,10},{3,11},{4,12},{5,13},{6,14},{7,15},{8,0},{9,1},... | collective-permute-start | bytes 110600 | tf_op jit(solution)/shard_map/ppermute | solution.py:71
  14.0 29.8 %all-to-all-start = ((bf16[16,64,128]{2,1,0:T(8,128)(2,1)}), bf16[16,64,128]{2,1,0:T(8,128)(2,1)S(1)}, u32[]{:S(2)}, u32[]{:S(2)}) async-start(bf16[16,64,128]{2,1,0:T(8,128)(2,1)} %bitcast.5), calls=%async_computation | async-start | bytes 524288 | tf_op jit(solution)/shard_map/all_to_all | solution.py:537
  21.2 8.1 %collective-permute-start.1 = (bf16[2,72,256]{2,1,0:T(8,128)(2,1)S(1)}, bf16[2,72,256]{2,1,0:T(8,128)(2,1)S(1)}, u32[]{:S(2)}, u32[]{:S(2)}) collective-permute-start(bf16[2,72,256]{2,1,0:T(8,128)(2,1)S(1)} %pad_maximum_fusion.6), channel_id=1, source_target_pairs={{0,4},{1,5},{2,6},{3,7},{4,0},{5,1},{6,2},{7,3},{8,12},{9,13},{10,... | collective-permute-start | bytes 221192 | tf_op jit(solution)/shard_map/ppermute | solution.py:71
  23.2 7.6 %collective-permute-start.5 = (bf16[2,72,256]{2,1,0:T(8,128)(2,1)S(1)}, bf16[2,72,256]{2,1,0:T(8,128)(2,1)S(1)}, u32[]{:S(2)}, u32[]{:S(2)}) collective-permute-start(bf16[2,72,256]{2,1,0:T(8,128)(2,1)S(1)} %pad_maximum_fusion.7), channel_id=1, source_target_pairs={{0,4},{1,5},{2,6},{3,7},{4,0},{5,1},{6,2},{7,3},{8,12},{9,13},{10,... | collective-permute-start | bytes 221192 | tf_op jit(solution)/shard_map/ppermute | solution.py:71
  29.4 7.5 %collective-permute-start.2 = (bf16[4,72,256]{2,1,0:T(8,128)(2,1)S(1)}, bf16[4,72,256]{2,1,0:T(8,128)(2,1)S(1)}, u32[]{:S(2)}, u32[]{:S(2)}) collective-permute-start(bf16[4,72,256]{2,1,0:T(8,128)(2,1)S(1)} %pad_maximum_fusion.4), channel_id=1, source_target_pairs={{0,2},{1,3},{2,0},{3,1},{4,6},{5,7},{6,4},{7,5},{8,10},{9,11},{10,... | collective-permute-start | bytes 442376 | tf_op jit(solution)/shard_map/ppermute | solution.py:71
  30.8 5.2 collective-permute-start.6
  36.1 6.8 collective-permute-start.7
  36.9 6.8 collective-permute-start.3
  42.9 2.1 collective-permute-start.9
  43.7 2.1 collective-permute-start.8
  44.4 245.5 %copy-start.54 = (s32[1024]{0:T(1024)}, s32[1024]{0:T(1024)S(1)}, u32[]{:S(2)}) copy-start(s32[1024]{0:T(1024)S(1)} %fusion.37) | copy-start | bytes 12292
  61.1 27.2 %collective-permute-start.11 = (bf16[4096,128]{1,0:T(8,128)(2,1)}, bf16[4096,128]{1,0:T(8,128)(2,1)S(1)}, u32[]{:S(2)}, u32[]{:S(2)}) collective-permute-start(bf16[4096,128]{1,0:T(8,128)(2,1)} %reshape.198), channel_id=1, source_target_pairs={{1,0},{2,1},{3,2},{4,3},{5,4},{6,5},{7,6},{8,7},{9,8},{10,9},{11,1... | collective-permute-start | bytes 3145736 | tf_op jit(solution)/shard_map/ppermute | solution.py:54
  65.2 44.4 %collective-permute-start.10 = (bf16[4096,128]{1,0:T(8,128)(2,1)}, bf16[4096,128]{1,0:T(8,128)(2,1)}, u32[]{:S(2)}, u32[]{:S(2)}) collective-permute-start(bf16[4096,128]{1,0:T(8,128)(2,1)} %reshape.198), channel_id=1, source_target_pairs={{0,1},{1,2},{2,3},{3,4},{4,5},{5,6},{6,7},{7,8},{8,9},{9,10},{10,1... | collective-permute-start | bytes 3145736 | tf_op jit(solution)/shard_map/ppermute | solution.py:54
  137.5 26.7 %collective-permute-start.13 = (bf16[4096,128]{1,0:T(8,128)(2,1)}, bf16[4096,128]{1,0:T(8,128)(2,1)S(1)}, u32[]{:S(2)}, u32[]{:S(2)}) collective-permute-start(bf16[4096,128]{1,0:T(8,128)(2,1)} %get-tuple-element.55), channel_id=1, source_target_pairs={{1,0},{2,1},{3,2},{4,3},{5,4},{6,5},{7,6},{8,7},{9,8},{10,9},{11,1... | collective-permute-start | bytes 3145736 | tf_op jit(solution)/shard_map/ppermute | solution.py:54
  141.4 43.5 %collective-permute-start.12 = (bf16[4096,128]{1,0:T(8,128)(2,1)}, bf16[4096,128]{1,0:T(8,128)(2,1)S(1)}, u32[]{:S(2)}, u32[]{:S(2)}) collective-permute-start(bf16[4096,128]{1,0:T(8,128)(2,1)} %get-tuple-element.55), channel_id=1, source_target_pairs={{0,1},{1,2},{2,3},{3,4},{4,5},{5,6},{6,7},{7,8},{8,9},{9,10},{10,1... | collective-permute-start | bytes 3145736 | tf_op jit(solution)/shard_map/ppermute | solution.py:54
  213.7 26.5 %collective-permute-start.15 = (bf16[4096,128]{1,0:T(8,128)(2,1)}, bf16[4096,128]{1,0:T(8,128)(2,1)S(1)}, u32[]{:S(2)}, u32[]{:S(2)}) collective-permute-start(bf16[4096,128]{1,0:T(8,128)(2,1)} %get-tuple-element.57), channel_id=1, source_target_pairs={{1,0},{2,1},{3,2},{4,3},{5,4},{6,5},{7,6},{8,7},{9,8},{10,9},{11,1... | collective-permute-start | bytes 3145736 | tf_op jit(solution)/shard_map/ppermute | solution.py:54
  218.8 43.8 %collective-permute-start.14 = (bf16[4096,128]{1,0:T(8,128)(2,1)}, bf16[4096,128]{1,0:T(8,128)(2,1)}, u32[]{:S(2)}, u32[]{:S(2)}) collective-permute-start(bf16[4096,128]{1,0:T(8,128)(2,1)} %get-tuple-element.57), channel_id=1, source_target_pairs={{0,1},{1,2},{2,3},{3,4},{4,5},{5,6},{6,7},{7,8},{8,9},{9,10},{10,1... | collective-permute-start | bytes 3145736 | tf_op jit(solution)/shard_map/ppermute | solution.py:54
  220.1 78.9 %collective-permute-start.18 = (f32[8,128]{1,0:T(8,128)S(1)}, f32[8,128]{1,0:T(8,128)S(1)}, u32[]{:S(2)}, u32[]{:S(2)}) collective-permute-start(f32[8,128]{1,0:T(8,128)S(1)} %broadcast_in_dim.114), channel_id=1, source_target_pairs={{0,16},{16,0},{1,17},{17,1},{2,18},{18,2},{3,19},{19,3},{4,20},{20... | collective-permute-start | bytes 12296 | tf_op jit(solution)/shard_map/ppermute | solution.py:71
  220.4 73.0 %copy-start.48 = (bf16[256,78]{1,0:T(8,128)(2,1)}, bf16[256,78]{1,0:T(8,128)(2,1)S(1)}, u32[]{:S(2)}) copy-start(bf16[256,78]{1,0:T(8,128)(2,1)S(1)} %reshape.210) | copy-start | bytes 119812
  294.5 22.5 %all-to-all-start.1 = ((bf16[16,64,128]{2,1,0:T(8,128)(2,1)}), bf16[16,64,128]{2,1,0:T(8,128)(2,1)S(1)}, u32[]{:S(2)}, u32[]{:S(2)}) async-start(bf16[16,64,128]{2,1,0:T(8,128)(2,1)} %bitcast.213), calls=%async_computation.1 | async-start | bytes 524288 | tf_op jit(solution)/shard_map/all_to_all | solution.py:537
  299.7 3.7 collective-permute-start.19
  304.0 3.9 collective-permute-start.20
  307.9 3.7 collective-permute-start.21
  310.3 11.4 %collective-permute-start.16 = (bf16[78,360]{1,0:T(8,128)(2,1)}, bf16[78,360]{1,0:T(8,128)(2,1)}, u32[]{:S(2)}, u32[]{:S(2)}) collective-permute-start(bf16[78,360]{1,0:T(8,128)(2,1)} %slice.424), channel_id=1, source_target_pairs={{1,0},{2,1},{3,2},{4,3},{5,4},{6,5},{7,6},{8,7},{9,8},{10,9},{11,1... | collective-permute-start | bytes 168488 | tf_op jit(solution)/shard_map/ppermute | solution.py:47
  312.3 8.1 %collective-permute-start.22 = (f32[8,128]{1,0:T(8,128)S(1)}, f32[8,128]{1,0:T(8,128)}, u32[]{:S(2)}, u32[]{:S(2)}) collective-permute-start(f32[8,128]{1,0:T(8,128)S(1)} %add.225), channel_id=1, source_target_pairs={{0,8},{1,9},{2,10},{3,11},{4,12},{5,13},{6,14},{7,15},{8,0},{9,1},... | collective-permute-start | bytes 12296 | tf_op jit(solution)/shard_map/ppermute | solution.py:71
  318.4 6.1 collective-permute-start.17
  326.5 4.9 collective-permute-start.23
  390.4 39.8 %collective-permute-start.24 = (bf16[4096,128]{1,0:T(8,128)(2,1)}, bf16[4096,128]{1,0:T(8,128)(2,1)}, u32[]{:S(2)}, u32[]{:S(2)}) collective-permute-start(bf16[4096,128]{1,0:T(8,128)(2,1)} %get-tuple-element.63), channel_id=1, source_target_pairs={{0,1},{1,2},{2,3},{3,4},{4,5},{5,6},{6,7},{7,8},{8,9},{9,10},{10,1... | collective-permute-start | bytes 3145736 | tf_op jit(solution)/shard_map/ppermute | solution.py:54
  391.9 39.5 %collective-permute-start.25 = (bf16[4096,128]{1,0:T(8,128)(2,1)}, bf16[4096,128]{1,0:T(8,128)(2,1)}, u32[]{:S(2)}, u32[]{:S(2)}) collective-permute-start(bf16[4096,128]{1,0:T(8,128)(2,1)} %get-tuple-element.64), channel_id=1, source_target_pairs={{1,0},{2,1},{3,2},{4,3},{5,4},{6,5},{7,6},{8,7},{9,8},{10,9},{11,1... | collective-permute-start | bytes 3145736 | tf_op jit(solution)/shard_map/ppermute | solution.py:54
  475.7 44.1 %collective-permute-start.26 = (bf16[4096,128]{1,0:T(8,128)(2,1)}, bf16[4096,128]{1,0:T(8,128)(2,1)}, u32[]{:S(2)}, u32[]{:S(2)}) collective-permute-start(bf16[4096,128]{1,0:T(8,128)(2,1)} %get-tuple-element.70), channel_id=1, source_target_pairs={{0,1},{1,2},{2,3},{3,4},{4,5},{5,6},{6,7},{7,8},{8,9},{9,10},{10,1... | collective-permute-start | bytes 3145736 | tf_op jit(solution)/shard_map/ppermute | solution.py:54
  477.0 45.3 %collective-permute-start.27 = (bf16[4096,128]{1,0:T(8,128)(2,1)S(1)}, bf16[4096,128]{1,0:T(8,128)(2,1)}, u32[]{:S(2)}, u32[]{:S(2)}) collective-permute-start(bf16[4096,128]{1,0:T(8,128)(2,1)S(1)} %copy-done.62), channel_id=1, source_target_pairs={{1,0},{2,1},{3,2},{4,3},{5,4},{6,5},{7,6},{8,7},{9,8},{10,9},{11,1... | collective-permute-start | bytes 3145736 | tf_op jit(solution)/shard_map/ppermute | solution.py:54
  567.5 44.6 %collective-permute-start.28 = (bf16[4096,128]{1,0:T(8,128)(2,1)S(1)}, bf16[4096,128]{1,0:T(8,128)(2,1)S(1)}, u32[]{:S(2)}, u32[]{:S(2)}) collective-permute-start(bf16[4096,128]{1,0:T(8,128)(2,1)S(1)} %copy-done.63), channel_id=1, source_target_pairs={{0,1},{1,2},{2,3},{3,4},{4,5},{5,6},{6,7},{7,8},{8,9},{9,10},{10,1... | collective-permute-start | bytes 3145736 | tf_op jit(solution)/shard_map/ppermute | solution.py:54
  567.8 45.3 %collective-permute-start.29 = (bf16[4096,128]{1,0:T(8,128)(2,1)S(1)}, bf16[4096,128]{1,0:T(8,128)(2,1)S(1)}, u32[]{:S(2)}, u32[]{:S(2)}) collective-permute-start(bf16[4096,128]{1,0:T(8,128)(2,1)S(1)} %copy-done.61), channel_id=1, source_target_pairs={{1,0},{2,1},{3,2},{4,3},{5,4},{6,5},{7,6},{8,7},{9,8},{10,9},{11,1... | collective-permute-start | bytes 3145736 | tf_op jit(solution)/shard_map/ppermute | solution.py:54
  640.9 3.1 collective-permute-start.30
  646.1 9.2 %collective-permute-start.31 = (bf16[2,2,2,72,256]{4,3,0,1,2:T(8,128)(2,1)S(1)}, bf16[2,2,2,72,256]{4,3,0,1,2:T(8,128)(2,1)S(1)}, u32[]{:S(2)}, u32[]{:S(2)}) collective-permute-start(bf16[2,2,2,72,256]{4,3,0,1,2:T(8,128)(2,1)S(1)} %fusion.40), channel_id=1, source_target_pairs={{0,1},{1,0},{2,3},{3,2},{4,5},{5,4},{6,7},{7,6},{8,9},{9,8},{10,11... | collective-permute-start | bytes 884744 | tf_op jit(solution)/shard_map/ppermute | solution.py:71
  649.2 9.3 %collective-permute-start.35 = (bf16[2,2,2,72,256]{4,3,2,1,0:T(8,128)(2,1)S(1)}, bf16[2,2,2,72,256]{4,3,2,1,0:T(8,128)(2,1)S(1)}, u32[]{:S(2)}, u32[]{:S(2)}) collective-permute-start(bf16[2,2,2,72,256]{4,3,2,1,0:T(8,128)(2,1)S(1)} %fusion.39), channel_id=1, source_target_pairs={{0,2},{1,3},{2,0},{3,1},{4,6},{5,7},{6,4},{7,5},{8,10},{9,11},{10,... | collective-permute-start | bytes 884744 | tf_op jit(solution)/shard_map/ppermute | solution.py:71
  655.4 6.5 collective-permute-start.32
  658.6 6.0 collective-permute-start.36
  661.9 5.5 collective-permute-start.33
  664.7 6.2 collective-permute-start.37
  667.4 5.6 collective-permute-start.34
  671.0 5.3 collective-permute-start.38
  677.8 1.2 collective-permute-start.39
  679.0 3.6 collective-permute-start.40
  682.6 3.6 collective-permute-start.41
  686.3 3.6 collective-permute-start.42
  689.9 4.5 collective-permute-start.43
  (62 other events, 549.9 us)

commit v3 on v2

--- a/solution.py
+++ b/solution.py
@@ -1,4 +1,4 @@
-import math
+import functools
 
 import jax
 import jax.numpy as jnp
@@ -47,9 +47,30 @@
     return lax.ppermute(shard, axis, pairs)
 
 
-def halo(last, initial):
-    peers = lax.axis_size("space")
-    up = [(i, (i + 1) % peers) for i in range(peers)]
+def walk_of(mesh):
+    count = mesh.shape["space"]
+    chips = [getattr(device, "coords", None) for device in mesh.devices[0].reshape(-1)]
+    if any(chip is None for chip in chips) or len(set(map(tuple, chips))) != count:
+        return list(range(count))
+    at = {tuple(chip): n for n, chip in enumerate(chips)}
+    xs, ys, zs = (sorted({chip[n] for chip in at}) for n in range(3))
+    if len(xs) * len(ys) * len(zs) != count:
+        return list(range(count))
+    if (len(xs), len(ys), len(zs)) == (2, 2, 4):
+        corners = [(0, 0), (1, 0), (0, 1), (1, 1)]
+        planes = [(0, 1, 3, 2), (2, 0, 1, 3), (3, 1, 0, 2), (2, 3, 1, 0)]
+        steps = [(*corners[n], z) for z, plane in enumerate(planes) for n in plane]
+        return [at[(xs[x], ys[y], zs[z])] for x, y, z in steps]
+    walk, plane = [], []
+    for n, y in enumerate(ys):
+        plane = plane + [(x, y) for x in (xs if n % 2 == 0 else xs[::-1])]
+    for n, z in enumerate(zs):
+        walk = walk + [at[(x, y, z)] for x, y in (plane if n % 2 == 0 else plane[::-1])]
+    return walk
+
+
+def halo(walk, last, initial):
+    up = list(zip(walk, walk[1:] + walk[:1]))
     down = [(j, i) for i, j in up]
     return lax.ppermute(last, "space", up), lax.ppermute(initial, "space", down)
 
@@ -496,7 +517,7 @@
     )(grad_mesh, own, first, last, grad_uin, dest_low, mats)
 
 
-def shards(master, moment1, moment2, inputs, targets, valid, owner, slot, neighbours, partner):
+def shards(walk, master, moment1, moment2, inputs, targets, valid, owner, slot, neighbours, partner):
     bands = lax.axis_size("space")
     band = lax.axis_index("space")
     peers = lax.axis_size(ALL)
@@ -517,7 +538,7 @@
     target_band = owner[0, :, 0]
     hits = (target_band[:, None] == jnp.arange(bands, dtype=jnp.int32)[None, :]).astype(jnp.int32)
     ranks = jnp.sum(jnp.cumsum(hits, 0) * hits, 1) - 1
-    places_out = target_band * capacity + ranks
+    places_out = jnp.sum(hits * jnp.asarray(walk, jnp.int32)[None, :], 1) * capacity + ranks
     poster = (
         jnp.arange(bands * capacity, dtype=jnp.int32)[:, None] == places_out[None, :]
     ).astype(jnp.bfloat16)
@@ -553,14 +574,17 @@
     enc_in = inner(arrived, w_in, 1, 0) + b_head[0]
     encoded = silu(enc_in).astype(jnp.bfloat16)
     gathered = inner(chooser, encoded, 0, 0).astype(jnp.bfloat16)
+    gathered, count = lax.optimization_barrier((gathered, count))
     node_in = inner(gathered, w_node, 1, 0) + b_head[1]
     mesh = silu(node_in)
     index = ((neighbours - band * blocks + H) % (blocks * bands)).T.reshape(-1)
+    index = lax.ppermute(index, "space", list(enumerate(walk)))
+    home = [(place, n) for n, place in enumerate(walk)]
     kept = []
     sent = inner(mesh.astype(jnp.bfloat16), w_round[0, 0], 1, 0).astype(jnp.bfloat16)
     sent = sent.reshape(2 * blocks, HALF)
     for layer in range(ROUNDS):
-        before, after = halo(sent[2 * (blocks - H) :], sent[: 2 * H])
+        before, after = halo(walk, sent[2 * (blocks - H) :], sent[: 2 * H])
         edges = gather_rows(
             index,
             before.reshape(H, 2, HALF),
@@ -613,6 +637,8 @@
     grad_wdec = inner(fetched, grad_dec, 0, 0)
     grad_fetched = inner(grad_dec, w_dec, 1, 1).astype(jnp.bfloat16)
     grad_mesh = inner(chooser, grad_fetched, 0, 0)
+    grad_mesh, leaving = lax.optimization_barrier((grad_mesh, mesh.astype(jnp.bfloat16)))
+    final_mesh = lax.ppermute(leaving, "space", home).astype(jnp.float32)
     mats_grads = [None] * (5 * ROUNDS)
     bias_grads = [None] * (2 * ROUNDS)
     for layer in reversed(range(ROUNDS)):
@@ -621,7 +647,7 @@
         grad_uin, dest_low, to_before, own, to_after = edges_backward(
             index, grad_mesh, old, uin, edges, mats, b_round[layer]
         )
-        from_before, from_after = halo(to_after, to_before)
+        from_before, from_after = halo(walk, to_after, to_before)
         lowered = old.astype(jnp.bfloat16)
         grad_out = grad_mesh.astype(jnp.bfloat16)
         update = silu(uin).astype(jnp.bfloat16)
@@ -639,6 +665,7 @@
         )
         grads[0] = inner(lowered, sent_low, 0, 0)
         mats_grads[5 * layer : 5 * layer + 5] = grads
+    node_grads = lax.ppermute(grad_mesh.astype(jnp.bfloat16), "space", home).astype(jnp.float32)
     grad_node = (grad_mesh * slope(node_in)).astype(jnp.bfloat16)
     grad_bnode = jnp.sum(grad_node.astype(jnp.float32), 0)
     grad_wnode = inner(gathered, grad_node, 0, 0)
@@ -669,15 +696,15 @@
         first,
         second,
         updated.astype(jnp.bfloat16),
-        mesh.reshape(1, blocks, D),
-        grad_mesh.reshape(1, blocks, D),
+        final_mesh.reshape(1, blocks, D),
+        node_grads.reshape(1, blocks, D),
         grad_pred.reshape(1, grad_pred.shape[0], points),
     )
 
 
 def solution(mesh):
     return jax.shard_map(
-        shards,
+        functools.partial(shards, walk_of(mesh)),
         mesh=mesh,
         in_specs=(
             P(("dp", "space")),

time: 709 us -> 608 us (0.86)
  waiting for transfers between devices: 266 us -> 126 us
  starting transfers between devices: 92.2 us -> 125 us
    ppermute x6, waiting for transfers between devices: 155 us -> 27 us  [halo(): lax.ppermute(last, 'space', up)]
    ppermute x29, starting transfers between devices: 43.7 us -> 83.3 us  [swapped(): lax.ppermute(value, axis, [(i, i ^ bit) for i in range(lax.axis_size(axis...]
    ppermute x6, waiting for transfers between devices: 61.3 us -> 45 us  [halo(): lax.ppermute(initial, 'space', down)]
    ppermute x6, starting transfers between devices: 27.7 us -> 14.5 us  [halo(): lax.ppermute(initial, 'space', down)]
  transfers between devices with their start and end apart: 46 -> 49, of which waited for: 33 -> 29; matrix products, arithmetic and copies ran while one was open for 7% -> 8% of each run, Pallas kernels for 4% -> 0%
where the time goes in v3:
time: 608 us; the launch traced here: 597 us
  Pallas kernels  217 us (36%)
  waiting for transfers between devices  126 us (21%)
  starting transfers between devices  125 us (21%)
  matrix products  52.3 us (9%)
  other arithmetic  30.3 us (5%)
  local copies, waits for them, and re-layouts  27.7 us (5%)
  blocking collectives  13.9 us (2%)
    pallas_call x3, Pallas kernels, edges_backward(): pl.pallas_call(body, grid_spec=pltpu.PrefetchScalarGridSpec(num_scalar_pr...  99.1 us
    ppermute x29, starting transfers between devices, swapped(): lax.ppermute(value, axis, [(i, i ^ bit) for i in range(lax.axis_size(axis...  83.3 us
    dot_general x31, matrix products, inner(): lax.dot_general(left, right, (((left_dim,), (right_dim,)), ((), ())), pre...  51.9 us
    pallas_call x3, Pallas kernels, gather_rows(): pl.pallas_call(body, grid_spec=pltpu.PrefetchScalarGridSpec(num_scalar_pr...  48.2 us
    ppermute x6, waiting for transfers between devices, halo(): lax.ppermute(initial, 'space', down)  45 us
    ppermute x29, waiting for transfers between devices, swapped(): lax.ppermute(value, axis, [(i, i ^ bit) for i in range(lax.axis_size(axis...  41.5 us
    pallas_call x3, Pallas kernels, round_forward(): pl.pallas_call(body, grid=(blocks // tile,), in_specs=ins, out_specs=outs...  34.7 us
    ppermute x6, waiting for transfers between devices, halo(): lax.ppermute(last, 'space', up)  27 us
  transfers between devices with their start and end apart: 49, of which 29 were waited for; matrix products, arithmetic and copies ran while one was open for 8% of the time, Pallas kernels for 0%

profile of v3, /device:TPU:0, one launch (start us, length us, event | category | flops | bytes accessed | tf_op | source)
XLA Modules:
  0.0 597.0 jit_solution(11129297384048553667)
XLA Ops:
  5.2 3.7 collective-permute-start
  15.6 7.2 %all-to-all-start = ((bf16[16,64,128]{2,1,0:T(8,128)(2,1)}), bf16[16,64,128]{2,1,0:T(8,128)(2,1)S(1)}, u32[]{:S(2)}, u32[]{:S(2)}) async-start(bf16[16,64,128]{2,1,0:T(8,128)(2,1)} %bitcast.5), calls=%async_computation | async-start | bytes 524288 | tf_op jit(solution)/shard_map/all_to_all | solution.py:558
  27.7 4.0 collective-permute-done.1
  34.9 3.7 collective-permute-done.6
  41.1 4.7 collective-permute-done.7
  48.5 2.6 collective-permute-done.12
  51.2 3.5 collective-permute-done.13
  56.6 2.6 collective-permute-done.14
  61.5 4.1 spread_rows.1
  70.7 2.7 fusion.102
  83.4 2.9 fusion.109
  89.7 9.1 %collective-permute-done.17 = bf16[4096,128]{1,0:T(8,128)(2,1)S(1)} collective-permute-done((bf16[4096,128]{1,0:T(8,128)(2,1)}, bf16[4096,128]{1,0:T(8,128)(2,1)S(1)}, u32[]{:S(2)}, u32[]{:S(2)}) %collective-permute-start.17) | collective-permute-done | bytes 1048608 | tf_op jit(solution)/shard_map/ppermute | solution.py:75
  98.8 3.9 collective-permute-done.16
  102.7 16.1 %gather_rows.3 = bf16[12288,2,128]{2,1,0:T(2,128)(2,1)} custom-call(s32[12288]{0:T(1024)} %copy-done.18, bf16[2048,2,128]{2,1,0:T(2,128)(2,1)} %bitcast.14.before_ref, bf16[2048,2,128]{2,1,0:T(2,128)(2,1)} %copy.53.own_ref, bf16[2048,2,128]{2,1,0:T(2,128)(2,1)} %bitcast.209), custom_call_target="tpu_custom_call" | custom-call | tf_op jit(solution)/shard_map/gather_rows/pallas_call | solution.py:287
  118.8 11.8 %round_forward.3 = (f32[2048,256]{1,0:T(8,128)}, f32[2048,256]{1,0:T(8,128)}, bf16[2048,256]{1,0:T(8,128)(2,1)}, bf16[4096,128]{1,0:T(8,128)(2,1)}) custom-call(f32[2048,256]{1,0:T(8,128)} %get-tuple-element.146.refs_0_.mesh_ref, bf16[6,4096,128]{2,1,0:T(8,128)(2,1)} %bitcast.182, bf16[5,256,256]{2,1,0:T(8,128)(2,1)} %bitcast.188, ...), custom_call_target="tpu_custom_call" | custom-call | tf_op jit(solution)/shard_map/round_forward/pallas_call | solution.py:371
  133.0 18.6 %collective-permute-done.19 = bf16[4096,128]{1,0:T(8,128)(2,1)S(1)} collective-permute-done((bf16[4096,128]{1,0:T(8,128)(2,1)}, bf16[4096,128]{1,0:T(8,128)(2,1)S(1)}, u32[]{:S(2)}, u32[]{:S(2)}) %collective-permute-start.19) | collective-permute-done | bytes 1048608 | tf_op jit(solution)/shard_map/ppermute | solution.py:75
  151.6 3.4 collective-permute-done.18
  156.0 16.1 %gather_rows.4 = bf16[12288,2,128]{2,1,0:T(2,128)(2,1)} custom-call(s32[12288]{0:T(1024)} %copy-done.18, bf16[2048,2,128]{2,1,0:T(2,128)(2,1)} %bitcast.215, bf16[2048,2,128]{2,1,0:T(2,128)(2,1)} %bitcast.211, bf16[2048,2,128]{2,1,0:T(2,128)(2,1)} %bitcast.213), custom_call_target="tpu_custom_call" | custom-call | tf_op jit(solution)/shard_map/gather_rows/pallas_call | solution.py:287
  172.1 11.8 %round_forward.4 = (f32[2048,256]{1,0:T(8,128)}, f32[2048,256]{1,0:T(8,128)}, bf16[2048,256]{1,0:T(8,128)(2,1)}, bf16[4096,128]{1,0:T(8,128)(2,1)}) custom-call(f32[2048,256]{1,0:T(8,128)} %get-tuple-element.59.refs_0_.mesh_ref, bf16[6,4096,128]{2,1,0:T(8,128)(2,1)} %bitcast.184, bf16[5,256,256]{2,1,0:T(8,128)(2,1)} %bitcast.191, ...), custom_call_target="tpu_custom_call" | custom-call | tf_op jit(solution)/shard_map/round_forward/pallas_call | solution.py:371
  186.7 17.3 %collective-permute-done.21 = bf16[4096,128]{1,0:T(8,128)(2,1)S(1)} collective-permute-done((bf16[4096,128]{1,0:T(8,128)(2,1)}, bf16[4096,128]{1,0:T(8,128)(2,1)S(1)}, u32[]{:S(2)}, u32[]{:S(2)}) %collective-permute-start.21) | collective-permute-done | bytes 1048608 | tf_op jit(solution)/shard_map/ppermute | solution.py:75
  206.9 16.1 %gather_rows.5 = bf16[12288,2,128]{2,1,0:T(2,128)(2,1)} custom-call(s32[12288]{0:T(1024)} %copy-done.18, bf16[2048,2,128]{2,1,0:T(2,128)(2,1)} %bitcast.214, bf16[2048,2,128]{2,1,0:T(2,128)(2,1)} %bitcast.210, bf16[2048,2,128]{2,1,0:T(2,128)(2,1)} %bitcast.212), custom_call_target="tpu_custom_call" | custom-call | tf_op jit(solution)/shard_map/gather_rows/pallas_call | solution.py:287
  223.0 11.2 %round_forward.5 = (f32[2048,256]{1,0:T(8,128)}, f32[2048,256]{1,0:T(8,128)}, bf16[2048,256]{1,0:T(8,128)(2,1)}) custom-call(f32[2048,256]{1,0:T(8,128)} %get-tuple-element.61.refs_0_.mesh_ref, bf16[6,4096,128]{2,1,0:T(8,128)(2,1)} %bitcast.186, bf16[5,256,256]{2,1,0:T(8,128)(2,1)} %bitcast.194, f32[2,256]{1,0:T(2,128)} %get-tuple-element.161.refs_3_.bias_ref), custom_call_target="tpu_custom_call" | custom-call | tf_op jit(solution)/shard_map/round_forward/pallas_call | solution.py:371
  238.9 3.5 all-to-all-start.1
  244.4 6.5 %all-to-all-done.1 = bf16[16,64,128]{2,1,0:T(8,128)(2,1)S(1)} async-done(((bf16[16,64,128]{2,1,0:T(8,128)(2,1)}), bf16[16,64,128]{2,1,0:T(8,128)(2,1)S(1)}, u32[]{:S(2)}, u32[]{:S(2)}) %all-to-all-start.1) | async-done | bytes 262176 | tf_op jit(solution)/shard_map/all_to_all | solution.py:558
  255.2 3.8 collective-permute-done.23
  261.0 3.9 collective-permute-start.24
  269.2 13.9 %all_to_all.15 = bf16[16,64,128]{2,1,0:T(8,128)(2,1)S(1)} all-to-all(bf16[16,64,128]{2,1,0:T(8,128)(2,1)S(1)} %bitcast.221), channel_id=1, replica_groups=mesh['dp'=2,'space'=16] {'space'}, dimensions={0} | all-to-all | bytes 524288 | tf_op jit(solution)/shard_map/all_to_all | solution.py:558
  286.4 4.9 fusion.1.grad_ref
  291.4 33.1 %edges_backward.3 = (bf16[2048,256]{1,0:T(8,128)(2,1)}, bf16[2048,256]{1,0:T(8,128)(2,1)}, bf16[4096,128]{1,0:T(8,128)(2,1)}, f32[4096,128]{1,0:T(8,128)}, bf16[4096,128]{1,0:T(8,128)(2,1)}) custom-call(s32[12288]{0:T(1024)} %copy-done.18, f32[2048,256]{1,0:T(8,128)} %fusion.1.grad_ref, f32[2048,256]{1,0:T(8,128)} %get-tuple-element.61.refs_0_.mesh_ref, ...), custom_call_target="tpu_custom_call" | custom-call | tf_op jit(solution)/shard_map/edges_backward/pallas_call | solution.py:450
  337.7 3.7 collective-permute-done.25.first_ref
  341.4 8.5 %round_backward.3 = (f32[2048,256]{1,0:T(8,128)}, bf16[2048,256]{1,0:T(8,128)(2,1)}) custom-call(f32[2048,256]{1,0:T(8,128)} %fusion.1.grad_ref, f32[4096,128]{1,0:T(8,128)} %get-tuple-element.69.own_ref, bf16[4096,128]{1,0:T(8,128)(2,1)} %collective-permute-done.25.first_ref, bf16[4096,128]{1,0:T(8,128)(2,1)} %collective-permute-done.26.last_ref, ...), custom_call_target="tpu_custom_call" | custom-call | tf_op jit(solution)/shard_map/round_backward/pallas_call | solution.py:505
  350.0 33.1 %edges_backward.4 = (bf16[2048,256]{1,0:T(8,128)(2,1)}, bf16[2048,256]{1,0:T(8,128)(2,1)}, bf16[4096,128]{1,0:T(8,128)(2,1)}, f32[4096,128]{1,0:T(8,128)}, bf16[4096,128]{1,0:T(8,128)(2,1)}) custom-call(s32[12288]{0:T(1024)} %copy-done.18, f32[2048,256]{1,0:T(8,128)} %get-tuple-element.74.grad_ref, f32[2048,256]{1,0:T(8,128)} %get-tuple-element.59.refs_0_.mesh_ref, ...), custom_call_target="tpu_custom_call" | custom-call | tf_op jit(solution)/shard_map/edges_backward/pallas_call | solution.py:450
  385.7 4.2 collective-permute-start.28
  395.9 6.9 %collective-permute-done.27.first_ref = bf16[4096,128]{1,0:T(8,128)(2,1)} collective-permute-done((bf16[4096,128]{1,0:T(8,128)(2,1)}, bf16[4096,128]{1,0:T(8,128)(2,1)}, u32[]{:S(2)}, u32[]{:S(2)}) %collective-permute-start.27) | collective-permute-done | bytes 1048608 | tf_op jit(solution)/shard_map/ppermute | solution.py:75
  402.8 8.5 %round_backward.4 = (f32[2048,256]{1,0:T(8,128)}, bf16[2048,256]{1,0:T(8,128)(2,1)}) custom-call(f32[2048,256]{1,0:T(8,128)} %get-tuple-element.74.grad_ref, f32[4096,128]{1,0:T(8,128)} %get-tuple-element.76.own_ref, bf16[4096,128]{1,0:T(8,128)(2,1)} %collective-permute-done.27.first_ref, bf16[4096,128]{1,0:T(8,128)(2,1)} %collective-permute-done.28.last_ref, ...), custom_call_target="tpu_custom_call" | custom-call | tf_op jit(solution)/shard_map/round_backward/pallas_call | solution.py:505
  411.4 32.9 %edges_backward.5 = (bf16[2048,256]{1,0:T(8,128)(2,1)}, bf16[2048,256]{1,0:T(8,128)(2,1)}, bf16[4096,128]{1,0:T(8,128)(2,1)}, f32[4096,128]{1,0:T(8,128)}, bf16[4096,128]{1,0:T(8,128)(2,1)}) custom-call(s32[12288]{0:T(1024)} %copy-done.18, f32[2048,256]{1,0:T(8,128)} %get-tuple-element.81.grad_ref, f32[2048,256]{1,0:T(8,128)} %get-tuple-element.146.refs_0_.mesh_ref, ...), custom_call_target="tpu_custom_call" | custom-call | tf_op jit(solution)/shard_map/edges_backward/pallas_call | solution.py:450
  448.1 4.2 collective-permute-start.30
  457.5 7.1 %collective-permute-done.29.first_ref = bf16[4096,128]{1,0:T(8,128)(2,1)S(1)} collective-permute-done((bf16[4096,128]{1,0:T(8,128)(2,1)S(1)}, bf16[4096,128]{1,0:T(8,128)(2,1)S(1)}, u32[]{:S(2)}, u32[]{:S(2)}) %collective-permute-start.29) | collective-permute-done | bytes 1048608 | tf_op jit(solution)/shard_map/ppermute | solution.py:75
  466.0 8.6 %round_backward.5 = (f32[2048,256]{1,0:T(8,128)}, bf16[2048,256]{1,0:T(8,128)(2,1)}) custom-call(f32[2048,256]{1,0:T(8,128)} %get-tuple-element.81.grad_ref, f32[4096,128]{1,0:T(8,128)} %get-tuple-element.83.own_ref, bf16[4096,128]{1,0:T(8,128)(2,1)} %copy-done.22, bf16[4096,128]{1,0:T(8,128)(2,1)} %copy-done.23, ...), custom_call_target="tpu_custom_call" | custom-call | tf_op jit(solution)/shard_map/round_backward/pallas_call | solution.py:505
  474.6 4.6 convert_reduce_fusion.6
  480.5 4.2 convert_reduce_fusion.8
  489.4 5.1 collect_rows.1
  494.5 3.0 collective-permute-done.31
  508.9 5.8 collective-permute-done.36
  517.1 42.9 %collective-permute-start.34 = (bf16[2,72,256]{2,1,0:T(8,128)(2,1)S(1)}, bf16[2,72,256]{2,1,0:T(8,128)(2,1)S(1)}, u32[]{:S(2)}, u32[]{:S(2)}) collective-permute-start(bf16[2,72,256]{2,1,0:T(8,128)(2,1)S(1)} %fusion.68), channel_id=1, source_target_pairs={{0,4},{1,5},{2,6},{3,7},{4,0},{5,1},{6,2},{7,3},{8,12},{9,13},{10,... | collective-permute-start | bytes 221192 | tf_op jit(solution)/shard_map/ppermute | solution.py:92
  560.0 2.7 collective-permute-start.38
  562.8 6.4 %collective-permute-start.35 = (bf16[72,256]{1,0:T(8,128)(2,1)S(1)}, bf16[72,256]{1,0:T(8,128)(2,1)S(1)}, u32[]{:S(2)}, u32[]{:S(2)}) collective-permute-start(bf16[72,256]{1,0:T(8,128)(2,1)S(1)} %fusion.76), channel_id=1, source_target_pairs={{0,8},{1,9},{2,10},{3,11},{4,12},{5,13},{6,14},{7,15},{8,0},{9,1},... | collective-permute-start | bytes 110600 | tf_op jit(solution)/shard_map/ppermute | solution.py:92
  577.6 2.9 collective-permute-done.41
  (332 shorter events, 149.6 us)
Async XLA Ops:
  2.9 20.0 %collective-permute-start.10 = (f32[8,128]{1,0:T(8,128)S(1)}, f32[8,128]{1,0:T(8,128)S(1)}, u32[]{:S(2)}, u32[]{:S(2)}) collective-permute-start(f32[8,128]{1,0:T(8,128)S(1)} %broadcast_in_dim.111), channel_id=1, source_target_pairs={{0,16},{16,0},{1,17},{17,1},{2,18},{18,2},{3,19},{19,3},{4,20},{20... | collective-permute-start | bytes 12296 | tf_op jit(solution)/shard_map/ppermute | solution.py:92
  5.2 20.3 %collective-permute-start = (bf16[1,72,256]{2,1,0:T(8,128)(2,1)S(1)}, bf16[1,72,256]{2,1,0:T(8,128)(2,1)S(1)}, u32[]{:S(2)}, u32[]{:S(2)}) collective-permute-start(bf16[1,72,256]{2,1,0:T(8,128)(2,1)S(1)} %slice.219), channel_id=1, source_target_pairs={{0,8},{1,9},{2,10},{3,11},{4,12},{5,13},{6,14},{7,15},{8,0},{9,1},... | collective-permute-start | bytes 110600 | tf_op jit(solution)/shard_map/ppermute | solution.py:92
  8.9 18.1 %collective-permute-start.4 = (bf16[1,72,256]{2,1,0:T(8,128)(2,1)S(1)}, bf16[1,72,256]{2,1,0:T(8,128)(2,1)S(1)}, u32[]{:S(2)}, u32[]{:S(2)}) collective-permute-start(bf16[1,72,256]{2,1,0:T(8,128)(2,1)S(1)} %slice.221), channel_id=1, source_target_pairs={{0,8},{1,9},{2,10},{3,11},{4,12},{5,13},{6,14},{7,15},{8,0},{9,1},... | collective-permute-start | bytes 110600 | tf_op jit(solution)/shard_map/ppermute | solution.py:92
  15.6 44.2 %all-to-all-start = ((bf16[16,64,128]{2,1,0:T(8,128)(2,1)}), bf16[16,64,128]{2,1,0:T(8,128)(2,1)S(1)}, u32[]{:S(2)}, u32[]{:S(2)}) async-start(bf16[16,64,128]{2,1,0:T(8,128)(2,1)} %bitcast.5), calls=%async_computation | async-start | bytes 524288 | tf_op jit(solution)/shard_map/all_to_all | solution.py:558
  23.5 23.3 %collective-permute-start.11 = (f32[8,128]{1,0:T(8,128)S(1)}, f32[8,128]{1,0:T(8,128)S(1)}, u32[]{:S(2)}, u32[]{:S(2)}) collective-permute-start(f32[8,128]{1,0:T(8,128)S(1)} %broadcast_add_fusion.1), channel_id=1, source_target_pairs={{0,1},{1,0},{2,3},{3,2},{4,5},{5,4},{6,7},{7,6},{8,9},{9,8},{10,11... | collective-permute-start | bytes 12296 | tf_op jit(solution)/shard_map/ppermute | solution.py:92
  25.5 6.2 %collective-permute-start.1 = (bf16[2,72,256]{2,1,0:T(8,128)(2,1)S(1)}, bf16[2,72,256]{2,1,0:T(8,128)(2,1)S(1)}, u32[]{:S(2)}, u32[]{:S(2)}) collective-permute-start(bf16[2,72,256]{2,1,0:T(8,128)(2,1)S(1)} %pad_maximum_fusion.6), channel_id=1, source_target_pairs={{0,4},{1,5},{2,6},{3,7},{4,0},{5,1},{6,2},{7,3},{8,12},{9,13},{10,... | collective-permute-start | bytes 221192 | tf_op jit(solution)/shard_map/ppermute | solution.py:92
  27.0 6.3 %collective-permute-start.5 = (bf16[2,72,256]{2,1,0:T(8,128)(2,1)S(1)}, bf16[2,72,256]{2,1,0:T(8,128)(2,1)S(1)}, u32[]{:S(2)}, u32[]{:S(2)}) collective-permute-start(bf16[2,72,256]{2,1,0:T(8,128)(2,1)S(1)} %pad_maximum_fusion.7), channel_id=1, source_target_pairs={{0,4},{1,5},{2,6},{3,7},{4,0},{5,1},{6,2},{7,3},{8,12},{9,13},{10,... | collective-permute-start | bytes 221192 | tf_op jit(solution)/shard_map/ppermute | solution.py:92
  31.7 7.9 %collective-permute-start.2 = (bf16[4,72,256]{2,1,0:T(8,128)(2,1)S(1)}, bf16[4,72,256]{2,1,0:T(8,128)(2,1)S(1)}, u32[]{:S(2)}, u32[]{:S(2)}) collective-permute-start(bf16[4,72,256]{2,1,0:T(8,128)(2,1)S(1)} %pad_maximum_fusion.4), channel_id=1, source_target_pairs={{0,2},{1,3},{2,0},{3,1},{4,6},{5,7},{6,4},{7,5},{8,10},{9,11},{10,... | collective-permute-start | bytes 442376 | tf_op jit(solution)/shard_map/ppermute | solution.py:92
  33.4 5.2 collective-permute-start.6
  38.6 7.2 %collective-permute-start.7 = (bf16[8,72,256]{2,1,0:T(8,128)(2,1)S(1)}, bf16[8,72,256]{2,1,0:T(8,128)(2,1)S(1)}, u32[]{:S(2)}, u32[]{:S(2)}) collective-permute-start(bf16[8,72,256]{2,1,0:T(8,128)(2,1)S(1)} %pad_maximum_fusion.1), channel_id=1, source_target_pairs={{0,2},{1,3},{2,0},{3,1},{4,6},{5,7},{6,4},{7,5},{8,10},{9,11},{10,... | collective-permute-start | bytes 884744 | tf_op jit(solution)/shard_map/ppermute | solution.py:92
  39.6 7.0 %collective-permute-start.3 = (bf16[8,72,256]{2,1,0:T(8,128)(2,1)S(1)}, bf16[8,72,256]{2,1,0:T(8,128)(2,1)S(1)}, u32[]{:S(2)}, u32[]{:S(2)}) collective-permute-start(bf16[8,72,256]{2,1,0:T(8,128)(2,1)S(1)} %pad_maximum_fusion), channel_id=1, source_target_pairs={{0,1},{1,0},{2,3},{3,2},{4,5},{5,4},{6,7},{7,6},{8,9},{9,8},{10,11... | collective-permute-start | bytes 884744 | tf_op jit(solution)/shard_map/ppermute | solution.py:92
  45.8 14.6 %collective-permute-start.9 = (bf16[16,72,256]{2,1,0:T(8,128)(2,1)S(1)}, bf16[16,72,256]{2,1,0:T(8,128)(2,1)S(1)}, u32[]{:S(2)}, u32[]{:S(2)}) collective-permute-start(bf16[16,72,256]{2,1,0:T(8,128)(2,1)S(1)} %constant_dynamic-update-slice_fusion.5.refs_1_), channel_id=1, source_target_pairs={{0,16},{16,0},{1,17},{17,1},{2,18},{18,2},{3,19},{19,3},{4,20},{20... | collective-permute-start | bytes 1769480 | tf_op jit(solution)/shard_map/ppermute | solution.py:92
  46.7 13.8 %collective-permute-start.8 = (bf16[16,72,256]{2,1,0:T(8,128)(2,1)S(1)}, bf16[16,72,256]{2,1,0:T(8,128)(2,1)S(1)}, u32[]{:S(2)}, u32[]{:S(2)}) collective-permute-start(bf16[16,72,256]{2,1,0:T(8,128)(2,1)S(1)} %constant_dynamic-update-slice_fusion.refs_0_), channel_id=1, source_target_pairs={{0,16},{16,0},{1,17},{17,1},{2,18},{18,2},{3,19},{19,3},{4,20},{20... | collective-permute-start | bytes 1769480 | tf_op jit(solution)/shard_map/ppermute | solution.py:92
  47.5 3.7 collective-permute-start.12
  51.1 3.6 collective-permute-start.13
  54.7 4.5 collective-permute-start.14
  76.5 22.3 %collective-permute-start.17 = (bf16[4096,128]{1,0:T(8,128)(2,1)}, bf16[4096,128]{1,0:T(8,128)(2,1)S(1)}, u32[]{:S(2)}, u32[]{:S(2)}) collective-permute-start(bf16[4096,128]{1,0:T(8,128)(2,1)} %reshape.206), channel_id=1, source_target_pairs={{1,0},{3,1},{2,3},{6,2},{4,6},{5,4},{7,5},{11,7},{9,11},{8,9},{10,... | collective-permute-start | bytes 3145736 | tf_op jit(solution)/shard_map/ppermute | solution.py:75
  78.8 23.9 %collective-permute-start.16 = (bf16[4096,128]{1,0:T(8,128)(2,1)}, bf16[4096,128]{1,0:T(8,128)(2,1)}, u32[]{:S(2)}, u32[]{:S(2)}) collective-permute-start(bf16[4096,128]{1,0:T(8,128)(2,1)} %reshape.206), channel_id=1, source_target_pairs={{0,1},{1,3},{3,2},{2,6},{6,4},{4,5},{5,7},{7,11},{11,9},{9,8},{8,1... | collective-permute-start | bytes 3145736 | tf_op jit(solution)/shard_map/ppermute | solution.py:75
  80.3 9.4 %collective-permute-start.15 = (s32[12288]{0:T(1024)}, s32[12288]{0:T(1024)S(1)}, u32[]{:S(2)}, u32[]{:S(2)}) collective-permute-start(s32[12288]{0:T(1024)} %reshape.204), channel_id=1, source_target_pairs={{0,0},{1,1},{2,3},{3,2},{4,6},{5,4},{6,5},{7,7},{8,11},{9,9},{10,8... | collective-permute-start | bytes 147464 | tf_op jit(solution)/shard_map/ppermute | solution.py:581
  130.5 21.1 %collective-permute-start.19 = (bf16[4096,128]{1,0:T(8,128)(2,1)}, bf16[4096,128]{1,0:T(8,128)(2,1)S(1)}, u32[]{:S(2)}, u32[]{:S(2)}) collective-permute-start(bf16[4096,128]{1,0:T(8,128)(2,1)} %get-tuple-element.60), channel_id=1, source_target_pairs={{1,0},{3,1},{2,3},{6,2},{4,6},{5,4},{7,5},{11,7},{9,11},{8,9},{10,... | collective-permute-start | bytes 3145736 | tf_op jit(solution)/shard_map/ppermute | solution.py:75
  131.7 23.3 %collective-permute-start.18 = (bf16[4096,128]{1,0:T(8,128)(2,1)}, bf16[4096,128]{1,0:T(8,128)(2,1)S(1)}, u32[]{:S(2)}, u32[]{:S(2)}) collective-permute-start(bf16[4096,128]{1,0:T(8,128)(2,1)} %get-tuple-element.60), channel_id=1, source_target_pairs={{0,1},{1,3},{3,2},{2,6},{6,4},{4,5},{5,7},{7,11},{11,9},{9,8},{8,1... | collective-permute-start | bytes 3145736 | tf_op jit(solution)/shard_map/ppermute | solution.py:75
  183.8 20.2 %collective-permute-start.21 = (bf16[4096,128]{1,0:T(8,128)(2,1)}, bf16[4096,128]{1,0:T(8,128)(2,1)S(1)}, u32[]{:S(2)}, u32[]{:S(2)}) collective-permute-start(bf16[4096,128]{1,0:T(8,128)(2,1)} %get-tuple-element.62), channel_id=1, source_target_pairs={{1,0},{3,1},{2,3},{6,2},{4,6},{5,4},{7,5},{11,7},{9,11},{8,9},{10,... | collective-permute-start | bytes 3145736 | tf_op jit(solution)/shard_map/ppermute | solution.py:75
  184.0 22.0 %collective-permute-start.20 = (bf16[4096,128]{1,0:T(8,128)(2,1)}, bf16[4096,128]{1,0:T(8,128)(2,1)S(1)}, u32[]{:S(2)}, u32[]{:S(2)}) collective-permute-start(bf16[4096,128]{1,0:T(8,128)(2,1)} %get-tuple-element.62), channel_id=1, source_target_pairs={{0,1},{1,3},{3,2},{2,6},{6,4},{4,5},{5,7},{7,11},{11,9},{9,8},{8,1... | collective-permute-start | bytes 3145736 | tf_op jit(solution)/shard_map/ppermute | solution.py:75
  238.9 12.0 %all-to-all-start.1 = ((bf16[16,64,128]{2,1,0:T(8,128)(2,1)}), bf16[16,64,128]{2,1,0:T(8,128)(2,1)S(1)}, u32[]{:S(2)}, u32[]{:S(2)}) async-start(bf16[16,64,128]{2,1,0:T(8,128)(2,1)} %bitcast.218), calls=%async_computation.1 | async-start | bytes 524288 | tf_op jit(solution)/shard_map/all_to_all | solution.py:558
  243.1 11.2 %collective-permute-start.22 = (bf16[78,360]{1,0:T(8,128)(2,1)}, bf16[78,360]{1,0:T(8,128)(2,1)}, u32[]{:S(2)}, u32[]{:S(2)}) collective-permute-start(bf16[78,360]{1,0:T(8,128)(2,1)} %slice.424), channel_id=1, source_target_pairs={{1,0},{2,1},{3,2},{4,3},{5,4},{6,5},{7,6},{8,7},{9,8},{10,9},{11,1... | collective-permute-start | bytes 168488 | tf_op jit(solution)/shard_map/ppermute | solution.py:47
  252.4 6.6 %collective-permute-start.23 = (bf16[78,360]{1,0:T(8,128)(2,1)S(1)}, bf16[78,360]{1,0:T(8,128)(2,1)S(1)}, u32[]{:S(2)}, u32[]{:S(2)}) collective-permute-start(bf16[78,360]{1,0:T(8,128)(2,1)S(1)} %slice.423), channel_id=1, source_target_pairs={{1,0},{2,1},{3,2},{4,3},{5,4},{6,5},{7,6},{8,7},{9,8},{10,9},{11,1... | collective-permute-start | bytes 168488 | tf_op jit(solution)/shard_map/ppermute | solution.py:47
  261.0 5.8 collective-permute-start.24
  324.5 17.0 %collective-permute-start.25 = (bf16[4096,128]{1,0:T(8,128)(2,1)}, bf16[4096,128]{1,0:T(8,128)(2,1)}, u32[]{:S(2)}, u32[]{:S(2)}) collective-permute-start(bf16[4096,128]{1,0:T(8,128)(2,1)} %get-tuple-element.70), channel_id=1, source_target_pairs={{0,1},{1,3},{3,2},{2,6},{6,4},{4,5},{5,7},{7,11},{11,9},{9,8},{8,1... | collective-permute-start | bytes 3145736 | tf_op jit(solution)/shard_map/ppermute | solution.py:75
  325.9 15.5 %collective-permute-start.26 = (bf16[4096,128]{1,0:T(8,128)(2,1)}, bf16[4096,128]{1,0:T(8,128)(2,1)}, u32[]{:S(2)}, u32[]{:S(2)}) collective-permute-start(bf16[4096,128]{1,0:T(8,128)(2,1)} %get-tuple-element.71), channel_id=1, source_target_pairs={{1,0},{3,1},{2,3},{6,2},{4,6},{5,4},{7,5},{11,7},{9,11},{8,9},{10,... | collective-permute-start | bytes 3145736 | tf_op jit(solution)/shard_map/ppermute | solution.py:75
  385.7 17.1 %collective-permute-start.27 = (bf16[4096,128]{1,0:T(8,128)(2,1)}, bf16[4096,128]{1,0:T(8,128)(2,1)}, u32[]{:S(2)}, u32[]{:S(2)}) collective-permute-start(bf16[4096,128]{1,0:T(8,128)(2,1)} %get-tuple-element.77), channel_id=1, source_target_pairs={{0,1},{1,3},{3,2},{2,6},{6,4},{4,5},{5,7},{7,11},{11,9},{9,8},{8,1... | collective-permute-start | bytes 3145736 | tf_op jit(solution)/shard_map/ppermute | solution.py:75
  385.7 17.1 %collective-permute-start.28 = (bf16[4096,128]{1,0:T(8,128)(2,1)S(1)}, bf16[4096,128]{1,0:T(8,128)(2,1)}, u32[]{:S(2)}, u32[]{:S(2)}) collective-permute-start(bf16[4096,128]{1,0:T(8,128)(2,1)S(1)} %copy-done.63), channel_id=1, source_target_pairs={{1,0},{3,1},{2,3},{6,2},{4,6},{5,4},{7,5},{11,7},{9,11},{8,9},{10,... | collective-permute-start | bytes 3145736 | tf_op jit(solution)/shard_map/ppermute | solution.py:75
  448.1 16.6 %collective-permute-start.29 = (bf16[4096,128]{1,0:T(8,128)(2,1)S(1)}, bf16[4096,128]{1,0:T(8,128)(2,1)S(1)}, u32[]{:S(2)}, u32[]{:S(2)}) collective-permute-start(bf16[4096,128]{1,0:T(8,128)(2,1)S(1)} %copy-done.64), channel_id=1, source_target_pairs={{0,1},{1,3},{3,2},{2,6},{6,4},{4,5},{5,7},{7,11},{11,9},{9,8},{8,1... | collective-permute-start | bytes 3145736 | tf_op jit(solution)/shard_map/ppermute | solution.py:75
  448.1 16.6 %collective-permute-start.30 = (bf16[4096,128]{1,0:T(8,128)(2,1)S(1)}, bf16[4096,128]{1,0:T(8,128)(2,1)S(1)}, u32[]{:S(2)}, u32[]{:S(2)}) collective-permute-start(bf16[4096,128]{1,0:T(8,128)(2,1)S(1)} %copy-done.62), channel_id=1, source_target_pairs={{1,0},{3,1},{2,3},{6,2},{4,6},{5,4},{7,5},{11,7},{9,11},{8,9},{10,... | collective-permute-start | bytes 3145736 | tf_op jit(solution)/shard_map/ppermute | solution.py:75
  494.4 3.1 collective-permute-start.31
  499.7 9.1 %collective-permute-start.32 = (bf16[2,2,2,72,256]{4,3,0,1,2:T(8,128)(2,1)S(1)}, bf16[2,2,2,72,256]{4,3,0,1,2:T(8,128)(2,1)S(1)}, u32[]{:S(2)}, u32[]{:S(2)}) collective-permute-start(bf16[2,2,2,72,256]{4,3,0,1,2:T(8,128)(2,1)S(1)} %fusion.39), channel_id=1, source_target_pairs={{0,1},{1,0},{2,3},{3,2},{4,5},{5,4},{6,7},{7,6},{8,9},{9,8},{10,11... | collective-permute-start | bytes 884744 | tf_op jit(solution)/shard_map/ppermute | solution.py:92
  501.0 86.0 %collective-permute-start.45 = (bf16[2048,256]{1,0:T(8,128)(2,1)}, bf16[2048,256]{1,0:T(8,128)(2,1)S(1)}, u32[]{:S(2)}, u32[]{:S(2)}) collective-permute-start(bf16[2048,256]{1,0:T(8,128)(2,1)} %copy-done.20), channel_id=1, source_target_pairs={{0,0},{1,1},{3,2},{2,3},{6,4},{4,5},{5,6},{7,7},{11,8},{9,9},{8,10... | collective-permute-start | bytes 3145736 | tf_op jit(solution)/shard_map/ppermute | solution.py:641
  502.9 87.9 %collective-permute-start.46 = (bf16[2048,256]{1,0:T(8,128)(2,1)}, bf16[2048,256]{1,0:T(8,128)(2,1)S(1)}, u32[]{:S(2)}, u32[]{:S(2)}) collective-permute-start(bf16[2048,256]{1,0:T(8,128)(2,1)} %get-tuple-element.144), channel_id=1, source_target_pairs={{0,0},{1,1},{3,2},{2,3},{6,4},{4,5},{5,6},{7,7},{11,8},{9,9},{8,10... | collective-permute-start | bytes 3145736 | tf_op jit(solution)/shard_map/ppermute | solution.py:668
  504.8 9.9 %collective-permute-start.36 = (bf16[2,2,2,72,256]{4,3,2,1,0:T(8,128)(2,1)S(1)}, bf16[2,2,2,72,256]{4,3,2,1,0:T(8,128)(2,1)S(1)}, u32[]{:S(2)}, u32[]{:S(2)}) collective-permute-start(bf16[2,2,2,72,256]{4,3,2,1,0:T(8,128)(2,1)S(1)} %fusion.38), channel_id=1, source_target_pairs={{0,2},{1,3},{2,0},{3,1},{4,6},{5,7},{6,4},{7,5},{8,10},{9,11},{10,... | collective-permute-start | bytes 884744 | tf_op jit(solution)/shard_map/ppermute | solution.py:92
  508.9 8.2 %collective-permute-start.33 = (bf16[2,2,72,256]{3,2,0,1:T(8,128)(2,1)S(1)}, bf16[2,2,72,256]{3,2,0,1:T(8,128)(2,1)S(1)}, u32[]{:S(2)}, u32[]{:S(2)}) collective-permute-start(bf16[2,2,72,256]{3,2,0,1:T(8,128)(2,1)S(1)} %fusion.63), channel_id=1, source_target_pairs={{0,2},{1,3},{2,0},{3,1},{4,6},{5,7},{6,4},{7,5},{8,10},{9,11},{10,... | collective-permute-start | bytes 442376 | tf_op jit(solution)/shard_map/ppermute | solution.py:92
  514.8 45.2 %collective-permute-start.37 = (bf16[2,2,72,256]{3,2,1,0:T(8,128)(2,1)S(1)}, bf16[2,2,72,256]{3,2,1,0:T(8,128)(2,1)S(1)}, u32[]{:S(2)}, u32[]{:S(2)}) collective-permute-start(bf16[2,2,72,256]{3,2,1,0:T(8,128)(2,1)S(1)} %fusion.64), channel_id=1, source_target_pairs={{0,1},{1,0},{2,3},{3,2},{4,5},{5,4},{6,7},{7,6},{8,9},{9,8},{10,11... | collective-permute-start | bytes 442376 | tf_op jit(solution)/shard_map/ppermute | solution.py:92
  517.1 45.6 %collective-permute-start.34 = (bf16[2,72,256]{2,1,0:T(8,128)(2,1)S(1)}, bf16[2,72,256]{2,1,0:T(8,128)(2,1)S(1)}, u32[]{:S(2)}, u32[]{:S(2)}) collective-permute-start(bf16[2,72,256]{2,1,0:T(8,128)(2,1)S(1)} %fusion.68), channel_id=1, source_target_pairs={{0,4},{1,5},{2,6},{3,7},{4,0},{5,1},{6,2},{7,3},{8,12},{9,13},{10,... | collective-permute-start | bytes 221192 | tf_op jit(solution)/shard_map/ppermute | solution.py:92
  560.0 9.2 %collective-permute-start.38 = (bf16[2,72,256]{2,1,0:T(8,128)(2,1)S(1)}, bf16[2,72,256]{2,1,0:T(8,128)(2,1)S(1)}, u32[]{:S(2)}, u32[]{:S(2)}) collective-permute-start(bf16[2,72,256]{2,1,0:T(8,128)(2,1)S(1)} %fusion.69), channel_id=1, source_target_pairs={{0,4},{1,5},{2,6},{3,7},{4,0},{5,1},{6,2},{7,3},{8,12},{9,13},{10,... | collective-permute-start | bytes 221192 | tf_op jit(solution)/shard_map/ppermute | solution.py:92
  562.8 8.9 %collective-permute-start.35 = (bf16[72,256]{1,0:T(8,128)(2,1)S(1)}, bf16[72,256]{1,0:T(8,128)(2,1)S(1)}, u32[]{:S(2)}, u32[]{:S(2)}) collective-permute-start(bf16[72,256]{1,0:T(8,128)(2,1)S(1)} %fusion.76), channel_id=1, source_target_pairs={{0,8},{1,9},{2,10},{3,11},{4,12},{5,13},{6,14},{7,15},{8,0},{9,1},... | collective-permute-start | bytes 110600 | tf_op jit(solution)/shard_map/ppermute | solution.py:92
  569.2 4.9 collective-permute-start.39
  576.9 3.6 collective-permute-start.41
  580.5 4.1 collective-permute-start.42
  584.6 4.0 collective-permute-start.43
  588.6 4.5 collective-permute-start.44
  (66 other events, 651.0 us)

commit v4 on v3

--- a/solution.py
+++ b/solution.py
@@ -20,6 +20,10 @@
 UNROLL = 32
 ALL = ("dp", "space")
 LIMIT = pltpu.CompilerParams(vmem_limit_bytes=56 * 2**20)
+
+
+def cost(micros):
+    return pl.CostEstimate(flops=0, bytes_accessed=micros * 3_000_000, transcendentals=0)
 
 
 def inner(left, right, left_dim, right_dim):
@@ -80,7 +84,7 @@
     starts = [share * d // D for d in range(peers)]
     counts = [-(-share * (d + 1) // D) - starts[d] for d in range(peers)]
     shared = [share * d % D != 0 for d in range(peers)]
-    height = -(-max(counts) // 16) * 16
+    height = -(-(max(counts) + 1) // 16) * 16
     return starts, counts, shared, height
 
 
@@ -161,8 +165,13 @@
             def _():
                 lay(sources[2], sources[3])
 
+        count = jnp.zeros((1, D), jnp.float32)
+        for source in (sources[1], sources[3]):
+            for spot in range(group):
+                count = count + source[spot, half - 1 : half, :].astype(jnp.float32)
+        outs[-1][...] = count
         start = 0
-        for out, size in zip(outs, sizes):
+        for out, size in zip(outs[:-1], sizes):
             out[:size, :] = buffer[start : start + size, :].astype(out.dtype)
             if out.shape[0] > size:
                 out[size:, :] = jnp.zeros((out.shape[0] - size, D), out.dtype)
@@ -176,11 +185,15 @@
             num_scalar_prefetch=1,
             grid=(1,),
             in_specs=[whole(first.shape)] * 4,
-            out_specs=[whole((tall, D)) for tall in talls],
+            out_specs=[whole((tall, D)) for tall in talls + [1]],
             scratch_shapes=[pltpu.VMEM((-(-rows // 8) * 8 + 8, D), jnp.float32)],
         ),
-        out_shape=[jax.ShapeDtypeStruct((tall, D), kind) for tall, kind in zip(talls, kinds)],
+        out_shape=[
+            jax.ShapeDtypeStruct((tall, D), kind)
+            for tall, kind in zip(talls + [1], kinds + [jnp.float32])
+        ],
         compiler_params=LIMIT,
+        cost_estimate=cost(4),
         name="spread_rows",
     )(place.reshape(1), first, second, first_far, second_far)
 
@@ -227,25 +240,27 @@
             jax.ShapeDtypeStruct(shape, jnp.bfloat16),
         ],
         compiler_params=LIMIT,
+        cost_estimate=cost(5),
         name="collect_rows",
     )(place.reshape(1), *parts)
 
 
-def reduced_piece(keep, send):
+def reduced_piece(keep, send, leaving):
     kept = keep + swapped(send, "dp", 1).astype(jnp.float32)
     half = kept.shape[1] // 2
-    done = []
-    for part, order in zip((kept[:, :half], kept[:, half:]), orders()):
-        names = bits_of("space")[::-1]
-        part = part.reshape((2,) * len(names) + (half, D))
-        for bit in order:
-            spot = names.index(bit)
-            names.pop(spot)
-            stay = lax.index_in_dim(part, 0, spot, keepdims=False)
-            leave = lax.index_in_dim(part, 1, spot, keepdims=False)
-            part = stay + swapped(leave.astype(jnp.bfloat16), "space", bit).astype(jnp.float32)
-        done.append(part)
-    return jnp.concatenate(done, 0)
+    names = [bits_of("space")[::-1], bits_of("space")[::-1]]
+    parts = [kept[:, :half], kept[:, half:]]
+    parts = [part.reshape((2,) * len(names[0]) + (half, D)) for part in parts]
+    for turn, bits in enumerate(zip(*orders())):
+        for n, bit in enumerate(bits):
+            spot = names[n].index(bit)
+            names[n].pop(spot)
+            stay = lax.index_in_dim(parts[n], 0, spot, keepdims=False)
+            leave = lax.index_in_dim(parts[n], 1, spot, keepdims=False)
+            parts[n] = stay + swapped(leave.astype(jnp.bfloat16), "space", bit).astype(jnp.float32)
+        if turn == 1:
+            parts[0], parts[1], leaving = lax.optimization_barrier((*parts, leaving))
+    return jnp.concatenate(parts, 0), leaving
 
 
 def tall_parts():
@@ -298,6 +313,7 @@
         ),
         out_shape=jax.ShapeDtypeStruct((edges, 2, HALF), own.dtype),
         compiler_params=LIMIT,
+        cost_estimate=cost(16),
         name="gather_rows",
     )(index, before, own, after)
 
@@ -376,6 +392,7 @@
         out_shape=shapes,
         scratch_shapes=[pltpu.VMEM((2 * tile, HALF), jnp.float32)],
         compiler_params=LIMIT,
+        cost_estimate=cost(11),
         name="round_forward",
     )(*args)
 
@@ -476,6 +493,7 @@
             jax.ShapeDtypeStruct((2 * H, HALF), jnp.bfloat16),
         ],
         compiler_params=LIMIT,
+        cost_estimate=cost(33),
         name="edges_backward",
     )(index, grad_mesh, mesh, uin, edges, mats, bias)
 
@@ -513,6 +531,7 @@
         ],
         scratch_shapes=[pltpu.VMEM((2 * tile, HALF), jnp.float32)],
         compiler_params=LIMIT,
+        cost_estimate=cost(8),
         name="round_backward",
     )(grad_mesh, own, first, last, grad_uin, dest_low, mats)
 
@@ -531,6 +550,11 @@
     )
     state_in = inputs[0]
     counted = valid[0].astype(jnp.float32)
+    local_count = jnp.sum(valid[0])
+    digits = (local_count >> jnp.array([16, 8, 0], jnp.int32)) & 255
+    piece = lax.dynamic_update_slice(
+        piece.reshape(height, D), digits.astype(jnp.bfloat16)[None, :], (height - 1, 0)
+    )
     points = state_in.shape[1]
     blocks = neighbours.shape[0]
     assert blocks == H
@@ -560,21 +584,20 @@
         ).reshape(bands * capacity, HALF)
 
     arrived = exchanged(inner(poster, columns, 1, 1).astype(jnp.bfloat16))
-    w_in, w_node, w_dec, w_out, w_round, biases = spread_rows(
-        gathered_blocks(piece.reshape(height, D)), total_size, peers, place
-    )
+    w_in, w_node, w_dec, w_out, w_round, biases, digits = spread_rows(
+        gathered_blocks(piece), total_size, peers, place
+    )
+    count = digits[0, 0] * 65536.0 + digits[0, 1] * 256.0 + digits[0, 2]
     w_out = jnp.pad(w_out.reshape(D, CH), ((0, 0), (0, HALF - CH)))
     w_round = w_round.reshape(ROUNDS, 5, D, D)
     b_head = biases[:3]
     b_round = biases[3:].reshape(ROUNDS, 2, D)
-    count = summed_everywhere(jnp.full((8, HALF), jnp.sum(counted)))[0, 0]
     ids = arrived[:, CH : CH + 3].astype(jnp.int32)
     ids = jnp.where(ids[:, 2:3] > 0, ids[:, 0:1] * 64 + ids[:, 1:2], -1)
     chooser = (ids == jnp.arange(blocks, dtype=jnp.int32)[None, :]).astype(jnp.bfloat16)
     enc_in = inner(arrived, w_in, 1, 0) + b_head[0]
     encoded = silu(enc_in).astype(jnp.bfloat16)
     gathered = inner(chooser, encoded, 0, 0).astype(jnp.bfloat16)
-    gathered, count = lax.optimization_barrier((gathered, count))
     node_in = inner(gathered, w_node, 1, 0) + b_head[1]
     mesh = silu(node_in)
     index = ((neighbours - band * blocks + H) % (blocks * bands)).T.reshape(-1)
@@ -638,7 +661,7 @@
     grad_fetched = inner(grad_dec, w_dec, 1, 1).astype(jnp.bfloat16)
     grad_mesh = inner(chooser, grad_fetched, 0, 0)
     grad_mesh, leaving = lax.optimization_barrier((grad_mesh, mesh.astype(jnp.bfloat16)))
-    final_mesh = lax.ppermute(leaving, "space", home).astype(jnp.float32)
+    final_mesh = lax.ppermute(leaving, "space", home)
     mats_grads = [None] * (5 * ROUNDS)
     bias_grads = [None] * (2 * ROUNDS)
     for layer in reversed(range(ROUNDS)):
@@ -647,6 +670,10 @@
         grad_uin, dest_low, to_before, own, to_after = edges_backward(
             index, grad_mesh, old, uin, edges, mats, b_round[layer]
         )
+        if layer == ROUNDS - 1:
+            to_before, to_after, final_mesh = lax.optimization_barrier(
+                (to_before, to_after, final_mesh)
+            )
         from_before, from_after = halo(walk, to_after, to_before)
         lowered = old.astype(jnp.bfloat16)
         grad_out = grad_mesh.astype(jnp.bfloat16)
@@ -665,7 +692,7 @@
         )
         grads[0] = inner(lowered, sent_low, 0, 0)
         mats_grads[5 * layer : 5 * layer + 5] = grads
-    node_grads = lax.ppermute(grad_mesh.astype(jnp.bfloat16), "space", home).astype(jnp.float32)
+    leaving = grad_mesh.astype(jnp.bfloat16)
     grad_node = (grad_mesh * slope(node_in)).astype(jnp.bfloat16)
     grad_bnode = jnp.sum(grad_node.astype(jnp.float32), 0)
     grad_wnode = inner(gathered, grad_node, 0, 0)
@@ -677,7 +704,9 @@
     parts = [grad_win, grad_wnode, grad_wdec, grad_wout.reshape(CH, D)]
     parts = parts + mats_grads
     parts.append(jnp.concatenate([jnp.stack([grad_bin, grad_bnode, grad_bdec])] + bias_grads, 0))
-    mine = reduced_piece(*collect_rows(parts, total_size, peers, place))
+    keep, send = collect_rows(parts, total_size, peers, place)
+    mine, leaving = reduced_piece(keep, send, leaving)
+    node_grads = lax.ppermute(leaving, "space", home)
     mine = lax.dynamic_slice_in_dim(mine.reshape(-1), offset, shard)
     lane = lax.broadcasted_iota(jnp.int32, (8, HALF), 1)
     sums = summed_everywhere(jnp.where(lane == 0, local_total, jnp.sum(mine * mine)))
@@ -696,8 +725,8 @@
         first,
         second,
         updated.astype(jnp.bfloat16),
-        final_mesh.reshape(1, blocks, D),
-        node_grads.reshape(1, blocks, D),
+        final_mesh.astype(jnp.float32).reshape(1, blocks, D),
+        node_grads.astype(jnp.float32).reshape(1, blocks, D),
         grad_pred.reshape(1, grad_pred.shape[0], points),
     )
 

time: 608 us -> 604 us (level)
  the two profiles are of different devices: /device:TPU:0 before, /device:TPU:12 now
where the time goes in v4:
time: 604 us; the launch traced here: 593 us
  Pallas kernels  217 us (36%)
  waiting for transfers between devices  163 us (27%)
  starting transfers between devices  84.4 us (14%)
  matrix products  51.2 us (8%)
  other arithmetic  29.2 us (5%)
  local copies, waits for them, and re-layouts  25.8 us (4%)
  blocking collectives  13.6 us (2%)
  between operations  8.36 us (1%)
    pallas_call x3, Pallas kernels, edges_backward(): pl.pallas_call(body, grid_spec=pltpu.PrefetchScalarGridSpec(num_scalar_pr...  99.1 us
    dot_general x31, matrix products, inner(): lax.dot_general(left, right, (((left_dim,), (right_dim,)), ((), ())), pre...  50.8 us
    pallas_call x3, Pallas kernels, gather_rows(): pl.pallas_call(body, grid_spec=pltpu.PrefetchScalarGridSpec(num_scalar_pr...  48.2 us
    ppermute x6, waiting for transfers between devices, halo(): lax.ppermute(initial, 'space', down)  46.3 us
    ppermute x24, waiting for transfers between devices, swapped(): lax.ppermute(value, axis, [(i, i ^ bit) for i in range(lax.axis_size(axis...  46.2 us
    pallas_call x3, Pallas kernels, round_forward(): pl.pallas_call(body, grid=(blocks // tile,), in_specs=ins, out_specs=outs...  34.7 us
    ppermute x6, waiting for transfers between devices, halo(): lax.ppermute(last, 'space', up)  31.6 us
    ppermute x24, starting transfers between devices, swapped(): lax.ppermute(value, axis, [(i, i ^ bit) for i in range(lax.axis_size(axis...  27.7 us
  transfers between devices with their start and end apart: 44, of which 35 were waited for; matrix products, arithmetic and copies ran while one was open for 7% of the time, Pallas kernels for 6%

profile of v4, /device:TPU:12, one launch (start us, length us, event | category | flops | bytes accessed | tf_op | source)
XLA Modules:
  0.0 592.5 jit_solution(8833349798872050782)
XLA Ops:
  15.4 7.2 %all-to-all-start = ((bf16[16,64,128]{2,1,0:T(8,128)(2,1)}), bf16[16,64,128]{2,1,0:T(8,128)(2,1)S(1)}, u32[]{:S(2)}, u32[]{:S(2)}) async-start(bf16[16,64,128]{2,1,0:T(8,128)(2,1)} %bitcast.5), calls=%async_computation | async-start | bytes 524288 | tf_op jit(solution)/shard_map/all_to_all | solution.py:582
  24.8 4.7 collective-permute-done.5
  31.7 4.6 collective-permute-done.2
  37.7 5.3 collective-permute-done.3
  46.8 4.2 spread_rows.1
  63.4 3.2 collective-permute-start.10
  68.3 2.8 fusion.107
  74.5 13.3 %collective-permute-done.10.index_ref = s32[12288]{0:T(1024)S(1)} collective-permute-done((s32[12288]{0:T(1024)S(1)}, s32[12288]{0:T(1024)S(1)}, u32[]{:S(2)}, u32[]{:S(2)}) %collective-permute-start.10) | collective-permute-done | bytes 49184 | tf_op jit(solution)/shard_map/ppermute | solution.py:604
  88.8 16.1 %gather_rows.3 = bf16[12288,2,128]{2,1,0:T(2,128)(2,1)} custom-call(s32[12288]{0:T(1024)} %copy-done.18, bf16[2048,2,128]{2,1,0:T(2,128)(2,1)} %bitcast.16.before_ref, bf16[2048,2,128]{2,1,0:T(2,128)(2,1)} %copy.54.own_ref, bf16[2048,2,128]{2,1,0:T(2,128)(2,1)} %bitcast.215), custom_call_target="tpu_custom_call" | custom-call | bytes 48000000 | tf_op jit(solution)/shard_map/gather_rows/pallas_call | solution.py:302
  104.9 11.8 %round_forward.3 = (f32[2048,256]{1,0:T(8,128)}, f32[2048,256]{1,0:T(8,128)}, bf16[2048,256]{1,0:T(8,128)(2,1)}, bf16[4096,128]{1,0:T(8,128)(2,1)}) custom-call(f32[2048,256]{1,0:T(8,128)} %get-tuple-element.156.refs_0_.mesh_ref, bf16[6,4096,128]{2,1,0:T(8,128)(2,1)} %bitcast.188, bf16[5,256,256]{2,1,0:T(8,128)(2,1)} %bitcast.194, ...), custom_call_target="tpu_custom_call" | custom-call | bytes 33000000 | tf_op jit(solution)/shard_map/round_forward/pallas_call | solution.py:387
  119.4 21.9 %collective-permute-done.14 = bf16[4096,128]{1,0:T(8,128)(2,1)S(1)} collective-permute-done((bf16[4096,128]{1,0:T(8,128)(2,1)}, bf16[4096,128]{1,0:T(8,128)(2,1)S(1)}, u32[]{:S(2)}, u32[]{:S(2)}) %collective-permute-start.14) | collective-permute-done | bytes 1048608 | tf_op jit(solution)/shard_map/ppermute | solution.py:79
  144.4 16.1 %gather_rows.4 = bf16[12288,2,128]{2,1,0:T(2,128)(2,1)} custom-call(s32[12288]{0:T(1024)} %copy-done.18, bf16[2048,2,128]{2,1,0:T(2,128)(2,1)} %bitcast.221, bf16[2048,2,128]{2,1,0:T(2,128)(2,1)} %bitcast.217, bf16[2048,2,128]{2,1,0:T(2,128)(2,1)} %bitcast.219), custom_call_target="tpu_custom_call" | custom-call | bytes 48000000 | tf_op jit(solution)/shard_map/gather_rows/pallas_call | solution.py:302
  160.5 11.8 %round_forward.4 = (f32[2048,256]{1,0:T(8,128)}, f32[2048,256]{1,0:T(8,128)}, bf16[2048,256]{1,0:T(8,128)(2,1)}, bf16[4096,128]{1,0:T(8,128)(2,1)}) custom-call(f32[2048,256]{1,0:T(8,128)} %get-tuple-element.63.refs_0_.mesh_ref, bf16[6,4096,128]{2,1,0:T(8,128)(2,1)} %bitcast.190, bf16[5,256,256]{2,1,0:T(8,128)(2,1)} %bitcast.197, ...), custom_call_target="tpu_custom_call" | custom-call | bytes 33000000 | tf_op jit(solution)/shard_map/round_forward/pallas_call | solution.py:387
  175.2 20.3 %collective-permute-done.16 = bf16[4096,128]{1,0:T(8,128)(2,1)S(1)} collective-permute-done((bf16[4096,128]{1,0:T(8,128)(2,1)}, bf16[4096,128]{1,0:T(8,128)(2,1)S(1)}, u32[]{:S(2)}, u32[]{:S(2)}) %collective-permute-start.16) | collective-permute-done | bytes 1048608 | tf_op jit(solution)/shard_map/ppermute | solution.py:79
  197.1 16.1 %gather_rows.5 = bf16[12288,2,128]{2,1,0:T(2,128)(2,1)} custom-call(s32[12288]{0:T(1024)} %copy-done.18, bf16[2048,2,128]{2,1,0:T(2,128)(2,1)} %bitcast.220, bf16[2048,2,128]{2,1,0:T(2,128)(2,1)} %bitcast.216, bf16[2048,2,128]{2,1,0:T(2,128)(2,1)} %bitcast.218), custom_call_target="tpu_custom_call" | custom-call | bytes 48000000 | tf_op jit(solution)/shard_map/gather_rows/pallas_call | solution.py:302
  213.2 11.2 %round_forward.5 = (f32[2048,256]{1,0:T(8,128)}, f32[2048,256]{1,0:T(8,128)}, bf16[2048,256]{1,0:T(8,128)(2,1)}) custom-call(f32[2048,256]{1,0:T(8,128)} %get-tuple-element.65.refs_0_.mesh_ref, bf16[6,4096,128]{2,1,0:T(8,128)(2,1)} %bitcast.192, bf16[5,256,256]{2,1,0:T(8,128)(2,1)} %bitcast.200, f32[2,256]{1,0:T(2,128)} %get-tuple-element.173.refs_3_.bias_ref), custom_call_target="tpu_custom_call" | custom-call | bytes 33000000 | tf_op jit(solution)/shard_map/round_forward/pallas_call | solution.py:387
  224.4 2.7 convert_element_type.241
  227.2 2.7 fusion.16
  231.3 10.1 %all-to-all-start.1 = ((bf16[16,64,128]{2,1,0:T(8,128)(2,1)}), bf16[16,64,128]{2,1,0:T(8,128)(2,1)}, u32[]{:S(2)}, u32[]{:S(2)}) async-start(bf16[16,64,128]{2,1,0:T(8,128)(2,1)} %bitcast.34), calls=%async_computation.1 | async-start | bytes 524288 | tf_op jit(solution)/shard_map/all_to_all | solution.py:582
  241.4 3.4 collective-permute-start.17
  244.8 3.4 collective-permute-done.17
  250.0 3.8 collective-permute-start.18
  257.8 5.7 collective-permute-start.19
  267.1 13.6 %all_to_all.15 = bf16[16,64,128]{2,1,0:T(8,128)(2,1)S(1)} all-to-all(bf16[16,64,128]{2,1,0:T(8,128)(2,1)S(1)} %bitcast.225), channel_id=1, replica_groups=mesh['dp'=2,'space'=16] {'space'}, dimensions={0} | all-to-all | bytes 524288 | tf_op jit(solution)/shard_map/all_to_all | solution.py:582
  282.6 3.9 fusion.1.grad_ref
  286.4 3.0 collective-permute-start.20
  289.5 33.1 %edges_backward.3 = (bf16[2048,256]{1,0:T(8,128)(2,1)}, bf16[2048,256]{1,0:T(8,128)(2,1)}, bf16[4096,128]{1,0:T(8,128)(2,1)}, f32[4096,128]{1,0:T(8,128)}, bf16[4096,128]{1,0:T(8,128)(2,1)}) custom-call(s32[12288]{0:T(1024)} %copy-done.18, f32[2048,256]{1,0:T(8,128)} %fusion.1.grad_ref, f32[2048,256]{1,0:T(8,128)} %get-tuple-element.65.refs_0_.mesh_ref, ...), custom_call_target="tpu_custom_call" | custom-call | bytes 99000000 | tf_op jit(solution)/shard_map/edges_backward/pallas_call | solution.py:467
  334.3 10.0 %collective-permute-done.21.first_ref = bf16[4096,128]{1,0:T(8,128)(2,1)} collective-permute-done((bf16[4096,128]{1,0:T(8,128)(2,1)}, bf16[4096,128]{1,0:T(8,128)(2,1)}, u32[]{:S(2)}, u32[]{:S(2)}) %collective-permute-start.21) | collective-permute-done | bytes 1048608 | tf_op jit(solution)/shard_map/ppermute | solution.py:79
  345.0 8.5 %round_backward.3 = (f32[2048,256]{1,0:T(8,128)}, bf16[2048,256]{1,0:T(8,128)(2,1)}) custom-call(f32[2048,256]{1,0:T(8,128)} %fusion.1.grad_ref, f32[4096,128]{1,0:T(8,128)} %get-tuple-element.73.own_ref, bf16[4096,128]{1,0:T(8,128)(2,1)} %collective-permute-done.21.first_ref, bf16[4096,128]{1,0:T(8,128)(2,1)} %collective-permute-done.22.last_ref, ...), custom_call_target="tpu_custom_call" | custom-call | bytes 24000000 | tf_op jit(solution)/shard_map/round_backward/pallas_call | solution.py:523
  353.5 33.1 %edges_backward.4 = (bf16[2048,256]{1,0:T(8,128)(2,1)}, bf16[2048,256]{1,0:T(8,128)(2,1)}, bf16[4096,128]{1,0:T(8,128)(2,1)}, f32[4096,128]{1,0:T(8,128)}, bf16[4096,128]{1,0:T(8,128)(2,1)}) custom-call(s32[12288]{0:T(1024)} %copy-done.18, f32[2048,256]{1,0:T(8,128)} %get-tuple-element.81.grad_ref, f32[2048,256]{1,0:T(8,128)} %get-tuple-element.63.refs_0_.mesh_ref, ...), custom_call_target="tpu_custom_call" | custom-call | bytes 99000000 | tf_op jit(solution)/shard_map/edges_backward/pallas_call | solution.py:467
  389.2 6.9 %collective-permute-start.23 = (bf16[4096,128]{1,0:T(8,128)(2,1)}, bf16[4096,128]{1,0:T(8,128)(2,1)}, u32[]{:S(2)}, u32[]{:S(2)}) collective-permute-start(bf16[4096,128]{1,0:T(8,128)(2,1)} %get-tuple-element.84), channel_id=1, source_target_pairs={{0,1},{1,3},{3,2},{2,6},{6,4},{4,5},{5,7},{7,11},{11,9},{9,8},{8,1... | collective-permute-start | bytes 3145736 | tf_op jit(solution)/shard_map/ppermute | solution.py:79
  402.3 9.6 %collective-permute-done.23.first_ref = bf16[4096,128]{1,0:T(8,128)(2,1)} collective-permute-done((bf16[4096,128]{1,0:T(8,128)(2,1)}, bf16[4096,128]{1,0:T(8,128)(2,1)}, u32[]{:S(2)}, u32[]{:S(2)}) %collective-permute-start.23) | collective-permute-done | bytes 1048608 | tf_op jit(solution)/shard_map/ppermute | solution.py:79
  414.1 8.5 %round_backward.4 = (f32[2048,256]{1,0:T(8,128)}, bf16[2048,256]{1,0:T(8,128)(2,1)}) custom-call(f32[2048,256]{1,0:T(8,128)} %get-tuple-element.81.grad_ref, f32[4096,128]{1,0:T(8,128)} %get-tuple-element.83.own_ref, bf16[4096,128]{1,0:T(8,128)(2,1)} %collective-permute-done.23.first_ref, bf16[4096,128]{1,0:T(8,128)(2,1)} %collective-permute-done.24.last_ref, ...), custom_call_target="tpu_custom_call" | custom-call | bytes 24000000 | tf_op jit(solution)/shard_map/round_backward/pallas_call | solution.py:523
  422.6 32.9 %edges_backward.5 = (bf16[2048,256]{1,0:T(8,128)(2,1)}, bf16[2048,256]{1,0:T(8,128)(2,1)}, bf16[4096,128]{1,0:T(8,128)(2,1)}, f32[4096,128]{1,0:T(8,128)}, bf16[4096,128]{1,0:T(8,128)(2,1)}) custom-call(s32[12288]{0:T(1024)} %copy-done.18, f32[2048,256]{1,0:T(8,128)} %get-tuple-element.88.grad_ref, f32[2048,256]{1,0:T(8,128)} %get-tuple-element.156.refs_0_.mesh_ref, ...), custom_call_target="tpu_custom_call" | custom-call | bytes 99000000 | tf_op jit(solution)/shard_map/edges_backward/pallas_call | solution.py:467
  466.8 9.2 %collective-permute-done.25.first_ref = bf16[4096,128]{1,0:T(8,128)(2,1)S(1)} collective-permute-done((bf16[4096,128]{1,0:T(8,128)(2,1)S(1)}, bf16[4096,128]{1,0:T(8,128)(2,1)S(1)}, u32[]{:S(2)}, u32[]{:S(2)}) %collective-permute-start.25) | collective-permute-done | bytes 1048608 | tf_op jit(solution)/shard_map/ppermute | solution.py:79
  478.2 8.6 %round_backward.5 = (f32[2048,256]{1,0:T(8,128)}, bf16[2048,256]{1,0:T(8,128)(2,1)}) custom-call(f32[2048,256]{1,0:T(8,128)} %get-tuple-element.88.grad_ref, f32[4096,128]{1,0:T(8,128)} %get-tuple-element.90.own_ref, bf16[4096,128]{1,0:T(8,128)(2,1)} %copy-done.21, bf16[4096,128]{1,0:T(8,128)(2,1)} %copy-done.22, ...), custom_call_target="tpu_custom_call" | custom-call | bytes 24000000 | tf_op jit(solution)/shard_map/round_backward/pallas_call | solution.py:523
  486.8 4.6 convert_reduce_fusion.6
  492.7 4.2 convert_reduce_fusion.8
  501.6 5.1 collect_rows.1
  506.7 3.0 collective-permute-done.27
  515.3 5.7 collective-permute-done.30
  528.3 6.1 %collective-permute-start.34 = (bf16[2,72,256]{2,1,0:T(8,128)(2,1)S(1)}, bf16[2,72,256]{2,1,0:T(8,128)(2,1)S(1)}, u32[]{:S(2)}, u32[]{:S(2)}) collective-permute-start(bf16[2,72,256]{2,1,0:T(8,128)(2,1)S(1)} %fusion.67), channel_id=1, source_target_pairs={{0,4},{1,5},{2,6},{3,7},{4,0},{5,1},{6,2},{7,3},{8,12},{9,13},{10,... | collective-permute-start | bytes 221192 | tf_op jit(solution)/shard_map/ppermute | solution.py:96
  536.7 4.1 collective-permute-start.35
  542.8 3.0 collective-permute-done.33
  548.9 3.3 collective-permute-done.37
  552.2 3.6 collective-permute-done.38
  561.3 2.7 bitcast_convert_fusion.1
  568.2 20.0 %collective-permute-done.41 = bf16[2048,256]{1,0:T(8,128)(2,1)S(1)} collective-permute-done((bf16[2048,256]{1,0:T(8,128)(2,1)S(1)}, bf16[2048,256]{1,0:T(8,128)(2,1)S(1)}, u32[]{:S(2)}, u32[]{:S(2)}) %collective-permute-start.41) | collective-permute-done | bytes 1048608 | tf_op jit(solution)/shard_map/ppermute | solution.py:709
  (314 shorter events, 135.5 us)
Async XLA Ops:
  5.8 16.8 %collective-permute-start.4 = (bf16[1,72,256]{2,1,0:T(8,128)(2,1)S(1)}, bf16[1,72,256]{2,1,0:T(8,128)(2,1)S(1)}, u32[]{:S(2)}, u32[]{:S(2)}) collective-permute-start(bf16[1,72,256]{2,1,0:T(8,128)(2,1)S(1)} %get-tuple-element.166), channel_id=1, source_target_pairs={{0,8},{1,9},{2,10},{3,11},{4,12},{5,13},{6,14},{7,15},{8,0},{9,1},... | collective-permute-start | bytes 110600 | tf_op jit(solution)/shard_map/ppermute | solution.py:96
  8.4 14.8 %collective-permute-start = (bf16[1,72,256]{2,1,0:T(8,128)(2,1)S(1)}, bf16[1,72,256]{2,1,0:T(8,128)(2,1)S(1)}, u32[]{:S(2)}, u32[]{:S(2)}) collective-permute-start(bf16[1,72,256]{2,1,0:T(8,128)(2,1)S(1)} %get-tuple-element.167), channel_id=1, source_target_pairs={{0,8},{1,9},{2,10},{3,11},{4,12},{5,13},{6,14},{7,15},{8,0},{9,1},... | collective-permute-start | bytes 110600 | tf_op jit(solution)/shard_map/ppermute | solution.py:96
  15.4 28.6 %all-to-all-start = ((bf16[16,64,128]{2,1,0:T(8,128)(2,1)}), bf16[16,64,128]{2,1,0:T(8,128)(2,1)S(1)}, u32[]{:S(2)}, u32[]{:S(2)}) async-start(bf16[16,64,128]{2,1,0:T(8,128)(2,1)} %bitcast.5), calls=%async_computation | async-start | bytes 524288 | tf_op jit(solution)/shard_map/all_to_all | solution.py:582
  22.6 6.9 %collective-permute-start.5 = (bf16[2,72,256]{2,1,0:T(8,128)(2,1)S(1)}, bf16[2,72,256]{2,1,0:T(8,128)(2,1)S(1)}, u32[]{:S(2)}, u32[]{:S(2)}) collective-permute-start(bf16[2,72,256]{2,1,0:T(8,128)(2,1)S(1)} %pad_maximum_fusion.7), channel_id=1, source_target_pairs={{0,4},{1,5},{2,6},{3,7},{4,0},{5,1},{6,2},{7,3},{8,12},{9,13},{10,... | collective-permute-start | bytes 221192 | tf_op jit(solution)/shard_map/ppermute | solution.py:96
  23.2 7.8 %collective-permute-start.1 = (bf16[2,72,256]{2,1,0:T(8,128)(2,1)S(1)}, bf16[2,72,256]{2,1,0:T(8,128)(2,1)S(1)}, u32[]{:S(2)}, u32[]{:S(2)}) collective-permute-start(bf16[2,72,256]{2,1,0:T(8,128)(2,1)S(1)} %pad_maximum_fusion.6), channel_id=1, source_target_pairs={{0,4},{1,5},{2,6},{3,7},{4,0},{5,1},{6,2},{7,3},{8,12},{9,13},{10,... | collective-permute-start | bytes 221192 | tf_op jit(solution)/shard_map/ppermute | solution.py:96
  29.5 7.6 %collective-permute-start.6 = (bf16[4,72,256]{2,1,0:T(8,128)(2,1)S(1)}, bf16[4,72,256]{2,1,0:T(8,128)(2,1)S(1)}, u32[]{:S(2)}, u32[]{:S(2)}) collective-permute-start(bf16[4,72,256]{2,1,0:T(8,128)(2,1)S(1)} %pad_maximum_fusion.5), channel_id=1, source_target_pairs={{0,1},{1,0},{2,3},{3,2},{4,5},{5,4},{6,7},{7,6},{8,9},{9,8},{10,11... | collective-permute-start | bytes 442376 | tf_op jit(solution)/shard_map/ppermute | solution.py:96
  31.0 5.2 collective-permute-start.2
  36.3 6.8 %collective-permute-start.3 = (bf16[8,72,256]{2,1,0:T(8,128)(2,1)S(1)}, bf16[8,72,256]{2,1,0:T(8,128)(2,1)S(1)}, u32[]{:S(2)}, u32[]{:S(2)}) collective-permute-start(bf16[8,72,256]{2,1,0:T(8,128)(2,1)S(1)} %pad_maximum_fusion), channel_id=1, source_target_pairs={{0,1},{1,0},{2,3},{3,2},{4,5},{5,4},{6,7},{7,6},{8,9},{9,8},{10,11... | collective-permute-start | bytes 884744 | tf_op jit(solution)/shard_map/ppermute | solution.py:96
  37.1 6.8 %collective-permute-start.7 = (bf16[8,72,256]{2,1,0:T(8,128)(2,1)S(1)}, bf16[8,72,256]{2,1,0:T(8,128)(2,1)S(1)}, u32[]{:S(2)}, u32[]{:S(2)}) collective-permute-start(bf16[8,72,256]{2,1,0:T(8,128)(2,1)S(1)} %pad_maximum_fusion.1), channel_id=1, source_target_pairs={{0,2},{1,3},{2,0},{3,1},{4,6},{5,7},{6,4},{7,5},{8,10},{9,11},{10,... | collective-permute-start | bytes 884744 | tf_op jit(solution)/shard_map/ppermute | solution.py:96
  43.1 2.1 collective-permute-start.8
  43.9 2.1 collective-permute-start.9
  44.7 237.9 %copy-start.55 = (s32[1024]{0:T(1024)}, s32[1024]{0:T(1024)S(1)}, u32[]{:S(2)}) copy-start(s32[1024]{0:T(1024)S(1)} %fusion.36) | copy-start | bytes 12292
  61.3 26.5 %collective-permute-start.12 = (bf16[4096,128]{1,0:T(8,128)(2,1)}, bf16[4096,128]{1,0:T(8,128)(2,1)S(1)}, u32[]{:S(2)}, u32[]{:S(2)}) collective-permute-start(bf16[4096,128]{1,0:T(8,128)(2,1)} %reshape.196), channel_id=1, source_target_pairs={{1,0},{3,1},{2,3},{6,2},{4,6},{5,4},{7,5},{11,7},{9,11},{8,9},{10,... | collective-permute-start | bytes 3145736 | tf_op jit(solution)/shard_map/ppermute | solution.py:79
  62.6 25.2 %collective-permute-start.11 = (bf16[4096,128]{1,0:T(8,128)(2,1)}, bf16[4096,128]{1,0:T(8,128)(2,1)}, u32[]{:S(2)}, u32[]{:S(2)}) collective-permute-start(bf16[4096,128]{1,0:T(8,128)(2,1)} %reshape.196), channel_id=1, source_target_pairs={{0,1},{1,3},{3,2},{2,6},{6,4},{4,5},{5,7},{7,11},{11,9},{9,8},{8,1... | collective-permute-start | bytes 3145736 | tf_op jit(solution)/shard_map/ppermute | solution.py:79
  63.4 24.4 %collective-permute-start.10 = (s32[12288]{0:T(1024)S(1)}, s32[12288]{0:T(1024)S(1)}, u32[]{:S(2)}, u32[]{:S(2)}) collective-permute-start(s32[12288]{0:T(1024)S(1)} %reshape.194), channel_id=1, source_target_pairs={{0,0},{1,1},{2,3},{3,2},{4,6},{5,4},{6,5},{7,7},{8,11},{9,9},{10,8... | collective-permute-start | bytes 147464 | tf_op jit(solution)/shard_map/ppermute | solution.py:604
  116.6 24.7 %collective-permute-start.14 = (bf16[4096,128]{1,0:T(8,128)(2,1)}, bf16[4096,128]{1,0:T(8,128)(2,1)S(1)}, u32[]{:S(2)}, u32[]{:S(2)}) collective-permute-start(bf16[4096,128]{1,0:T(8,128)(2,1)} %get-tuple-element.64), channel_id=1, source_target_pairs={{1,0},{3,1},{2,3},{6,2},{4,6},{5,4},{7,5},{11,7},{9,11},{8,9},{10,... | collective-permute-start | bytes 3145736 | tf_op jit(solution)/shard_map/ppermute | solution.py:79
  118.9 24.5 %collective-permute-start.13 = (bf16[4096,128]{1,0:T(8,128)(2,1)}, bf16[4096,128]{1,0:T(8,128)(2,1)S(1)}, u32[]{:S(2)}, u32[]{:S(2)}) collective-permute-start(bf16[4096,128]{1,0:T(8,128)(2,1)} %get-tuple-element.64), channel_id=1, source_target_pairs={{0,1},{1,3},{3,2},{2,6},{6,4},{4,5},{5,7},{7,11},{11,9},{9,8},{8,1... | collective-permute-start | bytes 3145736 | tf_op jit(solution)/shard_map/ppermute | solution.py:79
  172.3 23.2 %collective-permute-start.16 = (bf16[4096,128]{1,0:T(8,128)(2,1)}, bf16[4096,128]{1,0:T(8,128)(2,1)S(1)}, u32[]{:S(2)}, u32[]{:S(2)}) collective-permute-start(bf16[4096,128]{1,0:T(8,128)(2,1)} %get-tuple-element.66), channel_id=1, source_target_pairs={{1,0},{3,1},{2,3},{6,2},{4,6},{5,4},{7,5},{11,7},{9,11},{8,9},{10,... | collective-permute-start | bytes 3145736 | tf_op jit(solution)/shard_map/ppermute | solution.py:79
  172.9 23.2 %collective-permute-start.15 = (bf16[4096,128]{1,0:T(8,128)(2,1)}, bf16[4096,128]{1,0:T(8,128)(2,1)S(1)}, u32[]{:S(2)}, u32[]{:S(2)}) collective-permute-start(bf16[4096,128]{1,0:T(8,128)(2,1)} %get-tuple-element.66), channel_id=1, source_target_pairs={{0,1},{1,3},{3,2},{2,6},{6,4},{4,5},{5,7},{7,11},{11,9},{9,8},{8,1... | collective-permute-start | bytes 3145736 | tf_op jit(solution)/shard_map/ppermute | solution.py:79
  231.3 17.1 %all-to-all-start.1 = ((bf16[16,64,128]{2,1,0:T(8,128)(2,1)}), bf16[16,64,128]{2,1,0:T(8,128)(2,1)}, u32[]{:S(2)}, u32[]{:S(2)}) async-start(bf16[16,64,128]{2,1,0:T(8,128)(2,1)} %bitcast.34), calls=%async_computation.1 | async-start | bytes 524288 | tf_op jit(solution)/shard_map/all_to_all | solution.py:582
  241.4 6.8 %collective-permute-start.17 = (bf16[78,360]{1,0:T(8,128)(2,1)S(1)}, bf16[78,360]{1,0:T(8,128)(2,1)S(1)}, u32[]{:S(2)}, u32[]{:S(2)}) collective-permute-start(bf16[78,360]{1,0:T(8,128)(2,1)S(1)} %slice.411), channel_id=1, source_target_pairs={{1,0},{2,1},{3,2},{4,3},{5,4},{6,5},{7,6},{8,7},{9,8},{10,9},{11,1... | collective-permute-start | bytes 168488 | tf_op jit(solution)/shard_map/ppermute | solution.py:51
  250.0 6.5 %collective-permute-start.18 = (bf16[78,360]{1,0:T(8,128)(2,1)S(1)}, bf16[78,360]{1,0:T(8,128)(2,1)S(1)}, u32[]{:S(2)}, u32[]{:S(2)}) collective-permute-start(bf16[78,360]{1,0:T(8,128)(2,1)S(1)} %slice.410), channel_id=1, source_target_pairs={{1,0},{2,1},{3,2},{4,3},{5,4},{6,5},{7,6},{8,7},{9,8},{10,9},{11,1... | collective-permute-start | bytes 168488 | tf_op jit(solution)/shard_map/ppermute | solution.py:51
  257.8 7.6 %collective-permute-start.19 = (bf16[78,360]{1,0:T(8,128)(2,1)S(1)}, bf16[78,360]{1,0:T(8,128)(2,1)S(1)}, u32[]{:S(2)}, u32[]{:S(2)}) collective-permute-start(bf16[78,360]{1,0:T(8,128)(2,1)S(1)} %slice.409), channel_id=1, source_target_pairs={{0,1},{1,2},{2,3},{3,4},{4,5},{5,6},{6,7},{7,8},{8,9},{9,10},{10,1... | collective-permute-start | bytes 168488 | tf_op jit(solution)/shard_map/ppermute | solution.py:51
  286.4 39.0 %collective-permute-start.20 = (bf16[2048,256]{1,0:T(8,128)(2,1)}, bf16[2048,256]{1,0:T(8,128)(2,1)}, u32[]{:S(2)}, u32[]{:S(2)}) collective-permute-start(bf16[2048,256]{1,0:T(8,128)(2,1)} %convert_element_type.241), channel_id=1, source_target_pairs={{0,0},{1,1},{3,2},{2,3},{6,4},{4,5},{5,6},{7,7},{11,8},{9,9},{8,10... | collective-permute-start | bytes 3145736 | tf_op jit(solution)/shard_map/ppermute | solution.py:664
  289.5 34.2 %copy-start.43 = (bf16[16,64,128]{2,1,0:T(8,128)(2,1)S(1)}, bf16[16,64,128]{2,1,0:T(8,128)(2,1)}, u32[]{:S(2)}) copy-start(bf16[16,64,128]{2,1,0:T(8,128)(2,1)} %copy-done.42) | copy-start | bytes 786436
  325.4 18.9 %collective-permute-start.21 = (bf16[4096,128]{1,0:T(8,128)(2,1)}, bf16[4096,128]{1,0:T(8,128)(2,1)}, u32[]{:S(2)}, u32[]{:S(2)}) collective-permute-start(bf16[4096,128]{1,0:T(8,128)(2,1)} %get-tuple-element.77), channel_id=1, source_target_pairs={{0,1},{1,3},{3,2},{2,6},{6,4},{4,5},{5,7},{7,11},{11,9},{9,8},{8,1... | collective-permute-start | bytes 3145736 | tf_op jit(solution)/shard_map/ppermute | solution.py:79
  326.0 19.0 %collective-permute-start.22 = (bf16[4096,128]{1,0:T(8,128)(2,1)}, bf16[4096,128]{1,0:T(8,128)(2,1)}, u32[]{:S(2)}, u32[]{:S(2)}) collective-permute-start(bf16[4096,128]{1,0:T(8,128)(2,1)} %get-tuple-element.78), channel_id=1, source_target_pairs={{1,0},{3,1},{2,3},{6,2},{4,6},{5,4},{7,5},{11,7},{9,11},{8,9},{10,... | collective-permute-start | bytes 3145736 | tf_op jit(solution)/shard_map/ppermute | solution.py:79
  353.5 33.2 %copy-start = (f32[2048,256]{1,0:T(8,128)S(1)}, f32[2048,256]{1,0:T(8,128)}, u32[]{:S(2)}) copy-start(f32[2048,256]{1,0:T(8,128)} %get-tuple-element.63.refs_0_.mesh_ref) | copy-start | bytes 6291460
  389.2 22.7 %collective-permute-start.23 = (bf16[4096,128]{1,0:T(8,128)(2,1)}, bf16[4096,128]{1,0:T(8,128)(2,1)}, u32[]{:S(2)}, u32[]{:S(2)}) collective-permute-start(bf16[4096,128]{1,0:T(8,128)(2,1)} %get-tuple-element.84), channel_id=1, source_target_pairs={{0,1},{1,3},{3,2},{2,6},{6,4},{4,5},{5,7},{7,11},{11,9},{9,8},{8,1... | collective-permute-start | bytes 3145736 | tf_op jit(solution)/shard_map/ppermute | solution.py:79
  396.1 18.0 %collective-permute-start.24 = (bf16[4096,128]{1,0:T(8,128)(2,1)S(1)}, bf16[4096,128]{1,0:T(8,128)(2,1)}, u32[]{:S(2)}, u32[]{:S(2)}) collective-permute-start(bf16[4096,128]{1,0:T(8,128)(2,1)S(1)} %copy-done.62), channel_id=1, source_target_pairs={{1,0},{3,1},{2,3},{6,2},{4,6},{5,4},{7,5},{11,7},{9,11},{8,9},{10,... | collective-permute-start | bytes 3145736 | tf_op jit(solution)/shard_map/ppermute | solution.py:79
  459.3 16.7 %collective-permute-start.25 = (bf16[4096,128]{1,0:T(8,128)(2,1)S(1)}, bf16[4096,128]{1,0:T(8,128)(2,1)S(1)}, u32[]{:S(2)}, u32[]{:S(2)}) collective-permute-start(bf16[4096,128]{1,0:T(8,128)(2,1)S(1)} %copy-done.63), channel_id=1, source_target_pairs={{0,1},{1,3},{3,2},{2,6},{6,4},{4,5},{5,7},{7,11},{11,9},{9,8},{8,1... | collective-permute-start | bytes 3145736 | tf_op jit(solution)/shard_map/ppermute | solution.py:79
  460.8 16.4 %collective-permute-start.26 = (bf16[4096,128]{1,0:T(8,128)(2,1)S(1)}, bf16[4096,128]{1,0:T(8,128)(2,1)S(1)}, u32[]{:S(2)}, u32[]{:S(2)}) collective-permute-start(bf16[4096,128]{1,0:T(8,128)(2,1)S(1)} %copy-done.61), channel_id=1, source_target_pairs={{1,0},{3,1},{2,3},{6,2},{4,6},{5,4},{7,5},{11,7},{9,11},{8,9},{10,... | collective-permute-start | bytes 3145736 | tf_op jit(solution)/shard_map/ppermute | solution.py:79
  506.6 3.1 collective-permute-start.27
  511.9 9.1 %collective-permute-start.30 = (bf16[2,2,2,72,256]{4,3,2,1,0:T(8,128)(2,1)S(1)}, bf16[2,2,2,72,256]{4,3,2,1,0:T(8,128)(2,1)S(1)}, u32[]{:S(2)}, u32[]{:S(2)}) collective-permute-start(bf16[2,2,2,72,256]{4,3,2,1,0:T(8,128)(2,1)S(1)} %fusion.38), channel_id=1, source_target_pairs={{0,2},{1,3},{2,0},{3,1},{4,6},{5,7},{6,4},{7,5},{8,10},{9,11},{10,... | collective-permute-start | bytes 884744 | tf_op jit(solution)/shard_map/ppermute | solution.py:96
  514.0 8.8 %collective-permute-start.28 = (bf16[2,2,2,72,256]{4,3,0,1,2:T(8,128)(2,1)S(1)}, bf16[2,2,2,72,256]{4,3,0,1,2:T(8,128)(2,1)S(1)}, u32[]{:S(2)}, u32[]{:S(2)}) collective-permute-start(bf16[2,2,2,72,256]{4,3,0,1,2:T(8,128)(2,1)S(1)} %fusion.39), channel_id=1, source_target_pairs={{0,1},{1,0},{2,3},{3,2},{4,5},{5,4},{6,7},{7,6},{8,9},{9,8},{10,11... | collective-permute-start | bytes 884744 | tf_op jit(solution)/shard_map/ppermute | solution.py:96
  521.1 5.2 collective-permute-start.31
  523.0 33.2 %copy-start.37 = (f32[78,512]{1,0:T(8,128)S(1)}, f32[78,512]{1,0:T(8,128)}, u32[]{:S(2)}) copy-start(f32[78,512]{1,0:T(8,128)} %get-tuple-element.149) | copy-start | bytes 479236
  523.0 5.2 collective-permute-start.29
  528.3 8.4 %collective-permute-start.34 = (bf16[2,72,256]{2,1,0:T(8,128)(2,1)S(1)}, bf16[2,72,256]{2,1,0:T(8,128)(2,1)S(1)}, u32[]{:S(2)}, u32[]{:S(2)}) collective-permute-start(bf16[2,72,256]{2,1,0:T(8,128)(2,1)S(1)} %fusion.67), channel_id=1, source_target_pairs={{0,4},{1,5},{2,6},{3,7},{4,0},{5,1},{6,2},{7,3},{8,12},{9,13},{10,... | collective-permute-start | bytes 221192 | tf_op jit(solution)/shard_map/ppermute | solution.py:96
  534.4 6.5 %collective-permute-start.32 = (bf16[2,72,256]{2,1,0:T(8,128)(2,1)S(1)}, bf16[2,72,256]{2,1,0:T(8,128)(2,1)S(1)}, u32[]{:S(2)}, u32[]{:S(2)}) collective-permute-start(bf16[2,72,256]{2,1,0:T(8,128)(2,1)S(1)} %fusion.66), channel_id=1, source_target_pairs={{0,4},{1,5},{2,6},{3,7},{4,0},{5,1},{6,2},{7,3},{8,12},{9,13},{10,... | collective-permute-start | bytes 221192 | tf_op jit(solution)/shard_map/ppermute | solution.py:96
  536.7 6.1 %collective-permute-start.35 = (bf16[72,256]{1,0:T(8,128)(2,1)S(1)}, bf16[72,256]{1,0:T(8,128)(2,1)S(1)}, u32[]{:S(2)}, u32[]{:S(2)}) collective-permute-start(bf16[72,256]{1,0:T(8,128)(2,1)S(1)} %fusion.75), channel_id=1, source_target_pairs={{0,8},{1,9},{2,10},{3,11},{4,12},{5,13},{6,14},{7,15},{8,0},{9,1},... | collective-permute-start | bytes 110600 | tf_op jit(solution)/shard_map/ppermute | solution.py:96
  540.9 4.9 collective-permute-start.33
  547.3 1.2 collective-permute-start.36
  548.6 3.6 collective-permute-start.37
  552.2 3.6 collective-permute-start.38
  555.8 3.6 collective-permute-start.39
  559.4 6.5 %collective-permute-start.40 = (f32[8,128]{1,0:T(8,128)S(1)}, f32[8,128]{1,0:T(8,128)S(1)}, u32[]{:S(2)}, u32[]{:S(2)}) collective-permute-start(f32[8,128]{1,0:T(8,128)S(1)} %add.241), channel_id=1, source_target_pairs={{0,8},{1,9},{2,10},{3,11},{4,12},{5,13},{6,14},{7,15},{8,0},{9,1},... | collective-permute-start | bytes 12296 | tf_op jit(solution)/shard_map/ppermute | solution.py:96
  564.0 24.3 %collective-permute-start.41 = (bf16[2048,256]{1,0:T(8,128)(2,1)S(1)}, bf16[2048,256]{1,0:T(8,128)(2,1)S(1)}, u32[]{:S(2)}, u32[]{:S(2)}) collective-permute-start(bf16[2048,256]{1,0:T(8,128)(2,1)S(1)} %copy-done.34), channel_id=1, source_target_pairs={{0,0},{1,1},{3,2},{2,3},{6,4},{4,5},{5,6},{7,7},{11,8},{9,9},{8,10... | collective-permute-start | bytes 3145736 | tf_op jit(solution)/shard_map/ppermute | solution.py:709
  (60 other events, 333.4 us)

commit v5 on v4

--- a/solution.py
+++ b/solution.py
@@ -16,8 +16,6 @@
 NEAR = 358
 STEP = 10
 H = 2048
-TABLES = 4
-UNROLL = 32
 ALL = ("dp", "space")
 LIMIT = pltpu.CompilerParams(vmem_limit_bytes=56 * 2**20)
 
@@ -267,12 +265,34 @@
     return [CH, D, D, CH] + [D] * (5 * ROUNDS) + [3 + 2 * ROUNDS]
 
 
-def gather_rows(index, before, own, after):
-    edges = index.shape[0]
-    chunk = 1024
+def weave(ref, value):
+    rows = value.shape[0]
+    ref[pl.ds(0, rows, stride=2), :] = value[:, :HALF]
+    ref[pl.ds(1, rows, stride=2), :] = value[:, HALF:]
+
+
+def unweave(ref):
+    rows = ref.shape[0] // 2
+    return ref[pl.ds(0, rows, stride=2), :], ref[pl.ds(1, rows, stride=2), :]
+
+
+def whole(shape):
+    return pl.BlockSpec(shape, lambda *_: (0,) * len(shape))
+
+
+def round_forward(index, mesh, before, own, after, mats, bias, following):
+    blocks = mesh.shape[0]
+    tile, chunk = 512, 16
+    turns, high = tile // chunk, 2 * chunk
+    more = following is not None
     spans = [before.shape[0], own.shape[0], after.shape[0]]
-
-    def body(index_ref, before_ref, own_ref, after_ref, out_ref, table, sems):
+    reach = sum(spans)
+
+    def body(*refs):
+        index_ref, mesh_ref, before_ref, own_ref, after_ref, mats_ref, bias_ref = refs[:7]
+        next_ref, sent_ref = (refs[7], refs[13]) if more else (None, None)
+        new_ref, back_ref, update_ref, agg_ref, slope_ref = refs[8:13] if more else refs[7:12]
+        raw, table, rows, wide, wider, sems = refs[-6:]
         step = pl.program_id(0)
 
         @pl.when(step == 0)
@@ -281,7 +301,7 @@
             start = 0
             for n, (source, span) in enumerate(zip((before_ref, own_ref, after_ref), spans)):
                 copies.append(
-                    pltpu.make_async_copy(source, table.at[pl.ds(start, span)], sems.at[n])
+                    pltpu.make_async_copy(source, raw.at[pl.ds(start, span)], sems.at[n])
                 )
                 start = start + span
             for copy in copies:
@@ -289,69 +309,55 @@
             for copy in copies:
                 copy.wait()
 
-        def some(i, carry):
-            at = i * UNROLL
-            base = step * chunk + at
-            rows = [table[index_ref[base + u]] for u in range(UNROLL)]
-            for u in range(UNROLL):
-                out_ref[at + u] = rows[u]
-            return carry
-
-        lax.fori_loop(0, chunk // UNROLL, some, 0)
-
-    return pl.pallas_call(
-        body,
-        grid_spec=pltpu.PrefetchScalarGridSpec(
-            num_scalar_prefetch=1,
-            grid=(edges // chunk,),
-            in_specs=[pl.BlockSpec(memory_space=pl.ANY)] * 3,
-            out_specs=pl.BlockSpec((chunk, 2, HALF), lambda i, *_: (i, 0, 0)),
-            scratch_shapes=[
-                pltpu.VMEM((sum(spans), 2, HALF), own.dtype),
-                pltpu.SemaphoreType.DMA((3,)),
-            ],
-        ),
-        out_shape=jax.ShapeDtypeStruct((edges, 2, HALF), own.dtype),
-        compiler_params=LIMIT,
-        cost_estimate=cost(16),
-        name="gather_rows",
-    )(index, before, own, after)
-
-
-def weave(ref, value):
-    rows = value.shape[0]
-    ref[pl.ds(0, rows, stride=2), :] = value[:, :HALF]
-    ref[pl.ds(1, rows, stride=2), :] = value[:, HALF:]
-
-
-def unweave(ref):
-    rows = ref.shape[0] // 2
-    return ref[pl.ds(0, rows, stride=2), :], ref[pl.ds(1, rows, stride=2), :]
-
-
-def whole(shape):
-    return pl.BlockSpec(shape, lambda *_: (0,) * len(shape))
-
-
-def round_forward(mesh, edges, mats, bias, following):
-    blocks = mesh.shape[0]
-    tile = 256
-    more = following is not None
-
-    def body(*refs):
-        if more:
-            (mesh_ref, edge_ref, mats_ref, bias_ref, next_ref, new_ref, uin_ref, agg_ref, sent_ref, wide) = refs
-        else:
-            (mesh_ref, edge_ref, mats_ref, bias_ref, new_ref, uin_ref, agg_ref, wide) = refs
+            @pl.loop(0, reach // 256)
+            def _(i):
+                at = pl.multiple_of(i * 256, 256)
+                table[pl.ds(at, 256), :] = raw[pl.ds(at, 256), :].astype(jnp.float32)
+
         mesh_in = mesh_ref[...]
         lowered = mesh_in.astype(jnp.bfloat16)
         weave(wide, inner(lowered, mats_ref[1], 1, 0) + bias_ref[0:1, :])
-        dest = wide[...]
-        total = jnp.zeros(dest.shape, jnp.float32)
-        for edge in range(K):
-            total = total + silu(edge_ref[edge].astype(jnp.float32) + dest)
-        wide[...] = total * (1.0 / K)
-        first, second = unweave(wide)
+
+        def fetch(turn):
+            for edge in range(K):
+                base = edge * blocks + step * tile + turn * chunk
+                values = [
+                    table[pl.ds(pl.multiple_of(index_ref[base + u], 2), 2), :] for u in range(chunk)
+                ]
+                for u in range(chunk):
+                    spot = pl.multiple_of(edge * 2 * tile + turn * high + 2 * u, 2)
+                    rows[pl.ds(spot, 2), :] = values[u]
+
+        def load(turn):
+            at = pl.multiple_of(turn * high, high)
+            taken = [
+                rows[pl.ds(pl.multiple_of(edge * 2 * tile + turn * high, high), high), :]
+                for edge in range(K)
+            ]
+            return at, wide[pl.ds(at, high), :], taken
+
+        def dense(at, dest, taken):
+            total = None
+            for edge in range(K):
+                value = taken[edge] + dest
+                sigma = sigmoid(value)
+                out = value * sigma
+                slope_ref[edge, pl.ds(at, high), :] = (sigma + out * (1.0 - sigma)).astype(
+                    jnp.bfloat16
+                )
+                total = out if total is None else total + out
+            wider[pl.ds(at, high), :] = total * (1.0 / K)
+
+        def some(turn, carry):
+            loaded = load(turn - 1)
+            fetch(turn)
+            dense(*loaded)
+            return carry
+
+        fetch(0)
+        lax.fori_loop(1, turns, some, 0)
+        dense(*load(turns - 1))
+        first, second = unweave(wider)
         first, second = first.astype(jnp.bfloat16), second.astype(jnp.bfloat16)
         agg_ref[:, :HALF] = first
         agg_ref[:, HALF:] = second
@@ -361,24 +367,29 @@
             + inner(lowered, mats_ref[3], 1, 0)
             + bias_ref[1:2, :]
         )
-        uin_ref[...] = update_in
-        update = silu(update_in).astype(jnp.bfloat16)
+        sigma = sigmoid(update_in)
+        out = update_in * sigma
+        back_ref[...] = sigma + out * (1.0 - sigma)
+        update = out.astype(jnp.bfloat16)
+        update_ref[...] = update
         new = mesh_in + inner(update, mats_ref[4], 1, 0)
         new_ref[...] = new
         if more:
             weave(wide, inner(new.astype(jnp.bfloat16), next_ref[...], 1, 0))
             sent_ref[...] = wide[...].astype(jnp.bfloat16)
 
-    rows = pl.BlockSpec((tile, D), lambda i: (i, 0))
-    woven = pl.BlockSpec((2 * tile, HALF), lambda i: (i, 0))
-    ins = [rows, pl.BlockSpec((K, 2 * tile, HALF), lambda i: (0, i, 0)), whole(mats.shape), whole(bias.shape)]
-    outs = [rows, rows, rows]
+    whole_rows = pl.BlockSpec((tile, D), lambda i, *_: (i, 0))
+    woven = pl.BlockSpec((2 * tile, HALF), lambda i, *_: (i, 0))
+    ins = [whole_rows] + [pl.BlockSpec(memory_space=pl.ANY)] * 3 + [whole(mats.shape), whole(bias.shape)]
+    outs = [whole_rows] * 4 + [pl.BlockSpec((K, 2 * tile, HALF), lambda i, *_: (0, i, 0))]
     shapes = [
         jax.ShapeDtypeStruct((blocks, D), jnp.float32),
         jax.ShapeDtypeStruct((blocks, D), jnp.float32),
         jax.ShapeDtypeStruct((blocks, D), jnp.bfloat16),
+        jax.ShapeDtypeStruct((blocks, D), jnp.bfloat16),
+        jax.ShapeDtypeStruct((K, 2 * blocks, HALF), jnp.bfloat16),
     ]
-    args = [mesh, edges, mats, bias]
+    args = [index, mesh, before, own, after, mats, bias]
     if more:
         ins.append(whole(following.shape))
         outs.append(woven)
@@ -386,82 +397,113 @@
         args.append(following)
     return pl.pallas_call(
         body,
-        grid=(blocks // tile,),
-        in_specs=ins,
-        out_specs=outs,
+        grid_spec=pltpu.PrefetchScalarGridSpec(
+            num_scalar_prefetch=1,
+            grid=(blocks // tile,),
+            in_specs=ins,
+            out_specs=outs,
+            scratch_shapes=[
+                pltpu.VMEM((reach, HALF), jnp.bfloat16),
+                pltpu.VMEM((reach, HALF), jnp.float32),
+                pltpu.VMEM((K * 2 * tile, HALF), jnp.float32),
+                pltpu.VMEM((2 * tile, HALF), jnp.float32),
+                pltpu.VMEM((2 * tile, HALF), jnp.float32),
+                pltpu.SemaphoreType.DMA((3,)),
+            ],
+        ),
         out_shape=shapes,
-        scratch_shapes=[pltpu.VMEM((2 * tile, HALF), jnp.float32)],
         compiler_params=LIMIT,
-        cost_estimate=cost(11),
+        cost_estimate=cost(25),
         name="round_forward",
     )(*args)
 
 
-def edges_backward(index, grad_mesh, mesh, uin, edges, mats, bias):
-    blocks = mesh.shape[0]
-    tile = 256
-    steps = blocks // tile
+def edges_backward(index, grad_mesh, back, slopes, turned):
+    blocks = grad_mesh.shape[0]
+    tile, chunk = 512, 16
+    steps, turns, high = blocks // tile, tile // chunk, 2 * chunk
     reach = 2 * (blocks + 2 * H)
 
     def body(
-        index_ref, grad_ref, mesh_ref, uin_ref, edge_ref, mats_ref, bias_ref,
+        index_ref, grad_ref, back_ref, slope_ref, turned_ref,
         guin_ref, low_ref, before_ref, own_ref, after_ref, wide, wider, flows, *tables,
     ):
         step = pl.program_id(0)
 
         @pl.when(step == 0)
         def _():
-            for table in tables:
-                table[...] = jnp.zeros(table.shape, jnp.float32)
+            @pl.loop(0, reach // 256)
+            def _(i):
+                for table in tables:
+                    table[pl.ds(pl.multiple_of(i * 256, 256), 256), :] = jnp.zeros(
+                        (256, HALF), jnp.float32
+                    )
 
         grad_out = grad_ref[...].astype(jnp.bfloat16)
-        grad_update = inner(grad_out, mats_ref[4], 1, 1)
-        grad_uin = (grad_update * slope(uin_ref[...])).astype(jnp.bfloat16)
+        grad_uin = (inner(grad_out, turned_ref[4], 1, 0) * back_ref[...]).astype(jnp.bfloat16)
         guin_ref[...] = grad_uin
-        weave(wide, inner(grad_uin, mats_ref[2], 1, 1) * (1.0 / K))
-        lowered = mesh_ref[...].astype(jnp.bfloat16)
-        weave(wider, inner(lowered, mats_ref[1], 1, 0) + bias_ref[0:1, :])
-        grad_agg = wide[...]
-        dest = wider[...]
-        grad_dest = jnp.zeros(dest.shape, jnp.float32)
-        for edge in range(K):
-            flow = grad_agg * slope(edge_ref[edge].astype(jnp.float32) + dest)
-            grad_dest = grad_dest + flow
-            flows[edge * 2 * tile : (edge + 1) * 2 * tile, :] = flow
-        wide[...] = grad_dest
-        first, second = unweave(wide)
+        weave(wide, inner(grad_uin, turned_ref[2], 1, 0) * (1.0 / K))
+
+        def dense(turn):
+            at = pl.multiple_of(turn * high, high)
+            grad_agg = wide[pl.ds(at, high), :]
+            total, parts = None, []
+            for edge in range(K):
+                flow = grad_agg * slope_ref[edge, pl.ds(at, high), :].astype(jnp.float32)
+                parts.append(flow)
+                total = flow if total is None else total + flow
+            return at, total, parts
+
+        def keep(turn, at, total, parts):
+            for edge in range(K):
+                spot = pl.multiple_of(edge * 2 * tile + turn * high, high)
+                flows[pl.ds(spot, high), :] = parts[edge]
+            wider[pl.ds(at, high), :] = total
+
+        def scatter(turn):
+            for u in range(chunk):
+                spots, sums = [], []
+                for edge in range(K):
+                    base = edge * blocks + step * tile + turn * chunk
+                    spots.append(pl.multiple_of(index_ref[base + u], 2))
+                for edge in range(K):
+                    spot = pl.multiple_of(edge * 2 * tile + turn * high + 2 * u, 2)
+                    sums.append(tables[edge][pl.ds(spots[edge], 2), :] + flows[pl.ds(spot, 2), :])
+                for edge in range(K):
+                    tables[edge][pl.ds(spots[edge], 2), :] = sums[edge]
+
+        def some(turn, carry):
+            found = dense(turn)
+            scatter(turn - 1)
+            keep(turn, *found)
+            return carry
+
+        keep(0, *dense(0))
+        lax.fori_loop(1, turns, some, 0)
+        scatter(turns - 1)
+        first, second = unweave(wider)
         low_ref[:, :HALF] = first.astype(jnp.bfloat16)
         low_ref[:, HALF:] = second.astype(jnp.bfloat16)
-        for edge in range(K):
-
-            def some(i, carry):
-                at = i * UNROLL
-                base = edge * blocks + step * tile + at
-                for first in range(0, UNROLL, TABLES):
-                    spots, rows, sums = [], [], []
-                    for u in range(first, first + TABLES):
-                        spots.append(pl.multiple_of(index_ref[base + u] * 2, 2))
-                        spot = pl.multiple_of(2 * (edge * tile + at + u), 2)
-                        rows.append(flows[pl.ds(spot, 2), :])
-                    for u in range(TABLES):
-                        sums.append(tables[u][pl.ds(spots[u], 2), :] + rows[u])
-                    for u in range(TABLES):
-                        tables[u][pl.ds(spots[u], 2), :] = sums[u]
-                return carry
-
-            lax.fori_loop(0, tile // UNROLL, some, 0)
 
         @pl.when(step == steps - 1)
         def _():
-            def summed(start, size):
-                value = tables[0][start : start + size, :]
+            def summed(at):
+                value = tables[0][pl.ds(at, 256), :]
                 for table in tables[1:]:
-                    value = value + table[start : start + size, :]
+                    value = value + table[pl.ds(at, 256), :]
                 return value
 
-            before_ref[...] = summed(0, 2 * H).astype(jnp.bfloat16)
-            own_ref[...] = summed(2 * H, 2 * blocks)
-            after_ref[...] = summed(2 * H + 2 * blocks, 2 * H).astype(jnp.bfloat16)
+            @pl.loop(0, 2 * H // 256)
+            def _(i):
+                at = pl.multiple_of(i * 256, 256)
+                far = pl.multiple_of(2 * H + 2 * blocks + at, 256)
+                before_ref[pl.ds(at, 256), :] = summed(at).astype(jnp.bfloat16)
+                after_ref[pl.ds(at, 256), :] = summed(far).astype(jnp.bfloat16)
+
+            @pl.loop(0, 2 * blocks // 256)
+            def _(i):
+                at = pl.multiple_of(i * 256, 256)
+                own_ref[pl.ds(at, 256), :] = summed(pl.multiple_of(2 * H + at, 256))
 
     rows = pl.BlockSpec((tile, D), lambda i, *_: (i, 0))
     return pl.pallas_call(
@@ -470,9 +512,9 @@
             num_scalar_prefetch=1,
             grid=(steps,),
             in_specs=[
-                rows, rows, rows,
+                rows, rows,
                 pl.BlockSpec((K, 2 * tile, HALF), lambda i, *_: (0, i, 0)),
-                whole(mats.shape), whole(bias.shape),
+                whole(turned.shape),
             ],
             out_specs=[
                 rows, rows,
@@ -483,7 +525,7 @@
                 pltpu.VMEM((2 * tile, HALF), jnp.float32),
                 pltpu.VMEM((2 * tile * K, HALF), jnp.float32),
             ]
-            + [pltpu.VMEM((reach, HALF), jnp.float32)] * TABLES,
+            + [pltpu.VMEM((reach, HALF), jnp.float32)] * K,
         ),
         out_shape=[
             jax.ShapeDtypeStruct((blocks, D), jnp.bfloat16),
@@ -493,16 +535,18 @@
             jax.ShapeDtypeStruct((2 * H, HALF), jnp.bfloat16),
         ],
         compiler_params=LIMIT,
-        cost_estimate=cost(33),
+        cost_estimate=cost(25),
         name="edges_backward",
-    )(index, grad_mesh, mesh, uin, edges, mats, bias)
-
-
-def round_backward(grad_mesh, own, first, last, grad_uin, dest_low, mats):
+    )(index, grad_mesh, back, slopes, turned)
+
+
+def round_backward(grad_mesh, own, first, last, grad_uin, dest_low, turned):
     blocks = grad_mesh.shape[0]
-    tile = 256
-
-    def body(grad_ref, own_ref, first_ref, last_ref, guin_ref, dest_ref, mats_ref, new_ref, sent_ref, wide):
+    tile = 1024
+
+    def body(
+        grad_ref, own_ref, first_ref, last_ref, guin_ref, dest_ref, turned_ref, new_ref, sent_ref, wide
+    ):
         wide[...] = (
             own_ref[...] + first_ref[...].astype(jnp.float32) + last_ref[...].astype(jnp.float32)
         )
@@ -512,10 +556,10 @@
         sent_ref[:, HALF:] = two
         new_ref[...] = (
             grad_ref[...]
-            + inner(guin_ref[...], mats_ref[3], 1, 1)
-            + inner(dest_ref[...], mats_ref[1], 1, 1)
-            + inner(one, mats_ref[0, :, :HALF], 1, 1)
-            + inner(two, mats_ref[0, :, HALF:], 1, 1)
+            + inner(guin_ref[...], turned_ref[3], 1, 0)
+            + inner(dest_ref[...], turned_ref[1], 1, 0)
+            + inner(one, turned_ref[0, :HALF, :], 1, 0)
+            + inner(two, turned_ref[0, HALF:, :], 1, 0)
         )
 
     rows = pl.BlockSpec((tile, D), lambda i: (i, 0))
@@ -523,7 +567,7 @@
     return pl.pallas_call(
         body,
         grid=(blocks // tile,),
-        in_specs=[rows, woven, woven, woven, rows, rows, whole(mats.shape)],
+        in_specs=[rows, woven, woven, woven, rows, rows, whole(turned.shape)],
         out_specs=[rows, rows],
         out_shape=[
             jax.ShapeDtypeStruct((blocks, D), jnp.float32),
@@ -531,9 +575,9 @@
         ],
         scratch_shapes=[pltpu.VMEM((2 * tile, HALF), jnp.float32)],
         compiler_params=LIMIT,
-        cost_estimate=cost(8),
+        cost_estimate=cost(7),
         name="round_backward",
-    )(grad_mesh, own, first, last, grad_uin, dest_low, mats)
+    )(grad_mesh, own, first, last, grad_uin, dest_low, turned)
 
 
 def shards(walk, master, moment1, moment2, inputs, targets, valid, owner, slot, neighbours, partner):
@@ -600,7 +644,7 @@
     gathered = inner(chooser, encoded, 0, 0).astype(jnp.bfloat16)
     node_in = inner(gathered, w_node, 1, 0) + b_head[1]
     mesh = silu(node_in)
-    index = ((neighbours - band * blocks + H) % (blocks * bands)).T.reshape(-1)
+    index = 2 * ((neighbours - band * blocks + H) % (blocks * bands)).T.reshape(-1)
     index = lax.ppermute(index, "space", list(enumerate(walk)))
     home = [(place, n) for n, place in enumerate(walk)]
     kept = []
@@ -608,15 +652,13 @@
     sent = sent.reshape(2 * blocks, HALF)
     for layer in range(ROUNDS):
         before, after = halo(walk, sent[2 * (blocks - H) :], sent[: 2 * H])
-        edges = gather_rows(
-            index,
-            before.reshape(H, 2, HALF),
-            sent.reshape(blocks, 2, HALF),
-            after.reshape(H, 2, HALF),
-        ).reshape(K, 2 * blocks, HALF)
+        if layer == 0:
+            before, turned = lax.optimization_barrier((before, jnp.swapaxes(w_round, 2, 3)))
         following = w_round[layer + 1, 0] if layer + 1 < ROUNDS else None
-        new, uin, agg, *rest = round_forward(mesh, edges, w_round[layer], b_round[layer], following)
-        kept.append((mesh, edges, uin, agg))
+        new, back, update, agg, slopes, *rest = round_forward(
+            index, mesh, before, sent, after, w_round[layer], b_round[layer], following
+        )
+        kept.append((mesh, back, update, agg, slopes))
         mesh = new
         sent = rest[0] if rest else None
     fetched = inner(chooser, mesh.astype(jnp.bfloat16), 1, 0).astype(jnp.bfloat16)
@@ -665,10 +707,9 @@
     mats_grads = [None] * (5 * ROUNDS)
     bias_grads = [None] * (2 * ROUNDS)
     for layer in reversed(range(ROUNDS)):
-        old, edges, uin, agg = kept[layer]
-        mats = w_round[layer]
+        old, back, update, agg, slopes = kept[layer]
         grad_uin, dest_low, to_before, own, to_after = edges_backward(
-            index, grad_mesh, old, uin, edges, mats, b_round[layer]
+            index, grad_mesh, back, slopes, turned[layer]
         )
         if layer == ROUNDS - 1:
             to_before, to_after, final_mesh = lax.optimization_barrier(
@@ -677,7 +718,6 @@
         from_before, from_after = halo(walk, to_after, to_before)
         lowered = old.astype(jnp.bfloat16)
         grad_out = grad_mesh.astype(jnp.bfloat16)
-        update = silu(uin).astype(jnp.bfloat16)
         grads = [
             None,
             inner(lowered, dest_low, 0, 0),
@@ -688,11 +728,13 @@
         bias_grads[2 * layer] = jnp.sum(dest_low.astype(jnp.float32), 0, keepdims=True)
         bias_grads[2 * layer + 1] = jnp.sum(grad_uin.astype(jnp.float32), 0, keepdims=True)
         grad_mesh, sent_low = round_backward(
-            grad_mesh, own, from_before, from_after, grad_uin, dest_low, mats
+            grad_mesh, own, from_before, from_after, grad_uin, dest_low, turned[layer]
         )
         grads[0] = inner(lowered, sent_low, 0, 0)
         mats_grads[5 * layer : 5 * layer + 5] = grads
     leaving = grad_mesh.astype(jnp.bfloat16)
+    early = lax.ppermute(leaving[: blocks // 2], "space", home)
+    leaving = leaving[blocks // 2 :]
     grad_node = (grad_mesh * slope(node_in)).astype(jnp.bfloat16)
     grad_bnode = jnp.sum(grad_node.astype(jnp.float32), 0)
     grad_wnode = inner(gathered, grad_node, 0, 0)
@@ -701,16 +743,18 @@
     grad_enc = (grad_encoded * slope(enc_in)).astype(jnp.bfloat16)
     grad_bin = jnp.sum(grad_enc.astype(jnp.float32), 0)
     grad_win = inner(arrived, grad_enc, 0, 0)
+    grad_win, early = lax.optimization_barrier((grad_win, early))
     parts = [grad_win, grad_wnode, grad_wdec, grad_wout.reshape(CH, D)]
     parts = parts + mats_grads
     parts.append(jnp.concatenate([jnp.stack([grad_bin, grad_bnode, grad_bdec])] + bias_grads, 0))
     keep, send = collect_rows(parts, total_size, peers, place)
     mine, leaving = reduced_piece(keep, send, leaving)
-    node_grads = lax.ppermute(leaving, "space", home)
+    late = lax.ppermute(leaving, "space", home)
     mine = lax.dynamic_slice_in_dim(mine.reshape(-1), offset, shard)
     lane = lax.broadcasted_iota(jnp.int32, (8, HALF), 1)
     sums = summed_everywhere(jnp.where(lane == 0, local_total, jnp.sum(mine * mine)))
     total, norm = sums[0, 0], jnp.sqrt(sums[0, 1])
+    node_grads = jnp.concatenate([early, late], 0)
     clipped = mine * jnp.minimum(1.0, 0.05 / norm)
     first = 0.9 * moment1 + 0.1 * clipped
     second = 0.999 * moment2 + 0.001 * clipped * clipped

time: 604 us -> 560 us (0.927)
  Pallas kernels: 217 us -> 173 us
    pallas_call x3, Pallas kernels: 99.1 us -> 72.4 us  [edges_backward(): pl.pallas_call(body, grid_spec=pltpu.PrefetchScalarGridSpec(num_scalar_pr...]
    ppermute x6, waiting for transfers between devices: 31.6 us -> 50.6 us  [halo(): lax.ppermute(last, 'space', up)]
    ppermute x1, waiting for transfers between devices: 13.3 us -> 0.01 us  [shards(): index = lax.ppermute(index, 'space', list(enumerate(walk)))]
    pallas_call x6 -> x3, Pallas kernels: 83 us -> 74.1 us  [round_forward(): pl.pallas_call(body, grid_spec=pltpu.PrefetchScalarGridSpec(num_scalar_pr...]
    pallas_call x3, Pallas kernels: 25.7 us -> 17.3 us  [round_backward(): pl.pallas_call(body, grid=(blocks // tile,), in_specs=[rows, woven, woven...]
    ppermute x1 -> x2, waiting for transfers between devices: 20 us -> 13.3 us  [the longest x1 8.79 us: shards(): late = lax.ppermute(leaving, 'space', home)]
  transfers between devices with their start and end apart: 44 -> 45, of which waited for: 35 -> 35; matrix products, arithmetic and copies ran while one was open for 7% -> 8% of each run, Pallas kernels for 6% -> 4%
where the time goes in v5:
time: 560 us; the launch traced here: 549 us
  Pallas kernels  173 us (31%)
  waiting for transfers between devices  162 us (29%)
  starting transfers between devices  86.8 us (16%)
  matrix products  50.9 us (9%)
  other arithmetic  27.2 us (5%)
  local copies, waits for them, and re-layouts  27.2 us (5%)
  blocking collectives  13.6 us (2%)
  between operations  8.41 us (2%)
    pallas_call x3, Pallas kernels, round_forward(): pl.pallas_call(body, grid_spec=pltpu.PrefetchScalarGridSpec(num_scalar_pr...  74.1 us
    pallas_call x3, Pallas kernels, edges_backward(): pl.pallas_call(body, grid_spec=pltpu.PrefetchScalarGridSpec(num_scalar_pr...  72.4 us
    ppermute x6, waiting for transfers between devices, halo(): lax.ppermute(last, 'space', up)  50.6 us
    dot_general x31, matrix products, inner(): lax.dot_general(left, right, (((left_dim,), (right_dim,)), ((), ())), pre...  50.5 us
    ppermute x24, waiting for transfers between devices, swapped(): lax.ppermute(value, axis, [(i, i ^ bit) for i in range(lax.axis_size(axis...  46.6 us
    ppermute x6, waiting for transfers between devices, halo(): lax.ppermute(initial, 'space', down)  46.1 us
    ppermute x24, starting transfers between devices, swapped(): lax.ppermute(value, axis, [(i, i ^ bit) for i in range(lax.axis_size(axis...  27.7 us
    pallas_call x3, Pallas kernels, round_backward(): pl.pallas_call(body, grid=(blocks // tile,), in_specs=[rows, woven, woven...  17.3 us
  transfers between devices with their start and end apart: 45, of which 35 were waited for; matrix products, arithmetic and copies ran while one was open for 8% of the time, Pallas kernels for 4%

profile of v5, /device:TPU:12, one launch (start us, length us, event | category | flops | bytes accessed | tf_op | source)
XLA Modules:
  0.0 549.3 jit_solution(2969974390867397937)
XLA Ops:
  5.8 2.7 collective-permute-start.5
  15.4 7.2 %all-to-all-start = ((bf16[16,64,128]{2,1,0:T(8,128)(2,1)}), bf16[16,64,128]{2,1,0:T(8,128)(2,1)S(1)}, u32[]{:S(2)}, u32[]{:S(2)}) async-start(bf16[16,64,128]{2,1,0:T(8,128)(2,1)} %bitcast.5), calls=%async_computation | async-start | bytes 524288 | tf_op jit(solution)/shard_map/all_to_all | solution.py:626
  24.8 4.7 collective-permute-done.6
  31.7 4.6 collective-permute-done.3
  37.7 5.3 collective-permute-done.4
  46.8 4.2 spread_rows.1
  55.5 2.6 fusion.95
  64.1 3.2 collective-permute-start
  73.0 15.5 %collective-permute-done.11.refs_2_ = bf16[4096,128]{1,0:T(8,128)(2,1)} collective-permute-done((bf16[4096,128]{1,0:T(8,128)(2,1)}, bf16[4096,128]{1,0:T(8,128)(2,1)}, u32[]{:S(2)}, u32[]{:S(2)}) %collective-permute-start.11) | collective-permute-done | bytes 1048608 | tf_op jit(solution)/shard_map/ppermute | solution.py:77
  89.2 24.9 %round_forward.3 = (f32[2048,256]{1,0:T(8,128)}, f32[2048,256]{1,0:T(8,128)}, bf16[2048,256]{1,0:T(8,128)(2,1)}, bf16[2048,256]{1,0:T(8,128)(2,1)}, bf16[6,4096,...) custom-call(s32[12288]{0:T(1024)} %copy-done.18, f32[2048,256]{1,0:T(8,128)} %get-tuple-element.176.refs_1_, ...), custom_call_target="tpu_custom_call" | custom-call | bytes 75000000 | tf_op jit(solution)/shard_map/round_forward/pallas_call | solution.py:398
  116.5 22.2 %collective-permute-done.14.refs_4_ = bf16[4096,128]{1,0:T(8,128)(2,1)S(1)} collective-permute-done((bf16[4096,128]{1,0:T(8,128)(2,1)}, bf16[4096,128]{1,0:T(8,128)(2,1)S(1)}, u32[]{:S(2)}, u32[]{:S(2)}) %collective-permute-start.14) | collective-permute-done | bytes 1048608 | tf_op jit(solution)/shard_map/ppermute | solution.py:77
  141.6 25.1 %round_forward.4 = (f32[2048,256]{1,0:T(8,128)}, f32[2048,256]{1,0:T(8,128)}, bf16[2048,256]{1,0:T(8,128)(2,1)}, bf16[2048,256]{1,0:T(8,128)(2,1)}, bf16[6,4096,...) custom-call(s32[12288]{0:T(1024)} %copy-done.18, f32[2048,256]{1,0:T(8,128)} %get-tuple-element.74.refs_1_, ...), custom_call_target="tpu_custom_call" | custom-call | bytes 75000000 | tf_op jit(solution)/shard_map/round_forward/pallas_call | solution.py:398
  169.0 20.9 %collective-permute-done.16.refs_4_ = bf16[4096,128]{1,0:T(8,128)(2,1)S(1)} collective-permute-done((bf16[4096,128]{1,0:T(8,128)(2,1)}, bf16[4096,128]{1,0:T(8,128)(2,1)S(1)}, u32[]{:S(2)}, u32[]{:S(2)}) %collective-permute-start.16) | collective-permute-done | bytes 1048608 | tf_op jit(solution)/shard_map/ppermute | solution.py:77
  191.9 24.1 %round_forward.5 = (f32[2048,256]{1,0:T(8,128)}, f32[2048,256]{1,0:T(8,128)}, bf16[2048,256]{1,0:T(8,128)(2,1)}, bf16[2048,256]{1,0:T(8,128)(2,1)}, bf16[6,4096,128]{2,1,0:T(8,128)(2,1)}) custom-call(s32[12288]{0:T(1024)} %copy-done.18, f32[2048,256]{1,0:T(8,128)} %get-tuple-element.76.refs_1_, bf16[4096,128]{1,0:T(8,128)(2,1)} %copy-done.41, ...), custom_call_target="tpu_custom_call" | custom-call | bytes 75000000 | tf_op jit(solution)/shard_map/round_forward/pallas_call | solution.py:398
  221.4 9.5 %all-to-all-start.1 = ((bf16[16,64,128]{2,1,0:T(8,128)(2,1)}), bf16[16,64,128]{2,1,0:T(8,128)(2,1)S(1)}, u32[]{:S(2)}, u32[]{:S(2)}) async-start(bf16[16,64,128]{2,1,0:T(8,128)(2,1)} %bitcast.23), calls=%async_computation.1 | async-start | bytes 524288 | tf_op jit(solution)/shard_map/all_to_all | solution.py:626
  231.0 3.4 collective-permute-start.17
  234.4 3.4 collective-permute-done.17
  238.4 3.9 collective-permute-start.18
  246.4 5.7 %collective-permute-start.19 = (bf16[78,360]{1,0:T(8,128)(2,1)S(1)}, bf16[78,360]{1,0:T(8,128)(2,1)S(1)}, u32[]{:S(2)}, u32[]{:S(2)}) collective-permute-start(bf16[78,360]{1,0:T(8,128)(2,1)S(1)} %slice.431), channel_id=1, source_target_pairs={{0,1},{1,2},{2,3},{3,4},{4,5},{5,6},{6,7},{7,8},{8,9},{9,10},{10,1... | collective-permute-start | bytes 168488 | tf_op jit(solution)/shard_map/ppermute | solution.py:49
  255.8 13.6 %all_to_all.15 = bf16[16,64,128]{2,1,0:T(8,128)(2,1)S(1)} all-to-all(bf16[16,64,128]{2,1,0:T(8,128)(2,1)S(1)} %bitcast.207), channel_id=1, replica_groups=mesh['dp'=2,'space'=16] {'space'}, dimensions={0} | all-to-all | bytes 524288 | tf_op jit(solution)/shard_map/all_to_all | solution.py:626
  271.3 5.1 fusion.1.grad_ref
  276.4 3.2 collective-permute-start.20
  282.1 24.2 %edges_backward.3 = (bf16[2048,256]{1,0:T(8,128)(2,1)}, bf16[2048,256]{1,0:T(8,128)(2,1)}, bf16[4096,128]{1,0:T(8,128)(2,1)}, f32[4096,128]{1,0:T(8,128)}, bf16[4096,128]{1,0:T(8,128)(2,1)}) custom-call(s32[12288]{0:T(1024)} %copy-done.18, f32[2048,256]{1,0:T(8,128)} %fusion.1.grad_ref, f32[2048,256]{1,0:T(8,128)} %get-tuple-element.83.back_ref, ...), custom_call_target="tpu_custom_call" | custom-call | bytes 75000000 | tf_op jit(solution)/shard_map/edges_backward/pallas_call | solution.py:509
  307.4 2.5 fusion.116.refs_16_
  316.7 12.0 %collective-permute-done.21.first_ref = bf16[4096,128]{1,0:T(8,128)(2,1)S(1)} collective-permute-done((bf16[4096,128]{1,0:T(8,128)(2,1)}, bf16[4096,128]{1,0:T(8,128)(2,1)S(1)}, u32[]{:S(2)}, u32[]{:S(2)}) %collective-permute-start.21) | collective-permute-done | bytes 1048608 | tf_op jit(solution)/shard_map/ppermute | solution.py:77
  330.0 5.7 %round_backward.3 = (f32[2048,256]{1,0:T(8,128)}, bf16[2048,256]{1,0:T(8,128)(2,1)}) custom-call(f32[2048,256]{1,0:T(8,128)} %fusion.1.grad_ref, f32[4096,128]{1,0:T(8,128)} %get-tuple-element.86.own_ref, bf16[4096,128]{1,0:T(8,128)(2,1)} %copy-done.25, bf16[4096,128]{1,0:T(8,128)(2,1)} %copy-done.26, bf16[2048,256]{1,0:T(8,128)(2,1)} %get-tuple-element.92.guin_ref, ...), custom_call_target="tpu_custom_call" | custom-call | bytes 21000000 | tf_op jit(solution)/shard_map/round_backward/pallas_call | solution.py:567
  335.7 24.1 %edges_backward.4 = (bf16[2048,256]{1,0:T(8,128)(2,1)}, bf16[2048,256]{1,0:T(8,128)(2,1)}, bf16[4096,128]{1,0:T(8,128)(2,1)}, f32[4096,128]{1,0:T(8,128)}, bf16[4096,128]{1,0:T(8,128)(2,1)}) custom-call(s32[12288]{0:T(1024)} %copy-done.18, f32[2048,256]{1,0:T(8,128)} %get-tuple-element.94.grad_ref, f32[2048,256]{1,0:T(8,128)} %get-tuple-element.95.back_ref, ...), custom_call_target="tpu_custom_call" | custom-call | bytes 75000000 | tf_op jit(solution)/shard_map/edges_backward/pallas_call | solution.py:509
  359.9 2.6 fusion.87.refs_10_
  362.4 6.9 %collective-permute-start.23 = (bf16[4096,128]{1,0:T(8,128)(2,1)}, bf16[4096,128]{1,0:T(8,128)(2,1)S(1)}, u32[]{:S(2)}, u32[]{:S(2)}) collective-permute-start(bf16[4096,128]{1,0:T(8,128)(2,1)} %get-tuple-element.98), channel_id=1, source_target_pairs={{0,1},{1,3},{3,2},{2,6},{6,4},{4,5},{5,7},{7,11},{11,9},{9,8},{8,1... | collective-permute-start | bytes 3145736 | tf_op jit(solution)/shard_map/ppermute | solution.py:77
  375.2 9.8 %collective-permute-done.23.first_ref = bf16[4096,128]{1,0:T(8,128)(2,1)S(1)} collective-permute-done((bf16[4096,128]{1,0:T(8,128)(2,1)}, bf16[4096,128]{1,0:T(8,128)(2,1)S(1)}, u32[]{:S(2)}, u32[]{:S(2)}) %collective-permute-start.23) | collective-permute-done | bytes 1048608 | tf_op jit(solution)/shard_map/ppermute | solution.py:77
  387.9 5.7 %round_backward.4 = (f32[2048,256]{1,0:T(8,128)}, bf16[2048,256]{1,0:T(8,128)(2,1)}) custom-call(f32[2048,256]{1,0:T(8,128)} %get-tuple-element.94.grad_ref, f32[4096,128]{1,0:T(8,128)} %get-tuple-element.97.own_ref, bf16[4096,128]{1,0:T(8,128)(2,1)} %copy-done.21, bf16[4096,128]{1,0:T(8,128)(2,1)} %copy-done.23, ...), custom_call_target="tpu_custom_call" | custom-call | bytes 21000000 | tf_op jit(solution)/shard_map/round_backward/pallas_call | solution.py:567
  393.6 24.1 %edges_backward.5 = (bf16[2048,256]{1,0:T(8,128)(2,1)}, bf16[2048,256]{1,0:T(8,128)(2,1)}, bf16[4096,128]{1,0:T(8,128)(2,1)}, f32[4096,128]{1,0:T(8,128)}, bf16[4096,128]{1,0:T(8,128)(2,1)}) custom-call(s32[12288]{0:T(1024)} %copy-done.18, f32[2048,256]{1,0:T(8,128)} %get-tuple-element.102.grad_ref, f32[2048,256]{1,0:T(8,128)} %get-tuple-element.103.back_ref, ...), custom_call_target="tpu_custom_call" | custom-call | bytes 75000000 | tf_op jit(solution)/shard_map/edges_backward/pallas_call | solution.py:509
  417.7 2.6 fusion.112.refs_5_
  428.2 10.3 %collective-permute-done.25.first_ref = bf16[4096,128]{1,0:T(8,128)(2,1)S(1)} collective-permute-done((bf16[4096,128]{1,0:T(8,128)(2,1)S(1)}, bf16[4096,128]{1,0:T(8,128)(2,1)S(1)}, u32[]{:S(2)}, u32[]{:S(2)}) %collective-permute-start.25) | collective-permute-done | bytes 1048608 | tf_op jit(solution)/shard_map/ppermute | solution.py:77
  440.3 5.9 %round_backward.5 = (f32[2048,256]{1,0:T(8,128)}, bf16[2048,256]{1,0:T(8,128)(2,1)}) custom-call(f32[2048,256]{1,0:T(8,128)} %get-tuple-element.102.grad_ref, f32[4096,128]{1,0:T(8,128)} %get-tuple-element.105.own_ref, bf16[4096,128]{1,0:T(8,128)(2,1)} %copy-done.22, bf16[4096,128]{1,0:T(8,128)(2,1)} %copy-done.24, ...), custom_call_target="tpu_custom_call" | custom-call | bytes 21000000 | tf_op jit(solution)/shard_map/round_backward/pallas_call | solution.py:567
  446.2 3.7 convert_reduce_fusion.6
  451.0 4.8 convert_reduce_fusion.8
  456.9 3.3 collective-permute-start.27
  464.6 4.5 collective-permute-done.27
  469.0 5.2 collect_rows.1
  474.4 3.0 collective-permute-done.28
  482.6 6.1 %collective-permute-done.31 = bf16[2,2,2,72,256]{4,3,2,1,0:T(8,128)(2,1)S(1)} collective-permute-done((bf16[2,2,2,72,256]{4,3,2,1,0:T(8,128)(2,1)S(1)}, bf16[2,2,2,72,256]{4,3,2,1,0:T(8,128)(2,1)S(1)}, u32[]{:S(2)}, u32[]{:S(2)}) %collective-permute-start.31) | collective-permute-done | bytes 294944 | tf_op jit(solution)/shard_map/ppermute | solution.py:94
  500.0 8.9 %collective-permute-start.36 = (bf16[72,256]{1,0:T(8,128)(2,1)S(1)}, bf16[72,256]{1,0:T(8,128)(2,1)S(1)}, u32[]{:S(2)}, u32[]{:S(2)}) collective-permute-start(bf16[72,256]{1,0:T(8,128)(2,1)S(1)} %fusion.73), channel_id=1, source_target_pairs={{0,8},{1,9},{2,10},{3,11},{4,12},{5,13},{6,14},{7,15},{8,0},{9,1},... | collective-permute-start | bytes 110600 | tf_op jit(solution)/shard_map/ppermute | solution.py:94
  510.9 3.0 collective-permute-done.34
  516.7 3.6 collective-permute-done.38
  520.3 3.6 collective-permute-done.39
  529.4 2.7 bitcast_convert_fusion
  536.4 8.8 %collective-permute-done.42 = bf16[1024,256]{1,0:T(8,128)(2,1)S(1)} collective-permute-done((bf16[1024,256]{1,0:T(8,128)(2,1)S(1)}, bf16[1024,256]{1,0:T(8,128)(2,1)S(1)}, u32[]{:S(2)}, u32[]{:S(2)}) %collective-permute-start.42) | collective-permute-done | bytes 524320 | tf_op jit(solution)/shard_map/ppermute | solution.py:752
  (338 shorter events, 128.4 us)
Async XLA Ops:
  5.8 16.8 %collective-permute-start.5 = (bf16[1,72,256]{2,1,0:T(8,128)(2,1)S(1)}, bf16[1,72,256]{2,1,0:T(8,128)(2,1)S(1)}, u32[]{:S(2)}, u32[]{:S(2)}) collective-permute-start(bf16[1,72,256]{2,1,0:T(8,128)(2,1)S(1)} %get-tuple-element.191), channel_id=1, source_target_pairs={{0,8},{1,9},{2,10},{3,11},{4,12},{5,13},{6,14},{7,15},{8,0},{9,1},... | collective-permute-start | bytes 110600 | tf_op jit(solution)/shard_map/ppermute | solution.py:94
  8.4 14.8 %collective-permute-start.1 = (bf16[1,72,256]{2,1,0:T(8,128)(2,1)S(1)}, bf16[1,72,256]{2,1,0:T(8,128)(2,1)S(1)}, u32[]{:S(2)}, u32[]{:S(2)}) collective-permute-start(bf16[1,72,256]{2,1,0:T(8,128)(2,1)S(1)} %get-tuple-element.192), channel_id=1, source_target_pairs={{0,8},{1,9},{2,10},{3,11},{4,12},{5,13},{6,14},{7,15},{8,0},{9,1},... | collective-permute-start | bytes 110600 | tf_op jit(solution)/shard_map/ppermute | solution.py:94
  15.4 28.6 %all-to-all-start = ((bf16[16,64,128]{2,1,0:T(8,128)(2,1)}), bf16[16,64,128]{2,1,0:T(8,128)(2,1)S(1)}, u32[]{:S(2)}, u32[]{:S(2)}) async-start(bf16[16,64,128]{2,1,0:T(8,128)(2,1)} %bitcast.5), calls=%async_computation | async-start | bytes 524288 | tf_op jit(solution)/shard_map/all_to_all | solution.py:626
  22.6 6.9 %collective-permute-start.6 = (bf16[2,72,256]{2,1,0:T(8,128)(2,1)S(1)}, bf16[2,72,256]{2,1,0:T(8,128)(2,1)S(1)}, u32[]{:S(2)}, u32[]{:S(2)}) collective-permute-start(bf16[2,72,256]{2,1,0:T(8,128)(2,1)S(1)} %pad_maximum_fusion.7), channel_id=1, source_target_pairs={{0,4},{1,5},{2,6},{3,7},{4,0},{5,1},{6,2},{7,3},{8,12},{9,13},{10,... | collective-permute-start | bytes 221192 | tf_op jit(solution)/shard_map/ppermute | solution.py:94
  23.2 7.8 %collective-permute-start.2 = (bf16[2,72,256]{2,1,0:T(8,128)(2,1)S(1)}, bf16[2,72,256]{2,1,0:T(8,128)(2,1)S(1)}, u32[]{:S(2)}, u32[]{:S(2)}) collective-permute-start(bf16[2,72,256]{2,1,0:T(8,128)(2,1)S(1)} %pad_maximum_fusion.6), channel_id=1, source_target_pairs={{0,4},{1,5},{2,6},{3,7},{4,0},{5,1},{6,2},{7,3},{8,12},{9,13},{10,... | collective-permute-start | bytes 221192 | tf_op jit(solution)/shard_map/ppermute | solution.py:94
  29.5 7.6 %collective-permute-start.7 = (bf16[4,72,256]{2,1,0:T(8,128)(2,1)S(1)}, bf16[4,72,256]{2,1,0:T(8,128)(2,1)S(1)}, u32[]{:S(2)}, u32[]{:S(2)}) collective-permute-start(bf16[4,72,256]{2,1,0:T(8,128)(2,1)S(1)} %pad_maximum_fusion.5), channel_id=1, source_target_pairs={{0,1},{1,0},{2,3},{3,2},{4,5},{5,4},{6,7},{7,6},{8,9},{9,8},{10,11... | collective-permute-start | bytes 442376 | tf_op jit(solution)/shard_map/ppermute | solution.py:94
  31.0 5.2 collective-permute-start.3
  36.3 6.8 %collective-permute-start.4 = (bf16[8,72,256]{2,1,0:T(8,128)(2,1)S(1)}, bf16[8,72,256]{2,1,0:T(8,128)(2,1)S(1)}, u32[]{:S(2)}, u32[]{:S(2)}) collective-permute-start(bf16[8,72,256]{2,1,0:T(8,128)(2,1)S(1)} %pad_maximum_fusion), channel_id=1, source_target_pairs={{0,1},{1,0},{2,3},{3,2},{4,5},{5,4},{6,7},{7,6},{8,9},{9,8},{10,11... | collective-permute-start | bytes 884744 | tf_op jit(solution)/shard_map/ppermute | solution.py:94
  37.1 6.8 %collective-permute-start.8 = (bf16[8,72,256]{2,1,0:T(8,128)(2,1)S(1)}, bf16[8,72,256]{2,1,0:T(8,128)(2,1)S(1)}, u32[]{:S(2)}, u32[]{:S(2)}) collective-permute-start(bf16[8,72,256]{2,1,0:T(8,128)(2,1)S(1)} %pad_maximum_fusion.1), channel_id=1, source_target_pairs={{0,2},{1,3},{2,0},{3,1},{4,6},{5,7},{6,4},{7,5},{8,10},{9,11},{10,... | collective-permute-start | bytes 884744 | tf_op jit(solution)/shard_map/ppermute | solution.py:94
  43.1 2.1 collective-permute-start.9
  43.9 2.1 collective-permute-start.10
  44.6 226.6 %copy-start.65 = (s32[1024]{0:T(1024)}, s32[1024]{0:T(1024)S(1)}, u32[]{:S(2)}) copy-start(s32[1024]{0:T(1024)S(1)} %fusion.33) | copy-start | bytes 12292
  62.0 26.5 %collective-permute-start.12 = (bf16[4096,128]{1,0:T(8,128)(2,1)}, bf16[4096,128]{1,0:T(8,128)(2,1)}, u32[]{:S(2)}, u32[]{:S(2)}) collective-permute-start(bf16[4096,128]{1,0:T(8,128)(2,1)} %reshape.186.refs_3_), channel_id=1, source_target_pairs={{1,0},{3,1},{2,3},{6,2},{4,6},{5,4},{7,5},{11,7},{9,11},{8,9},{10,... | collective-permute-start | bytes 3145736 | tf_op jit(solution)/shard_map/ppermute | solution.py:77
  63.3 25.2 %collective-permute-start.11 = (bf16[4096,128]{1,0:T(8,128)(2,1)}, bf16[4096,128]{1,0:T(8,128)(2,1)}, u32[]{:S(2)}, u32[]{:S(2)}) collective-permute-start(bf16[4096,128]{1,0:T(8,128)(2,1)} %reshape.186.refs_3_), channel_id=1, source_target_pairs={{0,1},{1,3},{3,2},{2,6},{6,4},{4,5},{5,7},{7,11},{11,9},{9,8},{8,1... | collective-permute-start | bytes 3145736 | tf_op jit(solution)/shard_map/ppermute | solution.py:77
  64.1 24.4 %collective-permute-start = (s32[12288]{0:T(1024)S(1)}, s32[12288]{0:T(1024)S(1)}, u32[]{:S(2)}, u32[]{:S(2)}) collective-permute-start(s32[12288]{0:T(1024)S(1)} %mul.198), channel_id=1, source_target_pairs={{0,0},{1,1},{2,3},{3,2},{4,6},{5,4},{6,5},{7,7},{8,11},{9,9},{10,8... | collective-permute-start | bytes 147464 | tf_op jit(solution)/shard_map/ppermute | solution.py:648
  114.1 24.7 %collective-permute-start.14 = (bf16[4096,128]{1,0:T(8,128)(2,1)}, bf16[4096,128]{1,0:T(8,128)(2,1)S(1)}, u32[]{:S(2)}, u32[]{:S(2)}) collective-permute-start(bf16[4096,128]{1,0:T(8,128)(2,1)} %get-tuple-element.75.refs_3_), channel_id=1, source_target_pairs={{1,0},{3,1},{2,3},{6,2},{4,6},{5,4},{7,5},{11,7},{9,11},{8,9},{10,... | collective-permute-start | bytes 3145736 | tf_op jit(solution)/shard_map/ppermute | solution.py:77
  116.4 24.2 %collective-permute-start.13 = (bf16[4096,128]{1,0:T(8,128)(2,1)}, bf16[4096,128]{1,0:T(8,128)(2,1)S(1)}, u32[]{:S(2)}, u32[]{:S(2)}) collective-permute-start(bf16[4096,128]{1,0:T(8,128)(2,1)} %get-tuple-element.75.refs_3_), channel_id=1, source_target_pairs={{0,1},{1,3},{3,2},{2,6},{6,4},{4,5},{5,7},{7,11},{11,9},{9,8},{8,1... | collective-permute-start | bytes 3145736 | tf_op jit(solution)/shard_map/ppermute | solution.py:77
  166.6 23.2 %collective-permute-start.16 = (bf16[4096,128]{1,0:T(8,128)(2,1)}, bf16[4096,128]{1,0:T(8,128)(2,1)S(1)}, u32[]{:S(2)}, u32[]{:S(2)}) collective-permute-start(bf16[4096,128]{1,0:T(8,128)(2,1)} %get-tuple-element.77.refs_3_), channel_id=1, source_target_pairs={{1,0},{3,1},{2,3},{6,2},{4,6},{5,4},{7,5},{11,7},{9,11},{8,9},{10,... | collective-permute-start | bytes 3145736 | tf_op jit(solution)/shard_map/ppermute | solution.py:77
  167.3 23.6 %collective-permute-start.15 = (bf16[4096,128]{1,0:T(8,128)(2,1)}, bf16[4096,128]{1,0:T(8,128)(2,1)S(1)}, u32[]{:S(2)}, u32[]{:S(2)}) collective-permute-start(bf16[4096,128]{1,0:T(8,128)(2,1)} %get-tuple-element.77.refs_3_), channel_id=1, source_target_pairs={{0,1},{1,3},{3,2},{2,6},{6,4},{4,5},{5,7},{7,11},{11,9},{9,8},{8,1... | collective-permute-start | bytes 3145736 | tf_op jit(solution)/shard_map/ppermute | solution.py:77
  168.9 51.4 %copy-start.60 = (bf16[256,78]{1,0:T(8,128)(2,1)}, bf16[256,78]{1,0:T(8,128)(2,1)S(1)}, u32[]{:S(2)}) copy-start(bf16[256,78]{1,0:T(8,128)(2,1)S(1)} %reshape.187) | copy-start | bytes 119812
  220.4 49.1 %copy-start.34 = (f32[1024,256]{1,0:T(8,128)}, f32[1024,256]{1,0:T(8,128)S(1)}, u32[]{:S(2)}) copy-start(f32[1024,256]{1,0:T(8,128)S(1)} %convolution_add_fusion.1) | copy-start | bytes 3145732
  221.4 16.5 %all-to-all-start.1 = ((bf16[16,64,128]{2,1,0:T(8,128)(2,1)}), bf16[16,64,128]{2,1,0:T(8,128)(2,1)S(1)}, u32[]{:S(2)}, u32[]{:S(2)}) async-start(bf16[16,64,128]{2,1,0:T(8,128)(2,1)} %bitcast.23), calls=%async_computation.1 | async-start | bytes 524288 | tf_op jit(solution)/shard_map/all_to_all | solution.py:626
  231.0 6.8 %collective-permute-start.17 = (bf16[78,360]{1,0:T(8,128)(2,1)S(1)}, bf16[78,360]{1,0:T(8,128)(2,1)S(1)}, u32[]{:S(2)}, u32[]{:S(2)}) collective-permute-start(bf16[78,360]{1,0:T(8,128)(2,1)S(1)} %slice.433), channel_id=1, source_target_pairs={{1,0},{2,1},{3,2},{4,3},{5,4},{6,5},{7,6},{8,7},{9,8},{10,9},{11,1... | collective-permute-start | bytes 168488 | tf_op jit(solution)/shard_map/ppermute | solution.py:49
  238.4 6.6 %collective-permute-start.18 = (bf16[78,360]{1,0:T(8,128)(2,1)S(1)}, bf16[78,360]{1,0:T(8,128)(2,1)S(1)}, u32[]{:S(2)}, u32[]{:S(2)}) collective-permute-start(bf16[78,360]{1,0:T(8,128)(2,1)S(1)} %slice.432), channel_id=1, source_target_pairs={{1,0},{2,1},{3,2},{4,3},{5,4},{6,5},{7,6},{8,7},{9,8},{10,9},{11,1... | collective-permute-start | bytes 168488 | tf_op jit(solution)/shard_map/ppermute | solution.py:49
  246.4 7.6 %collective-permute-start.19 = (bf16[78,360]{1,0:T(8,128)(2,1)S(1)}, bf16[78,360]{1,0:T(8,128)(2,1)S(1)}, u32[]{:S(2)}, u32[]{:S(2)}) collective-permute-start(bf16[78,360]{1,0:T(8,128)(2,1)S(1)} %slice.431), channel_id=1, source_target_pairs={{0,1},{1,2},{2,3},{3,4},{4,5},{5,6},{6,7},{7,8},{8,9},{9,10},{10,1... | collective-permute-start | bytes 168488 | tf_op jit(solution)/shard_map/ppermute | solution.py:49
  276.4 33.6 %collective-permute-start.20 = (bf16[2048,256]{1,0:T(8,128)(2,1)}, bf16[2048,256]{1,0:T(8,128)(2,1)}, u32[]{:S(2)}, u32[]{:S(2)}) collective-permute-start(bf16[2048,256]{1,0:T(8,128)(2,1)} %copy-done.20), channel_id=1, source_target_pairs={{0,0},{1,1},{3,2},{2,3},{6,4},{4,5},{5,6},{7,7},{11,8},{9,9},{8,10... | collective-permute-start | bytes 3145736 | tf_op jit(solution)/shard_map/ppermute | solution.py:706
  310.0 18.7 %collective-permute-start.21 = (bf16[4096,128]{1,0:T(8,128)(2,1)}, bf16[4096,128]{1,0:T(8,128)(2,1)S(1)}, u32[]{:S(2)}, u32[]{:S(2)}) collective-permute-start(bf16[4096,128]{1,0:T(8,128)(2,1)} %get-tuple-element.90), channel_id=1, source_target_pairs={{0,1},{1,3},{3,2},{2,6},{6,4},{4,5},{5,7},{7,11},{11,9},{9,8},{8,1... | collective-permute-start | bytes 3145736 | tf_op jit(solution)/shard_map/ppermute | solution.py:77
  310.6 18.4 %collective-permute-start.22 = (bf16[4096,128]{1,0:T(8,128)(2,1)S(1)}, bf16[4096,128]{1,0:T(8,128)(2,1)S(1)}, u32[]{:S(2)}, u32[]{:S(2)}) collective-permute-start(bf16[4096,128]{1,0:T(8,128)(2,1)S(1)} %copy-done.71), channel_id=1, source_target_pairs={{1,0},{3,1},{2,3},{6,2},{4,6},{5,4},{7,5},{11,7},{9,11},{8,9},{10,... | collective-permute-start | bytes 3145736 | tf_op jit(solution)/shard_map/ppermute | solution.py:77
  362.4 22.6 %collective-permute-start.23 = (bf16[4096,128]{1,0:T(8,128)(2,1)}, bf16[4096,128]{1,0:T(8,128)(2,1)S(1)}, u32[]{:S(2)}, u32[]{:S(2)}) collective-permute-start(bf16[4096,128]{1,0:T(8,128)(2,1)} %get-tuple-element.98), channel_id=1, source_target_pairs={{0,1},{1,3},{3,2},{2,6},{6,4},{4,5},{5,7},{7,11},{11,9},{9,8},{8,1... | collective-permute-start | bytes 3145736 | tf_op jit(solution)/shard_map/ppermute | solution.py:77
  369.3 17.6 %collective-permute-start.24 = (bf16[4096,128]{1,0:T(8,128)(2,1)S(1)}, bf16[4096,128]{1,0:T(8,128)(2,1)S(1)}, u32[]{:S(2)}, u32[]{:S(2)}) collective-permute-start(bf16[4096,128]{1,0:T(8,128)(2,1)S(1)} %copy-done.73), channel_id=1, source_target_pairs={{1,0},{3,1},{2,3},{6,2},{4,6},{5,4},{7,5},{11,7},{9,11},{8,9},{10,... | collective-permute-start | bytes 3145736 | tf_op jit(solution)/shard_map/ppermute | solution.py:77
  421.5 17.0 %collective-permute-start.25 = (bf16[4096,128]{1,0:T(8,128)(2,1)S(1)}, bf16[4096,128]{1,0:T(8,128)(2,1)S(1)}, u32[]{:S(2)}, u32[]{:S(2)}) collective-permute-start(bf16[4096,128]{1,0:T(8,128)(2,1)S(1)} %copy-done.74), channel_id=1, source_target_pairs={{0,1},{1,3},{3,2},{2,6},{6,4},{4,5},{5,7},{7,11},{11,9},{9,8},{8,1... | collective-permute-start | bytes 3145736 | tf_op jit(solution)/shard_map/ppermute | solution.py:77
  422.9 16.3 %collective-permute-start.26 = (bf16[4096,128]{1,0:T(8,128)(2,1)S(1)}, bf16[4096,128]{1,0:T(8,128)(2,1)S(1)}, u32[]{:S(2)}, u32[]{:S(2)}) collective-permute-start(bf16[4096,128]{1,0:T(8,128)(2,1)S(1)} %copy-done.72), channel_id=1, source_target_pairs={{1,0},{3,1},{2,3},{6,2},{4,6},{5,4},{7,5},{11,7},{9,11},{8,9},{10,... | collective-permute-start | bytes 3145736 | tf_op jit(solution)/shard_map/ppermute | solution.py:77
  456.9 12.2 %collective-permute-start.27 = (bf16[1024,256]{1,0:T(8,128)(2,1)}, bf16[1024,256]{1,0:T(8,128)(2,1)S(1)}, u32[]{:S(2)}, u32[]{:S(2)}) collective-permute-start(bf16[1024,256]{1,0:T(8,128)(2,1)} %get-tuple-element.186), channel_id=1, source_target_pairs={{0,0},{1,1},{3,2},{2,3},{6,4},{4,5},{5,6},{7,7},{11,8},{9,9},{8,10... | collective-permute-start | bytes 1572872 | tf_op jit(solution)/shard_map/ppermute | solution.py:736
  474.3 3.1 collective-permute-start.28
  479.6 9.1 %collective-permute-start.31 = (bf16[2,2,2,72,256]{4,3,2,1,0:T(8,128)(2,1)S(1)}, bf16[2,2,2,72,256]{4,3,2,1,0:T(8,128)(2,1)S(1)}, u32[]{:S(2)}, u32[]{:S(2)}) collective-permute-start(bf16[2,2,2,72,256]{4,3,2,1,0:T(8,128)(2,1)S(1)} %fusion.35), channel_id=1, source_target_pairs={{0,2},{1,3},{2,0},{3,1},{4,6},{5,7},{6,4},{7,5},{8,10},{9,11},{10,... | collective-permute-start | bytes 884744 | tf_op jit(solution)/shard_map/ppermute | solution.py:94
  481.4 8.8 %collective-permute-start.29 = (bf16[2,2,2,72,256]{4,3,0,1,2:T(8,128)(2,1)S(1)}, bf16[2,2,2,72,256]{4,3,0,1,2:T(8,128)(2,1)S(1)}, u32[]{:S(2)}, u32[]{:S(2)}) collective-permute-start(bf16[2,2,2,72,256]{4,3,0,1,2:T(8,128)(2,1)S(1)} %fusion.36), channel_id=1, source_target_pairs={{0,1},{1,0},{2,3},{3,2},{4,5},{5,4},{6,7},{7,6},{8,9},{9,8},{10,11... | collective-permute-start | bytes 884744 | tf_op jit(solution)/shard_map/ppermute | solution.py:94
  488.8 5.2 collective-permute-start.32
  490.3 5.2 collective-permute-start.30
  495.6 4.4 collective-permute-start.35
  497.2 11.7 %collective-permute-start.33 = (bf16[2,72,256]{2,1,0:T(8,128)(2,1)S(1)}, bf16[2,72,256]{2,1,0:T(8,128)(2,1)S(1)}, u32[]{:S(2)}, u32[]{:S(2)}) collective-permute-start(bf16[2,72,256]{2,1,0:T(8,128)(2,1)S(1)} %fusion.63), channel_id=1, source_target_pairs={{0,4},{1,5},{2,6},{3,7},{4,0},{5,1},{6,2},{7,3},{8,12},{9,13},{10,... | collective-permute-start | bytes 221192 | tf_op jit(solution)/shard_map/ppermute | solution.py:94
  500.0 10.9 %collective-permute-start.36 = (bf16[72,256]{1,0:T(8,128)(2,1)S(1)}, bf16[72,256]{1,0:T(8,128)(2,1)S(1)}, u32[]{:S(2)}, u32[]{:S(2)}) collective-permute-start(bf16[72,256]{1,0:T(8,128)(2,1)S(1)} %fusion.73), channel_id=1, source_target_pairs={{0,8},{1,9},{2,10},{3,11},{4,12},{5,13},{6,14},{7,15},{8,0},{9,1},... | collective-permute-start | bytes 110600 | tf_op jit(solution)/shard_map/ppermute | solution.py:94
  509.0 4.9 collective-permute-start.34
  515.5 1.2 collective-permute-start.37
  516.7 3.6 collective-permute-start.38
  520.3 3.6 collective-permute-start.39
  523.9 3.6 collective-permute-start.40
  527.5 6.5 %collective-permute-start.41 = (f32[8,128]{1,0:T(8,128)S(1)}, f32[8,128]{1,0:T(8,128)S(1)}, u32[]{:S(2)}, u32[]{:S(2)}) collective-permute-start(f32[8,128]{1,0:T(8,128)S(1)} %add.229), channel_id=1, source_target_pairs={{0,8},{1,9},{2,10},{3,11},{4,12},{5,13},{6,14},{7,15},{8,0},{9,1},... | collective-permute-start | bytes 12296 | tf_op jit(solution)/shard_map/ppermute | solution.py:94
  532.1 13.0 %collective-permute-start.42 = (bf16[1024,256]{1,0:T(8,128)(2,1)S(1)}, bf16[1024,256]{1,0:T(8,128)(2,1)S(1)}, u32[]{:S(2)}, u32[]{:S(2)}) collective-permute-start(bf16[1024,256]{1,0:T(8,128)(2,1)S(1)} %copy-done.50), channel_id=1, source_target_pairs={{0,0},{1,1},{3,2},{2,3},{6,4},{4,5},{5,6},{7,7},{11,8},{9,9},{8,10... | collective-permute-start | bytes 1572872 | tf_op jit(solution)/shard_map/ppermute | solution.py:752
  (73 other events, 562.4 us)

commit v6 on v5

--- a/solution.py
+++ b/solution.py
@@ -262,7 +262,7 @@
 
 
 def tall_parts():
-    return [CH, D, D, CH] + [D] * (5 * ROUNDS) + [3 + 2 * ROUNDS]
+    return [CH, D, D, CH] + [D] * (5 * ROUNDS) + [2] + [1] * (1 + 2 * ROUNDS)
 
 
 def weave(ref, value):
@@ -578,6 +578,92 @@
         cost_estimate=cost(7),
         name="round_backward",
     )(grad_mesh, own, first, last, grad_uin, dest_low, turned)
+
+
+def encode_rows(arrived, ids, w_in, w_node, biases, source):
+    posts = arrived.shape[0]
+    tile = 512
+
+    def body(arrived_ref, ids_ref, in_ref, node_ref, bias_ref, source_ref, mesh_ref, gathered_ref, sent_ref, encoded, wide):
+        step = pl.program_id(0)
+
+        @pl.when(step == 0)
+        def _():
+            entering = inner(arrived_ref[...], in_ref[...], 1, 0) + bias_ref[0:1, :]
+            encoded[...] = silu(entering).astype(jnp.bfloat16)
+
+        nodes = lax.broadcasted_iota(jnp.int32, (tile, posts), 0) + step * tile
+        chooser = jnp.where(nodes == ids_ref[...], 1.0, 0.0).astype(jnp.bfloat16)
+        gathered = inner(chooser, encoded[...], 1, 0).astype(jnp.bfloat16)
+        gathered_ref[...] = gathered
+        mesh = silu(inner(gathered, node_ref[...], 1, 0) + bias_ref[1:2, :])
+        mesh_ref[...] = mesh
+        weave(wide, inner(mesh.astype(jnp.bfloat16), source_ref[...], 1, 0))
+        sent_ref[...] = wide[...].astype(jnp.bfloat16)
+
+    rows = pl.BlockSpec((tile, D), lambda i: (i, 0))
+    args = (arrived, ids, w_in, w_node, biases, source)
+    return pl.pallas_call(
+        body,
+        grid=(H // tile,),
+        in_specs=[whole(arg.shape) for arg in args],
+        out_specs=[rows, rows, pl.BlockSpec((2 * tile, HALF), lambda i: (i, 0))],
+        out_shape=[
+            jax.ShapeDtypeStruct((H, D), jnp.float32),
+            jax.ShapeDtypeStruct((H, D), jnp.bfloat16),
+            jax.ShapeDtypeStruct((2 * H, HALF), jnp.bfloat16),
+        ],
+        scratch_shapes=[pltpu.VMEM((posts, D), jnp.bfloat16), pltpu.VMEM((2 * tile, HALF), jnp.float32)],
+        compiler_params=LIMIT,
+        cost_estimate=cost(5),
+        name="encode_rows",
+    )(*args)
+
+
+def encode_backward(grad_mesh, gathered, arrived, ids, w_in, w_node, biases):
+    posts = arrived.shape[0]
+    tile = 512
+    steps = H // tile
+
+    def body(grad_ref, gathered_ref, arrived_ref, ids_ref, in_ref, node_ref, bias_ref, gin_ref, gnode_ref, gbias_ref, total):
+        step = pl.program_id(0)
+
+        @pl.when(step == 0)
+        def _():
+            total[...] = jnp.zeros(total.shape, jnp.float32)
+            gnode_ref[...] = jnp.zeros(gnode_ref.shape, jnp.float32)
+            gbias_ref[...] = jnp.zeros(gbias_ref.shape, jnp.float32)
+
+        node_in = inner(gathered_ref[...], node_ref[...], 1, 0) + bias_ref[1:2, :]
+        grad_node = (grad_ref[...] * slope(node_in)).astype(jnp.bfloat16)
+        gbias_ref[1:2, :] += jnp.sum(grad_node.astype(jnp.float32), 0, keepdims=True)
+        gnode_ref[...] += inner(gathered_ref[...], grad_node, 0, 0)
+        back = inner(grad_node, node_ref[...], 1, 1).astype(jnp.bfloat16)
+        nodes = lax.broadcasted_iota(jnp.int32, (posts, tile), 1) + step * tile
+        chooser = jnp.where(nodes == ids_ref[...], 1.0, 0.0).astype(jnp.bfloat16)
+        total[...] += inner(chooser, back, 1, 0)
+
+        @pl.when(step == steps - 1)
+        def _():
+            entering = inner(arrived_ref[...], in_ref[...], 1, 0) + bias_ref[0:1, :]
+            grad_enc = (total[...] * slope(entering)).astype(jnp.bfloat16)
+            gbias_ref[0:1, :] = jnp.sum(grad_enc.astype(jnp.float32), 0, keepdims=True)
+            gin_ref[...] = inner(arrived_ref[...], grad_enc, 0, 0)
+
+    rows = pl.BlockSpec((tile, D), lambda i: (i, 0))
+    args = (grad_mesh, gathered, arrived, ids, w_in, w_node, biases)
+    shapes = [(HALF, D), (D, D), (2, D)]
+    return pl.pallas_call(
+        body,
+        grid=(steps,),
+        in_specs=[rows, rows] + [whole(arg.shape) for arg in args[2:]],
+        out_specs=[whole(shape) for shape in shapes],
+        out_shape=[jax.ShapeDtypeStruct(shape, jnp.float32) for shape in shapes],
+        scratch_shapes=[pltpu.VMEM((posts, D), jnp.float32)],
+        compiler_params=LIMIT,
+        cost_estimate=cost(7),
+        name="encode_backward",
+    )(*args)
 
 
 def shards(walk, master, moment1, moment2, inputs, targets, valid, owner, slot, neighbours, partner):
@@ -639,17 +725,30 @@
     ids = arrived[:, CH : CH + 3].astype(jnp.int32)
     ids = jnp.where(ids[:, 2:3] > 0, ids[:, 0:1] * 64 + ids[:, 1:2], -1)
     chooser = (ids == jnp.arange(blocks, dtype=jnp.int32)[None, :]).astype(jnp.bfloat16)
-    enc_in = inner(arrived, w_in, 1, 0) + b_head[0]
-    encoded = silu(enc_in).astype(jnp.bfloat16)
-    gathered = inner(chooser, encoded, 0, 0).astype(jnp.bfloat16)
-    node_in = inner(gathered, w_node, 1, 0) + b_head[1]
-    mesh = silu(node_in)
+    mesh, gathered, sent = encode_rows(
+        arrived, ids.reshape(1, -1), w_in, w_node, biases, w_round[0, 0]
+    )
     index = 2 * ((neighbours - band * blocks + H) % (blocks * bands)).T.reshape(-1)
-    index = lax.ppermute(index, "space", list(enumerate(walk)))
-    home = [(place, n) for n, place in enumerate(walk)]
+    moved = [(n, place) for n, place in enumerate(walk) if n != place]
+    stays = jnp.asarray([n == place for n, place in enumerate(walk)])[band]
+    index = jnp.where(stays, index, lax.ppermute(index, "space", moved))
+
+    def at_home(rows):
+        return lax.ppermute(rows, "space", [(j, i) for i, j in moved])
+
+    def settled(own, came):
+        return jnp.where(stays, own, came.astype(jnp.float32))
+
+    low_valid = counted.astype(jnp.bfloat16)
+    valid_around = jnp.concatenate(
+        [
+            shifted(low_valid[:, points - ROWW :], "space", 1),
+            low_valid,
+            shifted(low_valid[:, :ROWW], "space", -1),
+        ],
+        1,
+    ).astype(jnp.float32)
     kept = []
-    sent = inner(mesh.astype(jnp.bfloat16), w_round[0, 0], 1, 0).astype(jnp.bfloat16)
-    sent = sent.reshape(2 * blocks, HALF)
     for layer in range(ROUNDS):
         before, after = halo(walk, sent[2 * (blocks - H) :], sent[: 2 * H])
         if layer == 0:
@@ -661,49 +760,57 @@
         kept.append((mesh, back, update, agg, slopes))
         mesh = new
         sent = rest[0] if rest else None
+    partner_by = partner - band * points - jnp.arange(points, dtype=jnp.int32)
+    partner_by = jnp.concatenate(
+        [shifted(partner_by[points - ROWW :], "space", 1), partner_by], 0
+    )[None, :]
+    wide_valid = valid_around
+    weights = [
+        (
+            by,
+            jnp.where(partner_by == by, 1.0, 0.0)
+            * wide_valid[:, : points + ROWW]
+            * wide_valid[:, by : by + points + ROWW],
+        )
+        for by in range(NEAR, ROWW + 1)
+    ]
     fetched = inner(chooser, mesh.astype(jnp.bfloat16), 1, 0).astype(jnp.bfloat16)
     dec_in = inner(fetched, w_dec, 1, 0) + b_head[2]
     decoded = silu(dec_in).astype(jnp.bfloat16)
     returned = exchanged(inner(decoded, w_out, 1, 0).astype(jnp.bfloat16))
     branch = inner(returned, poster, 0, 0)[:CH]
     err = state_in.astype(jnp.float32) + branch - targets[0].astype(jnp.float32)
-    head_err, head_valid = (
-        shifted(err[:, :ROWW].astype(jnp.bfloat16), "space", -1).astype(jnp.float32),
-        shifted(counted[:, :ROWW].astype(jnp.bfloat16), "space", -1).astype(jnp.float32),
-    )
-    wide_err = jnp.concatenate([err, head_err], 1)
-    wide_valid = jnp.concatenate([counted, head_valid], 1)
-    ahead = partner - band * points - jnp.arange(points, dtype=jnp.int32)
-    picks = [(ahead == by)[None, :] for by in range(NEAR, ROWW + 1)]
-    err_far = err
-    valid_far = counted
-    for by, pick in zip(range(NEAR, ROWW + 1), picks):
-        err_far = jnp.where(pick, wide_err[:, by : by + points], err_far)
-        valid_far = jnp.where(pick, wide_valid[:, by : by + points], valid_far)
-    gap = err - err_far
-    local_total = jnp.sum(counted * err * err) + 0.5 * jnp.sum(counted * valid_far * gap * gap)
-    paired = counted * valid_far * gap / count
-    grad_err = 2.0 * counted * err / count + paired
-    grad_wide = jnp.zeros(wide_err.shape, jnp.float32)
-    for by, pick in zip(range(NEAR, ROWW + 1), picks):
-        grad_wide = grad_wide - jnp.pad(
-            jnp.where(pick, paired, 0.0), ((0, 0), (by, ROWW - by))
+    def widened(values):
+        low = values.astype(jnp.bfloat16)
+        before = shifted(low[:, points - ROWW :], "space", 1).astype(jnp.float32)
+        after = shifted(low[:, :ROWW], "space", -1).astype(jnp.float32)
+        return jnp.concatenate([before, values, after], 1)
+
+    wide_err = widened(err)
+    paired = jnp.zeros((CH, points + ROWW), jnp.float32)
+    pair_total = jnp.zeros((CH, points), jnp.float32)
+    for by, both in weights:
+        gap = both * (wide_err[:, : points + ROWW] - wide_err[:, by : by + points + ROWW])
+        paired = paired + gap
+        pair_total = pair_total + gap[:, ROWW:] * (
+            wide_err[:, ROWW : ROWW + points] - wide_err[:, ROWW + by : ROWW + by + points]
         )
-    carried = shifted(grad_wide[:, points:].astype(jnp.bfloat16), "space", 1).astype(jnp.float32)
-    stays = jnp.where((ahead == 0)[None, :], paired, 0.0)
-    grad_pred = (
-        grad_err - stays + grad_wide[:, :points] + jnp.pad(carried, ((0, 0), (0, points - ROWW)))
-    )
+    local_total = jnp.sum(counted * err * err) + 0.5 * jnp.sum(pair_total)
+    grad_pred = 2.0 * counted * err + paired[:, ROWW:]
+    for by, both in weights:
+        gap = both * (wide_err[:, : points + ROWW] - wide_err[:, by : by + points + ROWW])
+        grad_pred = grad_pred - gap[:, ROWW - by : ROWW - by + points]
+    grad_pred = grad_pred / count
     grad_rows = jnp.pad(grad_pred.astype(jnp.bfloat16), ((0, HALF - CH), (0, 0)))
     landed = exchanged(inner(poster, grad_rows, 1, 1).astype(jnp.bfloat16))
     grad_wout = inner(decoded, landed, 0, 0)[:, :CH]
     grad_dec = (inner(landed, w_out, 1, 1) * slope(dec_in)).astype(jnp.bfloat16)
-    grad_bdec = jnp.sum(grad_dec.astype(jnp.float32), 0)
+    grad_bdec = jnp.sum(grad_dec.astype(jnp.float32), 0, keepdims=True)
     grad_wdec = inner(fetched, grad_dec, 0, 0)
     grad_fetched = inner(grad_dec, w_dec, 1, 1).astype(jnp.bfloat16)
     grad_mesh = inner(chooser, grad_fetched, 0, 0)
     grad_mesh, leaving = lax.optimization_barrier((grad_mesh, mesh.astype(jnp.bfloat16)))
-    final_mesh = lax.ppermute(leaving, "space", home)
+    final_mesh = at_home(leaving)
     mats_grads = [None] * (5 * ROUNDS)
     bias_grads = [None] * (2 * ROUNDS)
     for layer in reversed(range(ROUNDS)):
@@ -732,29 +839,28 @@
         )
         grads[0] = inner(lowered, sent_low, 0, 0)
         mats_grads[5 * layer : 5 * layer + 5] = grads
+    third = blocks // 4 // 16 * 16
     leaving = grad_mesh.astype(jnp.bfloat16)
-    early = lax.ppermute(leaving[: blocks // 2], "space", home)
-    leaving = leaving[blocks // 2 :]
-    grad_node = (grad_mesh * slope(node_in)).astype(jnp.bfloat16)
-    grad_bnode = jnp.sum(grad_node.astype(jnp.float32), 0)
-    grad_wnode = inner(gathered, grad_node, 0, 0)
-    grad_gathered = inner(grad_node, w_node, 1, 1).astype(jnp.bfloat16)
-    grad_encoded = inner(chooser, grad_gathered, 1, 0)
-    grad_enc = (grad_encoded * slope(enc_in)).astype(jnp.bfloat16)
-    grad_bin = jnp.sum(grad_enc.astype(jnp.float32), 0)
-    grad_win = inner(arrived, grad_enc, 0, 0)
-    grad_win, early = lax.optimization_barrier((grad_win, early))
+    early = at_home(leaving[:third])
+    grad_win, grad_wnode, grad_bpair = encode_backward(
+        grad_mesh, gathered, arrived, ids, w_in, w_node, biases
+    )
+    grad_win, grad_wnode, grad_bpair, early = lax.optimization_barrier(
+        (grad_win, grad_wnode, grad_bpair, early)
+    )
+    middle = at_home(leaving[third : 2 * third])
     parts = [grad_win, grad_wnode, grad_wdec, grad_wout.reshape(CH, D)]
     parts = parts + mats_grads
-    parts.append(jnp.concatenate([jnp.stack([grad_bin, grad_bnode, grad_bdec])] + bias_grads, 0))
+    parts = parts + [grad_bpair, grad_bdec] + bias_grads
     keep, send = collect_rows(parts, total_size, peers, place)
-    mine, leaving = reduced_piece(keep, send, leaving)
-    late = lax.ppermute(leaving, "space", home)
+    keep, send, middle = lax.optimization_barrier((keep, send, middle))
+    mine, leaving = reduced_piece(keep, send, leaving[2 * third :])
+    late = at_home(leaving)
     mine = lax.dynamic_slice_in_dim(mine.reshape(-1), offset, shard)
     lane = lax.broadcasted_iota(jnp.int32, (8, HALF), 1)
     sums = summed_everywhere(jnp.where(lane == 0, local_total, jnp.sum(mine * mine)))
     total, norm = sums[0, 0], jnp.sqrt(sums[0, 1])
-    node_grads = jnp.concatenate([early, late], 0)
+    node_grads = settled(grad_mesh, jnp.concatenate([early, middle, late], 0))
     clipped = mine * jnp.minimum(1.0, 0.05 / norm)
     first = 0.9 * moment1 + 0.1 * clipped
     second = 0.999 * moment2 + 0.001 * clipped * clipped
@@ -769,8 +875,8 @@
         first,
         second,
         updated.astype(jnp.bfloat16),
-        final_mesh.astype(jnp.float32).reshape(1, blocks, D),
-        node_grads.astype(jnp.float32).reshape(1, blocks, D),
+        settled(mesh, final_mesh).reshape(1, blocks, D),
+        node_grads.reshape(1, blocks, D),
         grad_pred.reshape(1, grad_pred.shape[0], points),
     )
 

time: 560 us -> 542 us (0.968)
  the two profiles are of different devices: /device:TPU:12 before, /device:TPU:8 now
where the time goes in v6:
time: 542 us; the launch traced here: 533 us
  Pallas kernels  186 us (34%)
  waiting for transfers between devices  145 us (27%)
  starting transfers between devices  87.1 us (16%)
  matrix products  35.1 us (6%)
  other arithmetic  31.1 us (6%)
  local copies, waits for them, and re-layouts  25.7 us (5%)
  blocking collectives  14.2 us (3%)
  between operations  8.37 us (2%)
    pallas_call x3, Pallas kernels, round_forward(): pl.pallas_call(body, grid_spec=pltpu.PrefetchScalarGridSpec(num_scalar_pr...  74.1 us
    pallas_call x3, Pallas kernels, edges_backward(): pl.pallas_call(body, grid_spec=pltpu.PrefetchScalarGridSpec(num_scalar_pr...  72.6 us
    ppermute x24, waiting for transfers between devices, swapped(): lax.ppermute(value, axis, [(i, i ^ bit) for i in range(lax.axis_size(axis...  44.4 us
    ppermute x6, waiting for transfers between devices, halo(): lax.ppermute(last, 'space', up)  44.3 us
    ppermute x6, waiting for transfers between devices, halo(): lax.ppermute(initial, 'space', down)  42.8 us
    dot_general x24, matrix products, inner(): lax.dot_general(left, right, (((left_dim,), (right_dim,)), ((), ())), pre...  34.7 us
    ppermute x24, starting transfers between devices, swapped(): lax.ppermute(value, axis, [(i, i ^ bit) for i in range(lax.axis_size(axis...  25.4 us
    all_to_all x2, starting transfers between devices, exchanged(): lax.all_to_all(rows.reshape(bands, capacity, HALF), 'space', split_axis=0...  17.8 us
  transfers between devices with their start and end apart: 48, of which 29 were waited for; matrix products, arithmetic and copies ran while one was open for 10% of the time, Pallas kernels for 13%

profile of v6, /device:TPU:8, one launch (start us, length us, event | category | flops | bytes accessed | tf_op | source)
XLA Modules:
  0.0 532.9 jit_solution(14669104296184874333)
XLA Ops:
  5.8 2.7 collective-permute-start.5
  15.4 7.2 %all-to-all-start = ((bf16[16,64,128]{2,1,0:T(8,128)(2,1)}), bf16[16,64,128]{2,1,0:T(8,128)(2,1)S(1)}, u32[]{:S(2)}, u32[]{:S(2)}) async-start(bf16[16,64,128]{2,1,0:T(8,128)(2,1)} %bitcast.5), calls=%async_computation | async-start | bytes 524288 | tf_op jit(solution)/shard_map/all_to_all | solution.py:712
  24.8 4.4 collective-permute-done.6
  32.6 3.7 collective-permute-done.3
  38.7 4.4 collective-permute-done.4
  44.1 3.4 collective-permute-start
  51.1 4.2 spread_rows.1
  57.1 5.8 %encode_rows.1 = (f32[2048,256]{1,0:T(8,128)}, bf16[2048,256]{1,0:T(8,128)(2,1)}, bf16[4096,128]{1,0:T(8,128)(2,1)}) custom-call(bf16[1024,128]{1,0:T(8,128)(2,1)} %bitcast.175, s32[1,1024]{1,0:T(1,128)} %bitcast.192, bf16[128,256]{1,0:T(8,128)(2,1)} %get-tuple-element.80.in_ref, bf16[256,256]{1,0:T(8,128)(2,1)} %get-tuple-element.81.node_ref, ...), custom_call_target="tpu_custom_call" | custom-call | bytes 15000000 | tf_op jit(solution)/shard_map/encode_rows/pallas_call | solution.py:606
  66.2 4.0 copy.36
  72.9 16.6 %collective-permute-done.11.refs_2_ = bf16[4096,128]{1,0:T(8,128)(2,1)} collective-permute-done((bf16[4096,128]{1,0:T(8,128)(2,1)}, bf16[4096,128]{1,0:T(8,128)(2,1)}, u32[]{:S(2)}, u32[]{:S(2)}) %collective-permute-start.11) | collective-permute-done | bytes 1048608 | tf_op jit(solution)/shard_map/ppermute | solution.py:77
  90.4 24.9 %round_forward.3 = (f32[2048,256]{1,0:T(8,128)}, f32[2048,256]{1,0:T(8,128)}, bf16[2048,256]{1,0:T(8,128)(2,1)}, bf16[2048,256]{1,0:T(8,128)(2,1)}, bf16[6,4096,...) custom-call(s32[12288]{0:T(1024)} %broadcast_select_fusion.refs_0_.index_ref, f32[2048,256]{1,0:T(8,128)} %get-tuple-element.84.refs_1_, ...), custom_call_target="tpu_custom_call" | custom-call | bytes 75000000 | tf_op jit(solution)/shard_map/round_forward/pallas_call | solution.py:398
  117.5 22.3 %collective-permute-done.14.refs_4_ = bf16[4096,128]{1,0:T(8,128)(2,1)S(1)} collective-permute-done((bf16[4096,128]{1,0:T(8,128)(2,1)}, bf16[4096,128]{1,0:T(8,128)(2,1)S(1)}, u32[]{:S(2)}, u32[]{:S(2)}) %collective-permute-start.14) | collective-permute-done | bytes 1048608 | tf_op jit(solution)/shard_map/ppermute | solution.py:77
  141.8 25.0 %round_forward.4 = (f32[2048,256]{1,0:T(8,128)}, f32[2048,256]{1,0:T(8,128)}, bf16[2048,256]{1,0:T(8,128)(2,1)}, bf16[2048,256]{1,0:T(8,128)(2,1)}, bf16[6,4096,...) custom-call(s32[12288]{0:T(1024)} %broadcast_select_fusion.refs_0_.index_ref, f32[2048,256]{1,0:T(8,128)} %get-tuple-element.87.refs_1_, ...), custom_call_target="tpu_custom_call" | custom-call | bytes 75000000 | tf_op jit(solution)/shard_map/round_forward/pallas_call | solution.py:398
  169.0 2.8 collective-permute-start.17
  172.7 17.3 %collective-permute-done.16.refs_4_ = bf16[4096,128]{1,0:T(8,128)(2,1)S(1)} collective-permute-done((bf16[4096,128]{1,0:T(8,128)(2,1)}, bf16[4096,128]{1,0:T(8,128)(2,1)S(1)}, u32[]{:S(2)}, u32[]{:S(2)}) %collective-permute-start.16) | collective-permute-done | bytes 1048608 | tf_op jit(solution)/shard_map/ppermute | solution.py:77
  191.9 24.2 %round_forward.5 = (f32[2048,256]{1,0:T(8,128)}, f32[2048,256]{1,0:T(8,128)}, bf16[2048,256]{1,0:T(8,128)(2,1)}, bf16[2048,256]{1,0:T(8,128)(2,1)}, bf16[6,4096,128]{2,1,0:T(8,128)(2,1)}) custom-call(s32[12288]{0:T(1024)} %broadcast_select_fusion.refs_0_.index_ref, f32[2048,256]{1,0:T(8,128)} %get-tuple-element.89.refs_1_, bf16[4096,128]{1,0:T(8,128)(2,1)} %copy-done.33, ...), custom_call_target="tpu_custom_call" | custom-call | bytes 75000000 | tf_op jit(solution)/shard_map/round_forward/pallas_call | solution.py:398
  221.7 10.5 %all-to-all-start.1 = ((bf16[16,64,128]{2,1,0:T(8,128)(2,1)}), bf16[16,64,128]{2,1,0:T(8,128)(2,1)S(1)}, u32[]{:S(2)}, u32[]{:S(2)}) async-start(bf16[16,64,128]{2,1,0:T(8,128)(2,1)} %bitcast.22), calls=%async_computation.1 | async-start | bytes 524288 | tf_op jit(solution)/shard_map/all_to_all | solution.py:712
  232.4 4.3 collective-permute-start.19
  239.8 4.7 collective-permute-done.18
  247.3 5.7 %collective-permute-start.21 = (bf16[78,360]{1,0:T(8,128)(2,1)S(1)}, bf16[78,360]{1,0:T(8,128)(2,1)S(1)}, u32[]{:S(2)}, u32[]{:S(2)}) collective-permute-start(bf16[78,360]{1,0:T(8,128)(2,1)S(1)} %get-tuple-element.203), channel_id=1, source_target_pairs={{1,0},{2,1},{3,2},{4,3},{5,4},{6,5},{7,6},{8,7},{9,8},{10,9},{11,1... | collective-permute-start | bytes 168488 | tf_op jit(solution)/shard_map/ppermute | solution.py:49
  258.5 14.2 %all_to_all.15 = bf16[16,64,128]{2,1,0:T(8,128)(2,1)S(1)} all-to-all(bf16[16,64,128]{2,1,0:T(8,128)(2,1)S(1)} %bitcast.190), channel_id=1, replica_groups=mesh['dp'=2,'space'=16] {'space'}, dimensions={0} | all-to-all | bytes 524288 | tf_op jit(solution)/shard_map/all_to_all | solution.py:712
  274.6 5.0 fusion.grad_ref
  279.6 2.6 collective-permute-start.22
  284.8 24.3 %edges_backward.3 = (bf16[2048,256]{1,0:T(8,128)(2,1)}, bf16[2048,256]{1,0:T(8,128)(2,1)}, bf16[4096,128]{1,0:T(8,128)(2,1)}, f32[4096,128]{1,0:T(8,128)}, bf16[4096,128]{1,0:T(8,128)(2,1)}) custom-call(s32[12288]{0:T(1024)} %broadcast_select_fusion.refs_0_.index_ref, f32[2048,256]{1,0:T(8,128)} %fusion.grad_ref, f32[2048,256]{1,0:T(8,128)} %get-tuple-element.96.back_ref, ...), custom_call_target="tpu_custom_call" | custom-call | bytes 75000000 | tf_op jit(solution)/shard_map/edges_backward/pallas_call | solution.py:509
  320.1 10.2 %collective-permute-done.23.first_ref = bf16[4096,128]{1,0:T(8,128)(2,1)S(1)} collective-permute-done((bf16[4096,128]{1,0:T(8,128)(2,1)}, bf16[4096,128]{1,0:T(8,128)(2,1)S(1)}, u32[]{:S(2)}, u32[]{:S(2)}) %collective-permute-start.23) | collective-permute-done | bytes 1048608 | tf_op jit(solution)/shard_map/ppermute | solution.py:77
  332.1 5.7 %round_backward.3 = (f32[2048,256]{1,0:T(8,128)}, bf16[2048,256]{1,0:T(8,128)(2,1)}) custom-call(f32[2048,256]{1,0:T(8,128)} %fusion.grad_ref, f32[4096,128]{1,0:T(8,128)} %get-tuple-element.99.own_ref, bf16[4096,128]{1,0:T(8,128)(2,1)} %copy-done.18, bf16[4096,128]{1,0:T(8,128)(2,1)} %collective-permute-done.24.last_ref, ...), custom_call_target="tpu_custom_call" | custom-call | bytes 21000000 | tf_op jit(solution)/shard_map/round_backward/pallas_call | solution.py:567
  337.8 24.1 %edges_backward.4 = (bf16[2048,256]{1,0:T(8,128)(2,1)}, bf16[2048,256]{1,0:T(8,128)(2,1)}, bf16[4096,128]{1,0:T(8,128)(2,1)}, f32[4096,128]{1,0:T(8,128)}, bf16[4096,128]{1,0:T(8,128)(2,1)}) custom-call(s32[12288]{0:T(1024)} %broadcast_select_fusion.refs_0_.index_ref, f32[2048,256]{1,0:T(8,128)} %get-tuple-element.107.grad_ref, ...), custom_call_target="tpu_custom_call" | custom-call | bytes 75000000 | tf_op jit(solution)/shard_map/edges_backward/pallas_call | solution.py:509
  362.0 2.6 fusion.81.refs_10_
  373.0 8.2 %collective-permute-done.25.first_ref = bf16[4096,128]{1,0:T(8,128)(2,1)} collective-permute-done((bf16[4096,128]{1,0:T(8,128)(2,1)}, bf16[4096,128]{1,0:T(8,128)(2,1)}, u32[]{:S(2)}, u32[]{:S(2)}) %collective-permute-start.25) | collective-permute-done | bytes 1048608 | tf_op jit(solution)/shard_map/ppermute | solution.py:77
  382.3 5.7 %round_backward.4 = (f32[2048,256]{1,0:T(8,128)}, bf16[2048,256]{1,0:T(8,128)(2,1)}) custom-call(f32[2048,256]{1,0:T(8,128)} %get-tuple-element.107.grad_ref, f32[4096,128]{1,0:T(8,128)} %get-tuple-element.110.own_ref, bf16[4096,128]{1,0:T(8,128)(2,1)} %collective-permute-done.25.first_ref, bf16[4096,128]{1,0:T(8,128)(2,1)} %collective-permute-done.26.last_ref, ...), custom_call_target="tpu_custom_call" | custom-call | bytes 21000000 | tf_op jit(solution)/shard_map/round_backward/pallas_call | solution.py:567
  388.0 24.2 %edges_backward.5 = (bf16[2048,256]{1,0:T(8,128)(2,1)}, bf16[2048,256]{1,0:T(8,128)(2,1)}, bf16[4096,128]{1,0:T(8,128)(2,1)}, f32[4096,128]{1,0:T(8,128)}, bf16[4096,128]{1,0:T(8,128)(2,1)}) custom-call(s32[12288]{0:T(1024)} %broadcast_select_fusion.refs_0_.index_ref, f32[2048,256]{1,0:T(8,128)} %get-tuple-element.115.grad_ref, ...), custom_call_target="tpu_custom_call" | custom-call | bytes 75000000 | tf_op jit(solution)/shard_map/edges_backward/pallas_call | solution.py:509
  412.2 2.6 fusion.87.refs_5_
  423.2 7.3 %collective-permute-done.27.first_ref = bf16[4096,128]{1,0:T(8,128)(2,1)} collective-permute-done((bf16[4096,128]{1,0:T(8,128)(2,1)}, bf16[4096,128]{1,0:T(8,128)(2,1)}, u32[]{:S(2)}, u32[]{:S(2)}) %collective-permute-start.27) | collective-permute-done | bytes 1048608 | tf_op jit(solution)/shard_map/ppermute | solution.py:77
  430.8 5.7 %round_backward.5 = (f32[2048,256]{1,0:T(8,128)}, bf16[2048,256]{1,0:T(8,128)(2,1)}) custom-call(f32[2048,256]{1,0:T(8,128)} %get-tuple-element.115.grad_ref, f32[4096,128]{1,0:T(8,128)} %get-tuple-element.118.own_ref, bf16[4096,128]{1,0:T(8,128)(2,1)} %collective-permute-done.27.first_ref, bf16[4096,128]{1,0:T(8,128)(2,1)} %collective-permute-done.28.last_ref, ...), custom_call_target="tpu_custom_call" | custom-call | bytes 21000000 | tf_op jit(solution)/shard_map/round_backward/pallas_call | solution.py:567
  438.2 3.1 collective-permute-start.30
  441.4 3.8 collective-permute-start.29
  445.2 6.9 %encode_backward.1 = (f32[128,256]{1,0:T(8,128)}, f32[256,256]{1,0:T(8,128)}, f32[2,256]{1,0:T(2,128)}) custom-call(f32[2048,256]{1,0:T(8,128)} %get-tuple-element.123.grad_ref, bf16[2048,256]{1,0:T(8,128)(2,1)} %get-tuple-element.124.gathered_ref, bf16[1024,128]{1,0:T(8,128)(2,1)} %bitcast.176, s32[1024,1]{1,0:T(8,128)} %get-tuple-element.181.ids_ref, ...), custom_call_target="tpu_custom_call" | custom-call | bytes 21000000 | tf_op jit(solution)/shard_map/encode_backward/pallas_call | solution.py:656
  453.3 5.2 collect_rows.1
  458.6 3.0 collective-permute-done.31
  466.7 7.2 %collective-permute-done.34 = bf16[2,2,2,72,256]{4,3,2,1,0:T(8,128)(2,1)} collective-permute-done((bf16[2,2,2,72,256]{4,3,2,1,0:T(8,128)(2,1)}, bf16[2,2,2,72,256]{4,3,2,1,0:T(8,128)(2,1)}, u32[]{:S(2)}, u32[]{:S(2)}) %collective-permute-start.34) | collective-permute-done | bytes 294944 | tf_op jit(solution)/shard_map/ppermute | solution.py:94
  476.8 3.3 collective-permute-done.35
  485.6 6.8 %collective-permute-start.39 = (bf16[72,256]{1,0:T(8,128)(2,1)S(1)}, bf16[72,256]{1,0:T(8,128)(2,1)S(1)}, u32[]{:S(2)}, u32[]{:S(2)}) collective-permute-start(bf16[72,256]{1,0:T(8,128)(2,1)S(1)} %fusion.67), channel_id=1, source_target_pairs={{0,8},{1,9},{2,10},{3,11},{4,12},{5,13},{6,14},{7,15},{8,0},{9,1},... | collective-permute-start | bytes 110600 | tf_op jit(solution)/shard_map/ppermute | solution.py:94
  494.4 3.0 collective-permute-done.37
  500.2 3.6 collective-permute-done.41
  504.0 3.3 collective-permute-done.42
  508.3 2.7 collective-permute-done.43
  512.2 3.6 select_bitcast_fusion.1
  520.0 8.0 %collective-permute-done.45 = bf16[1024,256]{1,0:T(8,128)(2,1)S(1)} collective-permute-done((bf16[1024,256]{1,0:T(8,128)(2,1)S(1)}, bf16[1024,256]{1,0:T(8,128)(2,1)S(1)}, u32[]{:S(2)}, u32[]{:S(2)}) %collective-permute-start.45) | collective-permute-done | bytes 524320 | tf_op jit(solution)/shard_map/ppermute | solution.py:737
  (316 shorter events, 120.5 us)
Async XLA Ops:
  5.8 16.9 %collective-permute-start.5 = (bf16[1,72,256]{2,1,0:T(8,128)(2,1)S(1)}, bf16[1,72,256]{2,1,0:T(8,128)(2,1)S(1)}, u32[]{:S(2)}, u32[]{:S(2)}) collective-permute-start(bf16[1,72,256]{2,1,0:T(8,128)(2,1)S(1)} %get-tuple-element.206), channel_id=1, source_target_pairs={{0,8},{1,9},{2,10},{3,11},{4,12},{5,13},{6,14},{7,15},{8,0},{9,1},... | collective-permute-start | bytes 110600 | tf_op jit(solution)/shard_map/ppermute | solution.py:94
  8.4 14.4 %collective-permute-start.1 = (bf16[1,72,256]{2,1,0:T(8,128)(2,1)S(1)}, bf16[1,72,256]{2,1,0:T(8,128)(2,1)S(1)}, u32[]{:S(2)}, u32[]{:S(2)}) collective-permute-start(bf16[1,72,256]{2,1,0:T(8,128)(2,1)S(1)} %get-tuple-element.207), channel_id=1, source_target_pairs={{0,8},{1,9},{2,10},{3,11},{4,12},{5,13},{6,14},{7,15},{8,0},{9,1},... | collective-permute-start | bytes 110600 | tf_op jit(solution)/shard_map/ppermute | solution.py:94
  15.4 32.8 %all-to-all-start = ((bf16[16,64,128]{2,1,0:T(8,128)(2,1)}), bf16[16,64,128]{2,1,0:T(8,128)(2,1)S(1)}, u32[]{:S(2)}, u32[]{:S(2)}) async-start(bf16[16,64,128]{2,1,0:T(8,128)(2,1)} %bitcast.5), calls=%async_computation | async-start | bytes 524288 | tf_op jit(solution)/shard_map/all_to_all | solution.py:712
  22.7 6.6 %collective-permute-start.6 = (bf16[2,72,256]{2,1,0:T(8,128)(2,1)S(1)}, bf16[2,72,256]{2,1,0:T(8,128)(2,1)S(1)}, u32[]{:S(2)}, u32[]{:S(2)}) collective-permute-start(bf16[2,72,256]{2,1,0:T(8,128)(2,1)S(1)} %pad_maximum_fusion.7), channel_id=1, source_target_pairs={{0,4},{1,5},{2,6},{3,7},{4,0},{5,1},{6,2},{7,3},{8,12},{9,13},{10,... | collective-permute-start | bytes 221192 | tf_op jit(solution)/shard_map/ppermute | solution.py:94
  22.8 8.2 %collective-permute-start.2 = (bf16[2,72,256]{2,1,0:T(8,128)(2,1)S(1)}, bf16[2,72,256]{2,1,0:T(8,128)(2,1)S(1)}, u32[]{:S(2)}, u32[]{:S(2)}) collective-permute-start(bf16[2,72,256]{2,1,0:T(8,128)(2,1)S(1)} %pad_maximum_fusion.6), channel_id=1, source_target_pairs={{0,4},{1,5},{2,6},{3,7},{4,0},{5,1},{6,2},{7,3},{8,12},{9,13},{10,... | collective-permute-start | bytes 221192 | tf_op jit(solution)/shard_map/ppermute | solution.py:94
  29.3 7.8 %collective-permute-start.7 = (bf16[4,72,256]{2,1,0:T(8,128)(2,1)S(1)}, bf16[4,72,256]{2,1,0:T(8,128)(2,1)S(1)}, u32[]{:S(2)}, u32[]{:S(2)}) collective-permute-start(bf16[4,72,256]{2,1,0:T(8,128)(2,1)S(1)} %pad_maximum_fusion.5), channel_id=1, source_target_pairs={{0,1},{1,0},{2,3},{3,2},{4,5},{5,4},{6,7},{7,6},{8,9},{9,8},{10,11... | collective-permute-start | bytes 442376 | tf_op jit(solution)/shard_map/ppermute | solution.py:94
  31.1 5.2 collective-permute-start.3
  36.3 6.8 %collective-permute-start.4 = (bf16[8,72,256]{2,1,0:T(8,128)(2,1)S(1)}, bf16[8,72,256]{2,1,0:T(8,128)(2,1)S(1)}, u32[]{:S(2)}, u32[]{:S(2)}) collective-permute-start(bf16[8,72,256]{2,1,0:T(8,128)(2,1)S(1)} %pad_maximum_fusion.1), channel_id=1, source_target_pairs={{0,1},{1,0},{2,3},{3,2},{4,5},{5,4},{6,7},{7,6},{8,9},{9,8},{10,11... | collective-permute-start | bytes 884744 | tf_op jit(solution)/shard_map/ppermute | solution.py:94
  37.1 6.8 %collective-permute-start.8 = (bf16[8,72,256]{2,1,0:T(8,128)(2,1)S(1)}, bf16[8,72,256]{2,1,0:T(8,128)(2,1)S(1)}, u32[]{:S(2)}, u32[]{:S(2)}) collective-permute-start(bf16[8,72,256]{2,1,0:T(8,128)(2,1)S(1)} %pad_maximum_fusion.2), channel_id=1, source_target_pairs={{0,2},{1,3},{2,0},{3,1},{4,6},{5,7},{6,4},{7,5},{8,10},{9,11},{10,... | collective-permute-start | bytes 884744 | tf_op jit(solution)/shard_map/ppermute | solution.py:94
  43.2 6.9 %collective-permute-start.9 = (bf16[16,72,256]{2,1,0:T(8,128)(2,1)S(1)}, bf16[16,72,256]{2,1,0:T(8,128)(2,1)S(1)}, u32[]{:S(2)}, u32[]{:S(2)}) collective-permute-start(bf16[16,72,256]{2,1,0:T(8,128)(2,1)S(1)} %constant_dynamic-update-slice_fusion.refs_0_), channel_id=1, source_target_pairs={{0,16},{16,0},{1,17},{17,1},{2,18},{18,2},{3,19},{19,3},{4,20},{20... | collective-permute-start | bytes 1769480 | tf_op jit(solution)/shard_map/ppermute | solution.py:94
  44.0 6.1 %collective-permute-start.10 = (bf16[16,72,256]{2,1,0:T(8,128)(2,1)S(1)}, bf16[16,72,256]{2,1,0:T(8,128)(2,1)S(1)}, u32[]{:S(2)}, u32[]{:S(2)}) collective-permute-start(bf16[16,72,256]{2,1,0:T(8,128)(2,1)S(1)} %constant_dynamic-update-slice_fusion.5.refs_1_), channel_id=1, source_target_pairs={{0,16},{16,0},{1,17},{17,1},{2,18},{18,2},{3,19},{19,3},{4,20},{20... | collective-permute-start | bytes 1769480 | tf_op jit(solution)/shard_map/ppermute | solution.py:94
  44.1 20.7 %collective-permute-start = (s32[12288]{0:T(1024)S(1)}, s32[12288]{0:T(1024)S(1)}, u32[]{:S(2)}, u32[]{:S(2)}) collective-permute-start(s32[12288]{0:T(1024)S(1)} %mul.201), channel_id=1, source_target_pairs={{2,3},{3,2},{4,6},{5,4},{6,5},{8,11},{10,8},{11,10},{12,14},{13,15... | collective-permute-start | bytes 147464 | tf_op jit(solution)/shard_map/ppermute | solution.py:734
  62.8 26.6 %collective-permute-start.12 = (bf16[4096,128]{1,0:T(8,128)(2,1)}, bf16[4096,128]{1,0:T(8,128)(2,1)S(1)}, u32[]{:S(2)}, u32[]{:S(2)}) collective-permute-start(bf16[4096,128]{1,0:T(8,128)(2,1)} %get-tuple-element.85.refs_3_), channel_id=1, source_target_pairs={{1,0},{3,1},{2,3},{6,2},{4,6},{5,4},{7,5},{11,7},{9,11},{8,9},{10,... | collective-permute-start | bytes 3145736 | tf_op jit(solution)/shard_map/ppermute | solution.py:77
  64.2 25.3 %collective-permute-start.11 = (bf16[4096,128]{1,0:T(8,128)(2,1)}, bf16[4096,128]{1,0:T(8,128)(2,1)}, u32[]{:S(2)}, u32[]{:S(2)}) collective-permute-start(bf16[4096,128]{1,0:T(8,128)(2,1)} %get-tuple-element.85.refs_3_), channel_id=1, source_target_pairs={{0,1},{1,3},{3,2},{2,6},{6,4},{4,5},{5,7},{7,11},{11,9},{9,8},{8,1... | collective-permute-start | bytes 3145736 | tf_op jit(solution)/shard_map/ppermute | solution.py:77
  115.4 24.4 %collective-permute-start.14 = (bf16[4096,128]{1,0:T(8,128)(2,1)}, bf16[4096,128]{1,0:T(8,128)(2,1)S(1)}, u32[]{:S(2)}, u32[]{:S(2)}) collective-permute-start(bf16[4096,128]{1,0:T(8,128)(2,1)} %get-tuple-element.88.refs_3_), channel_id=1, source_target_pairs={{1,0},{3,1},{2,3},{6,2},{4,6},{5,4},{7,5},{11,7},{9,11},{8,9},{10,... | collective-permute-start | bytes 3145736 | tf_op jit(solution)/shard_map/ppermute | solution.py:77
  116.7 24.1 %collective-permute-start.13 = (bf16[4096,128]{1,0:T(8,128)(2,1)}, bf16[4096,128]{1,0:T(8,128)(2,1)S(1)}, u32[]{:S(2)}, u32[]{:S(2)}) collective-permute-start(bf16[4096,128]{1,0:T(8,128)(2,1)} %get-tuple-element.88.refs_3_), channel_id=1, source_target_pairs={{0,1},{1,3},{3,2},{2,6},{6,4},{4,5},{5,7},{7,11},{11,9},{9,8},{8,1... | collective-permute-start | bytes 3145736 | tf_op jit(solution)/shard_map/ppermute | solution.py:77
  166.8 23.2 %collective-permute-start.16 = (bf16[4096,128]{1,0:T(8,128)(2,1)}, bf16[4096,128]{1,0:T(8,128)(2,1)S(1)}, u32[]{:S(2)}, u32[]{:S(2)}) collective-permute-start(bf16[4096,128]{1,0:T(8,128)(2,1)} %get-tuple-element.90.refs_3_), channel_id=1, source_target_pairs={{1,0},{3,1},{2,3},{6,2},{4,6},{5,4},{7,5},{11,7},{9,11},{8,9},{10,... | collective-permute-start | bytes 3145736 | tf_op jit(solution)/shard_map/ppermute | solution.py:77
  167.6 23.4 %collective-permute-start.15 = (bf16[4096,128]{1,0:T(8,128)(2,1)}, bf16[4096,128]{1,0:T(8,128)(2,1)S(1)}, u32[]{:S(2)}, u32[]{:S(2)}) collective-permute-start(bf16[4096,128]{1,0:T(8,128)(2,1)} %get-tuple-element.90.refs_3_), channel_id=1, source_target_pairs={{0,1},{1,3},{3,2},{2,6},{6,4},{4,5},{5,7},{7,11},{11,9},{9,8},{8,1... | collective-permute-start | bytes 3145736 | tf_op jit(solution)/shard_map/ppermute | solution.py:77
  169.0 69.6 %collective-permute-start.17 = (s32[360]{0:T(512)S(1)}, s32[360]{0:T(512)S(1)}, u32[]{:S(2)}, u32[]{:S(2)}) collective-permute-start(s32[360]{0:T(512)S(1)} %slice.269), channel_id=1, source_target_pairs={{0,1},{1,2},{2,3},{3,4},{4,5},{5,6},{6,7},{7,8},{8,9},{9,10},{10,1... | collective-permute-start | bytes 4328 | tf_op jit(solution)/shard_map/ppermute | solution.py:49
  221.7 23.1 %all-to-all-start.1 = ((bf16[16,64,128]{2,1,0:T(8,128)(2,1)}), bf16[16,64,128]{2,1,0:T(8,128)(2,1)S(1)}, u32[]{:S(2)}, u32[]{:S(2)}) async-start(bf16[16,64,128]{2,1,0:T(8,128)(2,1)} %bitcast.22), calls=%async_computation.1 | async-start | bytes 524288 | tf_op jit(solution)/shard_map/all_to_all | solution.py:712
  232.4 7.5 %collective-permute-start.19 = (bf16[78,360]{1,0:T(8,128)(2,1)S(1)}, bf16[78,360]{1,0:T(8,128)(2,1)S(1)}, u32[]{:S(2)}, u32[]{:S(2)}) collective-permute-start(bf16[78,360]{1,0:T(8,128)(2,1)S(1)} %get-tuple-element.204), channel_id=1, source_target_pairs={{1,0},{2,1},{3,2},{4,3},{5,4},{6,5},{7,6},{8,7},{9,8},{10,9},{11,1... | collective-permute-start | bytes 168488 | tf_op jit(solution)/shard_map/ppermute | solution.py:49
  236.6 7.9 %collective-permute-start.18 = (bf16[78,360]{1,0:T(8,128)(2,1)S(1)}, bf16[78,360]{1,0:T(8,128)(2,1)S(1)}, u32[]{:S(2)}, u32[]{:S(2)}) collective-permute-start(bf16[78,360]{1,0:T(8,128)(2,1)S(1)} %get-tuple-element.205), channel_id=1, source_target_pairs={{0,1},{1,2},{2,3},{3,4},{4,5},{5,6},{6,7},{7,8},{8,9},{9,10},{10,1... | collective-permute-start | bytes 168488 | tf_op jit(solution)/shard_map/ppermute | solution.py:49
  245.4 10.2 %collective-permute-start.20 = (bf16[78,360]{1,0:T(8,128)(2,1)S(1)}, bf16[78,360]{1,0:T(8,128)(2,1)S(1)}, u32[]{:S(2)}, u32[]{:S(2)}) collective-permute-start(bf16[78,360]{1,0:T(8,128)(2,1)S(1)} %get-tuple-element.202), channel_id=1, source_target_pairs={{0,1},{1,2},{2,3},{3,4},{4,5},{5,6},{6,7},{7,8},{8,9},{9,10},{10,1... | collective-permute-start | bytes 168488 | tf_op jit(solution)/shard_map/ppermute | solution.py:49
  247.3 8.3 %collective-permute-start.21 = (bf16[78,360]{1,0:T(8,128)(2,1)S(1)}, bf16[78,360]{1,0:T(8,128)(2,1)S(1)}, u32[]{:S(2)}, u32[]{:S(2)}) collective-permute-start(bf16[78,360]{1,0:T(8,128)(2,1)S(1)} %get-tuple-element.203), channel_id=1, source_target_pairs={{1,0},{2,1},{3,2},{4,3},{5,4},{6,5},{7,6},{8,7},{9,8},{10,9},{11,1... | collective-permute-start | bytes 168488 | tf_op jit(solution)/shard_map/ppermute | solution.py:49
  279.6 33.0 %collective-permute-start.22 = (bf16[2048,256]{1,0:T(8,128)(2,1)S(1)}, bf16[2048,256]{1,0:T(8,128)(2,1)}, u32[]{:S(2)}, u32[]{:S(2)}) collective-permute-start(bf16[2048,256]{1,0:T(8,128)(2,1)S(1)} %convert_element_type.204), channel_id=1, source_target_pairs={{3,2},{2,3},{6,4},{4,5},{5,6},{11,8},{8,10},{10,11},{14,12},{15,13... | collective-permute-start | bytes 3145736 | tf_op jit(solution)/shard_map/ppermute | solution.py:737
  312.7 17.7 %collective-permute-start.23 = (bf16[4096,128]{1,0:T(8,128)(2,1)}, bf16[4096,128]{1,0:T(8,128)(2,1)S(1)}, u32[]{:S(2)}, u32[]{:S(2)}) collective-permute-start(bf16[4096,128]{1,0:T(8,128)(2,1)} %get-tuple-element.103), channel_id=1, source_target_pairs={{0,1},{1,3},{3,2},{2,6},{6,4},{4,5},{5,7},{7,11},{11,9},{9,8},{8,1... | collective-permute-start | bytes 3145736 | tf_op jit(solution)/shard_map/ppermute | solution.py:77
  314.6 17.5 %collective-permute-start.24 = (bf16[4096,128]{1,0:T(8,128)(2,1)S(1)}, bf16[4096,128]{1,0:T(8,128)(2,1)}, u32[]{:S(2)}, u32[]{:S(2)}) collective-permute-start(bf16[4096,128]{1,0:T(8,128)(2,1)S(1)} %copy-done.58), channel_id=1, source_target_pairs={{1,0},{3,1},{2,3},{6,2},{4,6},{5,4},{7,5},{11,7},{9,11},{8,9},{10,... | collective-permute-start | bytes 3145736 | tf_op jit(solution)/shard_map/ppermute | solution.py:77
  364.6 16.6 %collective-permute-start.25 = (bf16[4096,128]{1,0:T(8,128)(2,1)}, bf16[4096,128]{1,0:T(8,128)(2,1)}, u32[]{:S(2)}, u32[]{:S(2)}) collective-permute-start(bf16[4096,128]{1,0:T(8,128)(2,1)} %get-tuple-element.111), channel_id=1, source_target_pairs={{0,1},{1,3},{3,2},{2,6},{6,4},{4,5},{5,7},{7,11},{11,9},{9,8},{8,1... | collective-permute-start | bytes 3145736 | tf_op jit(solution)/shard_map/ppermute | solution.py:77
  365.8 16.5 %collective-permute-start.26 = (bf16[4096,128]{1,0:T(8,128)(2,1)S(1)}, bf16[4096,128]{1,0:T(8,128)(2,1)}, u32[]{:S(2)}, u32[]{:S(2)}) collective-permute-start(bf16[4096,128]{1,0:T(8,128)(2,1)S(1)} %copy-done.60), channel_id=1, source_target_pairs={{1,0},{3,1},{2,3},{6,2},{4,6},{5,4},{7,5},{11,7},{9,11},{8,9},{10,... | collective-permute-start | bytes 3145736 | tf_op jit(solution)/shard_map/ppermute | solution.py:77
  414.7 15.8 %collective-permute-start.27 = (bf16[4096,128]{1,0:T(8,128)(2,1)}, bf16[4096,128]{1,0:T(8,128)(2,1)}, u32[]{:S(2)}, u32[]{:S(2)}) collective-permute-start(bf16[4096,128]{1,0:T(8,128)(2,1)} %get-tuple-element.119), channel_id=1, source_target_pairs={{0,1},{1,3},{3,2},{2,6},{6,4},{4,5},{5,7},{7,11},{11,9},{9,8},{8,1... | collective-permute-start | bytes 3145736 | tf_op jit(solution)/shard_map/ppermute | solution.py:77
  415.3 15.5 %collective-permute-start.28 = (bf16[4096,128]{1,0:T(8,128)(2,1)S(1)}, bf16[4096,128]{1,0:T(8,128)(2,1)}, u32[]{:S(2)}, u32[]{:S(2)}) collective-permute-start(bf16[4096,128]{1,0:T(8,128)(2,1)S(1)} %copy-done.59), channel_id=1, source_target_pairs={{1,0},{3,1},{2,3},{6,2},{4,6},{5,4},{7,5},{11,7},{9,11},{8,9},{10,... | collective-permute-start | bytes 3145736 | tf_op jit(solution)/shard_map/ppermute | solution.py:77
  438.2 20.2 %collective-permute-start.30 = (bf16[512,256]{1,0:T(8,128)(2,1)S(1)}, bf16[512,256]{1,0:T(8,128)(2,1)S(1)}, u32[]{:S(2)}, u32[]{:S(2)}) collective-permute-start(bf16[512,256]{1,0:T(8,128)(2,1)S(1)} %get-tuple-element.199), channel_id=1, source_target_pairs={{3,2},{2,3},{6,4},{4,5},{5,6},{11,8},{8,10},{10,11},{14,12},{15,13... | collective-permute-start | bytes 786440 | tf_op jit(solution)/shard_map/ppermute | solution.py:737
  441.4 11.9 %collective-permute-start.29 = (bf16[512,256]{1,0:T(8,128)(2,1)S(1)}, bf16[512,256]{1,0:T(8,128)(2,1)S(1)}, u32[]{:S(2)}, u32[]{:S(2)}) collective-permute-start(bf16[512,256]{1,0:T(8,128)(2,1)S(1)} %get-tuple-element.200), channel_id=1, source_target_pairs={{3,2},{2,3},{6,4},{4,5},{5,6},{11,8},{8,10},{10,11},{14,12},{15,13... | collective-permute-start | bytes 786440 | tf_op jit(solution)/shard_map/ppermute | solution.py:737
  458.5 3.1 collective-permute-start.31
  464.5 9.4 %collective-permute-start.34 = (bf16[2,2,2,72,256]{4,3,2,1,0:T(8,128)(2,1)}, bf16[2,2,2,72,256]{4,3,2,1,0:T(8,128)(2,1)}, u32[]{:S(2)}, u32[]{:S(2)}) collective-permute-start(bf16[2,2,2,72,256]{4,3,2,1,0:T(8,128)(2,1)} %fusion.25), channel_id=1, source_target_pairs={{0,2},{1,3},{2,0},{3,1},{4,6},{5,7},{6,4},{7,5},{8,10},{9,11},{10,... | collective-permute-start | bytes 884744 | tf_op jit(solution)/shard_map/ppermute | solution.py:94
  466.2 9.6 %collective-permute-start.32 = (bf16[2,2,2,72,256]{4,3,0,1,2:T(8,128)(2,1)S(1)}, bf16[2,2,2,72,256]{4,3,0,1,2:T(8,128)(2,1)S(1)}, u32[]{:S(2)}, u32[]{:S(2)}) collective-permute-start(bf16[2,2,2,72,256]{4,3,0,1,2:T(8,128)(2,1)S(1)} %fusion.26), channel_id=1, source_target_pairs={{0,1},{1,0},{2,3},{3,2},{4,5},{5,4},{6,7},{7,6},{8,9},{9,8},{10,11... | collective-permute-start | bytes 884744 | tf_op jit(solution)/shard_map/ppermute | solution.py:94
  474.9 5.2 collective-permute-start.35
  475.9 5.2 collective-permute-start.33
  481.1 4.4 collective-permute-start.38
  481.2 11.2 %collective-permute-start.36 = (bf16[2,72,256]{2,1,0:T(8,128)(2,1)S(1)}, bf16[2,72,256]{2,1,0:T(8,128)(2,1)S(1)}, u32[]{:S(2)}, u32[]{:S(2)}) collective-permute-start(bf16[2,72,256]{2,1,0:T(8,128)(2,1)S(1)} %fusion.57), channel_id=1, source_target_pairs={{0,4},{1,5},{2,6},{3,7},{4,0},{5,1},{6,2},{7,3},{8,12},{9,13},{10,... | collective-permute-start | bytes 221192 | tf_op jit(solution)/shard_map/ppermute | solution.py:94
  485.6 8.8 %collective-permute-start.39 = (bf16[72,256]{1,0:T(8,128)(2,1)S(1)}, bf16[72,256]{1,0:T(8,128)(2,1)S(1)}, u32[]{:S(2)}, u32[]{:S(2)}) collective-permute-start(bf16[72,256]{1,0:T(8,128)(2,1)S(1)} %fusion.67), channel_id=1, source_target_pairs={{0,8},{1,9},{2,10},{3,11},{4,12},{5,13},{6,14},{7,15},{8,0},{9,1},... | collective-permute-start | bytes 110600 | tf_op jit(solution)/shard_map/ppermute | solution.py:94
  492.5 4.9 collective-permute-start.37
  498.9 1.2 collective-permute-start.40
  500.1 3.6 collective-permute-start.41
  503.8 3.6 collective-permute-start.42
  507.4 3.6 collective-permute-start.43
  511.0 6.6 %collective-permute-start.44 = (f32[8,128]{1,0:T(8,128)S(1)}, f32[8,128]{1,0:T(8,128)S(1)}, u32[]{:S(2)}, u32[]{:S(2)}) collective-permute-start(f32[8,128]{1,0:T(8,128)S(1)} %add.189), channel_id=1, source_target_pairs={{0,8},{1,9},{2,10},{3,11},{4,12},{5,13},{6,14},{7,15},{8,0},{9,1},... | collective-permute-start | bytes 12296 | tf_op jit(solution)/shard_map/ppermute | solution.py:94
  515.7 12.2 %collective-permute-start.45 = (bf16[1024,256]{1,0:T(8,128)(2,1)S(1)}, bf16[1024,256]{1,0:T(8,128)(2,1)S(1)}, u32[]{:S(2)}, u32[]{:S(2)}) collective-permute-start(bf16[1024,256]{1,0:T(8,128)(2,1)S(1)} %slice.371), channel_id=1, source_target_pairs={{3,2},{2,3},{6,4},{4,5},{5,6},{11,8},{8,10},{10,11},{14,12},{15,13... | collective-permute-start | bytes 1572872 | tf_op jit(solution)/shard_map/ppermute | solution.py:737
  (63 other events, 610.7 us)

commit v7 on v6

--- a/solution.py
+++ b/solution.py
@@ -87,7 +87,7 @@
 
 
 def parts_of():
-    return [CH, D, D, CH, ROUNDS * 5 * D, 3 + 2 * ROUNDS]
+    return [CH, D, D, CH] + [5 * D] * ROUNDS + [3 + 2 * ROUNDS]
 
 
 def swapped(value, axis, bit):
@@ -98,11 +98,13 @@
     return [1 << n for n in range(lax.axis_size(axis).bit_length() - 1)]
 
 
-def summed_everywhere(value):
-    for axis in ALL:
-        for bit in bits_of(axis):
-            value = value + swapped(value, axis, bit)
-    return value
+def summed_everywhere(value, arriving):
+    turns = [(axis, bit) for axis in ALL for bit in bits_of(axis)]
+    for turn, (axis, bit) in enumerate(turns):
+        value = value + swapped(value, axis, bit)
+        if turn == len(turns) - 3:
+            value, arriving = lax.optimization_barrier((value, arriving))
+    return value, arriving
 
 
 def orders():
@@ -110,16 +112,16 @@
     return bits, bits[1:2] + bits[:1] + bits[2:]
 
 
-def gathered_blocks(piece):
+def gathered_blocks(piece, posted):
     half = piece.shape[0] // 2
-    held = []
-    for part, order in zip((piece[:half], piece[half:]), orders()):
-        names, part = [], part[None]
-        for bit in reversed(order):
-            part = jnp.concatenate([part, swapped(part, "space", bit)], 0)
-            names.insert(0, bit)
-        held.append(part)
-    return held, [swapped(part, "dp", 1) for part in held]
+    held = [piece[None, :half], piece[None, half:]]
+    last = len(orders()[0]) - 1
+    for turn, bits in enumerate(reversed(list(zip(*orders())))):
+        if turn == last:
+            held[0], held[1], posted = lax.optimization_barrier((*held, posted))
+        for n, bit in enumerate(bits):
+            held[n] = jnp.concatenate([held[n], swapped(held[n], "space", bit)], 0)
+    return (held, [swapped(part, "dp", 1) for part in held]), posted
 
 
 def spread_rows(gathered, total, peers, place):
@@ -175,7 +177,7 @@
                 out[size:, :] = jnp.zeros((out.shape[0] - size, D), out.dtype)
             start = start + size
 
-    kinds = [jnp.bfloat16] * 5 + [jnp.float32]
+    kinds = [jnp.bfloat16] * (4 + ROUNDS) + [jnp.float32]
     talls = [HALF] + sizes[1:]
     return pl.pallas_call(
         body,
@@ -375,7 +377,7 @@
         new = mesh_in + inner(update, mats_ref[4], 1, 0)
         new_ref[...] = new
         if more:
-            weave(wide, inner(new.astype(jnp.bfloat16), next_ref[...], 1, 0))
+            weave(wide, inner(new.astype(jnp.bfloat16), next_ref[0], 1, 0))
             sent_ref[...] = wide[...].astype(jnp.bfloat16)
 
     whole_rows = pl.BlockSpec((tile, D), lambda i, *_: (i, 0))
@@ -391,7 +393,7 @@
     ]
     args = [index, mesh, before, own, after, mats, bias]
     if more:
-        ins.append(whole(following.shape))
+        ins.append(pl.BlockSpec((1, D, D), lambda *_: (0, 0, 0)))
         outs.append(woven)
         shapes.append(jax.ShapeDtypeStruct((2 * blocks, HALF), jnp.bfloat16))
         args.append(following)
@@ -545,7 +547,7 @@
     tile = 1024
 
     def body(
-        grad_ref, own_ref, first_ref, last_ref, guin_ref, dest_ref, turned_ref, new_ref, sent_ref, wide
+        grad_ref, own_ref, first_ref, last_ref, guin_ref, dest_ref, turned_ref, new_ref, sent_ref, out_ref, wide
     ):
         wide[...] = (
             own_ref[...] + first_ref[...].astype(jnp.float32) + last_ref[...].astype(jnp.float32)
@@ -554,13 +556,15 @@
         one, two = one.astype(jnp.bfloat16), two.astype(jnp.bfloat16)
         sent_ref[:, :HALF] = one
         sent_ref[:, HALF:] = two
-        new_ref[...] = (
+        new = (
             grad_ref[...]
             + inner(guin_ref[...], turned_ref[3], 1, 0)
             + inner(dest_ref[...], turned_ref[1], 1, 0)
             + inner(one, turned_ref[0, :HALF, :], 1, 0)
             + inner(two, turned_ref[0, HALF:, :], 1, 0)
         )
+        new_ref[...] = new
+        out_ref[...] = new.astype(jnp.bfloat16)
 
     rows = pl.BlockSpec((tile, D), lambda i: (i, 0))
     woven = pl.BlockSpec((2 * tile, HALF), lambda i: (i, 0))
@@ -568,9 +572,10 @@
         body,
         grid=(blocks // tile,),
         in_specs=[rows, woven, woven, woven, rows, rows, whole(turned.shape)],
-        out_specs=[rows, rows],
+        out_specs=[rows, rows, rows],
         out_shape=[
             jax.ShapeDtypeStruct((blocks, D), jnp.float32),
+            jax.ShapeDtypeStruct((blocks, D), jnp.bfloat16),
             jax.ShapeDtypeStruct((blocks, D), jnp.bfloat16),
         ],
         scratch_shapes=[pltpu.VMEM((2 * tile, HALF), jnp.float32)],
@@ -598,7 +603,7 @@
         gathered_ref[...] = gathered
         mesh = silu(inner(gathered, node_ref[...], 1, 0) + bias_ref[1:2, :])
         mesh_ref[...] = mesh
-        weave(wide, inner(mesh.astype(jnp.bfloat16), source_ref[...], 1, 0))
+        weave(wide, inner(mesh.astype(jnp.bfloat16), source_ref[0], 1, 0))
         sent_ref[...] = wide[...].astype(jnp.bfloat16)
 
     rows = pl.BlockSpec((tile, D), lambda i: (i, 0))
@@ -606,7 +611,8 @@
     return pl.pallas_call(
         body,
         grid=(H // tile,),
-        in_specs=[whole(arg.shape) for arg in args],
+        in_specs=[whole(arg.shape) for arg in args[:-1]]
+        + [pl.BlockSpec((1, D, D), lambda *_: (0, 0, 0))],
         out_specs=[rows, rows, pl.BlockSpec((2 * tile, HALF), lambda i: (i, 0))],
         out_shape=[
             jax.ShapeDtypeStruct((H, D), jnp.float32),
@@ -713,20 +719,21 @@
             rows.reshape(bands, capacity, HALF), "space", split_axis=0, concat_axis=0, tiled=True
         ).reshape(bands * capacity, HALF)
 
-    arrived = exchanged(inner(poster, columns, 1, 1).astype(jnp.bfloat16))
-    w_in, w_node, w_dec, w_out, w_round, biases, digits = spread_rows(
-        gathered_blocks(piece), total_size, peers, place
+    held, posted = gathered_blocks(piece, inner(poster, columns, 1, 1).astype(jnp.bfloat16))
+    arrived = exchanged(posted)
+    w_in, w_node, w_dec, w_out, *w_round, biases, digits = spread_rows(
+        held, total_size, peers, place
     )
     count = digits[0, 0] * 65536.0 + digits[0, 1] * 256.0 + digits[0, 2]
     w_out = jnp.pad(w_out.reshape(D, CH), ((0, 0), (0, HALF - CH)))
-    w_round = w_round.reshape(ROUNDS, 5, D, D)
+    w_round = [mats.reshape(5, D, D) for mats in w_round]
     b_head = biases[:3]
     b_round = biases[3:].reshape(ROUNDS, 2, D)
     ids = arrived[:, CH : CH + 3].astype(jnp.int32)
     ids = jnp.where(ids[:, 2:3] > 0, ids[:, 0:1] * 64 + ids[:, 1:2], -1)
     chooser = (ids == jnp.arange(blocks, dtype=jnp.int32)[None, :]).astype(jnp.bfloat16)
     mesh, gathered, sent = encode_rows(
-        arrived, ids.reshape(1, -1), w_in, w_node, biases, w_round[0, 0]
+        arrived, ids.reshape(1, -1), w_in, w_node, biases, w_round[0]
     )
     index = 2 * ((neighbours - band * blocks + H) % (blocks * bands)).T.reshape(-1)
     moved = [(n, place) for n, place in enumerate(walk) if n != place]
@@ -739,6 +746,10 @@
     def settled(own, came):
         return jnp.where(stays, own, came.astype(jnp.float32))
 
+    partner_by = partner - band * points - jnp.arange(points, dtype=jnp.int32)
+    partner_by = jnp.concatenate(
+        [shifted(partner_by[points - ROWW :], "space", 1), partner_by], 0
+    )[None, :]
     low_valid = counted.astype(jnp.bfloat16)
     valid_around = jnp.concatenate(
         [
@@ -747,24 +758,23 @@
             shifted(low_valid[:, :ROWW], "space", -1),
         ],
         1,
-    ).astype(jnp.float32)
+    )
     kept = []
     for layer in range(ROUNDS):
         before, after = halo(walk, sent[2 * (blocks - H) :], sent[: 2 * H])
         if layer == 0:
-            before, turned = lax.optimization_barrier((before, jnp.swapaxes(w_round, 2, 3)))
-        following = w_round[layer + 1, 0] if layer + 1 < ROUNDS else None
+            turned = [jnp.swapaxes(mats, 1, 2) for mats in w_round]
+            before, turned, valid_around, partner_by = lax.optimization_barrier(
+                (before, turned, valid_around, partner_by)
+            )
+        following = w_round[layer + 1] if layer + 1 < ROUNDS else None
         new, back, update, agg, slopes, *rest = round_forward(
             index, mesh, before, sent, after, w_round[layer], b_round[layer], following
         )
         kept.append((mesh, back, update, agg, slopes))
         mesh = new
         sent = rest[0] if rest else None
-    partner_by = partner - band * points - jnp.arange(points, dtype=jnp.int32)
-    partner_by = jnp.concatenate(
-        [shifted(partner_by[points - ROWW :], "space", 1), partner_by], 0
-    )[None, :]
-    wide_valid = valid_around
+    wide_valid = valid_around.astype(jnp.float32)
     weights = [
         (
             by,
@@ -809,8 +819,9 @@
     grad_wdec = inner(fetched, grad_dec, 0, 0)
     grad_fetched = inner(grad_dec, w_dec, 1, 1).astype(jnp.bfloat16)
     grad_mesh = inner(chooser, grad_fetched, 0, 0)
-    grad_mesh, leaving = lax.optimization_barrier((grad_mesh, mesh.astype(jnp.bfloat16)))
-    final_mesh = at_home(leaving)
+    grad_mesh, final_mesh = lax.optimization_barrier((grad_mesh, mesh.astype(jnp.bfloat16)))
+    final_mesh = at_home(final_mesh)
+    leaving = grad_mesh.astype(jnp.bfloat16)
     mats_grads = [None] * (5 * ROUNDS)
     bias_grads = [None] * (2 * ROUNDS)
     for layer in reversed(range(ROUNDS)):
@@ -823,8 +834,12 @@
                 (to_before, to_after, final_mesh)
             )
         from_before, from_after = halo(walk, to_after, to_before)
+        if layer == ROUNDS - 1:
+            from_before, final_mesh = lax.optimization_barrier(
+                (from_before, settled(mesh, final_mesh))
+            )
         lowered = old.astype(jnp.bfloat16)
-        grad_out = grad_mesh.astype(jnp.bfloat16)
+        grad_out = leaving
         grads = [
             None,
             inner(lowered, dest_low, 0, 0),
@@ -834,13 +849,12 @@
         ]
         bias_grads[2 * layer] = jnp.sum(dest_low.astype(jnp.float32), 0, keepdims=True)
         bias_grads[2 * layer + 1] = jnp.sum(grad_uin.astype(jnp.float32), 0, keepdims=True)
-        grad_mesh, sent_low = round_backward(
+        grad_mesh, sent_low, leaving = round_backward(
             grad_mesh, own, from_before, from_after, grad_uin, dest_low, turned[layer]
         )
         grads[0] = inner(lowered, sent_low, 0, 0)
         mats_grads[5 * layer : 5 * layer + 5] = grads
     third = blocks // 4 // 16 * 16
-    leaving = grad_mesh.astype(jnp.bfloat16)
     early = at_home(leaving[:third])
     grad_win, grad_wnode, grad_bpair = encode_backward(
         grad_mesh, gathered, arrived, ids, w_in, w_node, biases
@@ -858,7 +872,9 @@
     late = at_home(leaving)
     mine = lax.dynamic_slice_in_dim(mine.reshape(-1), offset, shard)
     lane = lax.broadcasted_iota(jnp.int32, (8, HALF), 1)
-    sums = summed_everywhere(jnp.where(lane == 0, local_total, jnp.sum(mine * mine)))
+    sums, late = summed_everywhere(
+        jnp.where(lane == 0, local_total, jnp.sum(mine * mine)), late
+    )
     total, norm = sums[0, 0], jnp.sqrt(sums[0, 1])
     node_grads = settled(grad_mesh, jnp.concatenate([early, middle, late], 0))
     clipped = mine * jnp.minimum(1.0, 0.05 / norm)
@@ -875,7 +891,7 @@
         first,
         second,
         updated.astype(jnp.bfloat16),
-        settled(mesh, final_mesh).reshape(1, blocks, D),
+        final_mesh.reshape(1, blocks, D),
         node_grads.reshape(1, blocks, D),
         grad_pred.reshape(1, grad_pred.shape[0], points),
     )

time: 542 us -> 522 us (0.963)
  the two profiles are of different devices: /device:TPU:8 before, /device:TPU:0 now
where the time goes in v7:
time: 522 us; the launch traced here: 512 us
  Pallas kernels  186 us (36%)
  waiting for transfers between devices  132 us (25%)
  starting transfers between devices  83.9 us (16%)
  matrix products  33 us (6%)
  other arithmetic  30.2 us (6%)
  local copies, waits for them, and re-layouts  24 us (5%)
  blocking collectives  14.2 us (3%)
  between operations  8.34 us (2%)
    pallas_call x3, Pallas kernels, round_forward(): pl.pallas_call(body, grid_spec=pltpu.PrefetchScalarGridSpec(num_scalar_pr...  74 us
    pallas_call x3, Pallas kernels, edges_backward(): pl.pallas_call(body, grid_spec=pltpu.PrefetchScalarGridSpec(num_scalar_pr...  72.6 us
    ppermute x6, waiting for transfers between devices, halo(): lax.ppermute(initial, 'space', down)  41.3 us
    ppermute x24, starting transfers between devices, swapped(): lax.ppermute(value, axis, [(i, i ^ bit) for i in range(lax.axis_size(axis...  33.1 us
    dot_general x24, matrix products, inner(): lax.dot_general(left, right, (((left_dim,), (right_dim,)), ((), ())), pre...  32.6 us
    ppermute x24, waiting for transfers between devices, swapped(): lax.ppermute(value, axis, [(i, i ^ bit) for i in range(lax.axis_size(axis...  32 us
    ppermute x6, waiting for transfers between devices, halo(): lax.ppermute(last, 'space', up)  29.1 us
    ppermute x5, waiting for transfers between devices, shifted(): return lax.ppermute(shard, axis, pairs)  18.2 us
  transfers between devices with their start and end apart: 48, of which 27 were waited for; matrix products, arithmetic and copies ran while one was open for 10% of the time, Pallas kernels for 9%

profile of v7, /device:TPU:0, one launch (start us, length us, event | category | flops | bytes accessed | tf_op | source)
XLA Modules:
  0.0 512.2 jit_solution(18259929642093197494)
XLA Ops:
  5.8 4.1 collective-permute-start.3
  17.6 3.0 collective-permute-done.4
  29.1 3.5 collective-permute-start.14
  33.1 5.7 %all-to-all-start = ((bf16[16,64,128]{2,1,0:T(8,128)(2,1)}), bf16[16,64,128]{2,1,0:T(8,128)(2,1)S(1)}, u32[]{:S(2)}, u32[]{:S(2)}) async-start(bf16[16,64,128]{2,1,0:T(8,128)(2,1)} %bitcast.8), calls=%async_computation | async-start | bytes 524288 | tf_op jit(solution)/shard_map/all_to_all | solution.py:718
  41.8 5.5 %all-to-all-done = bf16[16,64,128]{2,1,0:T(8,128)(2,1)S(1)} async-done(((bf16[16,64,128]{2,1,0:T(8,128)(2,1)}), bf16[16,64,128]{2,1,0:T(8,128)(2,1)S(1)}, u32[]{:S(2)}, u32[]{:S(2)}) %all-to-all-start) | async-done | bytes 262176 | tf_op jit(solution)/shard_map/all_to_all | solution.py:718
  50.3 4.0 spread_rows.1
  54.4 5.9 %encode_rows.1 = (f32[2048,256]{1,0:T(8,128)}, bf16[2048,256]{1,0:T(8,128)(2,1)}, bf16[4096,128]{1,0:T(8,128)(2,1)}) custom-call(bf16[1024,128]{1,0:T(8,128)(2,1)} %bitcast.173, s32[1,1024]{1,0:T(1,128)} %bitcast.188, bf16[128,256]{1,0:T(8,128)(2,1)} %get-tuple-element.99.in_ref, bf16[256,256]{1,0:T(8,128)(2,1)} %get-tuple-element.100.node_ref, ...), custom_call_target="tpu_custom_call" | custom-call | bytes 15000000 | tf_op jit(solution)/shard_map/encode_rows/pallas_call | solution.py:611
  64.3 4.5 collective-permute-start.12
  70.9 11.6 %collective-permute-done.13 = bf16[78,360]{1,0:T(8,128)(2,1)S(1)} collective-permute-done((bf16[78,360]{1,0:T(8,128)(2,1)S(1)}, bf16[78,360]{1,0:T(8,128)(2,1)S(1)}, u32[]{:S(2)}, u32[]{:S(2)}) %collective-permute-start.13) | collective-permute-done | bytes 56192 | tf_op jit(solution)/shard_map/ppermute | solution.py:49
  90.8 24.9 %round_forward.3 = (f32[2048,256]{1,0:T(8,128)}, f32[2048,256]{1,0:T(8,128)}, bf16[2048,256]{1,0:T(8,128)(2,1)}, bf16[2048,256]{1,0:T(8,128)(2,1)}, bf16[6,4096,...) custom-call(s32[12288]{0:T(1024)} %broadcast_select_fusion.refs_0_.index_ref, f32[2048,256]{1,0:T(8,128)} %get-tuple-element.103.refs_1_, ...), custom_call_target="tpu_custom_call" | custom-call | bytes 75000000 | tf_op jit(solution)/shard_map/round_forward/pallas_call | solution.py:400
  115.7 3.6 collective-permute-start.17
  119.4 19.5 %collective-permute-done.17.refs_4_ = bf16[4096,128]{1,0:T(8,128)(2,1)S(1)} collective-permute-done((bf16[4096,128]{1,0:T(8,128)(2,1)}, bf16[4096,128]{1,0:T(8,128)(2,1)S(1)}, u32[]{:S(2)}, u32[]{:S(2)}) %collective-permute-start.17) | collective-permute-done | bytes 1048608 | tf_op jit(solution)/shard_map/ppermute | solution.py:77
  138.8 3.9 collective-permute-done.16.refs_2_
  143.7 25.1 %round_forward.4 = (f32[2048,256]{1,0:T(8,128)}, f32[2048,256]{1,0:T(8,128)}, bf16[2048,256]{1,0:T(8,128)(2,1)}, bf16[2048,256]{1,0:T(8,128)(2,1)}, bf16[6,4096,...) custom-call(s32[12288]{0:T(1024)} %broadcast_select_fusion.refs_0_.index_ref, f32[2048,256]{1,0:T(8,128)} %get-tuple-element.108.refs_1_, ...), custom_call_target="tpu_custom_call" | custom-call | bytes 75000000 | tf_op jit(solution)/shard_map/round_forward/pallas_call | solution.py:400
  169.5 2.8 collective-permute-start.18
  173.1 21.9 %collective-permute-done.19.refs_4_ = bf16[4096,128]{1,0:T(8,128)(2,1)S(1)} collective-permute-done((bf16[4096,128]{1,0:T(8,128)(2,1)}, bf16[4096,128]{1,0:T(8,128)(2,1)S(1)}, u32[]{:S(2)}, u32[]{:S(2)}) %collective-permute-start.19) | collective-permute-done | bytes 1048608 | tf_op jit(solution)/shard_map/ppermute | solution.py:77
  196.3 24.1 %round_forward.5 = (f32[2048,256]{1,0:T(8,128)}, f32[2048,256]{1,0:T(8,128)}, bf16[2048,256]{1,0:T(8,128)(2,1)}, bf16[2048,256]{1,0:T(8,128)(2,1)}, bf16[6,4096,128]{2,1,0:T(8,128)(2,1)}) custom-call(s32[12288]{0:T(1024)} %broadcast_select_fusion.refs_0_.index_ref, f32[2048,256]{1,0:T(8,128)} %get-tuple-element.110.refs_1_, bf16[4096,128]{1,0:T(8,128)(2,1)} %copy-done.39, ...), custom_call_target="tpu_custom_call" | custom-call | bytes 75000000 | tf_op jit(solution)/shard_map/round_forward/pallas_call | solution.py:400
  226.1 5.0 all-to-all-start.1
  233.6 6.0 %all-to-all-done.1 = bf16[16,64,128]{2,1,0:T(8,128)(2,1)S(1)} async-done(((bf16[16,64,128]{2,1,0:T(8,128)(2,1)}), bf16[16,64,128]{2,1,0:T(8,128)(2,1)S(1)}, u32[]{:S(2)}, u32[]{:S(2)}) %all-to-all-start.1) | async-done | bytes 262176 | tf_op jit(solution)/shard_map/all_to_all | solution.py:718
  240.2 3.3 collective-permute-start.20
  244.9 4.7 collective-permute-done.21
  252.6 14.2 %all_to_all.15 = bf16[16,64,128]{2,1,0:T(8,128)(2,1)S(1)} all-to-all(bf16[16,64,128]{2,1,0:T(8,128)(2,1)S(1)} %bitcast.186), channel_id=1, replica_groups=mesh['dp'=2,'space'=16] {'space'}, dimensions={0} | all-to-all | bytes 524288 | tf_op jit(solution)/shard_map/all_to_all | solution.py:718
  269.1 3.8 fusion.grad_ref
  274.5 24.3 %edges_backward.3 = (bf16[2048,256]{1,0:T(8,128)(2,1)}, bf16[2048,256]{1,0:T(8,128)(2,1)}, bf16[4096,128]{1,0:T(8,128)(2,1)}, f32[4096,128]{1,0:T(8,128)}, bf16[4096,128]{1,0:T(8,128)(2,1)}) custom-call(s32[12288]{0:T(1024)} %broadcast_select_fusion.refs_0_.index_ref, f32[2048,256]{1,0:T(8,128)} %fusion.grad_ref, f32[2048,256]{1,0:T(8,128)} %get-tuple-element.119.back_ref, ...), custom_call_target="tpu_custom_call" | custom-call | bytes 75000000 | tf_op jit(solution)/shard_map/edges_backward/pallas_call | solution.py:511
  299.9 2.4 fusion.112.refs_16_
  306.3 2.4 collective-permute-start.24
  311.3 3.5 convert_select_fusion
  314.8 10.6 %collective-permute-done.23.first_ref = bf16[4096,128]{1,0:T(8,128)(2,1)S(1)} collective-permute-done((bf16[4096,128]{1,0:T(8,128)(2,1)S(1)}, bf16[4096,128]{1,0:T(8,128)(2,1)S(1)}, u32[]{:S(2)}, u32[]{:S(2)}) %collective-permute-start.23) | collective-permute-done | bytes 1048608 | tf_op jit(solution)/shard_map/ppermute | solution.py:77
  326.4 5.9 %round_backward.3 = (f32[2048,256]{1,0:T(8,128)}, bf16[2048,256]{1,0:T(8,128)(2,1)}, bf16[2048,256]{1,0:T(8,128)(2,1)}) custom-call(f32[2048,256]{1,0:T(8,128)} %fusion.grad_ref, f32[4096,128]{1,0:T(8,128)} %get-tuple-element.122.own_ref, bf16[4096,128]{1,0:T(8,128)(2,1)} %copy-done.21, bf16[4096,128]{1,0:T(8,128)(2,1)} %collective-permute-done.24.last_ref, ...), custom_call_target="tpu_custom_call" | custom-call | bytes 21000000 | tf_op jit(solution)/shard_map/round_backward/pallas_call | solution.py:571
  332.3 24.3 %edges_backward.4 = (bf16[2048,256]{1,0:T(8,128)(2,1)}, bf16[2048,256]{1,0:T(8,128)(2,1)}, bf16[4096,128]{1,0:T(8,128)(2,1)}, f32[4096,128]{1,0:T(8,128)}, bf16[4096,128]{1,0:T(8,128)(2,1)}) custom-call(s32[12288]{0:T(1024)} %broadcast_select_fusion.refs_0_.index_ref, f32[2048,256]{1,0:T(8,128)} %get-tuple-element.132.grad_ref, ...), custom_call_target="tpu_custom_call" | custom-call | bytes 75000000 | tf_op jit(solution)/shard_map/edges_backward/pallas_call | solution.py:511
  356.6 3.8 collective-permute-start.26
  360.4 2.6 fusion.110.refs_11_
  368.6 7.8 %collective-permute-done.25.first_ref = bf16[4096,128]{1,0:T(8,128)(2,1)S(1)} collective-permute-done((bf16[4096,128]{1,0:T(8,128)(2,1)}, bf16[4096,128]{1,0:T(8,128)(2,1)S(1)}, u32[]{:S(2)}, u32[]{:S(2)}) %collective-permute-start.25) | collective-permute-done | bytes 1048608 | tf_op jit(solution)/shard_map/ppermute | solution.py:77
  377.5 6.0 %round_backward.4 = (f32[2048,256]{1,0:T(8,128)}, bf16[2048,256]{1,0:T(8,128)(2,1)}, bf16[2048,256]{1,0:T(8,128)(2,1)}) custom-call(f32[2048,256]{1,0:T(8,128)} %get-tuple-element.132.grad_ref, f32[4096,128]{1,0:T(8,128)} %get-tuple-element.136.own_ref, bf16[4096,128]{1,0:T(8,128)(2,1)} %copy-done.19, bf16[4096,128]{1,0:T(8,128)(2,1)} %collective-permute-done.26.last_ref, ...), custom_call_target="tpu_custom_call" | custom-call | bytes 21000000 | tf_op jit(solution)/shard_map/round_backward/pallas_call | solution.py:571
  383.5 24.1 %edges_backward.5 = (bf16[2048,256]{1,0:T(8,128)(2,1)}, bf16[2048,256]{1,0:T(8,128)(2,1)}, bf16[4096,128]{1,0:T(8,128)(2,1)}, f32[4096,128]{1,0:T(8,128)}, bf16[4096,128]{1,0:T(8,128)(2,1)}) custom-call(s32[12288]{0:T(1024)} %broadcast_select_fusion.refs_0_.index_ref, f32[2048,256]{1,0:T(8,128)} %get-tuple-element.141.grad_ref, ...), custom_call_target="tpu_custom_call" | custom-call | bytes 75000000 | tf_op jit(solution)/shard_map/edges_backward/pallas_call | solution.py:511
  407.7 3.8 collective-permute-start.28
  411.5 2.6 fusion.108.refs_6_
  419.7 6.8 %collective-permute-done.27.first_ref = bf16[4096,128]{1,0:T(8,128)(2,1)S(1)} collective-permute-done((bf16[4096,128]{1,0:T(8,128)(2,1)}, bf16[4096,128]{1,0:T(8,128)(2,1)S(1)}, u32[]{:S(2)}, u32[]{:S(2)}) %collective-permute-start.27) | collective-permute-done | bytes 1048608 | tf_op jit(solution)/shard_map/ppermute | solution.py:77
  427.5 5.9 %round_backward.5 = (f32[2048,256]{1,0:T(8,128)}, bf16[2048,256]{1,0:T(8,128)(2,1)}, bf16[2048,256]{1,0:T(8,128)(2,1)}) custom-call(f32[2048,256]{1,0:T(8,128)} %get-tuple-element.141.grad_ref, f32[4096,128]{1,0:T(8,128)} %get-tuple-element.145.own_ref, bf16[4096,128]{1,0:T(8,128)(2,1)} %copy-done.20, bf16[4096,128]{1,0:T(8,128)(2,1)} %collective-permute-done.28.last_ref, ...), custom_call_target="tpu_custom_call" | custom-call | bytes 21000000 | tf_op jit(solution)/shard_map/round_backward/pallas_call | solution.py:571
  436.3 6.9 %encode_backward.1 = (f32[128,256]{1,0:T(8,128)}, f32[256,256]{1,0:T(8,128)}, f32[2,256]{1,0:T(2,128)}) custom-call(f32[2048,256]{1,0:T(8,128)} %get-tuple-element.150.grad_ref, bf16[2048,256]{1,0:T(8,128)(2,1)} %get-tuple-element.151.gathered_ref, bf16[1024,128]{1,0:T(8,128)(2,1)} %bitcast.174, s32[1024,1]{1,0:T(8,128)} %get-tuple-element.216.ids_ref, ...), custom_call_target="tpu_custom_call" | custom-call | bytes 21000000 | tf_op jit(solution)/shard_map/encode_backward/pallas_call | solution.py:662
  444.4 5.2 %collect_rows.1 = (f32[16,144,256]{2,1,0:T(8,128)}, bf16[16,144,256]{2,1,0:T(8,128)(2,1)}) custom-call(s32[1]{0:T(128)} %bitcast.12.place_ref, f32[128,256]{1,0:T(8,128)} %get-tuple-element.156.refs_0_, f32[256,256]{1,0:T(8,128)} %get-tuple-element.157.refs_1_, f32[256,256]{1,0:T(8,128)} %fusion.107.refs_2_, f32[78,256]{1,0:T(8,128)} %reshape.160.refs_3_, ...), custom_call_target="tpu_custom_call" | custom-call | bytes 15000000 | tf_op jit(solution)/shard_map/collect_rows/pallas_call | solution.py:229
  449.7 3.0 collective-permute-done.31
  458.9 6.1 %collective-permute-done.34 = bf16[2,2,2,72,256]{4,3,2,1,0:T(8,128)(2,1)} collective-permute-done((bf16[2,2,2,72,256]{4,3,2,1,0:T(8,128)(2,1)}, bf16[2,2,2,72,256]{4,3,2,1,0:T(8,128)(2,1)}, u32[]{:S(2)}, u32[]{:S(2)}) %collective-permute-start.34) | collective-permute-done | bytes 294944 | tf_op jit(solution)/shard_map/ppermute | solution.py:94
  468.1 3.1 collective-permute-done.35
  476.4 6.8 %collective-permute-start.39 = (bf16[72,256]{1,0:T(8,128)(2,1)S(1)}, bf16[72,256]{1,0:T(8,128)(2,1)S(1)}, u32[]{:S(2)}, u32[]{:S(2)}) collective-permute-start(bf16[72,256]{1,0:T(8,128)(2,1)S(1)} %fusion.63), channel_id=1, source_target_pairs={{0,8},{1,9},{2,10},{3,11},{4,12},{5,13},{6,14},{7,15},{8,0},{9,1},... | collective-permute-start | bytes 110600 | tf_op jit(solution)/shard_map/ppermute | solution.py:94
  485.5 2.7 collective-permute-done.37
  491.1 3.4 collective-permute-done.41
  498.1 2.9 collective-permute-start.44
  (315 shorter events, 116.6 us)
Async XLA Ops:
  5.8 9.6 %collective-permute-start.3 = (bf16[1,72,256]{2,1,0:T(8,128)(2,1)S(1)}, bf16[1,72,256]{2,1,0:T(8,128)(2,1)S(1)}, u32[]{:S(2)}, u32[]{:S(2)}) collective-permute-start(bf16[1,72,256]{2,1,0:T(8,128)(2,1)S(1)} %get-tuple-element.232), channel_id=1, source_target_pairs={{0,8},{1,9},{2,10},{3,11},{4,12},{5,13},{6,14},{7,15},{8,0},{9,1},... | collective-permute-start | bytes 110600 | tf_op jit(solution)/shard_map/ppermute | solution.py:94
  9.9 7.5 %collective-permute-start = (bf16[1,72,256]{2,1,0:T(8,128)(2,1)S(1)}, bf16[1,72,256]{2,1,0:T(8,128)(2,1)S(1)}, u32[]{:S(2)}, u32[]{:S(2)}) collective-permute-start(bf16[1,72,256]{2,1,0:T(8,128)(2,1)S(1)} %get-tuple-element.233), channel_id=1, source_target_pairs={{0,8},{1,9},{2,10},{3,11},{4,12},{5,13},{6,14},{7,15},{8,0},{9,1},... | collective-permute-start | bytes 110600 | tf_op jit(solution)/shard_map/ppermute | solution.py:94
  15.4 5.2 %collective-permute-start.4 = (bf16[2,72,256]{2,1,0:T(8,128)(2,1)S(1)}, bf16[2,72,256]{2,1,0:T(8,128)(2,1)S(1)}, u32[]{:S(2)}, u32[]{:S(2)}) collective-permute-start(bf16[2,72,256]{2,1,0:T(8,128)(2,1)S(1)} %pad_maximum_fusion.7), channel_id=1, source_target_pairs={{0,4},{1,5},{2,6},{3,7},{4,0},{5,1},{6,2},{7,3},{8,12},{9,13},{10,... | collective-permute-start | bytes 221192 | tf_op jit(solution)/shard_map/ppermute | solution.py:94
  17.4 4.8 collective-permute-start.1
  20.6 5.2 %collective-permute-start.5 = (bf16[4,72,256]{2,1,0:T(8,128)(2,1)S(1)}, bf16[4,72,256]{2,1,0:T(8,128)(2,1)S(1)}, u32[]{:S(2)}, u32[]{:S(2)}) collective-permute-start(bf16[4,72,256]{2,1,0:T(8,128)(2,1)S(1)} %pad_maximum_fusion.5), channel_id=1, source_target_pairs={{0,1},{1,0},{2,3},{3,2},{4,5},{5,4},{6,7},{7,6},{8,9},{9,8},{10,11... | collective-permute-start | bytes 442376 | tf_op jit(solution)/shard_map/ppermute | solution.py:94
  22.2 5.2 %collective-permute-start.2 = (bf16[4,72,256]{2,1,0:T(8,128)(2,1)S(1)}, bf16[4,72,256]{2,1,0:T(8,128)(2,1)S(1)}, u32[]{:S(2)}, u32[]{:S(2)}) collective-permute-start(bf16[4,72,256]{2,1,0:T(8,128)(2,1)S(1)} %pad_maximum_fusion.4), channel_id=1, source_target_pairs={{0,2},{1,3},{2,0},{3,1},{4,6},{5,7},{6,4},{7,5},{8,10},{9,11},{10,... | collective-permute-start | bytes 442376 | tf_op jit(solution)/shard_map/ppermute | solution.py:94
  27.5 11.4 %collective-permute-start.8 = (bf16[8,72,256]{2,1,0:T(8,128)(2,1)S(1)}, bf16[8,72,256]{2,1,0:T(8,128)(2,1)S(1)}, u32[]{:S(2)}, u32[]{:S(2)}) collective-permute-start(bf16[8,72,256]{2,1,0:T(8,128)(2,1)S(1)} %pad_maximum_fusion.2), channel_id=1, source_target_pairs={{0,2},{1,3},{2,0},{3,1},{4,6},{5,7},{6,4},{7,5},{8,10},{9,11},{10,... | collective-permute-start | bytes 884744 | tf_op jit(solution)/shard_map/ppermute | solution.py:94
  29.1 35.2 %collective-permute-start.14 = (s32[360]{0:T(512)S(1)}, s32[360]{0:T(512)}, u32[]{:S(2)}, u32[]{:S(2)}) collective-permute-start(s32[360]{0:T(512)S(1)} %slice.227), channel_id=1, source_target_pairs={{0,1},{1,2},{2,3},{3,4},{4,5},{5,6},{6,7},{7,8},{8,9},{9,10},{10,1... | collective-permute-start | bytes 4328 | tf_op jit(solution)/shard_map/ppermute | solution.py:49
  32.6 7.7 %collective-permute-start.7 = (bf16[8,72,256]{2,1,0:T(8,128)(2,1)S(1)}, bf16[8,72,256]{2,1,0:T(8,128)(2,1)S(1)}, u32[]{:S(2)}, u32[]{:S(2)}) collective-permute-start(bf16[8,72,256]{2,1,0:T(8,128)(2,1)S(1)} %pad_maximum_fusion.1), channel_id=1, source_target_pairs={{0,1},{1,0},{2,3},{3,2},{4,5},{5,4},{6,7},{7,6},{8,9},{9,8},{10,11... | collective-permute-start | bytes 884744 | tf_op jit(solution)/shard_map/ppermute | solution.py:94
  33.1 14.3 %all-to-all-start = ((bf16[16,64,128]{2,1,0:T(8,128)(2,1)}), bf16[16,64,128]{2,1,0:T(8,128)(2,1)S(1)}, u32[]{:S(2)}, u32[]{:S(2)}) async-start(bf16[16,64,128]{2,1,0:T(8,128)(2,1)} %bitcast.8), calls=%async_computation | async-start | bytes 524288 | tf_op jit(solution)/shard_map/all_to_all | solution.py:718
  38.9 10.4 %collective-permute-start.10 = (bf16[16,72,256]{2,1,0:T(8,128)(2,1)S(1)}, bf16[16,72,256]{2,1,0:T(8,128)(2,1)S(1)}, u32[]{:S(2)}, u32[]{:S(2)}) collective-permute-start(bf16[16,72,256]{2,1,0:T(8,128)(2,1)S(1)} %constant_dynamic-update-slice_fusion.2.refs_1_), channel_id=1, source_target_pairs={{0,16},{16,0},{1,17},{17,1},{2,18},{18,2},{3,19},{19,3},{4,20},{20... | collective-permute-start | bytes 1769480 | tf_op jit(solution)/shard_map/ppermute | solution.py:94
  40.4 8.9 %collective-permute-start.9 = (bf16[16,72,256]{2,1,0:T(8,128)(2,1)S(1)}, bf16[16,72,256]{2,1,0:T(8,128)(2,1)S(1)}, u32[]{:S(2)}, u32[]{:S(2)}) collective-permute-start(bf16[16,72,256]{2,1,0:T(8,128)(2,1)S(1)} %constant_dynamic-update-slice_fusion.refs_0_), channel_id=1, source_target_pairs={{0,16},{16,0},{1,17},{17,1},{2,18},{18,2},{3,19},{19,3},{4,20},{20... | collective-permute-start | bytes 1769480 | tf_op jit(solution)/shard_map/ppermute | solution.py:94
  40.6 29.0 %collective-permute-start.6 = (s32[12288]{0:T(1024)S(1)}, s32[12288]{0:T(1024)}, u32[]{:S(2)}, u32[]{:S(2)}) collective-permute-start(s32[12288]{0:T(1024)S(1)} %mul.208), channel_id=1, source_target_pairs={{2,3},{3,2},{4,6},{5,4},{6,5},{8,11},{10,8},{11,10},{12,14},{13,15... | collective-permute-start | bytes 147464 | tf_op jit(solution)/shard_map/ppermute | solution.py:741
  60.3 29.6 %collective-permute-start.15 = (bf16[4096,128]{1,0:T(8,128)(2,1)}, bf16[4096,128]{1,0:T(8,128)(2,1)S(1)}, u32[]{:S(2)}, u32[]{:S(2)}) collective-permute-start(bf16[4096,128]{1,0:T(8,128)(2,1)} %get-tuple-element.104.refs_3_), channel_id=1, source_target_pairs={{1,0},{3,1},{2,3},{6,2},{4,6},{5,4},{7,5},{11,7},{9,11},{8,9},{10,... | collective-permute-start | bytes 3145736 | tf_op jit(solution)/shard_map/ppermute | solution.py:77
  62.1 27.8 %collective-permute-start.11 = (bf16[4096,128]{1,0:T(8,128)(2,1)}, bf16[4096,128]{1,0:T(8,128)(2,1)}, u32[]{:S(2)}, u32[]{:S(2)}) collective-permute-start(bf16[4096,128]{1,0:T(8,128)(2,1)} %get-tuple-element.104.refs_3_), channel_id=1, source_target_pairs={{0,1},{1,3},{3,2},{2,6},{6,4},{4,5},{5,7},{7,11},{11,9},{9,8},{8,1... | collective-permute-start | bytes 3145736 | tf_op jit(solution)/shard_map/ppermute | solution.py:77
  62.4 20.1 %collective-permute-start.13 = (bf16[78,360]{1,0:T(8,128)(2,1)S(1)}, bf16[78,360]{1,0:T(8,128)(2,1)S(1)}, u32[]{:S(2)}, u32[]{:S(2)}) collective-permute-start(bf16[78,360]{1,0:T(8,128)(2,1)S(1)} %get-tuple-element.230), channel_id=1, source_target_pairs={{1,0},{2,1},{3,2},{4,3},{5,4},{6,5},{7,6},{8,7},{9,8},{10,9},{11,1... | collective-permute-start | bytes 168488 | tf_op jit(solution)/shard_map/ppermute | solution.py:49
  64.3 20.0 %collective-permute-start.12 = (bf16[78,360]{1,0:T(8,128)(2,1)S(1)}, bf16[78,360]{1,0:T(8,128)(2,1)S(1)}, u32[]{:S(2)}, u32[]{:S(2)}) collective-permute-start(bf16[78,360]{1,0:T(8,128)(2,1)S(1)} %get-tuple-element.231), channel_id=1, source_target_pairs={{0,1},{1,2},{2,3},{3,4},{4,5},{5,6},{6,7},{7,8},{8,9},{9,10},{10,1... | collective-permute-start | bytes 168488 | tf_op jit(solution)/shard_map/ppermute | solution.py:49
  115.7 23.1 %collective-permute-start.17 = (bf16[4096,128]{1,0:T(8,128)(2,1)}, bf16[4096,128]{1,0:T(8,128)(2,1)S(1)}, u32[]{:S(2)}, u32[]{:S(2)}) collective-permute-start(bf16[4096,128]{1,0:T(8,128)(2,1)} %get-tuple-element.109.refs_3_), channel_id=1, source_target_pairs={{1,0},{3,1},{2,3},{6,2},{4,6},{5,4},{7,5},{11,7},{9,11},{8,9},{10,... | collective-permute-start | bytes 3145736 | tf_op jit(solution)/shard_map/ppermute | solution.py:77
  119.4 23.3 %collective-permute-start.16 = (bf16[4096,128]{1,0:T(8,128)(2,1)}, bf16[4096,128]{1,0:T(8,128)(2,1)S(1)}, u32[]{:S(2)}, u32[]{:S(2)}) collective-permute-start(bf16[4096,128]{1,0:T(8,128)(2,1)} %get-tuple-element.109.refs_3_), channel_id=1, source_target_pairs={{0,1},{1,3},{3,2},{2,6},{6,4},{4,5},{5,7},{7,11},{11,9},{9,8},{8,1... | collective-permute-start | bytes 3145736 | tf_op jit(solution)/shard_map/ppermute | solution.py:77
  168.8 26.2 %collective-permute-start.19 = (bf16[4096,128]{1,0:T(8,128)(2,1)}, bf16[4096,128]{1,0:T(8,128)(2,1)S(1)}, u32[]{:S(2)}, u32[]{:S(2)}) collective-permute-start(bf16[4096,128]{1,0:T(8,128)(2,1)} %get-tuple-element.111.refs_3_), channel_id=1, source_target_pairs={{1,0},{3,1},{2,3},{6,2},{4,6},{5,4},{7,5},{11,7},{9,11},{8,9},{10,... | collective-permute-start | bytes 3145736 | tf_op jit(solution)/shard_map/ppermute | solution.py:77
  169.5 25.6 %collective-permute-start.18 = (bf16[4096,128]{1,0:T(8,128)(2,1)}, bf16[4096,128]{1,0:T(8,128)(2,1)S(1)}, u32[]{:S(2)}, u32[]{:S(2)}) collective-permute-start(bf16[4096,128]{1,0:T(8,128)(2,1)} %get-tuple-element.111.refs_3_), channel_id=1, source_target_pairs={{0,1},{1,3},{3,2},{2,6},{6,4},{4,5},{5,7},{7,11},{11,9},{9,8},{8,1... | collective-permute-start | bytes 3145736 | tf_op jit(solution)/shard_map/ppermute | solution.py:77
  226.1 13.5 %all-to-all-start.1 = ((bf16[16,64,128]{2,1,0:T(8,128)(2,1)}), bf16[16,64,128]{2,1,0:T(8,128)(2,1)S(1)}, u32[]{:S(2)}, u32[]{:S(2)}) async-start(bf16[16,64,128]{2,1,0:T(8,128)(2,1)} %bitcast.20), calls=%async_computation.1 | async-start | bytes 524288 | tf_op jit(solution)/shard_map/all_to_all | solution.py:718
  240.2 9.5 %collective-permute-start.20 = (bf16[78,360]{1,0:T(8,128)(2,1)S(1)}, bf16[78,360]{1,0:T(8,128)(2,1)S(1)}, u32[]{:S(2)}, u32[]{:S(2)}) collective-permute-start(bf16[78,360]{1,0:T(8,128)(2,1)S(1)} %get-tuple-element.228), channel_id=1, source_target_pairs={{0,1},{1,2},{2,3},{3,4},{4,5},{5,6},{6,7},{7,8},{8,9},{9,10},{10,1... | collective-permute-start | bytes 168488 | tf_op jit(solution)/shard_map/ppermute | solution.py:49
  243.5 6.1 %collective-permute-start.21 = (bf16[78,360]{1,0:T(8,128)(2,1)S(1)}, bf16[78,360]{1,0:T(8,128)(2,1)S(1)}, u32[]{:S(2)}, u32[]{:S(2)}) collective-permute-start(bf16[78,360]{1,0:T(8,128)(2,1)S(1)} %get-tuple-element.229), channel_id=1, source_target_pairs={{1,0},{2,1},{3,2},{4,3},{5,4},{6,5},{7,6},{8,7},{9,8},{10,9},{11,1... | collective-permute-start | bytes 168488 | tf_op jit(solution)/shard_map/ppermute | solution.py:49
  272.9 31.8 %collective-permute-start.22 = (bf16[2048,256]{1,0:T(8,128)(2,1)S(1)}, bf16[2048,256]{1,0:T(8,128)(2,1)}, u32[]{:S(2)}, u32[]{:S(2)}) collective-permute-start(bf16[2048,256]{1,0:T(8,128)(2,1)S(1)} %convert_element_type.196), channel_id=1, source_target_pairs={{3,2},{2,3},{6,4},{4,5},{5,6},{11,8},{8,10},{10,11},{14,12},{15,13... | collective-permute-start | bytes 3145736 | tf_op jit(solution)/shard_map/ppermute | solution.py:744
  304.7 20.7 %collective-permute-start.23 = (bf16[4096,128]{1,0:T(8,128)(2,1)S(1)}, bf16[4096,128]{1,0:T(8,128)(2,1)S(1)}, u32[]{:S(2)}, u32[]{:S(2)}) collective-permute-start(bf16[4096,128]{1,0:T(8,128)(2,1)S(1)} %copy-done.62), channel_id=1, source_target_pairs={{0,1},{1,3},{3,2},{2,6},{6,4},{4,5},{5,7},{7,11},{11,9},{9,8},{8,1... | collective-permute-start | bytes 3145736 | tf_op jit(solution)/shard_map/ppermute | solution.py:77
  306.3 19.1 %collective-permute-start.24 = (bf16[4096,128]{1,0:T(8,128)(2,1)S(1)}, bf16[4096,128]{1,0:T(8,128)(2,1)}, u32[]{:S(2)}, u32[]{:S(2)}) collective-permute-start(bf16[4096,128]{1,0:T(8,128)(2,1)S(1)} %copy-done.61), channel_id=1, source_target_pairs={{1,0},{3,1},{2,3},{6,2},{4,6},{5,4},{7,5},{11,7},{9,11},{8,9},{10,... | collective-permute-start | bytes 3145736 | tf_op jit(solution)/shard_map/ppermute | solution.py:77
  356.6 19.9 %collective-permute-start.25 = (bf16[4096,128]{1,0:T(8,128)(2,1)}, bf16[4096,128]{1,0:T(8,128)(2,1)S(1)}, u32[]{:S(2)}, u32[]{:S(2)}) collective-permute-start(bf16[4096,128]{1,0:T(8,128)(2,1)} %get-tuple-element.137), channel_id=1, source_target_pairs={{0,1},{1,3},{3,2},{2,6},{6,4},{4,5},{5,7},{7,11},{11,9},{9,8},{8,1... | collective-permute-start | bytes 3145736 | tf_op jit(solution)/shard_map/ppermute | solution.py:77
  356.6 19.8 %collective-permute-start.26 = (bf16[4096,128]{1,0:T(8,128)(2,1)}, bf16[4096,128]{1,0:T(8,128)(2,1)}, u32[]{:S(2)}, u32[]{:S(2)}) collective-permute-start(bf16[4096,128]{1,0:T(8,128)(2,1)} %get-tuple-element.138), channel_id=1, source_target_pairs={{1,0},{3,1},{2,3},{6,2},{4,6},{5,4},{7,5},{11,7},{9,11},{8,9},{10,... | collective-permute-start | bytes 3145736 | tf_op jit(solution)/shard_map/ppermute | solution.py:77
  407.6 18.9 %collective-permute-start.27 = (bf16[4096,128]{1,0:T(8,128)(2,1)}, bf16[4096,128]{1,0:T(8,128)(2,1)S(1)}, u32[]{:S(2)}, u32[]{:S(2)}) collective-permute-start(bf16[4096,128]{1,0:T(8,128)(2,1)} %get-tuple-element.146), channel_id=1, source_target_pairs={{0,1},{1,3},{3,2},{2,6},{6,4},{4,5},{5,7},{7,11},{11,9},{9,8},{8,1... | collective-permute-start | bytes 3145736 | tf_op jit(solution)/shard_map/ppermute | solution.py:77
  407.7 18.9 %collective-permute-start.28 = (bf16[4096,128]{1,0:T(8,128)(2,1)}, bf16[4096,128]{1,0:T(8,128)(2,1)}, u32[]{:S(2)}, u32[]{:S(2)}) collective-permute-start(bf16[4096,128]{1,0:T(8,128)(2,1)} %get-tuple-element.147), channel_id=1, source_target_pairs={{1,0},{3,1},{2,3},{6,2},{4,6},{5,4},{7,5},{11,7},{9,11},{8,9},{10,... | collective-permute-start | bytes 3145736 | tf_op jit(solution)/shard_map/ppermute | solution.py:77
  434.5 15.1 %collective-permute-start.30 = (bf16[512,256]{1,0:T(8,128)(2,1)S(1)}, bf16[512,256]{1,0:T(8,128)(2,1)S(1)}, u32[]{:S(2)}, u32[]{:S(2)}) collective-permute-start(bf16[512,256]{1,0:T(8,128)(2,1)S(1)} %get-tuple-element.225), channel_id=1, source_target_pairs={{3,2},{2,3},{6,4},{4,5},{5,6},{11,8},{8,10},{10,11},{14,12},{15,13... | collective-permute-start | bytes 786440 | tf_op jit(solution)/shard_map/ppermute | solution.py:744
  435.3 9.1 %collective-permute-start.29 = (bf16[512,256]{1,0:T(8,128)(2,1)S(1)}, bf16[512,256]{1,0:T(8,128)(2,1)S(1)}, u32[]{:S(2)}, u32[]{:S(2)}) collective-permute-start(bf16[512,256]{1,0:T(8,128)(2,1)S(1)} %get-tuple-element.226), channel_id=1, source_target_pairs={{3,2},{2,3},{6,4},{4,5},{5,6},{11,8},{8,10},{10,11},{14,12},{15,13... | collective-permute-start | bytes 786440 | tf_op jit(solution)/shard_map/ppermute | solution.py:744
  449.6 3.1 collective-permute-start.31
  455.6 9.4 %collective-permute-start.34 = (bf16[2,2,2,72,256]{4,3,2,1,0:T(8,128)(2,1)}, bf16[2,2,2,72,256]{4,3,2,1,0:T(8,128)(2,1)}, u32[]{:S(2)}, u32[]{:S(2)}) collective-permute-start(bf16[2,2,2,72,256]{4,3,2,1,0:T(8,128)(2,1)} %fusion.21), channel_id=1, source_target_pairs={{0,2},{1,3},{2,0},{3,1},{4,6},{5,7},{6,4},{7,5},{8,10},{9,11},{10,... | collective-permute-start | bytes 884744 | tf_op jit(solution)/shard_map/ppermute | solution.py:94
  457.5 8.8 %collective-permute-start.32 = (bf16[2,2,2,72,256]{4,3,0,1,2:T(8,128)(2,1)S(1)}, bf16[2,2,2,72,256]{4,3,0,1,2:T(8,128)(2,1)S(1)}, u32[]{:S(2)}, u32[]{:S(2)}) collective-permute-start(bf16[2,2,2,72,256]{4,3,0,1,2:T(8,128)(2,1)S(1)} %fusion.22), channel_id=1, source_target_pairs={{0,1},{1,0},{2,3},{3,2},{4,5},{5,4},{6,7},{7,6},{8,9},{9,8},{10,11... | collective-permute-start | bytes 884744 | tf_op jit(solution)/shard_map/ppermute | solution.py:94
  466.0 5.2 %collective-permute-start.35 = (bf16[2,2,72,256]{3,2,1,0:T(8,128)(2,1)S(1)}, bf16[2,2,72,256]{3,2,1,0:T(8,128)(2,1)S(1)}, u32[]{:S(2)}, u32[]{:S(2)}) collective-permute-start(bf16[2,2,72,256]{3,2,1,0:T(8,128)(2,1)S(1)} %fusion.50), channel_id=1, source_target_pairs={{0,1},{1,0},{2,3},{3,2},{4,5},{5,4},{6,7},{7,6},{8,9},{9,8},{10,11... | collective-permute-start | bytes 442376 | tf_op jit(solution)/shard_map/ppermute | solution.py:94
  466.5 5.2 %collective-permute-start.33 = (bf16[2,2,72,256]{3,2,0,1:T(8,128)(2,1)S(1)}, bf16[2,2,72,256]{3,2,0,1:T(8,128)(2,1)S(1)}, u32[]{:S(2)}, u32[]{:S(2)}) collective-permute-start(bf16[2,2,72,256]{3,2,0,1:T(8,128)(2,1)S(1)} %fusion.49), channel_id=1, source_target_pairs={{0,2},{1,3},{2,0},{3,1},{4,6},{5,7},{6,4},{7,5},{8,10},{9,11},{10,... | collective-permute-start | bytes 442376 | tf_op jit(solution)/shard_map/ppermute | solution.py:94
  471.7 4.6 collective-permute-start.38
  474.0 9.2 %collective-permute-start.36 = (bf16[2,72,256]{2,1,0:T(8,128)(2,1)S(1)}, bf16[2,72,256]{2,1,0:T(8,128)(2,1)S(1)}, u32[]{:S(2)}, u32[]{:S(2)}) collective-permute-start(bf16[2,72,256]{2,1,0:T(8,128)(2,1)S(1)} %fusion.53), channel_id=1, source_target_pairs={{0,4},{1,5},{2,6},{3,7},{4,0},{5,1},{6,2},{7,3},{8,12},{9,13},{10,... | collective-permute-start | bytes 221192 | tf_op jit(solution)/shard_map/ppermute | solution.py:94
  474.1 24.0 %collective-permute-start.43 = (bf16[1024,256]{1,0:T(8,128)(2,1)S(1)}, bf16[1024,256]{1,0:T(8,128)(2,1)S(1)}, u32[]{:S(2)}, u32[]{:S(2)}) collective-permute-start(bf16[1024,256]{1,0:T(8,128)(2,1)S(1)} %slice.267), channel_id=1, source_target_pairs={{3,2},{2,3},{6,4},{4,5},{5,6},{11,8},{8,10},{10,11},{14,12},{15,13... | collective-permute-start | bytes 1572872 | tf_op jit(solution)/shard_map/ppermute | solution.py:744
  476.4 9.1 %collective-permute-start.39 = (bf16[72,256]{1,0:T(8,128)(2,1)S(1)}, bf16[72,256]{1,0:T(8,128)(2,1)S(1)}, u32[]{:S(2)}, u32[]{:S(2)}) collective-permute-start(bf16[72,256]{1,0:T(8,128)(2,1)S(1)} %fusion.63), channel_id=1, source_target_pairs={{0,8},{1,9},{2,10},{3,11},{4,12},{5,13},{6,14},{7,15},{8,0},{9,1},... | collective-permute-start | bytes 110600 | tf_op jit(solution)/shard_map/ppermute | solution.py:94
  483.2 4.9 collective-permute-start.37
  489.6 1.2 collective-permute-start.40
  490.9 3.6 collective-permute-start.41
  494.5 3.6 collective-permute-start.42
  498.1 4.4 collective-permute-start.44
  502.6 4.6 collective-permute-start.45
  (65 other events, 683.2 us)

commit v8 on v7

--- a/solution.py
+++ b/solution.py
@@ -17,7 +17,7 @@
 STEP = 10
 H = 2048
 ALL = ("dp", "space")
-LIMIT = pltpu.CompilerParams(vmem_limit_bytes=56 * 2**20)
+LIMIT = pltpu.CompilerParams(vmem_limit_bytes=60 * 2**20)
 
 
 def cost(micros):
@@ -102,7 +102,7 @@
     turns = [(axis, bit) for axis in ALL for bit in bits_of(axis)]
     for turn, (axis, bit) in enumerate(turns):
         value = value + swapped(value, axis, bit)
-        if turn == len(turns) - 3:
+        if turn == len(turns) - 2:
             value, arriving = lax.optimization_barrier((value, arriving))
     return value, arriving
 
@@ -282,6 +282,10 @@
     return pl.BlockSpec(shape, lambda *_: (0,) * len(shape))
 
 
+def index_block(tile):
+    return pl.BlockSpec((K, tile), lambda i: (0, i), memory_space=pltpu.SMEM)
+
+
 def round_forward(index, mesh, before, own, after, mats, bias, following):
     blocks = mesh.shape[0]
     tile, chunk = 512, 16
@@ -322,10 +326,8 @@
 
         def fetch(turn):
             for edge in range(K):
-                base = edge * blocks + step * tile + turn * chunk
-                values = [
-                    table[pl.ds(pl.multiple_of(index_ref[base + u], 2), 2), :] for u in range(chunk)
-                ]
+                spots = [index_ref[edge, turn * chunk + u] for u in range(chunk)]
+                values = [table[pl.ds(pl.multiple_of(spot, 2), 2), :] for spot in spots]
                 for u in range(chunk):
                     spot = pl.multiple_of(edge * 2 * tile + turn * high + 2 * u, 2)
                     rows[pl.ds(spot, 2), :] = values[u]
@@ -380,9 +382,9 @@
             weave(wide, inner(new.astype(jnp.bfloat16), next_ref[0], 1, 0))
             sent_ref[...] = wide[...].astype(jnp.bfloat16)
 
-    whole_rows = pl.BlockSpec((tile, D), lambda i, *_: (i, 0))
-    woven = pl.BlockSpec((2 * tile, HALF), lambda i, *_: (i, 0))
-    ins = [whole_rows] + [pl.BlockSpec(memory_space=pl.ANY)] * 3 + [whole(mats.shape), whole(bias.shape)]
+    whole_rows = pl.BlockSpec((tile, D), lambda i: (i, 0))
+    woven = pl.BlockSpec((2 * tile, HALF), lambda i: (i, 0))
+    ins = [index_block(tile), whole_rows] + [pl.BlockSpec(memory_space=pl.ANY)] * 3 + [whole(mats.shape), whole(bias.shape)]
     outs = [whole_rows] * 4 + [pl.BlockSpec((K, 2 * tile, HALF), lambda i, *_: (0, i, 0))]
     shapes = [
         jax.ShapeDtypeStruct((blocks, D), jnp.float32),
@@ -399,8 +401,7 @@
         args.append(following)
     return pl.pallas_call(
         body,
-        grid_spec=pltpu.PrefetchScalarGridSpec(
-            num_scalar_prefetch=1,
+        grid_spec=pl.GridSpec(
             grid=(blocks // tile,),
             in_specs=ins,
             out_specs=outs,
@@ -420,16 +421,19 @@
     )(*args)
 
 
-def edges_backward(index, grad_mesh, back, slopes, turned):
+def edges_backward(index, grad_mesh, back, slopes, mats, carried=()):
     blocks = grad_mesh.shape[0]
     tile, chunk = 512, 16
     steps, turns, high = blocks // tile, tile // chunk, 2 * chunk
     reach = 2 * (blocks + 2 * H)
 
-    def body(
-        index_ref, grad_ref, back_ref, slope_ref, turned_ref,
-        guin_ref, low_ref, before_ref, own_ref, after_ref, wide, wider, flows, *tables,
-    ):
+    def body(*refs):
+        index_ref, grad_ref, back_ref, slope_ref, mats_ref = refs[:5]
+        rest = refs[5:]
+        if carried:
+            past, rest = rest[:6], rest[6:]
+            (new_ref, out_ref, sent_ref), rest = rest[:3], rest[3:]
+        guin_ref, low_ref, before_ref, own_ref, after_ref, wide, wider, flows, *tables = rest
         step = pl.program_id(0)
 
         @pl.when(step == 0)
@@ -441,10 +445,16 @@
                         (256, HALF), jnp.float32
                     )
 
-        grad_out = grad_ref[...].astype(jnp.bfloat16)
-        grad_uin = (inner(grad_out, turned_ref[4], 1, 0) * back_ref[...]).astype(jnp.bfloat16)
+        if carried:
+            new = ended(grad_ref, *past, sent_ref, wide)
+            new_ref[...] = new
+            grad_out = new.astype(jnp.bfloat16)
+            out_ref[...] = grad_out
+        else:
+            grad_out = grad_ref[...].astype(jnp.bfloat16)
+        grad_uin = (inner(grad_out, mats_ref[4], 1, 1) * back_ref[...]).astype(jnp.bfloat16)
         guin_ref[...] = grad_uin
-        weave(wide, inner(grad_uin, turned_ref[2], 1, 0) * (1.0 / K))
+        weave(wide, inner(grad_uin, mats_ref[2], 1, 1) * (1.0 / K))
 
         def dense(turn):
             at = pl.multiple_of(turn * high, high)
@@ -466,8 +476,7 @@
             for u in range(chunk):
                 spots, sums = [], []
                 for edge in range(K):
-                    base = edge * blocks + step * tile + turn * chunk
-                    spots.append(pl.multiple_of(index_ref[base + u], 2))
+                    spots.append(pl.multiple_of(index_ref[edge, turn * chunk + u], 2))
                 for edge in range(K):
                     spot = pl.multiple_of(edge * 2 * tile + turn * high + 2 * u, 2)
                     sums.append(tables[edge][pl.ds(spots[edge], 2), :] + flows[pl.ds(spot, 2), :])
@@ -507,18 +516,20 @@
                 at = pl.multiple_of(i * 256, 256)
                 own_ref[pl.ds(at, 256), :] = summed(pl.multiple_of(2 * H + at, 256))
 
-    rows = pl.BlockSpec((tile, D), lambda i, *_: (i, 0))
+    rows = pl.BlockSpec((tile, D), lambda i: (i, 0))
+    woven = pl.BlockSpec((2 * tile, HALF), lambda i: (i, 0))
+    low = jax.ShapeDtypeStruct((blocks, D), jnp.bfloat16)
     return pl.pallas_call(
         body,
-        grid_spec=pltpu.PrefetchScalarGridSpec(
-            num_scalar_prefetch=1,
+        grid_spec=pl.GridSpec(
             grid=(steps,),
             in_specs=[
-                rows, rows,
-                pl.BlockSpec((K, 2 * tile, HALF), lambda i, *_: (0, i, 0)),
-                whole(turned.shape),
-            ],
-            out_specs=[
+                index_block(tile), rows, rows,
+                pl.BlockSpec((K, 2 * tile, HALF), lambda i: (0, i, 0)),
+                whole(mats.shape),
+            ]
+            + ([woven] * 3 + [rows] * 2 + [whole(mats.shape)] if carried else []),
+            out_specs=([rows] * 3 if carried else []) + [
                 rows, rows,
                 whole((2 * H, HALF)), whole((2 * blocks, HALF)), whole((2 * H, HALF)),
             ],
@@ -529,60 +540,62 @@
             ]
             + [pltpu.VMEM((reach, HALF), jnp.float32)] * K,
         ),
-        out_shape=[
-            jax.ShapeDtypeStruct((blocks, D), jnp.bfloat16),
-            jax.ShapeDtypeStruct((blocks, D), jnp.bfloat16),
+        out_shape=(
+            [jax.ShapeDtypeStruct((blocks, D), jnp.float32), low, low] if carried else []
+        ) + [
+            low,
+            low,
             jax.ShapeDtypeStruct((2 * H, HALF), jnp.bfloat16),
             jax.ShapeDtypeStruct((2 * blocks, HALF), jnp.float32),
             jax.ShapeDtypeStruct((2 * H, HALF), jnp.bfloat16),
         ],
         compiler_params=LIMIT,
-        cost_estimate=cost(25),
+        cost_estimate=cost(28 if carried else 25),
         name="edges_backward",
-    )(index, grad_mesh, back, slopes, turned)
-
-
-def round_backward(grad_mesh, own, first, last, grad_uin, dest_low, turned):
+    )(index, grad_mesh, back, slopes, mats, *carried)
+
+
+def ended(grad_ref, own_ref, first_ref, last_ref, guin_ref, dest_ref, mats_ref, sent_ref, wide):
+    wide[...] = (
+        own_ref[...] + first_ref[...].astype(jnp.float32) + last_ref[...].astype(jnp.float32)
+    )
+    one, two = unweave(wide)
+    one, two = one.astype(jnp.bfloat16), two.astype(jnp.bfloat16)
+    sent_ref[:, :HALF] = one
+    sent_ref[:, HALF:] = two
+    return (
+        grad_ref[...]
+        + inner(guin_ref[...], mats_ref[3], 1, 1)
+        + inner(dest_ref[...], mats_ref[1], 1, 1)
+        + inner(one, mats_ref[0, :, :HALF], 1, 1)
+        + inner(two, mats_ref[0, :, HALF:], 1, 1)
+    )
+
+
+def round_backward(grad_mesh, own, first, last, grad_uin, dest_low, mats):
     blocks = grad_mesh.shape[0]
     tile = 1024
 
-    def body(
-        grad_ref, own_ref, first_ref, last_ref, guin_ref, dest_ref, turned_ref, new_ref, sent_ref, out_ref, wide
-    ):
-        wide[...] = (
-            own_ref[...] + first_ref[...].astype(jnp.float32) + last_ref[...].astype(jnp.float32)
-        )
-        one, two = unweave(wide)
-        one, two = one.astype(jnp.bfloat16), two.astype(jnp.bfloat16)
-        sent_ref[:, :HALF] = one
-        sent_ref[:, HALF:] = two
-        new = (
-            grad_ref[...]
-            + inner(guin_ref[...], turned_ref[3], 1, 0)
-            + inner(dest_ref[...], turned_ref[1], 1, 0)
-            + inner(one, turned_ref[0, :HALF, :], 1, 0)
-            + inner(two, turned_ref[0, HALF:, :], 1, 0)
-        )
+    def body(*refs):
+        new_ref, out_ref, sent_ref, wide = refs[-4:]
+        new = ended(*refs[:-4], sent_ref, wide)
         new_ref[...] = new
         out_ref[...] = new.astype(jnp.bfloat16)
 
     rows = pl.BlockSpec((tile, D), lambda i: (i, 0))
     woven = pl.BlockSpec((2 * tile, HALF), lambda i: (i, 0))
+    low = jax.ShapeDtypeStruct((blocks, D), jnp.bfloat16)
     return pl.pallas_call(
         body,
         grid=(blocks // tile,),
-        in_specs=[rows, woven, woven, woven, rows, rows, whole(turned.shape)],
+        in_specs=[rows, woven, woven, woven, rows, rows, whole(mats.shape)],
         out_specs=[rows, rows, rows],
-        out_shape=[
-            jax.ShapeDtypeStruct((blocks, D), jnp.float32),
-            jax.ShapeDtypeStruct((blocks, D), jnp.bfloat16),
-            jax.ShapeDtypeStruct((blocks, D), jnp.bfloat16),
-        ],
+        out_shape=[jax.ShapeDtypeStruct((blocks, D), jnp.float32), low, low],
         scratch_shapes=[pltpu.VMEM((2 * tile, HALF), jnp.float32)],
         compiler_params=LIMIT,
         cost_estimate=cost(7),
         name="round_backward",
-    )(grad_mesh, own, first, last, grad_uin, dest_low, turned)
+    )(grad_mesh, own, first, last, grad_uin, dest_low, mats)
 
 
 def encode_rows(arrived, ids, w_in, w_node, biases, source):
@@ -735,7 +748,10 @@
     mesh, gathered, sent = encode_rows(
         arrived, ids.reshape(1, -1), w_in, w_node, biases, w_round[0]
     )
-    index = 2 * ((neighbours - band * blocks + H) % (blocks * bands)).T.reshape(-1)
+    sent, partner, neighbours, counted = lax.optimization_barrier(
+        (sent, partner, neighbours, counted)
+    )
+    index = 2 * ((neighbours - band * blocks + H) % (blocks * bands)).T
     moved = [(n, place) for n, place in enumerate(walk) if n != place]
     stays = jnp.asarray([n == place for n, place in enumerate(walk)])[band]
     index = jnp.where(stays, index, lax.ppermute(index, "space", moved))
@@ -763,9 +779,8 @@
     for layer in range(ROUNDS):
         before, after = halo(walk, sent[2 * (blocks - H) :], sent[: 2 * H])
         if layer == 0:
-            turned = [jnp.swapaxes(mats, 1, 2) for mats in w_round]
-            before, turned, valid_around, partner_by = lax.optimization_barrier(
-                (before, turned, valid_around, partner_by)
+            before, valid_around, partner_by = lax.optimization_barrier(
+                (before, valid_around, partner_by)
             )
         following = w_round[layer + 1] if layer + 1 < ROUNDS else None
         new, back, update, agg, slopes, *rest = round_forward(
@@ -824,51 +839,46 @@
     leaving = grad_mesh.astype(jnp.bfloat16)
     mats_grads = [None] * (5 * ROUNDS)
     bias_grads = [None] * (2 * ROUNDS)
+    carried = ()
     for layer in reversed(range(ROUNDS)):
         old, back, update, agg, slopes = kept[layer]
-        grad_uin, dest_low, to_before, own, to_after = edges_backward(
-            index, grad_mesh, back, slopes, turned[layer]
+        *ends, grad_uin, dest_low, to_before, own, to_after = edges_backward(
+            index, grad_mesh, back, slopes, w_round[layer], carried
         )
-        if layer == ROUNDS - 1:
+        if ends:
+            grad_mesh, leaving, sent_low = ends
+            mats_grads[5 * layer + 5] = inner(
+                kept[layer + 1][0].astype(jnp.bfloat16), sent_low, 0, 0
+            )
+        else:
             to_before, to_after, final_mesh = lax.optimization_barrier(
                 (to_before, to_after, final_mesh)
             )
         from_before, from_after = halo(walk, to_after, to_before)
-        if layer == ROUNDS - 1:
+        if not ends:
             from_before, final_mesh = lax.optimization_barrier(
                 (from_before, settled(mesh, final_mesh))
             )
         lowered = old.astype(jnp.bfloat16)
-        grad_out = leaving
-        grads = [
-            None,
+        mats_grads[5 * layer + 1 : 5 * layer + 5] = [
             inner(lowered, dest_low, 0, 0),
             inner(agg, grad_uin, 0, 0),
             inner(lowered, grad_uin, 0, 0),
-            inner(update, grad_out, 0, 0),
+            inner(update, leaving, 0, 0),
         ]
         bias_grads[2 * layer] = jnp.sum(dest_low.astype(jnp.float32), 0, keepdims=True)
         bias_grads[2 * layer + 1] = jnp.sum(grad_uin.astype(jnp.float32), 0, keepdims=True)
-        grad_mesh, sent_low, leaving = round_backward(
-            grad_mesh, own, from_before, from_after, grad_uin, dest_low, turned[layer]
-        )
-        grads[0] = inner(lowered, sent_low, 0, 0)
-        mats_grads[5 * layer : 5 * layer + 5] = grads
-    third = blocks // 4 // 16 * 16
-    early = at_home(leaving[:third])
+        carried = (own, from_before, from_after, grad_uin, dest_low, w_round[layer])
+    grad_mesh, leaving, sent_low = round_backward(grad_mesh, *carried)
+    mats_grads[0] = inner(kept[0][0].astype(jnp.bfloat16), sent_low, 0, 0)
     grad_win, grad_wnode, grad_bpair = encode_backward(
         grad_mesh, gathered, arrived, ids, w_in, w_node, biases
     )
-    grad_win, grad_wnode, grad_bpair, early = lax.optimization_barrier(
-        (grad_win, grad_wnode, grad_bpair, early)
-    )
-    middle = at_home(leaving[third : 2 * third])
     parts = [grad_win, grad_wnode, grad_wdec, grad_wout.reshape(CH, D)]
     parts = parts + mats_grads
     parts = parts + [grad_bpair, grad_bdec] + bias_grads
     keep, send = collect_rows(parts, total_size, peers, place)
-    keep, send, middle = lax.optimization_barrier((keep, send, middle))
-    mine, leaving = reduced_piece(keep, send, leaving[2 * third :])
+    mine, leaving = reduced_piece(keep, send, leaving)
     late = at_home(leaving)
     mine = lax.dynamic_slice_in_dim(mine.reshape(-1), offset, shard)
     lane = lax.broadcasted_iota(jnp.int32, (8, HALF), 1)
@@ -876,7 +886,7 @@
         jnp.where(lane == 0, local_total, jnp.sum(mine * mine)), late
     )
     total, norm = sums[0, 0], jnp.sqrt(sums[0, 1])
-    node_grads = settled(grad_mesh, jnp.concatenate([early, middle, late], 0))
+    node_grads = settled(grad_mesh, late)
     clipped = mine * jnp.minimum(1.0, 0.05 / norm)
     first = 0.9 * moment1 + 0.1 * clipped
     second = 0.999 * moment2 + 0.001 * clipped * clipped

time: 522 us -> 537 us (1.029)
  Pallas kernels: 186 us -> 215 us
  local copies, waits for them, and re-layouts: 24 us -> 15.2 us
  waiting for transfers between devices: 132 us -> 126 us
    pallas_call x6, Pallas kernels: 147 us -> 187 us  [the longest x3 102 us: round_forward(): pl.pallas_call(body, grid_spec=pl.GridSpec(grid=(blocks // tile,), in_spe...]
    pallas_call x3 -> x1, Pallas kernels: 17.7 us -> 6.14 us  [round_backward(): pl.pallas_call(body, grid=(blocks // tile,), in_specs=[rows, woven, woven...]
    ppermute x6, waiting for transfers between devices: 41.3 us -> 35 us  [halo(): lax.ppermute(initial, 'space', down)]
  transfers between devices with their start and end apart: 48 -> 46, of which waited for: 27 -> 28; matrix products, arithmetic and copies ran while one was open for 10% -> 9% of each run, Pallas kernels for 9% -> 5%
where the time goes in v8:
time: 537 us; the launch traced here: 528 us
  Pallas kernels  215 us (40%)
  waiting for transfers between devices  126 us (23%)
  starting transfers between devices  84.4 us (16%)
  matrix products  36 us (7%)
  other arithmetic  28.7 us (5%)
  local copies, waits for them, and re-layouts  15.2 us (3%)
  blocking collectives  14.2 us (3%)
  between operations  8.36 us (2%)
    pallas_call x3, Pallas kernels, round_forward(): pl.pallas_call(body, grid_spec=pl.GridSpec(grid=(blocks // tile,), in_spe...  102 us
    pallas_call x3, Pallas kernels, edges_backward(): pl.pallas_call(body, grid_spec=pl.GridSpec(grid=(steps,), in_specs=[index...  85.8 us
    ppermute x24, starting transfers between devices, swapped(): lax.ppermute(value, axis, [(i, i ^ bit) for i in range(lax.axis_size(axis...  35.7 us
    dot_general x24, matrix products, inner(): lax.dot_general(left, right, (((left_dim,), (right_dim,)), ((), ())), pre...  35.6 us
    ppermute x6, waiting for transfers between devices, halo(): lax.ppermute(initial, 'space', down)  35 us
    ppermute x24, waiting for transfers between devices, swapped(): lax.ppermute(value, axis, [(i, i ^ bit) for i in range(lax.axis_size(axis...  34.5 us
    ppermute x6, waiting for transfers between devices, halo(): lax.ppermute(last, 'space', up)  25.1 us
    ppermute x5, waiting for transfers between devices, shifted(): return lax.ppermute(shard, axis, pairs)  18.5 us
  transfers between devices with their start and end apart: 46, of which 28 were waited for; matrix products, arithmetic and copies ran while one was open for 9% of the time, Pallas kernels for 5%

profile of v8, /device:TPU:0, one launch (start us, length us, event | category | flops | bytes accessed | tf_op | source)
XLA Modules:
  0.0 527.8 jit_solution(14004441888071570952)
XLA Ops:
  5.8 4.1 collective-permute-start.3
  17.6 3.0 collective-permute-done.4
  30.1 5.2 all-to-all-start
  37.2 6.6 %all-to-all-done = bf16[16,64,128]{2,1,0:T(8,128)(2,1)S(1)} async-done(((bf16[16,64,128]{2,1,0:T(8,128)(2,1)}), bf16[16,64,128]{2,1,0:T(8,128)(2,1)S(1)}, u32[]{:S(2)}, u32[]{:S(2)}) %all-to-all-start) | async-done | bytes 262176 | tf_op jit(solution)/shard_map/all_to_all | solution.py:731
  46.8 4.0 spread_rows.1
  50.8 5.8 %encode_rows.1 = (f32[2048,256]{1,0:T(8,128)}, bf16[2048,256]{1,0:T(8,128)(2,1)}, bf16[4096,128]{1,0:T(8,128)(2,1)}) custom-call(bf16[1024,128]{1,0:T(8,128)(2,1)} %bitcast.160, s32[1,1024]{1,0:T(1,128)} %bitcast.175, bf16[128,256]{1,0:T(8,128)(2,1)} %get-tuple-element.93.in_ref, bf16[256,256]{1,0:T(8,128)(2,1)} %get-tuple-element.94.node_ref, ...), custom_call_target="tpu_custom_call" | custom-call | bytes 15000000 | tf_op jit(solution)/shard_map/encode_rows/pallas_call | solution.py:624
  58.7 3.3 collective-permute-start.14
  65.6 13.3 %collective-permute-done.14 = s32[360]{0:T(512)S(1)} collective-permute-done((s32[360]{0:T(512)S(1)}, s32[360]{0:T(512)S(1)}, u32[]{:S(2)}, u32[]{:S(2)}) %collective-permute-start.14) | collective-permute-done | bytes 1472 | tf_op jit(solution)/shard_map/ppermute | solution.py:49
  78.9 4.3 collective-permute-start.12
  86.6 34.2 %round_forward.3 = (f32[2048,256]{1,0:T(8,128)}, f32[2048,256]{1,0:T(8,128)}, bf16[2048,256]{1,0:T(8,128)(2,1)}, bf16[2048,256]{1,0:T(8,128)(2,1)}, bf16[6,4096,...) custom-call(s32[6,2048]{1,0:T(8,128)} %broadcast_select_fusion.refs_0_, f32[2048,256]{1,0:T(8,128)} %get-tuple-element.100.refs_1_, ...), custom_call_target="tpu_custom_call" | custom-call | bytes 75000000 | tf_op jit(solution)/shard_map/round_forward/pallas_call | solution.py:402
  123.2 17.1 %collective-permute-done.17.refs_4_ = bf16[4096,128]{1,0:T(8,128)(2,1)S(1)} collective-permute-done((bf16[4096,128]{1,0:T(8,128)(2,1)}, bf16[4096,128]{1,0:T(8,128)(2,1)S(1)}, u32[]{:S(2)}, u32[]{:S(2)}) %collective-permute-start.17) | collective-permute-done | bytes 1048608 | tf_op jit(solution)/shard_map/ppermute | solution.py:77
  140.3 2.8 collective-permute-done.16.refs_2_
  144.2 34.2 %round_forward.4 = (f32[2048,256]{1,0:T(8,128)}, f32[2048,256]{1,0:T(8,128)}, bf16[2048,256]{1,0:T(8,128)(2,1)}, bf16[2048,256]{1,0:T(8,128)(2,1)}, bf16[6,4096,...) custom-call(s32[6,2048]{1,0:T(8,128)} %broadcast_select_fusion.refs_0_, f32[2048,256]{1,0:T(8,128)} %get-tuple-element.105.refs_1_, ...), custom_call_target="tpu_custom_call" | custom-call | bytes 75000000 | tf_op jit(solution)/shard_map/round_forward/pallas_call | solution.py:402
  181.6 17.9 %collective-permute-done.19.refs_4_ = bf16[4096,128]{1,0:T(8,128)(2,1)S(1)} collective-permute-done((bf16[4096,128]{1,0:T(8,128)(2,1)}, bf16[4096,128]{1,0:T(8,128)(2,1)S(1)}, u32[]{:S(2)}, u32[]{:S(2)}) %collective-permute-start.19) | collective-permute-done | bytes 1048608 | tf_op jit(solution)/shard_map/ppermute | solution.py:77
  200.8 33.2 %round_forward.5 = (f32[2048,256]{1,0:T(8,128)}, f32[2048,256]{1,0:T(8,128)}, bf16[2048,256]{1,0:T(8,128)(2,1)}, bf16[2048,256]{1,0:T(8,128)(2,1)}, bf16[6,4096,128]{2,1,0:T(8,128)(2,1)}) custom-call(s32[6,2048]{1,0:T(8,128)} %broadcast_select_fusion.refs_0_, f32[2048,256]{1,0:T(8,128)} %get-tuple-element.108.refs_1_, bf16[4096,128]{1,0:T(8,128)(2,1)} %copy-done.29, ...), custom_call_target="tpu_custom_call" | custom-call | bytes 75000000 | tf_op jit(solution)/shard_map/round_forward/pallas_call | solution.py:402
  234.1 2.7 convert_element_type.199
  236.7 2.7 fusion.8
  240.9 8.1 %all-to-all-start.1 = ((bf16[16,64,128]{2,1,0:T(8,128)(2,1)}), bf16[16,64,128]{2,1,0:T(8,128)(2,1)S(1)}, u32[]{:S(2)}, u32[]{:S(2)}) async-start(bf16[16,64,128]{2,1,0:T(8,128)(2,1)} %bitcast.17), calls=%async_computation.1 | async-start | bytes 524288 | tf_op jit(solution)/shard_map/all_to_all | solution.py:731
  251.7 5.9 %all-to-all-done.1 = bf16[16,64,128]{2,1,0:T(8,128)(2,1)S(1)} async-done(((bf16[16,64,128]{2,1,0:T(8,128)(2,1)}), bf16[16,64,128]{2,1,0:T(8,128)(2,1)S(1)}, u32[]{:S(2)}, u32[]{:S(2)}) %all-to-all-start.1) | async-done | bytes 262176 | tf_op jit(solution)/shard_map/all_to_all | solution.py:731
  258.1 3.3 collective-permute-start.20
  262.9 4.7 collective-permute-done.21
  269.9 14.2 %all_to_all.15 = bf16[16,64,128]{2,1,0:T(8,128)(2,1)S(1)} all-to-all(bf16[16,64,128]{2,1,0:T(8,128)(2,1)S(1)} %bitcast.173), channel_id=1, replica_groups=mesh['dp'=2,'space'=16] {'space'}, dimensions={0} | all-to-all | bytes 524288 | tf_op jit(solution)/shard_map/all_to_all | solution.py:731
  286.4 4.0 fusion.refs_1_
  292.1 26.6 %edges_backward.3 = (bf16[2048,256]{1,0:T(8,128)(2,1)}, bf16[2048,256]{1,0:T(8,128)(2,1)}, bf16[4096,128]{1,0:T(8,128)(2,1)}, f32[4096,128]{1,0:T(8,128)}, bf16[4096,128]{1,0:T(8,128)(2,1)}) custom-call(s32[6,2048]{1,0:T(8,128)} %broadcast_select_fusion.refs_0_, f32[2048,256]{1,0:T(8,128)} %fusion.refs_1_, f32[2048,256]{1,0:T(8,128)} %get-tuple-element.119.refs_2_, ...), custom_call_target="tpu_custom_call" | custom-call | bytes 75000000 | tf_op jit(solution)/shard_map/edges_backward/pallas_call | solution.py:522
  319.8 2.7 fusion.110.refs_16_
  326.4 2.4 collective-permute-start.24
  331.3 3.4 convert_select_fusion
  334.7 10.0 %collective-permute-done.23.refs_6_ = bf16[4096,128]{1,0:T(8,128)(2,1)} collective-permute-done((bf16[4096,128]{1,0:T(8,128)(2,1)S(1)}, bf16[4096,128]{1,0:T(8,128)(2,1)}, u32[]{:S(2)}, u32[]{:S(2)}) %collective-permute-start.23) | collective-permute-done | bytes 1048608 | tf_op jit(solution)/shard_map/ppermute | solution.py:77
  344.8 29.6 %edges_backward.4 = (f32[2048,256]{1,0:T(8,128)}, bf16[2048,256]{1,0:T(8,128)(2,1)}, bf16[2048,256]{1,0:T(8,128)(2,1)}, bf16[2048,256]{1,0:T(8,128)(2,1)}, bf16[...) custom-call(s32[6,2048]{1,0:T(8,128)} %broadcast_select_fusion.refs_0_, ...), custom_call_target="tpu_custom_call" | custom-call | bytes 84000000 | tf_op jit(solution)/shard_map/edges_backward/pallas_call | solution.py:522
  375.2 3.1 collective-permute-start.26
  378.3 2.6 fusion.108.refs_11_
  386.5 7.0 %collective-permute-done.25.refs_6_ = bf16[4096,128]{1,0:T(8,128)(2,1)} collective-permute-done((bf16[4096,128]{1,0:T(8,128)(2,1)}, bf16[4096,128]{1,0:T(8,128)(2,1)}, u32[]{:S(2)}, u32[]{:S(2)}) %collective-permute-start.25) | collective-permute-done | bytes 1048608 | tf_op jit(solution)/shard_map/ppermute | solution.py:77
  393.6 29.7 %edges_backward.5 = (f32[2048,256]{1,0:T(8,128)}, bf16[2048,256]{1,0:T(8,128)(2,1)}, bf16[2048,256]{1,0:T(8,128)(2,1)}, bf16[2048,256]{1,0:T(8,128)(2,1)}, bf16[...) custom-call(s32[6,2048]{1,0:T(8,128)} %broadcast_select_fusion.refs_0_, ...), custom_call_target="tpu_custom_call" | custom-call | bytes 84000000 | tf_op jit(solution)/shard_map/edges_backward/pallas_call | solution.py:522
  423.3 4.0 collective-permute-start.28
  427.4 2.6 fusion.106.refs_6_
  436.3 5.1 collective-permute-done.27.refs_2_
  441.5 6.1 %round_backward.1 = (f32[2048,256]{1,0:T(8,128)}, bf16[2048,256]{1,0:T(8,128)(2,1)}, bf16[2048,256]{1,0:T(8,128)(2,1)}) custom-call(f32[2048,256]{1,0:T(8,128)} %get-tuple-element.139.refs_0_, f32[4096,128]{1,0:T(8,128)} %get-tuple-element.140.refs_1_, bf16[4096,128]{1,0:T(8,128)(2,1)} %collective-permute-done.27.refs_2_, ...), custom_call_target="tpu_custom_call" | custom-call | bytes 21000000 | tf_op jit(solution)/shard_map/round_backward/pallas_call | solution.py:588
  447.6 2.4 fusion.87.refs_4_
  450.0 6.9 %encode_backward.1 = (f32[128,256]{1,0:T(8,128)}, f32[256,256]{1,0:T(8,128)}, f32[2,256]{1,0:T(2,128)}) custom-call(f32[2048,256]{1,0:T(8,128)} %get-tuple-element.145.grad_ref, bf16[2048,256]{1,0:T(8,128)(2,1)} %get-tuple-element.146.gathered_ref, bf16[1024,128]{1,0:T(8,128)(2,1)} %bitcast.161, s32[1024,1]{1,0:T(8,128)} %get-tuple-element.204.ids_ref, ...), custom_call_target="tpu_custom_call" | custom-call | bytes 21000000 | tf_op jit(solution)/shard_map/encode_backward/pallas_call | solution.py:675
  456.9 5.1 collect_rows.1
  462.1 3.0 collective-permute-done.29
  468.8 7.6 %collective-permute-done.32 = bf16[2,2,2,72,256]{4,3,2,1,0:T(8,128)(2,1)S(1)} collective-permute-done((bf16[2,2,2,72,256]{4,3,2,1,0:T(8,128)(2,1)S(1)}, bf16[2,2,2,72,256]{4,3,2,1,0:T(8,128)(2,1)S(1)}, u32[]{:S(2)}, u32[]{:S(2)}) %collective-permute-start.32) | collective-permute-done | bytes 294944 | tf_op jit(solution)/shard_map/ppermute | solution.py:94
  477.9 2.2 collective-permute-start.31
  487.8 4.1 collective-permute-start.37
  494.0 2.8 collective-permute-done.35
  499.6 3.6 collective-permute-done.39
  503.2 8.3 %collective-permute-start.40 = (f32[8,128]{1,0:T(8,128)S(1)}, f32[8,128]{1,0:T(8,128)S(1)}, u32[]{:S(2)}, u32[]{:S(2)}) collective-permute-start(f32[8,128]{1,0:T(8,128)S(1)} %fusion.140), channel_id=1, source_target_pairs={{0,2},{1,3},{2,0},{3,1},{4,6},{5,7},{6,4},{7,5},{8,10},{9,11},{10,... | collective-permute-start | bytes 12296 | tf_op jit(solution)/shard_map/ppermute | solution.py:94
  516.7 3.8 collective-permute-start.43
  (278 shorter events, 99.9 us)
Async XLA Ops:
  5.8 9.6 %collective-permute-start.3 = (bf16[1,72,256]{2,1,0:T(8,128)(2,1)S(1)}, bf16[1,72,256]{2,1,0:T(8,128)(2,1)S(1)}, u32[]{:S(2)}, u32[]{:S(2)}) collective-permute-start(bf16[1,72,256]{2,1,0:T(8,128)(2,1)S(1)} %get-tuple-element.218), channel_id=1, source_target_pairs={{0,8},{1,9},{2,10},{3,11},{4,12},{5,13},{6,14},{7,15},{8,0},{9,1},... | collective-permute-start | bytes 110600 | tf_op jit(solution)/shard_map/ppermute | solution.py:94
  9.9 7.5 %collective-permute-start = (bf16[1,72,256]{2,1,0:T(8,128)(2,1)S(1)}, bf16[1,72,256]{2,1,0:T(8,128)(2,1)S(1)}, u32[]{:S(2)}, u32[]{:S(2)}) collective-permute-start(bf16[1,72,256]{2,1,0:T(8,128)(2,1)S(1)} %get-tuple-element.219), channel_id=1, source_target_pairs={{0,8},{1,9},{2,10},{3,11},{4,12},{5,13},{6,14},{7,15},{8,0},{9,1},... | collective-permute-start | bytes 110600 | tf_op jit(solution)/shard_map/ppermute | solution.py:94
  15.4 5.2 collective-permute-start.4
  17.3 4.8 collective-permute-start.1
  20.6 5.2 collective-permute-start.5
  22.2 5.2 collective-permute-start.2
  27.4 7.9 %collective-permute-start.7 = (bf16[8,72,256]{2,1,0:T(8,128)(2,1)S(1)}, bf16[8,72,256]{2,1,0:T(8,128)(2,1)S(1)}, u32[]{:S(2)}, u32[]{:S(2)}) collective-permute-start(bf16[8,72,256]{2,1,0:T(8,128)(2,1)S(1)} %pad_maximum_fusion.2), channel_id=1, source_target_pairs={{0,2},{1,3},{2,0},{3,1},{4,6},{5,7},{6,4},{7,5},{8,10},{9,11},{10,... | collective-permute-start | bytes 884744 | tf_op jit(solution)/shard_map/ppermute | solution.py:94
  29.0 7.4 %collective-permute-start.6 = (bf16[8,72,256]{2,1,0:T(8,128)(2,1)S(1)}, bf16[8,72,256]{2,1,0:T(8,128)(2,1)S(1)}, u32[]{:S(2)}, u32[]{:S(2)}) collective-permute-start(bf16[8,72,256]{2,1,0:T(8,128)(2,1)S(1)} %pad_maximum_fusion.1), channel_id=1, source_target_pairs={{0,1},{1,0},{2,3},{3,2},{4,5},{5,4},{6,7},{7,6},{8,9},{9,8},{10,11... | collective-permute-start | bytes 884744 | tf_op jit(solution)/shard_map/ppermute | solution.py:94
  30.1 13.7 %all-to-all-start = ((bf16[16,64,128]{2,1,0:T(8,128)(2,1)}), bf16[16,64,128]{2,1,0:T(8,128)(2,1)S(1)}, u32[]{:S(2)}, u32[]{:S(2)}) async-start(bf16[16,64,128]{2,1,0:T(8,128)(2,1)} %bitcast.7), calls=%async_computation | async-start | bytes 524288 | tf_op jit(solution)/shard_map/all_to_all | solution.py:731
  35.4 10.3 %collective-permute-start.9 = (bf16[16,72,256]{2,1,0:T(8,128)(2,1)S(1)}, bf16[16,72,256]{2,1,0:T(8,128)(2,1)S(1)}, u32[]{:S(2)}, u32[]{:S(2)}) collective-permute-start(bf16[16,72,256]{2,1,0:T(8,128)(2,1)S(1)} %constant_dynamic-update-slice_fusion.2.refs_1_), channel_id=1, source_target_pairs={{0,16},{16,0},{1,17},{17,1},{2,18},{18,2},{3,19},{19,3},{4,20},{20... | collective-permute-start | bytes 1769480 | tf_op jit(solution)/shard_map/ppermute | solution.py:94
  36.5 9.2 %collective-permute-start.8 = (bf16[16,72,256]{2,1,0:T(8,128)(2,1)S(1)}, bf16[16,72,256]{2,1,0:T(8,128)(2,1)S(1)}, u32[]{:S(2)}, u32[]{:S(2)}) collective-permute-start(bf16[16,72,256]{2,1,0:T(8,128)(2,1)S(1)} %constant_dynamic-update-slice_fusion.refs_0_), channel_id=1, source_target_pairs={{0,16},{16,0},{1,17},{17,1},{2,18},{18,2},{3,19},{19,3},{4,20},{20... | collective-permute-start | bytes 1769480 | tf_op jit(solution)/shard_map/ppermute | solution.py:94
  56.6 28.7 %collective-permute-start.15 = (bf16[4096,128]{1,0:T(8,128)(2,1)}, bf16[4096,128]{1,0:T(8,128)(2,1)S(1)}, u32[]{:S(2)}, u32[]{:S(2)}) collective-permute-start(bf16[4096,128]{1,0:T(8,128)(2,1)} %get-tuple-element.101.refs_3_), channel_id=1, source_target_pairs={{1,0},{3,1},{2,3},{6,2},{4,6},{5,4},{7,5},{11,7},{9,11},{8,9},{10,... | collective-permute-start | bytes 3145736 | tf_op jit(solution)/shard_map/ppermute | solution.py:77
  58.4 26.9 %collective-permute-start.11 = (bf16[4096,128]{1,0:T(8,128)(2,1)}, bf16[4096,128]{1,0:T(8,128)(2,1)S(1)}, u32[]{:S(2)}, u32[]{:S(2)}) collective-permute-start(bf16[4096,128]{1,0:T(8,128)(2,1)} %get-tuple-element.101.refs_3_), channel_id=1, source_target_pairs={{0,1},{1,3},{3,2},{2,6},{6,4},{4,5},{5,7},{7,11},{11,9},{9,8},{8,1... | collective-permute-start | bytes 3145736 | tf_op jit(solution)/shard_map/ppermute | solution.py:77
  58.7 20.2 %collective-permute-start.14 = (s32[360]{0:T(512)S(1)}, s32[360]{0:T(512)S(1)}, u32[]{:S(2)}, u32[]{:S(2)}) collective-permute-start(s32[360]{0:T(512)S(1)} %slice.218), channel_id=1, source_target_pairs={{0,1},{1,2},{2,3},{3,4},{4,5},{5,6},{6,7},{7,8},{8,9},{9,10},{10,1... | collective-permute-start | bytes 4328 | tf_op jit(solution)/shard_map/ppermute | solution.py:49
  62.1 21.2 %collective-permute-start.10 = (s32[6,2048]{1,0:T(8,128)S(1)}, s32[6,2048]{1,0:T(8,128)S(1)}, u32[]{:S(2)}, u32[]{:S(2)}) collective-permute-start(s32[6,2048]{1,0:T(8,128)S(1)} %fusion.58), channel_id=1, source_target_pairs={{2,3},{3,2},{4,6},{5,4},{6,5},{8,11},{10,8},{11,10},{12,14},{13,15... | collective-permute-start | bytes 147464 | tf_op jit(solution)/shard_map/ppermute | solution.py:757
  64.3 20.3 %collective-permute-start.13 = (bf16[78,360]{1,0:T(8,128)(2,1)S(1)}, bf16[78,360]{1,0:T(8,128)(2,1)S(1)}, u32[]{:S(2)}, u32[]{:S(2)}) collective-permute-start(bf16[78,360]{1,0:T(8,128)(2,1)S(1)} %get-tuple-element.216), channel_id=1, source_target_pairs={{1,0},{2,1},{3,2},{4,3},{5,4},{6,5},{7,6},{8,7},{9,8},{10,9},{11,1... | collective-permute-start | bytes 168488 | tf_op jit(solution)/shard_map/ppermute | solution.py:49
  78.9 6.1 %collective-permute-start.12 = (bf16[78,360]{1,0:T(8,128)(2,1)S(1)}, bf16[78,360]{1,0:T(8,128)(2,1)S(1)}, u32[]{:S(2)}, u32[]{:S(2)}) collective-permute-start(bf16[78,360]{1,0:T(8,128)(2,1)S(1)} %get-tuple-element.217), channel_id=1, source_target_pairs={{0,1},{1,2},{2,3},{3,4},{4,5},{5,6},{6,7},{7,8},{8,9},{9,10},{10,1... | collective-permute-start | bytes 168488 | tf_op jit(solution)/shard_map/ppermute | solution.py:49
  120.7 19.6 %collective-permute-start.17 = (bf16[4096,128]{1,0:T(8,128)(2,1)}, bf16[4096,128]{1,0:T(8,128)(2,1)S(1)}, u32[]{:S(2)}, u32[]{:S(2)}) collective-permute-start(bf16[4096,128]{1,0:T(8,128)(2,1)} %get-tuple-element.106.refs_3_), channel_id=1, source_target_pairs={{1,0},{3,1},{2,3},{6,2},{4,6},{5,4},{7,5},{11,7},{9,11},{8,9},{10,... | collective-permute-start | bytes 3145736 | tf_op jit(solution)/shard_map/ppermute | solution.py:77
  121.8 21.3 %collective-permute-start.16 = (bf16[4096,128]{1,0:T(8,128)(2,1)}, bf16[4096,128]{1,0:T(8,128)(2,1)S(1)}, u32[]{:S(2)}, u32[]{:S(2)}) collective-permute-start(bf16[4096,128]{1,0:T(8,128)(2,1)} %get-tuple-element.106.refs_3_), channel_id=1, source_target_pairs={{0,1},{1,3},{3,2},{2,6},{6,4},{4,5},{5,7},{7,11},{11,9},{9,8},{8,1... | collective-permute-start | bytes 3145736 | tf_op jit(solution)/shard_map/ppermute | solution.py:77
  178.4 21.1 %collective-permute-start.19 = (bf16[4096,128]{1,0:T(8,128)(2,1)}, bf16[4096,128]{1,0:T(8,128)(2,1)S(1)}, u32[]{:S(2)}, u32[]{:S(2)}) collective-permute-start(bf16[4096,128]{1,0:T(8,128)(2,1)} %get-tuple-element.109.refs_3_), channel_id=1, source_target_pairs={{1,0},{3,1},{2,3},{6,2},{4,6},{5,4},{7,5},{11,7},{9,11},{8,9},{10,... | collective-permute-start | bytes 3145736 | tf_op jit(solution)/shard_map/ppermute | solution.py:77
  179.1 20.5 %collective-permute-start.18 = (bf16[4096,128]{1,0:T(8,128)(2,1)}, bf16[4096,128]{1,0:T(8,128)(2,1)S(1)}, u32[]{:S(2)}, u32[]{:S(2)}) collective-permute-start(bf16[4096,128]{1,0:T(8,128)(2,1)} %get-tuple-element.109.refs_3_), channel_id=1, source_target_pairs={{0,1},{1,3},{3,2},{2,6},{6,4},{4,5},{5,7},{7,11},{11,9},{9,8},{8,1... | collective-permute-start | bytes 3145736 | tf_op jit(solution)/shard_map/ppermute | solution.py:77
  181.6 58.2 %copy-start.41 = (bf16[256,78]{1,0:T(8,128)(2,1)}, bf16[256,78]{1,0:T(8,128)(2,1)S(1)}, u32[]{:S(2)}) copy-start(bf16[256,78]{1,0:T(8,128)(2,1)S(1)} %reshape.152) | copy-start | bytes 119812
  240.9 16.6 %all-to-all-start.1 = ((bf16[16,64,128]{2,1,0:T(8,128)(2,1)}), bf16[16,64,128]{2,1,0:T(8,128)(2,1)S(1)}, u32[]{:S(2)}, u32[]{:S(2)}) async-start(bf16[16,64,128]{2,1,0:T(8,128)(2,1)} %bitcast.17), calls=%async_computation.1 | async-start | bytes 524288 | tf_op jit(solution)/shard_map/all_to_all | solution.py:731
  258.1 9.5 %collective-permute-start.20 = (bf16[78,360]{1,0:T(8,128)(2,1)S(1)}, bf16[78,360]{1,0:T(8,128)(2,1)S(1)}, u32[]{:S(2)}, u32[]{:S(2)}) collective-permute-start(bf16[78,360]{1,0:T(8,128)(2,1)S(1)} %get-tuple-element.214), channel_id=1, source_target_pairs={{0,1},{1,2},{2,3},{3,4},{4,5},{5,6},{6,7},{7,8},{8,9},{9,10},{10,1... | collective-permute-start | bytes 168488 | tf_op jit(solution)/shard_map/ppermute | solution.py:49
  261.5 6.1 %collective-permute-start.21 = (bf16[78,360]{1,0:T(8,128)(2,1)S(1)}, bf16[78,360]{1,0:T(8,128)(2,1)S(1)}, u32[]{:S(2)}, u32[]{:S(2)}) collective-permute-start(bf16[78,360]{1,0:T(8,128)(2,1)S(1)} %get-tuple-element.215), channel_id=1, source_target_pairs={{1,0},{2,1},{3,2},{4,3},{5,4},{6,5},{7,6},{8,7},{9,8},{10,9},{11,1... | collective-permute-start | bytes 168488 | tf_op jit(solution)/shard_map/ppermute | solution.py:49
  290.3 34.6 %collective-permute-start.22 = (bf16[2048,256]{1,0:T(8,128)(2,1)}, bf16[2048,256]{1,0:T(8,128)(2,1)}, u32[]{:S(2)}, u32[]{:S(2)}) collective-permute-start(bf16[2048,256]{1,0:T(8,128)(2,1)} %convert_element_type.199), channel_id=1, source_target_pairs={{3,2},{2,3},{6,4},{4,5},{5,6},{11,8},{8,10},{10,11},{14,12},{15,13... | collective-permute-start | bytes 3145736 | tf_op jit(solution)/shard_map/ppermute | solution.py:760
  325.0 19.8 %collective-permute-start.23 = (bf16[4096,128]{1,0:T(8,128)(2,1)S(1)}, bf16[4096,128]{1,0:T(8,128)(2,1)}, u32[]{:S(2)}, u32[]{:S(2)}) collective-permute-start(bf16[4096,128]{1,0:T(8,128)(2,1)S(1)} %copy-done.49), channel_id=1, source_target_pairs={{0,1},{1,3},{3,2},{2,6},{6,4},{4,5},{5,7},{7,11},{11,9},{9,8},{8,1... | collective-permute-start | bytes 3145736 | tf_op jit(solution)/shard_map/ppermute | solution.py:77
  326.4 18.4 %collective-permute-start.24 = (bf16[4096,128]{1,0:T(8,128)(2,1)S(1)}, bf16[4096,128]{1,0:T(8,128)(2,1)}, u32[]{:S(2)}, u32[]{:S(2)}) collective-permute-start(bf16[4096,128]{1,0:T(8,128)(2,1)S(1)} %copy-done.48), channel_id=1, source_target_pairs={{1,0},{3,1},{2,3},{6,2},{4,6},{5,4},{7,5},{11,7},{9,11},{8,9},{10,... | collective-permute-start | bytes 3145736 | tf_op jit(solution)/shard_map/ppermute | solution.py:77
  374.4 19.2 %collective-permute-start.25 = (bf16[4096,128]{1,0:T(8,128)(2,1)}, bf16[4096,128]{1,0:T(8,128)(2,1)}, u32[]{:S(2)}, u32[]{:S(2)}) collective-permute-start(bf16[4096,128]{1,0:T(8,128)(2,1)} %get-tuple-element.135), channel_id=1, source_target_pairs={{0,1},{1,3},{3,2},{2,6},{6,4},{4,5},{5,7},{7,11},{11,9},{9,8},{8,1... | collective-permute-start | bytes 3145736 | tf_op jit(solution)/shard_map/ppermute | solution.py:77
  375.2 18.4 %collective-permute-start.26 = (bf16[4096,128]{1,0:T(8,128)(2,1)}, bf16[4096,128]{1,0:T(8,128)(2,1)}, u32[]{:S(2)}, u32[]{:S(2)}) collective-permute-start(bf16[4096,128]{1,0:T(8,128)(2,1)} %get-tuple-element.136), channel_id=1, source_target_pairs={{1,0},{3,1},{2,3},{6,2},{4,6},{5,4},{7,5},{11,7},{9,11},{8,9},{10,... | collective-permute-start | bytes 3145736 | tf_op jit(solution)/shard_map/ppermute | solution.py:77
  423.2 18.2 %collective-permute-start.27 = (bf16[4096,128]{1,0:T(8,128)(2,1)}, bf16[4096,128]{1,0:T(8,128)(2,1)}, u32[]{:S(2)}, u32[]{:S(2)}) collective-permute-start(bf16[4096,128]{1,0:T(8,128)(2,1)} %get-tuple-element.141), channel_id=1, source_target_pairs={{0,1},{1,3},{3,2},{2,6},{6,4},{4,5},{5,7},{7,11},{11,9},{9,8},{8,1... | collective-permute-start | bytes 3145736 | tf_op jit(solution)/shard_map/ppermute | solution.py:77
  423.3 18.2 %collective-permute-start.28 = (bf16[4096,128]{1,0:T(8,128)(2,1)}, bf16[4096,128]{1,0:T(8,128)(2,1)}, u32[]{:S(2)}, u32[]{:S(2)}) collective-permute-start(bf16[4096,128]{1,0:T(8,128)(2,1)} %get-tuple-element.142), channel_id=1, source_target_pairs={{1,0},{3,1},{2,3},{6,2},{4,6},{5,4},{7,5},{11,7},{9,11},{8,9},{10,... | collective-permute-start | bytes 3145736 | tf_op jit(solution)/shard_map/ppermute | solution.py:77
  462.0 3.1 collective-permute-start.29
  467.3 9.1 %collective-permute-start.32 = (bf16[2,2,2,72,256]{4,3,2,1,0:T(8,128)(2,1)S(1)}, bf16[2,2,2,72,256]{4,3,2,1,0:T(8,128)(2,1)S(1)}, u32[]{:S(2)}, u32[]{:S(2)}) collective-permute-start(bf16[2,2,2,72,256]{4,3,2,1,0:T(8,128)(2,1)S(1)} %fusion.21), channel_id=1, source_target_pairs={{0,2},{1,3},{2,0},{3,1},{4,6},{5,7},{6,4},{7,5},{8,10},{9,11},{10,... | collective-permute-start | bytes 884744 | tf_op jit(solution)/shard_map/ppermute | solution.py:94
  468.7 9.1 %collective-permute-start.30 = (bf16[2,2,2,72,256]{4,3,0,1,2:T(8,128)(2,1)S(1)}, bf16[2,2,2,72,256]{4,3,0,1,2:T(8,128)(2,1)S(1)}, u32[]{:S(2)}, u32[]{:S(2)}) collective-permute-start(bf16[2,2,2,72,256]{4,3,0,1,2:T(8,128)(2,1)S(1)} %fusion.22), channel_id=1, source_target_pairs={{0,1},{1,0},{2,3},{3,2},{4,5},{5,4},{6,7},{7,6},{8,9},{9,8},{10,11... | collective-permute-start | bytes 884744 | tf_op jit(solution)/shard_map/ppermute | solution.py:94
  476.5 5.2 collective-permute-start.33
  477.9 42.7 %copy-start.11 = (f32[2048,256]{1,0:T(8,128)S(1)}, f32[2048,256]{1,0:T(8,128)}, u32[]{:S(2)}) copy-start(f32[2048,256]{1,0:T(8,128)} %get-tuple-element.145.grad_ref) | copy-start | bytes 6291460
  477.9 5.4 %collective-permute-start.31 = (bf16[2,2,72,256]{3,2,0,1:T(8,128)(2,1)S(1)}, bf16[2,2,72,256]{3,2,0,1:T(8,128)(2,1)S(1)}, u32[]{:S(2)}, u32[]{:S(2)}) collective-permute-start(bf16[2,2,72,256]{3,2,0,1:T(8,128)(2,1)S(1)} %fusion.48), channel_id=1, source_target_pairs={{0,2},{1,3},{2,0},{3,1},{4,6},{5,7},{6,4},{7,5},{8,10},{9,11},{10,... | collective-permute-start | bytes 442376 | tf_op jit(solution)/shard_map/ppermute | solution.py:94
  483.3 4.4 collective-permute-start.36
  483.4 8.5 %collective-permute-start.34 = (bf16[2,72,256]{2,1,0:T(8,128)(2,1)S(1)}, bf16[2,72,256]{2,1,0:T(8,128)(2,1)S(1)}, u32[]{:S(2)}, u32[]{:S(2)}) collective-permute-start(bf16[2,72,256]{2,1,0:T(8,128)(2,1)S(1)} %fusion.52), channel_id=1, source_target_pairs={{0,4},{1,5},{2,6},{3,7},{4,0},{5,1},{6,2},{7,3},{8,12},{9,13},{10,... | collective-permute-start | bytes 221192 | tf_op jit(solution)/shard_map/ppermute | solution.py:94
  485.5 31.2 %collective-permute-start.42 = (bf16[2048,256]{1,0:T(8,128)(2,1)S(1)}, bf16[2048,256]{1,0:T(8,128)(2,1)S(1)}, u32[]{:S(2)}, u32[]{:S(2)}) collective-permute-start(bf16[2048,256]{1,0:T(8,128)(2,1)S(1)} %copy-done.47), channel_id=1, source_target_pairs={{3,2},{2,3},{6,4},{4,5},{5,6},{11,8},{8,10},{10,11},{14,12},{15,13... | collective-permute-start | bytes 3145736 | tf_op jit(solution)/shard_map/ppermute | solution.py:760
  487.8 6.2 %collective-permute-start.37 = (bf16[72,256]{1,0:T(8,128)(2,1)S(1)}, bf16[72,256]{1,0:T(8,128)(2,1)S(1)}, u32[]{:S(2)}, u32[]{:S(2)}) collective-permute-start(bf16[72,256]{1,0:T(8,128)(2,1)S(1)} %fusion.62), channel_id=1, source_target_pairs={{0,8},{1,9},{2,10},{3,11},{4,12},{5,13},{6,14},{7,15},{8,0},{9,1},... | collective-permute-start | bytes 110600 | tf_op jit(solution)/shard_map/ppermute | solution.py:94
  491.9 4.9 collective-permute-start.35
  498.3 1.2 collective-permute-start.38
  499.6 3.6 collective-permute-start.39
  503.2 9.9 %collective-permute-start.40 = (f32[8,128]{1,0:T(8,128)S(1)}, f32[8,128]{1,0:T(8,128)S(1)}, u32[]{:S(2)}, u32[]{:S(2)}) collective-permute-start(f32[8,128]{1,0:T(8,128)S(1)} %fusion.140), channel_id=1, source_target_pairs={{0,2},{1,3},{2,0},{3,1},{4,6},{5,7},{6,4},{7,5},{8,10},{9,11},{10,... | collective-permute-start | bytes 12296 | tf_op jit(solution)/shard_map/ppermute | solution.py:94
  513.1 3.6 collective-permute-start.41
  516.7 6.0 %collective-permute-start.43 = (f32[8,128]{1,0:T(8,128)S(1)}, f32[8,128]{1,0:T(8,128)S(1)}, u32[]{:S(2)}, u32[]{:S(2)}) collective-permute-start(f32[8,128]{1,0:T(8,128)S(1)} %add.189), channel_id=1, source_target_pairs={{0,8},{1,9},{2,10},{3,11},{4,12},{5,13},{6,14},{7,15},{8,0},{9,1},... | collective-permute-start | bytes 12296 | tf_op jit(solution)/shard_map/ppermute | solution.py:94
  (50 other events, 370.0 us)

commit v9 on v8

--- a/solution.py
+++ b/solution.py
@@ -99,10 +99,10 @@
 
 
 def summed_everywhere(value, arriving):
-    turns = [(axis, bit) for axis in ALL for bit in bits_of(axis)]
+    turns = [(axis, bit) for axis in ALL for bit in reversed(bits_of(axis))]
     for turn, (axis, bit) in enumerate(turns):
         value = value + swapped(value, axis, bit)
-        if turn == len(turns) - 2:
+        if turn == len(turns) - 3:
             value, arriving = lax.optimization_barrier((value, arriving))
     return value, arriving
 
@@ -282,10 +282,6 @@
     return pl.BlockSpec(shape, lambda *_: (0,) * len(shape))
 
 
-def index_block(tile):
-    return pl.BlockSpec((K, tile), lambda i: (0, i), memory_space=pltpu.SMEM)
-
-
 def round_forward(index, mesh, before, own, after, mats, bias, following):
     blocks = mesh.shape[0]
     tile, chunk = 512, 16
@@ -326,7 +322,8 @@
 
         def fetch(turn):
             for edge in range(K):
-                spots = [index_ref[edge, turn * chunk + u] for u in range(chunk)]
+                base = edge * blocks + step * tile + turn * chunk
+                spots = [index_ref[base + u] for u in range(chunk)]
                 values = [table[pl.ds(pl.multiple_of(spot, 2), 2), :] for spot in spots]
                 for u in range(chunk):
                     spot = pl.multiple_of(edge * 2 * tile + turn * high + 2 * u, 2)
@@ -382,9 +379,9 @@
             weave(wide, inner(new.astype(jnp.bfloat16), next_ref[0], 1, 0))
             sent_ref[...] = wide[...].astype(jnp.bfloat16)
 
-    whole_rows = pl.BlockSpec((tile, D), lambda i: (i, 0))
-    woven = pl.BlockSpec((2 * tile, HALF), lambda i: (i, 0))
-    ins = [index_block(tile), whole_rows] + [pl.BlockSpec(memory_space=pl.ANY)] * 3 + [whole(mats.shape), whole(bias.shape)]
+    whole_rows = pl.BlockSpec((tile, D), lambda i, *_: (i, 0))
+    woven = pl.BlockSpec((2 * tile, HALF), lambda i, *_: (i, 0))
+    ins = [whole_rows] + [pl.BlockSpec(memory_space=pl.ANY)] * 3 + [whole(mats.shape), whole(bias.shape)]
     outs = [whole_rows] * 4 + [pl.BlockSpec((K, 2 * tile, HALF), lambda i, *_: (0, i, 0))]
     shapes = [
         jax.ShapeDtypeStruct((blocks, D), jnp.float32),
@@ -401,7 +398,8 @@
         args.append(following)
     return pl.pallas_call(
         body,
-        grid_spec=pl.GridSpec(
+        grid_spec=pltpu.PrefetchScalarGridSpec(
+            num_scalar_prefetch=1,
             grid=(blocks // tile,),
             in_specs=ins,
             out_specs=outs,
@@ -476,7 +474,8 @@
             for u in range(chunk):
                 spots, sums = [], []
                 for edge in range(K):
-                    spots.append(pl.multiple_of(index_ref[edge, turn * chunk + u], 2))
+                    base = edge * blocks + step * tile + turn * chunk
+                    spots.append(pl.multiple_of(index_ref[base + u], 2))
                 for edge in range(K):
                     spot = pl.multiple_of(edge * 2 * tile + turn * high + 2 * u, 2)
                     sums.append(tables[edge][pl.ds(spots[edge], 2), :] + flows[pl.ds(spot, 2), :])
@@ -516,16 +515,17 @@
                 at = pl.multiple_of(i * 256, 256)
                 own_ref[pl.ds(at, 256), :] = summed(pl.multiple_of(2 * H + at, 256))
 
-    rows = pl.BlockSpec((tile, D), lambda i: (i, 0))
-    woven = pl.BlockSpec((2 * tile, HALF), lambda i: (i, 0))
+    rows = pl.BlockSpec((tile, D), lambda i, *_: (i, 0))
+    woven = pl.BlockSpec((2 * tile, HALF), lambda i, *_: (i, 0))
     low = jax.ShapeDtypeStruct((blocks, D), jnp.bfloat16)
     return pl.pallas_call(
         body,
-        grid_spec=pl.GridSpec(
+        grid_spec=pltpu.PrefetchScalarGridSpec(
+            num_scalar_prefetch=1,
             grid=(steps,),
             in_specs=[
-                index_block(tile), rows, rows,
-                pl.BlockSpec((K, 2 * tile, HALF), lambda i: (0, i, 0)),
+                rows, rows,
+                pl.BlockSpec((K, 2 * tile, HALF), lambda i, *_: (0, i, 0)),
                 whole(mats.shape),
             ]
             + ([woven] * 3 + [rows] * 2 + [whole(mats.shape)] if carried else []),
@@ -751,7 +751,7 @@
     sent, partner, neighbours, counted = lax.optimization_barrier(
         (sent, partner, neighbours, counted)
     )
-    index = 2 * ((neighbours - band * blocks + H) % (blocks * bands)).T
+    index = 2 * ((neighbours - band * blocks + H) % (blocks * bands)).T.reshape(-1)
     moved = [(n, place) for n, place in enumerate(walk) if n != place]
     stays = jnp.asarray([n == place for n, place in enumerate(walk)])[band]
     index = jnp.where(stays, index, lax.ppermute(index, "space", moved))
@@ -763,10 +763,8 @@
         return jnp.where(stays, own, came.astype(jnp.float32))
 
     partner_by = partner - band * points - jnp.arange(points, dtype=jnp.int32)
-    partner_by = jnp.concatenate(
-        [shifted(partner_by[points - ROWW :], "space", 1), partner_by], 0
-    )[None, :]
-    low_valid = counted.astype(jnp.bfloat16)
+    coded = jnp.where(partner_by >= NEAR, partner_by - NEAR + 1, 0).astype(jnp.bfloat16)
+    low_valid = jnp.concatenate([counted.astype(jnp.bfloat16), coded[None, :]], 0)
     valid_around = jnp.concatenate(
         [
             shifted(low_valid[:, points - ROWW :], "space", 1),
@@ -779,9 +777,7 @@
     for layer in range(ROUNDS):
         before, after = halo(walk, sent[2 * (blocks - H) :], sent[: 2 * H])
         if layer == 0:
-            before, valid_around, partner_by = lax.optimization_barrier(
-                (before, valid_around, partner_by)
-            )
+            before, valid_around = lax.optimization_barrier((before, valid_around))
         following = w_round[layer + 1] if layer + 1 < ROUNDS else None
         new, back, update, agg, slopes, *rest = round_forward(
             index, mesh, before, sent, after, w_round[layer], b_round[layer], following
@@ -789,11 +785,12 @@
         kept.append((mesh, back, update, agg, slopes))
         mesh = new
         sent = rest[0] if rest else None
-    wide_valid = valid_around.astype(jnp.float32)
+    wide_valid = valid_around[:CH].astype(jnp.float32)
+    coded = valid_around[CH : CH + 1, : points + ROWW].astype(jnp.float32)
     weights = [
         (
             by,
-            jnp.where(partner_by == by, 1.0, 0.0)
+            jnp.where(coded == by - NEAR + 1, 1.0, 0.0)
             * wide_valid[:, : points + ROWW]
             * wide_valid[:, by : by + points + ROWW],
         )

time: 537 us -> 505 us (0.940)
  Pallas kernels: 215 us -> 181 us
  waiting for transfers between devices: 126 us -> 133 us
    pallas_call x6, Pallas kernels: 187 us -> 153 us  [the longest x3 78.6 us: edges_backward(): pl.pallas_call(body, grid_spec=pltpu.PrefetchScalarGridSpec(num_scalar_pr...]
    ppermute x6, starting transfers between devices: 5.56 us -> 19.1 us  [halo(): lax.ppermute(last, 'space', up)]
    ppermute x24, starting transfers between devices: 35.7 us -> 28.5 us  [swapped(): lax.ppermute(value, axis, [(i, i ^ bit) for i in range(lax.axis_size(axis...]
    ppermute x5 -> x4, starting transfers between devices: 13.5 us -> 10.5 us  [shifted(): return lax.ppermute(shard, axis, pairs)]
    ppermute x5 -> x4, waiting for transfers between devices: 18.5 us -> 16.1 us  [shifted(): return lax.ppermute(shard, axis, pairs)]
  transfers between devices with their start and end apart: 46 -> 45, of which waited for: 28 -> 29; matrix products, arithmetic and copies ran while one was open for 9% -> 9% of each run, Pallas kernels for 5% -> 5%
where the time goes in v9:
time: 505 us; the launch traced here: 501 us
  Pallas kernels  181 us (36%)
  waiting for transfers between devices  133 us (26%)
  starting transfers between devices  85 us (17%)
  matrix products  35.8 us (7%)
  other arithmetic  28.7 us (6%)
  local copies, waits for them, and re-layouts  15.2 us (3%)
  blocking collectives  14.2 us (3%)
  between operations  8.01 us (2%)
    pallas_call x3, Pallas kernels, edges_backward(): pl.pallas_call(body, grid_spec=pltpu.PrefetchScalarGridSpec(num_scalar_pr...  78.6 us
    pallas_call x3, Pallas kernels, round_forward(): pl.pallas_call(body, grid_spec=pltpu.PrefetchScalarGridSpec(num_scalar_pr...  74.2 us
    ppermute x6, waiting for transfers between devices, halo(): lax.ppermute(initial, 'space', down)  39.4 us
    ppermute x24, waiting for transfers between devices, swapped(): lax.ppermute(value, axis, [(i, i ^ bit) for i in range(lax.axis_size(axis...  35.7 us
    dot_general x24, matrix products, inner(): lax.dot_general(left, right, (((left_dim,), (right_dim,)), ((), ())), pre...  35.4 us
    ppermute x6, waiting for transfers between devices, halo(): lax.ppermute(last, 'space', up)  29.9 us
    ppermute x24, starting transfers between devices, swapped(): lax.ppermute(value, axis, [(i, i ^ bit) for i in range(lax.axis_size(axis...  28.5 us
    ppermute x6, starting transfers between devices, halo(): lax.ppermute(last, 'space', up)  19.1 us
  transfers between devices with their start and end apart: 45, of which 29 were waited for; matrix products, arithmetic and copies ran while one was open for 9% of the time, Pallas kernels for 5%

profile of v9, /device:TPU:0, one launch (start us, length us, event | category | flops | bytes accessed | tf_op | source)
XLA Modules:
  0.0 501.1 jit_solution(15496567377893770319)
XLA Ops:
  5.8 4.1 collective-permute-start.3
  17.6 3.0 collective-permute-done.4
  30.1 5.2 %all-to-all-start = ((bf16[16,64,128]{2,1,0:T(8,128)(2,1)}), bf16[16,64,128]{2,1,0:T(8,128)(2,1)S(1)}, u32[]{:S(2)}, u32[]{:S(2)}) async-start(bf16[16,64,128]{2,1,0:T(8,128)(2,1)} %bitcast.7), calls=%async_computation | async-start | bytes 524288 | tf_op jit(solution)/shard_map/all_to_all | solution.py:731
  37.2 6.6 %all-to-all-done = bf16[16,64,128]{2,1,0:T(8,128)(2,1)S(1)} async-done(((bf16[16,64,128]{2,1,0:T(8,128)(2,1)}), bf16[16,64,128]{2,1,0:T(8,128)(2,1)S(1)}, u32[]{:S(2)}, u32[]{:S(2)}) %all-to-all-start) | async-done | bytes 262176 | tf_op jit(solution)/shard_map/all_to_all | solution.py:731
  46.8 4.0 spread_rows.1
  50.8 5.8 %encode_rows.1 = (f32[2048,256]{1,0:T(8,128)}, bf16[2048,256]{1,0:T(8,128)(2,1)}, bf16[4096,128]{1,0:T(8,128)(2,1)}) custom-call(bf16[1024,128]{1,0:T(8,128)(2,1)} %bitcast.158, s32[1,1024]{1,0:T(1,128)} %bitcast.173, bf16[128,256]{1,0:T(8,128)(2,1)} %get-tuple-element.92.in_ref, bf16[256,256]{1,0:T(8,128)(2,1)} %get-tuple-element.93.node_ref, ...), custom_call_target="tpu_custom_call" | custom-call | bytes 15000000 | tf_op jit(solution)/shard_map/encode_rows/pallas_call | solution.py:624
  62.3 4.5 collective-permute-start.12
  68.1 10.5 %collective-permute-done.13 = bf16[79,360]{1,0:T(8,128)(2,1)S(1)} collective-permute-done((bf16[79,360]{1,0:T(8,128)(2,1)S(1)}, bf16[79,360]{1,0:T(8,128)(2,1)S(1)}, u32[]{:S(2)}, u32[]{:S(2)}) %collective-permute-start.13) | collective-permute-done | bytes 56912 | tf_op jit(solution)/shard_map/ppermute | solution.py:49
  79.6 2.5 collective-permute-done.11.refs_2_
  83.4 25.0 %round_forward.3 = (f32[2048,256]{1,0:T(8,128)}, f32[2048,256]{1,0:T(8,128)}, bf16[2048,256]{1,0:T(8,128)(2,1)}, bf16[2048,256]{1,0:T(8,128)(2,1)}, bf16[6,4096,...) custom-call(s32[12288]{0:T(1024)} %broadcast_select_fusion.refs_0_, f32[2048,256]{1,0:T(8,128)} %get-tuple-element.99.refs_1_, ...), custom_call_target="tpu_custom_call" | custom-call | bytes 75000000 | tf_op jit(solution)/shard_map/round_forward/pallas_call | solution.py:399
  110.4 17.6 %collective-permute-done.16.refs_4_ = bf16[4096,128]{1,0:T(8,128)(2,1)S(1)} collective-permute-done((bf16[4096,128]{1,0:T(8,128)(2,1)}, bf16[4096,128]{1,0:T(8,128)(2,1)S(1)}, u32[]{:S(2)}, u32[]{:S(2)}) %collective-permute-start.16) | collective-permute-done | bytes 1048608 | tf_op jit(solution)/shard_map/ppermute | solution.py:77
  128.0 2.5 collective-permute-done.15.refs_2_
  131.6 25.1 %round_forward.4 = (f32[2048,256]{1,0:T(8,128)}, f32[2048,256]{1,0:T(8,128)}, bf16[2048,256]{1,0:T(8,128)(2,1)}, bf16[2048,256]{1,0:T(8,128)(2,1)}, bf16[6,4096,...) custom-call(s32[12288]{0:T(1024)} %broadcast_select_fusion.refs_0_, f32[2048,256]{1,0:T(8,128)} %get-tuple-element.104.refs_1_, ...), custom_call_target="tpu_custom_call" | custom-call | bytes 75000000 | tf_op jit(solution)/shard_map/round_forward/pallas_call | solution.py:399
  157.4 5.1 %collective-permute-start.17 = (bf16[4096,128]{1,0:T(8,128)(2,1)}, bf16[4096,128]{1,0:T(8,128)(2,1)S(1)}, u32[]{:S(2)}, u32[]{:S(2)}) collective-permute-start(bf16[4096,128]{1,0:T(8,128)(2,1)} %get-tuple-element.108.refs_3_), channel_id=1, source_target_pairs={{0,1},{1,3},{3,2},{2,6},{6,4},{4,5},{5,7},{7,11},{11,9},{9,8},{8,1... | collective-permute-start | bytes 3145736 | tf_op jit(solution)/shard_map/ppermute | solution.py:77
  163.4 21.8 %collective-permute-done.18.refs_4_ = bf16[4096,128]{1,0:T(8,128)(2,1)S(1)} collective-permute-done((bf16[4096,128]{1,0:T(8,128)(2,1)}, bf16[4096,128]{1,0:T(8,128)(2,1)S(1)}, u32[]{:S(2)}, u32[]{:S(2)}) %collective-permute-start.18) | collective-permute-done | bytes 1048608 | tf_op jit(solution)/shard_map/ppermute | solution.py:77
  186.5 24.1 %round_forward.5 = (f32[2048,256]{1,0:T(8,128)}, f32[2048,256]{1,0:T(8,128)}, bf16[2048,256]{1,0:T(8,128)(2,1)}, bf16[2048,256]{1,0:T(8,128)(2,1)}, bf16[6,4096,128]{2,1,0:T(8,128)(2,1)}) custom-call(s32[12288]{0:T(1024)} %broadcast_select_fusion.refs_0_, f32[2048,256]{1,0:T(8,128)} %get-tuple-element.107.refs_1_, bf16[4096,128]{1,0:T(8,128)(2,1)} %copy-done.29, ...), custom_call_target="tpu_custom_call" | custom-call | bytes 75000000 | tf_op jit(solution)/shard_map/round_forward/pallas_call | solution.py:399
  210.6 2.7 convert_element_type.206
  213.3 2.7 fusion.8
  217.5 5.0 %all-to-all-start.1 = ((bf16[16,64,128]{2,1,0:T(8,128)(2,1)}), bf16[16,64,128]{2,1,0:T(8,128)(2,1)S(1)}, u32[]{:S(2)}, u32[]{:S(2)}) async-start(bf16[16,64,128]{2,1,0:T(8,128)(2,1)} %bitcast.17), calls=%async_computation.1 | async-start | bytes 524288 | tf_op jit(solution)/shard_map/all_to_all | solution.py:731
  225.2 5.8 %all-to-all-done.1 = bf16[16,64,128]{2,1,0:T(8,128)(2,1)S(1)} async-done(((bf16[16,64,128]{2,1,0:T(8,128)(2,1)}), bf16[16,64,128]{2,1,0:T(8,128)(2,1)S(1)}, u32[]{:S(2)}, u32[]{:S(2)}) %all-to-all-start.1) | async-done | bytes 262176 | tf_op jit(solution)/shard_map/all_to_all | solution.py:731
  231.7 3.3 collective-permute-start.19
  236.3 4.8 collective-permute-done.20
  243.4 14.2 %all_to_all.15 = bf16[16,64,128]{2,1,0:T(8,128)(2,1)S(1)} all-to-all(bf16[16,64,128]{2,1,0:T(8,128)(2,1)S(1)} %bitcast.171), channel_id=1, replica_groups=mesh['dp'=2,'space'=16] {'space'}, dimensions={0} | all-to-all | bytes 524288 | tf_op jit(solution)/shard_map/all_to_all | solution.py:731
  259.8 3.9 fusion.refs_1_
  265.4 24.1 %edges_backward.3 = (bf16[2048,256]{1,0:T(8,128)(2,1)}, bf16[2048,256]{1,0:T(8,128)(2,1)}, bf16[4096,128]{1,0:T(8,128)(2,1)}, f32[4096,128]{1,0:T(8,128)}, bf16[4096,128]{1,0:T(8,128)(2,1)}) custom-call(s32[12288]{0:T(1024)} %broadcast_select_fusion.refs_0_, f32[2048,256]{1,0:T(8,128)} %fusion.refs_1_, f32[2048,256]{1,0:T(8,128)} %get-tuple-element.117.refs_2_, ...), custom_call_target="tpu_custom_call" | custom-call | bytes 75000000 | tf_op jit(solution)/shard_map/edges_backward/pallas_call | solution.py:521
  290.6 2.7 fusion.111.refs_16_
  295.7 12.7 %collective-permute-start.22 = (bf16[4096,128]{1,0:T(8,128)(2,1)S(1)}, bf16[4096,128]{1,0:T(8,128)(2,1)}, u32[]{:S(2)}, u32[]{:S(2)}) collective-permute-start(bf16[4096,128]{1,0:T(8,128)(2,1)S(1)} %copy-done.49), channel_id=1, source_target_pairs={{0,1},{1,3},{3,2},{2,6},{6,4},{4,5},{5,7},{7,11},{11,9},{9,8},{8,1... | collective-permute-start | bytes 3145736 | tf_op jit(solution)/shard_map/ppermute | solution.py:77
  308.5 2.4 collective-permute-start.23
  313.4 3.4 convert_select_fusion
  316.8 10.8 %collective-permute-done.22.refs_6_ = bf16[4096,128]{1,0:T(8,128)(2,1)} collective-permute-done((bf16[4096,128]{1,0:T(8,128)(2,1)S(1)}, bf16[4096,128]{1,0:T(8,128)(2,1)}, u32[]{:S(2)}, u32[]{:S(2)}) %collective-permute-start.22) | collective-permute-done | bytes 1048608 | tf_op jit(solution)/shard_map/ppermute | solution.py:77
  327.7 27.2 %edges_backward.4 = (f32[2048,256]{1,0:T(8,128)}, bf16[2048,256]{1,0:T(8,128)(2,1)}, bf16[2048,256]{1,0:T(8,128)(2,1)}, bf16[2048,256]{1,0:T(8,128)(2,1)}, bf16[...) custom-call(s32[12288]{0:T(1024)} %broadcast_select_fusion.refs_0_, ...), custom_call_target="tpu_custom_call" | custom-call | bytes 84000000 | tf_op jit(solution)/shard_map/edges_backward/pallas_call | solution.py:521
  355.7 3.1 collective-permute-start.25
  358.8 2.6 fusion.109.refs_11_
  367.0 7.8 %collective-permute-done.24.refs_6_ = bf16[4096,128]{1,0:T(8,128)(2,1)} collective-permute-done((bf16[4096,128]{1,0:T(8,128)(2,1)}, bf16[4096,128]{1,0:T(8,128)(2,1)}, u32[]{:S(2)}, u32[]{:S(2)}) %collective-permute-start.24) | collective-permute-done | bytes 1048608 | tf_op jit(solution)/shard_map/ppermute | solution.py:77
  374.8 27.2 %edges_backward.5 = (f32[2048,256]{1,0:T(8,128)}, bf16[2048,256]{1,0:T(8,128)(2,1)}, bf16[2048,256]{1,0:T(8,128)(2,1)}, bf16[2048,256]{1,0:T(8,128)(2,1)}, bf16[...) custom-call(s32[12288]{0:T(1024)} %broadcast_select_fusion.refs_0_, ...), custom_call_target="tpu_custom_call" | custom-call | bytes 84000000 | tf_op jit(solution)/shard_map/edges_backward/pallas_call | solution.py:521
  402.2 3.8 collective-permute-start.27
  406.0 2.6 fusion.107.refs_6_
  414.9 6.2 %collective-permute-done.26.refs_2_ = bf16[4096,128]{1,0:T(8,128)(2,1)} collective-permute-done((bf16[4096,128]{1,0:T(8,128)(2,1)}, bf16[4096,128]{1,0:T(8,128)(2,1)}, u32[]{:S(2)}, u32[]{:S(2)}) %collective-permute-start.26) | collective-permute-done | bytes 1048608 | tf_op jit(solution)/shard_map/ppermute | solution.py:77
  421.1 6.1 %round_backward.1 = (f32[2048,256]{1,0:T(8,128)}, bf16[2048,256]{1,0:T(8,128)(2,1)}, bf16[2048,256]{1,0:T(8,128)(2,1)}) custom-call(f32[2048,256]{1,0:T(8,128)} %get-tuple-element.137.refs_0_, f32[4096,128]{1,0:T(8,128)} %get-tuple-element.138.refs_1_, bf16[4096,128]{1,0:T(8,128)(2,1)} %collective-permute-done.26.refs_2_, ...), custom_call_target="tpu_custom_call" | custom-call | bytes 21000000 | tf_op jit(solution)/shard_map/round_backward/pallas_call | solution.py:588
  427.3 2.4 fusion.89.refs_4_
  429.7 6.9 %encode_backward.1 = (f32[128,256]{1,0:T(8,128)}, f32[256,256]{1,0:T(8,128)}, f32[2,256]{1,0:T(2,128)}) custom-call(f32[2048,256]{1,0:T(8,128)} %get-tuple-element.143.grad_ref, bf16[2048,256]{1,0:T(8,128)(2,1)} %get-tuple-element.144.gathered_ref, bf16[1024,128]{1,0:T(8,128)(2,1)} %bitcast.159, s32[1024,1]{1,0:T(8,128)} %get-tuple-element.202.ids_ref, ...), custom_call_target="tpu_custom_call" | custom-call | bytes 21000000 | tf_op jit(solution)/shard_map/encode_backward/pallas_call | solution.py:675
  436.6 5.1 %collect_rows.1 = (f32[16,144,256]{2,1,0:T(8,128)}, bf16[16,144,256]{2,1,0:T(8,128)(2,1)}) custom-call(s32[1]{0:T(128)} %bitcast.9.place_ref, f32[128,256]{1,0:T(8,128)} %get-tuple-element.145.refs_0_, f32[256,256]{1,0:T(8,128)} %get-tuple-element.146.refs_1_, f32[256,256]{1,0:T(8,128)} %fusion.106.refs_2_, f32[78,256]{1,0:T(8,128)} %reshape.160.refs_3_, ...), custom_call_target="tpu_custom_call" | custom-call | bytes 15000000 | tf_op jit(solution)/shard_map/collect_rows/pallas_call | solution.py:229
  441.7 3.0 collective-permute-done.28
  448.4 7.7 %collective-permute-done.31 = bf16[2,2,2,72,256]{4,3,2,1,0:T(8,128)(2,1)S(1)} collective-permute-done((bf16[2,2,2,72,256]{4,3,2,1,0:T(8,128)(2,1)S(1)}, bf16[2,2,2,72,256]{4,3,2,1,0:T(8,128)(2,1)S(1)}, u32[]{:S(2)}, u32[]{:S(2)}) %collective-permute-start.31) | collective-permute-done | bytes 294944 | tf_op jit(solution)/shard_map/ppermute | solution.py:94
  467.3 3.9 collective-permute-start.36
  473.4 2.7 collective-permute-done.34
  479.5 3.8 collective-permute-done.38
  487.0 4.0 collective-permute-start.41
  (276 shorter events, 100.8 us)
Async XLA Ops:
  5.8 9.6 %collective-permute-start.3 = (bf16[1,72,256]{2,1,0:T(8,128)(2,1)S(1)}, bf16[1,72,256]{2,1,0:T(8,128)(2,1)S(1)}, u32[]{:S(2)}, u32[]{:S(2)}) collective-permute-start(bf16[1,72,256]{2,1,0:T(8,128)(2,1)S(1)} %get-tuple-element.216), channel_id=1, source_target_pairs={{0,8},{1,9},{2,10},{3,11},{4,12},{5,13},{6,14},{7,15},{8,0},{9,1},... | collective-permute-start | bytes 110600 | tf_op jit(solution)/shard_map/ppermute | solution.py:94
  9.9 7.5 %collective-permute-start = (bf16[1,72,256]{2,1,0:T(8,128)(2,1)S(1)}, bf16[1,72,256]{2,1,0:T(8,128)(2,1)S(1)}, u32[]{:S(2)}, u32[]{:S(2)}) collective-permute-start(bf16[1,72,256]{2,1,0:T(8,128)(2,1)S(1)} %get-tuple-element.217), channel_id=1, source_target_pairs={{0,8},{1,9},{2,10},{3,11},{4,12},{5,13},{6,14},{7,15},{8,0},{9,1},... | collective-permute-start | bytes 110600 | tf_op jit(solution)/shard_map/ppermute | solution.py:94
  15.4 5.2 %collective-permute-start.4 = (bf16[2,72,256]{2,1,0:T(8,128)(2,1)S(1)}, bf16[2,72,256]{2,1,0:T(8,128)(2,1)S(1)}, u32[]{:S(2)}, u32[]{:S(2)}) collective-permute-start(bf16[2,72,256]{2,1,0:T(8,128)(2,1)S(1)} %pad_maximum_fusion.8), channel_id=1, source_target_pairs={{0,4},{1,5},{2,6},{3,7},{4,0},{5,1},{6,2},{7,3},{8,12},{9,13},{10,... | collective-permute-start | bytes 221192 | tf_op jit(solution)/shard_map/ppermute | solution.py:94
  17.3 4.8 collective-permute-start.1
  20.6 5.2 %collective-permute-start.5 = (bf16[4,72,256]{2,1,0:T(8,128)(2,1)S(1)}, bf16[4,72,256]{2,1,0:T(8,128)(2,1)S(1)}, u32[]{:S(2)}, u32[]{:S(2)}) collective-permute-start(bf16[4,72,256]{2,1,0:T(8,128)(2,1)S(1)} %pad_maximum_fusion.5), channel_id=1, source_target_pairs={{0,1},{1,0},{2,3},{3,2},{4,5},{5,4},{6,7},{7,6},{8,9},{9,8},{10,11... | collective-permute-start | bytes 442376 | tf_op jit(solution)/shard_map/ppermute | solution.py:94
  22.2 5.2 %collective-permute-start.2 = (bf16[4,72,256]{2,1,0:T(8,128)(2,1)S(1)}, bf16[4,72,256]{2,1,0:T(8,128)(2,1)S(1)}, u32[]{:S(2)}, u32[]{:S(2)}) collective-permute-start(bf16[4,72,256]{2,1,0:T(8,128)(2,1)S(1)} %pad_maximum_fusion.4), channel_id=1, source_target_pairs={{0,2},{1,3},{2,0},{3,1},{4,6},{5,7},{6,4},{7,5},{8,10},{9,11},{10,... | collective-permute-start | bytes 442376 | tf_op jit(solution)/shard_map/ppermute | solution.py:94
  27.4 7.9 %collective-permute-start.7 = (bf16[8,72,256]{2,1,0:T(8,128)(2,1)S(1)}, bf16[8,72,256]{2,1,0:T(8,128)(2,1)S(1)}, u32[]{:S(2)}, u32[]{:S(2)}) collective-permute-start(bf16[8,72,256]{2,1,0:T(8,128)(2,1)S(1)} %pad_maximum_fusion.2), channel_id=1, source_target_pairs={{0,2},{1,3},{2,0},{3,1},{4,6},{5,7},{6,4},{7,5},{8,10},{9,11},{10,... | collective-permute-start | bytes 884744 | tf_op jit(solution)/shard_map/ppermute | solution.py:94
  29.0 7.4 %collective-permute-start.6 = (bf16[8,72,256]{2,1,0:T(8,128)(2,1)S(1)}, bf16[8,72,256]{2,1,0:T(8,128)(2,1)S(1)}, u32[]{:S(2)}, u32[]{:S(2)}) collective-permute-start(bf16[8,72,256]{2,1,0:T(8,128)(2,1)S(1)} %pad_maximum_fusion.1), channel_id=1, source_target_pairs={{0,1},{1,0},{2,3},{3,2},{4,5},{5,4},{6,7},{7,6},{8,9},{9,8},{10,11... | collective-permute-start | bytes 884744 | tf_op jit(solution)/shard_map/ppermute | solution.py:94
  30.1 13.7 %all-to-all-start = ((bf16[16,64,128]{2,1,0:T(8,128)(2,1)}), bf16[16,64,128]{2,1,0:T(8,128)(2,1)S(1)}, u32[]{:S(2)}, u32[]{:S(2)}) async-start(bf16[16,64,128]{2,1,0:T(8,128)(2,1)} %bitcast.7), calls=%async_computation | async-start | bytes 524288 | tf_op jit(solution)/shard_map/all_to_all | solution.py:731
  35.4 10.3 %collective-permute-start.9 = (bf16[16,72,256]{2,1,0:T(8,128)(2,1)S(1)}, bf16[16,72,256]{2,1,0:T(8,128)(2,1)S(1)}, u32[]{:S(2)}, u32[]{:S(2)}) collective-permute-start(bf16[16,72,256]{2,1,0:T(8,128)(2,1)S(1)} %constant_dynamic-update-slice_fusion.2.refs_1_), channel_id=1, source_target_pairs={{0,16},{16,0},{1,17},{17,1},{2,18},{18,2},{3,19},{19,3},{4,20},{20... | collective-permute-start | bytes 1769480 | tf_op jit(solution)/shard_map/ppermute | solution.py:94
  36.5 9.2 %collective-permute-start.8 = (bf16[16,72,256]{2,1,0:T(8,128)(2,1)S(1)}, bf16[16,72,256]{2,1,0:T(8,128)(2,1)S(1)}, u32[]{:S(2)}, u32[]{:S(2)}) collective-permute-start(bf16[16,72,256]{2,1,0:T(8,128)(2,1)S(1)} %constant_dynamic-update-slice_fusion.refs_0_), channel_id=1, source_target_pairs={{0,16},{16,0},{1,17},{17,1},{2,18},{18,2},{3,19},{19,3},{4,20},{20... | collective-permute-start | bytes 1769480 | tf_op jit(solution)/shard_map/ppermute | solution.py:94
  56.6 25.5 %collective-permute-start.14 = (bf16[4096,128]{1,0:T(8,128)(2,1)}, bf16[4096,128]{1,0:T(8,128)(2,1)S(1)}, u32[]{:S(2)}, u32[]{:S(2)}) collective-permute-start(bf16[4096,128]{1,0:T(8,128)(2,1)} %get-tuple-element.100.refs_3_), channel_id=1, source_target_pairs={{1,0},{3,1},{2,3},{6,2},{4,6},{5,4},{7,5},{11,7},{9,11},{8,9},{10,... | collective-permute-start | bytes 3145736 | tf_op jit(solution)/shard_map/ppermute | solution.py:77
  58.4 23.7 %collective-permute-start.11 = (bf16[4096,128]{1,0:T(8,128)(2,1)}, bf16[4096,128]{1,0:T(8,128)(2,1)S(1)}, u32[]{:S(2)}, u32[]{:S(2)}) collective-permute-start(bf16[4096,128]{1,0:T(8,128)(2,1)} %get-tuple-element.100.refs_3_), channel_id=1, source_target_pairs={{0,1},{1,3},{3,2},{2,6},{6,4},{4,5},{5,7},{7,11},{11,9},{9,8},{8,1... | collective-permute-start | bytes 3145736 | tf_op jit(solution)/shard_map/ppermute | solution.py:77
  58.7 8.1 %collective-permute-start.10 = (s32[12288]{0:T(1024)S(1)}, s32[12288]{0:T(1024)S(1)}, u32[]{:S(2)}, u32[]{:S(2)}) collective-permute-start(s32[12288]{0:T(1024)S(1)} %mul.208), channel_id=1, source_target_pairs={{2,3},{3,2},{4,6},{5,4},{6,5},{8,11},{10,8},{11,10},{12,14},{13,15... | collective-permute-start | bytes 147464 | tf_op jit(solution)/shard_map/ppermute | solution.py:757
  61.0 17.6 %collective-permute-start.13 = (bf16[79,360]{1,0:T(8,128)(2,1)S(1)}, bf16[79,360]{1,0:T(8,128)(2,1)S(1)}, u32[]{:S(2)}, u32[]{:S(2)}) collective-permute-start(bf16[79,360]{1,0:T(8,128)(2,1)S(1)} %get-tuple-element.212), channel_id=1, source_target_pairs={{1,0},{2,1},{3,2},{4,3},{5,4},{6,5},{7,6},{8,7},{9,8},{10,9},{11,1... | collective-permute-start | bytes 170648 | tf_op jit(solution)/shard_map/ppermute | solution.py:49
  62.3 17.2 %collective-permute-start.12 = (bf16[79,360]{1,0:T(8,128)(2,1)S(1)}, bf16[79,360]{1,0:T(8,128)(2,1)S(1)}, u32[]{:S(2)}, u32[]{:S(2)}) collective-permute-start(bf16[79,360]{1,0:T(8,128)(2,1)S(1)} %get-tuple-element.213), channel_id=1, source_target_pairs={{0,1},{1,2},{2,3},{3,4},{4,5},{5,6},{6,7},{7,8},{8,9},{9,10},{10,1... | collective-permute-start | bytes 170648 | tf_op jit(solution)/shard_map/ppermute | solution.py:49
  108.3 19.7 %collective-permute-start.16 = (bf16[4096,128]{1,0:T(8,128)(2,1)}, bf16[4096,128]{1,0:T(8,128)(2,1)S(1)}, u32[]{:S(2)}, u32[]{:S(2)}) collective-permute-start(bf16[4096,128]{1,0:T(8,128)(2,1)} %get-tuple-element.105.refs_3_), channel_id=1, source_target_pairs={{1,0},{3,1},{2,3},{6,2},{4,6},{5,4},{7,5},{11,7},{9,11},{8,9},{10,... | collective-permute-start | bytes 3145736 | tf_op jit(solution)/shard_map/ppermute | solution.py:77
  110.2 20.3 %collective-permute-start.15 = (bf16[4096,128]{1,0:T(8,128)(2,1)}, bf16[4096,128]{1,0:T(8,128)(2,1)S(1)}, u32[]{:S(2)}, u32[]{:S(2)}) collective-permute-start(bf16[4096,128]{1,0:T(8,128)(2,1)} %get-tuple-element.105.refs_3_), channel_id=1, source_target_pairs={{0,1},{1,3},{3,2},{2,6},{6,4},{4,5},{5,7},{7,11},{11,9},{9,8},{8,1... | collective-permute-start | bytes 3145736 | tf_op jit(solution)/shard_map/ppermute | solution.py:77
  131.6 31.6 %copy-start.43 = (bf16[78,256]{1,0:T(8,128)(2,1)S(1)}, bf16[78,256]{1,0:T(8,128)(2,1)}, u32[]{:S(2)}) copy-start(bf16[78,256]{1,0:T(8,128)(2,1)} %get-tuple-element.111) | copy-start | bytes 119812
  156.6 28.6 %collective-permute-start.18 = (bf16[4096,128]{1,0:T(8,128)(2,1)}, bf16[4096,128]{1,0:T(8,128)(2,1)S(1)}, u32[]{:S(2)}, u32[]{:S(2)}) collective-permute-start(bf16[4096,128]{1,0:T(8,128)(2,1)} %get-tuple-element.108.refs_3_), channel_id=1, source_target_pairs={{1,0},{3,1},{2,3},{6,2},{4,6},{5,4},{7,5},{11,7},{9,11},{8,9},{10,... | collective-permute-start | bytes 3145736 | tf_op jit(solution)/shard_map/ppermute | solution.py:77
  157.4 27.8 %collective-permute-start.17 = (bf16[4096,128]{1,0:T(8,128)(2,1)}, bf16[4096,128]{1,0:T(8,128)(2,1)S(1)}, u32[]{:S(2)}, u32[]{:S(2)}) collective-permute-start(bf16[4096,128]{1,0:T(8,128)(2,1)} %get-tuple-element.108.refs_3_), channel_id=1, source_target_pairs={{0,1},{1,3},{3,2},{2,6},{6,4},{4,5},{5,7},{7,11},{11,9},{9,8},{8,1... | collective-permute-start | bytes 3145736 | tf_op jit(solution)/shard_map/ppermute | solution.py:77
  163.4 53.0 %copy-start.41 = (bf16[256,78]{1,0:T(8,128)(2,1)}, bf16[256,78]{1,0:T(8,128)(2,1)S(1)}, u32[]{:S(2)}) copy-start(bf16[256,78]{1,0:T(8,128)(2,1)S(1)} %reshape.155) | copy-start | bytes 119812
  217.5 13.5 %all-to-all-start.1 = ((bf16[16,64,128]{2,1,0:T(8,128)(2,1)}), bf16[16,64,128]{2,1,0:T(8,128)(2,1)S(1)}, u32[]{:S(2)}, u32[]{:S(2)}) async-start(bf16[16,64,128]{2,1,0:T(8,128)(2,1)} %bitcast.17), calls=%async_computation.1 | async-start | bytes 524288 | tf_op jit(solution)/shard_map/all_to_all | solution.py:731
  231.7 9.5 %collective-permute-start.19 = (bf16[78,360]{1,0:T(8,128)(2,1)S(1)}, bf16[78,360]{1,0:T(8,128)(2,1)S(1)}, u32[]{:S(2)}, u32[]{:S(2)}) collective-permute-start(bf16[78,360]{1,0:T(8,128)(2,1)S(1)} %get-tuple-element.214), channel_id=1, source_target_pairs={{0,1},{1,2},{2,3},{3,4},{4,5},{5,6},{6,7},{7,8},{8,9},{9,10},{10,1... | collective-permute-start | bytes 168488 | tf_op jit(solution)/shard_map/ppermute | solution.py:49
  235.0 6.1 %collective-permute-start.20 = (bf16[78,360]{1,0:T(8,128)(2,1)S(1)}, bf16[78,360]{1,0:T(8,128)(2,1)S(1)}, u32[]{:S(2)}, u32[]{:S(2)}) collective-permute-start(bf16[78,360]{1,0:T(8,128)(2,1)S(1)} %get-tuple-element.215), channel_id=1, source_target_pairs={{1,0},{2,1},{3,2},{4,3},{5,4},{6,5},{7,6},{8,7},{9,8},{10,9},{11,1... | collective-permute-start | bytes 168488 | tf_op jit(solution)/shard_map/ppermute | solution.py:49
  263.8 32.0 %collective-permute-start.21 = (bf16[2048,256]{1,0:T(8,128)(2,1)}, bf16[2048,256]{1,0:T(8,128)(2,1)}, u32[]{:S(2)}, u32[]{:S(2)}) collective-permute-start(bf16[2048,256]{1,0:T(8,128)(2,1)} %convert_element_type.206), channel_id=1, source_target_pairs={{3,2},{2,3},{6,4},{4,5},{5,6},{11,8},{8,10},{10,11},{14,12},{15,13... | collective-permute-start | bytes 3145736 | tf_op jit(solution)/shard_map/ppermute | solution.py:760
  295.7 31.9 %collective-permute-start.22 = (bf16[4096,128]{1,0:T(8,128)(2,1)S(1)}, bf16[4096,128]{1,0:T(8,128)(2,1)}, u32[]{:S(2)}, u32[]{:S(2)}) collective-permute-start(bf16[4096,128]{1,0:T(8,128)(2,1)S(1)} %copy-done.49), channel_id=1, source_target_pairs={{0,1},{1,3},{3,2},{2,6},{6,4},{4,5},{5,7},{7,11},{11,9},{9,8},{8,1... | collective-permute-start | bytes 3145736 | tf_op jit(solution)/shard_map/ppermute | solution.py:77
  308.5 19.2 %collective-permute-start.23 = (bf16[4096,128]{1,0:T(8,128)(2,1)S(1)}, bf16[4096,128]{1,0:T(8,128)(2,1)}, u32[]{:S(2)}, u32[]{:S(2)}) collective-permute-start(bf16[4096,128]{1,0:T(8,128)(2,1)S(1)} %copy-done.48), channel_id=1, source_target_pairs={{1,0},{3,1},{2,3},{6,2},{4,6},{5,4},{7,5},{11,7},{9,11},{8,9},{10,... | collective-permute-start | bytes 3145736 | tf_op jit(solution)/shard_map/ppermute | solution.py:77
  354.9 20.0 %collective-permute-start.24 = (bf16[4096,128]{1,0:T(8,128)(2,1)}, bf16[4096,128]{1,0:T(8,128)(2,1)}, u32[]{:S(2)}, u32[]{:S(2)}) collective-permute-start(bf16[4096,128]{1,0:T(8,128)(2,1)} %get-tuple-element.133), channel_id=1, source_target_pairs={{0,1},{1,3},{3,2},{2,6},{6,4},{4,5},{5,7},{7,11},{11,9},{9,8},{8,1... | collective-permute-start | bytes 3145736 | tf_op jit(solution)/shard_map/ppermute | solution.py:77
  355.7 19.2 %collective-permute-start.25 = (bf16[4096,128]{1,0:T(8,128)(2,1)}, bf16[4096,128]{1,0:T(8,128)(2,1)}, u32[]{:S(2)}, u32[]{:S(2)}) collective-permute-start(bf16[4096,128]{1,0:T(8,128)(2,1)} %get-tuple-element.134), channel_id=1, source_target_pairs={{1,0},{3,1},{2,3},{6,2},{4,6},{5,4},{7,5},{11,7},{9,11},{8,9},{10,... | collective-permute-start | bytes 3145736 | tf_op jit(solution)/shard_map/ppermute | solution.py:77
  402.1 19.0 %collective-permute-start.26 = (bf16[4096,128]{1,0:T(8,128)(2,1)}, bf16[4096,128]{1,0:T(8,128)(2,1)}, u32[]{:S(2)}, u32[]{:S(2)}) collective-permute-start(bf16[4096,128]{1,0:T(8,128)(2,1)} %get-tuple-element.139), channel_id=1, source_target_pairs={{0,1},{1,3},{3,2},{2,6},{6,4},{4,5},{5,7},{7,11},{11,9},{9,8},{8,1... | collective-permute-start | bytes 3145736 | tf_op jit(solution)/shard_map/ppermute | solution.py:77
  402.2 19.0 %collective-permute-start.27 = (bf16[4096,128]{1,0:T(8,128)(2,1)}, bf16[4096,128]{1,0:T(8,128)(2,1)}, u32[]{:S(2)}, u32[]{:S(2)}) collective-permute-start(bf16[4096,128]{1,0:T(8,128)(2,1)} %get-tuple-element.140), channel_id=1, source_target_pairs={{1,0},{3,1},{2,3},{6,2},{4,6},{5,4},{7,5},{11,7},{9,11},{8,9},{10,... | collective-permute-start | bytes 3145736 | tf_op jit(solution)/shard_map/ppermute | solution.py:77
  441.7 3.1 collective-permute-start.28
  446.9 9.1 %collective-permute-start.31 = (bf16[2,2,2,72,256]{4,3,2,1,0:T(8,128)(2,1)S(1)}, bf16[2,2,2,72,256]{4,3,2,1,0:T(8,128)(2,1)S(1)}, u32[]{:S(2)}, u32[]{:S(2)}) collective-permute-start(bf16[2,2,2,72,256]{4,3,2,1,0:T(8,128)(2,1)S(1)} %fusion.21), channel_id=1, source_target_pairs={{0,2},{1,3},{2,0},{3,1},{4,6},{5,7},{6,4},{7,5},{8,10},{9,11},{10,... | collective-permute-start | bytes 884744 | tf_op jit(solution)/shard_map/ppermute | solution.py:94
  448.3 9.1 %collective-permute-start.29 = (bf16[2,2,2,72,256]{4,3,0,1,2:T(8,128)(2,1)S(1)}, bf16[2,2,2,72,256]{4,3,0,1,2:T(8,128)(2,1)S(1)}, u32[]{:S(2)}, u32[]{:S(2)}) collective-permute-start(bf16[2,2,2,72,256]{4,3,0,1,2:T(8,128)(2,1)S(1)} %fusion.22), channel_id=1, source_target_pairs={{0,1},{1,0},{2,3},{3,2},{4,5},{5,4},{6,7},{7,6},{8,9},{9,8},{10,11... | collective-permute-start | bytes 884744 | tf_op jit(solution)/shard_map/ppermute | solution.py:94
  456.1 5.2 %collective-permute-start.32 = (bf16[2,2,72,256]{3,2,1,0:T(8,128)(2,1)S(1)}, bf16[2,2,72,256]{3,2,1,0:T(8,128)(2,1)S(1)}, u32[]{:S(2)}, u32[]{:S(2)}) collective-permute-start(bf16[2,2,72,256]{3,2,1,0:T(8,128)(2,1)S(1)} %fusion.49), channel_id=1, source_target_pairs={{0,1},{1,0},{2,3},{3,2},{4,5},{5,4},{6,7},{7,6},{8,9},{9,8},{10,11... | collective-permute-start | bytes 442376 | tf_op jit(solution)/shard_map/ppermute | solution.py:94
  457.5 35.7 %copy-start.11 = (f32[2048,256]{1,0:T(8,128)S(1)}, f32[2048,256]{1,0:T(8,128)}, u32[]{:S(2)}) copy-start(f32[2048,256]{1,0:T(8,128)} %get-tuple-element.143.grad_ref) | copy-start | bytes 6291460
  457.5 5.3 %collective-permute-start.30 = (bf16[2,2,72,256]{3,2,0,1:T(8,128)(2,1)S(1)}, bf16[2,2,72,256]{3,2,0,1:T(8,128)(2,1)S(1)}, u32[]{:S(2)}, u32[]{:S(2)}) collective-permute-start(bf16[2,2,72,256]{3,2,0,1:T(8,128)(2,1)S(1)} %fusion.48), channel_id=1, source_target_pairs={{0,2},{1,3},{2,0},{3,1},{4,6},{5,7},{6,4},{7,5},{8,10},{9,11},{10,... | collective-permute-start | bytes 442376 | tf_op jit(solution)/shard_map/ppermute | solution.py:94
  462.9 4.4 collective-permute-start.35
  463.0 8.2 %collective-permute-start.33 = (bf16[2,72,256]{2,1,0:T(8,128)(2,1)S(1)}, bf16[2,72,256]{2,1,0:T(8,128)(2,1)S(1)}, u32[]{:S(2)}, u32[]{:S(2)}) collective-permute-start(bf16[2,72,256]{2,1,0:T(8,128)(2,1)S(1)} %fusion.52), channel_id=1, source_target_pairs={{0,4},{1,5},{2,6},{3,7},{4,0},{5,1},{6,2},{7,3},{8,12},{9,13},{10,... | collective-permute-start | bytes 221192 | tf_op jit(solution)/shard_map/ppermute | solution.py:94
  465.0 22.0 %collective-permute-start.40 = (bf16[2048,256]{1,0:T(8,128)(2,1)S(1)}, bf16[2048,256]{1,0:T(8,128)(2,1)S(1)}, u32[]{:S(2)}, u32[]{:S(2)}) collective-permute-start(bf16[2048,256]{1,0:T(8,128)(2,1)S(1)} %copy-done.47), channel_id=1, source_target_pairs={{3,2},{2,3},{6,4},{4,5},{5,6},{11,8},{8,10},{10,11},{14,12},{15,13... | collective-permute-start | bytes 3145736 | tf_op jit(solution)/shard_map/ppermute | solution.py:760
  467.3 6.1 %collective-permute-start.36 = (bf16[72,256]{1,0:T(8,128)(2,1)S(1)}, bf16[72,256]{1,0:T(8,128)(2,1)S(1)}, u32[]{:S(2)}, u32[]{:S(2)}) collective-permute-start(bf16[72,256]{1,0:T(8,128)(2,1)S(1)} %fusion.64), channel_id=1, source_target_pairs={{0,8},{1,9},{2,10},{3,11},{4,12},{5,13},{6,14},{7,15},{8,0},{9,1},... | collective-permute-start | bytes 110600 | tf_op jit(solution)/shard_map/ppermute | solution.py:94
  471.2 4.9 collective-permute-start.34
  477.6 1.2 collective-permute-start.37
  478.9 4.5 collective-permute-start.38
  483.4 3.6 collective-permute-start.39
  487.0 5.6 %collective-permute-start.41 = (f32[8,128]{1,0:T(8,128)S(1)}, f32[8,128]{1,0:T(8,128)S(1)}, u32[]{:S(2)}, u32[]{:S(2)}) collective-permute-start(f32[8,128]{1,0:T(8,128)S(1)} %add.198), channel_id=1, source_target_pairs={{0,2},{1,3},{2,0},{3,1},{4,6},{5,7},{6,4},{7,5},{8,10},{9,11},{10,... | collective-permute-start | bytes 12296 | tf_op jit(solution)/shard_map/ppermute | solution.py:94
  492.6 3.7 collective-permute-start.42
  (49 other events, 341.1 us)

commit v10 on v9

--- a/solution.py
+++ b/solution.py
@@ -98,42 +98,54 @@
     return [1 << n for n in range(lax.axis_size(axis).bit_length() - 1)]
 
 
+def others(value, axis, bits):
+    masks = [sum(bit for n, bit in enumerate(bits) if m >> n & 1) for m in range(1, 1 << len(bits))]
+    return [swapped(value, axis, mask) for mask in masks]
+
+
+def upper_groups():
+    bits = bits_of("space")[2:]
+    return [tuple(bits[n : n + 2]) for n in range(0, len(bits), 2)]
+
+
+def orders():
+    return [(1, 2), (2, 1)]
+
+
 def summed_everywhere(value, arriving):
-    turns = [(axis, bit) for axis in ALL for bit in reversed(bits_of(axis))]
-    for turn, (axis, bit) in enumerate(turns):
-        value = value + swapped(value, axis, bit)
-        if turn == len(turns) - 3:
-            value, arriving = lax.optimization_barrier((value, arriving))
-    return value, arriving
-
-
-def orders():
-    bits = bits_of("space")
-    return bits, bits[1:2] + bits[:1] + bits[2:]
+    for bits in reversed(upper_groups()):
+        value = sum(others(value, "space", bits), value)
+    value = value + swapped(value, "dp", 1)
+    value, arriving = lax.optimization_barrier((value, arriving))
+    return sum(others(value, "space", (1, 2)), value), arriving
 
 
 def gathered_blocks(piece, posted):
+    held, weights, size = piece[None], {}, 1
+    for bits in reversed(upper_groups()):
+        held = jnp.concatenate([held] + others(held, "space", bits), 0)
+        for n, bit in enumerate(bits):
+            weights[bit] = size << n
+        size = size << len(bits)
     half = piece.shape[0] // 2
-    held = [piece[None, :half], piece[None, half:]]
-    last = len(orders()[0]) - 1
-    for turn, bits in enumerate(reversed(list(zip(*orders())))):
-        if turn == last:
+    held = [held[:, :half], held[:, half:]]
+    ranks = [dict(weights), dict(weights)]
+    for turn in (1, 0):
+        if turn == 0:
             held[0], held[1], posted = lax.optimization_barrier((*held, posted))
-        for n, bit in enumerate(bits):
-            held[n] = jnp.concatenate([held[n], swapped(held[n], "space", bit)], 0)
-    return (held, [swapped(part, "dp", 1) for part in held]), posted
+        for n, order in enumerate(orders()):
+            held[n] = jnp.concatenate([held[n], swapped(held[n], "space", order[turn])], 0)
+            ranks[n][order[turn]] = size
+        size = size << 1
+    return (held, [swapped(part, "dp", 1) for part in held], ranks), posted
 
 
 def spread_rows(gathered, total, peers, place):
-    (first, second), (first_far, second_far) = gathered
+    (first, second), (first_far, second_far), ranks = gathered
     starts, counts, shared, height = pieces_of(total, peers)
     half, group = height // 2, first.shape[0]
     rows = -(-total // D)
     sizes = parts_of()
-    ranks = []
-    for order in orders():
-        ranks.append({bit: group >> (n + 1) for n, bit in enumerate(order)})
-
     def at(rank, relative):
         spot = 0
         for bit, weight in rank.items():
@@ -248,19 +260,30 @@
 def reduced_piece(keep, send, leaving):
     kept = keep + swapped(send, "dp", 1).astype(jnp.float32)
     half = kept.shape[1] // 2
-    names = [bits_of("space")[::-1], bits_of("space")[::-1]]
-    parts = [kept[:, :half], kept[:, half:]]
-    parts = [part.reshape((2,) * len(names[0]) + (half, D)) for part in parts]
-    for turn, bits in enumerate(zip(*orders())):
-        for n, bit in enumerate(bits):
-            spot = names[n].index(bit)
-            names[n].pop(spot)
+    groups = upper_groups()
+    inner_shape = (kept.shape[0] // 4, 2, 2, half, D)
+    parts = [kept[:, :half].reshape(inner_shape), kept[:, half:].reshape(inner_shape)]
+    for n, order in enumerate(orders()):
+        for bit in order:
+            spot = 2 if bit == 1 and parts[n].ndim == 5 else 1
             stay = lax.index_in_dim(parts[n], 0, spot, keepdims=False)
             leave = lax.index_in_dim(parts[n], 1, spot, keepdims=False)
             parts[n] = stay + swapped(leave.astype(jnp.bfloat16), "space", bit).astype(jnp.float32)
-        if turn == 1:
-            parts[0], parts[1], leaving = lax.optimization_barrier((*parts, leaving))
-    return jnp.concatenate(parts, 0), leaving
+    part = jnp.concatenate(parts, 1)
+    part, leaving = lax.optimization_barrier((part, leaving))
+    for bits in groups:
+        part = part.reshape((-1, 1 << len(bits)) + part.shape[1:])
+        masks = [sum(bit for n, bit in enumerate(bits) if m >> n & 1) for m in range(1 << len(bits))]
+        low = part.astype(jnp.bfloat16)
+        part = sum(
+            [
+                swapped(low[:, m], "space", mask).astype(jnp.float32)
+                for m, mask in enumerate(masks)
+                if m
+            ],
+            part[:, 0],
+        )
+    return part[0], leaving
 
 
 def tall_parts():
@@ -282,7 +305,7 @@
     return pl.BlockSpec(shape, lambda *_: (0,) * len(shape))
 
 
-def round_forward(index, mesh, before, own, after, mats, bias, following):
+def round_forward(index, mesh, before, own, after, mats, bias, following, decoder=()):
     blocks = mesh.shape[0]
     tile, chunk = 512, 16
     turns, high = tile // chunk, 2 * chunk
@@ -292,9 +315,15 @@
 
     def body(*refs):
         index_ref, mesh_ref, before_ref, own_ref, after_ref, mats_ref, bias_ref = refs[:7]
-        next_ref, sent_ref = (refs[7], refs[13]) if more else (None, None)
-        new_ref, back_ref, update_ref, agg_ref, slope_ref = refs[8:13] if more else refs[7:12]
         raw, table, rows, wide, wider, sems = refs[-6:]
+        if more:
+            next_ref, sent_ref = refs[7], refs[13]
+            new_ref, back_ref, update_ref, agg_ref, slope_ref = refs[8:13]
+        else:
+            ids_ref, dec_ref, out_ref, head_ref = refs[7:11]
+            new_ref, back_ref, update_ref, agg_ref, slope_ref = refs[11:16]
+            branch_ref, fetched_ref, decoded_ref, turn_ref = refs[16:20]
+            total_ref = refs[20]
         step = pl.program_id(0)
 
         @pl.when(step == 0)
@@ -375,9 +404,34 @@
         update_ref[...] = update
         new = mesh_in + inner(update, mats_ref[4], 1, 0)
         new_ref[...] = new
+        lowered = new.astype(jnp.bfloat16)
         if more:
-            weave(wide, inner(new.astype(jnp.bfloat16), next_ref[0], 1, 0))
+            weave(wide, inner(lowered, next_ref[0], 1, 0))
             sent_ref[...] = wide[...].astype(jnp.bfloat16)
+            return
+        nodes = lax.broadcasted_iota(jnp.int32, (ids_ref.shape[0], tile), 1) + step * tile
+        chooser = jnp.where(nodes == ids_ref[...], 1.0, 0.0).astype(jnp.bfloat16)
+        found = inner(chooser, lowered, 1, 0)
+
+        @pl.when(step == 0)
+        def _():
+            total_ref[...] = found
+
+        @pl.when(step > 0)
+        def _():
+            total_ref[...] += found
+
+        @pl.when(step == blocks // tile - 1)
+        def _():
+            fetched = total_ref[...].astype(jnp.bfloat16)
+            fetched_ref[...] = fetched
+            value = inner(fetched, dec_ref[...], 1, 0) + head_ref[2:3, :]
+            sigma = sigmoid(value)
+            out = value * sigma
+            turn_ref[...] = sigma + out * (1.0 - sigma)
+            decoded = out.astype(jnp.bfloat16)
+            decoded_ref[...] = decoded
+            branch_ref[...] = inner(decoded, out_ref[...], 1, 0).astype(jnp.bfloat16)
 
     whole_rows = pl.BlockSpec((tile, D), lambda i, *_: (i, 0))
     woven = pl.BlockSpec((2 * tile, HALF), lambda i, *_: (i, 0))
@@ -396,6 +450,15 @@
         outs.append(woven)
         shapes.append(jax.ShapeDtypeStruct((2 * blocks, HALF), jnp.bfloat16))
         args.append(following)
+    scratch = []
+    if decoder:
+        posts = decoder[0].shape[0]
+        ins = ins + [whole(arg.shape) for arg in decoder]
+        args = args + list(decoder)
+        for width, kind in ((HALF, jnp.bfloat16), (D, jnp.bfloat16), (D, jnp.bfloat16), (D, jnp.float32)):
+            outs.append(whole((posts, width)))
+            shapes.append(jax.ShapeDtypeStruct((posts, width), kind))
+        scratch = [pltpu.VMEM((posts, D), jnp.float32)]
     return pl.pallas_call(
         body,
         grid_spec=pltpu.PrefetchScalarGridSpec(
@@ -403,7 +466,8 @@
             grid=(blocks // tile,),
             in_specs=ins,
             out_specs=outs,
-            scratch_shapes=[
+            scratch_shapes=scratch
+            + [
                 pltpu.VMEM((reach, HALF), jnp.bfloat16),
                 pltpu.VMEM((reach, HALF), jnp.float32),
                 pltpu.VMEM((K * 2 * tile, HALF), jnp.float32),
@@ -419,18 +483,22 @@
     )(*args)
 
 
-def edges_backward(index, grad_mesh, back, slopes, mats, carried=()):
-    blocks = grad_mesh.shape[0]
+def edges_backward(index, grad_mesh, back, slopes, mats, carried=(), landed=()):
+    blocks = back.shape[0]
     tile, chunk = 512, 16
     steps, turns, high = blocks // tile, tile // chunk, 2 * chunk
     reach = 2 * (blocks + 2 * H)
 
     def body(*refs):
-        index_ref, grad_ref, back_ref, slope_ref, mats_ref = refs[:5]
-        rest = refs[5:]
         if carried:
-            past, rest = rest[:6], rest[6:]
+            index_ref, grad_ref, back_ref, slope_ref, mats_ref = refs[:5]
+            past, rest = refs[5:11], refs[11:]
             (new_ref, out_ref, sent_ref), rest = rest[:3], rest[3:]
+        else:
+            index_ref, back_ref, slope_ref, mats_ref = refs[:4]
+            (ids_ref, landed_ref, turn_ref, w_out_ref, w_dec_ref), rest = refs[4:9], refs[9:]
+            (new_ref, out_ref, gdec_ref), rest = rest[:3], rest[3:]
+            gathered, rest = rest[5], rest[:5] + rest[6:]
         guin_ref, low_ref, before_ref, own_ref, after_ref, wide, wider, flows, *tables = rest
         step = pl.program_id(0)
 
@@ -449,7 +517,20 @@
             grad_out = new.astype(jnp.bfloat16)
             out_ref[...] = grad_out
         else:
-            grad_out = grad_ref[...].astype(jnp.bfloat16)
+
+            @pl.when(step == 0)
+            def _():
+                grad_dec = inner(landed_ref[...], w_out_ref[...], 1, 1) * turn_ref[...]
+                grad_dec = grad_dec.astype(jnp.bfloat16)
+                gdec_ref[...] = grad_dec
+                gathered[...] = inner(grad_dec, w_dec_ref[...], 1, 1).astype(jnp.bfloat16)
+
+            nodes = lax.broadcasted_iota(jnp.int32, (tile, landed_ref.shape[0]), 0) + step * tile
+            chooser = jnp.where(nodes == ids_ref[...], 1.0, 0.0).astype(jnp.bfloat16)
+            new = inner(chooser, gathered[...], 1, 0)
+            new_ref[...] = new
+            grad_out = new.astype(jnp.bfloat16)
+            out_ref[...] = grad_out
         grad_uin = (inner(grad_out, mats_ref[4], 1, 1) * back_ref[...]).astype(jnp.bfloat16)
         guin_ref[...] = grad_uin
         weave(wide, inner(grad_uin, mats_ref[2], 1, 1) * (1.0 / K))
@@ -518,31 +599,38 @@
     rows = pl.BlockSpec((tile, D), lambda i, *_: (i, 0))
     woven = pl.BlockSpec((2 * tile, HALF), lambda i, *_: (i, 0))
     low = jax.ShapeDtypeStruct((blocks, D), jnp.bfloat16)
+    low_posts = (landed[1].shape[0], D) if landed else None
+    last = low if carried else jax.ShapeDtypeStruct(low_posts, jnp.bfloat16)
     return pl.pallas_call(
         body,
         grid_spec=pltpu.PrefetchScalarGridSpec(
             num_scalar_prefetch=1,
             grid=(steps,),
-            in_specs=[
-                rows, rows,
+            in_specs=([rows] if carried else [])
+            + [
+                rows,
                 pl.BlockSpec((K, 2 * tile, HALF), lambda i, *_: (0, i, 0)),
                 whole(mats.shape),
             ]
-            + ([woven] * 3 + [rows] * 2 + [whole(mats.shape)] if carried else []),
-            out_specs=([rows] * 3 if carried else []) + [
+            + ([woven] * 3 + [rows] * 2 + [whole(mats.shape)] if carried else [])
+            + [whole(arg.shape) for arg in landed],
+            out_specs=([rows] * 3 if carried else [rows, rows, whole(low_posts)])
+            + [
                 rows, rows,
                 whole((2 * H, HALF)), whole((2 * blocks, HALF)), whole((2 * H, HALF)),
             ],
-            scratch_shapes=[
+            scratch_shapes=([] if carried else [pltpu.VMEM(low_posts, jnp.bfloat16)])
+            + [
                 pltpu.VMEM((2 * tile, HALF), jnp.float32),
                 pltpu.VMEM((2 * tile, HALF), jnp.float32),
                 pltpu.VMEM((2 * tile * K, HALF), jnp.float32),
             ]
             + [pltpu.VMEM((reach, HALF), jnp.float32)] * K,
         ),
-        out_shape=(
-            [jax.ShapeDtypeStruct((blocks, D), jnp.float32), low, low] if carried else []
-        ) + [
+        out_shape=[
+            jax.ShapeDtypeStruct((blocks, D), jnp.float32),
+            low,
+            last,
             low,
             low,
             jax.ShapeDtypeStruct((2 * H, HALF), jnp.bfloat16),
@@ -552,7 +640,7 @@
         compiler_params=LIMIT,
         cost_estimate=cost(28 if carried else 25),
         name="edges_backward",
-    )(index, grad_mesh, back, slopes, mats, *carried)
+    )(index, *([grad_mesh] if carried else []), back, slopes, mats, *carried, *landed)
 
 
 def ended(grad_ref, own_ref, first_ref, last_ref, guin_ref, dest_ref, mats_ref, sent_ref, wide):
@@ -742,11 +830,12 @@
     w_round = [mats.reshape(5, D, D) for mats in w_round]
     b_head = biases[:3]
     b_round = biases[3:].reshape(ROUNDS, 2, D)
+    arrived, biases = lax.optimization_barrier((arrived, biases))
     ids = arrived[:, CH : CH + 3].astype(jnp.int32)
     ids = jnp.where(ids[:, 2:3] > 0, ids[:, 0:1] * 64 + ids[:, 1:2], -1)
-    chooser = (ids == jnp.arange(blocks, dtype=jnp.int32)[None, :]).astype(jnp.bfloat16)
+    ids_row = ids.reshape(1, -1)
     mesh, gathered, sent = encode_rows(
-        arrived, ids.reshape(1, -1), w_in, w_node, biases, w_round[0]
+        arrived, ids_row, w_in, w_node, biases, w_round[0]
     )
     sent, partner, neighbours, counted = lax.optimization_barrier(
         (sent, partner, neighbours, counted)
@@ -780,11 +869,12 @@
             before, valid_around = lax.optimization_barrier((before, valid_around))
         following = w_round[layer + 1] if layer + 1 < ROUNDS else None
         new, back, update, agg, slopes, *rest = round_forward(
-            index, mesh, before, sent, after, w_round[layer], b_round[layer], following
+            index, mesh, before, sent, after, w_round[layer], b_round[layer], following,
+            () if following is not None else (ids, w_dec, w_out, biases),
         )
         kept.append((mesh, back, update, agg, slopes))
         mesh = new
-        sent = rest[0] if rest else None
+        sent = rest[0]
     wide_valid = valid_around[:CH].astype(jnp.float32)
     coded = valid_around[CH : CH + 1, : points + ROWW].astype(jnp.float32)
     weights = [
@@ -796,10 +886,8 @@
         )
         for by in range(NEAR, ROWW + 1)
     ]
-    fetched = inner(chooser, mesh.astype(jnp.bfloat16), 1, 0).astype(jnp.bfloat16)
-    dec_in = inner(fetched, w_dec, 1, 0) + b_head[2]
-    decoded = silu(dec_in).astype(jnp.bfloat16)
-    returned = exchanged(inner(decoded, w_out, 1, 0).astype(jnp.bfloat16))
+    branch_rows, fetched, decoded, dec_turn = rest
+    returned = exchanged(branch_rows)
     branch = inner(returned, poster, 0, 0)[:CH]
     err = state_in.astype(jnp.float32) + branch - targets[0].astype(jnp.float32)
     def widened(values):
@@ -825,34 +913,31 @@
     grad_pred = grad_pred / count
     grad_rows = jnp.pad(grad_pred.astype(jnp.bfloat16), ((0, HALF - CH), (0, 0)))
     landed = exchanged(inner(poster, grad_rows, 1, 1).astype(jnp.bfloat16))
-    grad_wout = inner(decoded, landed, 0, 0)[:, :CH]
-    grad_dec = (inner(landed, w_out, 1, 1) * slope(dec_in)).astype(jnp.bfloat16)
-    grad_bdec = jnp.sum(grad_dec.astype(jnp.float32), 0, keepdims=True)
-    grad_wdec = inner(fetched, grad_dec, 0, 0)
-    grad_fetched = inner(grad_dec, w_dec, 1, 1).astype(jnp.bfloat16)
-    grad_mesh = inner(chooser, grad_fetched, 0, 0)
-    grad_mesh, final_mesh = lax.optimization_barrier((grad_mesh, mesh.astype(jnp.bfloat16)))
+    landed, final_mesh = lax.optimization_barrier((landed, mesh.astype(jnp.bfloat16)))
     final_mesh = at_home(final_mesh)
-    leaving = grad_mesh.astype(jnp.bfloat16)
     mats_grads = [None] * (5 * ROUNDS)
     bias_grads = [None] * (2 * ROUNDS)
-    carried = ()
+    carried, grad_mesh = (), None
     for layer in reversed(range(ROUNDS)):
         old, back, update, agg, slopes = kept[layer]
-        *ends, grad_uin, dest_low, to_before, own, to_after = edges_backward(
-            index, grad_mesh, back, slopes, w_round[layer], carried
+        first_step = not carried
+        grad_mesh, leaving, extra, grad_uin, dest_low, to_before, own, to_after = edges_backward(
+            index, grad_mesh, back, slopes, w_round[layer], carried,
+            (ids_row, landed, dec_turn, w_out, w_dec) if first_step else (),
         )
-        if ends:
-            grad_mesh, leaving, sent_low = ends
+        if not first_step:
             mats_grads[5 * layer + 5] = inner(
-                kept[layer + 1][0].astype(jnp.bfloat16), sent_low, 0, 0
+                kept[layer + 1][0].astype(jnp.bfloat16), extra, 0, 0
             )
         else:
+            grad_wout = inner(decoded, landed, 0, 0)[:, :CH]
+            grad_bdec = jnp.sum(extra.astype(jnp.float32), 0, keepdims=True)
+            grad_wdec = inner(fetched, extra, 0, 0)
             to_before, to_after, final_mesh = lax.optimization_barrier(
                 (to_before, to_after, final_mesh)
             )
         from_before, from_after = halo(walk, to_after, to_before)
-        if not ends:
+        if first_step:
             from_before, final_mesh = lax.optimization_barrier(
                 (from_before, settled(mesh, final_mesh))
             )

time: 505 us -> 490 us (0.970)
  blocking collectives: 14.2 us -> 0 us
  starting transfers between devices: 85 us -> 76.9 us
  waiting for transfers between devices: 133 us -> 140 us
  matrix products: 35.8 us -> 29.6 us
  Pallas kernels: 181 us -> 187 us
    ppermute x6, starting transfers between devices: 19.1 us -> 3.98 us  [halo(): lax.ppermute(last, 'space', up)]
    all_to_all x1 -> x0, blocking collectives: 14.2 us -> none  [exchanged(): lax.all_to_all(rows.reshape(bands, capacity, HALF), 'space', split_axis=0...]
    dot_general x24 -> x19, matrix products: 35.4 us -> 28.3 us  [inner(): lax.dot_general(left, right, (((left_dim,), (right_dim,)), ((), ())), pre...]
    all_to_all x2 -> x3, waiting for transfers between devices: 12.4 us -> 18 us  [exchanged(): lax.all_to_all(rows.reshape(bands, capacity, HALF), 'space', split_axis=0...]
    all_to_all x2 -> x3, starting transfers between devices: 10.2 us -> 14.6 us  [exchanged(): lax.all_to_all(rows.reshape(bands, capacity, HALF), 'space', split_axis=0...]
  transfers between devices with their start and end apart: 45 -> 46, of which waited for: 29 -> 28; matrix products, arithmetic and copies ran while one was open for 9% -> 11% of each run, Pallas kernels for 5% -> 6%
where the time goes in v10:
time: 490 us; the launch traced here: 488 us
  Pallas kernels  187 us (38%)
  waiting for transfers between devices  140 us (29%)
  starting transfers between devices  76.9 us (16%)
  other arithmetic  30.5 us (6%)
  matrix products  29.6 us (6%)
  local copies, waits for them, and re-layouts  16.1 us (3%)
  between operations  7.78 us (2%)
    pallas_call x3, Pallas kernels, edges_backward(): pl.pallas_call(body, grid_spec=pltpu.PrefetchScalarGridSpec(num_scalar_pr...  80.9 us
    pallas_call x3, Pallas kernels, round_forward(): pl.pallas_call(body, grid_spec=pltpu.PrefetchScalarGridSpec(num_scalar_pr...  78.3 us
    ppermute x6, waiting for transfers between devices, halo(): lax.ppermute(initial, 'space', down)  41.1 us
    ppermute x24, waiting for transfers between devices, swapped(): lax.ppermute(value, axis, [(i, i ^ bit) for i in range(lax.axis_size(axis...  31.8 us
    ppermute x6, waiting for transfers between devices, halo(): lax.ppermute(last, 'space', up)  29.5 us
    ppermute x24, starting transfers between devices, swapped(): lax.ppermute(value, axis, [(i, i ^ bit) for i in range(lax.axis_size(axis...  29.2 us
    dot_general x19, matrix products, inner(): lax.dot_general(left, right, (((left_dim,), (right_dim,)), ((), ())), pre...  28.3 us
    ppermute x4, waiting for transfers between devices, shifted(): return lax.ppermute(shard, axis, pairs)  19.1 us
  transfers between devices with their start and end apart: 46, of which 28 were waited for; matrix products, arithmetic and copies ran while one was open for 11% of the time, Pallas kernels for 6%

profile of v10, /device:TPU:0, one launch (start us, length us, event | category | flops | bytes accessed | tf_op | source)
XLA Modules:
  0.0 487.7 jit_solution(7766174449980380979)
XLA Ops:
  5.7 5.1 %collective-permute-start.2 = (bf16[1,144,256]{2,1,0:T(8,128)(2,1)S(1)}, bf16[1,144,256]{2,1,0:T(8,128)(2,1)S(1)}, u32[]{:S(2)}, u32[]{:S(2)}) collective-permute-start(bf16[1,144,256]{2,1,0:T(8,128)(2,1)S(1)} %dynamic_update_slice.8), channel_id=1, source_target_pairs={{0,12},{1,13},{2,14},{3,15},{4,8},{5,9},{6,10},{7,11},{8,4},{9,5},... | collective-permute-start | bytes 221192 | tf_op jit(solution)/shard_map/ppermute | solution.py:94
  26.1 5.3 %collective-permute-done.6 = bf16[8,72,256]{2,1,0:T(8,128)(2,1)S(1)} collective-permute-done((bf16[8,72,256]{2,1,0:T(8,128)(2,1)S(1)}, bf16[8,72,256]{2,1,0:T(8,128)(2,1)S(1)}, u32[]{:S(2)}, u32[]{:S(2)}) %collective-permute-start.6) | collective-permute-done | bytes 294944 | tf_op jit(solution)/shard_map/ppermute | solution.py:94
  32.7 4.7 all-to-all-start
  39.1 4.0 spread_rows.1
  43.2 4.7 all-to-all-done
  49.8 5.8 %encode_rows.1 = (f32[2048,256]{1,0:T(8,128)}, bf16[2048,256]{1,0:T(8,128)(2,1)}, bf16[4096,128]{1,0:T(8,128)(2,1)}) custom-call(bf16[1024,128]{1,0:T(8,128)(2,1)} %bitcast.146, s32[1,1024]{1,0:T(1,128)} %bitcast.162, bf16[128,256]{1,0:T(8,128)(2,1)} %get-tuple-element.102.in_ref, bf16[256,256]{1,0:T(8,128)(2,1)} %get-tuple-element.103.node_ref, ...), custom_call_target="tpu_custom_call" | custom-call | bytes 15000000 | tf_op jit(solution)/shard_map/encode_rows/pallas_call | solution.py:712
  61.2 4.5 collective-permute-start.11
  67.1 14.4 %collective-permute-done.12 = bf16[79,360]{1,0:T(8,128)(2,1)S(1)} collective-permute-done((bf16[79,360]{1,0:T(8,128)(2,1)S(1)}, bf16[79,360]{1,0:T(8,128)(2,1)S(1)}, u32[]{:S(2)}, u32[]{:S(2)}) %collective-permute-start.12) | collective-permute-done | bytes 56912 | tf_op jit(solution)/shard_map/ppermute | solution.py:49
  81.6 2.5 collective-permute-done.10.refs_2_
  85.4 24.9 %round_forward.3 = (f32[2048,256]{1,0:T(8,128)}, f32[2048,256]{1,0:T(8,128)}, bf16[2048,256]{1,0:T(8,128)(2,1)}, bf16[2048,256]{1,0:T(8,128)(2,1)}, bf16[6,4096,...) custom-call(s32[12288]{0:T(1024)} %broadcast_select_fusion.refs_0_, f32[2048,256]{1,0:T(8,128)} %get-tuple-element.109.refs_1_, ...), custom_call_target="tpu_custom_call" | custom-call | bytes 75000000 | tf_op jit(solution)/shard_map/round_forward/pallas_call | solution.py:462
  110.4 2.8 collective-permute-start.15
  113.2 20.7 %collective-permute-done.15.refs_4_ = bf16[4096,128]{1,0:T(8,128)(2,1)S(1)} collective-permute-done((bf16[4096,128]{1,0:T(8,128)(2,1)}, bf16[4096,128]{1,0:T(8,128)(2,1)S(1)}, u32[]{:S(2)}, u32[]{:S(2)}) %collective-permute-start.15) | collective-permute-done | bytes 1048608 | tf_op jit(solution)/shard_map/ppermute | solution.py:77
  133.9 3.9 collective-permute-done.14.refs_2_
  138.8 25.1 %round_forward.4 = (f32[2048,256]{1,0:T(8,128)}, f32[2048,256]{1,0:T(8,128)}, bf16[2048,256]{1,0:T(8,128)(2,1)}, bf16[2048,256]{1,0:T(8,128)(2,1)}, bf16[6,4096,...) custom-call(s32[12288]{0:T(1024)} %broadcast_select_fusion.refs_0_, f32[2048,256]{1,0:T(8,128)} %get-tuple-element.114.refs_1_, ...), custom_call_target="tpu_custom_call" | custom-call | bytes 75000000 | tf_op jit(solution)/shard_map/round_forward/pallas_call | solution.py:462
  166.8 20.4 %collective-permute-done.17.refs_4_ = bf16[4096,128]{1,0:T(8,128)(2,1)S(1)} collective-permute-done((bf16[4096,128]{1,0:T(8,128)(2,1)}, bf16[4096,128]{1,0:T(8,128)(2,1)S(1)}, u32[]{:S(2)}, u32[]{:S(2)}) %collective-permute-start.17) | collective-permute-done | bytes 1048608 | tf_op jit(solution)/shard_map/ppermute | solution.py:77
  189.2 28.3 %round_forward.5 = (f32[2048,256]{1,0:T(8,128)}, f32[2048,256]{1,0:T(8,128)}, bf16[2048,256]{1,0:T(8,128)(2,1)}, bf16[2048,256]{1,0:T(8,128)(2,1)}, bf16[6,4096,...) custom-call(s32[12288]{0:T(1024)} %broadcast_select_fusion.refs_0_, ...), custom_call_target="tpu_custom_call" | custom-call | bytes 75000000 | tf_op jit(solution)/shard_map/round_forward/pallas_call | solution.py:462
  217.5 4.0 all-to-all-start.1
  224.2 5.8 %all-to-all-done.1 = bf16[16,64,128]{2,1,0:T(8,128)(2,1)S(1)} async-done(((bf16[16,64,128]{2,1,0:T(8,128)(2,1)}), bf16[16,64,128]{2,1,0:T(8,128)(2,1)S(1)}, u32[]{:S(2)}, u32[]{:S(2)}) %all-to-all-start.1) | async-done | bytes 262176 | tf_op jit(solution)/shard_map/all_to_all | solution.py:819
  230.7 3.3 collective-permute-start.18
  235.4 4.8 collective-permute-done.19
  243.2 5.9 %all-to-all-start.2 = ((bf16[16,64,128]{2,1,0:T(8,128)(2,1)}), bf16[16,64,128]{2,1,0:T(8,128)(2,1)S(1)}, u32[]{:S(2)}, u32[]{:S(2)}) async-start(bf16[16,64,128]{2,1,0:T(8,128)(2,1)} %bitcast.18), calls=%async_computation.2 | async-start | bytes 524288 | tf_op jit(solution)/shard_map/all_to_all | solution.py:819
  250.2 7.4 %all-to-all-done.2 = bf16[16,64,128]{2,1,0:T(8,128)(2,1)S(1)} async-done(((bf16[16,64,128]{2,1,0:T(8,128)(2,1)}), bf16[16,64,128]{2,1,0:T(8,128)(2,1)S(1)}, u32[]{:S(2)}, u32[]{:S(2)}) %all-to-all-start.2) | async-done | bytes 262176 | tf_op jit(solution)/shard_map/all_to_all | solution.py:819
  259.2 26.8 %edges_backward.3 = (f32[2048,256]{1,0:T(8,128)}, bf16[2048,256]{1,0:T(8,128)(2,1)}, bf16[1024,256]{1,0:T(8,128)(2,1)}, bf16[2048,256]{1,0:T(8,128)(2,1)}, bf16[...) custom-call(s32[12288]{0:T(1024)} %broadcast_select_fusion.refs_0_, ...), custom_call_target="tpu_custom_call" | custom-call | bytes 75000000 | tf_op jit(solution)/shard_map/edges_backward/pallas_call | solution.py:604
  286.0 2.2 fusion.92.refs_2_
  290.8 2.4 fusion.98.refs_18_
  295.8 2.4 collective-permute-start.22
  303.1 3.5 convert_select_fusion
  306.6 8.6 %collective-permute-done.21.refs_6_ = bf16[4096,128]{1,0:T(8,128)(2,1)} collective-permute-done((bf16[4096,128]{1,0:T(8,128)(2,1)}, bf16[4096,128]{1,0:T(8,128)(2,1)}, u32[]{:S(2)}, u32[]{:S(2)}) %collective-permute-start.21) | collective-permute-done | bytes 1048608 | tf_op jit(solution)/shard_map/ppermute | solution.py:77
  315.2 27.0 %edges_backward.4 = (f32[2048,256]{1,0:T(8,128)}, bf16[2048,256]{1,0:T(8,128)(2,1)}, bf16[2048,256]{1,0:T(8,128)(2,1)}, bf16[2048,256]{1,0:T(8,128)(2,1)}, bf16[...) custom-call(s32[12288]{0:T(1024)} %broadcast_select_fusion.refs_0_, ...), custom_call_target="tpu_custom_call" | custom-call | bytes 84000000 | tf_op jit(solution)/shard_map/edges_backward/pallas_call | solution.py:604
  343.1 3.1 collective-permute-start.24
  346.2 2.9 fusion.95.refs_11_
  354.7 7.4 %collective-permute-done.23.refs_6_ = bf16[4096,128]{1,0:T(8,128)(2,1)S(1)} collective-permute-done((bf16[4096,128]{1,0:T(8,128)(2,1)}, bf16[4096,128]{1,0:T(8,128)(2,1)S(1)}, u32[]{:S(2)}, u32[]{:S(2)}) %collective-permute-start.23) | collective-permute-done | bytes 1048608 | tf_op jit(solution)/shard_map/ppermute | solution.py:77
  363.2 27.1 %edges_backward.5 = (f32[2048,256]{1,0:T(8,128)}, bf16[2048,256]{1,0:T(8,128)(2,1)}, bf16[2048,256]{1,0:T(8,128)(2,1)}, bf16[2048,256]{1,0:T(8,128)(2,1)}, bf16[...) custom-call(s32[12288]{0:T(1024)} %broadcast_select_fusion.refs_0_, ...), custom_call_target="tpu_custom_call" | custom-call | bytes 84000000 | tf_op jit(solution)/shard_map/edges_backward/pallas_call | solution.py:604
  390.4 3.8 collective-permute-start.26
  394.2 2.6 fusion.93.refs_6_
  403.2 6.1 %collective-permute-done.25.refs_2_ = bf16[4096,128]{1,0:T(8,128)(2,1)S(1)} collective-permute-done((bf16[4096,128]{1,0:T(8,128)(2,1)}, bf16[4096,128]{1,0:T(8,128)(2,1)S(1)}, u32[]{:S(2)}, u32[]{:S(2)}) %collective-permute-start.25) | collective-permute-done | bytes 1048608 | tf_op jit(solution)/shard_map/ppermute | solution.py:77
  410.2 6.1 %round_backward.1 = (f32[2048,256]{1,0:T(8,128)}, bf16[2048,256]{1,0:T(8,128)(2,1)}, bf16[2048,256]{1,0:T(8,128)(2,1)}) custom-call(f32[2048,256]{1,0:T(8,128)} %get-tuple-element.150.refs_0_, f32[4096,128]{1,0:T(8,128)} %get-tuple-element.151.refs_1_, bf16[4096,128]{1,0:T(8,128)(2,1)} %copy-done.18, bf16[4096,128]{1,0:T(8,128)(2,1)} %collective-permute-done.26.refs_3_, ...), custom_call_target="tpu_custom_call" | custom-call | bytes 21000000 | tf_op jit(solution)/shard_map/round_backward/pallas_call | solution.py:676
  416.3 2.4 fusion.76.refs_4_
  418.7 6.9 %encode_backward.1 = (f32[128,256]{1,0:T(8,128)}, f32[256,256]{1,0:T(8,128)}, f32[2,256]{1,0:T(2,128)}) custom-call(f32[2048,256]{1,0:T(8,128)} %get-tuple-element.156.grad_ref, bf16[2048,256]{1,0:T(8,128)(2,1)} %get-tuple-element.157.gathered_ref, bf16[1024,128]{1,0:T(8,128)(2,1)} %bitcast.147, s32[1024,1]{1,0:T(8,128)} %get-tuple-element.218.refs_7_.ids_ref, ...), custom_call_target="tpu_custom_call" | custom-call | bytes 21000000 | tf_op jit(solution)/shard_map/encode_backward/pallas_call | solution.py:763
  425.6 5.1 %collect_rows.1 = (f32[16,144,256]{2,1,0:T(8,128)}, bf16[16,144,256]{2,1,0:T(8,128)(2,1)}) custom-call(s32[1]{0:T(128)} %bitcast.7.place_ref, f32[128,256]{1,0:T(8,128)} %get-tuple-element.158.refs_0_, f32[256,256]{1,0:T(8,128)} %get-tuple-element.159.refs_1_, f32[256,256]{1,0:T(8,128)} %fusion.92.refs_2_, f32[78,256]{1,0:T(8,128)} %reshape.158.refs_3_, ...), custom_call_target="tpu_custom_call" | custom-call | bytes 15000000 | tf_op jit(solution)/shard_map/collect_rows/pallas_call | solution.py:241
  430.7 3.0 collective-permute-done.27
  436.1 8.9 %collective-permute-done.28 = bf16[4,2,72,256]{3,2,0,1:T(8,128)(2,1)S(1)} collective-permute-done((bf16[4,2,72,256]{3,2,0,1:T(8,128)(2,1)S(1)}, bf16[4,2,72,256]{3,2,0,1:T(8,128)(2,1)S(1)}, u32[]{:S(2)}, u32[]{:S(2)}) %collective-permute-start.28) | collective-permute-done | bytes 294944 | tf_op jit(solution)/shard_map/ppermute | solution.py:94
  447.0 3.3 collective-permute-done.29
  452.6 4.7 collective-permute-start.34
  461.2 2.2 collective-permute-done.33
  465.3 2.3 collective-permute-start.37
  472.4 5.8 %collective-permute-start.42 = (f32[8,128]{1,0:T(8,128)S(1)}, f32[8,128]{1,0:T(8,128)S(1)}, u32[]{:S(2)}, u32[]{:S(2)}) collective-permute-start(f32[8,128]{1,0:T(8,128)S(1)} %add.179), channel_id=1, source_target_pairs={{0,3},{1,2},{2,1},{3,0},{4,7},{5,6},{6,5},{7,4},{8,11},{9,10},{10,... | collective-permute-start | bytes 12296 | tf_op jit(solution)/shard_map/ppermute | solution.py:94
  479.7 3.4 select_bitcast_fusion
  (257 shorter events, 91.3 us)
Async XLA Ops:
  5.7 11.2 %collective-permute-start.2 = (bf16[1,144,256]{2,1,0:T(8,128)(2,1)S(1)}, bf16[1,144,256]{2,1,0:T(8,128)(2,1)S(1)}, u32[]{:S(2)}, u32[]{:S(2)}) collective-permute-start(bf16[1,144,256]{2,1,0:T(8,128)(2,1)S(1)} %dynamic_update_slice.8), channel_id=1, source_target_pairs={{0,12},{1,13},{2,14},{3,15},{4,8},{5,9},{6,10},{7,11},{8,4},{9,5},... | collective-permute-start | bytes 221192 | tf_op jit(solution)/shard_map/ppermute | solution.py:94
  10.9 6.2 %collective-permute-start.1 = (bf16[1,144,256]{2,1,0:T(8,128)(2,1)S(1)}, bf16[1,144,256]{2,1,0:T(8,128)(2,1)S(1)}, u32[]{:S(2)}, u32[]{:S(2)}) collective-permute-start(bf16[1,144,256]{2,1,0:T(8,128)(2,1)S(1)} %dynamic_update_slice.8), channel_id=1, source_target_pairs={{0,8},{1,9},{2,10},{3,11},{4,12},{5,13},{6,14},{7,15},{8,0},{9,1},... | collective-permute-start | bytes 221192 | tf_op jit(solution)/shard_map/ppermute | solution.py:94
  10.9 6.2 %collective-permute-start = (bf16[1,144,256]{2,1,0:T(8,128)(2,1)S(1)}, bf16[1,144,256]{2,1,0:T(8,128)(2,1)S(1)}, u32[]{:S(2)}, u32[]{:S(2)}) collective-permute-start(bf16[1,144,256]{2,1,0:T(8,128)(2,1)S(1)} %dynamic_update_slice.8), channel_id=1, source_target_pairs={{0,4},{1,5},{2,6},{3,7},{4,0},{5,1},{6,2},{7,3},{8,12},{9,13},{10,... | collective-permute-start | bytes 221192 | tf_op jit(solution)/shard_map/ppermute | solution.py:94
  17.2 5.3 %collective-permute-start.4 = (bf16[4,72,256]{2,1,0:T(8,128)(2,1)S(1)}, bf16[4,72,256]{2,1,0:T(8,128)(2,1)S(1)}, u32[]{:S(2)}, u32[]{:S(2)}) collective-permute-start(bf16[4,72,256]{2,1,0:T(8,128)(2,1)S(1)} %get-tuple-element.231), channel_id=1, source_target_pairs={{0,1},{1,0},{2,3},{3,2},{4,5},{5,4},{6,7},{7,6},{8,9},{9,8},{10,11... | collective-permute-start | bytes 442376 | tf_op jit(solution)/shard_map/ppermute | solution.py:94
  18.8 5.1 %collective-permute-start.3 = (bf16[4,72,256]{2,1,0:T(8,128)(2,1)S(1)}, bf16[4,72,256]{2,1,0:T(8,128)(2,1)S(1)}, u32[]{:S(2)}, u32[]{:S(2)}) collective-permute-start(bf16[4,72,256]{2,1,0:T(8,128)(2,1)S(1)} %get-tuple-element.232), channel_id=1, source_target_pairs={{0,2},{1,3},{2,0},{3,1},{4,6},{5,7},{6,4},{7,5},{8,10},{9,11},{10,... | collective-permute-start | bytes 442376 | tf_op jit(solution)/shard_map/ppermute | solution.py:94
  23.9 7.4 %collective-permute-start.6 = (bf16[8,72,256]{2,1,0:T(8,128)(2,1)S(1)}, bf16[8,72,256]{2,1,0:T(8,128)(2,1)S(1)}, u32[]{:S(2)}, u32[]{:S(2)}) collective-permute-start(bf16[8,72,256]{2,1,0:T(8,128)(2,1)S(1)} %pad_maximum_fusion.4), channel_id=1, source_target_pairs={{0,2},{1,3},{2,0},{3,1},{4,6},{5,7},{6,4},{7,5},{8,10},{9,11},{10,... | collective-permute-start | bytes 884744 | tf_op jit(solution)/shard_map/ppermute | solution.py:94
  25.5 7.1 %collective-permute-start.5 = (bf16[8,72,256]{2,1,0:T(8,128)(2,1)S(1)}, bf16[8,72,256]{2,1,0:T(8,128)(2,1)S(1)}, u32[]{:S(2)}, u32[]{:S(2)}) collective-permute-start(bf16[8,72,256]{2,1,0:T(8,128)(2,1)S(1)} %pad_maximum_fusion.3), channel_id=1, source_target_pairs={{0,1},{1,0},{2,3},{3,2},{4,5},{5,4},{6,7},{7,6},{8,9},{9,8},{10,11... | collective-permute-start | bytes 884744 | tf_op jit(solution)/shard_map/ppermute | solution.py:94
  31.4 6.6 %collective-permute-start.8 = (bf16[16,72,256]{2,1,0:T(8,128)(2,1)S(1)}, bf16[16,72,256]{2,1,0:T(8,128)(2,1)S(1)}, u32[]{:S(2)}, u32[]{:S(2)}) collective-permute-start(bf16[16,72,256]{2,1,0:T(8,128)(2,1)S(1)} %constant_dynamic-update-slice_fusion.2.refs_1_), channel_id=1, source_target_pairs={{0,16},{16,0},{1,17},{17,1},{2,18},{18,2},{3,19},{19,3},{4,20},{20... | collective-permute-start | bytes 1769480 | tf_op jit(solution)/shard_map/ppermute | solution.py:94
  32.7 5.4 %collective-permute-start.7 = (bf16[16,72,256]{2,1,0:T(8,128)(2,1)S(1)}, bf16[16,72,256]{2,1,0:T(8,128)(2,1)S(1)}, u32[]{:S(2)}, u32[]{:S(2)}) collective-permute-start(bf16[16,72,256]{2,1,0:T(8,128)(2,1)S(1)} %constant_dynamic-update-slice_fusion.refs_0_), channel_id=1, source_target_pairs={{0,16},{16,0},{1,17},{17,1},{2,18},{18,2},{3,19},{19,3},{4,20},{20... | collective-permute-start | bytes 1769480 | tf_op jit(solution)/shard_map/ppermute | solution.py:94
  32.7 15.1 %all-to-all-start = ((bf16[16,64,128]{2,1,0:T(8,128)(2,1)}), bf16[16,64,128]{2,1,0:T(8,128)(2,1)S(1)}, u32[]{:S(2)}, u32[]{:S(2)}) async-start(bf16[16,64,128]{2,1,0:T(8,128)(2,1)} %bitcast.5), calls=%async_computation | async-start | bytes 524288 | tf_op jit(solution)/shard_map/all_to_all | solution.py:819
  55.6 28.5 %collective-permute-start.13 = (bf16[4096,128]{1,0:T(8,128)(2,1)}, bf16[4096,128]{1,0:T(8,128)(2,1)S(1)}, u32[]{:S(2)}, u32[]{:S(2)}) collective-permute-start(bf16[4096,128]{1,0:T(8,128)(2,1)} %get-tuple-element.110.refs_3_), channel_id=1, source_target_pairs={{1,0},{3,1},{2,3},{6,2},{4,6},{5,4},{7,5},{11,7},{9,11},{8,9},{10,... | collective-permute-start | bytes 3145736 | tf_op jit(solution)/shard_map/ppermute | solution.py:77
  57.3 26.8 %collective-permute-start.10 = (bf16[4096,128]{1,0:T(8,128)(2,1)}, bf16[4096,128]{1,0:T(8,128)(2,1)S(1)}, u32[]{:S(2)}, u32[]{:S(2)}) collective-permute-start(bf16[4096,128]{1,0:T(8,128)(2,1)} %get-tuple-element.110.refs_3_), channel_id=1, source_target_pairs={{0,1},{1,3},{3,2},{2,6},{6,4},{4,5},{5,7},{7,11},{11,9},{9,8},{8,1... | collective-permute-start | bytes 3145736 | tf_op jit(solution)/shard_map/ppermute | solution.py:77
  57.7 8.1 %collective-permute-start.9 = (s32[12288]{0:T(1024)S(1)}, s32[12288]{0:T(1024)S(1)}, u32[]{:S(2)}, u32[]{:S(2)}) collective-permute-start(s32[12288]{0:T(1024)S(1)} %mul.185), channel_id=1, source_target_pairs={{2,3},{3,2},{4,6},{5,4},{6,5},{8,11},{10,8},{11,10},{12,14},{13,15... | collective-permute-start | bytes 147464 | tf_op jit(solution)/shard_map/ppermute | solution.py:846
  59.9 21.5 %collective-permute-start.12 = (bf16[79,360]{1,0:T(8,128)(2,1)S(1)}, bf16[79,360]{1,0:T(8,128)(2,1)S(1)}, u32[]{:S(2)}, u32[]{:S(2)}) collective-permute-start(bf16[79,360]{1,0:T(8,128)(2,1)S(1)} %get-tuple-element.233), channel_id=1, source_target_pairs={{1,0},{2,1},{3,2},{4,3},{5,4},{6,5},{7,6},{8,7},{9,8},{10,9},{11,1... | collective-permute-start | bytes 170648 | tf_op jit(solution)/shard_map/ppermute | solution.py:49
  61.2 20.2 %collective-permute-start.11 = (bf16[79,360]{1,0:T(8,128)(2,1)S(1)}, bf16[79,360]{1,0:T(8,128)(2,1)S(1)}, u32[]{:S(2)}, u32[]{:S(2)}) collective-permute-start(bf16[79,360]{1,0:T(8,128)(2,1)S(1)} %get-tuple-element.234), channel_id=1, source_target_pairs={{0,1},{1,2},{2,3},{3,4},{4,5},{5,6},{6,7},{7,8},{8,9},{9,10},{10,1... | collective-permute-start | bytes 170648 | tf_op jit(solution)/shard_map/ppermute | solution.py:49
  110.4 23.5 %collective-permute-start.15 = (bf16[4096,128]{1,0:T(8,128)(2,1)}, bf16[4096,128]{1,0:T(8,128)(2,1)S(1)}, u32[]{:S(2)}, u32[]{:S(2)}) collective-permute-start(bf16[4096,128]{1,0:T(8,128)(2,1)} %get-tuple-element.115.refs_3_), channel_id=1, source_target_pairs={{1,0},{3,1},{2,3},{6,2},{4,6},{5,4},{7,5},{11,7},{9,11},{8,9},{10,... | collective-permute-start | bytes 3145736 | tf_op jit(solution)/shard_map/ppermute | solution.py:77
  113.2 24.6 %collective-permute-start.14 = (bf16[4096,128]{1,0:T(8,128)(2,1)}, bf16[4096,128]{1,0:T(8,128)(2,1)S(1)}, u32[]{:S(2)}, u32[]{:S(2)}) collective-permute-start(bf16[4096,128]{1,0:T(8,128)(2,1)} %get-tuple-element.115.refs_3_), channel_id=1, source_target_pairs={{0,1},{1,3},{3,2},{2,6},{6,4},{4,5},{5,7},{7,11},{11,9},{9,8},{8,1... | collective-permute-start | bytes 3145736 | tf_op jit(solution)/shard_map/ppermute | solution.py:77
  163.9 23.3 %collective-permute-start.17 = (bf16[4096,128]{1,0:T(8,128)(2,1)}, bf16[4096,128]{1,0:T(8,128)(2,1)S(1)}, u32[]{:S(2)}, u32[]{:S(2)}) collective-permute-start(bf16[4096,128]{1,0:T(8,128)(2,1)} %get-tuple-element.118.refs_3_), channel_id=1, source_target_pairs={{1,0},{3,1},{2,3},{6,2},{4,6},{5,4},{7,5},{11,7},{9,11},{8,9},{10,... | collective-permute-start | bytes 3145736 | tf_op jit(solution)/shard_map/ppermute | solution.py:77
  164.6 23.7 %collective-permute-start.16 = (bf16[4096,128]{1,0:T(8,128)(2,1)}, bf16[4096,128]{1,0:T(8,128)(2,1)S(1)}, u32[]{:S(2)}, u32[]{:S(2)}) collective-permute-start(bf16[4096,128]{1,0:T(8,128)(2,1)} %get-tuple-element.118.refs_3_), channel_id=1, source_target_pairs={{0,1},{1,3},{3,2},{2,6},{6,4},{4,5},{5,7},{7,11},{11,9},{9,8},{8,1... | collective-permute-start | bytes 3145736 | tf_op jit(solution)/shard_map/ppermute | solution.py:77
  189.2 40.9 %copy-start.42 = (bf16[1,78,512]{2,1,0:T(8,128)(2,1)S(1)}, bf16[1,78,512]{2,1,0:T(8,128)(2,1)}, u32[]{:S(2)}) copy-start(bf16[1,78,512]{2,1,0:T(8,128)(2,1)} %param.16) | copy-start | bytes 239620
  189.2 40.9 %copy-start.47 = (bf16[1,78,512]{2,1,0:T(8,128)(2,1)S(1)}, bf16[1,78,512]{2,1,0:T(8,128)(2,1)}, u32[]{:S(2)}) copy-start(bf16[1,78,512]{2,1,0:T(8,128)(2,1)} %param.17) | copy-start | bytes 239620
  217.5 12.5 %all-to-all-start.1 = ((bf16[16,64,128]{2,1,0:T(8,128)(2,1)}), bf16[16,64,128]{2,1,0:T(8,128)(2,1)S(1)}, u32[]{:S(2)}, u32[]{:S(2)}) async-start(bf16[16,64,128]{2,1,0:T(8,128)(2,1)} %bitcast.159), calls=%async_computation.1 | async-start | bytes 524288 | tf_op jit(solution)/shard_map/all_to_all | solution.py:819
  230.7 9.5 %collective-permute-start.18 = (bf16[78,360]{1,0:T(8,128)(2,1)S(1)}, bf16[78,360]{1,0:T(8,128)(2,1)S(1)}, u32[]{:S(2)}, u32[]{:S(2)}) collective-permute-start(bf16[78,360]{1,0:T(8,128)(2,1)S(1)} %get-tuple-element.235), channel_id=1, source_target_pairs={{0,1},{1,2},{2,3},{3,4},{4,5},{5,6},{6,7},{7,8},{8,9},{9,10},{10,1... | collective-permute-start | bytes 168488 | tf_op jit(solution)/shard_map/ppermute | solution.py:49
  234.0 6.1 %collective-permute-start.19 = (bf16[78,360]{1,0:T(8,128)(2,1)S(1)}, bf16[78,360]{1,0:T(8,128)(2,1)S(1)}, u32[]{:S(2)}, u32[]{:S(2)}) collective-permute-start(bf16[78,360]{1,0:T(8,128)(2,1)S(1)} %get-tuple-element.236), channel_id=1, source_target_pairs={{1,0},{2,1},{3,2},{4,3},{5,4},{6,5},{7,6},{8,7},{9,8},{10,9},{11,1... | collective-permute-start | bytes 168488 | tf_op jit(solution)/shard_map/ppermute | solution.py:49
  243.2 14.4 %all-to-all-start.2 = ((bf16[16,64,128]{2,1,0:T(8,128)(2,1)}), bf16[16,64,128]{2,1,0:T(8,128)(2,1)S(1)}, u32[]{:S(2)}, u32[]{:S(2)}) async-start(bf16[16,64,128]{2,1,0:T(8,128)(2,1)} %bitcast.18), calls=%async_computation.2 | async-start | bytes 524288 | tf_op jit(solution)/shard_map/all_to_all | solution.py:819
  257.6 36.8 %collective-permute-start.20 = (bf16[2048,256]{1,0:T(8,128)(2,1)}, bf16[2048,256]{1,0:T(8,128)(2,1)}, u32[]{:S(2)}, u32[]{:S(2)}) collective-permute-start(bf16[2048,256]{1,0:T(8,128)(2,1)} %convert_element_type.182), channel_id=1, source_target_pairs={{3,2},{2,3},{6,4},{4,5},{5,6},{11,8},{8,10},{10,11},{14,12},{15,13... | collective-permute-start | bytes 3145736 | tf_op jit(solution)/shard_map/ppermute | solution.py:849
  294.4 20.8 %collective-permute-start.21 = (bf16[4096,128]{1,0:T(8,128)(2,1)}, bf16[4096,128]{1,0:T(8,128)(2,1)}, u32[]{:S(2)}, u32[]{:S(2)}) collective-permute-start(bf16[4096,128]{1,0:T(8,128)(2,1)} %get-tuple-element.136), channel_id=1, source_target_pairs={{0,1},{1,3},{3,2},{2,6},{6,4},{4,5},{5,7},{7,11},{11,9},{9,8},{8,1... | collective-permute-start | bytes 3145736 | tf_op jit(solution)/shard_map/ppermute | solution.py:77
  295.8 19.4 %collective-permute-start.22 = (bf16[4096,128]{1,0:T(8,128)(2,1)}, bf16[4096,128]{1,0:T(8,128)(2,1)}, u32[]{:S(2)}, u32[]{:S(2)}) collective-permute-start(bf16[4096,128]{1,0:T(8,128)(2,1)} %get-tuple-element.139), channel_id=1, source_target_pairs={{1,0},{3,1},{2,3},{6,2},{4,6},{5,4},{7,5},{11,7},{9,11},{8,9},{10,... | collective-permute-start | bytes 3145736 | tf_op jit(solution)/shard_map/ppermute | solution.py:77
  342.3 19.8 %collective-permute-start.23 = (bf16[4096,128]{1,0:T(8,128)(2,1)}, bf16[4096,128]{1,0:T(8,128)(2,1)S(1)}, u32[]{:S(2)}, u32[]{:S(2)}) collective-permute-start(bf16[4096,128]{1,0:T(8,128)(2,1)} %get-tuple-element.146), channel_id=1, source_target_pairs={{0,1},{1,3},{3,2},{2,6},{6,4},{4,5},{5,7},{7,11},{11,9},{9,8},{8,1... | collective-permute-start | bytes 3145736 | tf_op jit(solution)/shard_map/ppermute | solution.py:77
  343.1 19.1 %collective-permute-start.24 = (bf16[4096,128]{1,0:T(8,128)(2,1)}, bf16[4096,128]{1,0:T(8,128)(2,1)}, u32[]{:S(2)}, u32[]{:S(2)}) collective-permute-start(bf16[4096,128]{1,0:T(8,128)(2,1)} %get-tuple-element.147), channel_id=1, source_target_pairs={{1,0},{3,1},{2,3},{6,2},{4,6},{5,4},{7,5},{11,7},{9,11},{8,9},{10,... | collective-permute-start | bytes 3145736 | tf_op jit(solution)/shard_map/ppermute | solution.py:77
  390.3 18.9 %collective-permute-start.25 = (bf16[4096,128]{1,0:T(8,128)(2,1)}, bf16[4096,128]{1,0:T(8,128)(2,1)S(1)}, u32[]{:S(2)}, u32[]{:S(2)}) collective-permute-start(bf16[4096,128]{1,0:T(8,128)(2,1)} %get-tuple-element.152), channel_id=1, source_target_pairs={{0,1},{1,3},{3,2},{2,6},{6,4},{4,5},{5,7},{7,11},{11,9},{9,8},{8,1... | collective-permute-start | bytes 3145736 | tf_op jit(solution)/shard_map/ppermute | solution.py:77
  390.4 18.9 %collective-permute-start.26 = (bf16[4096,128]{1,0:T(8,128)(2,1)}, bf16[4096,128]{1,0:T(8,128)(2,1)}, u32[]{:S(2)}, u32[]{:S(2)}) collective-permute-start(bf16[4096,128]{1,0:T(8,128)(2,1)} %get-tuple-element.153), channel_id=1, source_target_pairs={{1,0},{3,1},{2,3},{6,2},{4,6},{5,4},{7,5},{11,7},{9,11},{8,9},{10,... | collective-permute-start | bytes 3145736 | tf_op jit(solution)/shard_map/ppermute | solution.py:77
  430.7 3.1 collective-permute-start.27
  435.9 9.1 %collective-permute-start.28 = (bf16[4,2,72,256]{3,2,0,1:T(8,128)(2,1)S(1)}, bf16[4,2,72,256]{3,2,0,1:T(8,128)(2,1)S(1)}, u32[]{:S(2)}, u32[]{:S(2)}) collective-permute-start(bf16[4,2,72,256]{3,2,0,1:T(8,128)(2,1)S(1)} %fusion.14), channel_id=1, source_target_pairs={{0,1},{1,0},{2,3},{3,2},{4,5},{5,4},{6,7},{7,6},{8,9},{9,8},{10,11... | collective-permute-start | bytes 884744 | tf_op jit(solution)/shard_map/ppermute | solution.py:94
  436.0 9.2 %collective-permute-start.30 = (bf16[4,2,72,256]{3,2,1,0:T(8,128)(2,1)S(1)}, bf16[4,2,72,256]{3,2,1,0:T(8,128)(2,1)S(1)}, u32[]{:S(2)}, u32[]{:S(2)}) collective-permute-start(bf16[4,2,72,256]{3,2,1,0:T(8,128)(2,1)S(1)} %fusion.13), channel_id=1, source_target_pairs={{0,2},{1,3},{2,0},{3,1},{4,6},{5,7},{6,4},{7,5},{8,10},{9,11},{10,... | collective-permute-start | bytes 884744 | tf_op jit(solution)/shard_map/ppermute | solution.py:94
  445.1 5.2 %collective-permute-start.29 = (bf16[4,72,256]{2,1,0:T(8,128)(2,1)S(1)}, bf16[4,72,256]{2,1,0:T(8,128)(2,1)S(1)}, u32[]{:S(2)}, u32[]{:S(2)}) collective-permute-start(bf16[4,72,256]{2,1,0:T(8,128)(2,1)S(1)} %fusion.40), channel_id=1, source_target_pairs={{0,2},{1,3},{2,0},{3,1},{4,6},{5,7},{6,4},{7,5},{8,10},{9,11},{10,... | collective-permute-start | bytes 442376 | tf_op jit(solution)/shard_map/ppermute | solution.py:94
  445.3 5.2 %collective-permute-start.31 = (bf16[4,72,256]{2,1,0:T(8,128)(2,1)S(1)}, bf16[4,72,256]{2,1,0:T(8,128)(2,1)S(1)}, u32[]{:S(2)}, u32[]{:S(2)}) collective-permute-start(bf16[4,72,256]{2,1,0:T(8,128)(2,1)S(1)} %fusion.41), channel_id=1, source_target_pairs={{0,1},{1,0},{2,3},{3,2},{4,5},{5,4},{6,7},{7,6},{8,9},{9,8},{10,11... | collective-permute-start | bytes 442376 | tf_op jit(solution)/shard_map/ppermute | solution.py:94
  450.6 21.8 %collective-permute-start.39 = (bf16[2048,256]{1,0:T(8,128)(2,1)}, bf16[2048,256]{1,0:T(8,128)(2,1)}, u32[]{:S(2)}, u32[]{:S(2)}) collective-permute-start(bf16[2048,256]{1,0:T(8,128)(2,1)} %get-tuple-element.180), channel_id=1, source_target_pairs={{3,2},{2,3},{6,4},{4,5},{5,6},{11,8},{8,10},{10,11},{14,12},{15,13... | collective-permute-start | bytes 3145736 | tf_op jit(solution)/shard_map/ppermute | solution.py:849
  452.5 6.5 %collective-permute-start.32 = (bf16[1,144,256]{2,1,0:T(8,128)(2,1)S(1)}, bf16[1,144,256]{2,1,0:T(8,128)(2,1)S(1)}, u32[]{:S(2)}, u32[]{:S(2)}) collective-permute-start(bf16[1,144,256]{2,1,0:T(8,128)(2,1)S(1)} %get-tuple-element.228), channel_id=1, source_target_pairs={{0,4},{1,5},{2,6},{3,7},{4,0},{5,1},{6,2},{7,3},{8,12},{9,13},{10,... | collective-permute-start | bytes 221192 | tf_op jit(solution)/shard_map/ppermute | solution.py:94
  452.6 8.6 %collective-permute-start.34 = (bf16[1,144,256]{2,1,0:T(8,128)(2,1)S(1)}, bf16[1,144,256]{2,1,0:T(8,128)(2,1)S(1)}, u32[]{:S(2)}, u32[]{:S(2)}) collective-permute-start(bf16[1,144,256]{2,1,0:T(8,128)(2,1)S(1)} %get-tuple-element.229), channel_id=1, source_target_pairs={{0,12},{1,13},{2,14},{3,15},{4,8},{5,9},{6,10},{7,11},{8,4},{9,5},... | collective-permute-start | bytes 221192 | tf_op jit(solution)/shard_map/ppermute | solution.py:94
  457.3 6.1 %collective-permute-start.33 = (bf16[1,144,256]{2,1,0:T(8,128)(2,1)S(1)}, bf16[1,144,256]{2,1,0:T(8,128)(2,1)S(1)}, u32[]{:S(2)}, u32[]{:S(2)}) collective-permute-start(bf16[1,144,256]{2,1,0:T(8,128)(2,1)S(1)} %get-tuple-element.230), channel_id=1, source_target_pairs={{0,8},{1,9},{2,10},{3,11},{4,12},{5,13},{6,14},{7,15},{8,0},{9,1},... | collective-permute-start | bytes 221192 | tf_op jit(solution)/shard_map/ppermute | solution.py:94
  464.9 4.6 collective-permute-start.36
  465.3 5.4 %collective-permute-start.37 = (f32[8,128]{1,0:T(8,128)S(1)}, f32[8,128]{1,0:T(8,128)S(1)}, u32[]{:S(2)}, u32[]{:S(2)}) collective-permute-start(f32[8,128]{1,0:T(8,128)S(1)} %iota.23), channel_id=1, source_target_pairs={{0,12},{1,13},{2,14},{3,15},{4,8},{5,9},{6,10},{7,11},{8,4},{9,5},... | collective-permute-start | bytes 12296 | tf_op jit(solution)/shard_map/ppermute | solution.py:94
  467.6 3.6 collective-permute-start.35
  471.2 1.2 collective-permute-start.38
  472.4 10.6 %collective-permute-start.42 = (f32[8,128]{1,0:T(8,128)S(1)}, f32[8,128]{1,0:T(8,128)S(1)}, u32[]{:S(2)}, u32[]{:S(2)}) collective-permute-start(f32[8,128]{1,0:T(8,128)S(1)} %add.179), channel_id=1, source_target_pairs={{0,3},{1,2},{2,1},{3,0},{4,7},{5,6},{6,5},{7,4},{8,11},{9,10},{10,... | collective-permute-start | bytes 12296 | tf_op jit(solution)/shard_map/ppermute | solution.py:94
  478.2 4.8 collective-permute-start.41
  478.2 4.8 collective-permute-start.40
  (47 other events, 383.6 us)

commit v11 on v10

--- a/solution.py
+++ b/solution.py
@@ -71,6 +71,21 @@
     return walk
 
 
+def staggered(walk, last, initial):
+    peers = lax.axis_size("space")
+    up = list(zip(walk, walk[1:] + walk[:1]))
+    before, after = [], []
+    for core in (1, 0):
+        pairs = [(core * peers + i, core * peers + j) for i, j in up]
+        before.append(lax.ppermute(last, ALL, pairs))
+        after.append(lax.ppermute(initial, ALL, [(j, i) for i, j in pairs]))
+        if core == 1:
+            word = jnp.concatenate([before[0][:16], after[0][:16]], 0)
+            word = lax.ppermute(word, "dp", [(1, 0)])
+            last, initial, word = lax.optimization_barrier((last, initial, word))
+    return before, after + [word]
+
+
 def halo(walk, last, initial):
     up = list(zip(walk, walk[1:] + walk[:1]))
     down = [(j, i) for i, j in up]
@@ -131,7 +146,7 @@
     held = [held[:, :half], held[:, half:]]
     ranks = [dict(weights), dict(weights)]
     for turn in (1, 0):
-        if turn == 0:
+        if turn == 1:
             held[0], held[1], posted = lax.optimization_barrier((*held, posted))
         for n, order in enumerate(orders()):
             held[n] = jnp.concatenate([held[n], swapped(held[n], "space", order[turn])], 0)
@@ -301,26 +316,47 @@
     return ref[pl.ds(0, rows, stride=2), :], ref[pl.ds(1, rows, stride=2), :]
 
 
+def selector():
+    row = lax.broadcasted_iota(jnp.int32, (8, HALF), 0)
+    lane = lax.broadcasted_iota(jnp.int32, (8, HALF), 1)
+    slot = jnp.where(lane == CH, 64.0, jnp.where(lane == CH + 1, 1.0, 0.0))
+    known = jnp.where(lane == CH + 2, 1.0, 0.0)
+    return jnp.where(row == 0, slot, jnp.where(row == 1, known, 0.0)).astype(jnp.bfloat16)
+
+
+def ids_along(arrived):
+    codes = inner(selector(), arrived, 1, 1)
+    return jnp.where(codes[1:2, :] > 0, codes[0:1, :], -1.0).astype(jnp.int32)
+
+
+def ids_down(arrived):
+    codes = inner(arrived, selector(), 1, 1)
+    return jnp.where(codes[:, 1:2] > 0, codes[:, 0:1], -1.0).astype(jnp.int32)
+
+
 def whole(shape):
     return pl.BlockSpec(shape, lambda *_: (0,) * len(shape))
 
 
-def round_forward(index, mesh, before, own, after, mats, bias, following, decoder=()):
+def round_forward(index, place, mesh, before, own, after, mats, bias, following, decoder=()):
     blocks = mesh.shape[0]
+    choices = len(before)
     tile, chunk = 512, 16
     turns, high = tile // chunk, 2 * chunk
     more = following is not None
-    spans = [before.shape[0], own.shape[0], after.shape[0]]
+    spans = [before[0].shape[0], own.shape[0], after[0].shape[0]]
     reach = sum(spans)
 
     def body(*refs):
-        index_ref, mesh_ref, before_ref, own_ref, after_ref, mats_ref, bias_ref = refs[:7]
+        index_ref, place_ref, mesh_ref, own_ref, mats_ref, bias_ref = refs[:6]
+        sides = 2 * choices + choices - 1
+        near, refs = refs[6 : 6 + sides], (None,) + refs[:6] + refs[6 + sides :]
         raw, table, rows, wide, wider, sems = refs[-6:]
         if more:
             next_ref, sent_ref = refs[7], refs[13]
             new_ref, back_ref, update_ref, agg_ref, slope_ref = refs[8:13]
         else:
-            ids_ref, dec_ref, out_ref, head_ref = refs[7:11]
+            arrived_ref, dec_ref, out_ref, head_ref = refs[7:11]
             new_ref, back_ref, update_ref, agg_ref, slope_ref = refs[11:16]
             branch_ref, fetched_ref, decoded_ref, turn_ref = refs[16:20]
             total_ref = refs[20]
@@ -328,17 +364,28 @@
 
         @pl.when(step == 0)
         def _():
-            copies = []
-            start = 0
-            for n, (source, span) in enumerate(zip((before_ref, own_ref, after_ref), spans)):
-                copies.append(
+            def brought(sources):
+                starts = [0, spans[0], spans[0] + spans[1]]
+                copies = [
                     pltpu.make_async_copy(source, raw.at[pl.ds(start, span)], sems.at[n])
-                )
-                start = start + span
-            for copy in copies:
-                copy.start()
-            for copy in copies:
-                copy.wait()
+                    for n, (source, start, span) in enumerate(zip(sources, starts, spans))
+                ]
+                for copy in copies:
+                    copy.start()
+                for copy in copies:
+                    copy.wait()
+
+            if choices == 1:
+                brought((near[0], own_ref, near[1]))
+            else:
+
+                @pl.when(place_ref[0] == 1)
+                def _():
+                    brought((near[0], own_ref, near[2]))
+
+                @pl.when(place_ref[0] == 0)
+                def _():
+                    brought((near[1], own_ref, near[3]))
 
             @pl.loop(0, reach // 256)
             def _(i):
@@ -409,8 +456,8 @@
             weave(wide, inner(lowered, next_ref[0], 1, 0))
             sent_ref[...] = wide[...].astype(jnp.bfloat16)
             return
-        nodes = lax.broadcasted_iota(jnp.int32, (ids_ref.shape[0], tile), 1) + step * tile
-        chooser = jnp.where(nodes == ids_ref[...], 1.0, 0.0).astype(jnp.bfloat16)
+        nodes = lax.broadcasted_iota(jnp.int32, (arrived_ref.shape[0], tile), 1) + step * tile
+        chooser = jnp.where(nodes == ids_down(arrived_ref[...]), 1.0, 0.0).astype(jnp.bfloat16)
         found = inner(chooser, lowered, 1, 0)
 
         @pl.when(step == 0)
@@ -435,7 +482,8 @@
 
     whole_rows = pl.BlockSpec((tile, D), lambda i, *_: (i, 0))
     woven = pl.BlockSpec((2 * tile, HALF), lambda i, *_: (i, 0))
-    ins = [whole_rows] + [pl.BlockSpec(memory_space=pl.ANY)] * 3 + [whole(mats.shape), whole(bias.shape)]
+    far = pl.BlockSpec(memory_space=pl.ANY)
+    ins = [whole_rows, far, whole(mats.shape), whole(bias.shape)] + [far] * (2 * choices + choices - 1)
     outs = [whole_rows] * 4 + [pl.BlockSpec((K, 2 * tile, HALF), lambda i, *_: (0, i, 0))]
     shapes = [
         jax.ShapeDtypeStruct((blocks, D), jnp.float32),
@@ -444,7 +492,7 @@
         jax.ShapeDtypeStruct((blocks, D), jnp.bfloat16),
         jax.ShapeDtypeStruct((K, 2 * blocks, HALF), jnp.bfloat16),
     ]
-    args = [index, mesh, before, own, after, mats, bias]
+    args = [index, place, mesh, own, mats, bias, *before, *after]
     if more:
         ins.append(pl.BlockSpec((1, D, D), lambda *_: (0, 0, 0)))
         outs.append(woven)
@@ -462,7 +510,7 @@
     return pl.pallas_call(
         body,
         grid_spec=pltpu.PrefetchScalarGridSpec(
-            num_scalar_prefetch=1,
+            num_scalar_prefetch=2,
             grid=(blocks // tile,),
             in_specs=ins,
             out_specs=outs,
@@ -496,7 +544,7 @@
             (new_ref, out_ref, sent_ref), rest = rest[:3], rest[3:]
         else:
             index_ref, back_ref, slope_ref, mats_ref = refs[:4]
-            (ids_ref, landed_ref, turn_ref, w_out_ref, w_dec_ref), rest = refs[4:9], refs[9:]
+            (arrived_ref, landed_ref, turn_ref, w_out_ref, w_dec_ref), rest = refs[4:9], refs[9:]
             (new_ref, out_ref, gdec_ref), rest = rest[:3], rest[3:]
             gathered, rest = rest[5], rest[:5] + rest[6:]
         guin_ref, low_ref, before_ref, own_ref, after_ref, wide, wider, flows, *tables = rest
@@ -526,7 +574,8 @@
                 gathered[...] = inner(grad_dec, w_dec_ref[...], 1, 1).astype(jnp.bfloat16)
 
             nodes = lax.broadcasted_iota(jnp.int32, (tile, landed_ref.shape[0]), 0) + step * tile
-            chooser = jnp.where(nodes == ids_ref[...], 1.0, 0.0).astype(jnp.bfloat16)
+            chooser = jnp.where(nodes == ids_along(arrived_ref[...]), 1.0, 0.0)
+            chooser = chooser.astype(jnp.bfloat16)
             new = inner(chooser, gathered[...], 1, 0)
             new_ref[...] = new
             grad_out = new.astype(jnp.bfloat16)
@@ -686,11 +735,11 @@
     )(grad_mesh, own, first, last, grad_uin, dest_low, mats)
 
 
-def encode_rows(arrived, ids, w_in, w_node, biases, source):
+def encode_rows(arrived, w_in, w_node, biases, source):
     posts = arrived.shape[0]
     tile = 512
 
-    def body(arrived_ref, ids_ref, in_ref, node_ref, bias_ref, source_ref, mesh_ref, gathered_ref, sent_ref, encoded, wide):
+    def body(arrived_ref, in_ref, node_ref, bias_ref, source_ref, mesh_ref, gathered_ref, sent_ref, encoded, wide):
         step = pl.program_id(0)
 
         @pl.when(step == 0)
@@ -699,7 +748,7 @@
             encoded[...] = silu(entering).astype(jnp.bfloat16)
 
         nodes = lax.broadcasted_iota(jnp.int32, (tile, posts), 0) + step * tile
-        chooser = jnp.where(nodes == ids_ref[...], 1.0, 0.0).astype(jnp.bfloat16)
+        chooser = jnp.where(nodes == ids_along(arrived_ref[...]), 1.0, 0.0).astype(jnp.bfloat16)
         gathered = inner(chooser, encoded[...], 1, 0).astype(jnp.bfloat16)
         gathered_ref[...] = gathered
         mesh = silu(inner(gathered, node_ref[...], 1, 0) + bias_ref[1:2, :])
@@ -708,7 +757,7 @@
         sent_ref[...] = wide[...].astype(jnp.bfloat16)
 
     rows = pl.BlockSpec((tile, D), lambda i: (i, 0))
-    args = (arrived, ids, w_in, w_node, biases, source)
+    args = (arrived, w_in, w_node, biases, source)
     return pl.pallas_call(
         body,
         grid=(H // tile,),
@@ -727,12 +776,12 @@
     )(*args)
 
 
-def encode_backward(grad_mesh, gathered, arrived, ids, w_in, w_node, biases):
+def encode_backward(grad_mesh, gathered, arrived, w_in, w_node, biases):
     posts = arrived.shape[0]
     tile = 512
     steps = H // tile
 
-    def body(grad_ref, gathered_ref, arrived_ref, ids_ref, in_ref, node_ref, bias_ref, gin_ref, gnode_ref, gbias_ref, total):
+    def body(grad_ref, gathered_ref, arrived_ref, in_ref, node_ref, bias_ref, gin_ref, gnode_ref, gbias_ref, total):
         step = pl.program_id(0)
 
         @pl.when(step == 0)
@@ -747,7 +796,7 @@
         gnode_ref[...] += inner(gathered_ref[...], grad_node, 0, 0)
         back = inner(grad_node, node_ref[...], 1, 1).astype(jnp.bfloat16)
         nodes = lax.broadcasted_iota(jnp.int32, (posts, tile), 1) + step * tile
-        chooser = jnp.where(nodes == ids_ref[...], 1.0, 0.0).astype(jnp.bfloat16)
+        chooser = jnp.where(nodes == ids_down(arrived_ref[...]), 1.0, 0.0).astype(jnp.bfloat16)
         total[...] += inner(chooser, back, 1, 0)
 
         @pl.when(step == steps - 1)
@@ -758,7 +807,7 @@
             gin_ref[...] = inner(arrived_ref[...], grad_enc, 0, 0)
 
     rows = pl.BlockSpec((tile, D), lambda i: (i, 0))
-    args = (grad_mesh, gathered, arrived, ids, w_in, w_node, biases)
+    args = (grad_mesh, gathered, arrived, w_in, w_node, biases)
     shapes = [(HALF, D), (D, D), (2, D)]
     return pl.pallas_call(
         body,
@@ -825,17 +874,14 @@
     w_in, w_node, w_dec, w_out, *w_round, biases, digits = spread_rows(
         held, total_size, peers, place
     )
+    arrived, biases = lax.optimization_barrier((arrived, biases))
     count = digits[0, 0] * 65536.0 + digits[0, 1] * 256.0 + digits[0, 2]
     w_out = jnp.pad(w_out.reshape(D, CH), ((0, 0), (0, HALF - CH)))
     w_round = [mats.reshape(5, D, D) for mats in w_round]
     b_head = biases[:3]
     b_round = biases[3:].reshape(ROUNDS, 2, D)
-    arrived, biases = lax.optimization_barrier((arrived, biases))
-    ids = arrived[:, CH : CH + 3].astype(jnp.int32)
-    ids = jnp.where(ids[:, 2:3] > 0, ids[:, 0:1] * 64 + ids[:, 1:2], -1)
-    ids_row = ids.reshape(1, -1)
     mesh, gathered, sent = encode_rows(
-        arrived, ids_row, w_in, w_node, biases, w_round[0]
+        arrived, w_in, w_node, biases, w_round[0]
     )
     sent, partner, neighbours, counted = lax.optimization_barrier(
         (sent, partner, neighbours, counted)
@@ -843,7 +889,7 @@
     index = 2 * ((neighbours - band * blocks + H) % (blocks * bands)).T.reshape(-1)
     moved = [(n, place) for n, place in enumerate(walk) if n != place]
     stays = jnp.asarray([n == place for n, place in enumerate(walk)])[band]
-    index = jnp.where(stays, index, lax.ppermute(index, "space", moved))
+    index = lax.ppermute(index, "space", list(enumerate(walk)))
 
     def at_home(rows):
         return lax.ppermute(rows, "space", [(j, i) for i, j in moved])
@@ -862,15 +908,18 @@
         ],
         1,
     )
+    core = lax.axis_index("dp").reshape(1)
     kept = []
     for layer in range(ROUNDS):
-        before, after = halo(walk, sent[2 * (blocks - H) :], sent[: 2 * H])
         if layer == 0:
+            before, after = staggered(walk, sent, sent)
             before, valid_around = lax.optimization_barrier((before, valid_around))
+        else:
+            before, after = [[rows] for rows in halo(walk, sent, sent)]
         following = w_round[layer + 1] if layer + 1 < ROUNDS else None
         new, back, update, agg, slopes, *rest = round_forward(
-            index, mesh, before, sent, after, w_round[layer], b_round[layer], following,
-            () if following is not None else (ids, w_dec, w_out, biases),
+            index, core, mesh, before, sent, after, w_round[layer], b_round[layer], following,
+            () if following is not None else (arrived, w_dec, w_out, biases),
         )
         kept.append((mesh, back, update, agg, slopes))
         mesh = new
@@ -923,7 +972,7 @@
         first_step = not carried
         grad_mesh, leaving, extra, grad_uin, dest_low, to_before, own, to_after = edges_backward(
             index, grad_mesh, back, slopes, w_round[layer], carried,
-            (ids_row, landed, dec_turn, w_out, w_dec) if first_step else (),
+            (arrived, landed, dec_turn, w_out, w_dec) if first_step else (),
         )
         if not first_step:
             mats_grads[5 * layer + 5] = inner(
@@ -954,7 +1003,7 @@
     grad_mesh, leaving, sent_low = round_backward(grad_mesh, *carried)
     mats_grads[0] = inner(kept[0][0].astype(jnp.bfloat16), sent_low, 0, 0)
     grad_win, grad_wnode, grad_bpair = encode_backward(
-        grad_mesh, gathered, arrived, ids, w_in, w_node, biases
+        grad_mesh, gathered, arrived, w_in, w_node, biases
     )
     parts = [grad_win, grad_wnode, grad_wdec, grad_wout.reshape(CH, D)]
     parts = parts + mats_grads

time: 490 us -> 514 us (1.049); the launches traced: 488 us -> 505 us
  starting transfers between devices: 76.9 us -> 87.9 us
    ppermute x1 -> x6, waiting for transfers between devices: 0.01 us -> 19.4 us  [the longest x1 19.4 us: staggered(): word = lax.ppermute(word, 'dp', [(1, 0)])]
    ppermute x6 -> x5, waiting for transfers between devices: 41.1 us -> 29.3 us  [halo(): lax.ppermute(initial, 'space', down)]
    ppermute x1 -> x6, starting transfers between devices: 0.66 us -> 11 us  [the longest x2 6.44 us: staggered(): after.append(lax.ppermute(initial, ALL, [(j, i) for i, j in pairs]))]
    ppermute x4, waiting for transfers between devices: 19.1 us -> 9.48 us  [shifted(): return lax.ppermute(shard, axis, pairs)]
    ppermute x6 -> x5, starting transfers between devices: 14.5 us -> 11 us  [halo(): lax.ppermute(initial, 'space', down)]
    ppermute x6 -> x5, waiting for transfers between devices: 29.5 us -> 27.3 us  [halo(): lax.ppermute(last, 'space', up)]
  transfers between devices with their start and end apart: 46 -> 49, of which waited for: 28 -> 27; matrix products, arithmetic and copies ran while one was open for 11% -> 10% of each run, Pallas kernels for 6% -> 6%
where the time goes in v11:
time: 514 us; the launch traced here: 505 us
  Pallas kernels  192 us (37%)
  waiting for transfers between devices  135 us (26%)
  starting transfers between devices  87.9 us (17%)
  other arithmetic  33.3 us (6%)
  matrix products  29.8 us (6%)
  local copies, waits for them, and re-layouts  18.3 us (4%)
  between operations  8.36 us (2%)
    pallas_call x3, Pallas kernels, edges_backward(): pl.pallas_call(body, grid_spec=pltpu.PrefetchScalarGridSpec(num_scalar_pr...  81.8 us
    pallas_call x3, Pallas kernels, round_forward(): pl.pallas_call(body, grid_spec=pltpu.PrefetchScalarGridSpec(num_scalar_pr...  80.1 us
    ppermute x24, waiting for transfers between devices, swapped(): lax.ppermute(value, axis, [(i, i ^ bit) for i in range(lax.axis_size(axis...  31.4 us
    ppermute x24, starting transfers between devices, swapped(): lax.ppermute(value, axis, [(i, i ^ bit) for i in range(lax.axis_size(axis...  29.8 us
    dot_general x19, matrix products, inner(): lax.dot_general(left, right, (((left_dim,), (right_dim,)), ((), ())), pre...  29.5 us
    ppermute x5, waiting for transfers between devices, halo(): lax.ppermute(initial, 'space', down)  29.3 us
    ppermute x5, waiting for transfers between devices, halo(): lax.ppermute(last, 'space', up)  27.3 us
    ppermute x1, waiting for transfers between devices, staggered(): word = lax.ppermute(word, 'dp', [(1, 0)])  19.4 us
  transfers between devices with their start and end apart: 49, of which 27 were waited for; matrix products, arithmetic and copies ran while one was open for 10% of the time, Pallas kernels for 6%

profile of v11, /device:TPU:0, one launch (start us, length us, event | category | flops | bytes accessed | tf_op | source)
XLA Modules:
  0.0 504.6 jit_solution(15764971215489341528)
XLA Ops:
  5.8 5.1 %collective-permute-start.2 = (bf16[1,144,256]{2,1,0:T(8,128)(2,1)S(1)}, bf16[1,144,256]{2,1,0:T(8,128)(2,1)S(1)}, u32[]{:S(2)}, u32[]{:S(2)}) collective-permute-start(bf16[1,144,256]{2,1,0:T(8,128)(2,1)S(1)} %dynamic_update_slice.8), channel_id=1, source_target_pairs={{0,12},{1,13},{2,14},{3,15},{4,8},{5,9},{6,10},{7,11},{8,4},{9,5},... | collective-permute-start | bytes 221192 | tf_op jit(solution)/shard_map/ppermute | solution.py:109
  26.9 4.6 collective-permute-done.6
  32.9 6.2 %all-to-all-start = ((bf16[16,64,128]{2,1,0:T(8,128)(2,1)}), bf16[16,64,128]{2,1,0:T(8,128)(2,1)S(1)}, u32[]{:S(2)}, u32[]{:S(2)}) async-start(bf16[16,64,128]{2,1,0:T(8,128)(2,1)} %bitcast.5), calls=%async_computation | async-start | bytes 524288 | tf_op jit(solution)/shard_map/all_to_all | solution.py:868
  40.3 4.0 spread_rows.1
  44.3 5.4 %all-to-all-done = bf16[16,64,128]{2,1,0:T(8,128)(2,1)S(1)} async-done(((bf16[16,64,128]{2,1,0:T(8,128)(2,1)}), bf16[16,64,128]{2,1,0:T(8,128)(2,1)S(1)}, u32[]{:S(2)}, u32[]{:S(2)}) %all-to-all-start) | async-done | bytes 262176 | tf_op jit(solution)/shard_map/all_to_all | solution.py:868
  50.4 6.3 %encode_rows.1 = (f32[2048,256]{1,0:T(8,128)}, bf16[2048,256]{1,0:T(8,128)(2,1)}, bf16[4096,128]{1,0:T(8,128)(2,1)}) custom-call(bf16[1024,128]{1,0:T(8,128)(2,1)} %bitcast.145, bf16[128,256]{1,0:T(8,128)(2,1)} %get-tuple-element.106.in_ref, bf16[256,256]{1,0:T(8,128)(2,1)} %get-tuple-element.107.node_ref, f32[9,256]{1,0:T(8,128)} %get-tuple-element.108.bias_ref.refs_11_, ...), custom_call_target="tpu_custom_call" | custom-call | bytes 15000000 | tf_op jit(solution)/shard_map/encode_rows/pallas_call | solution.py:761
  59.5 19.4 %collective-permute-done.12.refs_10_ = bf16[32,128]{1,0:T(8,128)(2,1)} collective-permute-done((bf16[32,128]{1,0:T(8,128)(2,1)S(1)}, bf16[32,128]{1,0:T(8,128)(2,1)}, u32[]{:S(2)}, u32[]{:S(2)}) %collective-permute-start.12) | collective-permute-done | bytes 8224 | tf_op jit(solution)/shard_map/ppermute | solution.py:84
  80.9 5.7 %collective-permute-start.16 = (bf16[4096,128]{1,0:T(8,128)(2,1)}, bf16[4096,128]{1,0:T(8,128)(2,1)}, u32[]{:S(2)}, u32[]{:S(2)}) collective-permute-start(bf16[4096,128]{1,0:T(8,128)(2,1)} %get-tuple-element.119.refs_3_), channel_id=1, source_target_pairs={{1,0},{3,1},{2,3},{6,2},{4,6},{5,4},{7,5},{11,7},{9,11},{8,9},{10,... | collective-permute-start | bytes 3145736 | tf_op jit(solution)/shard_map/ppermute | solution.py:81
  88.8 5.2 %collective-permute-start.14 = (bf16[79,360]{1,0:T(8,128)(2,1)S(1)}, bf16[79,360]{1,0:T(8,128)(2,1)}, u32[]{:S(2)}, u32[]{:S(2)}) collective-permute-start(bf16[79,360]{1,0:T(8,128)(2,1)S(1)} %get-tuple-element.240), channel_id=1, source_target_pairs={{0,1},{1,2},{2,3},{3,4},{4,5},{5,6},{6,7},{7,8},{8,9},{9,10},{10,1... | collective-permute-start | bytes 170648 | tf_op jit(solution)/shard_map/ppermute | solution.py:49
  95.4 4.4 collective-permute-done.15
  102.5 24.9 %round_forward.3 = (f32[2048,256]{1,0:T(8,128)}, f32[2048,256]{1,0:T(8,128)}, bf16[2048,256]{1,0:T(8,128)(2,1)}, bf16[2048,256]{1,0:T(8,128)(2,1)}, bf16[6,4096,...) custom-call(s32[12288]{0:T(1024)} %copy-done.15, s32[1]{0:T(128)} %bitcast.11.refs_1_, ...), custom_call_target="tpu_custom_call" | custom-call | bytes 75000000 | tf_op jit(solution)/shard_map/round_forward/pallas_call | solution.py:510
  129.5 15.1 %collective-permute-done.18.refs_7_ = bf16[4096,128]{1,0:T(8,128)(2,1)S(1)} collective-permute-done((bf16[4096,128]{1,0:T(8,128)(2,1)}, bf16[4096,128]{1,0:T(8,128)(2,1)S(1)}, u32[]{:S(2)}, u32[]{:S(2)}) %collective-permute-start.18) | collective-permute-done | bytes 1048608 | tf_op jit(solution)/shard_map/ppermute | solution.py:92
  144.6 3.9 collective-permute-done.17.refs_6_
  149.5 25.1 %round_forward.4 = (f32[2048,256]{1,0:T(8,128)}, f32[2048,256]{1,0:T(8,128)}, bf16[2048,256]{1,0:T(8,128)(2,1)}, bf16[2048,256]{1,0:T(8,128)(2,1)}, bf16[6,4096,...) custom-call(s32[12288]{0:T(1024)} %copy-done.15, s32[1]{0:T(128)} %bitcast.11.refs_1_, ...), custom_call_target="tpu_custom_call" | custom-call | bytes 75000000 | tf_op jit(solution)/shard_map/round_forward/pallas_call | solution.py:510
  177.7 14.2 %collective-permute-done.20.refs_7_ = bf16[4096,128]{1,0:T(8,128)(2,1)S(1)} collective-permute-done((bf16[4096,128]{1,0:T(8,128)(2,1)}, bf16[4096,128]{1,0:T(8,128)(2,1)S(1)}, u32[]{:S(2)}, u32[]{:S(2)}) %collective-permute-start.20) | collective-permute-done | bytes 1048608 | tf_op jit(solution)/shard_map/ppermute | solution.py:92
  191.9 2.6 collective-permute-done.19.refs_6_
  195.5 30.1 %round_forward.5 = (f32[2048,256]{1,0:T(8,128)}, f32[2048,256]{1,0:T(8,128)}, bf16[2048,256]{1,0:T(8,128)(2,1)}, bf16[2048,256]{1,0:T(8,128)(2,1)}, bf16[6,4096,...) custom-call(s32[12288]{0:T(1024)} %copy-done.15, ...), custom_call_target="tpu_custom_call" | custom-call | bytes 75000000 | tf_op jit(solution)/shard_map/round_forward/pallas_call | solution.py:510
  225.6 3.5 all-to-all-start.1
  231.8 5.8 %all-to-all-done.1 = bf16[16,64,128]{2,1,0:T(8,128)(2,1)S(1)} async-done(((bf16[16,64,128]{2,1,0:T(8,128)(2,1)}), bf16[16,64,128]{2,1,0:T(8,128)(2,1)S(1)}, u32[]{:S(2)}, u32[]{:S(2)}) %all-to-all-start.1) | async-done | bytes 262176 | tf_op jit(solution)/shard_map/all_to_all | solution.py:868
  238.2 3.3 collective-permute-start.21
  242.9 5.1 %collective-permute-done.22 = bf16[78,360]{1,0:T(8,128)(2,1)S(1)} collective-permute-done((bf16[78,360]{1,0:T(8,128)(2,1)S(1)}, bf16[78,360]{1,0:T(8,128)(2,1)S(1)}, u32[]{:S(2)}, u32[]{:S(2)}) %collective-permute-start.22) | collective-permute-done | bytes 56192 | tf_op jit(solution)/shard_map/ppermute | solution.py:49
  251.0 6.4 %all-to-all-start.2 = ((bf16[16,64,128]{2,1,0:T(8,128)(2,1)}), bf16[16,64,128]{2,1,0:T(8,128)(2,1)S(1)}, u32[]{:S(2)}, u32[]{:S(2)}) async-start(bf16[16,64,128]{2,1,0:T(8,128)(2,1)} %bitcast.18), calls=%async_computation.2 | async-start | bytes 524288 | tf_op jit(solution)/shard_map/all_to_all | solution.py:868
  259.2 6.8 %all-to-all-done.2 = bf16[16,64,128]{2,1,0:T(8,128)(2,1)S(1)} async-done(((bf16[16,64,128]{2,1,0:T(8,128)(2,1)}), bf16[16,64,128]{2,1,0:T(8,128)(2,1)S(1)}, u32[]{:S(2)}, u32[]{:S(2)}) %all-to-all-start.2) | async-done | bytes 262176 | tf_op jit(solution)/shard_map/all_to_all | solution.py:868
  267.9 27.4 %edges_backward.3 = (f32[2048,256]{1,0:T(8,128)}, bf16[2048,256]{1,0:T(8,128)(2,1)}, bf16[1024,256]{1,0:T(8,128)(2,1)}, bf16[2048,256]{1,0:T(8,128)(2,1)}, bf16[...) custom-call(s32[12288]{0:T(1024)} %copy-done.15, ...), custom_call_target="tpu_custom_call" | custom-call | bytes 75000000 | tf_op jit(solution)/shard_map/edges_backward/pallas_call | solution.py:653
  302.2 2.6 fusion.94.refs_16_
  304.7 2.7 fusion.95.refs_18_
  310.1 2.6 collective-permute-start.25
  314.7 3.4 convert_select_fusion
  318.2 7.2 %collective-permute-done.24.refs_6_ = bf16[4096,128]{1,0:T(8,128)(2,1)} collective-permute-done((bf16[4096,128]{1,0:T(8,128)(2,1)S(1)}, bf16[4096,128]{1,0:T(8,128)(2,1)}, u32[]{:S(2)}, u32[]{:S(2)}) %collective-permute-start.24) | collective-permute-done | bytes 1048608 | tf_op jit(solution)/shard_map/ppermute | solution.py:92
  325.4 27.2 %edges_backward.4 = (f32[2048,256]{1,0:T(8,128)}, bf16[2048,256]{1,0:T(8,128)(2,1)}, bf16[2048,256]{1,0:T(8,128)(2,1)}, bf16[2048,256]{1,0:T(8,128)(2,1)}, bf16[...) custom-call(s32[12288]{0:T(1024)} %copy-done.15, ...), custom_call_target="tpu_custom_call" | custom-call | bytes 84000000 | tf_op jit(solution)/shard_map/edges_backward/pallas_call | solution.py:653
  354.8 2.5 fusion.92.refs_11_
  358.8 2.6 collective-permute-start.27
  367.0 7.3 %collective-permute-done.26.refs_6_ = bf16[4096,128]{1,0:T(8,128)(2,1)S(1)} collective-permute-done((bf16[4096,128]{1,0:T(8,128)(2,1)}, bf16[4096,128]{1,0:T(8,128)(2,1)S(1)}, u32[]{:S(2)}, u32[]{:S(2)}) %collective-permute-start.26) | collective-permute-done | bytes 1048608 | tf_op jit(solution)/shard_map/ppermute | solution.py:92
  375.4 27.2 %edges_backward.5 = (f32[2048,256]{1,0:T(8,128)}, bf16[2048,256]{1,0:T(8,128)(2,1)}, bf16[2048,256]{1,0:T(8,128)(2,1)}, bf16[2048,256]{1,0:T(8,128)(2,1)}, bf16[...) custom-call(s32[12288]{0:T(1024)} %copy-done.15, ...), custom_call_target="tpu_custom_call" | custom-call | bytes 84000000 | tf_op jit(solution)/shard_map/edges_backward/pallas_call | solution.py:653
  404.8 2.5 fusion.90.refs_6_
  407.3 4.0 collective-permute-start.29
  417.7 6.4 %collective-permute-done.28.refs_2_ = bf16[4096,128]{1,0:T(8,128)(2,1)S(1)} collective-permute-done((bf16[4096,128]{1,0:T(8,128)(2,1)}, bf16[4096,128]{1,0:T(8,128)(2,1)S(1)}, u32[]{:S(2)}, u32[]{:S(2)}) %collective-permute-start.28) | collective-permute-done | bytes 1048608 | tf_op jit(solution)/shard_map/ppermute | solution.py:92
  425.1 6.1 %round_backward.1 = (f32[2048,256]{1,0:T(8,128)}, bf16[2048,256]{1,0:T(8,128)(2,1)}, bf16[2048,256]{1,0:T(8,128)(2,1)}) custom-call(f32[2048,256]{1,0:T(8,128)} %get-tuple-element.158.refs_0_, f32[4096,128]{1,0:T(8,128)} %get-tuple-element.159.refs_1_, bf16[4096,128]{1,0:T(8,128)(2,1)} %copy-done.20, bf16[4096,128]{1,0:T(8,128)(2,1)} %collective-permute-done.29.refs_3_, ...), custom_call_target="tpu_custom_call" | custom-call | bytes 21000000 | tf_op jit(solution)/shard_map/round_backward/pallas_call | solution.py:725
  431.2 2.4 fusion.75.refs_4_
  433.6 8.6 %encode_backward.1 = (f32[128,256]{1,0:T(8,128)}, f32[256,256]{1,0:T(8,128)}, f32[2,256]{1,0:T(2,128)}) custom-call(f32[2048,256]{1,0:T(8,128)} %get-tuple-element.164.grad_ref, bf16[2048,256]{1,0:T(8,128)(2,1)} %get-tuple-element.165.gathered_ref, bf16[1024,128]{1,0:T(8,128)(2,1)} %bitcast.148, bf16[128,256]{1,0:T(8,128)(2,1)} %get-tuple-element.106.in_ref, ...), custom_call_target="tpu_custom_call" | custom-call | bytes 21000000 | tf_op jit(solution)/shard_map/encode_backward/pallas_call | solution.py:812
  442.2 5.1 %collect_rows.1 = (f32[16,144,256]{2,1,0:T(8,128)}, bf16[16,144,256]{2,1,0:T(8,128)(2,1)}) custom-call(s32[1]{0:T(128)} %bitcast.7.place_ref, f32[128,256]{1,0:T(8,128)} %get-tuple-element.166.refs_0_, f32[256,256]{1,0:T(8,128)} %get-tuple-element.167.refs_1_, f32[256,256]{1,0:T(8,128)} %fusion.89.refs_2_, f32[78,256]{1,0:T(8,128)} %reshape.158.refs_3_, ...), custom_call_target="tpu_custom_call" | custom-call | bytes 15000000 | tf_op jit(solution)/shard_map/collect_rows/pallas_call | solution.py:256
  447.3 3.0 collective-permute-done.30
  452.7 8.9 %collective-permute-done.31 = bf16[4,2,72,256]{3,2,0,1:T(8,128)(2,1)S(1)} collective-permute-done((bf16[4,2,72,256]{3,2,0,1:T(8,128)(2,1)S(1)}, bf16[4,2,72,256]{3,2,0,1:T(8,128)(2,1)S(1)}, u32[]{:S(2)}, u32[]{:S(2)}) %collective-permute-start.31) | collective-permute-done | bytes 294944 | tf_op jit(solution)/shard_map/ppermute | solution.py:109
  463.6 3.3 collective-permute-done.32
  469.4 4.7 collective-permute-start.37
  482.3 2.3 collective-permute-start.40
  489.3 5.5 %collective-permute-start.45 = (f32[8,128]{1,0:T(8,128)S(1)}, f32[8,128]{1,0:T(8,128)S(1)}, u32[]{:S(2)}, u32[]{:S(2)}) collective-permute-start(f32[8,128]{1,0:T(8,128)S(1)} %add.175), channel_id=1, source_target_pairs={{0,3},{1,2},{2,1},{3,0},{4,7},{5,6},{6,5},{7,4},{8,11},{9,10},{10,... | collective-permute-start | bytes 12296 | tf_op jit(solution)/shard_map/ppermute | solution.py:109
  496.3 3.3 select_bitcast_fusion
  (283 shorter events, 104.2 us)
Async XLA Ops:
  5.8 12.4 %collective-permute-start.2 = (bf16[1,144,256]{2,1,0:T(8,128)(2,1)S(1)}, bf16[1,144,256]{2,1,0:T(8,128)(2,1)S(1)}, u32[]{:S(2)}, u32[]{:S(2)}) collective-permute-start(bf16[1,144,256]{2,1,0:T(8,128)(2,1)S(1)} %dynamic_update_slice.8), channel_id=1, source_target_pairs={{0,12},{1,13},{2,14},{3,15},{4,8},{5,9},{6,10},{7,11},{8,4},{9,5},... | collective-permute-start | bytes 221192 | tf_op jit(solution)/shard_map/ppermute | solution.py:109
  10.9 7.3 %collective-permute-start.1 = (bf16[1,144,256]{2,1,0:T(8,128)(2,1)S(1)}, bf16[1,144,256]{2,1,0:T(8,128)(2,1)S(1)}, u32[]{:S(2)}, u32[]{:S(2)}) collective-permute-start(bf16[1,144,256]{2,1,0:T(8,128)(2,1)S(1)} %dynamic_update_slice.8), channel_id=1, source_target_pairs={{0,8},{1,9},{2,10},{3,11},{4,12},{5,13},{6,14},{7,15},{8,0},{9,1},... | collective-permute-start | bytes 221192 | tf_op jit(solution)/shard_map/ppermute | solution.py:109
  10.9 7.3 %collective-permute-start = (bf16[1,144,256]{2,1,0:T(8,128)(2,1)S(1)}, bf16[1,144,256]{2,1,0:T(8,128)(2,1)S(1)}, u32[]{:S(2)}, u32[]{:S(2)}) collective-permute-start(bf16[1,144,256]{2,1,0:T(8,128)(2,1)S(1)} %dynamic_update_slice.8), channel_id=1, source_target_pairs={{0,4},{1,5},{2,6},{3,7},{4,0},{5,1},{6,2},{7,3},{8,12},{9,13},{10,... | collective-permute-start | bytes 221192 | tf_op jit(solution)/shard_map/ppermute | solution.py:109
  18.3 5.2 %collective-permute-start.5 = (bf16[4,72,256]{2,1,0:T(8,128)(2,1)S(1)}, bf16[4,72,256]{2,1,0:T(8,128)(2,1)S(1)}, u32[]{:S(2)}, u32[]{:S(2)}) collective-permute-start(bf16[4,72,256]{2,1,0:T(8,128)(2,1)S(1)} %get-tuple-element.103), channel_id=1, source_target_pairs={{0,1},{1,0},{2,3},{3,2},{4,5},{5,4},{6,7},{7,6},{8,9},{9,8},{10,11... | collective-permute-start | bytes 442376 | tf_op jit(solution)/shard_map/ppermute | solution.py:109
  20.0 6.0 %collective-permute-start.3 = (bf16[4,72,256]{2,1,0:T(8,128)(2,1)S(1)}, bf16[4,72,256]{2,1,0:T(8,128)(2,1)S(1)}, u32[]{:S(2)}, u32[]{:S(2)}) collective-permute-start(bf16[4,72,256]{2,1,0:T(8,128)(2,1)S(1)} %get-tuple-element.102), channel_id=1, source_target_pairs={{0,2},{1,3},{2,0},{3,1},{4,6},{5,7},{6,4},{7,5},{8,10},{9,11},{10,... | collective-permute-start | bytes 442376 | tf_op jit(solution)/shard_map/ppermute | solution.py:109
  23.5 7.9 %collective-permute-start.6 = (bf16[8,72,256]{2,1,0:T(8,128)(2,1)S(1)}, bf16[8,72,256]{2,1,0:T(8,128)(2,1)S(1)}, u32[]{:S(2)}, u32[]{:S(2)}) collective-permute-start(bf16[8,72,256]{2,1,0:T(8,128)(2,1)S(1)} %pad_maximum_fusion.4), channel_id=1, source_target_pairs={{0,2},{1,3},{2,0},{3,1},{4,6},{5,7},{6,4},{7,5},{8,10},{9,11},{10,... | collective-permute-start | bytes 884744 | tf_op jit(solution)/shard_map/ppermute | solution.py:109
  26.0 6.8 %collective-permute-start.4 = (bf16[8,72,256]{2,1,0:T(8,128)(2,1)S(1)}, bf16[8,72,256]{2,1,0:T(8,128)(2,1)S(1)}, u32[]{:S(2)}, u32[]{:S(2)}) collective-permute-start(bf16[8,72,256]{2,1,0:T(8,128)(2,1)S(1)} %pad_maximum_fusion.3), channel_id=1, source_target_pairs={{0,1},{1,0},{2,3},{3,2},{4,5},{5,4},{6,7},{7,6},{8,9},{9,8},{10,11... | collective-permute-start | bytes 884744 | tf_op jit(solution)/shard_map/ppermute | solution.py:109
  31.5 7.7 %collective-permute-start.8 = (bf16[16,72,256]{2,1,0:T(8,128)(2,1)S(1)}, bf16[16,72,256]{2,1,0:T(8,128)(2,1)S(1)}, u32[]{:S(2)}, u32[]{:S(2)}) collective-permute-start(bf16[16,72,256]{2,1,0:T(8,128)(2,1)S(1)} %constant_dynamic-update-slice_fusion.3.refs_1_), channel_id=1, source_target_pairs={{0,16},{16,0},{1,17},{17,1},{2,18},{18,2},{3,19},{19,3},{4,20},{20... | collective-permute-start | bytes 1769480 | tf_op jit(solution)/shard_map/ppermute | solution.py:109
  32.8 6.4 %collective-permute-start.7 = (bf16[16,72,256]{2,1,0:T(8,128)(2,1)S(1)}, bf16[16,72,256]{2,1,0:T(8,128)(2,1)S(1)}, u32[]{:S(2)}, u32[]{:S(2)}) collective-permute-start(bf16[16,72,256]{2,1,0:T(8,128)(2,1)S(1)} %constant_dynamic-update-slice_fusion.refs_0_), channel_id=1, source_target_pairs={{0,16},{16,0},{1,17},{17,1},{2,18},{18,2},{3,19},{19,3},{4,20},{20... | collective-permute-start | bytes 1769480 | tf_op jit(solution)/shard_map/ppermute | solution.py:109
  32.9 16.7 %all-to-all-start = ((bf16[16,64,128]{2,1,0:T(8,128)(2,1)}), bf16[16,64,128]{2,1,0:T(8,128)(2,1)S(1)}, u32[]{:S(2)}, u32[]{:S(2)}) async-start(bf16[16,64,128]{2,1,0:T(8,128)(2,1)} %bitcast.5), calls=%async_computation | async-start | bytes 524288 | tf_op jit(solution)/shard_map/all_to_all | solution.py:868
  56.7 1.5 collective-permute-start.11
  58.2 20.7 %collective-permute-start.12 = (bf16[32,128]{1,0:T(8,128)(2,1)S(1)}, bf16[32,128]{1,0:T(8,128)(2,1)}, u32[]{:S(2)}, u32[]{:S(2)}) collective-permute-start(bf16[32,128]{1,0:T(8,128)(2,1)S(1)} %pad_maximum_fusion.7), channel_id=1, source_target_pairs={{16,0},{17,1},{18,2},{19,3},{20,4},{21,5},{22,6},{23,7},{24,8},{25... | collective-permute-start | bytes 24584 | tf_op jit(solution)/shard_map/ppermute | solution.py:84
  79.0 22.5 %collective-permute-start.13 = (bf16[4096,128]{1,0:T(8,128)(2,1)}, bf16[4096,128]{1,0:T(8,128)(2,1)S(1)}, u32[]{:S(2)}, u32[]{:S(2)}) collective-permute-start(bf16[4096,128]{1,0:T(8,128)(2,1)} %get-tuple-element.119.refs_3_), channel_id=1, source_target_pairs={{0,1},{1,3},{3,2},{2,6},{6,4},{4,5},{5,7},{7,11},{11,9},{9,8},{8,1... | collective-permute-start | bytes 3145736 | tf_op jit(solution)/shard_map/ppermute | solution.py:80
  80.9 20.6 %collective-permute-start.16 = (bf16[4096,128]{1,0:T(8,128)(2,1)}, bf16[4096,128]{1,0:T(8,128)(2,1)}, u32[]{:S(2)}, u32[]{:S(2)}) collective-permute-start(bf16[4096,128]{1,0:T(8,128)(2,1)} %get-tuple-element.119.refs_3_), channel_id=1, source_target_pairs={{1,0},{3,1},{2,3},{6,2},{4,6},{5,4},{7,5},{11,7},{9,11},{8,9},{10,... | collective-permute-start | bytes 3145736 | tf_op jit(solution)/shard_map/ppermute | solution.py:81
  86.7 14.7 %collective-permute-start.9 = (s32[12288]{0:T(1024)S(1)}, s32[12288]{0:T(1024)S(1)}, u32[]{:S(2)}, u32[]{:S(2)}) collective-permute-start(s32[12288]{0:T(1024)S(1)} %mul.177), channel_id=1, source_target_pairs={{0,0},{1,1},{2,3},{3,2},{4,6},{5,4},{6,5},{7,7},{8,11},{9,9},{10,8... | collective-permute-start | bytes 147464 | tf_op jit(solution)/shard_map/ppermute | solution.py:892
  87.5 12.2 %collective-permute-start.15 = (bf16[79,360]{1,0:T(8,128)(2,1)S(1)}, bf16[79,360]{1,0:T(8,128)(2,1)S(1)}, u32[]{:S(2)}, u32[]{:S(2)}) collective-permute-start(bf16[79,360]{1,0:T(8,128)(2,1)S(1)} %get-tuple-element.239), channel_id=1, source_target_pairs={{1,0},{2,1},{3,2},{4,3},{5,4},{6,5},{7,6},{8,7},{9,8},{10,9},{11,1... | collective-permute-start | bytes 170648 | tf_op jit(solution)/shard_map/ppermute | solution.py:49
  88.8 10.9 %collective-permute-start.14 = (bf16[79,360]{1,0:T(8,128)(2,1)S(1)}, bf16[79,360]{1,0:T(8,128)(2,1)}, u32[]{:S(2)}, u32[]{:S(2)}) collective-permute-start(bf16[79,360]{1,0:T(8,128)(2,1)S(1)} %get-tuple-element.240), channel_id=1, source_target_pairs={{0,1},{1,2},{2,3},{3,4},{4,5},{5,6},{6,7},{7,8},{8,9},{9,10},{10,1... | collective-permute-start | bytes 170648 | tf_op jit(solution)/shard_map/ppermute | solution.py:49
  127.5 17.2 %collective-permute-start.18 = (bf16[4096,128]{1,0:T(8,128)(2,1)}, bf16[4096,128]{1,0:T(8,128)(2,1)S(1)}, u32[]{:S(2)}, u32[]{:S(2)}) collective-permute-start(bf16[4096,128]{1,0:T(8,128)(2,1)} %get-tuple-element.123.refs_3_), channel_id=1, source_target_pairs={{1,0},{3,1},{2,3},{6,2},{4,6},{5,4},{7,5},{11,7},{9,11},{8,9},{10,... | collective-permute-start | bytes 3145736 | tf_op jit(solution)/shard_map/ppermute | solution.py:92
  128.5 20.0 %collective-permute-start.17 = (bf16[4096,128]{1,0:T(8,128)(2,1)}, bf16[4096,128]{1,0:T(8,128)(2,1)S(1)}, u32[]{:S(2)}, u32[]{:S(2)}) collective-permute-start(bf16[4096,128]{1,0:T(8,128)(2,1)} %get-tuple-element.123.refs_3_), channel_id=1, source_target_pairs={{0,1},{1,3},{3,2},{2,6},{6,4},{4,5},{5,7},{7,11},{11,9},{9,8},{8,1... | collective-permute-start | bytes 3145736 | tf_op jit(solution)/shard_map/ppermute | solution.py:92
  174.6 17.3 %collective-permute-start.20 = (bf16[4096,128]{1,0:T(8,128)(2,1)}, bf16[4096,128]{1,0:T(8,128)(2,1)S(1)}, u32[]{:S(2)}, u32[]{:S(2)}) collective-permute-start(bf16[4096,128]{1,0:T(8,128)(2,1)} %get-tuple-element.126.refs_3_), channel_id=1, source_target_pairs={{1,0},{3,1},{2,3},{6,2},{4,6},{5,4},{7,5},{11,7},{9,11},{8,9},{10,... | collective-permute-start | bytes 3145736 | tf_op jit(solution)/shard_map/ppermute | solution.py:92
  175.3 19.2 %collective-permute-start.19 = (bf16[4096,128]{1,0:T(8,128)(2,1)}, bf16[4096,128]{1,0:T(8,128)(2,1)S(1)}, u32[]{:S(2)}, u32[]{:S(2)}) collective-permute-start(bf16[4096,128]{1,0:T(8,128)(2,1)} %get-tuple-element.126.refs_3_), channel_id=1, source_target_pairs={{0,1},{1,3},{3,2},{2,6},{6,4},{4,5},{5,7},{7,11},{11,9},{9,8},{8,1... | collective-permute-start | bytes 3145736 | tf_op jit(solution)/shard_map/ppermute | solution.py:92
  225.6 12.0 %all-to-all-start.1 = ((bf16[16,64,128]{2,1,0:T(8,128)(2,1)}), bf16[16,64,128]{2,1,0:T(8,128)(2,1)S(1)}, u32[]{:S(2)}, u32[]{:S(2)}) async-start(bf16[16,64,128]{2,1,0:T(8,128)(2,1)} %bitcast.160), calls=%async_computation.1 | async-start | bytes 524288 | tf_op jit(solution)/shard_map/all_to_all | solution.py:868
  238.2 9.8 %collective-permute-start.21 = (bf16[78,360]{1,0:T(8,128)(2,1)S(1)}, bf16[78,360]{1,0:T(8,128)(2,1)S(1)}, u32[]{:S(2)}, u32[]{:S(2)}) collective-permute-start(bf16[78,360]{1,0:T(8,128)(2,1)S(1)} %get-tuple-element.241), channel_id=1, source_target_pairs={{0,1},{1,2},{2,3},{3,4},{4,5},{5,6},{6,7},{7,8},{8,9},{9,10},{10,1... | collective-permute-start | bytes 168488 | tf_op jit(solution)/shard_map/ppermute | solution.py:49
  241.6 6.5 %collective-permute-start.22 = (bf16[78,360]{1,0:T(8,128)(2,1)S(1)}, bf16[78,360]{1,0:T(8,128)(2,1)S(1)}, u32[]{:S(2)}, u32[]{:S(2)}) collective-permute-start(bf16[78,360]{1,0:T(8,128)(2,1)S(1)} %get-tuple-element.242), channel_id=1, source_target_pairs={{1,0},{2,1},{3,2},{4,3},{5,4},{6,5},{7,6},{8,7},{9,8},{10,9},{11,1... | collective-permute-start | bytes 168488 | tf_op jit(solution)/shard_map/ppermute | solution.py:49
  251.0 14.9 %all-to-all-start.2 = ((bf16[16,64,128]{2,1,0:T(8,128)(2,1)}), bf16[16,64,128]{2,1,0:T(8,128)(2,1)S(1)}, u32[]{:S(2)}, u32[]{:S(2)}) async-start(bf16[16,64,128]{2,1,0:T(8,128)(2,1)} %bitcast.18), calls=%async_computation.2 | async-start | bytes 524288 | tf_op jit(solution)/shard_map/all_to_all | solution.py:868
  266.0 42.7 %collective-permute-start.23 = (bf16[2048,256]{1,0:T(8,128)(2,1)}, bf16[2048,256]{1,0:T(8,128)(2,1)}, u32[]{:S(2)}, u32[]{:S(2)}) collective-permute-start(bf16[2048,256]{1,0:T(8,128)(2,1)} %convert_element_type.178), channel_id=1, source_target_pairs={{3,2},{2,3},{6,4},{4,5},{5,6},{11,8},{8,10},{10,11},{14,12},{15,13... | collective-permute-start | bytes 3145736 | tf_op jit(solution)/shard_map/ppermute | solution.py:895
  308.7 16.7 %collective-permute-start.24 = (bf16[4096,128]{1,0:T(8,128)(2,1)S(1)}, bf16[4096,128]{1,0:T(8,128)(2,1)}, u32[]{:S(2)}, u32[]{:S(2)}) collective-permute-start(bf16[4096,128]{1,0:T(8,128)(2,1)S(1)} %copy-done.52), channel_id=1, source_target_pairs={{0,1},{1,3},{3,2},{2,6},{6,4},{4,5},{5,7},{7,11},{11,9},{9,8},{8,1... | collective-permute-start | bytes 3145736 | tf_op jit(solution)/shard_map/ppermute | solution.py:92
  310.1 15.3 %collective-permute-start.25 = (bf16[4096,128]{1,0:T(8,128)(2,1)S(1)}, bf16[4096,128]{1,0:T(8,128)(2,1)}, u32[]{:S(2)}, u32[]{:S(2)}) collective-permute-start(bf16[4096,128]{1,0:T(8,128)(2,1)S(1)} %copy-done.51), channel_id=1, source_target_pairs={{1,0},{3,1},{2,3},{6,2},{4,6},{5,4},{7,5},{11,7},{9,11},{8,9},{10,... | collective-permute-start | bytes 3145736 | tf_op jit(solution)/shard_map/ppermute | solution.py:92
  357.3 17.0 %collective-permute-start.26 = (bf16[4096,128]{1,0:T(8,128)(2,1)}, bf16[4096,128]{1,0:T(8,128)(2,1)S(1)}, u32[]{:S(2)}, u32[]{:S(2)}) collective-permute-start(bf16[4096,128]{1,0:T(8,128)(2,1)} %get-tuple-element.154), channel_id=1, source_target_pairs={{0,1},{1,3},{3,2},{2,6},{6,4},{4,5},{5,7},{7,11},{11,9},{9,8},{8,1... | collective-permute-start | bytes 3145736 | tf_op jit(solution)/shard_map/ppermute | solution.py:92
  358.8 15.5 %collective-permute-start.27 = (bf16[4096,128]{1,0:T(8,128)(2,1)S(1)}, bf16[4096,128]{1,0:T(8,128)(2,1)}, u32[]{:S(2)}, u32[]{:S(2)}) collective-permute-start(bf16[4096,128]{1,0:T(8,128)(2,1)S(1)} %copy-done.54), channel_id=1, source_target_pairs={{1,0},{3,1},{2,3},{6,2},{4,6},{5,4},{7,5},{11,7},{9,11},{8,9},{10,... | collective-permute-start | bytes 3145736 | tf_op jit(solution)/shard_map/ppermute | solution.py:92
  407.3 16.8 %collective-permute-start.28 = (bf16[4096,128]{1,0:T(8,128)(2,1)}, bf16[4096,128]{1,0:T(8,128)(2,1)S(1)}, u32[]{:S(2)}, u32[]{:S(2)}) collective-permute-start(bf16[4096,128]{1,0:T(8,128)(2,1)} %get-tuple-element.160), channel_id=1, source_target_pairs={{0,1},{1,3},{3,2},{2,6},{6,4},{4,5},{5,7},{7,11},{11,9},{9,8},{8,1... | collective-permute-start | bytes 3145736 | tf_op jit(solution)/shard_map/ppermute | solution.py:92
  407.3 16.8 %collective-permute-start.29 = (bf16[4096,128]{1,0:T(8,128)(2,1)S(1)}, bf16[4096,128]{1,0:T(8,128)(2,1)}, u32[]{:S(2)}, u32[]{:S(2)}) collective-permute-start(bf16[4096,128]{1,0:T(8,128)(2,1)S(1)} %copy-done.53), channel_id=1, source_target_pairs={{1,0},{3,1},{2,3},{6,2},{4,6},{5,4},{7,5},{11,7},{9,11},{8,9},{10,... | collective-permute-start | bytes 3145736 | tf_op jit(solution)/shard_map/ppermute | solution.py:92
  447.3 3.1 collective-permute-start.30
  452.5 9.1 %collective-permute-start.31 = (bf16[4,2,72,256]{3,2,0,1:T(8,128)(2,1)S(1)}, bf16[4,2,72,256]{3,2,0,1:T(8,128)(2,1)S(1)}, u32[]{:S(2)}, u32[]{:S(2)}) collective-permute-start(bf16[4,2,72,256]{3,2,0,1:T(8,128)(2,1)S(1)} %fusion.13), channel_id=1, source_target_pairs={{0,1},{1,0},{2,3},{3,2},{4,5},{5,4},{6,7},{7,6},{8,9},{9,8},{10,11... | collective-permute-start | bytes 884744 | tf_op jit(solution)/shard_map/ppermute | solution.py:109
  452.6 9.2 %collective-permute-start.33 = (bf16[4,2,72,256]{3,2,1,0:T(8,128)(2,1)S(1)}, bf16[4,2,72,256]{3,2,1,0:T(8,128)(2,1)S(1)}, u32[]{:S(2)}, u32[]{:S(2)}) collective-permute-start(bf16[4,2,72,256]{3,2,1,0:T(8,128)(2,1)S(1)} %fusion.12), channel_id=1, source_target_pairs={{0,2},{1,3},{2,0},{3,1},{4,6},{5,7},{6,4},{7,5},{8,10},{9,11},{10,... | collective-permute-start | bytes 884744 | tf_op jit(solution)/shard_map/ppermute | solution.py:109
  461.7 5.2 %collective-permute-start.32 = (bf16[4,72,256]{2,1,0:T(8,128)(2,1)S(1)}, bf16[4,72,256]{2,1,0:T(8,128)(2,1)S(1)}, u32[]{:S(2)}, u32[]{:S(2)}) collective-permute-start(bf16[4,72,256]{2,1,0:T(8,128)(2,1)S(1)} %fusion.39), channel_id=1, source_target_pairs={{0,2},{1,3},{2,0},{3,1},{4,6},{5,7},{6,4},{7,5},{8,10},{9,11},{10,... | collective-permute-start | bytes 442376 | tf_op jit(solution)/shard_map/ppermute | solution.py:109
  461.9 5.2 %collective-permute-start.34 = (bf16[4,72,256]{2,1,0:T(8,128)(2,1)S(1)}, bf16[4,72,256]{2,1,0:T(8,128)(2,1)S(1)}, u32[]{:S(2)}, u32[]{:S(2)}) collective-permute-start(bf16[4,72,256]{2,1,0:T(8,128)(2,1)S(1)} %fusion.40), channel_id=1, source_target_pairs={{0,1},{1,0},{2,3},{3,2},{4,5},{5,4},{6,7},{7,6},{8,9},{9,8},{10,11... | collective-permute-start | bytes 442376 | tf_op jit(solution)/shard_map/ppermute | solution.py:109
  467.2 22.1 %collective-permute-start.42 = (bf16[2048,256]{1,0:T(8,128)(2,1)}, bf16[2048,256]{1,0:T(8,128)(2,1)}, u32[]{:S(2)}, u32[]{:S(2)}) collective-permute-start(bf16[2048,256]{1,0:T(8,128)(2,1)} %get-tuple-element.188), channel_id=1, source_target_pairs={{3,2},{2,3},{6,4},{4,5},{5,6},{11,8},{8,10},{10,11},{14,12},{15,13... | collective-permute-start | bytes 3145736 | tf_op jit(solution)/shard_map/ppermute | solution.py:895
  469.1 6.9 %collective-permute-start.35 = (bf16[1,144,256]{2,1,0:T(8,128)(2,1)S(1)}, bf16[1,144,256]{2,1,0:T(8,128)(2,1)S(1)}, u32[]{:S(2)}, u32[]{:S(2)}) collective-permute-start(bf16[1,144,256]{2,1,0:T(8,128)(2,1)S(1)} %get-tuple-element.234), channel_id=1, source_target_pairs={{0,4},{1,5},{2,6},{3,7},{4,0},{5,1},{6,2},{7,3},{8,12},{9,13},{10,... | collective-permute-start | bytes 221192 | tf_op jit(solution)/shard_map/ppermute | solution.py:109
  469.4 8.7 %collective-permute-start.37 = (bf16[1,144,256]{2,1,0:T(8,128)(2,1)S(1)}, bf16[1,144,256]{2,1,0:T(8,128)(2,1)S(1)}, u32[]{:S(2)}, u32[]{:S(2)}) collective-permute-start(bf16[1,144,256]{2,1,0:T(8,128)(2,1)S(1)} %get-tuple-element.235), channel_id=1, source_target_pairs={{0,12},{1,13},{2,14},{3,15},{4,8},{5,9},{6,10},{7,11},{8,4},{9,5},... | collective-permute-start | bytes 221192 | tf_op jit(solution)/shard_map/ppermute | solution.py:109
  474.2 6.1 %collective-permute-start.36 = (bf16[1,144,256]{2,1,0:T(8,128)(2,1)S(1)}, bf16[1,144,256]{2,1,0:T(8,128)(2,1)S(1)}, u32[]{:S(2)}, u32[]{:S(2)}) collective-permute-start(bf16[1,144,256]{2,1,0:T(8,128)(2,1)S(1)} %get-tuple-element.236), channel_id=1, source_target_pairs={{0,8},{1,9},{2,10},{3,11},{4,12},{5,13},{6,14},{7,15},{8,0},{9,1},... | collective-permute-start | bytes 221192 | tf_op jit(solution)/shard_map/ppermute | solution.py:109
  481.8 4.6 collective-permute-start.39
  482.3 5.4 %collective-permute-start.40 = (f32[8,128]{1,0:T(8,128)S(1)}, f32[8,128]{1,0:T(8,128)S(1)}, u32[]{:S(2)}, u32[]{:S(2)}) collective-permute-start(f32[8,128]{1,0:T(8,128)S(1)} %iota.23), channel_id=1, source_target_pairs={{0,12},{1,13},{2,14},{3,15},{4,8},{5,9},{6,10},{7,11},{8,4},{9,5},... | collective-permute-start | bytes 12296 | tf_op jit(solution)/shard_map/ppermute | solution.py:109
  484.5 3.6 collective-permute-start.38
  488.1 1.2 collective-permute-start.41
  489.3 10.3 %collective-permute-start.45 = (f32[8,128]{1,0:T(8,128)S(1)}, f32[8,128]{1,0:T(8,128)S(1)}, u32[]{:S(2)}, u32[]{:S(2)}) collective-permute-start(f32[8,128]{1,0:T(8,128)S(1)} %add.175), channel_id=1, source_target_pairs={{0,3},{1,2},{2,1},{3,0},{4,7},{5,6},{6,5},{7,4},{8,11},{9,10},{10,... | collective-permute-start | bytes 12296 | tf_op jit(solution)/shard_map/ppermute | solution.py:109
  494.8 4.8 collective-permute-start.44
  494.8 4.8 collective-permute-start.43
  (58 other events, 770.8 us)

commit v12 on v10

--- a/solution.py
+++ b/solution.py
@@ -301,11 +301,55 @@
     return ref[pl.ds(0, rows, stride=2), :], ref[pl.ds(1, rows, stride=2), :]
 
 
+def selector():
+    row = lax.broadcasted_iota(jnp.int32, (8, HALF), 0)
+    lane = lax.broadcasted_iota(jnp.int32, (8, HALF), 1)
+    slot = jnp.where(lane == CH, 64.0, jnp.where(lane == CH + 1, 1.0, 0.0))
+    known = jnp.where(lane == CH + 2, 1.0, 0.0)
+    return jnp.where(row == 0, slot, jnp.where(row == 1, known, 0.0)).astype(jnp.bfloat16)
+
+
+def ids_along(arrived):
+    codes = inner(selector(), arrived, 1, 1)
+    return jnp.where(codes[1:2, :] > 0, codes[0:1, :], -1.0).astype(jnp.int32)
+
+
+def ids_down(arrived):
+    codes = inner(arrived, selector(), 1, 1)
+    return jnp.where(codes[:, 1:2] > 0, codes[:, 0:1], -1.0).astype(jnp.int32)
+
+
 def whole(shape):
     return pl.BlockSpec(shape, lambda *_: (0,) * len(shape))
 
 
-def round_forward(index, mesh, before, own, after, mats, bias, following, decoder=()):
+def node_terms(mesh, mats, bias):
+    blocks = mesh.shape[0]
+    tile = 1024
+
+    def body(mesh_ref, mats_ref, bias_ref, dest_ref, self_ref):
+        lowered = mesh_ref[...].astype(jnp.bfloat16)
+        weave(dest_ref, inner(lowered, mats_ref[1], 1, 0) + bias_ref[0:1, :])
+        self_ref[...] = inner(lowered, mats_ref[3], 1, 0) + bias_ref[1:2, :]
+
+    rows = pl.BlockSpec((tile, D), lambda i: (i, 0))
+    woven = pl.BlockSpec((2 * tile, HALF), lambda i: (i, 0))
+    return pl.pallas_call(
+        body,
+        grid=(blocks // tile,),
+        in_specs=[rows, whole(mats.shape), whole(bias.shape)],
+        out_specs=[woven, rows],
+        out_shape=[
+            jax.ShapeDtypeStruct((2 * blocks, HALF), jnp.float32),
+            jax.ShapeDtypeStruct((blocks, D), jnp.float32),
+        ],
+        compiler_params=LIMIT,
+        cost_estimate=cost(4),
+        name="node_terms",
+    )(mesh, mats, bias)
+
+
+def round_forward(index, mesh, before, own, after, mats, terms, following, decoder=()):
     blocks = mesh.shape[0]
     tile, chunk = 512, 16
     turns, high = tile // chunk, 2 * chunk
@@ -314,8 +358,9 @@
     reach = sum(spans)
 
     def body(*refs):
-        index_ref, mesh_ref, before_ref, own_ref, after_ref, mats_ref, bias_ref = refs[:7]
-        raw, table, rows, wide, wider, sems = refs[-6:]
+        index_ref, mesh_ref, before_ref, own_ref, after_ref, mats_ref, dest_ref = refs[:7]
+        self_ref, refs = refs[7], refs[:7] + refs[8:]
+        raw, table, rows, wide, sems = refs[-5:]
         if more:
             next_ref, sent_ref = refs[7], refs[13]
             new_ref, back_ref, update_ref, agg_ref, slope_ref = refs[8:13]
@@ -346,8 +391,6 @@
                 table[pl.ds(at, 256), :] = raw[pl.ds(at, 256), :].astype(jnp.float32)
 
         mesh_in = mesh_ref[...]
-        lowered = mesh_in.astype(jnp.bfloat16)
-        weave(wide, inner(lowered, mats_ref[1], 1, 0) + bias_ref[0:1, :])
 
         def fetch(turn):
             for edge in range(K):
@@ -364,7 +407,7 @@
                 rows[pl.ds(pl.multiple_of(edge * 2 * tile + turn * high, high), high), :]
                 for edge in range(K)
             ]
-            return at, wide[pl.ds(at, high), :], taken
+            return at, dest_ref[pl.ds(at, high), :], taken
 
         def dense(at, dest, taken):
             total = None
@@ -376,7 +419,7 @@
                     jnp.bfloat16
                 )
                 total = out if total is None else total + out
-            wider[pl.ds(at, high), :] = total * (1.0 / K)
+            wide[pl.ds(at, high), :] = total * (1.0 / K)
 
         def some(turn, carry):
             loaded = load(turn - 1)
@@ -387,15 +430,14 @@
         fetch(0)
         lax.fori_loop(1, turns, some, 0)
         dense(*load(turns - 1))
-        first, second = unweave(wider)
+        first, second = unweave(wide)
         first, second = first.astype(jnp.bfloat16), second.astype(jnp.bfloat16)
         agg_ref[:, :HALF] = first
         agg_ref[:, HALF:] = second
         update_in = (
             inner(first, mats_ref[2, :HALF, :], 1, 0)
             + inner(second, mats_ref[2, HALF:, :], 1, 0)
-            + inner(lowered, mats_ref[3], 1, 0)
-            + bias_ref[1:2, :]
+            + self_ref[...]
         )
         sigma = sigmoid(update_in)
         out = update_in * sigma
@@ -435,7 +477,8 @@
 
     whole_rows = pl.BlockSpec((tile, D), lambda i, *_: (i, 0))
     woven = pl.BlockSpec((2 * tile, HALF), lambda i, *_: (i, 0))
-    ins = [whole_rows] + [pl.BlockSpec(memory_space=pl.ANY)] * 3 + [whole(mats.shape), whole(bias.shape)]
+    ins = [whole_rows] + [pl.BlockSpec(memory_space=pl.ANY)] * 3
+    ins = ins + [whole(mats.shape), woven, whole_rows]
     outs = [whole_rows] * 4 + [pl.BlockSpec((K, 2 * tile, HALF), lambda i, *_: (0, i, 0))]
     shapes = [
         jax.ShapeDtypeStruct((blocks, D), jnp.float32),
@@ -444,7 +487,7 @@
         jax.ShapeDtypeStruct((blocks, D), jnp.bfloat16),
         jax.ShapeDtypeStruct((K, 2 * blocks, HALF), jnp.bfloat16),
     ]
-    args = [index, mesh, before, own, after, mats, bias]
+    args = [index, mesh, before, own, after, mats, *terms]
     if more:
         ins.append(pl.BlockSpec((1, D, D), lambda *_: (0, 0, 0)))
         outs.append(woven)
@@ -472,7 +515,6 @@
                 pltpu.VMEM((reach, HALF), jnp.float32),
                 pltpu.VMEM((K * 2 * tile, HALF), jnp.float32),
                 pltpu.VMEM((2 * tile, HALF), jnp.float32),
-                pltpu.VMEM((2 * tile, HALF), jnp.float32),
                 pltpu.SemaphoreType.DMA((3,)),
             ],
         ),
@@ -483,7 +525,7 @@
     )(*args)
 
 
-def edges_backward(index, grad_mesh, back, slopes, mats, carried=(), landed=()):
+def edges_backward(index, back, slopes, mats, carried=(), landed=()):
     blocks = back.shape[0]
     tile, chunk = 512, 16
     steps, turns, high = blocks // tile, tile // chunk, 2 * chunk
@@ -491,8 +533,8 @@
 
     def body(*refs):
         if carried:
-            index_ref, grad_ref, back_ref, slope_ref, mats_ref = refs[:5]
-            past, rest = refs[5:11], refs[11:]
+            index_ref, back_ref, slope_ref, mats_ref = refs[:4]
+            past, rest = refs[4:9], refs[9:]
             (new_ref, out_ref, sent_ref), rest = rest[:3], rest[3:]
         else:
             index_ref, back_ref, slope_ref, mats_ref = refs[:4]
@@ -512,7 +554,9 @@
                     )
 
         if carried:
-            new = ended(grad_ref, *past, sent_ref, wide)
+            new, one, two = ended(*past, wide)
+            sent_ref[:, :HALF] = one
+            sent_ref[:, HALF:] = two
             new_ref[...] = new
             grad_out = new.astype(jnp.bfloat16)
             out_ref[...] = grad_out
@@ -606,13 +650,12 @@
         grid_spec=pltpu.PrefetchScalarGridSpec(
             num_scalar_prefetch=1,
             grid=(steps,),
-            in_specs=([rows] if carried else [])
-            + [
+            in_specs=[
                 rows,
                 pl.BlockSpec((K, 2 * tile, HALF), lambda i, *_: (0, i, 0)),
                 whole(mats.shape),
             ]
-            + ([woven] * 3 + [rows] * 2 + [whole(mats.shape)] if carried else [])
+            + ([rows] + [woven] * 3 + [whole(mats.shape)] if carried else [])
             + [whole(arg.shape) for arg in landed],
             out_specs=([rows] * 3 if carried else [rows, rows, whole(low_posts)])
             + [
@@ -640,63 +683,63 @@
         compiler_params=LIMIT,
         cost_estimate=cost(28 if carried else 25),
         name="edges_backward",
-    )(index, *([grad_mesh] if carried else []), back, slopes, mats, *carried, *landed)
-
-
-def ended(grad_ref, own_ref, first_ref, last_ref, guin_ref, dest_ref, mats_ref, sent_ref, wide):
+    )(index, back, slopes, mats, *carried, *landed)
+
+
+def ended(part_ref, own_ref, first_ref, last_ref, mats_ref, wide):
     wide[...] = (
         own_ref[...] + first_ref[...].astype(jnp.float32) + last_ref[...].astype(jnp.float32)
     )
     one, two = unweave(wide)
     one, two = one.astype(jnp.bfloat16), two.astype(jnp.bfloat16)
-    sent_ref[:, :HALF] = one
-    sent_ref[:, HALF:] = two
-    return (
-        grad_ref[...]
-        + inner(guin_ref[...], mats_ref[3], 1, 1)
-        + inner(dest_ref[...], mats_ref[1], 1, 1)
+    new = (
+        part_ref[...]
         + inner(one, mats_ref[0, :, :HALF], 1, 1)
         + inner(two, mats_ref[0, :, HALF:], 1, 1)
     )
-
-
-def round_backward(grad_mesh, own, first, last, grad_uin, dest_low, mats):
+    return new, one, two
+
+
+def carried_terms(grad_mesh, grad_uin, dest_low, mats):
     blocks = grad_mesh.shape[0]
     tile = 1024
 
-    def body(*refs):
-        new_ref, out_ref, sent_ref, wide = refs[-4:]
-        new = ended(*refs[:-4], sent_ref, wide)
-        new_ref[...] = new
-        out_ref[...] = new.astype(jnp.bfloat16)
+    def body(grad_ref, guin_ref, dest_ref, mats_ref, part_ref):
+        part_ref[...] = (
+            grad_ref[...]
+            + inner(guin_ref[...], mats_ref[3], 1, 1)
+            + inner(dest_ref[...], mats_ref[1], 1, 1)
+        )
 
     rows = pl.BlockSpec((tile, D), lambda i: (i, 0))
-    woven = pl.BlockSpec((2 * tile, HALF), lambda i: (i, 0))
-    low = jax.ShapeDtypeStruct((blocks, D), jnp.bfloat16)
     return pl.pallas_call(
         body,
         grid=(blocks // tile,),
-        in_specs=[rows, woven, woven, woven, rows, rows, whole(mats.shape)],
-        out_specs=[rows, rows, rows],
-        out_shape=[jax.ShapeDtypeStruct((blocks, D), jnp.float32), low, low],
-        scratch_shapes=[pltpu.VMEM((2 * tile, HALF), jnp.float32)],
+        in_specs=[rows, rows, rows, whole(mats.shape)],
+        out_specs=rows,
+        out_shape=jax.ShapeDtypeStruct((blocks, D), jnp.float32),
         compiler_params=LIMIT,
-        cost_estimate=cost(7),
-        name="round_backward",
-    )(grad_mesh, own, first, last, grad_uin, dest_low, mats)
-
-
-def encode_rows(arrived, ids, w_in, w_node, biases, source):
+        cost_estimate=cost(4),
+        name="carried_terms",
+    )(grad_mesh, grad_uin, dest_low, mats)
+
+
+def encode_rows(arrived, w_in, w_node, biases, source):
     posts = arrived.shape[0]
     tile = 512
 
-    def body(arrived_ref, ids_ref, in_ref, node_ref, bias_ref, source_ref, mesh_ref, gathered_ref, sent_ref, encoded, wide):
+    def body(
+        arrived_ref, in_ref, node_ref, bias_ref, source_ref,
+        mesh_ref, gathered_ref, sent_ref, ids_ref, down_ref, encoded, wide,
+    ):
         step = pl.program_id(0)
 
         @pl.when(step == 0)
         def _():
             entering = inner(arrived_ref[...], in_ref[...], 1, 0) + bias_ref[0:1, :]
             encoded[...] = silu(entering).astype(jnp.bfloat16)
+            ids_ref[...] = ids_along(arrived_ref[...])
+            down_ref[...] = ids_down(arrived_ref[...])
 
         nodes = lax.broadcasted_iota(jnp.int32, (tile, posts), 0) + step * tile
         chooser = jnp.where(nodes == ids_ref[...], 1.0, 0.0).astype(jnp.bfloat16)
@@ -708,17 +751,20 @@
         sent_ref[...] = wide[...].astype(jnp.bfloat16)
 
     rows = pl.BlockSpec((tile, D), lambda i: (i, 0))
-    args = (arrived, ids, w_in, w_node, biases, source)
+    args = (arrived, w_in, w_node, biases, source)
     return pl.pallas_call(
         body,
         grid=(H // tile,),
         in_specs=[whole(arg.shape) for arg in args[:-1]]
         + [pl.BlockSpec((1, D, D), lambda *_: (0, 0, 0))],
-        out_specs=[rows, rows, pl.BlockSpec((2 * tile, HALF), lambda i: (i, 0))],
+        out_specs=[rows, rows, pl.BlockSpec((2 * tile, HALF), lambda i: (i, 0))]
+        + [whole((1, posts)), whole((posts, 1))],
         out_shape=[
             jax.ShapeDtypeStruct((H, D), jnp.float32),
             jax.ShapeDtypeStruct((H, D), jnp.bfloat16),
             jax.ShapeDtypeStruct((2 * H, HALF), jnp.bfloat16),
+            jax.ShapeDtypeStruct((1, posts), jnp.int32),
+            jax.ShapeDtypeStruct((posts, 1), jnp.int32),
         ],
         scratch_shapes=[pltpu.VMEM((posts, D), jnp.bfloat16), pltpu.VMEM((2 * tile, HALF), jnp.float32)],
         compiler_params=LIMIT,
@@ -727,22 +773,32 @@
     )(*args)
 
 
-def encode_backward(grad_mesh, gathered, arrived, ids, w_in, w_node, biases):
+def encode_backward(carried, mesh, gathered, arrived, ids, w_in, w_node, biases):
+    blocks = mesh.shape[0]
     posts = arrived.shape[0]
     tile = 512
-    steps = H // tile
-
-    def body(grad_ref, gathered_ref, arrived_ref, ids_ref, in_ref, node_ref, bias_ref, gin_ref, gnode_ref, gbias_ref, total):
+    steps = blocks // tile
+
+    def body(
+        part_ref, own_ref, first_ref, last_ref, mats_ref,
+        mesh_ref, gathered_ref, arrived_ref, ids_ref, in_ref, node_ref, bias_ref,
+        new_ref, out_ref, gin_ref, gnode_ref, gbias_ref, gsource_ref, total, wide,
+    ):
         step = pl.program_id(0)
 
         @pl.when(step == 0)
         def _():
-            total[...] = jnp.zeros(total.shape, jnp.float32)
-            gnode_ref[...] = jnp.zeros(gnode_ref.shape, jnp.float32)
-            gbias_ref[...] = jnp.zeros(gbias_ref.shape, jnp.float32)
-
+            for ref in (total, gnode_ref, gbias_ref, gsource_ref):
+                ref[...] = jnp.zeros(ref.shape, jnp.float32)
+
+        new, one, two = ended(part_ref, own_ref, first_ref, last_ref, mats_ref, wide)
+        new_ref[...] = new
+        out_ref[...] = new.astype(jnp.bfloat16)
+        lowered = mesh_ref[...].astype(jnp.bfloat16)
+        gsource_ref[:, :HALF] += inner(lowered, one, 0, 0)
+        gsource_ref[:, HALF:] += inner(lowered, two, 0, 0)
         node_in = inner(gathered_ref[...], node_ref[...], 1, 0) + bias_ref[1:2, :]
-        grad_node = (grad_ref[...] * slope(node_in)).astype(jnp.bfloat16)
+        grad_node = (new * slope(node_in)).astype(jnp.bfloat16)
         gbias_ref[1:2, :] += jnp.sum(grad_node.astype(jnp.float32), 0, keepdims=True)
         gnode_ref[...] += inner(gathered_ref[...], grad_node, 0, 0)
         back = inner(grad_node, node_ref[...], 1, 1).astype(jnp.bfloat16)
@@ -758,19 +814,25 @@
             gin_ref[...] = inner(arrived_ref[...], grad_enc, 0, 0)
 
     rows = pl.BlockSpec((tile, D), lambda i: (i, 0))
-    args = (grad_mesh, gathered, arrived, ids, w_in, w_node, biases)
-    shapes = [(HALF, D), (D, D), (2, D)]
+    woven = pl.BlockSpec((2 * tile, HALF), lambda i: (i, 0))
+    args = (arrived, ids, w_in, w_node, biases)
+    shapes = [(HALF, D), (D, D), (2, D), (D, D)]
     return pl.pallas_call(
         body,
         grid=(steps,),
-        in_specs=[rows, rows] + [whole(arg.shape) for arg in args[2:]],
-        out_specs=[whole(shape) for shape in shapes],
-        out_shape=[jax.ShapeDtypeStruct(shape, jnp.float32) for shape in shapes],
-        scratch_shapes=[pltpu.VMEM((posts, D), jnp.float32)],
+        in_specs=[rows] + [woven] * 3 + [whole(carried[4].shape), rows, rows]
+        + [whole(arg.shape) for arg in args],
+        out_specs=[rows, rows] + [whole(shape) for shape in shapes],
+        out_shape=[
+            jax.ShapeDtypeStruct((blocks, D), jnp.float32),
+            jax.ShapeDtypeStruct((blocks, D), jnp.bfloat16),
+        ]
+        + [jax.ShapeDtypeStruct(shape, jnp.float32) for shape in shapes],
+        scratch_shapes=[pltpu.VMEM((posts, D), jnp.float32), pltpu.VMEM((2 * tile, HALF), jnp.float32)],
         compiler_params=LIMIT,
-        cost_estimate=cost(7),
+        cost_estimate=cost(10),
         name="encode_backward",
-    )(*args)
+    )(*carried, mesh, gathered, *args)
 
 
 def shards(walk, master, moment1, moment2, inputs, targets, valid, owner, slot, neighbours, partner):
@@ -825,17 +887,14 @@
     w_in, w_node, w_dec, w_out, *w_round, biases, digits = spread_rows(
         held, total_size, peers, place
     )
+    arrived, biases = lax.optimization_barrier((arrived, biases))
     count = digits[0, 0] * 65536.0 + digits[0, 1] * 256.0 + digits[0, 2]
     w_out = jnp.pad(w_out.reshape(D, CH), ((0, 0), (0, HALF - CH)))
     w_round = [mats.reshape(5, D, D) for mats in w_round]
     b_head = biases[:3]
     b_round = biases[3:].reshape(ROUNDS, 2, D)
-    arrived, biases = lax.optimization_barrier((arrived, biases))
-    ids = arrived[:, CH : CH + 3].astype(jnp.int32)
-    ids = jnp.where(ids[:, 2:3] > 0, ids[:, 0:1] * 64 + ids[:, 1:2], -1)
-    ids_row = ids.reshape(1, -1)
-    mesh, gathered, sent = encode_rows(
-        arrived, ids_row, w_in, w_node, biases, w_round[0]
+    mesh, gathered, sent, ids_row, ids = encode_rows(
+        arrived, w_in, w_node, biases, w_round[0]
     )
     sent, partner, neighbours, counted = lax.optimization_barrier(
         (sent, partner, neighbours, counted)
@@ -843,7 +902,7 @@
     index = 2 * ((neighbours - band * blocks + H) % (blocks * bands)).T.reshape(-1)
     moved = [(n, place) for n, place in enumerate(walk) if n != place]
     stays = jnp.asarray([n == place for n, place in enumerate(walk)])[band]
-    index = jnp.where(stays, index, lax.ppermute(index, "space", moved))
+    index = lax.ppermute(index, "space", list(enumerate(walk)))
 
     def at_home(rows):
         return lax.ppermute(rows, "space", [(j, i) for i, j in moved])
@@ -864,12 +923,13 @@
     )
     kept = []
     for layer in range(ROUNDS):
-        before, after = halo(walk, sent[2 * (blocks - H) :], sent[: 2 * H])
+        before, after = halo(walk, sent, sent)
+        terms = node_terms(mesh, w_round[layer], b_round[layer])
         if layer == 0:
             before, valid_around = lax.optimization_barrier((before, valid_around))
         following = w_round[layer + 1] if layer + 1 < ROUNDS else None
         new, back, update, agg, slopes, *rest = round_forward(
-            index, mesh, before, sent, after, w_round[layer], b_round[layer], following,
+            index, mesh, before, sent, after, w_round[layer], terms, following,
             () if following is not None else (ids, w_dec, w_out, biases),
         )
         kept.append((mesh, back, update, agg, slopes))
@@ -922,7 +982,7 @@
         old, back, update, agg, slopes = kept[layer]
         first_step = not carried
         grad_mesh, leaving, extra, grad_uin, dest_low, to_before, own, to_after = edges_backward(
-            index, grad_mesh, back, slopes, w_round[layer], carried,
+            index, back, slopes, w_round[layer], carried,
             (ids_row, landed, dec_turn, w_out, w_dec) if first_step else (),
         )
         if not first_step:
@@ -950,11 +1010,10 @@
         ]
         bias_grads[2 * layer] = jnp.sum(dest_low.astype(jnp.float32), 0, keepdims=True)
         bias_grads[2 * layer + 1] = jnp.sum(grad_uin.astype(jnp.float32), 0, keepdims=True)
-        carried = (own, from_before, from_after, grad_uin, dest_low, w_round[layer])
-    grad_mesh, leaving, sent_low = round_backward(grad_mesh, *carried)
-    mats_grads[0] = inner(kept[0][0].astype(jnp.bfloat16), sent_low, 0, 0)
-    grad_win, grad_wnode, grad_bpair = encode_backward(
-        grad_mesh, gathered, arrived, ids, w_in, w_node, biases
+        part = carried_terms(grad_mesh, grad_uin, dest_low, w_round[layer])
+        carried = (part, own, from_before, from_after, w_round[layer])
+    grad_mesh, leaving, grad_win, grad_wnode, grad_bpair, mats_grads[0] = encode_backward(
+        carried, kept[0][0], gathered, arrived, ids, w_in, w_node, biases
     )
     parts = [grad_win, grad_wnode, grad_wdec, grad_wout.reshape(CH, D)]
     parts = parts + mats_grads

time: 490 us -> 480 us (0.980)
  waiting for transfers between devices: 140 us -> 117 us
  Pallas kernels: 187 us -> 204 us
    pallas_call x2 -> x7, Pallas kernels: 13 us -> 33.7 us  [the longest x3 11.9 us: carried_terms(): pl.pallas_call(body, grid=(blocks // tile,), in_specs=[rows, rows, rows,...]
    ppermute x6, waiting for transfers between devices: 29.5 us -> 14.5 us  [halo(): lax.ppermute(last, 'space', up)]
    ppermute x6, waiting for transfers between devices: 41.1 us -> 34.9 us  [halo(): lax.ppermute(initial, 'space', down)]
    dot_general x19 -> x18, matrix products: 28.3 us -> 26.5 us  [inner(): lax.dot_general(left, right, (((left_dim,), (right_dim,)), ((), ())), pre...]
  transfers between devices with their start and end apart: 46 -> 46, of which waited for: 28 -> 27; matrix products, arithmetic and copies ran while one was open for 11% -> 11% of each run, Pallas kernels for 6% -> 11%
where the time goes in v12:
time: 480 us; the launch traced here: 478 us
  Pallas kernels  204 us (42%)
  waiting for transfers between devices  117 us (24%)
  starting transfers between devices  77.5 us (16%)
  matrix products  27.8 us (6%)
  other arithmetic  26.9 us (6%)
  local copies, waits for them, and re-layouts  16.8 us (4%)
  between operations  7.83 us (2%)
    pallas_call x3, Pallas kernels, edges_backward(): pl.pallas_call(body, grid_spec=pltpu.PrefetchScalarGridSpec(num_scalar_pr...  79.5 us
    pallas_call x3, Pallas kernels, round_forward(): pl.pallas_call(body, grid_spec=pltpu.PrefetchScalarGridSpec(num_scalar_pr...  75.8 us
    ppermute x6, waiting for transfers between devices, halo(): lax.ppermute(initial, 'space', down)  34.9 us
    ppermute x24, waiting for transfers between devices, swapped(): lax.ppermute(value, axis, [(i, i ^ bit) for i in range(lax.axis_size(axis...  31.8 us
    ppermute x24, starting transfers between devices, swapped(): lax.ppermute(value, axis, [(i, i ^ bit) for i in range(lax.axis_size(axis...  29.2 us
    dot_general x18, matrix products, inner(): lax.dot_general(left, right, (((left_dim,), (right_dim,)), ((), ())), pre...  26.5 us
    all_to_all x3, waiting for transfers between devices, exchanged(): lax.all_to_all(rows.reshape(bands, capacity, HALF), 'space', split_axis=0...  19.1 us
    ppermute x4, waiting for transfers between devices, shifted(): return lax.ppermute(shard, axis, pairs)  16.5 us
  transfers between devices with their start and end apart: 46, of which 27 were waited for; matrix products, arithmetic and copies ran while one was open for 11% of the time, Pallas kernels for 11%

profile of v12, /device:TPU:0, one launch (start us, length us, event | category | flops | bytes accessed | tf_op | source)
XLA Modules:
  0.0 477.6 jit_solution(18179152830927151403)
XLA Ops:
  5.7 5.1 %collective-permute-start.2 = (bf16[1,144,256]{2,1,0:T(8,128)(2,1)S(1)}, bf16[1,144,256]{2,1,0:T(8,128)(2,1)S(1)}, u32[]{:S(2)}, u32[]{:S(2)}) collective-permute-start(bf16[1,144,256]{2,1,0:T(8,128)(2,1)S(1)} %dynamic_update_slice.8), channel_id=1, source_target_pairs={{0,12},{1,13},{2,14},{3,15},{4,8},{5,9},{6,10},{7,11},{8,4},{9,5},... | collective-permute-start | bytes 221192 | tf_op jit(solution)/shard_map/ppermute | solution.py:94
  26.1 5.3 %collective-permute-done.6 = bf16[8,72,256]{2,1,0:T(8,128)(2,1)S(1)} collective-permute-done((bf16[8,72,256]{2,1,0:T(8,128)(2,1)S(1)}, bf16[8,72,256]{2,1,0:T(8,128)(2,1)S(1)}, u32[]{:S(2)}, u32[]{:S(2)}) %collective-permute-start.6) | collective-permute-done | bytes 294944 | tf_op jit(solution)/shard_map/ppermute | solution.py:94
  32.8 4.8 %all-to-all-start = ((bf16[16,64,128]{2,1,0:T(8,128)(2,1)}), bf16[16,64,128]{2,1,0:T(8,128)(2,1)S(1)}, u32[]{:S(2)}, u32[]{:S(2)}) async-start(bf16[16,64,128]{2,1,0:T(8,128)(2,1)} %bitcast.162), calls=%async_computation | async-start | bytes 524288 | tf_op jit(solution)/shard_map/all_to_all | solution.py:881
  38.7 4.0 spread_rows.1
  42.7 5.4 %all-to-all-done = bf16[16,64,128]{2,1,0:T(8,128)(2,1)S(1)} async-done(((bf16[16,64,128]{2,1,0:T(8,128)(2,1)}), bf16[16,64,128]{2,1,0:T(8,128)(2,1)S(1)}, u32[]{:S(2)}, u32[]{:S(2)}) %all-to-all-start) | async-done | bytes 262176 | tf_op jit(solution)/shard_map/all_to_all | solution.py:881
  48.7 6.0 %encode_rows.1 = (f32[2048,256]{1,0:T(8,128)}, bf16[2048,256]{1,0:T(8,128)(2,1)}, bf16[4096,128]{1,0:T(8,128)(2,1)}, s32[1,1024]{1,0:T(1,128)}, s32[1024,1]{1,0:T(8,128)}) custom-call(bf16[1024,128]{1,0:T(8,128)(2,1)} %bitcast.154, bf16[128,256]{1,0:T(8,128)(2,1)} %get-tuple-element.110.in_ref, bf16[256,256]{1,0:T(8,128)(2,1)} %get-tuple-element.111.node_ref, ...), custom_call_target="tpu_custom_call" | custom-call | bytes 15000000 | tf_op jit(solution)/shard_map/encode_rows/pallas_call | solution.py:755
  59.0 4.5 collective-permute-start.11
  64.9 4.0 node_terms.3
  68.9 11.7 %collective-permute-done.12 = bf16[79,360]{1,0:T(8,128)(2,1)S(1)} collective-permute-done((bf16[79,360]{1,0:T(8,128)(2,1)S(1)}, bf16[79,360]{1,0:T(8,128)(2,1)S(1)}, u32[]{:S(2)}, u32[]{:S(2)}) %collective-permute-start.12) | collective-permute-done | bytes 56912 | tf_op jit(solution)/shard_map/ppermute | solution.py:49
  80.8 2.5 collective-permute-done.10.refs_2_
  84.6 24.1 %round_forward.3 = (f32[2048,256]{1,0:T(8,128)}, f32[2048,256]{1,0:T(8,128)}, bf16[2048,256]{1,0:T(8,128)(2,1)}, bf16[2048,256]{1,0:T(8,128)(2,1)}, bf16[6,4096,...) custom-call(s32[12288]{0:T(1024)} %copy-done.16, f32[2048,256]{1,0:T(8,128)} %get-tuple-element.117.mesh_ref.refs_1_, ...), custom_call_target="tpu_custom_call" | custom-call | bytes 75000000 | tf_op jit(solution)/shard_map/round_forward/pallas_call | solution.py:505
  110.9 3.9 node_terms.4
  114.7 16.8 %collective-permute-done.15.refs_4_ = bf16[4096,128]{1,0:T(8,128)(2,1)S(1)} collective-permute-done((bf16[4096,128]{1,0:T(8,128)(2,1)}, bf16[4096,128]{1,0:T(8,128)(2,1)S(1)}, u32[]{:S(2)}, u32[]{:S(2)}) %collective-permute-start.15) | collective-permute-done | bytes 1048608 | tf_op jit(solution)/shard_map/ppermute | solution.py:77
  131.5 2.9 collective-permute-done.14.refs_2_
  135.4 24.3 %round_forward.4 = (f32[2048,256]{1,0:T(8,128)}, f32[2048,256]{1,0:T(8,128)}, bf16[2048,256]{1,0:T(8,128)(2,1)}, bf16[2048,256]{1,0:T(8,128)(2,1)}, bf16[6,4096,...) custom-call(s32[12288]{0:T(1024)} %copy-done.16, f32[2048,256]{1,0:T(8,128)} %get-tuple-element.124.mesh_ref.refs_1_, ...), custom_call_target="tpu_custom_call" | custom-call | bytes 75000000 | tf_op jit(solution)/shard_map/round_forward/pallas_call | solution.py:505
  162.9 3.9 node_terms.5
  166.8 18.1 %collective-permute-done.17.refs_4_ = bf16[4096,128]{1,0:T(8,128)(2,1)S(1)} collective-permute-done((bf16[4096,128]{1,0:T(8,128)(2,1)}, bf16[4096,128]{1,0:T(8,128)(2,1)S(1)}, u32[]{:S(2)}, u32[]{:S(2)}) %collective-permute-start.17) | collective-permute-done | bytes 1048608 | tf_op jit(solution)/shard_map/ppermute | solution.py:77
  186.2 27.3 %round_forward.5 = (f32[2048,256]{1,0:T(8,128)}, f32[2048,256]{1,0:T(8,128)}, bf16[2048,256]{1,0:T(8,128)(2,1)}, bf16[2048,256]{1,0:T(8,128)(2,1)}, bf16[6,4096,...) custom-call(s32[12288]{0:T(1024)} %copy-done.16, ...), custom_call_target="tpu_custom_call" | custom-call | bytes 75000000 | tf_op jit(solution)/shard_map/round_forward/pallas_call | solution.py:505
  213.5 4.7 all-to-all-start.1
  220.8 5.9 %all-to-all-done.1 = bf16[16,64,128]{2,1,0:T(8,128)(2,1)S(1)} async-done(((bf16[16,64,128]{2,1,0:T(8,128)(2,1)}), bf16[16,64,128]{2,1,0:T(8,128)(2,1)S(1)}, u32[]{:S(2)}, u32[]{:S(2)}) %all-to-all-start.1) | async-done | bytes 262176 | tf_op jit(solution)/shard_map/all_to_all | solution.py:881
  227.3 3.3 collective-permute-start.18
  232.0 4.8 collective-permute-done.19
  240.4 5.9 %all-to-all-start.2 = ((bf16[16,64,128]{2,1,0:T(8,128)(2,1)}), bf16[16,64,128]{2,1,0:T(8,128)(2,1)S(1)}, u32[]{:S(2)}, u32[]{:S(2)}) async-start(bf16[16,64,128]{2,1,0:T(8,128)(2,1)} %bitcast.17), calls=%async_computation.2 | async-start | bytes 524288 | tf_op jit(solution)/shard_map/all_to_all | solution.py:881
  247.0 7.8 %all-to-all-done.2 = bf16[16,64,128]{2,1,0:T(8,128)(2,1)S(1)} async-done(((bf16[16,64,128]{2,1,0:T(8,128)(2,1)}), bf16[16,64,128]{2,1,0:T(8,128)(2,1)S(1)}, u32[]{:S(2)}, u32[]{:S(2)}) %all-to-all-start.2) | async-done | bytes 262176 | tf_op jit(solution)/shard_map/all_to_all | solution.py:881
  256.5 26.9 %edges_backward.3 = (f32[2048,256]{1,0:T(8,128)}, bf16[2048,256]{1,0:T(8,128)(2,1)}, bf16[1024,256]{1,0:T(8,128)(2,1)}, bf16[2048,256]{1,0:T(8,128)(2,1)}, bf16[...) custom-call(s32[12288]{0:T(1024)} %copy-done.16, ...), custom_call_target="tpu_custom_call" | custom-call | bytes 75000000 | tf_op jit(solution)/shard_map/edges_backward/pallas_call | solution.py:648
  288.2 2.4 fusion.93.refs_18_
  293.2 2.4 collective-permute-start.22
  297.3 3.9 carried_terms.3.refs_4_
  303.2 3.4 convert_select_fusion
  306.6 6.0 %collective-permute-done.21.refs_6_ = bf16[4096,128]{1,0:T(8,128)(2,1)} collective-permute-done((bf16[4096,128]{1,0:T(8,128)(2,1)}, bf16[4096,128]{1,0:T(8,128)(2,1)}, u32[]{:S(2)}, u32[]{:S(2)}) %collective-permute-start.21) | collective-permute-done | bytes 1048608 | tf_op jit(solution)/shard_map/ppermute | solution.py:77
  312.6 26.2 %edges_backward.4 = (f32[2048,256]{1,0:T(8,128)}, bf16[2048,256]{1,0:T(8,128)(2,1)}, bf16[2048,256]{1,0:T(8,128)(2,1)}, bf16[2048,256]{1,0:T(8,128)(2,1)}, bf16[...) custom-call(s32[12288]{0:T(1024)} %copy-done.16, ...), custom_call_target="tpu_custom_call" | custom-call | bytes 84000000 | tf_op jit(solution)/shard_map/edges_backward/pallas_call | solution.py:648
  339.8 3.1 collective-permute-start.24
  343.0 2.4 fusion.90.refs_11_
  346.6 4.0 carried_terms.4.refs_4_
  352.8 2.4 fusion.71.refs_10_
  359.1 26.4 %edges_backward.5 = (f32[2048,256]{1,0:T(8,128)}, bf16[2048,256]{1,0:T(8,128)(2,1)}, bf16[2048,256]{1,0:T(8,128)(2,1)}, bf16[2048,256]{1,0:T(8,128)(2,1)}, bf16[...) custom-call(s32[12288]{0:T(1024)} %copy-done.16, ...), custom_call_target="tpu_custom_call" | custom-call | bytes 84000000 | tf_op jit(solution)/shard_map/edges_backward/pallas_call | solution.py:648
  385.5 3.8 collective-permute-start.26
  389.4 2.4 fusion.88.refs_6_
  392.9 4.0 carried_terms.5.part_ref
  405.4 10.1 %encode_backward.1 = (f32[2048,256]{1,0:T(8,128)}, bf16[2048,256]{1,0:T(8,128)(2,1)}, f32[128,256]{1,0:T(8,128)}, f32[256,256]{1,0:T(8,128)}, f32[2,256]{1,0:T(2,128)}, /*index=5*/f32[256,256]{1,0:T(8,128)}) custom-call(f32[2048,256]{1,0:T(8,128)} %carried_terms.5.part_ref, f32[4096,128]{1,0:T(8,128)} %get-tuple-element.169.own_ref, ...), custom_call_target="tpu_custom_call" | custom-call | bytes 30000000 | tf_op jit(solution)/shard_map/encode_backward/pallas_call | solution.py:820
  415.5 5.1 %collect_rows.1 = (f32[16,144,256]{2,1,0:T(8,128)}, bf16[16,144,256]{2,1,0:T(8,128)(2,1)}) custom-call(s32[1]{0:T(128)} %bitcast.7.place_ref, f32[128,256]{1,0:T(8,128)} %get-tuple-element.173.refs_0_, f32[256,256]{1,0:T(8,128)} %get-tuple-element.174.refs_1_, f32[256,256]{1,0:T(8,128)} %fusion.87.refs_2_, f32[78,256]{1,0:T(8,128)} %reshape.154.refs_3_, ...), custom_call_target="tpu_custom_call" | custom-call | bytes 15000000 | tf_op jit(solution)/shard_map/collect_rows/pallas_call | solution.py:241
  420.7 3.0 collective-permute-done.27
  426.0 8.9 %collective-permute-done.28 = bf16[4,2,72,256]{3,2,0,1:T(8,128)(2,1)S(1)} collective-permute-done((bf16[4,2,72,256]{3,2,0,1:T(8,128)(2,1)S(1)}, bf16[4,2,72,256]{3,2,0,1:T(8,128)(2,1)S(1)}, u32[]{:S(2)}, u32[]{:S(2)}) %collective-permute-start.28) | collective-permute-done | bytes 294944 | tf_op jit(solution)/shard_map/ppermute | solution.py:94
  437.0 3.3 collective-permute-done.29
  442.5 4.7 collective-permute-start.34
  455.3 2.3 collective-permute-start.37
  462.3 5.8 %collective-permute-start.42 = (f32[8,128]{1,0:T(8,128)S(1)}, f32[8,128]{1,0:T(8,128)S(1)}, u32[]{:S(2)}, u32[]{:S(2)}) collective-permute-start(f32[8,128]{1,0:T(8,128)S(1)} %add.175), channel_id=1, source_target_pairs={{0,3},{1,2},{2,1},{3,0},{4,7},{5,6},{6,5},{7,4},{8,11},{9,10},{10,... | collective-permute-start | bytes 12296 | tf_op jit(solution)/shard_map/ppermute | solution.py:94
  469.6 3.3 select_bitcast_fusion
  (264 shorter events, 96.3 us)
Async XLA Ops:
  5.7 11.2 %collective-permute-start.2 = (bf16[1,144,256]{2,1,0:T(8,128)(2,1)S(1)}, bf16[1,144,256]{2,1,0:T(8,128)(2,1)S(1)}, u32[]{:S(2)}, u32[]{:S(2)}) collective-permute-start(bf16[1,144,256]{2,1,0:T(8,128)(2,1)S(1)} %dynamic_update_slice.8), channel_id=1, source_target_pairs={{0,12},{1,13},{2,14},{3,15},{4,8},{5,9},{6,10},{7,11},{8,4},{9,5},... | collective-permute-start | bytes 221192 | tf_op jit(solution)/shard_map/ppermute | solution.py:94
  10.9 6.2 %collective-permute-start.1 = (bf16[1,144,256]{2,1,0:T(8,128)(2,1)S(1)}, bf16[1,144,256]{2,1,0:T(8,128)(2,1)S(1)}, u32[]{:S(2)}, u32[]{:S(2)}) collective-permute-start(bf16[1,144,256]{2,1,0:T(8,128)(2,1)S(1)} %dynamic_update_slice.8), channel_id=1, source_target_pairs={{0,8},{1,9},{2,10},{3,11},{4,12},{5,13},{6,14},{7,15},{8,0},{9,1},... | collective-permute-start | bytes 221192 | tf_op jit(solution)/shard_map/ppermute | solution.py:94
  10.9 6.2 %collective-permute-start = (bf16[1,144,256]{2,1,0:T(8,128)(2,1)S(1)}, bf16[1,144,256]{2,1,0:T(8,128)(2,1)S(1)}, u32[]{:S(2)}, u32[]{:S(2)}) collective-permute-start(bf16[1,144,256]{2,1,0:T(8,128)(2,1)S(1)} %dynamic_update_slice.8), channel_id=1, source_target_pairs={{0,4},{1,5},{2,6},{3,7},{4,0},{5,1},{6,2},{7,3},{8,12},{9,13},{10,... | collective-permute-start | bytes 221192 | tf_op jit(solution)/shard_map/ppermute | solution.py:94
  17.2 5.3 %collective-permute-start.4 = (bf16[4,72,256]{2,1,0:T(8,128)(2,1)S(1)}, bf16[4,72,256]{2,1,0:T(8,128)(2,1)S(1)}, u32[]{:S(2)}, u32[]{:S(2)}) collective-permute-start(bf16[4,72,256]{2,1,0:T(8,128)(2,1)S(1)} %get-tuple-element.245), channel_id=1, source_target_pairs={{0,1},{1,0},{2,3},{3,2},{4,5},{5,4},{6,7},{7,6},{8,9},{9,8},{10,11... | collective-permute-start | bytes 442376 | tf_op jit(solution)/shard_map/ppermute | solution.py:94
  18.8 5.1 %collective-permute-start.3 = (bf16[4,72,256]{2,1,0:T(8,128)(2,1)S(1)}, bf16[4,72,256]{2,1,0:T(8,128)(2,1)S(1)}, u32[]{:S(2)}, u32[]{:S(2)}) collective-permute-start(bf16[4,72,256]{2,1,0:T(8,128)(2,1)S(1)} %get-tuple-element.246), channel_id=1, source_target_pairs={{0,2},{1,3},{2,0},{3,1},{4,6},{5,7},{6,4},{7,5},{8,10},{9,11},{10,... | collective-permute-start | bytes 442376 | tf_op jit(solution)/shard_map/ppermute | solution.py:94
  23.9 7.4 %collective-permute-start.6 = (bf16[8,72,256]{2,1,0:T(8,128)(2,1)S(1)}, bf16[8,72,256]{2,1,0:T(8,128)(2,1)S(1)}, u32[]{:S(2)}, u32[]{:S(2)}) collective-permute-start(bf16[8,72,256]{2,1,0:T(8,128)(2,1)S(1)} %pad_maximum_fusion.4), channel_id=1, source_target_pairs={{0,2},{1,3},{2,0},{3,1},{4,6},{5,7},{6,4},{7,5},{8,10},{9,11},{10,... | collective-permute-start | bytes 884744 | tf_op jit(solution)/shard_map/ppermute | solution.py:94
  25.5 7.1 %collective-permute-start.5 = (bf16[8,72,256]{2,1,0:T(8,128)(2,1)S(1)}, bf16[8,72,256]{2,1,0:T(8,128)(2,1)S(1)}, u32[]{:S(2)}, u32[]{:S(2)}) collective-permute-start(bf16[8,72,256]{2,1,0:T(8,128)(2,1)S(1)} %pad_maximum_fusion.3), channel_id=1, source_target_pairs={{0,1},{1,0},{2,3},{3,2},{4,5},{5,4},{6,7},{7,6},{8,9},{9,8},{10,11... | collective-permute-start | bytes 884744 | tf_op jit(solution)/shard_map/ppermute | solution.py:94
  31.4 6.2 %collective-permute-start.8 = (bf16[16,72,256]{2,1,0:T(8,128)(2,1)S(1)}, bf16[16,72,256]{2,1,0:T(8,128)(2,1)S(1)}, u32[]{:S(2)}, u32[]{:S(2)}) collective-permute-start(bf16[16,72,256]{2,1,0:T(8,128)(2,1)S(1)} %constant_dynamic-update-slice_fusion.2.refs_1_), channel_id=1, source_target_pairs={{0,16},{16,0},{1,17},{17,1},{2,18},{18,2},{3,19},{19,3},{4,20},{20... | collective-permute-start | bytes 1769480 | tf_op jit(solution)/shard_map/ppermute | solution.py:94
  32.7 5.0 %collective-permute-start.7 = (bf16[16,72,256]{2,1,0:T(8,128)(2,1)S(1)}, bf16[16,72,256]{2,1,0:T(8,128)(2,1)S(1)}, u32[]{:S(2)}, u32[]{:S(2)}) collective-permute-start(bf16[16,72,256]{2,1,0:T(8,128)(2,1)S(1)} %constant_dynamic-update-slice_fusion.refs_0_), channel_id=1, source_target_pairs={{0,16},{16,0},{1,17},{17,1},{2,18},{18,2},{3,19},{19,3},{4,20},{20... | collective-permute-start | bytes 1769480 | tf_op jit(solution)/shard_map/ppermute | solution.py:94
  32.8 15.3 %all-to-all-start = ((bf16[16,64,128]{2,1,0:T(8,128)(2,1)}), bf16[16,64,128]{2,1,0:T(8,128)(2,1)S(1)}, u32[]{:S(2)}, u32[]{:S(2)}) async-start(bf16[16,64,128]{2,1,0:T(8,128)(2,1)} %bitcast.162), calls=%async_computation | async-start | bytes 524288 | tf_op jit(solution)/shard_map/all_to_all | solution.py:881
  54.8 28.6 %collective-permute-start.13 = (bf16[4096,128]{1,0:T(8,128)(2,1)}, bf16[4096,128]{1,0:T(8,128)(2,1)S(1)}, u32[]{:S(2)}, u32[]{:S(2)}) collective-permute-start(bf16[4096,128]{1,0:T(8,128)(2,1)} %get-tuple-element.118.refs_3_), channel_id=1, source_target_pairs={{1,0},{3,1},{2,3},{6,2},{4,6},{5,4},{7,5},{11,7},{9,11},{8,9},{10,... | collective-permute-start | bytes 3145736 | tf_op jit(solution)/shard_map/ppermute | solution.py:77
  56.5 26.8 %collective-permute-start.10 = (bf16[4096,128]{1,0:T(8,128)(2,1)}, bf16[4096,128]{1,0:T(8,128)(2,1)S(1)}, u32[]{:S(2)}, u32[]{:S(2)}) collective-permute-start(bf16[4096,128]{1,0:T(8,128)(2,1)} %get-tuple-element.118.refs_3_), channel_id=1, source_target_pairs={{0,1},{1,3},{3,2},{2,6},{6,4},{4,5},{5,7},{7,11},{11,9},{9,8},{8,1... | collective-permute-start | bytes 3145736 | tf_op jit(solution)/shard_map/ppermute | solution.py:77
  56.9 26.4 %collective-permute-start.9 = (s32[12288]{0:T(1024)S(1)}, s32[12288]{0:T(1024)S(1)}, u32[]{:S(2)}, u32[]{:S(2)}) collective-permute-start(s32[12288]{0:T(1024)S(1)} %mul.177), channel_id=1, source_target_pairs={{0,0},{1,1},{2,3},{3,2},{4,6},{5,4},{6,5},{7,7},{8,11},{9,9},{10,8... | collective-permute-start | bytes 147464 | tf_op jit(solution)/shard_map/ppermute | solution.py:905
  57.7 22.9 %collective-permute-start.12 = (bf16[79,360]{1,0:T(8,128)(2,1)S(1)}, bf16[79,360]{1,0:T(8,128)(2,1)S(1)}, u32[]{:S(2)}, u32[]{:S(2)}) collective-permute-start(bf16[79,360]{1,0:T(8,128)(2,1)S(1)} %get-tuple-element.247), channel_id=1, source_target_pairs={{1,0},{2,1},{3,2},{4,3},{5,4},{6,5},{7,6},{8,7},{9,8},{10,9},{11,1... | collective-permute-start | bytes 170648 | tf_op jit(solution)/shard_map/ppermute | solution.py:49
  59.0 21.6 %collective-permute-start.11 = (bf16[79,360]{1,0:T(8,128)(2,1)S(1)}, bf16[79,360]{1,0:T(8,128)(2,1)S(1)}, u32[]{:S(2)}, u32[]{:S(2)}) collective-permute-start(bf16[79,360]{1,0:T(8,128)(2,1)S(1)} %get-tuple-element.248), channel_id=1, source_target_pairs={{0,1},{1,2},{2,3},{3,4},{4,5},{5,6},{6,7},{7,8},{8,9},{9,10},{10,1... | collective-permute-start | bytes 170648 | tf_op jit(solution)/shard_map/ppermute | solution.py:49
  108.8 22.7 %collective-permute-start.15 = (bf16[4096,128]{1,0:T(8,128)(2,1)}, bf16[4096,128]{1,0:T(8,128)(2,1)S(1)}, u32[]{:S(2)}, u32[]{:S(2)}) collective-permute-start(bf16[4096,128]{1,0:T(8,128)(2,1)} %get-tuple-element.125.refs_3_), channel_id=1, source_target_pairs={{1,0},{3,1},{2,3},{6,2},{4,6},{5,4},{7,5},{11,7},{9,11},{8,9},{10,... | collective-permute-start | bytes 3145736 | tf_op jit(solution)/shard_map/ppermute | solution.py:77
  109.8 24.6 %collective-permute-start.14 = (bf16[4096,128]{1,0:T(8,128)(2,1)}, bf16[4096,128]{1,0:T(8,128)(2,1)S(1)}, u32[]{:S(2)}, u32[]{:S(2)}) collective-permute-start(bf16[4096,128]{1,0:T(8,128)(2,1)} %get-tuple-element.125.refs_3_), channel_id=1, source_target_pairs={{0,1},{1,3},{3,2},{2,6},{6,4},{4,5},{5,7},{7,11},{11,9},{9,8},{8,1... | collective-permute-start | bytes 3145736 | tf_op jit(solution)/shard_map/ppermute | solution.py:77
  159.7 25.1 %collective-permute-start.17 = (bf16[4096,128]{1,0:T(8,128)(2,1)}, bf16[4096,128]{1,0:T(8,128)(2,1)S(1)}, u32[]{:S(2)}, u32[]{:S(2)}) collective-permute-start(bf16[4096,128]{1,0:T(8,128)(2,1)} %get-tuple-element.130.refs_3_), channel_id=1, source_target_pairs={{1,0},{3,1},{2,3},{6,2},{4,6},{5,4},{7,5},{11,7},{9,11},{8,9},{10,... | collective-permute-start | bytes 3145736 | tf_op jit(solution)/shard_map/ppermute | solution.py:77
  160.4 24.5 %collective-permute-start.16 = (bf16[4096,128]{1,0:T(8,128)(2,1)}, bf16[4096,128]{1,0:T(8,128)(2,1)S(1)}, u32[]{:S(2)}, u32[]{:S(2)}) collective-permute-start(bf16[4096,128]{1,0:T(8,128)(2,1)} %get-tuple-element.130.refs_3_), channel_id=1, source_target_pairs={{0,1},{1,3},{3,2},{2,6},{6,4},{4,5},{5,7},{7,11},{11,9},{9,8},{8,1... | collective-permute-start | bytes 3145736 | tf_op jit(solution)/shard_map/ppermute | solution.py:77
  186.1 40.5 %copy-start.45 = (bf16[1,78,512]{2,1,0:T(8,128)(2,1)S(1)}, bf16[1,78,512]{2,1,0:T(8,128)(2,1)}, u32[]{:S(2)}) copy-start(bf16[1,78,512]{2,1,0:T(8,128)(2,1)} %param.16) | copy-start | bytes 239620
  186.2 40.5 %copy-start.50 = (bf16[1,78,512]{2,1,0:T(8,128)(2,1)S(1)}, bf16[1,78,512]{2,1,0:T(8,128)(2,1)}, u32[]{:S(2)}) copy-start(bf16[1,78,512]{2,1,0:T(8,128)(2,1)} %param.17) | copy-start | bytes 239620
  213.5 13.2 %all-to-all-start.1 = ((bf16[16,64,128]{2,1,0:T(8,128)(2,1)}), bf16[16,64,128]{2,1,0:T(8,128)(2,1)S(1)}, u32[]{:S(2)}, u32[]{:S(2)}) async-start(bf16[16,64,128]{2,1,0:T(8,128)(2,1)} %bitcast.163), calls=%async_computation.1 | async-start | bytes 524288 | tf_op jit(solution)/shard_map/all_to_all | solution.py:881
  227.3 9.5 %collective-permute-start.18 = (bf16[78,360]{1,0:T(8,128)(2,1)S(1)}, bf16[78,360]{1,0:T(8,128)(2,1)S(1)}, u32[]{:S(2)}, u32[]{:S(2)}) collective-permute-start(bf16[78,360]{1,0:T(8,128)(2,1)S(1)} %get-tuple-element.249), channel_id=1, source_target_pairs={{0,1},{1,2},{2,3},{3,4},{4,5},{5,6},{6,7},{7,8},{8,9},{9,10},{10,1... | collective-permute-start | bytes 168488 | tf_op jit(solution)/shard_map/ppermute | solution.py:49
  230.6 6.1 %collective-permute-start.19 = (bf16[78,360]{1,0:T(8,128)(2,1)S(1)}, bf16[78,360]{1,0:T(8,128)(2,1)S(1)}, u32[]{:S(2)}, u32[]{:S(2)}) collective-permute-start(bf16[78,360]{1,0:T(8,128)(2,1)S(1)} %get-tuple-element.250), channel_id=1, source_target_pairs={{1,0},{2,1},{3,2},{4,3},{5,4},{6,5},{7,6},{8,7},{9,8},{10,9},{11,1... | collective-permute-start | bytes 168488 | tf_op jit(solution)/shard_map/ppermute | solution.py:49
  240.4 14.4 %all-to-all-start.2 = ((bf16[16,64,128]{2,1,0:T(8,128)(2,1)}), bf16[16,64,128]{2,1,0:T(8,128)(2,1)S(1)}, u32[]{:S(2)}, u32[]{:S(2)}) async-start(bf16[16,64,128]{2,1,0:T(8,128)(2,1)} %bitcast.17), calls=%async_computation.2 | async-start | bytes 524288 | tf_op jit(solution)/shard_map/all_to_all | solution.py:881
  254.8 36.9 %collective-permute-start.20 = (bf16[2048,256]{1,0:T(8,128)(2,1)S(1)}, bf16[2048,256]{1,0:T(8,128)(2,1)}, u32[]{:S(2)}, u32[]{:S(2)}) collective-permute-start(bf16[2048,256]{1,0:T(8,128)(2,1)S(1)} %convert_element_type.177), channel_id=1, source_target_pairs={{3,2},{2,3},{6,4},{4,5},{5,6},{11,8},{8,10},{10,11},{14,12},{15,13... | collective-permute-start | bytes 3145736 | tf_op jit(solution)/shard_map/ppermute | solution.py:908
  291.8 20.8 %collective-permute-start.21 = (bf16[4096,128]{1,0:T(8,128)(2,1)}, bf16[4096,128]{1,0:T(8,128)(2,1)}, u32[]{:S(2)}, u32[]{:S(2)}) collective-permute-start(bf16[4096,128]{1,0:T(8,128)(2,1)} %get-tuple-element.156), channel_id=1, source_target_pairs={{0,1},{1,3},{3,2},{2,6},{6,4},{4,5},{5,7},{7,11},{11,9},{9,8},{8,1... | collective-permute-start | bytes 3145736 | tf_op jit(solution)/shard_map/ppermute | solution.py:77
  293.2 19.4 %collective-permute-start.22 = (bf16[4096,128]{1,0:T(8,128)(2,1)}, bf16[4096,128]{1,0:T(8,128)(2,1)}, u32[]{:S(2)}, u32[]{:S(2)}) collective-permute-start(bf16[4096,128]{1,0:T(8,128)(2,1)} %get-tuple-element.159), channel_id=1, source_target_pairs={{1,0},{3,1},{2,3},{6,2},{4,6},{5,4},{7,5},{11,7},{9,11},{8,9},{10,... | collective-permute-start | bytes 3145736 | tf_op jit(solution)/shard_map/ppermute | solution.py:77
  338.9 20.2 %collective-permute-start.23 = (bf16[4096,128]{1,0:T(8,128)(2,1)}, bf16[4096,128]{1,0:T(8,128)(2,1)}, u32[]{:S(2)}, u32[]{:S(2)}) collective-permute-start(bf16[4096,128]{1,0:T(8,128)(2,1)} %get-tuple-element.164), channel_id=1, source_target_pairs={{0,1},{1,3},{3,2},{2,6},{6,4},{4,5},{5,7},{7,11},{11,9},{9,8},{8,1... | collective-permute-start | bytes 3145736 | tf_op jit(solution)/shard_map/ppermute | solution.py:77
  339.8 19.2 %collective-permute-start.24 = (bf16[4096,128]{1,0:T(8,128)(2,1)}, bf16[4096,128]{1,0:T(8,128)(2,1)}, u32[]{:S(2)}, u32[]{:S(2)}) collective-permute-start(bf16[4096,128]{1,0:T(8,128)(2,1)} %get-tuple-element.165), channel_id=1, source_target_pairs={{1,0},{3,1},{2,3},{6,2},{4,6},{5,4},{7,5},{11,7},{9,11},{8,9},{10,... | collective-permute-start | bytes 3145736 | tf_op jit(solution)/shard_map/ppermute | solution.py:77
  385.5 18.9 %collective-permute-start.25 = (bf16[4096,128]{1,0:T(8,128)(2,1)}, bf16[4096,128]{1,0:T(8,128)(2,1)S(1)}, u32[]{:S(2)}, u32[]{:S(2)}) collective-permute-start(bf16[4096,128]{1,0:T(8,128)(2,1)} %get-tuple-element.170), channel_id=1, source_target_pairs={{0,1},{1,3},{3,2},{2,6},{6,4},{4,5},{5,7},{7,11},{11,9},{9,8},{8,1... | collective-permute-start | bytes 3145736 | tf_op jit(solution)/shard_map/ppermute | solution.py:77
  385.5 18.9 %collective-permute-start.26 = (bf16[4096,128]{1,0:T(8,128)(2,1)}, bf16[4096,128]{1,0:T(8,128)(2,1)}, u32[]{:S(2)}, u32[]{:S(2)}) collective-permute-start(bf16[4096,128]{1,0:T(8,128)(2,1)} %get-tuple-element.171), channel_id=1, source_target_pairs={{1,0},{3,1},{2,3},{6,2},{4,6},{5,4},{7,5},{11,7},{9,11},{8,9},{10,... | collective-permute-start | bytes 3145736 | tf_op jit(solution)/shard_map/ppermute | solution.py:77
  420.6 3.1 collective-permute-start.27
  425.8 9.1 %collective-permute-start.28 = (bf16[4,2,72,256]{3,2,0,1:T(8,128)(2,1)S(1)}, bf16[4,2,72,256]{3,2,0,1:T(8,128)(2,1)S(1)}, u32[]{:S(2)}, u32[]{:S(2)}) collective-permute-start(bf16[4,2,72,256]{3,2,0,1:T(8,128)(2,1)S(1)} %fusion.17), channel_id=1, source_target_pairs={{0,1},{1,0},{2,3},{3,2},{4,5},{5,4},{6,7},{7,6},{8,9},{9,8},{10,11... | collective-permute-start | bytes 884744 | tf_op jit(solution)/shard_map/ppermute | solution.py:94
  426.0 9.2 %collective-permute-start.30 = (bf16[4,2,72,256]{3,2,1,0:T(8,128)(2,1)S(1)}, bf16[4,2,72,256]{3,2,1,0:T(8,128)(2,1)S(1)}, u32[]{:S(2)}, u32[]{:S(2)}) collective-permute-start(bf16[4,2,72,256]{3,2,1,0:T(8,128)(2,1)S(1)} %fusion.16), channel_id=1, source_target_pairs={{0,2},{1,3},{2,0},{3,1},{4,6},{5,7},{6,4},{7,5},{8,10},{9,11},{10,... | collective-permute-start | bytes 884744 | tf_op jit(solution)/shard_map/ppermute | solution.py:94
  435.1 5.2 %collective-permute-start.29 = (bf16[4,72,256]{2,1,0:T(8,128)(2,1)S(1)}, bf16[4,72,256]{2,1,0:T(8,128)(2,1)S(1)}, u32[]{:S(2)}, u32[]{:S(2)}) collective-permute-start(bf16[4,72,256]{2,1,0:T(8,128)(2,1)S(1)} %fusion.43), channel_id=1, source_target_pairs={{0,2},{1,3},{2,0},{3,1},{4,6},{5,7},{6,4},{7,5},{8,10},{9,11},{10,... | collective-permute-start | bytes 442376 | tf_op jit(solution)/shard_map/ppermute | solution.py:94
  435.3 5.2 %collective-permute-start.31 = (bf16[4,72,256]{2,1,0:T(8,128)(2,1)S(1)}, bf16[4,72,256]{2,1,0:T(8,128)(2,1)S(1)}, u32[]{:S(2)}, u32[]{:S(2)}) collective-permute-start(bf16[4,72,256]{2,1,0:T(8,128)(2,1)S(1)} %fusion.44), channel_id=1, source_target_pairs={{0,1},{1,0},{2,3},{3,2},{4,5},{5,4},{6,7},{7,6},{8,9},{9,8},{10,11... | collective-permute-start | bytes 442376 | tf_op jit(solution)/shard_map/ppermute | solution.py:94
  440.6 21.8 %collective-permute-start.39 = (bf16[2048,256]{1,0:T(8,128)(2,1)}, bf16[2048,256]{1,0:T(8,128)(2,1)}, u32[]{:S(2)}, u32[]{:S(2)}) collective-permute-start(bf16[2048,256]{1,0:T(8,128)(2,1)} %get-tuple-element.195), channel_id=1, source_target_pairs={{3,2},{2,3},{6,4},{4,5},{5,6},{11,8},{8,10},{10,11},{14,12},{15,13... | collective-permute-start | bytes 3145736 | tf_op jit(solution)/shard_map/ppermute | solution.py:908
  442.4 6.6 %collective-permute-start.32 = (bf16[1,144,256]{2,1,0:T(8,128)(2,1)S(1)}, bf16[1,144,256]{2,1,0:T(8,128)(2,1)S(1)}, u32[]{:S(2)}, u32[]{:S(2)}) collective-permute-start(bf16[1,144,256]{2,1,0:T(8,128)(2,1)S(1)} %get-tuple-element.242), channel_id=1, source_target_pairs={{0,4},{1,5},{2,6},{3,7},{4,0},{5,1},{6,2},{7,3},{8,12},{9,13},{10,... | collective-permute-start | bytes 221192 | tf_op jit(solution)/shard_map/ppermute | solution.py:94
  442.5 8.6 %collective-permute-start.34 = (bf16[1,144,256]{2,1,0:T(8,128)(2,1)S(1)}, bf16[1,144,256]{2,1,0:T(8,128)(2,1)S(1)}, u32[]{:S(2)}, u32[]{:S(2)}) collective-permute-start(bf16[1,144,256]{2,1,0:T(8,128)(2,1)S(1)} %get-tuple-element.243), channel_id=1, source_target_pairs={{0,12},{1,13},{2,14},{3,15},{4,8},{5,9},{6,10},{7,11},{8,4},{9,5},... | collective-permute-start | bytes 221192 | tf_op jit(solution)/shard_map/ppermute | solution.py:94
  447.2 6.1 %collective-permute-start.33 = (bf16[1,144,256]{2,1,0:T(8,128)(2,1)S(1)}, bf16[1,144,256]{2,1,0:T(8,128)(2,1)S(1)}, u32[]{:S(2)}, u32[]{:S(2)}) collective-permute-start(bf16[1,144,256]{2,1,0:T(8,128)(2,1)S(1)} %get-tuple-element.244), channel_id=1, source_target_pairs={{0,8},{1,9},{2,10},{3,11},{4,12},{5,13},{6,14},{7,15},{8,0},{9,1},... | collective-permute-start | bytes 221192 | tf_op jit(solution)/shard_map/ppermute | solution.py:94
  454.8 4.6 collective-permute-start.36
  455.3 5.4 %collective-permute-start.37 = (f32[8,128]{1,0:T(8,128)S(1)}, f32[8,128]{1,0:T(8,128)S(1)}, u32[]{:S(2)}, u32[]{:S(2)}) collective-permute-start(f32[8,128]{1,0:T(8,128)S(1)} %iota.23), channel_id=1, source_target_pairs={{0,12},{1,13},{2,14},{3,15},{4,8},{5,9},{6,10},{7,11},{8,4},{9,5},... | collective-permute-start | bytes 12296 | tf_op jit(solution)/shard_map/ppermute | solution.py:94
  457.5 3.6 collective-permute-start.35
  461.2 1.2 collective-permute-start.38
  462.3 10.6 %collective-permute-start.42 = (f32[8,128]{1,0:T(8,128)S(1)}, f32[8,128]{1,0:T(8,128)S(1)}, u32[]{:S(2)}, u32[]{:S(2)}) collective-permute-start(f32[8,128]{1,0:T(8,128)S(1)} %add.175), channel_id=1, source_target_pairs={{0,3},{1,2},{2,1},{3,0},{4,7},{5,6},{6,5},{7,4},{8,11},{9,10},{10,... | collective-permute-start | bytes 12296 | tf_op jit(solution)/shard_map/ppermute | solution.py:94
  468.2 4.8 %collective-permute-start.41 = (f32[8,128]{1,0:T(8,128)S(1)}, f32[8,128]{1,0:T(8,128)S(1)}, u32[]{:S(2)}, u32[]{:S(2)}) collective-permute-start(f32[8,128]{1,0:T(8,128)S(1)} %add.175), channel_id=1, source_target_pairs={{0,2},{1,3},{2,0},{3,1},{4,6},{5,7},{6,4},{7,5},{8,10},{9,11},{10,... | collective-permute-start | bytes 12296 | tf_op jit(solution)/shard_map/ppermute | solution.py:94
  468.2 4.8 %collective-permute-start.40 = (f32[8,128]{1,0:T(8,128)S(1)}, f32[8,128]{1,0:T(8,128)S(1)}, u32[]{:S(2)}, u32[]{:S(2)}) collective-permute-start(f32[8,128]{1,0:T(8,128)S(1)} %add.175), channel_id=1, source_target_pairs={{0,1},{1,0},{2,3},{3,2},{4,5},{5,4},{6,7},{7,6},{8,9},{9,8},{10,11... | collective-permute-start | bytes 12296 | tf_op jit(solution)/shard_map/ppermute | solution.py:94
  (50 other events, 424.1 us)

commit v13 on v12

--- a/solution.py
+++ b/solution.py
@@ -82,7 +82,7 @@
     starts = [share * d // D for d in range(peers)]
     counts = [-(-share * (d + 1) // D) - starts[d] for d in range(peers)]
     shared = [share * d % D != 0 for d in range(peers)]
-    height = -(-(max(counts) + 1) // 16) * 16
+    height = -(-max(counts) // 16) * 16
     return starts, counts, shared, height
 
 
@@ -177,13 +177,8 @@
             def _():
                 lay(sources[2], sources[3])
 
-        count = jnp.zeros((1, D), jnp.float32)
-        for source in (sources[1], sources[3]):
-            for spot in range(group):
-                count = count + source[spot, half - 1 : half, :].astype(jnp.float32)
-        outs[-1][...] = count
         start = 0
-        for out, size in zip(outs[:-1], sizes):
+        for out, size in zip(outs, sizes):
             out[:size, :] = buffer[start : start + size, :].astype(out.dtype)
             if out.shape[0] > size:
                 out[size:, :] = jnp.zeros((out.shape[0] - size, D), out.dtype)
@@ -197,13 +192,10 @@
             num_scalar_prefetch=1,
             grid=(1,),
             in_specs=[whole(first.shape)] * 4,
-            out_specs=[whole((tall, D)) for tall in talls + [1]],
+            out_specs=[whole((tall, D)) for tall in talls],
             scratch_shapes=[pltpu.VMEM((-(-rows // 8) * 8 + 8, D), jnp.float32)],
         ),
-        out_shape=[
-            jax.ShapeDtypeStruct((tall, D), kind)
-            for tall, kind in zip(talls + [1], kinds + [jnp.float32])
-        ],
+        out_shape=[jax.ShapeDtypeStruct((tall, D), kind) for tall, kind in zip(talls, kinds)],
         compiler_params=LIMIT,
         cost_estimate=cost(4),
         name="spread_rows",
@@ -477,7 +469,7 @@
 
     whole_rows = pl.BlockSpec((tile, D), lambda i, *_: (i, 0))
     woven = pl.BlockSpec((2 * tile, HALF), lambda i, *_: (i, 0))
-    ins = [whole_rows] + [pl.BlockSpec(memory_space=pl.ANY)] * 3
+    ins = [whole_rows] + [pl.BlockSpec(memory_space=pltpu.HBM)] * 3
     ins = ins + [whole(mats.shape), woven, whole_rows]
     outs = [whole_rows] * 4 + [pl.BlockSpec((K, 2 * tile, HALF), lambda i, *_: (0, i, 0))]
     shapes = [
@@ -851,9 +843,7 @@
     counted = valid[0].astype(jnp.float32)
     local_count = jnp.sum(valid[0])
     digits = (local_count >> jnp.array([16, 8, 0], jnp.int32)) & 255
-    piece = lax.dynamic_update_slice(
-        piece.reshape(height, D), digits.astype(jnp.bfloat16)[None, :], (height - 1, 0)
-    )
+    digits = jnp.pad(digits, (CH + 3, HALF - CH - 6)).astype(jnp.float32)[None, :]
     points = state_in.shape[1]
     blocks = neighbours.shape[0]
     assert blocks == H
@@ -882,13 +872,16 @@
             rows.reshape(bands, capacity, HALF), "space", split_axis=0, concat_axis=0, tiled=True
         ).reshape(bands * capacity, HALF)
 
-    held, posted = gathered_blocks(piece, inner(poster, columns, 1, 1).astype(jnp.bfloat16))
+    held, posted = gathered_blocks(
+        piece.reshape(height, D), (inner(poster, columns, 1, 1) + digits).astype(jnp.bfloat16)
+    )
     arrived = exchanged(posted)
-    w_in, w_node, w_dec, w_out, *w_round, biases, digits = spread_rows(
+    w_in, w_node, w_dec, w_out, *w_round, biases = spread_rows(
         held, total_size, peers, place
     )
     arrived, biases = lax.optimization_barrier((arrived, biases))
-    count = digits[0, 0] * 65536.0 + digits[0, 1] * 256.0 + digits[0, 2]
+    counts = arrived.reshape(bands, capacity, HALF)[:, 0, CH + 3 : CH + 6].astype(jnp.float32)
+    counts = jnp.sum(counts, 0, keepdims=True)
     w_out = jnp.pad(w_out.reshape(D, CH), ((0, 0), (0, HALF - CH)))
     w_round = [mats.reshape(5, D, D) for mats in w_round]
     b_head = biases[:3]
@@ -896,9 +889,10 @@
     mesh, gathered, sent, ids_row, ids = encode_rows(
         arrived, w_in, w_node, biases, w_round[0]
     )
-    sent, partner, neighbours, counted = lax.optimization_barrier(
-        (sent, partner, neighbours, counted)
-    )
+    sent, partner, neighbours, counted, counts = lax.optimization_barrier(
+        (sent, partner, neighbours, counted, counts)
+    )
+    counts = counts + swapped(counts, "dp", 1)
     index = 2 * ((neighbours - band * blocks + H) % (blocks * bands)).T.reshape(-1)
     moved = [(n, place) for n, place in enumerate(walk) if n != place]
     stays = jnp.asarray([n == place for n, place in enumerate(walk)])[band]
@@ -926,7 +920,7 @@
         before, after = halo(walk, sent, sent)
         terms = node_terms(mesh, w_round[layer], b_round[layer])
         if layer == 0:
-            before, valid_around = lax.optimization_barrier((before, valid_around))
+            before, valid_around, counts = lax.optimization_barrier((before, valid_around, counts))
         following = w_round[layer + 1] if layer + 1 < ROUNDS else None
         new, back, update, agg, slopes, *rest = round_forward(
             index, mesh, before, sent, after, w_round[layer], terms, following,
@@ -935,6 +929,7 @@
         kept.append((mesh, back, update, agg, slopes))
         mesh = new
         sent = rest[0]
+    count = counts[0, 0] * 65536.0 + counts[0, 1] * 256.0 + counts[0, 2]
     wide_valid = valid_around[:CH].astype(jnp.float32)
     coded = valid_around[CH : CH + 1, : points + ROWW].astype(jnp.float32)
     weights = [

time: 480 us -> 480 us (level)
    ppermute x24 -> x25, waiting for transfers between devices: 31.8 us -> 31.3 us  [swapped(): lax.ppermute(value, axis, [(i, i ^ bit) for i in range(lax.axis_size(axis...]
    ppermute x24 -> x25, starting transfers between devices: 29.2 us -> 29.4 us  [swapped(): lax.ppermute(value, axis, [(i, i ^ bit) for i in range(lax.axis_size(axis...]
  transfers between devices with their start and end apart: 46 -> 47, of which waited for: 27 -> 26; matrix products, arithmetic and copies ran while one was open for 11% -> 11% of each run, Pallas kernels for 11% -> 11%
where the time goes in v13:
time: 480 us; the launch traced here: 478 us
  Pallas kernels  204 us (42%)
  waiting for transfers between devices  116 us (24%)
  starting transfers between devices  78.2 us (16%)
  matrix products  27.8 us (6%)
  other arithmetic  27.4 us (6%)
  local copies, waits for them, and re-layouts  16.7 us (3%)
  between operations  7.86 us (2%)
    pallas_call x3, Pallas kernels, edges_backward(): pl.pallas_call(body, grid_spec=pltpu.PrefetchScalarGridSpec(num_scalar_pr...  79.5 us
    pallas_call x3, Pallas kernels, round_forward(): pl.pallas_call(body, grid_spec=pltpu.PrefetchScalarGridSpec(num_scalar_pr...  75.9 us
    ppermute x6, waiting for transfers between devices, halo(): lax.ppermute(initial, 'space', down)  34.9 us
    ppermute x25, waiting for transfers between devices, swapped(): lax.ppermute(value, axis, [(i, i ^ bit) for i in range(lax.axis_size(axis...  31.3 us
    ppermute x25, starting transfers between devices, swapped(): lax.ppermute(value, axis, [(i, i ^ bit) for i in range(lax.axis_size(axis...  29.4 us
    dot_general x18, matrix products, inner(): lax.dot_general(left, right, (((left_dim,), (right_dim,)), ((), ())), pre...  26.5 us
    all_to_all x3, waiting for transfers between devices, exchanged(): lax.all_to_all(rows.reshape(bands, capacity, HALF), 'space', split_axis=0...  21.5 us
    all_to_all x3, starting transfers between devices, exchanged(): lax.all_to_all(rows.reshape(bands, capacity, HALF), 'space', split_axis=0...  15.9 us
  transfers between devices with their start and end apart: 47, of which 26 were waited for; matrix products, arithmetic and copies ran while one was open for 11% of the time, Pallas kernels for 11%

profile of v13, /device:TPU:0, one launch (start us, length us, event | category | flops | bytes accessed | tf_op | source)
XLA Modules:
  0.0 478.2 jit_solution(7170366842795243498)
XLA Ops:
  2.5 5.1 %collective-permute-start.2 = (bf16[1,144,256]{2,1,0:T(8,128)(2,1)S(1)}, bf16[1,144,256]{2,1,0:T(8,128)(2,1)S(1)}, u32[]{:S(2)}, u32[]{:S(2)}) collective-permute-start(bf16[1,144,256]{2,1,0:T(8,128)(2,1)S(1)} %broadcast_in_dim_reshape.3), channel_id=1, source_target_pairs={{0,12},{1,13},{2,14},{3,15},{4,8},{5,9},{6,10},{7,11},{8,4},{9,5},... | collective-permute-start | bytes 221192 | tf_op jit(solution)/shard_map/ppermute | solution.py:94
  26.1 4.8 %collective-permute-done.6 = bf16[8,72,256]{2,1,0:T(8,128)(2,1)S(1)} collective-permute-done((bf16[8,72,256]{2,1,0:T(8,128)(2,1)S(1)}, bf16[8,72,256]{2,1,0:T(8,128)(2,1)S(1)}, u32[]{:S(2)}, u32[]{:S(2)}) %collective-permute-start.6) | collective-permute-done | bytes 294944 | tf_op jit(solution)/shard_map/ppermute | solution.py:94
  32.4 5.2 %all-to-all-start = ((bf16[16,64,128]{2,1,0:T(8,128)(2,1)}), bf16[16,64,128]{2,1,0:T(8,128)(2,1)S(1)}, u32[]{:S(2)}, u32[]{:S(2)}) async-start(bf16[16,64,128]{2,1,0:T(8,128)(2,1)} %bitcast.162), calls=%async_computation | async-start | bytes 524288 | tf_op jit(solution)/shard_map/all_to_all | solution.py:871
  38.6 4.0 spread_rows.1
  42.6 5.4 %all-to-all-done = bf16[16,64,128]{2,1,0:T(8,128)(2,1)S(1)} async-done(((bf16[16,64,128]{2,1,0:T(8,128)(2,1)}), bf16[16,64,128]{2,1,0:T(8,128)(2,1)S(1)}, u32[]{:S(2)}, u32[]{:S(2)}) %all-to-all-start) | async-done | bytes 262176 | tf_op jit(solution)/shard_map/all_to_all | solution.py:871
  48.7 6.0 %encode_rows.1 = (f32[2048,256]{1,0:T(8,128)}, bf16[2048,256]{1,0:T(8,128)(2,1)}, bf16[4096,128]{1,0:T(8,128)(2,1)}, s32[1,1024]{1,0:T(1,128)}, s32[1024,1]{1,0:T(8,128)}) custom-call(bf16[1024,128]{1,0:T(8,128)(2,1)} %bitcast.154, bf16[128,256]{1,0:T(8,128)(2,1)} %get-tuple-element.111.in_ref, bf16[256,256]{1,0:T(8,128)(2,1)} %get-tuple-element.112.node_ref, ...), custom_call_target="tpu_custom_call" | custom-call | bytes 15000000 | tf_op jit(solution)/shard_map/encode_rows/pallas_call | solution.py:747
  60.4 4.5 collective-permute-start.11
  65.0 4.0 node_terms.3
  68.9 11.6 %collective-permute-done.12 = bf16[79,360]{1,0:T(8,128)(2,1)S(1)} collective-permute-done((bf16[79,360]{1,0:T(8,128)(2,1)S(1)}, bf16[79,360]{1,0:T(8,128)(2,1)S(1)}, u32[]{:S(2)}, u32[]{:S(2)}) %collective-permute-start.12) | collective-permute-done | bytes 56912 | tf_op jit(solution)/shard_map/ppermute | solution.py:49
  80.7 2.5 collective-permute-done.10.refs_2_
  84.6 24.2 %round_forward.3 = (f32[2048,256]{1,0:T(8,128)}, f32[2048,256]{1,0:T(8,128)}, bf16[2048,256]{1,0:T(8,128)(2,1)}, bf16[2048,256]{1,0:T(8,128)(2,1)}, bf16[6,4096,...) custom-call(s32[12288]{0:T(1024)} %copy-done.16, f32[2048,256]{1,0:T(8,128)} %get-tuple-element.118.mesh_ref.refs_1_, ...), custom_call_target="tpu_custom_call" | custom-call | bytes 75000000 | tf_op jit(solution)/shard_map/round_forward/pallas_call | solution.py:497
  110.9 3.9 node_terms.4
  114.7 16.8 %collective-permute-done.16.refs_4_ = bf16[4096,128]{1,0:T(8,128)(2,1)S(1)} collective-permute-done((bf16[4096,128]{1,0:T(8,128)(2,1)}, bf16[4096,128]{1,0:T(8,128)(2,1)S(1)}, u32[]{:S(2)}, u32[]{:S(2)}) %collective-permute-start.16) | collective-permute-done | bytes 1048608 | tf_op jit(solution)/shard_map/ppermute | solution.py:77
  131.5 2.9 collective-permute-done.15.refs_2_
  135.4 24.3 %round_forward.4 = (f32[2048,256]{1,0:T(8,128)}, f32[2048,256]{1,0:T(8,128)}, bf16[2048,256]{1,0:T(8,128)(2,1)}, bf16[2048,256]{1,0:T(8,128)(2,1)}, bf16[6,4096,...) custom-call(s32[12288]{0:T(1024)} %copy-done.16, f32[2048,256]{1,0:T(8,128)} %get-tuple-element.126.mesh_ref.refs_1_, ...), custom_call_target="tpu_custom_call" | custom-call | bytes 75000000 | tf_op jit(solution)/shard_map/round_forward/pallas_call | solution.py:497
  163.0 3.9 node_terms.5
  166.9 18.1 %collective-permute-done.18.refs_4_ = bf16[4096,128]{1,0:T(8,128)(2,1)S(1)} collective-permute-done((bf16[4096,128]{1,0:T(8,128)(2,1)}, bf16[4096,128]{1,0:T(8,128)(2,1)S(1)}, u32[]{:S(2)}, u32[]{:S(2)}) %collective-permute-start.18) | collective-permute-done | bytes 1048608 | tf_op jit(solution)/shard_map/ppermute | solution.py:77
  186.3 27.4 %round_forward.5 = (f32[2048,256]{1,0:T(8,128)}, f32[2048,256]{1,0:T(8,128)}, bf16[2048,256]{1,0:T(8,128)(2,1)}, bf16[2048,256]{1,0:T(8,128)(2,1)}, bf16[6,4096,...) custom-call(s32[12288]{0:T(1024)} %copy-done.16, ...), custom_call_target="tpu_custom_call" | custom-call | bytes 75000000 | tf_op jit(solution)/shard_map/round_forward/pallas_call | solution.py:497
  213.7 4.8 %all-to-all-start.1 = ((bf16[16,64,128]{2,1,0:T(8,128)(2,1)}), bf16[16,64,128]{2,1,0:T(8,128)(2,1)S(1)}, u32[]{:S(2)}, u32[]{:S(2)}) async-start(bf16[16,64,128]{2,1,0:T(8,128)(2,1)} %bitcast.163), calls=%async_computation.1 | async-start | bytes 524288 | tf_op jit(solution)/shard_map/all_to_all | solution.py:871
  218.6 8.4 %all-to-all-done.1 = bf16[16,64,128]{2,1,0:T(8,128)(2,1)S(1)} async-done(((bf16[16,64,128]{2,1,0:T(8,128)(2,1)}), bf16[16,64,128]{2,1,0:T(8,128)(2,1)S(1)}, u32[]{:S(2)}, u32[]{:S(2)}) %all-to-all-start.1) | async-done | bytes 262176 | tf_op jit(solution)/shard_map/all_to_all | solution.py:871
  227.6 3.3 collective-permute-start.19
  234.8 2.3 collective-permute-done.20
  240.7 5.9 %all-to-all-start.2 = ((bf16[16,64,128]{2,1,0:T(8,128)(2,1)}), bf16[16,64,128]{2,1,0:T(8,128)(2,1)S(1)}, u32[]{:S(2)}, u32[]{:S(2)}) async-start(bf16[16,64,128]{2,1,0:T(8,128)(2,1)} %bitcast.18), calls=%async_computation.2 | async-start | bytes 524288 | tf_op jit(solution)/shard_map/all_to_all | solution.py:871
  247.4 7.7 %all-to-all-done.2 = bf16[16,64,128]{2,1,0:T(8,128)(2,1)S(1)} async-done(((bf16[16,64,128]{2,1,0:T(8,128)(2,1)}), bf16[16,64,128]{2,1,0:T(8,128)(2,1)S(1)}, u32[]{:S(2)}, u32[]{:S(2)}) %all-to-all-start.2) | async-done | bytes 262176 | tf_op jit(solution)/shard_map/all_to_all | solution.py:871
  256.8 26.8 %edges_backward.3 = (f32[2048,256]{1,0:T(8,128)}, bf16[2048,256]{1,0:T(8,128)(2,1)}, bf16[1024,256]{1,0:T(8,128)(2,1)}, bf16[2048,256]{1,0:T(8,128)(2,1)}, bf16[...) custom-call(s32[12288]{0:T(1024)} %copy-done.16, ...), custom_call_target="tpu_custom_call" | custom-call | bytes 75000000 | tf_op jit(solution)/shard_map/edges_backward/pallas_call | solution.py:640
  288.4 2.4 fusion.95.refs_18_
  293.4 2.4 collective-permute-start.23
  297.5 4.0 carried_terms.3.refs_4_
  303.4 3.6 convert_select_fusion
  307.0 6.0 %collective-permute-done.22.refs_6_ = bf16[4096,128]{1,0:T(8,128)(2,1)} collective-permute-done((bf16[4096,128]{1,0:T(8,128)(2,1)}, bf16[4096,128]{1,0:T(8,128)(2,1)}, u32[]{:S(2)}, u32[]{:S(2)}) %collective-permute-start.22) | collective-permute-done | bytes 1048608 | tf_op jit(solution)/shard_map/ppermute | solution.py:77
  312.9 26.3 %edges_backward.4 = (f32[2048,256]{1,0:T(8,128)}, bf16[2048,256]{1,0:T(8,128)(2,1)}, bf16[2048,256]{1,0:T(8,128)(2,1)}, bf16[2048,256]{1,0:T(8,128)(2,1)}, bf16[...) custom-call(s32[12288]{0:T(1024)} %copy-done.16, ...), custom_call_target="tpu_custom_call" | custom-call | bytes 84000000 | tf_op jit(solution)/shard_map/edges_backward/pallas_call | solution.py:640
  340.2 3.1 collective-permute-start.25
  343.3 2.4 fusion.92.refs_11_
  346.9 4.0 carried_terms.4.refs_4_
  350.9 2.3 convert_reduce_fusion.2
  353.2 2.4 fusion.73.refs_10_
  359.5 26.4 %edges_backward.5 = (f32[2048,256]{1,0:T(8,128)}, bf16[2048,256]{1,0:T(8,128)(2,1)}, bf16[2048,256]{1,0:T(8,128)(2,1)}, bf16[2048,256]{1,0:T(8,128)(2,1)}, bf16[...) custom-call(s32[12288]{0:T(1024)} %copy-done.16, ...), custom_call_target="tpu_custom_call" | custom-call | bytes 84000000 | tf_op jit(solution)/shard_map/edges_backward/pallas_call | solution.py:640
  386.0 3.8 collective-permute-start.27
  389.8 2.4 fusion.90.refs_6_
  393.4 4.0 carried_terms.5.part_ref
  405.9 10.1 %encode_backward.1 = (f32[2048,256]{1,0:T(8,128)}, bf16[2048,256]{1,0:T(8,128)(2,1)}, f32[128,256]{1,0:T(8,128)}, f32[256,256]{1,0:T(8,128)}, f32[2,256]{1,0:T(2,128)}, /*index=5*/f32[256,256]{1,0:T(8,128)}) custom-call(f32[2048,256]{1,0:T(8,128)} %carried_terms.5.part_ref, f32[4096,128]{1,0:T(8,128)} %get-tuple-element.171.own_ref, ...), custom_call_target="tpu_custom_call" | custom-call | bytes 30000000 | tf_op jit(solution)/shard_map/encode_backward/pallas_call | solution.py:812
  416.0 5.1 %collect_rows.1 = (f32[16,144,256]{2,1,0:T(8,128)}, bf16[16,144,256]{2,1,0:T(8,128)(2,1)}) custom-call(s32[1]{0:T(128)} %bitcast.6.place_ref, f32[128,256]{1,0:T(8,128)} %get-tuple-element.175.refs_0_, f32[256,256]{1,0:T(8,128)} %get-tuple-element.176.refs_1_, f32[256,256]{1,0:T(8,128)} %fusion.89.refs_2_, f32[78,256]{1,0:T(8,128)} %reshape.155.refs_3_, ...), custom_call_target="tpu_custom_call" | custom-call | bytes 15000000 | tf_op jit(solution)/shard_map/collect_rows/pallas_call | solution.py:233
  421.2 3.0 collective-permute-done.28
  426.5 8.9 %collective-permute-done.29 = bf16[4,2,72,256]{3,2,0,1:T(8,128)(2,1)S(1)} collective-permute-done((bf16[4,2,72,256]{3,2,0,1:T(8,128)(2,1)S(1)}, bf16[4,2,72,256]{3,2,0,1:T(8,128)(2,1)S(1)}, u32[]{:S(2)}, u32[]{:S(2)}) %collective-permute-start.29) | collective-permute-done | bytes 294944 | tf_op jit(solution)/shard_map/ppermute | solution.py:94
  437.5 3.3 collective-permute-done.30
  443.0 4.7 collective-permute-start.35
  462.8 5.8 %collective-permute-start.43 = (f32[8,128]{1,0:T(8,128)S(1)}, f32[8,128]{1,0:T(8,128)S(1)}, u32[]{:S(2)}, u32[]{:S(2)}) collective-permute-start(f32[8,128]{1,0:T(8,128)S(1)} %add.191), channel_id=1, source_target_pairs={{0,3},{1,2},{2,1},{3,0},{4,7},{5,6},{6,5},{7,4},{8,11},{9,10},{10,... | collective-permute-start | bytes 12296 | tf_op jit(solution)/shard_map/ppermute | solution.py:94
  470.1 3.5 select_bitcast_fusion
  (269 shorter events, 96.8 us)
Async XLA Ops:
  2.5 14.5 %collective-permute-start.2 = (bf16[1,144,256]{2,1,0:T(8,128)(2,1)S(1)}, bf16[1,144,256]{2,1,0:T(8,128)(2,1)S(1)}, u32[]{:S(2)}, u32[]{:S(2)}) collective-permute-start(bf16[1,144,256]{2,1,0:T(8,128)(2,1)S(1)} %broadcast_in_dim_reshape.3), channel_id=1, source_target_pairs={{0,12},{1,13},{2,14},{3,15},{4,8},{5,9},{6,10},{7,11},{8,4},{9,5},... | collective-permute-start | bytes 221192 | tf_op jit(solution)/shard_map/ppermute | solution.py:94
  7.6 9.4 %collective-permute-start.1 = (bf16[1,144,256]{2,1,0:T(8,128)(2,1)S(1)}, bf16[1,144,256]{2,1,0:T(8,128)(2,1)S(1)}, u32[]{:S(2)}, u32[]{:S(2)}) collective-permute-start(bf16[1,144,256]{2,1,0:T(8,128)(2,1)S(1)} %broadcast_in_dim_reshape.3), channel_id=1, source_target_pairs={{0,8},{1,9},{2,10},{3,11},{4,12},{5,13},{6,14},{7,15},{8,0},{9,1},... | collective-permute-start | bytes 221192 | tf_op jit(solution)/shard_map/ppermute | solution.py:94
  7.6 9.4 %collective-permute-start = (bf16[1,144,256]{2,1,0:T(8,128)(2,1)S(1)}, bf16[1,144,256]{2,1,0:T(8,128)(2,1)S(1)}, u32[]{:S(2)}, u32[]{:S(2)}) collective-permute-start(bf16[1,144,256]{2,1,0:T(8,128)(2,1)S(1)} %broadcast_in_dim_reshape.3), channel_id=1, source_target_pairs={{0,4},{1,5},{2,6},{3,7},{4,0},{5,1},{6,2},{7,3},{8,12},{9,13},{10,... | collective-permute-start | bytes 221192 | tf_op jit(solution)/shard_map/ppermute | solution.py:94
  17.0 5.2 %collective-permute-start.4 = (bf16[4,72,256]{2,1,0:T(8,128)(2,1)S(1)}, bf16[4,72,256]{2,1,0:T(8,128)(2,1)S(1)}, u32[]{:S(2)}, u32[]{:S(2)}) collective-permute-start(bf16[4,72,256]{2,1,0:T(8,128)(2,1)S(1)} %get-tuple-element.247), channel_id=1, source_target_pairs={{0,1},{1,0},{2,3},{3,2},{4,5},{5,4},{6,7},{7,6},{8,9},{9,8},{10,11... | collective-permute-start | bytes 442376 | tf_op jit(solution)/shard_map/ppermute | solution.py:94
  18.7 5.1 %collective-permute-start.3 = (bf16[4,72,256]{2,1,0:T(8,128)(2,1)S(1)}, bf16[4,72,256]{2,1,0:T(8,128)(2,1)S(1)}, u32[]{:S(2)}, u32[]{:S(2)}) collective-permute-start(bf16[4,72,256]{2,1,0:T(8,128)(2,1)S(1)} %get-tuple-element.248), channel_id=1, source_target_pairs={{0,2},{1,3},{2,0},{3,1},{4,6},{5,7},{6,4},{7,5},{8,10},{9,11},{10,... | collective-permute-start | bytes 442376 | tf_op jit(solution)/shard_map/ppermute | solution.py:94
  23.9 7.0 %collective-permute-start.6 = (bf16[8,72,256]{2,1,0:T(8,128)(2,1)S(1)}, bf16[8,72,256]{2,1,0:T(8,128)(2,1)S(1)}, u32[]{:S(2)}, u32[]{:S(2)}) collective-permute-start(bf16[8,72,256]{2,1,0:T(8,128)(2,1)S(1)} %pad_maximum_fusion.3), channel_id=1, source_target_pairs={{0,2},{1,3},{2,0},{3,1},{4,6},{5,7},{6,4},{7,5},{8,10},{9,11},{10,... | collective-permute-start | bytes 884744 | tf_op jit(solution)/shard_map/ppermute | solution.py:94
  25.5 6.7 %collective-permute-start.5 = (bf16[8,72,256]{2,1,0:T(8,128)(2,1)S(1)}, bf16[8,72,256]{2,1,0:T(8,128)(2,1)S(1)}, u32[]{:S(2)}, u32[]{:S(2)}) collective-permute-start(bf16[8,72,256]{2,1,0:T(8,128)(2,1)S(1)} %pad_maximum_fusion.2), channel_id=1, source_target_pairs={{0,1},{1,0},{2,3},{3,2},{4,5},{5,4},{6,7},{7,6},{8,9},{9,8},{10,11... | collective-permute-start | bytes 884744 | tf_op jit(solution)/shard_map/ppermute | solution.py:94
  30.9 6.7 %collective-permute-start.8 = (bf16[16,72,256]{2,1,0:T(8,128)(2,1)S(1)}, bf16[16,72,256]{2,1,0:T(8,128)(2,1)S(1)}, u32[]{:S(2)}, u32[]{:S(2)}) collective-permute-start(bf16[16,72,256]{2,1,0:T(8,128)(2,1)S(1)} %constant_dynamic-update-slice_fusion.6.refs_1_), channel_id=1, source_target_pairs={{0,16},{16,0},{1,17},{17,1},{2,18},{18,2},{3,19},{19,3},{4,20},{20... | collective-permute-start | bytes 1769480 | tf_op jit(solution)/shard_map/ppermute | solution.py:94
  32.3 5.3 %collective-permute-start.7 = (bf16[16,72,256]{2,1,0:T(8,128)(2,1)S(1)}, bf16[16,72,256]{2,1,0:T(8,128)(2,1)S(1)}, u32[]{:S(2)}, u32[]{:S(2)}) collective-permute-start(bf16[16,72,256]{2,1,0:T(8,128)(2,1)S(1)} %constant_dynamic-update-slice_fusion.4.refs_0_), channel_id=1, source_target_pairs={{0,16},{16,0},{1,17},{17,1},{2,18},{18,2},{3,19},{19,3},{4,20},{20... | collective-permute-start | bytes 1769480 | tf_op jit(solution)/shard_map/ppermute | solution.py:94
  32.4 15.6 %all-to-all-start = ((bf16[16,64,128]{2,1,0:T(8,128)(2,1)}), bf16[16,64,128]{2,1,0:T(8,128)(2,1)S(1)}, u32[]{:S(2)}, u32[]{:S(2)}) async-start(bf16[16,64,128]{2,1,0:T(8,128)(2,1)} %bitcast.162), calls=%async_computation | async-start | bytes 524288 | tf_op jit(solution)/shard_map/all_to_all | solution.py:871
  54.7 28.6 %collective-permute-start.14 = (bf16[4096,128]{1,0:T(8,128)(2,1)}, bf16[4096,128]{1,0:T(8,128)(2,1)S(1)}, u32[]{:S(2)}, u32[]{:S(2)}) collective-permute-start(bf16[4096,128]{1,0:T(8,128)(2,1)} %get-tuple-element.119.refs_3_), channel_id=1, source_target_pairs={{1,0},{3,1},{2,3},{6,2},{4,6},{5,4},{7,5},{11,7},{9,11},{8,9},{10,... | collective-permute-start | bytes 3145736 | tf_op jit(solution)/shard_map/ppermute | solution.py:77
  56.4 26.8 %collective-permute-start.10 = (bf16[4096,128]{1,0:T(8,128)(2,1)}, bf16[4096,128]{1,0:T(8,128)(2,1)S(1)}, u32[]{:S(2)}, u32[]{:S(2)}) collective-permute-start(bf16[4096,128]{1,0:T(8,128)(2,1)} %get-tuple-element.119.refs_3_), channel_id=1, source_target_pairs={{0,1},{1,3},{3,2},{2,6},{6,4},{4,5},{5,7},{7,11},{11,9},{9,8},{8,1... | collective-permute-start | bytes 3145736 | tf_op jit(solution)/shard_map/ppermute | solution.py:77
  56.8 3.7 collective-permute-start.13
  56.9 26.3 %collective-permute-start.9 = (s32[12288]{0:T(1024)S(1)}, s32[12288]{0:T(1024)S(1)}, u32[]{:S(2)}, u32[]{:S(2)}) collective-permute-start(s32[12288]{0:T(1024)S(1)} %mul.177), channel_id=1, source_target_pairs={{0,0},{1,1},{2,3},{3,2},{4,6},{5,4},{6,5},{7,7},{8,11},{9,9},{10,8... | collective-permute-start | bytes 147464 | tf_op jit(solution)/shard_map/ppermute | solution.py:899
  57.7 22.8 %collective-permute-start.12 = (bf16[79,360]{1,0:T(8,128)(2,1)S(1)}, bf16[79,360]{1,0:T(8,128)(2,1)S(1)}, u32[]{:S(2)}, u32[]{:S(2)}) collective-permute-start(bf16[79,360]{1,0:T(8,128)(2,1)S(1)} %get-tuple-element.249), channel_id=1, source_target_pairs={{1,0},{2,1},{3,2},{4,3},{5,4},{6,5},{7,6},{8,7},{9,8},{10,9},{11,1... | collective-permute-start | bytes 170648 | tf_op jit(solution)/shard_map/ppermute | solution.py:49
  60.4 20.1 %collective-permute-start.11 = (bf16[79,360]{1,0:T(8,128)(2,1)S(1)}, bf16[79,360]{1,0:T(8,128)(2,1)S(1)}, u32[]{:S(2)}, u32[]{:S(2)}) collective-permute-start(bf16[79,360]{1,0:T(8,128)(2,1)S(1)} %get-tuple-element.250), channel_id=1, source_target_pairs={{0,1},{1,2},{2,3},{3,4},{4,5},{5,6},{6,7},{7,8},{8,9},{9,10},{10,1... | collective-permute-start | bytes 170648 | tf_op jit(solution)/shard_map/ppermute | solution.py:49
  108.8 22.7 %collective-permute-start.16 = (bf16[4096,128]{1,0:T(8,128)(2,1)}, bf16[4096,128]{1,0:T(8,128)(2,1)S(1)}, u32[]{:S(2)}, u32[]{:S(2)}) collective-permute-start(bf16[4096,128]{1,0:T(8,128)(2,1)} %get-tuple-element.127.refs_3_), channel_id=1, source_target_pairs={{1,0},{3,1},{2,3},{6,2},{4,6},{5,4},{7,5},{11,7},{9,11},{8,9},{10,... | collective-permute-start | bytes 3145736 | tf_op jit(solution)/shard_map/ppermute | solution.py:77
  109.8 24.6 %collective-permute-start.15 = (bf16[4096,128]{1,0:T(8,128)(2,1)}, bf16[4096,128]{1,0:T(8,128)(2,1)S(1)}, u32[]{:S(2)}, u32[]{:S(2)}) collective-permute-start(bf16[4096,128]{1,0:T(8,128)(2,1)} %get-tuple-element.127.refs_3_), channel_id=1, source_target_pairs={{0,1},{1,3},{3,2},{2,6},{6,4},{4,5},{5,7},{7,11},{11,9},{9,8},{8,1... | collective-permute-start | bytes 3145736 | tf_op jit(solution)/shard_map/ppermute | solution.py:77
  159.7 25.2 %collective-permute-start.18 = (bf16[4096,128]{1,0:T(8,128)(2,1)}, bf16[4096,128]{1,0:T(8,128)(2,1)S(1)}, u32[]{:S(2)}, u32[]{:S(2)}) collective-permute-start(bf16[4096,128]{1,0:T(8,128)(2,1)} %get-tuple-element.132.refs_3_), channel_id=1, source_target_pairs={{1,0},{3,1},{2,3},{6,2},{4,6},{5,4},{7,5},{11,7},{9,11},{8,9},{10,... | collective-permute-start | bytes 3145736 | tf_op jit(solution)/shard_map/ppermute | solution.py:77
  160.4 24.6 %collective-permute-start.17 = (bf16[4096,128]{1,0:T(8,128)(2,1)}, bf16[4096,128]{1,0:T(8,128)(2,1)S(1)}, u32[]{:S(2)}, u32[]{:S(2)}) collective-permute-start(bf16[4096,128]{1,0:T(8,128)(2,1)} %get-tuple-element.132.refs_3_), channel_id=1, source_target_pairs={{0,1},{1,3},{3,2},{2,6},{6,4},{4,5},{5,7},{7,11},{11,9},{9,8},{8,1... | collective-permute-start | bytes 3145736 | tf_op jit(solution)/shard_map/ppermute | solution.py:77
  186.3 40.7 %copy-start.49 = (bf16[1,78,512]{2,1,0:T(8,128)(2,1)S(1)}, bf16[1,78,512]{2,1,0:T(8,128)(2,1)}, u32[]{:S(2)}) copy-start(bf16[1,78,512]{2,1,0:T(8,128)(2,1)} %param.17) | copy-start | bytes 239620
  213.7 13.3 %all-to-all-start.1 = ((bf16[16,64,128]{2,1,0:T(8,128)(2,1)}), bf16[16,64,128]{2,1,0:T(8,128)(2,1)S(1)}, u32[]{:S(2)}, u32[]{:S(2)}) async-start(bf16[16,64,128]{2,1,0:T(8,128)(2,1)} %bitcast.163), calls=%async_computation.1 | async-start | bytes 524288 | tf_op jit(solution)/shard_map/all_to_all | solution.py:871
  227.6 9.5 %collective-permute-start.19 = (bf16[78,360]{1,0:T(8,128)(2,1)S(1)}, bf16[78,360]{1,0:T(8,128)(2,1)S(1)}, u32[]{:S(2)}, u32[]{:S(2)}) collective-permute-start(bf16[78,360]{1,0:T(8,128)(2,1)S(1)} %get-tuple-element.251), channel_id=1, source_target_pairs={{0,1},{1,2},{2,3},{3,4},{4,5},{5,6},{6,7},{7,8},{8,9},{9,10},{10,1... | collective-permute-start | bytes 168488 | tf_op jit(solution)/shard_map/ppermute | solution.py:49
  230.9 6.1 %collective-permute-start.20 = (bf16[78,360]{1,0:T(8,128)(2,1)S(1)}, bf16[78,360]{1,0:T(8,128)(2,1)S(1)}, u32[]{:S(2)}, u32[]{:S(2)}) collective-permute-start(bf16[78,360]{1,0:T(8,128)(2,1)S(1)} %get-tuple-element.252), channel_id=1, source_target_pairs={{1,0},{2,1},{3,2},{4,3},{5,4},{6,5},{7,6},{8,7},{9,8},{10,9},{11,1... | collective-permute-start | bytes 168488 | tf_op jit(solution)/shard_map/ppermute | solution.py:49
  240.7 14.4 %all-to-all-start.2 = ((bf16[16,64,128]{2,1,0:T(8,128)(2,1)}), bf16[16,64,128]{2,1,0:T(8,128)(2,1)S(1)}, u32[]{:S(2)}, u32[]{:S(2)}) async-start(bf16[16,64,128]{2,1,0:T(8,128)(2,1)} %bitcast.18), calls=%async_computation.2 | async-start | bytes 524288 | tf_op jit(solution)/shard_map/all_to_all | solution.py:871
  255.1 36.9 %collective-permute-start.21 = (bf16[2048,256]{1,0:T(8,128)(2,1)S(1)}, bf16[2048,256]{1,0:T(8,128)(2,1)}, u32[]{:S(2)}, u32[]{:S(2)}) collective-permute-start(bf16[2048,256]{1,0:T(8,128)(2,1)S(1)} %convert_element_type.182), channel_id=1, source_target_pairs={{3,2},{2,3},{6,4},{4,5},{5,6},{11,8},{8,10},{10,11},{14,12},{15,13... | collective-permute-start | bytes 3145736 | tf_op jit(solution)/shard_map/ppermute | solution.py:902
  292.0 20.9 %collective-permute-start.22 = (bf16[4096,128]{1,0:T(8,128)(2,1)}, bf16[4096,128]{1,0:T(8,128)(2,1)}, u32[]{:S(2)}, u32[]{:S(2)}) collective-permute-start(bf16[4096,128]{1,0:T(8,128)(2,1)} %get-tuple-element.158), channel_id=1, source_target_pairs={{0,1},{1,3},{3,2},{2,6},{6,4},{4,5},{5,7},{7,11},{11,9},{9,8},{8,1... | collective-permute-start | bytes 3145736 | tf_op jit(solution)/shard_map/ppermute | solution.py:77
  293.4 19.5 %collective-permute-start.23 = (bf16[4096,128]{1,0:T(8,128)(2,1)}, bf16[4096,128]{1,0:T(8,128)(2,1)}, u32[]{:S(2)}, u32[]{:S(2)}) collective-permute-start(bf16[4096,128]{1,0:T(8,128)(2,1)} %get-tuple-element.161), channel_id=1, source_target_pairs={{1,0},{3,1},{2,3},{6,2},{4,6},{5,4},{7,5},{11,7},{9,11},{8,9},{10,... | collective-permute-start | bytes 3145736 | tf_op jit(solution)/shard_map/ppermute | solution.py:77
  339.2 20.3 %collective-permute-start.24 = (bf16[4096,128]{1,0:T(8,128)(2,1)}, bf16[4096,128]{1,0:T(8,128)(2,1)}, u32[]{:S(2)}, u32[]{:S(2)}) collective-permute-start(bf16[4096,128]{1,0:T(8,128)(2,1)} %get-tuple-element.166), channel_id=1, source_target_pairs={{0,1},{1,3},{3,2},{2,6},{6,4},{4,5},{5,7},{7,11},{11,9},{9,8},{8,1... | collective-permute-start | bytes 3145736 | tf_op jit(solution)/shard_map/ppermute | solution.py:77
  340.2 19.3 %collective-permute-start.25 = (bf16[4096,128]{1,0:T(8,128)(2,1)}, bf16[4096,128]{1,0:T(8,128)(2,1)}, u32[]{:S(2)}, u32[]{:S(2)}) collective-permute-start(bf16[4096,128]{1,0:T(8,128)(2,1)} %get-tuple-element.167), channel_id=1, source_target_pairs={{1,0},{3,1},{2,3},{6,2},{4,6},{5,4},{7,5},{11,7},{9,11},{8,9},{10,... | collective-permute-start | bytes 3145736 | tf_op jit(solution)/shard_map/ppermute | solution.py:77
  385.9 19.0 %collective-permute-start.26 = (bf16[4096,128]{1,0:T(8,128)(2,1)}, bf16[4096,128]{1,0:T(8,128)(2,1)S(1)}, u32[]{:S(2)}, u32[]{:S(2)}) collective-permute-start(bf16[4096,128]{1,0:T(8,128)(2,1)} %get-tuple-element.172), channel_id=1, source_target_pairs={{0,1},{1,3},{3,2},{2,6},{6,4},{4,5},{5,7},{7,11},{11,9},{9,8},{8,1... | collective-permute-start | bytes 3145736 | tf_op jit(solution)/shard_map/ppermute | solution.py:77
  386.0 19.0 %collective-permute-start.27 = (bf16[4096,128]{1,0:T(8,128)(2,1)}, bf16[4096,128]{1,0:T(8,128)(2,1)}, u32[]{:S(2)}, u32[]{:S(2)}) collective-permute-start(bf16[4096,128]{1,0:T(8,128)(2,1)} %get-tuple-element.173), channel_id=1, source_target_pairs={{1,0},{3,1},{2,3},{6,2},{4,6},{5,4},{7,5},{11,7},{9,11},{8,9},{10,... | collective-permute-start | bytes 3145736 | tf_op jit(solution)/shard_map/ppermute | solution.py:77
  421.1 3.1 collective-permute-start.28
  426.3 9.1 %collective-permute-start.29 = (bf16[4,2,72,256]{3,2,0,1:T(8,128)(2,1)S(1)}, bf16[4,2,72,256]{3,2,0,1:T(8,128)(2,1)S(1)}, u32[]{:S(2)}, u32[]{:S(2)}) collective-permute-start(bf16[4,2,72,256]{3,2,0,1:T(8,128)(2,1)S(1)} %fusion.18), channel_id=1, source_target_pairs={{0,1},{1,0},{2,3},{3,2},{4,5},{5,4},{6,7},{7,6},{8,9},{9,8},{10,11... | collective-permute-start | bytes 884744 | tf_op jit(solution)/shard_map/ppermute | solution.py:94
  426.5 9.2 %collective-permute-start.31 = (bf16[4,2,72,256]{3,2,1,0:T(8,128)(2,1)S(1)}, bf16[4,2,72,256]{3,2,1,0:T(8,128)(2,1)S(1)}, u32[]{:S(2)}, u32[]{:S(2)}) collective-permute-start(bf16[4,2,72,256]{3,2,1,0:T(8,128)(2,1)S(1)} %fusion.17), channel_id=1, source_target_pairs={{0,2},{1,3},{2,0},{3,1},{4,6},{5,7},{6,4},{7,5},{8,10},{9,11},{10,... | collective-permute-start | bytes 884744 | tf_op jit(solution)/shard_map/ppermute | solution.py:94
  435.6 5.2 %collective-permute-start.30 = (bf16[4,72,256]{2,1,0:T(8,128)(2,1)S(1)}, bf16[4,72,256]{2,1,0:T(8,128)(2,1)S(1)}, u32[]{:S(2)}, u32[]{:S(2)}) collective-permute-start(bf16[4,72,256]{2,1,0:T(8,128)(2,1)S(1)} %fusion.44), channel_id=1, source_target_pairs={{0,2},{1,3},{2,0},{3,1},{4,6},{5,7},{6,4},{7,5},{8,10},{9,11},{10,... | collective-permute-start | bytes 442376 | tf_op jit(solution)/shard_map/ppermute | solution.py:94
  435.8 5.2 %collective-permute-start.32 = (bf16[4,72,256]{2,1,0:T(8,128)(2,1)S(1)}, bf16[4,72,256]{2,1,0:T(8,128)(2,1)S(1)}, u32[]{:S(2)}, u32[]{:S(2)}) collective-permute-start(bf16[4,72,256]{2,1,0:T(8,128)(2,1)S(1)} %fusion.45), channel_id=1, source_target_pairs={{0,1},{1,0},{2,3},{3,2},{4,5},{5,4},{6,7},{7,6},{8,9},{9,8},{10,11... | collective-permute-start | bytes 442376 | tf_op jit(solution)/shard_map/ppermute | solution.py:94
  441.1 21.8 %collective-permute-start.40 = (bf16[2048,256]{1,0:T(8,128)(2,1)}, bf16[2048,256]{1,0:T(8,128)(2,1)}, u32[]{:S(2)}, u32[]{:S(2)}) collective-permute-start(bf16[2048,256]{1,0:T(8,128)(2,1)} %get-tuple-element.197), channel_id=1, source_target_pairs={{3,2},{2,3},{6,4},{4,5},{5,6},{11,8},{8,10},{10,11},{14,12},{15,13... | collective-permute-start | bytes 3145736 | tf_op jit(solution)/shard_map/ppermute | solution.py:902
  442.9 6.5 %collective-permute-start.33 = (bf16[1,144,256]{2,1,0:T(8,128)(2,1)S(1)}, bf16[1,144,256]{2,1,0:T(8,128)(2,1)S(1)}, u32[]{:S(2)}, u32[]{:S(2)}) collective-permute-start(bf16[1,144,256]{2,1,0:T(8,128)(2,1)S(1)} %get-tuple-element.244), channel_id=1, source_target_pairs={{0,4},{1,5},{2,6},{3,7},{4,0},{5,1},{6,2},{7,3},{8,12},{9,13},{10,... | collective-permute-start | bytes 221192 | tf_op jit(solution)/shard_map/ppermute | solution.py:94
  443.0 8.6 %collective-permute-start.35 = (bf16[1,144,256]{2,1,0:T(8,128)(2,1)S(1)}, bf16[1,144,256]{2,1,0:T(8,128)(2,1)S(1)}, u32[]{:S(2)}, u32[]{:S(2)}) collective-permute-start(bf16[1,144,256]{2,1,0:T(8,128)(2,1)S(1)} %get-tuple-element.245), channel_id=1, source_target_pairs={{0,12},{1,13},{2,14},{3,15},{4,8},{5,9},{6,10},{7,11},{8,4},{9,5},... | collective-permute-start | bytes 221192 | tf_op jit(solution)/shard_map/ppermute | solution.py:94
  447.7 6.1 %collective-permute-start.34 = (bf16[1,144,256]{2,1,0:T(8,128)(2,1)S(1)}, bf16[1,144,256]{2,1,0:T(8,128)(2,1)S(1)}, u32[]{:S(2)}, u32[]{:S(2)}) collective-permute-start(bf16[1,144,256]{2,1,0:T(8,128)(2,1)S(1)} %get-tuple-element.246), channel_id=1, source_target_pairs={{0,8},{1,9},{2,10},{3,11},{4,12},{5,13},{6,14},{7,15},{8,0},{9,1},... | collective-permute-start | bytes 221192 | tf_op jit(solution)/shard_map/ppermute | solution.py:94
  455.3 4.6 collective-permute-start.37
  455.8 5.4 %collective-permute-start.38 = (f32[8,128]{1,0:T(8,128)S(1)}, f32[8,128]{1,0:T(8,128)S(1)}, u32[]{:S(2)}, u32[]{:S(2)}) collective-permute-start(f32[8,128]{1,0:T(8,128)S(1)} %iota.23), channel_id=1, source_target_pairs={{0,12},{1,13},{2,14},{3,15},{4,8},{5,9},{6,10},{7,11},{8,4},{9,5},... | collective-permute-start | bytes 12296 | tf_op jit(solution)/shard_map/ppermute | solution.py:94
  458.0 3.6 collective-permute-start.36
  461.7 1.2 collective-permute-start.39
  462.8 10.8 %collective-permute-start.43 = (f32[8,128]{1,0:T(8,128)S(1)}, f32[8,128]{1,0:T(8,128)S(1)}, u32[]{:S(2)}, u32[]{:S(2)}) collective-permute-start(f32[8,128]{1,0:T(8,128)S(1)} %add.191), channel_id=1, source_target_pairs={{0,3},{1,2},{2,1},{3,0},{4,7},{5,6},{6,5},{7,4},{8,11},{9,10},{10,... | collective-permute-start | bytes 12296 | tf_op jit(solution)/shard_map/ppermute | solution.py:94
  468.7 4.9 %collective-permute-start.42 = (f32[8,128]{1,0:T(8,128)S(1)}, f32[8,128]{1,0:T(8,128)S(1)}, u32[]{:S(2)}, u32[]{:S(2)}) collective-permute-start(f32[8,128]{1,0:T(8,128)S(1)} %add.191), channel_id=1, source_target_pairs={{0,2},{1,3},{2,0},{3,1},{4,6},{5,7},{6,4},{7,5},{8,10},{9,11},{10,... | collective-permute-start | bytes 12296 | tf_op jit(solution)/shard_map/ppermute | solution.py:94
  468.7 4.9 %collective-permute-start.41 = (f32[8,128]{1,0:T(8,128)S(1)}, f32[8,128]{1,0:T(8,128)S(1)}, u32[]{:S(2)}, u32[]{:S(2)}) collective-permute-start(f32[8,128]{1,0:T(8,128)S(1)} %add.191), channel_id=1, source_target_pairs={{0,1},{1,0},{2,3},{3,2},{4,5},{5,4},{6,7},{7,6},{8,9},{9,8},{10,11... | collective-permute-start | bytes 12296 | tf_op jit(solution)/shard_map/ppermute | solution.py:94
  (50 other events, 434.9 us)

commit v14 on v13

--- a/solution.py
+++ b/solution.py
@@ -120,13 +120,15 @@
     return sum(others(value, "space", (1, 2)), value), arriving
 
 
-def gathered_blocks(piece, posted):
+def gathered_blocks(piece, sources, posting):
     held, weights, size = piece[None], {}, 1
     for bits in reversed(upper_groups()):
         held = jnp.concatenate([held] + others(held, "space", bits), 0)
         for n, bit in enumerate(bits):
             weights[bit] = size << n
         size = size << len(bits)
+    held, sources = lax.optimization_barrier((held, sources))
+    poster, posted = posting(*sources)
     half = piece.shape[0] // 2
     held = [held[:, :half], held[:, half:]]
     ranks = [dict(weights), dict(weights)]
@@ -137,7 +139,7 @@
             held[n] = jnp.concatenate([held[n], swapped(held[n], "space", order[turn])], 0)
             ranks[n][order[turn]] = size
         size = size << 1
-    return (held, [swapped(part, "dp", 1) for part in held], ranks), posted
+    return (held, [swapped(part, "dp", 1) for part in held], ranks), poster, posted
 
 
 def spread_rows(gathered, total, peers, place):
@@ -352,7 +354,7 @@
     def body(*refs):
         index_ref, mesh_ref, before_ref, own_ref, after_ref, mats_ref, dest_ref = refs[:7]
         self_ref, refs = refs[7], refs[:7] + refs[8:]
-        raw, table, rows, wide, sems = refs[-5:]
+        table, rows, wide = refs[-3:]
         if more:
             next_ref, sent_ref = refs[7], refs[13]
             new_ref, back_ref, update_ref, agg_ref, slope_ref = refs[8:13]
@@ -365,22 +367,16 @@
 
         @pl.when(step == 0)
         def _():
-            copies = []
             start = 0
-            for n, (source, span) in enumerate(zip((before_ref, own_ref, after_ref), spans)):
-                copies.append(
-                    pltpu.make_async_copy(source, raw.at[pl.ds(start, span)], sems.at[n])
-                )
+            for source, span in zip((before_ref, own_ref, after_ref), spans):
+
+                @pl.loop(0, span // 256)
+                def _(i, source=source, start=start):
+                    at = pl.multiple_of(i * 256, 256)
+                    to = pl.multiple_of(start + at, 256)
+                    table[pl.ds(to, 256), :] = source[pl.ds(at, 256), :].astype(jnp.float32)
+
                 start = start + span
-            for copy in copies:
-                copy.start()
-            for copy in copies:
-                copy.wait()
-
-            @pl.loop(0, reach // 256)
-            def _(i):
-                at = pl.multiple_of(i * 256, 256)
-                table[pl.ds(at, 256), :] = raw[pl.ds(at, 256), :].astype(jnp.float32)
 
         mesh_in = mesh_ref[...]
 
@@ -469,7 +465,7 @@
 
     whole_rows = pl.BlockSpec((tile, D), lambda i, *_: (i, 0))
     woven = pl.BlockSpec((2 * tile, HALF), lambda i, *_: (i, 0))
-    ins = [whole_rows] + [pl.BlockSpec(memory_space=pltpu.HBM)] * 3
+    ins = [whole_rows] + [pl.BlockSpec(memory_space=pltpu.VMEM)] * 3
     ins = ins + [whole(mats.shape), woven, whole_rows]
     outs = [whole_rows] * 4 + [pl.BlockSpec((K, 2 * tile, HALF), lambda i, *_: (0, i, 0))]
     shapes = [
@@ -503,15 +499,13 @@
             out_specs=outs,
             scratch_shapes=scratch
             + [
-                pltpu.VMEM((reach, HALF), jnp.bfloat16),
                 pltpu.VMEM((reach, HALF), jnp.float32),
                 pltpu.VMEM((K * 2 * tile, HALF), jnp.float32),
                 pltpu.VMEM((2 * tile, HALF), jnp.float32),
-                pltpu.SemaphoreType.DMA((3,)),
             ],
         ),
         out_shape=shapes,
-        compiler_params=LIMIT,
+        compiler_params=pltpu.CompilerParams(vmem_limit_bytes=40 * 2**20),
         cost_estimate=cost(25),
         name="round_forward",
     )(*args)
@@ -841,39 +835,44 @@
     )
     state_in = inputs[0]
     counted = valid[0].astype(jnp.float32)
-    local_count = jnp.sum(valid[0])
-    digits = (local_count >> jnp.array([16, 8, 0], jnp.int32)) & 255
-    digits = jnp.pad(digits, (CH + 3, HALF - CH - 6)).astype(jnp.float32)[None, :]
     points = state_in.shape[1]
     blocks = neighbours.shape[0]
     assert blocks == H
     capacity = max(2, 2 * points // bands)
-    target_band = owner[0, :, 0]
-    hits = (target_band[:, None] == jnp.arange(bands, dtype=jnp.int32)[None, :]).astype(jnp.int32)
-    ranks = jnp.sum(jnp.cumsum(hits, 0) * hits, 1) - 1
-    places_out = jnp.sum(hits * jnp.asarray(walk, jnp.int32)[None, :], 1) * capacity + ranks
-    poster = (
-        jnp.arange(bands * capacity, dtype=jnp.int32)[:, None] == places_out[None, :]
-    ).astype(jnp.bfloat16)
-    spots = slot[0][None, :]
-    columns = jnp.concatenate(
-        [
-            state_in,
-            (spots // 64).astype(jnp.bfloat16),
-            (spots % 64).astype(jnp.bfloat16),
-            jnp.ones((1, points), jnp.bfloat16),
-            jnp.zeros((HALF - CH - 3, points), jnp.bfloat16),
-        ],
-        0,
-    )
+
+    def posting(state_in, valid, owner, slot):
+        local_count = jnp.sum(valid[0])
+        digits = (local_count >> jnp.array([16, 8, 0], jnp.int32)) & 255
+        digits = jnp.pad(digits, (CH + 3, HALF - CH - 6)).astype(jnp.float32)[None, :]
+        target_band = owner[0, :, 0]
+        hits = (
+            target_band[:, None] == jnp.arange(bands, dtype=jnp.int32)[None, :]
+        ).astype(jnp.int32)
+        ranks = jnp.sum(jnp.cumsum(hits, 0) * hits, 1) - 1
+        places_out = jnp.sum(hits * jnp.asarray(walk, jnp.int32)[None, :], 1) * capacity + ranks
+        poster = (
+            jnp.arange(bands * capacity, dtype=jnp.int32)[:, None] == places_out[None, :]
+        ).astype(jnp.bfloat16)
+        spots = slot[0][None, :]
+        columns = jnp.concatenate(
+            [
+                state_in,
+                (spots // 64).astype(jnp.bfloat16),
+                (spots % 64).astype(jnp.bfloat16),
+                jnp.ones((1, points), jnp.bfloat16),
+                jnp.zeros((HALF - CH - 3, points), jnp.bfloat16),
+            ],
+            0,
+        )
+        return poster, (inner(poster, columns, 1, 1) + digits).astype(jnp.bfloat16)
 
     def exchanged(rows):
         return lax.all_to_all(
             rows.reshape(bands, capacity, HALF), "space", split_axis=0, concat_axis=0, tiled=True
         ).reshape(bands * capacity, HALF)
 
-    held, posted = gathered_blocks(
-        piece.reshape(height, D), (inner(poster, columns, 1, 1) + digits).astype(jnp.bfloat16)
+    held, poster, posted = gathered_blocks(
+        piece.reshape(height, D), (state_in, valid, owner, slot), posting
     )
     arrived = exchanged(posted)
     w_in, w_node, w_dec, w_out, *w_round, biases = spread_rows(

time: 480 us -> 504 us (1.050); the launches traced: 478 us -> 494 us
  local copies, waits for them, and re-layouts: 16.7 us -> 35.2 us
  other arithmetic: 27.4 us -> 35.8 us
  waiting for transfers between devices: 116 us -> 108 us
  Pallas kernels: 204 us -> 197 us
    unnamed x109 -> x154, local copies, waits for them, and re-layouts: 8.83 us -> 25 us
    pallas_call x3, Pallas kernels: 75.9 us -> 68.7 us  [round_forward(): pl.pallas_call(body, grid_spec=pltpu.PrefetchScalarGridSpec(num_scalar_pr...]
    ppermute x25, waiting for transfers between devices: 31.3 us -> 36.8 us  [swapped(): lax.ppermute(value, axis, [(i, i ^ bit) for i in range(lax.axis_size(axis...]
    all_to_all x3, waiting for transfers between devices: 21.5 us -> 16.1 us  [exchanged(): lax.all_to_all(rows.reshape(bands, capacity, HALF), 'space', split_axis=0...]
  transfers between devices with their start and end apart: 47 -> 47, of which waited for: 26 -> 28; matrix products, arithmetic and copies ran while one was open for 11% -> 12% of each run, Pallas kernels for 11% -> 11%
where the time goes in v14:
time: 504 us; the launch traced here: 494 us
  Pallas kernels  197 us (39%)
  waiting for transfers between devices  108 us (21%)
  starting transfers between devices  79.7 us (16%)
  other arithmetic  35.8 us (7%)
  local copies, waits for them, and re-layouts  35.2 us (7%)
  matrix products  30.3 us (6%)
  between operations  8.11 us (2%)
    pallas_call x3, Pallas kernels, edges_backward(): pl.pallas_call(body, grid_spec=pltpu.PrefetchScalarGridSpec(num_scalar_pr...  79.4 us
    pallas_call x3, Pallas kernels, round_forward(): pl.pallas_call(body, grid_spec=pltpu.PrefetchScalarGridSpec(num_scalar_pr...  68.7 us
    ppermute x25, waiting for transfers between devices, swapped(): lax.ppermute(value, axis, [(i, i ^ bit) for i in range(lax.axis_size(axis...  36.8 us
    ppermute x6, waiting for transfers between devices, halo(): lax.ppermute(initial, 'space', down)  34.6 us
    ppermute x25, starting transfers between devices, swapped(): lax.ppermute(value, axis, [(i, i ^ bit) for i in range(lax.axis_size(axis...  29.3 us
    dot_general x18, matrix products, inner(): lax.dot_general(left, right, (((left_dim,), (right_dim,)), ((), ())), pre...  29 us
    unnamed x154, local copies, waits for them, and re-layouts  25 us
    all_to_all x3, waiting for transfers between devices, exchanged(): lax.all_to_all(rows.reshape(bands, capacity, HALF), 'space', split_axis=0...  16.1 us
  transfers between devices with their start and end apart: 47, of which 28 were waited for; matrix products, arithmetic and copies ran while one was open for 12% of the time, Pallas kernels for 11%

profile of v14, /device:TPU:0, one launch (start us, length us, event | category | flops | bytes accessed | tf_op | source)
XLA Modules:
  0.0 494.3 jit_solution(11361019179881137105)
XLA Ops:
  2.5 5.1 %collective-permute-start.2 = (bf16[1,144,256]{2,1,0:T(8,128)(2,1)S(1)}, bf16[1,144,256]{2,1,0:T(8,128)(2,1)S(1)}, u32[]{:S(2)}, u32[]{:S(2)}) collective-permute-start(bf16[1,144,256]{2,1,0:T(8,128)(2,1)S(1)} %broadcast_in_dim_reshape.3), channel_id=1, source_target_pairs={{0,12},{1,13},{2,14},{3,15},{4,8},{5,9},{6,10},{7,11},{8,4},{9,5},... | collective-permute-start | bytes 221192 | tf_op jit(solution)/shard_map/ppermute | solution.py:94
  10.4 3.5 collective-permute-done.1
  29.6 5.3 %collective-permute-done.6 = bf16[8,72,256]{2,1,0:T(8,128)(2,1)S(1)} collective-permute-done((bf16[8,72,256]{2,1,0:T(8,128)(2,1)S(1)}, bf16[8,72,256]{2,1,0:T(8,128)(2,1)S(1)}, u32[]{:S(2)}, u32[]{:S(2)}) %collective-permute-start.6) | collective-permute-done | bytes 294944 | tf_op jit(solution)/shard_map/ppermute | solution.py:94
  36.3 4.0 all-to-all-start
  42.0 4.0 spread_rows.1
  46.0 4.7 all-to-all-done
  51.4 6.0 %encode_rows.1 = (f32[2048,256]{1,0:T(8,128)}, bf16[2048,256]{1,0:T(8,128)(2,1)}, bf16[4096,128]{1,0:T(8,128)(2,1)}, s32[1,1024]{1,0:T(1,128)}, s32[1024,1]{1,0:T(8,128)}) custom-call(bf16[1024,128]{1,0:T(8,128)(2,1)} %bitcast.155, bf16[128,256]{1,0:T(8,128)(2,1)} %get-tuple-element.121.in_ref, bf16[256,256]{1,0:T(8,128)(2,1)} %get-tuple-element.122.node_ref, ...), custom_call_target="tpu_custom_call" | custom-call | bytes 15000000 | tf_op jit(solution)/shard_map/encode_rows/pallas_call | solution.py:741
  66.3 5.2 %collective-permute-start.11 = (bf16[79,360]{1,0:T(8,128)(2,1)S(1)}, bf16[79,360]{1,0:T(8,128)(2,1)}, u32[]{:S(2)}, u32[]{:S(2)}) collective-permute-start(bf16[79,360]{1,0:T(8,128)(2,1)S(1)} %get-tuple-element.260), channel_id=1, source_target_pairs={{0,1},{1,2},{2,3},{3,4},{4,5},{5,6},{6,7},{7,8},{8,9},{9,10},{10,1... | collective-permute-start | bytes 170648 | tf_op jit(solution)/shard_map/ppermute | solution.py:49
  71.5 3.9 node_terms.3
  76.0 7.5 %collective-permute-done.12 = bf16[79,360]{1,0:T(8,128)(2,1)} collective-permute-done((bf16[79,360]{1,0:T(8,128)(2,1)S(1)}, bf16[79,360]{1,0:T(8,128)(2,1)}, u32[]{:S(2)}, u32[]{:S(2)}) %collective-permute-start.12) | collective-permute-done | bytes 56912 | tf_op jit(solution)/shard_map/ppermute | solution.py:49
  87.4 21.9 %round_forward.3 = (f32[2048,256]{1,0:T(8,128)S(1)}, f32[2048,256]{1,0:T(8,128)S(1)}, bf16[2048,256]{1,0:T(8,128)(2,1)S(1)}, bf16[2048,256]{1,0:T(8,128)(2,1)S(1...) custom-call(s32[12288]{0:T(1024)S(1)} %collective-permute-done.9.refs_0_, f32[2048,256]{1,0:T(8,128)S(1)} %copy-done, ...), custom_call_target="tpu_custom_call" | custom-call | bytes 75000000 | tf_op jit(solution)/shard_map/round_forward/pallas_call | solution.py:493
  116.0 3.9 node_terms.4
  119.9 16.9 %collective-permute-done.16.refs_4_ = bf16[4096,128]{1,0:T(8,128)(2,1)} collective-permute-done((bf16[4096,128]{1,0:T(8,128)(2,1)}, bf16[4096,128]{1,0:T(8,128)(2,1)}, u32[]{:S(2)}, u32[]{:S(2)}) %collective-permute-start.16) | collective-permute-done | bytes 1048608 | tf_op jit(solution)/shard_map/ppermute | solution.py:77
  136.8 4.0 collective-permute-done.15.refs_2_
  142.4 22.3 %round_forward.4 = (f32[2048,256]{1,0:T(8,128)S(1)}, f32[2048,256]{1,0:T(8,128)S(1)}, bf16[2048,256]{1,0:T(8,128)(2,1)S(1)}, bf16[2048,256]{1,0:T(8,128)(2,1)S(1...) custom-call(s32[12288]{0:T(1024)S(1)} %collective-permute-done.9.refs_0_, f32[2048,256]{1,0:T(8,128)S(1)} %copy-done.2, ...), custom_call_target="tpu_custom_call" | custom-call | bytes 75000000 | tf_op jit(solution)/shard_map/round_forward/pallas_call | solution.py:493
  173.2 3.9 node_terms.5
  177.1 17.7 %collective-permute-done.18.refs_4_ = bf16[4096,128]{1,0:T(8,128)(2,1)} collective-permute-done((bf16[4096,128]{1,0:T(8,128)(2,1)}, bf16[4096,128]{1,0:T(8,128)(2,1)}, u32[]{:S(2)}, u32[]{:S(2)}) %collective-permute-start.18) | collective-permute-done | bytes 1048608 | tf_op jit(solution)/shard_map/ppermute | solution.py:77
  194.8 24.5 %round_forward.5 = (f32[2048,256]{1,0:T(8,128)S(1)}, f32[2048,256]{1,0:T(8,128)S(1)}, bf16[2048,256]{1,0:T(8,128)(2,1)S(1)}, bf16[2048,256]{1,0:T(8,128)(2,1)S(1...) custom-call(s32[12288]{0:T(1024)S(1)} %collective-permute-done.9.ref, ...), custom_call_target="tpu_custom_call" | custom-call | bytes 75000000 | tf_op jit(solution)/shard_map/round_forward/pallas_call | solution.py:493
  227.4 5.7 %all-to-all-start.1 = ((bf16[16,64,128]{2,1,0:T(8,128)(2,1)}), bf16[16,64,128]{2,1,0:T(8,128)(2,1)S(1)}, u32[]{:S(2)}, u32[]{:S(2)}) async-start(bf16[16,64,128]{2,1,0:T(8,128)(2,1)} %bitcast.149), calls=%async_computation.1 | async-start | bytes 524288 | tf_op jit(solution)/shard_map/all_to_all | solution.py:870
  235.4 6.2 %all-to-all-done.1 = bf16[16,64,128]{2,1,0:T(8,128)(2,1)S(1)} async-done(((bf16[16,64,128]{2,1,0:T(8,128)(2,1)}), bf16[16,64,128]{2,1,0:T(8,128)(2,1)S(1)}, u32[]{:S(2)}, u32[]{:S(2)}) %all-to-all-start.1) | async-done | bytes 262176 | tf_op jit(solution)/shard_map/all_to_all | solution.py:870
  243.1 3.5 collective-permute-start.19
  257.9 5.9 %all-to-all-start.2 = ((bf16[16,64,128]{2,1,0:T(8,128)(2,1)}), bf16[16,64,128]{2,1,0:T(8,128)(2,1)S(1)}, u32[]{:S(2)}, u32[]{:S(2)}) async-start(bf16[16,64,128]{2,1,0:T(8,128)(2,1)} %bitcast.18), calls=%async_computation.2 | async-start | bytes 524288 | tf_op jit(solution)/shard_map/all_to_all | solution.py:870
  264.4 2.7 convert_element_type.182
  267.1 5.2 %all-to-all-done.2 = bf16[16,64,128]{2,1,0:T(8,128)(2,1)S(1)} async-done(((bf16[16,64,128]{2,1,0:T(8,128)(2,1)}), bf16[16,64,128]{2,1,0:T(8,128)(2,1)S(1)}, u32[]{:S(2)}, u32[]{:S(2)}) %all-to-all-start.2) | async-done | bytes 262176 | tf_op jit(solution)/shard_map/all_to_all | solution.py:870
  273.9 26.7 %edges_backward.3 = (f32[2048,256]{1,0:T(8,128)}, bf16[2048,256]{1,0:T(8,128)(2,1)}, bf16[1024,256]{1,0:T(8,128)(2,1)}, bf16[2048,256]{1,0:T(8,128)(2,1)}, bf16[...) custom-call(s32[12288]{0:T(1024)} %copy-done.19, ...), custom_call_target="tpu_custom_call" | custom-call | bytes 75000000 | tf_op jit(solution)/shard_map/edges_backward/pallas_call | solution.py:634
  305.4 2.4 fusion.95.refs_18_
  310.4 2.5 collective-permute-start.23
  314.7 4.0 carried_terms.3.refs_4_
  319.4 2.8 fusion.65.refs_17_
  322.2 3.5 convert_select_fusion
  325.7 4.2 collective-permute-done.22.refs_6_
  329.9 26.3 %edges_backward.4 = (f32[2048,256]{1,0:T(8,128)}, bf16[2048,256]{1,0:T(8,128)(2,1)}, bf16[2048,256]{1,0:T(8,128)(2,1)}, bf16[2048,256]{1,0:T(8,128)(2,1)}, bf16[...) custom-call(s32[12288]{0:T(1024)} %copy-done.19, ...), custom_call_target="tpu_custom_call" | custom-call | bytes 84000000 | tf_op jit(solution)/shard_map/edges_backward/pallas_call | solution.py:634
  357.2 2.9 collective-permute-start.25
  360.2 2.4 fusion.92.refs_11_
  363.7 3.9 carried_terms.4.refs_4_
  370.0 2.4 fusion.73.refs_10_
  376.3 26.3 %edges_backward.5 = (f32[2048,256]{1,0:T(8,128)}, bf16[2048,256]{1,0:T(8,128)(2,1)}, bf16[2048,256]{1,0:T(8,128)(2,1)}, bf16[2048,256]{1,0:T(8,128)(2,1)}, bf16[...) custom-call(s32[12288]{0:T(1024)} %copy-done.19, ...), custom_call_target="tpu_custom_call" | custom-call | bytes 84000000 | tf_op jit(solution)/shard_map/edges_backward/pallas_call | solution.py:634
  402.7 4.0 collective-permute-start.27
  406.7 2.4 fusion.90.refs_6_
  410.3 3.9 carried_terms.5.part_ref
  421.8 10.1 %encode_backward.1 = (f32[2048,256]{1,0:T(8,128)}, bf16[2048,256]{1,0:T(8,128)(2,1)}, f32[128,256]{1,0:T(8,128)}, f32[256,256]{1,0:T(8,128)}, f32[2,256]{1,0:T(2,128)}, /*index=5*/f32[256,256]{1,0:T(8,128)}) custom-call(f32[2048,256]{1,0:T(8,128)} %carried_terms.5.part_ref, f32[4096,128]{1,0:T(8,128)} %get-tuple-element.181.own_ref, ...), custom_call_target="tpu_custom_call" | custom-call | bytes 30000000 | tf_op jit(solution)/shard_map/encode_backward/pallas_call | solution.py:806
  431.9 5.1 %collect_rows.1 = (f32[16,144,256]{2,1,0:T(8,128)}, bf16[16,144,256]{2,1,0:T(8,128)(2,1)}) custom-call(s32[1]{0:T(128)} %bitcast.6.place_ref, f32[128,256]{1,0:T(8,128)} %get-tuple-element.185.refs_0_, f32[256,256]{1,0:T(8,128)} %get-tuple-element.186.refs_1_, f32[256,256]{1,0:T(8,128)} %fusion.89.refs_2_, f32[78,256]{1,0:T(8,128)} %reshape.155.refs_3_, ...), custom_call_target="tpu_custom_call" | custom-call | bytes 15000000 | tf_op jit(solution)/shard_map/collect_rows/pallas_call | solution.py:235
  437.1 3.0 collective-permute-done.28
  442.4 8.9 %collective-permute-done.29 = bf16[4,2,72,256]{3,2,0,1:T(8,128)(2,1)S(1)} collective-permute-done((bf16[4,2,72,256]{3,2,0,1:T(8,128)(2,1)S(1)}, bf16[4,2,72,256]{3,2,0,1:T(8,128)(2,1)S(1)}, u32[]{:S(2)}, u32[]{:S(2)}) %collective-permute-start.29) | collective-permute-done | bytes 294944 | tf_op jit(solution)/shard_map/ppermute | solution.py:94
  453.4 3.3 collective-permute-done.30
  458.9 5.8 %collective-permute-start.35 = (bf16[1,144,256]{2,1,0:T(8,128)(2,1)S(1)}, bf16[1,144,256]{2,1,0:T(8,128)(2,1)S(1)}, u32[]{:S(2)}, u32[]{:S(2)}) collective-permute-start(bf16[1,144,256]{2,1,0:T(8,128)(2,1)S(1)} %get-tuple-element.255), channel_id=1, source_target_pairs={{0,12},{1,13},{2,14},{3,15},{4,8},{5,9},{6,10},{7,11},{8,4},{9,5},... | collective-permute-start | bytes 221192 | tf_op jit(solution)/shard_map/ppermute | solution.py:94
  479.8 4.7 collective-permute-start.43
  486.0 3.4 select_bitcast_fusion
  (314 shorter events, 127.5 us)
Async XLA Ops:
  2.5 7.9 %collective-permute-start.2 = (bf16[1,144,256]{2,1,0:T(8,128)(2,1)S(1)}, bf16[1,144,256]{2,1,0:T(8,128)(2,1)S(1)}, u32[]{:S(2)}, u32[]{:S(2)}) collective-permute-start(bf16[1,144,256]{2,1,0:T(8,128)(2,1)S(1)} %broadcast_in_dim_reshape.3), channel_id=1, source_target_pairs={{0,12},{1,13},{2,14},{3,15},{4,8},{5,9},{6,10},{7,11},{8,4},{9,5},... | collective-permute-start | bytes 221192 | tf_op jit(solution)/shard_map/ppermute | solution.py:94
  7.7 6.2 %collective-permute-start.1 = (bf16[1,144,256]{2,1,0:T(8,128)(2,1)S(1)}, bf16[1,144,256]{2,1,0:T(8,128)(2,1)S(1)}, u32[]{:S(2)}, u32[]{:S(2)}) collective-permute-start(bf16[1,144,256]{2,1,0:T(8,128)(2,1)S(1)} %broadcast_in_dim_reshape.3), channel_id=1, source_target_pairs={{0,8},{1,9},{2,10},{3,11},{4,12},{5,13},{6,14},{7,15},{8,0},{9,1},... | collective-permute-start | bytes 221192 | tf_op jit(solution)/shard_map/ppermute | solution.py:94
  7.7 6.2 %collective-permute-start = (bf16[1,144,256]{2,1,0:T(8,128)(2,1)S(1)}, bf16[1,144,256]{2,1,0:T(8,128)(2,1)S(1)}, u32[]{:S(2)}, u32[]{:S(2)}) collective-permute-start(bf16[1,144,256]{2,1,0:T(8,128)(2,1)S(1)} %broadcast_in_dim_reshape.3), channel_id=1, source_target_pairs={{0,4},{1,5},{2,6},{3,7},{4,0},{5,1},{6,2},{7,3},{8,12},{9,13},{10,... | collective-permute-start | bytes 221192 | tf_op jit(solution)/shard_map/ppermute | solution.py:94
  20.7 5.2 %collective-permute-start.4 = (bf16[4,72,256]{2,1,0:T(8,128)(2,1)S(1)}, bf16[4,72,256]{2,1,0:T(8,128)(2,1)S(1)}, u32[]{:S(2)}, u32[]{:S(2)}) collective-permute-start(bf16[4,72,256]{2,1,0:T(8,128)(2,1)S(1)} %get-tuple-element.257), channel_id=1, source_target_pairs={{0,1},{1,0},{2,3},{3,2},{4,5},{5,4},{6,7},{7,6},{8,9},{9,8},{10,11... | collective-permute-start | bytes 442376 | tf_op jit(solution)/shard_map/ppermute | solution.py:94
  22.2 5.1 %collective-permute-start.3 = (bf16[4,72,256]{2,1,0:T(8,128)(2,1)S(1)}, bf16[4,72,256]{2,1,0:T(8,128)(2,1)S(1)}, u32[]{:S(2)}, u32[]{:S(2)}) collective-permute-start(bf16[4,72,256]{2,1,0:T(8,128)(2,1)S(1)} %get-tuple-element.258), channel_id=1, source_target_pairs={{0,2},{1,3},{2,0},{3,1},{4,6},{5,7},{6,4},{7,5},{8,10},{9,11},{10,... | collective-permute-start | bytes 442376 | tf_op jit(solution)/shard_map/ppermute | solution.py:94
  27.4 7.5 %collective-permute-start.6 = (bf16[8,72,256]{2,1,0:T(8,128)(2,1)S(1)}, bf16[8,72,256]{2,1,0:T(8,128)(2,1)S(1)}, u32[]{:S(2)}, u32[]{:S(2)}) collective-permute-start(bf16[8,72,256]{2,1,0:T(8,128)(2,1)S(1)} %pad_maximum_fusion.4), channel_id=1, source_target_pairs={{0,2},{1,3},{2,0},{3,1},{4,6},{5,7},{6,4},{7,5},{8,10},{9,11},{10,... | collective-permute-start | bytes 884744 | tf_op jit(solution)/shard_map/ppermute | solution.py:94
  29.0 7.2 %collective-permute-start.5 = (bf16[8,72,256]{2,1,0:T(8,128)(2,1)S(1)}, bf16[8,72,256]{2,1,0:T(8,128)(2,1)S(1)}, u32[]{:S(2)}, u32[]{:S(2)}) collective-permute-start(bf16[8,72,256]{2,1,0:T(8,128)(2,1)S(1)} %pad_maximum_fusion.3), channel_id=1, source_target_pairs={{0,1},{1,0},{2,3},{3,2},{4,5},{5,4},{6,7},{7,6},{8,9},{9,8},{10,11... | collective-permute-start | bytes 884744 | tf_op jit(solution)/shard_map/ppermute | solution.py:94
  35.0 6.0 %collective-permute-start.8 = (bf16[16,72,256]{2,1,0:T(8,128)(2,1)S(1)}, bf16[16,72,256]{2,1,0:T(8,128)(2,1)S(1)}, u32[]{:S(2)}, u32[]{:S(2)}) collective-permute-start(bf16[16,72,256]{2,1,0:T(8,128)(2,1)S(1)} %constant_dynamic-update-slice_fusion.2.refs_1_), channel_id=1, source_target_pairs={{0,16},{16,0},{1,17},{17,1},{2,18},{18,2},{3,19},{19,3},{4,20},{20... | collective-permute-start | bytes 1769480 | tf_op jit(solution)/shard_map/ppermute | solution.py:94
  36.2 4.8 collective-permute-start.7
  36.3 14.4 %all-to-all-start = ((bf16[16,64,128]{2,1,0:T(8,128)(2,1)}), bf16[16,64,128]{2,1,0:T(8,128)(2,1)S(1)}, u32[]{:S(2)}, u32[]{:S(2)}) async-start(bf16[16,64,128]{2,1,0:T(8,128)(2,1)} %bitcast.4), calls=%async_computation | async-start | bytes 524288 | tf_op jit(solution)/shard_map/all_to_all | solution.py:870
  57.5 28.7 %collective-permute-start.14 = (bf16[4096,128]{1,0:T(8,128)(2,1)}, bf16[4096,128]{1,0:T(8,128)(2,1)}, u32[]{:S(2)}, u32[]{:S(2)}) collective-permute-start(bf16[4096,128]{1,0:T(8,128)(2,1)} %get-tuple-element.129.refs_3_), channel_id=1, source_target_pairs={{1,0},{3,1},{2,3},{6,2},{4,6},{5,4},{7,5},{11,7},{9,11},{8,9},{10,... | collective-permute-start | bytes 3145736 | tf_op jit(solution)/shard_map/ppermute | solution.py:77
  59.2 26.9 %collective-permute-start.10 = (bf16[4096,128]{1,0:T(8,128)(2,1)}, bf16[4096,128]{1,0:T(8,128)(2,1)}, u32[]{:S(2)}, u32[]{:S(2)}) collective-permute-start(bf16[4096,128]{1,0:T(8,128)(2,1)} %get-tuple-element.129.refs_3_), channel_id=1, source_target_pairs={{0,1},{1,3},{3,2},{2,6},{6,4},{4,5},{5,7},{7,11},{11,9},{9,8},{8,1... | collective-permute-start | bytes 3145736 | tf_op jit(solution)/shard_map/ppermute | solution.py:77
  59.6 6.8 %collective-permute-start.13 = (f32[1,3]{1,0:T(1,128)S(1)}, f32[1,3]{1,0:T(1,128)S(1)}, u32[]{:S(2)}, u32[]{:S(2)}) collective-permute-start(f32[1,3]{1,0:T(1,128)S(1)} %bitcast.174), channel_id=1, source_target_pairs={{0,16},{16,0},{1,17},{17,1},{2,18},{18,2},{3,19},{19,3},{4,20},{20... | collective-permute-start | bytes 44 | tf_op jit(solution)/shard_map/ppermute | solution.py:94
  61.2 25.0 %collective-permute-start.9 = (s32[12288]{0:T(1024)}, s32[12288]{0:T(1024)S(1)}, u32[]{:S(2)}, u32[]{:S(2)}) collective-permute-start(s32[12288]{0:T(1024)} %mul.177), channel_id=1, source_target_pairs={{0,0},{1,1},{2,3},{3,2},{4,6},{5,4},{6,5},{7,7},{8,11},{9,9},{10,8... | collective-permute-start | bytes 147464 | tf_op jit(solution)/shard_map/ppermute | solution.py:898
  63.6 19.8 %collective-permute-start.12 = (bf16[79,360]{1,0:T(8,128)(2,1)S(1)}, bf16[79,360]{1,0:T(8,128)(2,1)}, u32[]{:S(2)}, u32[]{:S(2)}) collective-permute-start(bf16[79,360]{1,0:T(8,128)(2,1)S(1)} %get-tuple-element.259), channel_id=1, source_target_pairs={{1,0},{2,1},{3,2},{4,3},{5,4},{6,5},{7,6},{8,7},{9,8},{10,9},{11,1... | collective-permute-start | bytes 170648 | tf_op jit(solution)/shard_map/ppermute | solution.py:49
  66.3 17.1 %collective-permute-start.11 = (bf16[79,360]{1,0:T(8,128)(2,1)S(1)}, bf16[79,360]{1,0:T(8,128)(2,1)}, u32[]{:S(2)}, u32[]{:S(2)}) collective-permute-start(bf16[79,360]{1,0:T(8,128)(2,1)S(1)} %get-tuple-element.260), channel_id=1, source_target_pairs={{0,1},{1,2},{2,3},{3,4},{4,5},{5,6},{6,7},{7,8},{8,9},{9,10},{10,1... | collective-permute-start | bytes 170648 | tf_op jit(solution)/shard_map/ppermute | solution.py:49
  86.2 108.6 %copy-start.19 = (s32[12288]{0:T(1024)}, s32[12288]{0:T(1024)S(1)}, u32[]{:S(2)}) copy-start(s32[12288]{0:T(1024)S(1)} %collective-permute-done.9.refs_0_) | copy-start | bytes 147460
  114.0 22.8 %collective-permute-start.16 = (bf16[4096,128]{1,0:T(8,128)(2,1)}, bf16[4096,128]{1,0:T(8,128)(2,1)}, u32[]{:S(2)}, u32[]{:S(2)}) collective-permute-start(bf16[4096,128]{1,0:T(8,128)(2,1)} %get-tuple-element.137.refs_3_), channel_id=1, source_target_pairs={{1,0},{3,1},{2,3},{6,2},{4,6},{5,4},{7,5},{11,7},{9,11},{8,9},{10,... | collective-permute-start | bytes 3145736 | tf_op jit(solution)/shard_map/ppermute | solution.py:77
  115.8 25.0 %collective-permute-start.15 = (bf16[4096,128]{1,0:T(8,128)(2,1)}, bf16[4096,128]{1,0:T(8,128)(2,1)}, u32[]{:S(2)}, u32[]{:S(2)}) collective-permute-start(bf16[4096,128]{1,0:T(8,128)(2,1)} %get-tuple-element.137.refs_3_), channel_id=1, source_target_pairs={{0,1},{1,3},{3,2},{2,6},{6,4},{4,5},{5,7},{7,11},{11,9},{9,8},{8,1... | collective-permute-start | bytes 3145736 | tf_op jit(solution)/shard_map/ppermute | solution.py:77
  169.4 25.4 %collective-permute-start.18 = (bf16[4096,128]{1,0:T(8,128)(2,1)}, bf16[4096,128]{1,0:T(8,128)(2,1)}, u32[]{:S(2)}, u32[]{:S(2)}) collective-permute-start(bf16[4096,128]{1,0:T(8,128)(2,1)} %get-tuple-element.142.refs_3_), channel_id=1, source_target_pairs={{1,0},{3,1},{2,3},{6,2},{4,6},{5,4},{7,5},{11,7},{9,11},{8,9},{10,... | collective-permute-start | bytes 3145736 | tf_op jit(solution)/shard_map/ppermute | solution.py:77
  170.2 24.6 %collective-permute-start.17 = (bf16[4096,128]{1,0:T(8,128)(2,1)}, bf16[4096,128]{1,0:T(8,128)(2,1)}, u32[]{:S(2)}, u32[]{:S(2)}) collective-permute-start(bf16[4096,128]{1,0:T(8,128)(2,1)} %get-tuple-element.142.refs_3_), channel_id=1, source_target_pairs={{0,1},{1,3},{3,2},{2,6},{6,4},{4,5},{5,7},{7,11},{11,9},{9,8},{8,1... | collective-permute-start | bytes 3145736 | tf_op jit(solution)/shard_map/ppermute | solution.py:77
  227.4 14.2 %all-to-all-start.1 = ((bf16[16,64,128]{2,1,0:T(8,128)(2,1)}), bf16[16,64,128]{2,1,0:T(8,128)(2,1)S(1)}, u32[]{:S(2)}, u32[]{:S(2)}) async-start(bf16[16,64,128]{2,1,0:T(8,128)(2,1)} %bitcast.149), calls=%async_computation.1 | async-start | bytes 524288 | tf_op jit(solution)/shard_map/all_to_all | solution.py:870
  243.1 10.2 %collective-permute-start.19 = (bf16[78,360]{1,0:T(8,128)(2,1)S(1)}, bf16[78,360]{1,0:T(8,128)(2,1)S(1)}, u32[]{:S(2)}, u32[]{:S(2)}) collective-permute-start(bf16[78,360]{1,0:T(8,128)(2,1)S(1)} %get-tuple-element.261), channel_id=1, source_target_pairs={{0,1},{1,2},{2,3},{3,4},{4,5},{5,6},{6,7},{7,8},{8,9},{9,10},{10,1... | collective-permute-start | bytes 168488 | tf_op jit(solution)/shard_map/ppermute | solution.py:49
  246.6 6.1 %collective-permute-start.20 = (bf16[78,360]{1,0:T(8,128)(2,1)S(1)}, bf16[78,360]{1,0:T(8,128)(2,1)S(1)}, u32[]{:S(2)}, u32[]{:S(2)}) collective-permute-start(bf16[78,360]{1,0:T(8,128)(2,1)S(1)} %get-tuple-element.262), channel_id=1, source_target_pairs={{1,0},{2,1},{3,2},{4,3},{5,4},{6,5},{7,6},{8,7},{9,8},{10,9},{11,1... | collective-permute-start | bytes 168488 | tf_op jit(solution)/shard_map/ppermute | solution.py:49
  257.9 14.4 %all-to-all-start.2 = ((bf16[16,64,128]{2,1,0:T(8,128)(2,1)}), bf16[16,64,128]{2,1,0:T(8,128)(2,1)S(1)}, u32[]{:S(2)}, u32[]{:S(2)}) async-start(bf16[16,64,128]{2,1,0:T(8,128)(2,1)} %bitcast.18), calls=%async_computation.2 | async-start | bytes 524288 | tf_op jit(solution)/shard_map/all_to_all | solution.py:870
  272.3 36.7 %collective-permute-start.21 = (bf16[2048,256]{1,0:T(8,128)(2,1)}, bf16[2048,256]{1,0:T(8,128)(2,1)}, u32[]{:S(2)}, u32[]{:S(2)}) collective-permute-start(bf16[2048,256]{1,0:T(8,128)(2,1)} %convert_element_type.182), channel_id=1, source_target_pairs={{3,2},{2,3},{6,4},{4,5},{5,6},{11,8},{8,10},{10,11},{14,12},{15,13... | collective-permute-start | bytes 3145736 | tf_op jit(solution)/shard_map/ppermute | solution.py:901
  309.0 20.9 %collective-permute-start.22 = (bf16[4096,128]{1,0:T(8,128)(2,1)}, bf16[4096,128]{1,0:T(8,128)(2,1)}, u32[]{:S(2)}, u32[]{:S(2)}) collective-permute-start(bf16[4096,128]{1,0:T(8,128)(2,1)} %get-tuple-element.168), channel_id=1, source_target_pairs={{0,1},{1,3},{3,2},{2,6},{6,4},{4,5},{5,7},{7,11},{11,9},{9,8},{8,1... | collective-permute-start | bytes 3145736 | tf_op jit(solution)/shard_map/ppermute | solution.py:77
  310.4 19.5 %collective-permute-start.23 = (bf16[4096,128]{1,0:T(8,128)(2,1)}, bf16[4096,128]{1,0:T(8,128)(2,1)}, u32[]{:S(2)}, u32[]{:S(2)}) collective-permute-start(bf16[4096,128]{1,0:T(8,128)(2,1)} %get-tuple-element.171), channel_id=1, source_target_pairs={{1,0},{3,1},{2,3},{6,2},{4,6},{5,4},{7,5},{11,7},{9,11},{8,9},{10,... | collective-permute-start | bytes 3145736 | tf_op jit(solution)/shard_map/ppermute | solution.py:77
  356.3 20.0 %collective-permute-start.24 = (bf16[4096,128]{1,0:T(8,128)(2,1)}, bf16[4096,128]{1,0:T(8,128)(2,1)}, u32[]{:S(2)}, u32[]{:S(2)}) collective-permute-start(bf16[4096,128]{1,0:T(8,128)(2,1)} %get-tuple-element.176), channel_id=1, source_target_pairs={{0,1},{1,3},{3,2},{2,6},{6,4},{4,5},{5,7},{7,11},{11,9},{9,8},{8,1... | collective-permute-start | bytes 3145736 | tf_op jit(solution)/shard_map/ppermute | solution.py:77
  357.2 19.1 %collective-permute-start.25 = (bf16[4096,128]{1,0:T(8,128)(2,1)}, bf16[4096,128]{1,0:T(8,128)(2,1)}, u32[]{:S(2)}, u32[]{:S(2)}) collective-permute-start(bf16[4096,128]{1,0:T(8,128)(2,1)} %get-tuple-element.177), channel_id=1, source_target_pairs={{1,0},{3,1},{2,3},{6,2},{4,6},{5,4},{7,5},{11,7},{9,11},{8,9},{10,... | collective-permute-start | bytes 3145736 | tf_op jit(solution)/shard_map/ppermute | solution.py:77
  402.7 19.1 %collective-permute-start.26 = (bf16[4096,128]{1,0:T(8,128)(2,1)}, bf16[4096,128]{1,0:T(8,128)(2,1)}, u32[]{:S(2)}, u32[]{:S(2)}) collective-permute-start(bf16[4096,128]{1,0:T(8,128)(2,1)} %get-tuple-element.182), channel_id=1, source_target_pairs={{0,1},{1,3},{3,2},{2,6},{6,4},{4,5},{5,7},{7,11},{11,9},{9,8},{8,1... | collective-permute-start | bytes 3145736 | tf_op jit(solution)/shard_map/ppermute | solution.py:77
  402.7 19.1 %collective-permute-start.27 = (bf16[4096,128]{1,0:T(8,128)(2,1)}, bf16[4096,128]{1,0:T(8,128)(2,1)}, u32[]{:S(2)}, u32[]{:S(2)}) collective-permute-start(bf16[4096,128]{1,0:T(8,128)(2,1)} %get-tuple-element.183), channel_id=1, source_target_pairs={{1,0},{3,1},{2,3},{6,2},{4,6},{5,4},{7,5},{11,7},{9,11},{8,9},{10,... | collective-permute-start | bytes 3145736 | tf_op jit(solution)/shard_map/ppermute | solution.py:77
  437.0 3.1 collective-permute-start.28
  442.2 9.1 %collective-permute-start.29 = (bf16[4,2,72,256]{3,2,0,1:T(8,128)(2,1)S(1)}, bf16[4,2,72,256]{3,2,0,1:T(8,128)(2,1)S(1)}, u32[]{:S(2)}, u32[]{:S(2)}) collective-permute-start(bf16[4,2,72,256]{3,2,0,1:T(8,128)(2,1)S(1)} %fusion.18), channel_id=1, source_target_pairs={{0,1},{1,0},{2,3},{3,2},{4,5},{5,4},{6,7},{7,6},{8,9},{9,8},{10,11... | collective-permute-start | bytes 884744 | tf_op jit(solution)/shard_map/ppermute | solution.py:94
  442.4 9.2 %collective-permute-start.31 = (bf16[4,2,72,256]{3,2,1,0:T(8,128)(2,1)S(1)}, bf16[4,2,72,256]{3,2,1,0:T(8,128)(2,1)S(1)}, u32[]{:S(2)}, u32[]{:S(2)}) collective-permute-start(bf16[4,2,72,256]{3,2,1,0:T(8,128)(2,1)S(1)} %fusion.17), channel_id=1, source_target_pairs={{0,2},{1,3},{2,0},{3,1},{4,6},{5,7},{6,4},{7,5},{8,10},{9,11},{10,... | collective-permute-start | bytes 884744 | tf_op jit(solution)/shard_map/ppermute | solution.py:94
  451.5 5.2 %collective-permute-start.30 = (bf16[4,72,256]{2,1,0:T(8,128)(2,1)S(1)}, bf16[4,72,256]{2,1,0:T(8,128)(2,1)S(1)}, u32[]{:S(2)}, u32[]{:S(2)}) collective-permute-start(bf16[4,72,256]{2,1,0:T(8,128)(2,1)S(1)} %fusion.44), channel_id=1, source_target_pairs={{0,2},{1,3},{2,0},{3,1},{4,6},{5,7},{6,4},{7,5},{8,10},{9,11},{10,... | collective-permute-start | bytes 442376 | tf_op jit(solution)/shard_map/ppermute | solution.py:94
  451.7 5.2 %collective-permute-start.32 = (bf16[4,72,256]{2,1,0:T(8,128)(2,1)S(1)}, bf16[4,72,256]{2,1,0:T(8,128)(2,1)S(1)}, u32[]{:S(2)}, u32[]{:S(2)}) collective-permute-start(bf16[4,72,256]{2,1,0:T(8,128)(2,1)S(1)} %fusion.45), channel_id=1, source_target_pairs={{0,1},{1,0},{2,3},{3,2},{4,5},{5,4},{6,7},{7,6},{8,9},{9,8},{10,11... | collective-permute-start | bytes 442376 | tf_op jit(solution)/shard_map/ppermute | solution.py:94
  457.0 22.8 %collective-permute-start.40 = (bf16[2048,256]{1,0:T(8,128)(2,1)}, bf16[2048,256]{1,0:T(8,128)(2,1)}, u32[]{:S(2)}, u32[]{:S(2)}) collective-permute-start(bf16[2048,256]{1,0:T(8,128)(2,1)} %get-tuple-element.207), channel_id=1, source_target_pairs={{3,2},{2,3},{6,4},{4,5},{5,6},{11,8},{8,10},{10,11},{14,12},{15,13... | collective-permute-start | bytes 3145736 | tf_op jit(solution)/shard_map/ppermute | solution.py:901
  458.8 7.7 %collective-permute-start.33 = (bf16[1,144,256]{2,1,0:T(8,128)(2,1)S(1)}, bf16[1,144,256]{2,1,0:T(8,128)(2,1)S(1)}, u32[]{:S(2)}, u32[]{:S(2)}) collective-permute-start(bf16[1,144,256]{2,1,0:T(8,128)(2,1)S(1)} %get-tuple-element.254), channel_id=1, source_target_pairs={{0,4},{1,5},{2,6},{3,7},{4,0},{5,1},{6,2},{7,3},{8,12},{9,13},{10,... | collective-permute-start | bytes 221192 | tf_op jit(solution)/shard_map/ppermute | solution.py:94
  458.9 9.7 %collective-permute-start.35 = (bf16[1,144,256]{2,1,0:T(8,128)(2,1)S(1)}, bf16[1,144,256]{2,1,0:T(8,128)(2,1)S(1)}, u32[]{:S(2)}, u32[]{:S(2)}) collective-permute-start(bf16[1,144,256]{2,1,0:T(8,128)(2,1)S(1)} %get-tuple-element.255), channel_id=1, source_target_pairs={{0,12},{1,13},{2,14},{3,15},{4,8},{5,9},{6,10},{7,11},{8,4},{9,5},... | collective-permute-start | bytes 221192 | tf_op jit(solution)/shard_map/ppermute | solution.py:94
  464.7 6.1 %collective-permute-start.34 = (bf16[1,144,256]{2,1,0:T(8,128)(2,1)S(1)}, bf16[1,144,256]{2,1,0:T(8,128)(2,1)S(1)}, u32[]{:S(2)}, u32[]{:S(2)}) collective-permute-start(bf16[1,144,256]{2,1,0:T(8,128)(2,1)S(1)} %get-tuple-element.256), channel_id=1, source_target_pairs={{0,8},{1,9},{2,10},{3,11},{4,12},{5,13},{6,14},{7,15},{8,0},{9,1},... | collective-permute-start | bytes 221192 | tf_op jit(solution)/shard_map/ppermute | solution.py:94
  472.3 4.6 collective-permute-start.37
  472.7 5.4 %collective-permute-start.38 = (f32[8,128]{1,0:T(8,128)S(1)}, f32[8,128]{1,0:T(8,128)S(1)}, u32[]{:S(2)}, u32[]{:S(2)}) collective-permute-start(f32[8,128]{1,0:T(8,128)S(1)} %iota.23), channel_id=1, source_target_pairs={{0,12},{1,13},{2,14},{3,15},{4,8},{5,9},{6,10},{7,11},{8,4},{9,5},... | collective-permute-start | bytes 12296 | tf_op jit(solution)/shard_map/ppermute | solution.py:94
  475.0 3.6 collective-permute-start.36
  478.6 1.2 collective-permute-start.39
  479.8 9.7 %collective-permute-start.43 = (f32[8,128]{1,0:T(8,128)S(1)}, f32[8,128]{1,0:T(8,128)S(1)}, u32[]{:S(2)}, u32[]{:S(2)}) collective-permute-start(f32[8,128]{1,0:T(8,128)S(1)} %add.191), channel_id=1, source_target_pairs={{0,3},{1,2},{2,1},{3,0},{4,7},{5,6},{6,5},{7,4},{8,11},{9,10},{10,... | collective-permute-start | bytes 12296 | tf_op jit(solution)/shard_map/ppermute | solution.py:94
  484.5 4.9 collective-permute-start.42
  484.5 4.9 collective-permute-start.41
  (74 other events, 768.9 us)

commit v15 on v13

--- a/solution.py
+++ b/solution.py
@@ -352,7 +352,7 @@
     def body(*refs):
         index_ref, mesh_ref, before_ref, own_ref, after_ref, mats_ref, dest_ref = refs[:7]
         self_ref, refs = refs[7], refs[:7] + refs[8:]
-        raw, table, rows, wide, sems = refs[-5:]
+        table, rows, wide = refs[-3:]
         if more:
             next_ref, sent_ref = refs[7], refs[13]
             new_ref, back_ref, update_ref, agg_ref, slope_ref = refs[8:13]
@@ -365,22 +365,16 @@
 
         @pl.when(step == 0)
         def _():
-            copies = []
             start = 0
-            for n, (source, span) in enumerate(zip((before_ref, own_ref, after_ref), spans)):
-                copies.append(
-                    pltpu.make_async_copy(source, raw.at[pl.ds(start, span)], sems.at[n])
-                )
+            for source, span in zip((before_ref, own_ref, after_ref), spans):
+
+                @pl.loop(0, span // 256)
+                def _(i, source=source, start=start):
+                    at = pl.multiple_of(i * 256, 256)
+                    to = pl.multiple_of(start + at, 256)
+                    table[pl.ds(to, 256), :] = source[pl.ds(at, 256), :].astype(jnp.float32)
+
                 start = start + span
-            for copy in copies:
-                copy.start()
-            for copy in copies:
-                copy.wait()
-
-            @pl.loop(0, reach // 256)
-            def _(i):
-                at = pl.multiple_of(i * 256, 256)
-                table[pl.ds(at, 256), :] = raw[pl.ds(at, 256), :].astype(jnp.float32)
 
         mesh_in = mesh_ref[...]
 
@@ -469,7 +463,7 @@
 
     whole_rows = pl.BlockSpec((tile, D), lambda i, *_: (i, 0))
     woven = pl.BlockSpec((2 * tile, HALF), lambda i, *_: (i, 0))
-    ins = [whole_rows] + [pl.BlockSpec(memory_space=pltpu.HBM)] * 3
+    ins = [whole_rows] + [pl.BlockSpec(memory_space=pltpu.VMEM)] * 3
     ins = ins + [whole(mats.shape), woven, whole_rows]
     outs = [whole_rows] * 4 + [pl.BlockSpec((K, 2 * tile, HALF), lambda i, *_: (0, i, 0))]
     shapes = [
@@ -503,15 +497,13 @@
             out_specs=outs,
             scratch_shapes=scratch
             + [
-                pltpu.VMEM((reach, HALF), jnp.bfloat16),
                 pltpu.VMEM((reach, HALF), jnp.float32),
                 pltpu.VMEM((K * 2 * tile, HALF), jnp.float32),
                 pltpu.VMEM((2 * tile, HALF), jnp.float32),
-                pltpu.SemaphoreType.DMA((3,)),
             ],
         ),
         out_shape=shapes,
-        compiler_params=LIMIT,
+        compiler_params=pltpu.CompilerParams(vmem_limit_bytes=51 * 2**20),
         cost_estimate=cost(25),
         name="round_forward",
     )(*args)

time: 480 us -> 474 us (0.988)
  Pallas kernels: 204 us -> 199 us
    pallas_call x3, Pallas kernels: 75.9 us -> 70.8 us  [round_forward(): pl.pallas_call(body, grid_spec=pltpu.PrefetchScalarGridSpec(num_scalar_pr...]
  transfers between devices with their start and end apart: 47 -> 47, of which waited for: 26 -> 26; matrix products, arithmetic and copies ran while one was open for 11% -> 12% of each run, Pallas kernels for 11% -> 12%
where the time goes in v15:
time: 474 us; the launch traced here: 472 us
  Pallas kernels  199 us (42%)
  waiting for transfers between devices  113 us (24%)
  starting transfers between devices  78.2 us (16%)
  matrix products  30.4 us (6%)
  other arithmetic  28.5 us (6%)
  local copies, waits for them, and re-layouts  15.1 us (3%)
  between operations  7.94 us (2%)
    pallas_call x3, Pallas kernels, edges_backward(): pl.pallas_call(body, grid_spec=pltpu.PrefetchScalarGridSpec(num_scalar_pr...  79.3 us
    pallas_call x3, Pallas kernels, round_forward(): pl.pallas_call(body, grid_spec=pltpu.PrefetchScalarGridSpec(num_scalar_pr...  70.8 us
    ppermute x6, waiting for transfers between devices, halo(): lax.ppermute(initial, 'space', down)  35.4 us
    ppermute x25, waiting for transfers between devices, swapped(): lax.ppermute(value, axis, [(i, i ^ bit) for i in range(lax.axis_size(axis...  31.2 us
    ppermute x25, starting transfers between devices, swapped(): lax.ppermute(value, axis, [(i, i ^ bit) for i in range(lax.axis_size(axis...  29.4 us
    dot_general x18, matrix products, inner(): lax.dot_general(left, right, (((left_dim,), (right_dim,)), ((), ())), pre...  29.1 us
    all_to_all x3, waiting for transfers between devices, exchanged(): lax.all_to_all(rows.reshape(bands, capacity, HALF), 'space', split_axis=0...  20 us
    all_to_all x3, starting transfers between devices, exchanged(): lax.all_to_all(rows.reshape(bands, capacity, HALF), 'space', split_axis=0...  16.2 us
  transfers between devices with their start and end apart: 47, of which 26 were waited for; matrix products, arithmetic and copies ran while one was open for 12% of the time, Pallas kernels for 12%

profile of v15, /device:TPU:0, one launch (start us, length us, event | category | flops | bytes accessed | tf_op | source)
XLA Modules:
  0.0 472.5 jit_solution(13457696192836359176)
XLA Ops:
  2.5 5.1 %collective-permute-start.2 = (bf16[1,144,256]{2,1,0:T(8,128)(2,1)S(1)}, bf16[1,144,256]{2,1,0:T(8,128)(2,1)S(1)}, u32[]{:S(2)}, u32[]{:S(2)}) collective-permute-start(bf16[1,144,256]{2,1,0:T(8,128)(2,1)S(1)} %broadcast_in_dim_reshape.3), channel_id=1, source_target_pairs={{0,12},{1,13},{2,14},{3,15},{4,8},{5,9},{6,10},{7,11},{8,4},{9,5},... | collective-permute-start | bytes 221192 | tf_op jit(solution)/shard_map/ppermute | solution.py:94
  26.1 4.8 %collective-permute-done.6 = bf16[8,72,256]{2,1,0:T(8,128)(2,1)S(1)} collective-permute-done((bf16[8,72,256]{2,1,0:T(8,128)(2,1)S(1)}, bf16[8,72,256]{2,1,0:T(8,128)(2,1)S(1)}, u32[]{:S(2)}, u32[]{:S(2)}) %collective-permute-start.6) | collective-permute-done | bytes 294944 | tf_op jit(solution)/shard_map/ppermute | solution.py:94
  32.4 5.2 %all-to-all-start = ((bf16[16,64,128]{2,1,0:T(8,128)(2,1)}), bf16[16,64,128]{2,1,0:T(8,128)(2,1)S(1)}, u32[]{:S(2)}, u32[]{:S(2)}) async-start(bf16[16,64,128]{2,1,0:T(8,128)(2,1)} %bitcast.4), calls=%async_computation | async-start | bytes 524288 | tf_op jit(solution)/shard_map/all_to_all | solution.py:863
  38.6 4.0 spread_rows.1
  42.6 5.4 %all-to-all-done = bf16[16,64,128]{2,1,0:T(8,128)(2,1)S(1)} async-done(((bf16[16,64,128]{2,1,0:T(8,128)(2,1)}), bf16[16,64,128]{2,1,0:T(8,128)(2,1)S(1)}, u32[]{:S(2)}, u32[]{:S(2)}) %all-to-all-start) | async-done | bytes 262176 | tf_op jit(solution)/shard_map/all_to_all | solution.py:863
  48.7 6.0 %encode_rows.1 = (f32[2048,256]{1,0:T(8,128)}, bf16[2048,256]{1,0:T(8,128)(2,1)}, bf16[4096,128]{1,0:T(8,128)(2,1)}, s32[1,1024]{1,0:T(1,128)}, s32[1024,1]{1,0:T(8,128)}) custom-call(bf16[1024,128]{1,0:T(8,128)(2,1)} %bitcast.154, bf16[128,256]{1,0:T(8,128)(2,1)} %get-tuple-element.111.in_ref, bf16[256,256]{1,0:T(8,128)(2,1)} %get-tuple-element.112.node_ref, ...), custom_call_target="tpu_custom_call" | custom-call | bytes 15000000 | tf_op jit(solution)/shard_map/encode_rows/pallas_call | solution.py:739
  60.5 4.5 collective-permute-start.11
  65.1 4.0 node_terms.3
  69.0 11.6 %collective-permute-done.12 = bf16[79,360]{1,0:T(8,128)(2,1)S(1)} collective-permute-done((bf16[79,360]{1,0:T(8,128)(2,1)S(1)}, bf16[79,360]{1,0:T(8,128)(2,1)S(1)}, u32[]{:S(2)}, u32[]{:S(2)}) %collective-permute-start.12) | collective-permute-done | bytes 56912 | tf_op jit(solution)/shard_map/ppermute | solution.py:49
  80.8 2.7 collective-permute-done.10.refs_2_
  84.4 22.7 %round_forward.3 = (f32[2048,256]{1,0:T(8,128)}, f32[2048,256]{1,0:T(8,128)}, bf16[2048,256]{1,0:T(8,128)(2,1)S(1)}, bf16[2048,256]{1,0:T(8,128)(2,1)}, bf16[6,4...) custom-call(s32[12288]{0:T(1024)S(1)} %collective-permute-done.9.refs_0_, ...), custom_call_target="tpu_custom_call" | custom-call | bytes 75000000 | tf_op jit(solution)/shard_map/round_forward/pallas_call | solution.py:491
  109.2 3.9 node_terms.4
  113.1 16.9 %collective-permute-done.16.refs_4_ = bf16[4096,128]{1,0:T(8,128)(2,1)} collective-permute-done((bf16[4096,128]{1,0:T(8,128)(2,1)}, bf16[4096,128]{1,0:T(8,128)(2,1)}, u32[]{:S(2)}, u32[]{:S(2)}) %collective-permute-start.16) | collective-permute-done | bytes 1048608 | tf_op jit(solution)/shard_map/ppermute | solution.py:77
  130.0 3.1 collective-permute-done.15.refs_2_
  133.1 22.7 %round_forward.4 = (f32[2048,256]{1,0:T(8,128)}, f32[2048,256]{1,0:T(8,128)}, bf16[2048,256]{1,0:T(8,128)(2,1)S(1)}, bf16[2048,256]{1,0:T(8,128)(2,1)}, bf16[6,4...) custom-call(s32[12288]{0:T(1024)S(1)} %collective-permute-done.9.refs_0_, ...), custom_call_target="tpu_custom_call" | custom-call | bytes 75000000 | tf_op jit(solution)/shard_map/round_forward/pallas_call | solution.py:491
  159.1 3.9 node_terms.5
  163.0 18.4 %collective-permute-done.18.refs_4_ = bf16[4096,128]{1,0:T(8,128)(2,1)} collective-permute-done((bf16[4096,128]{1,0:T(8,128)(2,1)}, bf16[4096,128]{1,0:T(8,128)(2,1)}, u32[]{:S(2)}, u32[]{:S(2)}) %collective-permute-start.18) | collective-permute-done | bytes 1048608 | tf_op jit(solution)/shard_map/ppermute | solution.py:77
  181.5 25.4 %round_forward.5 = (f32[2048,256]{1,0:T(8,128)}, f32[2048,256]{1,0:T(8,128)}, bf16[2048,256]{1,0:T(8,128)(2,1)}, bf16[2048,256]{1,0:T(8,128)(2,1)}, bf16[6,4096,...) custom-call(s32[12288]{0:T(1024)S(1)} %collective-permute-done.9.ref, ...), custom_call_target="tpu_custom_call" | custom-call | bytes 75000000 | tf_op jit(solution)/shard_map/round_forward/pallas_call | solution.py:491
  207.7 5.2 %all-to-all-start.1 = ((bf16[16,64,128]{2,1,0:T(8,128)(2,1)}), bf16[16,64,128]{2,1,0:T(8,128)(2,1)S(1)}, u32[]{:S(2)}, u32[]{:S(2)}) async-start(bf16[16,64,128]{2,1,0:T(8,128)(2,1)} %bitcast.14), calls=%async_computation.1 | async-start | bytes 524288 | tf_op jit(solution)/shard_map/all_to_all | solution.py:863
  212.9 8.4 %all-to-all-done.1 = bf16[16,64,128]{2,1,0:T(8,128)(2,1)S(1)} async-done(((bf16[16,64,128]{2,1,0:T(8,128)(2,1)}), bf16[16,64,128]{2,1,0:T(8,128)(2,1)S(1)}, u32[]{:S(2)}, u32[]{:S(2)}) %all-to-all-start.1) | async-done | bytes 262176 | tf_op jit(solution)/shard_map/all_to_all | solution.py:863
  222.9 3.3 collective-permute-start.19
  235.3 5.9 %all-to-all-start.2 = ((bf16[16,64,128]{2,1,0:T(8,128)(2,1)}), bf16[16,64,128]{2,1,0:T(8,128)(2,1)S(1)}, u32[]{:S(2)}, u32[]{:S(2)}) async-start(bf16[16,64,128]{2,1,0:T(8,128)(2,1)} %bitcast.18), calls=%async_computation.2 | async-start | bytes 524288 | tf_op jit(solution)/shard_map/all_to_all | solution.py:863
  243.5 6.2 %all-to-all-done.2 = bf16[16,64,128]{2,1,0:T(8,128)(2,1)S(1)} async-done(((bf16[16,64,128]{2,1,0:T(8,128)(2,1)}), bf16[16,64,128]{2,1,0:T(8,128)(2,1)S(1)}, u32[]{:S(2)}, u32[]{:S(2)}) %all-to-all-start.2) | async-done | bytes 262176 | tf_op jit(solution)/shard_map/all_to_all | solution.py:863
  251.4 26.8 %edges_backward.3 = (f32[2048,256]{1,0:T(8,128)}, bf16[2048,256]{1,0:T(8,128)(2,1)}, bf16[1024,256]{1,0:T(8,128)(2,1)}, bf16[2048,256]{1,0:T(8,128)(2,1)}, bf16[...) custom-call(s32[12288]{0:T(1024)} %copy-done.6, ...), custom_call_target="tpu_custom_call" | custom-call | bytes 75000000 | tf_op jit(solution)/shard_map/edges_backward/pallas_call | solution.py:632
  283.0 2.4 fusion.95.refs_18_
  288.1 2.4 collective-permute-start.23
  292.2 4.0 carried_terms.3.refs_4_
  296.9 2.4 fusion.65.refs_17_
  299.3 3.5 convert_select_fusion
  302.7 4.8 %collective-permute-done.22.refs_6_ = bf16[4096,128]{1,0:T(8,128)(2,1)} collective-permute-done((bf16[4096,128]{1,0:T(8,128)(2,1)}, bf16[4096,128]{1,0:T(8,128)(2,1)}, u32[]{:S(2)}, u32[]{:S(2)}) %collective-permute-start.22) | collective-permute-done | bytes 1048608 | tf_op jit(solution)/shard_map/ppermute | solution.py:77
  307.5 26.1 %edges_backward.4 = (f32[2048,256]{1,0:T(8,128)}, bf16[2048,256]{1,0:T(8,128)(2,1)}, bf16[2048,256]{1,0:T(8,128)(2,1)}, bf16[2048,256]{1,0:T(8,128)(2,1)}, bf16[...) custom-call(s32[12288]{0:T(1024)} %copy-done.6, ...), custom_call_target="tpu_custom_call" | custom-call | bytes 84000000 | tf_op jit(solution)/shard_map/edges_backward/pallas_call | solution.py:632
  334.6 3.1 collective-permute-start.25
  337.7 2.7 fusion.92.refs_11_
  341.7 3.9 carried_terms.4.refs_4_
  345.6 2.6 convert_reduce_fusion.2
  348.2 2.5 fusion.73.refs_10_
  353.9 26.4 %edges_backward.5 = (f32[2048,256]{1,0:T(8,128)}, bf16[2048,256]{1,0:T(8,128)(2,1)}, bf16[2048,256]{1,0:T(8,128)(2,1)}, bf16[2048,256]{1,0:T(8,128)(2,1)}, bf16[...) custom-call(s32[12288]{0:T(1024)} %copy-done.6, ...), custom_call_target="tpu_custom_call" | custom-call | bytes 84000000 | tf_op jit(solution)/shard_map/edges_backward/pallas_call | solution.py:632
  380.4 3.8 collective-permute-start.27
  384.2 2.4 fusion.90.refs_6_
  387.8 4.0 carried_terms.5.part_ref
  400.3 10.0 %encode_backward.1 = (f32[2048,256]{1,0:T(8,128)}, bf16[2048,256]{1,0:T(8,128)(2,1)}, f32[128,256]{1,0:T(8,128)}, f32[256,256]{1,0:T(8,128)}, f32[2,256]{1,0:T(2,128)}, /*index=5*/f32[256,256]{1,0:T(8,128)}) custom-call(f32[2048,256]{1,0:T(8,128)} %carried_terms.5.part_ref, f32[4096,128]{1,0:T(8,128)} %get-tuple-element.171.own_ref, ...), custom_call_target="tpu_custom_call" | custom-call | bytes 30000000 | tf_op jit(solution)/shard_map/encode_backward/pallas_call | solution.py:804
  410.3 5.1 %collect_rows.1 = (f32[16,144,256]{2,1,0:T(8,128)}, bf16[16,144,256]{2,1,0:T(8,128)(2,1)}) custom-call(s32[1]{0:T(128)} %bitcast.6.place_ref, f32[128,256]{1,0:T(8,128)} %get-tuple-element.175.refs_0_, f32[256,256]{1,0:T(8,128)} %get-tuple-element.176.refs_1_, f32[256,256]{1,0:T(8,128)} %fusion.89.refs_2_, f32[78,256]{1,0:T(8,128)} %reshape.155.refs_3_, ...), custom_call_target="tpu_custom_call" | custom-call | bytes 15000000 | tf_op jit(solution)/shard_map/collect_rows/pallas_call | solution.py:233
  415.6 3.0 collective-permute-done.28
  420.9 8.9 %collective-permute-done.29 = bf16[4,2,72,256]{3,2,0,1:T(8,128)(2,1)S(1)} collective-permute-done((bf16[4,2,72,256]{3,2,0,1:T(8,128)(2,1)S(1)}, bf16[4,2,72,256]{3,2,0,1:T(8,128)(2,1)S(1)}, u32[]{:S(2)}, u32[]{:S(2)}) %collective-permute-start.29) | collective-permute-done | bytes 294944 | tf_op jit(solution)/shard_map/ppermute | solution.py:94
  431.8 3.3 collective-permute-done.30
  437.4 4.7 collective-permute-start.35
  457.2 5.8 %collective-permute-start.43 = (f32[8,128]{1,0:T(8,128)S(1)}, f32[8,128]{1,0:T(8,128)S(1)}, u32[]{:S(2)}, u32[]{:S(2)}) collective-permute-start(f32[8,128]{1,0:T(8,128)S(1)} %add.191), channel_id=1, source_target_pairs={{0,3},{1,2},{2,1},{3,0},{4,7},{5,6},{6,5},{7,4},{8,11},{9,10},{10,... | collective-permute-start | bytes 12296 | tf_op jit(solution)/shard_map/ppermute | solution.py:94
  464.5 3.4 select_bitcast_fusion
  (269 shorter events, 97.1 us)
Async XLA Ops:
  2.5 14.5 %collective-permute-start.2 = (bf16[1,144,256]{2,1,0:T(8,128)(2,1)S(1)}, bf16[1,144,256]{2,1,0:T(8,128)(2,1)S(1)}, u32[]{:S(2)}, u32[]{:S(2)}) collective-permute-start(bf16[1,144,256]{2,1,0:T(8,128)(2,1)S(1)} %broadcast_in_dim_reshape.3), channel_id=1, source_target_pairs={{0,12},{1,13},{2,14},{3,15},{4,8},{5,9},{6,10},{7,11},{8,4},{9,5},... | collective-permute-start | bytes 221192 | tf_op jit(solution)/shard_map/ppermute | solution.py:94
  7.6 9.4 %collective-permute-start.1 = (bf16[1,144,256]{2,1,0:T(8,128)(2,1)S(1)}, bf16[1,144,256]{2,1,0:T(8,128)(2,1)S(1)}, u32[]{:S(2)}, u32[]{:S(2)}) collective-permute-start(bf16[1,144,256]{2,1,0:T(8,128)(2,1)S(1)} %broadcast_in_dim_reshape.3), channel_id=1, source_target_pairs={{0,8},{1,9},{2,10},{3,11},{4,12},{5,13},{6,14},{7,15},{8,0},{9,1},... | collective-permute-start | bytes 221192 | tf_op jit(solution)/shard_map/ppermute | solution.py:94
  7.6 9.4 %collective-permute-start = (bf16[1,144,256]{2,1,0:T(8,128)(2,1)S(1)}, bf16[1,144,256]{2,1,0:T(8,128)(2,1)S(1)}, u32[]{:S(2)}, u32[]{:S(2)}) collective-permute-start(bf16[1,144,256]{2,1,0:T(8,128)(2,1)S(1)} %broadcast_in_dim_reshape.3), channel_id=1, source_target_pairs={{0,4},{1,5},{2,6},{3,7},{4,0},{5,1},{6,2},{7,3},{8,12},{9,13},{10,... | collective-permute-start | bytes 221192 | tf_op jit(solution)/shard_map/ppermute | solution.py:94
  17.0 5.2 %collective-permute-start.4 = (bf16[4,72,256]{2,1,0:T(8,128)(2,1)S(1)}, bf16[4,72,256]{2,1,0:T(8,128)(2,1)S(1)}, u32[]{:S(2)}, u32[]{:S(2)}) collective-permute-start(bf16[4,72,256]{2,1,0:T(8,128)(2,1)S(1)} %get-tuple-element.247), channel_id=1, source_target_pairs={{0,1},{1,0},{2,3},{3,2},{4,5},{5,4},{6,7},{7,6},{8,9},{9,8},{10,11... | collective-permute-start | bytes 442376 | tf_op jit(solution)/shard_map/ppermute | solution.py:94
  18.7 5.1 %collective-permute-start.3 = (bf16[4,72,256]{2,1,0:T(8,128)(2,1)S(1)}, bf16[4,72,256]{2,1,0:T(8,128)(2,1)S(1)}, u32[]{:S(2)}, u32[]{:S(2)}) collective-permute-start(bf16[4,72,256]{2,1,0:T(8,128)(2,1)S(1)} %get-tuple-element.248), channel_id=1, source_target_pairs={{0,2},{1,3},{2,0},{3,1},{4,6},{5,7},{6,4},{7,5},{8,10},{9,11},{10,... | collective-permute-start | bytes 442376 | tf_op jit(solution)/shard_map/ppermute | solution.py:94
  23.9 7.0 %collective-permute-start.6 = (bf16[8,72,256]{2,1,0:T(8,128)(2,1)S(1)}, bf16[8,72,256]{2,1,0:T(8,128)(2,1)S(1)}, u32[]{:S(2)}, u32[]{:S(2)}) collective-permute-start(bf16[8,72,256]{2,1,0:T(8,128)(2,1)S(1)} %pad_maximum_fusion.3), channel_id=1, source_target_pairs={{0,2},{1,3},{2,0},{3,1},{4,6},{5,7},{6,4},{7,5},{8,10},{9,11},{10,... | collective-permute-start | bytes 884744 | tf_op jit(solution)/shard_map/ppermute | solution.py:94
  25.5 6.7 %collective-permute-start.5 = (bf16[8,72,256]{2,1,0:T(8,128)(2,1)S(1)}, bf16[8,72,256]{2,1,0:T(8,128)(2,1)S(1)}, u32[]{:S(2)}, u32[]{:S(2)}) collective-permute-start(bf16[8,72,256]{2,1,0:T(8,128)(2,1)S(1)} %pad_maximum_fusion.2), channel_id=1, source_target_pairs={{0,1},{1,0},{2,3},{3,2},{4,5},{5,4},{6,7},{7,6},{8,9},{9,8},{10,11... | collective-permute-start | bytes 884744 | tf_op jit(solution)/shard_map/ppermute | solution.py:94
  30.9 6.7 %collective-permute-start.8 = (bf16[16,72,256]{2,1,0:T(8,128)(2,1)S(1)}, bf16[16,72,256]{2,1,0:T(8,128)(2,1)S(1)}, u32[]{:S(2)}, u32[]{:S(2)}) collective-permute-start(bf16[16,72,256]{2,1,0:T(8,128)(2,1)S(1)} %constant_dynamic-update-slice_fusion.6.refs_1_), channel_id=1, source_target_pairs={{0,16},{16,0},{1,17},{17,1},{2,18},{18,2},{3,19},{19,3},{4,20},{20... | collective-permute-start | bytes 1769480 | tf_op jit(solution)/shard_map/ppermute | solution.py:94
  32.3 5.3 %collective-permute-start.7 = (bf16[16,72,256]{2,1,0:T(8,128)(2,1)S(1)}, bf16[16,72,256]{2,1,0:T(8,128)(2,1)S(1)}, u32[]{:S(2)}, u32[]{:S(2)}) collective-permute-start(bf16[16,72,256]{2,1,0:T(8,128)(2,1)S(1)} %constant_dynamic-update-slice_fusion.4.refs_0_), channel_id=1, source_target_pairs={{0,16},{16,0},{1,17},{17,1},{2,18},{18,2},{3,19},{19,3},{4,20},{20... | collective-permute-start | bytes 1769480 | tf_op jit(solution)/shard_map/ppermute | solution.py:94
  32.4 15.6 %all-to-all-start = ((bf16[16,64,128]{2,1,0:T(8,128)(2,1)}), bf16[16,64,128]{2,1,0:T(8,128)(2,1)S(1)}, u32[]{:S(2)}, u32[]{:S(2)}) async-start(bf16[16,64,128]{2,1,0:T(8,128)(2,1)} %bitcast.4), calls=%async_computation | async-start | bytes 524288 | tf_op jit(solution)/shard_map/all_to_all | solution.py:863
  54.7 28.7 %collective-permute-start.14 = (bf16[4096,128]{1,0:T(8,128)(2,1)}, bf16[4096,128]{1,0:T(8,128)(2,1)S(1)}, u32[]{:S(2)}, u32[]{:S(2)}) collective-permute-start(bf16[4096,128]{1,0:T(8,128)(2,1)} %get-tuple-element.119.refs_3_), channel_id=1, source_target_pairs={{1,0},{3,1},{2,3},{6,2},{4,6},{5,4},{7,5},{11,7},{9,11},{8,9},{10,... | collective-permute-start | bytes 3145736 | tf_op jit(solution)/shard_map/ppermute | solution.py:77
  56.5 26.9 %collective-permute-start.10 = (bf16[4096,128]{1,0:T(8,128)(2,1)}, bf16[4096,128]{1,0:T(8,128)(2,1)}, u32[]{:S(2)}, u32[]{:S(2)}) collective-permute-start(bf16[4096,128]{1,0:T(8,128)(2,1)} %get-tuple-element.119.refs_3_), channel_id=1, source_target_pairs={{0,1},{1,3},{3,2},{2,6},{6,4},{4,5},{5,7},{7,11},{11,9},{9,8},{8,1... | collective-permute-start | bytes 3145736 | tf_op jit(solution)/shard_map/ppermute | solution.py:77
  56.8 3.7 collective-permute-start.13
  57.0 26.4 %collective-permute-start.9 = (s32[12288]{0:T(1024)S(1)}, s32[12288]{0:T(1024)S(1)}, u32[]{:S(2)}, u32[]{:S(2)}) collective-permute-start(s32[12288]{0:T(1024)S(1)} %mul.177), channel_id=1, source_target_pairs={{0,0},{1,1},{2,3},{3,2},{4,6},{5,4},{6,5},{7,7},{8,11},{9,9},{10,8... | collective-permute-start | bytes 147464 | tf_op jit(solution)/shard_map/ppermute | solution.py:891
  57.8 22.8 %collective-permute-start.12 = (bf16[79,360]{1,0:T(8,128)(2,1)S(1)}, bf16[79,360]{1,0:T(8,128)(2,1)S(1)}, u32[]{:S(2)}, u32[]{:S(2)}) collective-permute-start(bf16[79,360]{1,0:T(8,128)(2,1)S(1)} %get-tuple-element.249), channel_id=1, source_target_pairs={{1,0},{2,1},{3,2},{4,3},{5,4},{6,5},{7,6},{8,7},{9,8},{10,9},{11,1... | collective-permute-start | bytes 170648 | tf_op jit(solution)/shard_map/ppermute | solution.py:49
  60.5 20.1 %collective-permute-start.11 = (bf16[79,360]{1,0:T(8,128)(2,1)S(1)}, bf16[79,360]{1,0:T(8,128)(2,1)S(1)}, u32[]{:S(2)}, u32[]{:S(2)}) collective-permute-start(bf16[79,360]{1,0:T(8,128)(2,1)S(1)} %get-tuple-element.250), channel_id=1, source_target_pairs={{0,1},{1,2},{2,3},{3,4},{4,5},{5,6},{6,7},{7,8},{8,9},{9,10},{10,1... | collective-permute-start | bytes 170648 | tf_op jit(solution)/shard_map/ppermute | solution.py:49
  83.4 98.0 %copy-start.6 = (s32[12288]{0:T(1024)}, s32[12288]{0:T(1024)S(1)}, u32[]{:S(2)}) copy-start(s32[12288]{0:T(1024)S(1)} %collective-permute-done.9.refs_0_) | copy-start | bytes 147460
  107.1 22.8 %collective-permute-start.16 = (bf16[4096,128]{1,0:T(8,128)(2,1)}, bf16[4096,128]{1,0:T(8,128)(2,1)}, u32[]{:S(2)}, u32[]{:S(2)}) collective-permute-start(bf16[4096,128]{1,0:T(8,128)(2,1)} %get-tuple-element.127.refs_3_), channel_id=1, source_target_pairs={{1,0},{3,1},{2,3},{6,2},{4,6},{5,4},{7,5},{11,7},{9,11},{8,9},{10,... | collective-permute-start | bytes 3145736 | tf_op jit(solution)/shard_map/ppermute | solution.py:77
  108.4 24.7 %collective-permute-start.15 = (bf16[4096,128]{1,0:T(8,128)(2,1)}, bf16[4096,128]{1,0:T(8,128)(2,1)}, u32[]{:S(2)}, u32[]{:S(2)}) collective-permute-start(bf16[4096,128]{1,0:T(8,128)(2,1)} %get-tuple-element.127.refs_3_), channel_id=1, source_target_pairs={{0,1},{1,3},{3,2},{2,6},{6,4},{4,5},{5,7},{7,11},{11,9},{9,8},{8,1... | collective-permute-start | bytes 3145736 | tf_op jit(solution)/shard_map/ppermute | solution.py:77
  156.8 24.7 %collective-permute-start.18 = (bf16[4096,128]{1,0:T(8,128)(2,1)}, bf16[4096,128]{1,0:T(8,128)(2,1)}, u32[]{:S(2)}, u32[]{:S(2)}) collective-permute-start(bf16[4096,128]{1,0:T(8,128)(2,1)} %get-tuple-element.132.refs_3_), channel_id=1, source_target_pairs={{1,0},{3,1},{2,3},{6,2},{4,6},{5,4},{7,5},{11,7},{9,11},{8,9},{10,... | collective-permute-start | bytes 3145736 | tf_op jit(solution)/shard_map/ppermute | solution.py:77
  157.1 24.3 %collective-permute-start.17 = (bf16[4096,128]{1,0:T(8,128)(2,1)}, bf16[4096,128]{1,0:T(8,128)(2,1)}, u32[]{:S(2)}, u32[]{:S(2)}) collective-permute-start(bf16[4096,128]{1,0:T(8,128)(2,1)} %get-tuple-element.132.refs_3_), channel_id=1, source_target_pairs={{0,1},{1,3},{3,2},{2,6},{6,4},{4,5},{5,7},{7,11},{11,9},{9,8},{8,1... | collective-permute-start | bytes 3145736 | tf_op jit(solution)/shard_map/ppermute | solution.py:77
  207.7 13.7 %all-to-all-start.1 = ((bf16[16,64,128]{2,1,0:T(8,128)(2,1)}), bf16[16,64,128]{2,1,0:T(8,128)(2,1)S(1)}, u32[]{:S(2)}, u32[]{:S(2)}) async-start(bf16[16,64,128]{2,1,0:T(8,128)(2,1)} %bitcast.14), calls=%async_computation.1 | async-start | bytes 524288 | tf_op jit(solution)/shard_map/all_to_all | solution.py:863
  222.9 9.5 %collective-permute-start.19 = (bf16[78,360]{1,0:T(8,128)(2,1)S(1)}, bf16[78,360]{1,0:T(8,128)(2,1)S(1)}, u32[]{:S(2)}, u32[]{:S(2)}) collective-permute-start(bf16[78,360]{1,0:T(8,128)(2,1)S(1)} %get-tuple-element.251), channel_id=1, source_target_pairs={{0,1},{1,2},{2,3},{3,4},{4,5},{5,6},{6,7},{7,8},{8,9},{9,10},{10,1... | collective-permute-start | bytes 168488 | tf_op jit(solution)/shard_map/ppermute | solution.py:49
  226.2 6.1 %collective-permute-start.20 = (bf16[78,360]{1,0:T(8,128)(2,1)S(1)}, bf16[78,360]{1,0:T(8,128)(2,1)S(1)}, u32[]{:S(2)}, u32[]{:S(2)}) collective-permute-start(bf16[78,360]{1,0:T(8,128)(2,1)S(1)} %get-tuple-element.252), channel_id=1, source_target_pairs={{1,0},{2,1},{3,2},{4,3},{5,4},{6,5},{7,6},{8,7},{9,8},{10,9},{11,1... | collective-permute-start | bytes 168488 | tf_op jit(solution)/shard_map/ppermute | solution.py:49
  235.3 14.4 %all-to-all-start.2 = ((bf16[16,64,128]{2,1,0:T(8,128)(2,1)}), bf16[16,64,128]{2,1,0:T(8,128)(2,1)S(1)}, u32[]{:S(2)}, u32[]{:S(2)}) async-start(bf16[16,64,128]{2,1,0:T(8,128)(2,1)} %bitcast.18), calls=%async_computation.2 | async-start | bytes 524288 | tf_op jit(solution)/shard_map/all_to_all | solution.py:863
  249.8 36.9 %collective-permute-start.21 = (bf16[2048,256]{1,0:T(8,128)(2,1)S(1)}, bf16[2048,256]{1,0:T(8,128)(2,1)}, u32[]{:S(2)}, u32[]{:S(2)}) collective-permute-start(bf16[2048,256]{1,0:T(8,128)(2,1)S(1)} %convert_element_type.182), channel_id=1, source_target_pairs={{3,2},{2,3},{6,4},{4,5},{5,6},{11,8},{8,10},{10,11},{14,12},{15,13... | collective-permute-start | bytes 3145736 | tf_op jit(solution)/shard_map/ppermute | solution.py:894
  286.6 20.9 %collective-permute-start.22 = (bf16[4096,128]{1,0:T(8,128)(2,1)}, bf16[4096,128]{1,0:T(8,128)(2,1)}, u32[]{:S(2)}, u32[]{:S(2)}) collective-permute-start(bf16[4096,128]{1,0:T(8,128)(2,1)} %get-tuple-element.158), channel_id=1, source_target_pairs={{0,1},{1,3},{3,2},{2,6},{6,4},{4,5},{5,7},{7,11},{11,9},{9,8},{8,1... | collective-permute-start | bytes 3145736 | tf_op jit(solution)/shard_map/ppermute | solution.py:77
  288.1 19.5 %collective-permute-start.23 = (bf16[4096,128]{1,0:T(8,128)(2,1)}, bf16[4096,128]{1,0:T(8,128)(2,1)}, u32[]{:S(2)}, u32[]{:S(2)}) collective-permute-start(bf16[4096,128]{1,0:T(8,128)(2,1)} %get-tuple-element.161), channel_id=1, source_target_pairs={{1,0},{3,1},{2,3},{6,2},{4,6},{5,4},{7,5},{11,7},{9,11},{8,9},{10,... | collective-permute-start | bytes 3145736 | tf_op jit(solution)/shard_map/ppermute | solution.py:77
  333.6 20.2 %collective-permute-start.24 = (bf16[4096,128]{1,0:T(8,128)(2,1)}, bf16[4096,128]{1,0:T(8,128)(2,1)}, u32[]{:S(2)}, u32[]{:S(2)}) collective-permute-start(bf16[4096,128]{1,0:T(8,128)(2,1)} %get-tuple-element.166), channel_id=1, source_target_pairs={{0,1},{1,3},{3,2},{2,6},{6,4},{4,5},{5,7},{7,11},{11,9},{9,8},{8,1... | collective-permute-start | bytes 3145736 | tf_op jit(solution)/shard_map/ppermute | solution.py:77
  334.6 19.3 %collective-permute-start.25 = (bf16[4096,128]{1,0:T(8,128)(2,1)}, bf16[4096,128]{1,0:T(8,128)(2,1)}, u32[]{:S(2)}, u32[]{:S(2)}) collective-permute-start(bf16[4096,128]{1,0:T(8,128)(2,1)} %get-tuple-element.167), channel_id=1, source_target_pairs={{1,0},{3,1},{2,3},{6,2},{4,6},{5,4},{7,5},{11,7},{9,11},{8,9},{10,... | collective-permute-start | bytes 3145736 | tf_op jit(solution)/shard_map/ppermute | solution.py:77
  380.3 19.0 %collective-permute-start.26 = (bf16[4096,128]{1,0:T(8,128)(2,1)}, bf16[4096,128]{1,0:T(8,128)(2,1)S(1)}, u32[]{:S(2)}, u32[]{:S(2)}) collective-permute-start(bf16[4096,128]{1,0:T(8,128)(2,1)} %get-tuple-element.172), channel_id=1, source_target_pairs={{0,1},{1,3},{3,2},{2,6},{6,4},{4,5},{5,7},{7,11},{11,9},{9,8},{8,1... | collective-permute-start | bytes 3145736 | tf_op jit(solution)/shard_map/ppermute | solution.py:77
  380.4 18.9 %collective-permute-start.27 = (bf16[4096,128]{1,0:T(8,128)(2,1)}, bf16[4096,128]{1,0:T(8,128)(2,1)}, u32[]{:S(2)}, u32[]{:S(2)}) collective-permute-start(bf16[4096,128]{1,0:T(8,128)(2,1)} %get-tuple-element.173), channel_id=1, source_target_pairs={{1,0},{3,1},{2,3},{6,2},{4,6},{5,4},{7,5},{11,7},{9,11},{8,9},{10,... | collective-permute-start | bytes 3145736 | tf_op jit(solution)/shard_map/ppermute | solution.py:77
  415.5 3.1 collective-permute-start.28
  420.7 9.1 %collective-permute-start.29 = (bf16[4,2,72,256]{3,2,0,1:T(8,128)(2,1)S(1)}, bf16[4,2,72,256]{3,2,0,1:T(8,128)(2,1)S(1)}, u32[]{:S(2)}, u32[]{:S(2)}) collective-permute-start(bf16[4,2,72,256]{3,2,0,1:T(8,128)(2,1)S(1)} %fusion.18), channel_id=1, source_target_pairs={{0,1},{1,0},{2,3},{3,2},{4,5},{5,4},{6,7},{7,6},{8,9},{9,8},{10,11... | collective-permute-start | bytes 884744 | tf_op jit(solution)/shard_map/ppermute | solution.py:94
  420.8 9.2 %collective-permute-start.31 = (bf16[4,2,72,256]{3,2,1,0:T(8,128)(2,1)S(1)}, bf16[4,2,72,256]{3,2,1,0:T(8,128)(2,1)S(1)}, u32[]{:S(2)}, u32[]{:S(2)}) collective-permute-start(bf16[4,2,72,256]{3,2,1,0:T(8,128)(2,1)S(1)} %fusion.17), channel_id=1, source_target_pairs={{0,2},{1,3},{2,0},{3,1},{4,6},{5,7},{6,4},{7,5},{8,10},{9,11},{10,... | collective-permute-start | bytes 884744 | tf_op jit(solution)/shard_map/ppermute | solution.py:94
  430.0 5.2 %collective-permute-start.30 = (bf16[4,72,256]{2,1,0:T(8,128)(2,1)S(1)}, bf16[4,72,256]{2,1,0:T(8,128)(2,1)S(1)}, u32[]{:S(2)}, u32[]{:S(2)}) collective-permute-start(bf16[4,72,256]{2,1,0:T(8,128)(2,1)S(1)} %fusion.44), channel_id=1, source_target_pairs={{0,2},{1,3},{2,0},{3,1},{4,6},{5,7},{6,4},{7,5},{8,10},{9,11},{10,... | collective-permute-start | bytes 442376 | tf_op jit(solution)/shard_map/ppermute | solution.py:94
  430.1 5.2 %collective-permute-start.32 = (bf16[4,72,256]{2,1,0:T(8,128)(2,1)S(1)}, bf16[4,72,256]{2,1,0:T(8,128)(2,1)S(1)}, u32[]{:S(2)}, u32[]{:S(2)}) collective-permute-start(bf16[4,72,256]{2,1,0:T(8,128)(2,1)S(1)} %fusion.45), channel_id=1, source_target_pairs={{0,1},{1,0},{2,3},{3,2},{4,5},{5,4},{6,7},{7,6},{8,9},{9,8},{10,11... | collective-permute-start | bytes 442376 | tf_op jit(solution)/shard_map/ppermute | solution.py:94
  435.4 21.8 %collective-permute-start.40 = (bf16[2048,256]{1,0:T(8,128)(2,1)}, bf16[2048,256]{1,0:T(8,128)(2,1)}, u32[]{:S(2)}, u32[]{:S(2)}) collective-permute-start(bf16[2048,256]{1,0:T(8,128)(2,1)} %get-tuple-element.197), channel_id=1, source_target_pairs={{3,2},{2,3},{6,4},{4,5},{5,6},{11,8},{8,10},{10,11},{14,12},{15,13... | collective-permute-start | bytes 3145736 | tf_op jit(solution)/shard_map/ppermute | solution.py:894
  437.3 6.6 %collective-permute-start.33 = (bf16[1,144,256]{2,1,0:T(8,128)(2,1)S(1)}, bf16[1,144,256]{2,1,0:T(8,128)(2,1)S(1)}, u32[]{:S(2)}, u32[]{:S(2)}) collective-permute-start(bf16[1,144,256]{2,1,0:T(8,128)(2,1)S(1)} %get-tuple-element.244), channel_id=1, source_target_pairs={{0,4},{1,5},{2,6},{3,7},{4,0},{5,1},{6,2},{7,3},{8,12},{9,13},{10,... | collective-permute-start | bytes 221192 | tf_op jit(solution)/shard_map/ppermute | solution.py:94
  437.4 8.6 %collective-permute-start.35 = (bf16[1,144,256]{2,1,0:T(8,128)(2,1)S(1)}, bf16[1,144,256]{2,1,0:T(8,128)(2,1)S(1)}, u32[]{:S(2)}, u32[]{:S(2)}) collective-permute-start(bf16[1,144,256]{2,1,0:T(8,128)(2,1)S(1)} %get-tuple-element.245), channel_id=1, source_target_pairs={{0,12},{1,13},{2,14},{3,15},{4,8},{5,9},{6,10},{7,11},{8,4},{9,5},... | collective-permute-start | bytes 221192 | tf_op jit(solution)/shard_map/ppermute | solution.py:94
  442.1 6.1 %collective-permute-start.34 = (bf16[1,144,256]{2,1,0:T(8,128)(2,1)S(1)}, bf16[1,144,256]{2,1,0:T(8,128)(2,1)S(1)}, u32[]{:S(2)}, u32[]{:S(2)}) collective-permute-start(bf16[1,144,256]{2,1,0:T(8,128)(2,1)S(1)} %get-tuple-element.246), channel_id=1, source_target_pairs={{0,8},{1,9},{2,10},{3,11},{4,12},{5,13},{6,14},{7,15},{8,0},{9,1},... | collective-permute-start | bytes 221192 | tf_op jit(solution)/shard_map/ppermute | solution.py:94
  449.7 4.6 collective-permute-start.37
  450.2 5.4 %collective-permute-start.38 = (f32[8,128]{1,0:T(8,128)S(1)}, f32[8,128]{1,0:T(8,128)S(1)}, u32[]{:S(2)}, u32[]{:S(2)}) collective-permute-start(f32[8,128]{1,0:T(8,128)S(1)} %iota.23), channel_id=1, source_target_pairs={{0,12},{1,13},{2,14},{3,15},{4,8},{5,9},{6,10},{7,11},{8,4},{9,5},... | collective-permute-start | bytes 12296 | tf_op jit(solution)/shard_map/ppermute | solution.py:94
  452.4 3.6 collective-permute-start.36
  456.0 1.2 collective-permute-start.39
  457.2 10.7 %collective-permute-start.43 = (f32[8,128]{1,0:T(8,128)S(1)}, f32[8,128]{1,0:T(8,128)S(1)}, u32[]{:S(2)}, u32[]{:S(2)}) collective-permute-start(f32[8,128]{1,0:T(8,128)S(1)} %add.191), channel_id=1, source_target_pairs={{0,3},{1,2},{2,1},{3,0},{4,7},{5,6},{6,5},{7,4},{8,11},{9,10},{10,... | collective-permute-start | bytes 12296 | tf_op jit(solution)/shard_map/ppermute | solution.py:94
  463.1 4.8 %collective-permute-start.42 = (f32[8,128]{1,0:T(8,128)S(1)}, f32[8,128]{1,0:T(8,128)S(1)}, u32[]{:S(2)}, u32[]{:S(2)}) collective-permute-start(f32[8,128]{1,0:T(8,128)S(1)} %add.191), channel_id=1, source_target_pairs={{0,2},{1,3},{2,0},{3,1},{4,6},{5,7},{6,4},{7,5},{8,10},{9,11},{10,... | collective-permute-start | bytes 12296 | tf_op jit(solution)/shard_map/ppermute | solution.py:94
  463.1 4.8 %collective-permute-start.41 = (f32[8,128]{1,0:T(8,128)S(1)}, f32[8,128]{1,0:T(8,128)S(1)}, u32[]{:S(2)}, u32[]{:S(2)}) collective-permute-start(f32[8,128]{1,0:T(8,128)S(1)} %add.191), channel_id=1, source_target_pairs={{0,1},{1,0},{2,3},{3,2},{4,5},{5,4},{6,7},{7,6},{8,9},{9,8},{10,11... | collective-permute-start | bytes 12296 | tf_op jit(solution)/shard_map/ppermute | solution.py:94
  (50 other events, 588.0 us)
